TPU v7x, 32 devices: a whole 2x2x4 slice. The times are simulated.
32 devices in a mesh: row: 8 (over z, y), col: 4 (over x, core).
Axes of the slice: x: 2, y: 2, z: 4, core: 2. Of those that a mesh axis runs over, the one named last changes fastest.
Arguments:
- tokens_in: bfloat16 [10240, 1024], P('row', 'col'), may hold values from -6 to 6
- grad_out: bfloat16 [10240, 1024], P('row', 'col'), may hold values from -6 to 6
- keep_mask: int32 [32, 256], P('row'), may hold values 0 or 1
- adapter_index: int32 [32], P('row'), may hold values from 0 to 7
- ln_gain: float32 [2, 1024], replicated, may hold values from 0.25 to 1.75
- ln_shift: float32 [2, 1024], replicated, may hold values from -1.8 to 1.8
- w_qkv: bfloat16 [3, 1024, 1024], P(None, 'row', 'col'), may hold values from -0.1875 to 0.1875
- bias_qv: bfloat16 [2, 1024], P(None, 'col'), may hold values from -1.796875 to 1.796875
- w_proj: bfloat16 [1024, 1024], P('col', 'row'), may hold values from -1.5 to 1.5
- w_fc1: bfloat16 [1024, 4096], P('row', 'col'), may hold values from -0.1875 to 0.1875
- bias_fc1: bfloat16 [4096], P('col'), may hold values from -1.796875 to 1.796875
- w_fc2: bfloat16 [4096, 1024], P('col', 'row'), may hold values from -0.09375 to 0.09375
- bias_out: bfloat16 [2, 1024], replicated, may hold values from -1.796875 to 1.796875
- qkv_down: bfloat16 [8, 16, 1024], replicated, may hold values from -0.1875 to 0.1875
- qkv_up: bfloat16 [8, 16, 3, 1024], replicated, may hold values from -0.75 to 0.75
- proj_down: bfloat16 [8, 16, 1024], replicated, may hold values from -1.5 to 1.5
- proj_up: bfloat16 [8, 16, 1024], replicated, may hold values from -0.75 to 0.75
- fc1_down: bfloat16 [8, 16, 1024], replicated, may hold values from -0.1875 to 0.1875
- fc1_up: bfloat16 [8, 16, 4096], replicated, may hold values from -0.75 to 0.75
- fc2_down: bfloat16 [8, 16, 4096], replicated, may hold values from -0.09375 to 0.09375
- fc2_up: bfloat16 [8, 16, 1024], replicated, may hold values from -0.75 to 0.75
Outputs:
- layer_out: bfloat16 [10240, 1024], P('row', 'col')
- grad_in: bfloat16 [10240, 1024], P('row', 'col')
- grad_qkv_down: float32 [8, 16, 1024], replicated
- grad_qkv_up: float32 [8, 16, 3, 1024], replicated
- grad_proj_down: float32 [8, 16, 1024], replicated
- grad_proj_up: float32 [8, 16, 1024], replicated
- grad_fc1_down: float32 [8, 16, 1024], replicated
- grad_fc1_up: float32 [8, 16, 4096], replicated
- grad_fc2_down: float32 [8, 16, 4096], replicated
- grad_fc2_up: float32 [8, 16, 1024], replicated
All inputs are finite; a program needn't handle non-finite values. No bound on the sum of `keep_mask` on one device may be relied on, other than what follows from the above.
Results may differ from a plain program's by a relative error of at most 0.013.
Values may be sent and summed in bfloat16 or wider, within the bound.
No kernel may reach another device: no remote copies, remote signals or barrier semaphores. Data moves between devices by JAX's collectives and lax.ppermute only.
A program may use at most 192 MiB of HBM per device.

v0:
```python
import jax
import jax.numpy as jnp
from jax import lax
from jax.sharding import PartitionSpec as P

D = 1024
H = 16
HD = 64
FF = 4096
BUF = 64
R = 16
NA = 8
SEQ = 320


highest = lax.Precision.HIGHEST


def norm_parts(values):
    row_mean = jnp.mean(values, axis=-1, keepdims=True)
    centered = values - row_mean
    variance = jnp.mean(centered * centered, axis=-1, keepdims=True)
    inverse = lax.rsqrt(variance + 1e-06)
    return (centered * inverse, inverse)


def norm_back(grad_normed, gain_row, unit_rows, inverse):
    scaled = grad_normed * gain_row
    first_mean = jnp.mean(scaled, axis=-1, keepdims=True)
    second_mean = jnp.mean(scaled * unit_rows, axis=-1, keepdims=True)
    return inverse * (scaled - first_mean - unit_rows * second_mean)


def gelu_slope(pre_gelu):
    cumulative = 0.5 * (1.0 + lax.erf(pre_gelu * 0.7071067811865476))
    return cumulative + pre_gelu * jnp.exp(-0.5 * pre_gelu * pre_gelu) * 0.3989422804014327


def narrow_dot(formula, left_side, right_side):
    return jnp.einsum(formula, left_side, right_side, preferred_element_type=jnp.float32)


def exact_dot(formula, left_side, right_side):
    return jnp.einsum(
        formula, left_side, right_side, precision=highest, preferred_element_type=jnp.float32
    )


def attention_pair(query_heads, key_heads, value_heads, key_open):

    def scores_of():
        raw_scores = narrow_dot("gqhd,gkhd->ghqk", query_heads, key_heads) * 0.125
        return jnp.where(key_open[:, None, None, :], raw_scores, -1e30)

    scores = scores_of()
    top_score = jnp.max(scores, axis=-1, keepdims=True)
    exponent = jnp.exp(scores - top_score)
    row_total = jnp.sum(exponent, axis=-1, keepdims=True)
    log_total = top_score + jnp.log(row_total)
    soft_low = (exponent / row_total).astype(jnp.bfloat16)
    attended = narrow_dot("ghqk,gkhd->gqhd", soft_low, value_heads)

    def backward(grad_heads):
        soft_again = jnp.exp(scores_of() - log_total)
        grad_values = narrow_dot("ghqk,gqhd->gkhd", soft_again.astype(jnp.bfloat16), grad_heads)
        grad_soft = narrow_dot("gqhd,gkhd->ghqk", grad_heads, value_heads)
        grad_scores = (
            soft_again * (grad_soft - jnp.sum(grad_soft * soft_again, axis=-1, keepdims=True))
        ).astype(jnp.bfloat16)
        grad_queries = narrow_dot("ghqk,gkhd->gqhd", grad_scores, key_heads) * 0.125
        grad_keys = narrow_dot("ghqk,gqhd->gkhd", grad_scores, query_heads) * 0.125
        return (grad_queries, grad_keys, grad_values)

    return (attended, backward)


def images_layer(
    x_rows,
    g_rows,
    keep_rows,
    select,
    key_open,
    ln_gain,
    ln_shift,
    w_qkv,
    bias_qv,
    w_proj,
    w_fc1,
    bias_fc1,
    w_fc2,
    bias_out,
    flats,
):
    (
        qkv_down_flat,
        qkv_up_flat,
        proj_down_flat,
        proj_up_flat,
        fc1_down_flat,
        fc1_up_flat,
        fc2_down_flat,
        fc2_up_flat,
    ) = flats
    images = key_open.shape[0]
    tok_rows = images * SEQ
    bias_pair = bias_qv.astype(jnp.float32)
    bias_pair_out = bias_out.astype(jnp.float32)
    hidden = x_rows.astype(jnp.float32)
    unit_one, inverse_one = norm_parts(hidden)
    normed_one = (unit_one * ln_gain[0] + ln_shift[0]).astype(jnp.bfloat16)
    latent_one = narrow_dot("td,rd->tr", normed_one, qkv_down_flat) * select
    projected = narrow_dot("td,cde->cte", normed_one, w_qkv) + exact_dot(
        "tr,rce->cte", latent_one, qkv_up_flat.astype(jnp.float32)
    )
    queries = (projected[0] + bias_pair[0]).astype(jnp.bfloat16)
    key_side = projected[1].astype(jnp.bfloat16)
    value_side = (projected[2] + bias_pair[1]).astype(jnp.bfloat16)
    head_shape = (images, SEQ, H, HD)
    attended_heads, attention_back = attention_pair(
        queries.reshape(head_shape),
        key_side.reshape(head_shape),
        value_side.reshape(head_shape),
        key_open,
    )
    attended = attended_heads.reshape(tok_rows, D).astype(jnp.bfloat16)
    latent_two = narrow_dot("th,rh->tr", attended, proj_down_flat) * select
    branch = (
        narrow_dot("th,hd->td", attended, w_proj)
        + exact_dot("tr,rd->td", latent_two, proj_up_flat.astype(jnp.float32))
        + bias_pair_out[0]
    )
    middle = hidden + branch
    unit_two, inverse_two = norm_parts(middle)
    normed_two = (unit_two * ln_gain[1] + ln_shift[1]).astype(jnp.bfloat16)
    latent_three = narrow_dot("td,rd->tr", normed_two, fc1_down_flat) * select
    pre_gelu = (
        narrow_dot("td,df->tf", normed_two, w_fc1)
        + exact_dot("tr,rf->tf", latent_three, fc1_up_flat.astype(jnp.float32))
        + bias_fc1.astype(jnp.float32)
    )
    activated = jax.nn.gelu(pre_gelu, approximate=False).astype(jnp.bfloat16)
    latent_four = narrow_dot("tf,rf->tr", activated, fc2_down_flat) * select
    result = (
        narrow_dot("tf,fd->td", activated, w_fc2)
        + exact_dot("tr,rd->td", latent_four, fc2_up_flat.astype(jnp.float32))
        + bias_pair_out[1]
    )
    out_rows = (keep_rows * (middle + result)).astype(jnp.bfloat16)
    grad_result = g_rows.astype(jnp.float32) * keep_rows
    grad_result_low = grad_result.astype(jnp.bfloat16)
    grad_latent_four = narrow_dot("td,rd->tr", grad_result_low, fc2_up_flat) * select
    grad_act = narrow_dot("td,fd->tf", grad_result_low, w_fc2) + exact_dot(
        "tr,rf->tf", grad_latent_four, fc2_down_flat.astype(jnp.float32)
    )
    grad_pre = (grad_act * gelu_slope(pre_gelu)).astype(jnp.bfloat16)
    grad_latent_three = narrow_dot("tf,rf->tr", grad_pre, fc1_up_flat) * select
    grad_normed_two = narrow_dot("tf,df->td", grad_pre, w_fc1) + exact_dot(
        "tr,rd->td", grad_latent_three, fc1_down_flat.astype(jnp.float32)
    )
    grad_fc2_up = exact_dot("tr,td->rd", latent_four, grad_result)
    grad_fc2_down = exact_dot("tr,tf->rf", grad_latent_four, activated.astype(jnp.float32))
    grad_fc1_up = exact_dot("tr,tf->rf", latent_three, grad_pre.astype(jnp.float32))
    grad_fc1_down = exact_dot("tr,td->rd", grad_latent_three, normed_two.astype(jnp.float32))
    grad_middle = grad_result + norm_back(grad_normed_two, ln_gain[1], unit_two, inverse_two)
    grad_branch = grad_middle.astype(jnp.bfloat16)
    grad_latent_two = narrow_dot("td,rd->tr", grad_branch, proj_up_flat) * select
    grad_attended = (
        narrow_dot("td,hd->th", grad_branch, w_proj)
        + exact_dot("tr,rh->th", grad_latent_two, proj_down_flat.astype(jnp.float32))
    ).astype(jnp.bfloat16)
    grad_proj_up = exact_dot("tr,td->rd", latent_two, grad_branch.astype(jnp.float32))
    grad_proj_down = exact_dot("tr,th->rh", grad_latent_two, attended.astype(jnp.float32))
    grad_queries, grad_keys, grad_values = attention_back(grad_attended.reshape(head_shape))
    grad_qkv = (
        jnp.stack([grad_queries, grad_keys, grad_values])
        .reshape(3, tok_rows, D)
        .astype(jnp.bfloat16)
    )
    grad_latent_one = narrow_dot("cte,rce->tr", grad_qkv, qkv_up_flat) * select
    grad_normed_one = narrow_dot("cte,cde->td", grad_qkv, w_qkv) + exact_dot(
        "tr,rd->td", grad_latent_one, qkv_down_flat.astype(jnp.float32)
    )
    grad_qkv_up = exact_dot("tr,cte->rce", latent_one, grad_qkv.astype(jnp.float32))
    grad_qkv_down = exact_dot("tr,td->rd", grad_latent_one, normed_one.astype(jnp.float32))
    grad_hidden = grad_middle + norm_back(grad_normed_one, ln_gain[0], unit_one, inverse_one)
    grads = (
        grad_qkv_down,
        grad_qkv_up,
        grad_proj_down,
        grad_proj_up,
        grad_fc1_down,
        grad_fc1_up,
        grad_fc2_down,
        grad_fc2_up,
    )
    return (out_rows, grad_hidden.astype(jnp.bfloat16), grads)


def per_device(
    tokens_in,
    grad_out,
    keep_mask,
    adapter_index,
    ln_gain,
    ln_shift,
    w_qkv,
    bias_qv,
    w_proj,
    w_fc1,
    bias_fc1,
    w_fc2,
    bias_out,
    qkv_down,
    qkv_up,
    proj_down,
    proj_up,
    fc1_down,
    fc1_up,
    fc2_down,
    fc2_up,
):
    columns = lax.axis_size("col")
    column = lax.axis_index("col")
    images = adapter_index.shape[0]
    tok_rows = images * SEQ
    rank_total = NA * R
    keep_full = jnp.concatenate([jnp.ones((images, BUF), jnp.int32), keep_mask], axis=1)
    key_open = keep_full > 0
    keep_rows = keep_full.reshape(tok_rows, 1).astype(jnp.float32)
    owner_rows = jnp.broadcast_to(adapter_index[:, None], (images, SEQ)).reshape(tok_rows, 1)
    select = (owner_rows == lax.broadcasted_iota(jnp.int32, (1, rank_total), 1) // R).astype(
        jnp.float32
    )
    flats = (
        qkv_down.reshape(rank_total, D),
        qkv_up.reshape(rank_total, 3, D),
        proj_down.reshape(rank_total, D),
        proj_up.reshape(rank_total, D),
        fc1_down.reshape(rank_total, D),
        fc1_up.reshape(rank_total, FF),
        fc2_down.reshape(rank_total, FF),
        fc2_up.reshape(rank_total, D),
    )
    qkv_cols, proj_rows, fc1_cols, fc2_rows = (
        lax.all_gather(w_qkv, "row", axis=1, tiled=True),
        lax.all_gather(w_proj, "row", axis=1, tiled=True),
        lax.all_gather(w_fc1, "row", axis=0, tiled=True),
        lax.all_gather(w_fc2, "row", axis=1, tiled=True),
    )
    qkv_full, proj_full, fc1_full, fc2_full, bias_qv_full, bias_fc1_full = (
        lax.all_gather(qkv_cols, "col", axis=2, tiled=True),
        lax.all_gather(proj_rows, "col", axis=0, tiled=True),
        lax.all_gather(fc1_cols, "col", axis=1, tiled=True),
        lax.all_gather(fc2_rows, "col", axis=0, tiled=True),
        lax.all_gather(bias_qv, "col", axis=1, tiled=True),
        lax.all_gather(bias_fc1, "col", axis=0, tiled=True),
    )
    x_rows, g_rows = (
        lax.all_to_all(tokens_in, "col", split_axis=0, concat_axis=1, tiled=True),
        lax.all_to_all(grad_out, "col", split_axis=0, concat_axis=1, tiled=True),
    )
    local_images = images // columns
    slice_rows = local_images * SEQ
    row_start = column * slice_rows
    out_rows, grad_rows, grads = images_layer(
        x_rows,
        g_rows,
        lax.dynamic_slice_in_dim(keep_rows, row_start, slice_rows, 0),
        lax.dynamic_slice_in_dim(select, row_start, slice_rows, 0),
        lax.dynamic_slice_in_dim(key_open, column * local_images, local_images, 0),
        ln_gain,
        ln_shift,
        qkv_full,
        bias_qv_full,
        proj_full,
        fc1_full,
        bias_fc1_full,
        fc2_full,
        bias_out,
        flats,
    )
    layer_out, grad_in = (
        lax.all_to_all(out_rows, "col", split_axis=1, concat_axis=0, tiled=True),
        lax.all_to_all(grad_rows, "col", split_axis=1, concat_axis=0, tiled=True),
    )
    summed = lax.psum(
        (grads[0], grads[1], grads[2], grads[3], grads[4], grads[5], grads[6], grads[7]),
        ("row", "col"),
    )
    return (
        layer_out,
        grad_in,
        summed[0].reshape(NA, R, D),
        summed[1].reshape(NA, R, 3, D),
        summed[2].reshape(NA, R, D),
        summed[3].reshape(NA, R, D),
        summed[4].reshape(NA, R, D),
        summed[5].reshape(NA, R, FF),
        summed[6].reshape(NA, R, FF),
        summed[7].reshape(NA, R, D),
    )


def solution(mesh):
    return jax.shard_map(
        per_device,
        mesh=mesh,
        in_specs=(
            P("row", "col"),
            P("row", "col"),
            P("row", None),
            P("row"),
            P(),
            P(),
            P(None, "row", "col"),
            P(None, "col"),
            P("col", "row"),
            P("row", "col"),
            P("col"),
            P("col", "row"),
            P(),
            P(),
            P(),
            P(),
            P(),
            P(),
            P(),
            P(),
            P(),
        ),
        out_specs=(P("row", "col"), P("row", "col"), P(), P(), P(), P(), P(), P(), P(), P()),
        check_vma=False,
    )
```

profile of v0, /device:TPU:0, one launch (start us, length us, event | category | flops | bytes accessed | tf_op | source)
XLA Modules:
  0.0 625.2 jit_solution(14303194922403295950)
XLA Ops:
  9.5 47.7 %all-gather.8.cloned.1.call-done = bf16[3,1024,256]{2,1,0:T(8,128)(2,1)} async-done(((bf16[3,128,256]{2,1,0:T(8,128)(2,1)}), bf16[3,1024,256]{2,1,0:T(8,128)(2,1)}) %all-gather.8.cloned.1.call-update) | async-done | bytes 1572880 | tf_op jit(solution)/shard_map/all_gather | solution.py:245
  57.3 31.2 %all_gather.33 = bf16[256,1024]{1,0:T(8,128)(2,1)} all-gather(bf16[256,128]{1,0:T(8,128)(2,1)} %param.29), channel_id=1, replica_groups=mesh['row'=8,'col'=4] {'row'}, dimensions={1}, use_global_device_ids=true | all-gather | bytes 589824 | tf_op jit(solution)/shard_map/all_gather | solution.py:246
  88.6 22.1 %all-gather.14.cloned.1.call-done = bf16[1024,1024]{1,0:T(8,128)(2,1)} async-done(((bf16[128,1024]{1,0:T(8,128)(2,1)}), bf16[1024,1024]{1,0:T(8,128)(2,1)}) %all-gather.14.cloned.1.call-update) | async-done | bytes 2097168 | tf_op jit(solution)/shard_map/all_gather | solution.py:247
  110.8 3.5 all-to-all-start
  114.3 11.0 %all_gather.32 = bf16[2,1024]{1,0:T(2,128)(2,1)S(1)} all-gather(bf16[2,256]{1,0:T(2,128)(2,1)S(1)} %copy-done.61), channel_id=1, replica_groups=mesh['row'=8,'col'=4] {'col'}, dimensions={1}, use_global_device_ids=true | all-gather | bytes 5120 | tf_op jit(solution)/shard_map/all_gather | solution.py:255
  125.7 5.2 all_gather.37
  131.1 0.9 copy.85
  132.3 30.0 %all-gather.18.cloned.1.call-done = bf16[1024,1024]{1,0:T(8,128)(2,1)} async-done(((bf16[1024,128]{1,0:T(8,128)(2,1)}), bf16[1024,1024]{1,0:T(8,128)(2,1)}) %all-gather.18.cloned.1.call-update) | async-done | bytes 2097168 | tf_op jit(solution)/shard_map/all_gather | solution.py:248
  163.0 3.5 all-to-all-start.2
  168.6 12.2 %all-to-all-done.2 = bf16[4,320,256]{2,1,0:T(8,128)(2,1)S(1)} async-done(((bf16[4,320,256]{2,1,0:T(8,128)(2,1)}), bf16[4,320,256]{2,1,0:T(8,128)(2,1)S(1)}, u32[]{:S(2)}, u32[]{:S(2)}) %all-to-all-start.2) | async-done | bytes 655392 | tf_op jit(solution)/shard_map/all_to_all | solution.py:260
  181.2 1.3 copy.110
  182.9 1.0 convolution_multiply_fusion.1
  184.2 28.8 %all-gather.10.cloned.1.call-done = bf16[3,1024,1024]{2,1,0:T(8,128)(2,1)} async-done(((bf16[3,1024,256]{2,1,0:T(8,128)(2,1)}), bf16[3,1024,1024]{2,1,0:T(8,128)(2,1)}) %all-gather.10.cloned.1.call-update) | async-done | bytes 6291472 | tf_op jit(solution)/shard_map/all_gather | solution.py:251
  213.0 5.0 fusion.50
  218.0 1.7 add_bitcast_fusion
  219.7 1.9 copy-done.7
  222.1 3.3 fusion.63
  225.4 1.6 copy.86
  227.0 1.8 copy.87
  228.8 2.1 fusion.67
  231.0 1.2 fusion
  232.2 2.0 copy-done.1
  234.2 2.3 fusion.32
  236.9 2.4 fusion.69
  239.3 2.3 fusion.68
  243.4 50.6 %all-gather.16.cloned.1.call-done = bf16[1024,4096]{1,0:T(8,128)(2,1)} async-done(((bf16[1024,1024]{1,0:T(8,128)(2,1)}), bf16[1024,4096]{1,0:T(8,128)(2,1)}) %all-gather.16.cloned.1.call-update) | async-done | bytes 8388624 | tf_op jit(solution)/shard_map/all_gather | solution.py:253
  294.0 5.4 fusion.70
  299.5 15.6 %fusion.7 = (bf16[320,4096]{1,0:T(8,128)(2,1)}, f32[320,4096]{1,0:T(8,128)}) fusion(f32[4096]{0:T(1024)S(1)} %convert_element_type.177, f32[320,4096]{1,0:T(8,128)S(1)} %fusion.70, f32[320,128]{1,0:T(8,128)S(1)} %convolution_multiply_fusion.2, bf16[128,4096]{1,0:T(8,128)(2,1)S(1)} %bitcast.152), kind=kOutput, calls=%fused_computation.17 | convolution fusion | flops 2101084160 | bytes 14336000 | tf_op jit(solution)/shard_map/tr,rf->tf/dot_general | solution.py:44
  315.1 38.8 %all-gather.20.cloned.1.call-done = bf16[4096,1024]{1,0:T(8,128)(2,1)} async-done(((bf16[1024,1024]{1,0:T(8,128)(2,1)}), bf16[4096,1024]{1,0:T(8,128)(2,1)}) %all-gather.20.cloned.1.call-update) | async-done | bytes 8388624 | tf_op jit(solution)/shard_map/all_gather | solution.py:254
  353.9 5.9 fusion.47
  359.8 4.8 fusion.4
  365.5 3.2 fusion.76
  369.5 3.2 fusion.77
  372.7 1.4 fusion.75
  374.1 2.9 fusion.72
  377.0 1.1 fusion.62
  379.6 1.4 fusion.55
  381.0 1.8 fusion.74
  383.8 1.8 fusion.37
  385.5 1.4 copy.93
  387.0 5.6 fusion.33
  392.6 6.2 multiply_reduce_fusion
  398.9 7.1 %multiply_convert_fusion = bf16[16,320,320]{1,2,0:T(8,128)(2,1)S(1)} fusion(f32[16,320,320]{1,2,0:T(8,128)} %get-tuple-element.42, f32[16,320,320]{1,2,0:T(8,128)} %copy-done.1, f32[16,320]{1,0:T(8,128)S(1)} %get-tuple-element.41, f32[16,320]{1,0:T(8,128)S(1)} %log_add_fusion), kind=kLoop, calls=%fused_computation | loop fusion | flops 6553600 | bytes 16424960 | tf_op jit(solution)/shard_map/convert_element_type | solution.py:69
  406.0 3.7 multiply_convert_fusion.1
  409.7 1.7 multiply_convert_fusion.2
  411.4 2.3 copy.99
  413.7 2.3 copy.97
  416.0 2.2 copy.98
  418.2 2.3 fusion.45
  420.6 1.4 fusion.60
  422.1 2.0 fusion.43
  424.0 1.4 fusion.73
  425.4 1.2 copy.101
  426.7 6.4 %fusion.71 = f32[320,1024]{1,0:T(8,128)S(1)} fusion(bf16[320,4096]{1,0:T(8,128)(2,1)} %get-tuple-element.38, bf16[4096,1024]{1,0:T(8,128)(2,1)} %all-gather.20.cloned.1.call-done), kind=kOutput, calls=%fused_computation.145 | convolution fusion | flops 2684354560 | bytes 12320768 | tf_op jit(solution)/shard_map/tf,fd->td/dot_general | solution.py:40
  434.9 3.5 all-to-all-start.1
  438.5 5.5 convolution_bitcast_fusion
  444.0 1.1 fusion.61
  446.6 8.7 %all-to-all-done.1 = bf16[320,4,256]{2,0,1:T(8,128)(2,1)S(1)} async-done(((bf16[320,4,256]{2,0,1:T(8,128)(2,1)}), bf16[320,4,256]{2,0,1:T(8,128)(2,1)S(1)}, u32[]{:S(2)}, u32[]{:S(2)}) %all-to-all-start.1) | async-done | bytes 655392 | tf_op jit(solution)/shard_map/all_to_all | solution.py:283
  455.3 3.5 all-to-all-start.3
  458.8 10.2 %all-to-all-done.3 = bf16[320,4,256]{2,0,1:T(8,128)(2,1)S(1)} async-done(((bf16[320,4,256]{2,0,1:T(8,128)(2,1)}), bf16[320,4,256]{2,0,1:T(8,128)(2,1)S(1)}, u32[]{:S(2)}, u32[]{:S(2)}) %all-to-all-start.3) | async-done | bytes 655392 | tf_op jit(solution)/shard_map/all_to_all | solution.py:284
  469.0 139.4 %all-reduce.4.cloned.1.call-done = (f32[8,16,1024]{2,1,0:T(8,128)}, f32[8,16,3,1024]{3,1,2,0:T(8,128)}, f32[8,16,1024]{2,1,0:T(8,128)}, f32[8,16,1024]{2,1,0:T(8...) async-done(((f32[8,16,1024]{2,1,0:T(8,128)}, f32[8,16,3,1024]{3,1,2,0:T(8,128)}, ...) | async-done | bytes 8388624 | tf_op jit(solution)/shard_map/psum | solution.py:286
  610.9 1.1 copy.129
  614.4 1.3 copy.133
  615.7 1.3 copy.134
  (210 shorter events, 22.8 us)
Async XLA Ops:
  7.2 292.3 %copy-start = (bf16[8,16,4096]{2,1,0:T(8,128)(2,1)S(1)}, bf16[8,16,4096]{2,1,0:T(8,128)(2,1)}, u32[]{:S(2)}) copy-start(bf16[8,16,4096]{2,1,0:T(8,128)(2,1)} %param.39) | copy-start | bytes 3145732
  7.2 49.9 %all-gather.8.cloned.1.call-start = ((), (), s32[]{:S(2)}) async-start(), calls=%async_computation.4 | async-start | bytes 1769472 | tf_op jit(solution)/shard_map/all_gather | solution.py:245
  7.9 102.8 %all-gather.14.cloned.1.call-start = ((), (), s32[]{:S(2)}) async-start(), calls=%async_computation.7 | async-start | bytes 2359296 | tf_op jit(solution)/shard_map/all_gather | solution.py:247
  8.7 153.7 %all-gather.18.cloned.1.call-start = ((), (), s32[]{:S(2)}) async-start(), calls=%async_computation.9 | async-start | bytes 2359296 | tf_op jit(solution)/shard_map/all_gather | solution.py:248
  9.4 203.6 %all-gather.10.cloned.1.call-start = ((), (), s32[]{:S(2)}) async-start(), calls=%async_computation.5 | async-start | bytes 7864320 | tf_op jit(solution)/shard_map/all_gather | solution.py:251
  57.2 57.2 %copy-start.61 = (bf16[2,256]{1,0:T(2,128)(2,1)S(1)}, bf16[2,256]{1,0:T(2,128)(2,1)}, u32[]{:S(2)}) copy-start(bf16[2,256]{1,0:T(2,128)(2,1)} %param.28) | copy-start | bytes 3076
  57.2 68.2 %copy-start.62 = (s32[4]{0:T(128)S(1)}, s32[4]{0:T(128)}, u32[]{:S(2)}) copy-start(s32[4]{0:T(128)} %param.24) | copy-start | bytes 52
  57.2 68.4 %copy-start.55 = (s32[4,256]{1,0:T(4,128)S(1)}, s32[4,256]{1,0:T(4,128)}, u32[]{:S(2)}) copy-start(s32[4,256]{1,0:T(4,128)} %param.23) | copy-start | bytes 12292
  57.2 68.5 %copy-start.60 = (bf16[1024]{0:T(1024)(128)(2,1)S(1)}, bf16[1024]{0:T(1024)(128)(2,1)}, u32[]{:S(2)}) copy-start(bf16[1024]{0:T(1024)(128)(2,1)} %param.31) | copy-start | bytes 6148
  57.2 73.7 %copy-start.59 = (f32[2,1024]{1,0:T(2,128)S(1)}, f32[2,1024]{1,0:T(2,128)}, u32[]{:S(2)}) copy-start(f32[2,1024]{1,0:T(2,128)} %param.25) | copy-start | bytes 24580
  57.2 73.8 %copy-start.58 = (f32[2,1024]{1,0:T(2,128)S(1)}, f32[2,1024]{1,0:T(2,128)}, u32[]{:S(2)}) copy-start(f32[2,1024]{1,0:T(2,128)} %param.26) | copy-start | bytes 24580
  57.2 73.9 %copy-start.35 = (bf16[8,16,3,1024]{3,1,2,0:T(8,128)(2,1)S(1)}, bf16[8,16,3,1024]{3,1,2,0:T(8,128)(2,1)}, u32[]{:S(2)}) copy-start(bf16[8,16,3,1024]{3,1,2,0:T(8,128)(2,1)} %param.35) | copy-start | bytes 2359300
  57.2 179.6 %all-gather.12.cloned.1.call-start = ((), (), s32[]{:S(2)}) async-start(), calls=%async_computation.6 | async-start | bytes 2621440 | tf_op jit(solution)/shard_map/all_gather | solution.py:252
  88.5 205.5 %all-gather.16.cloned.1.call-start = ((), (), s32[]{:S(2)}) async-start(), calls=%async_computation.8 | async-start | bytes 10485760 | tf_op jit(solution)/shard_map/all_gather | solution.py:253
  110.8 51.6 %copy-start.56 = (bf16[2,1024]{1,0:T(2,128)(2,1)S(1)}, bf16[2,1024]{1,0:T(2,128)(2,1)}, u32[]{:S(2)}) copy-start(bf16[2,1024]{1,0:T(2,128)(2,1)} %param.33) | copy-start | bytes 12292
  110.8 52.2 %all-to-all-start = ((bf16[4,320,256]{2,1,0:T(8,128)(2,1)}), bf16[4,320,256]{2,1,0:T(8,128)(2,1)S(1)}, u32[]{:S(2)}, u32[]{:S(2)}) async-start(bf16[4,320,256]{2,1,0:T(8,128)(2,1)} %bitcast), calls=%async_computation | async-start | bytes 1310720 | tf_op jit(solution)/shard_map/all_to_all | solution.py:259
  114.3 239.6 %all-gather.20.cloned.1.call-start = ((), (), s32[]{:S(2)}) async-start(), calls=%async_computation.10 | async-start | bytes 10485760 | tf_op jit(solution)/shard_map/all_gather | solution.py:254
  130.9 53.0 %copy-start.53 = (f32[1,1024]{1,0:T(1,128)}, f32[1,1024]{1,0:T(1,128)S(1)}, u32[]{:S(2)}) copy-start(f32[1,1024]{1,0:T(1,128)S(1)} %get-tuple-element.44) | copy-start | bytes 12292
  163.0 17.8 %all-to-all-start.2 = ((bf16[4,320,256]{2,1,0:T(8,128)(2,1)}), bf16[4,320,256]{2,1,0:T(8,128)(2,1)S(1)}, u32[]{:S(2)}, u32[]{:S(2)}) async-start(bf16[4,320,256]{2,1,0:T(8,128)(2,1)} %bitcast.201), calls=%async_computation.2 | async-start | bytes 1310720 | tf_op jit(solution)/shard_map/all_to_all | solution.py:260
  166.5 441.9 %all-reduce.4.cloned.1.call-start = ((), (), s32[]{:S(2)}) async-start(), calls=%async_computation.11 | async-start | bytes 16777216 | tf_op jit(solution)/shard_map/psum | solution.py:286
  166.7 17.1 %copy-start.49 = (f32[320]{0:T(512)}, f32[320]{0:T(512)S(1)}, u32[]{:S(2)}) copy-start(f32[320]{0:T(512)S(1)} %broadcast_multiply_fusion.5) | copy-start | bytes 3844
  167.1 16.8 %copy-start.51 = (f32[320]{0:T(512)}, f32[320]{0:T(512)S(1)}, u32[]{:S(2)}) copy-start(f32[320]{0:T(512)S(1)} %add_rsqrt_fusion.1) | copy-start | bytes 3844
  168.6 15.2 %copy-start.2 = (f32[4,40,8,256]{3,2,0,1:T(8,128)}, f32[4,40,8,256]{3,2,0,1:T(8,128)S(1)}, u32[]{:S(2)}) copy-start(f32[4,40,8,256]{3,2,0,1:T(8,128)S(1)} %copy.108) | copy-start | bytes 3932164
  182.8 35.1 %copy-start.42 = (f32[320,128,1]{1,0,2:T(8,128)}, f32[320,128,1]{1,0,2:T(8,128)S(1)}, u32[]{:S(2)}) copy-start(f32[320,128,1]{1,0,2:T(8,128)S(1)} %fusion.46) | copy-start | bytes 491524
  184.2 33.8 %copy-start.21 = (bf16[320,1024]{1,0:T(8,128)(2,1)}, bf16[320,1024]{1,0:T(8,128)(2,1)S(1)}, u32[]{:S(2)}) copy-start(bf16[320,1024]{1,0:T(8,128)(2,1)S(1)} %add_convert_fusion.4) | copy-start | bytes 1966084
  184.2 33.8 %copy-start.17 = (bf16[8,16,3,1024]{3,1,0,2:T(8,128)(2,1)S(1)}, bf16[8,16,3,1024]{3,1,0,2:T(8,128)(2,1)}, u32[]{:S(2)}) copy-start(bf16[8,16,3,1024]{3,1,0,2:T(8,128)(2,1)} %copy.85) | copy-start | bytes 2359300
  222.1 6.7 %copy-start.11 = (bf16[1,320,1024]{1,2,0:T(8,128)(2,1)}, bf16[1,320,1024]{1,2,0:T(8,128)(2,1)S(1)}, u32[]{:S(2)}) copy-start(bf16[1,320,1024]{1,2,0:T(8,128)(2,1)S(1)} %copy.88) | copy-start | bytes 1966084
  231.0 3.2 copy-start.1
  231.0 3.2 copy-start.13
  234.2 2.3 copy-start.29
  353.9 5.9 copy-start.36
  353.9 5.9 copy-start.63
  353.9 5.9 copy-start.64
  364.6 9.5 %slice-start = ((s8[8388608]{0:T(1024)(128)(4,1)}), s8[4194304]{0:T(1024)(128)(4,1)S(1)}, s32[]{:S(2)}) async-start(s8[8388608]{0:T(1024)(128)(4,1)} %bitcast.210), calls=%async_computation.12 | async-start | bytes 8388608
  365.5 3.2 copy-start.19
  368.7 5.4 slice-start.1
  369.5 3.2 copy-start.16
  374.1 2.9 copy-start.28
  379.3 4.4 copy-start.4
  379.3 3.5 copy-start.10
  387.0 5.6 copy-start.14
  406.0 3.7 copy-start.12
  411.4 6.8 %copy-start.18 = (bf16[8,16,3,1024]{3,1,0,2:T(8,128)(2,1)S(1)}, bf16[8,16,3,1024]{3,1,0,2:T(8,128)(2,1)}, u32[]{:S(2)}) copy-start(bf16[8,16,3,1024]{3,1,0,2:T(8,128)(2,1)} %copy.85) | copy-start | bytes 2359300
  418.2 2.3 copy-start.37
  418.2 2.3 copy-start.39
  418.2 2.3 copy-start.41
  418.2 2.4 copy-start.43
  420.6 3.4 copy-start.22
  426.7 6.4 %copy-start.32 = (bf16[8,16,1024]{2,1,0:T(8,128)(2,1)S(1)}, bf16[8,16,1024]{2,1,0:T(8,128)(2,1)}, u32[]{:S(2)}) copy-start(bf16[8,16,1024]{2,1,0:T(8,128)(2,1)} %param.41) | copy-start | bytes 786436
  426.7 6.4 %copy-start.57 = (f32[1,1024]{1,0:T(1,128)S(1)}, f32[1,1024]{1,0:T(1,128)}, u32[]{:S(2)}) copy-start(f32[1,1024]{1,0:T(1,128)} %get-tuple-element.32) | copy-start | bytes 12292
  433.1 5.2 copy-start.38
  434.0 4.4 copy-start.40
  434.9 20.4 %all-to-all-start.1 = ((bf16[320,4,256]{2,0,1:T(8,128)(2,1)}), bf16[320,4,256]{2,0,1:T(8,128)(2,1)S(1)}, u32[]{:S(2)}, u32[]{:S(2)}) async-start(bf16[320,4,256]{2,0,1:T(8,128)(2,1)} %bitcast.151), calls=%async_computation.1 | async-start | bytes 1310720 | tf_op jit(solution)/shard_map/all_to_all | solution.py:283
  438.4 5.5 copy-start.3
  438.4 5.5 copy-start.34
  438.4 5.5 copy-start.50
  438.4 5.5 copy-start.52
  438.4 5.5 copy-start.54
  455.3 13.7 %all-to-all-start.3 = ((bf16[320,4,256]{2,0,1:T(8,128)(2,1)}), bf16[320,4,256]{2,0,1:T(8,128)(2,1)S(1)}, u32[]{:S(2)}, u32[]{:S(2)}) async-start(bf16[320,4,256]{2,0,1:T(8,128)(2,1)} %bitcast.150), calls=%async_computation.3 | async-start | bytes 1310720 | tf_op jit(solution)/shard_map/all_to_all | solution.py:284
  608.4 2.5 copy-start.25
  609.2 2.8 copy-start.47
  610.1 2.7 copy-start.46
  610.9 2.7 copy-start.45
  610.9 3.5 copy-start.24
  (15 other events, 22.2 us)
Sparse Core Ops, SparseCore 0:
  10.2 46.8 all-gather.7
  59.3 51.4 all-gather.13
  112.8 49.5 all-gather.17
  163.8 49.1 all-gather.9
  214.4 19.8 all-gather.11
  235.7 58.3 all-gather.15
  295.6 58.2 all-gather.19
  426.8 181.5 all-reduce.3
where the time goes:
time: 635 us; the launch traced here: 625 us
  waiting for transfers between devices  391 us (62%)
  matrix products  107 us (17%)
  blocking collectives  47.4 us (7%)
  local copies, waits for them, and re-layouts  38.4 us (6%)
  between operations  15.6 us (2%)
  starting transfers between devices  14.3 us (2%)
  other arithmetic  11.5 us (2%)
    psum x1, waiting for transfers between devices, per_device(): lax.psum((grads[0], grads[1], grads[2], grads[3], grads[4], grads[5], gra...  139 us
    dot_general x22, matrix products, narrow_dot(): jnp.einsum(formula, left_side, right_side, preferred_element_type=jnp.flo...  62.5 us
    all_gather x1, waiting for transfers between devices, per_device(): lax.all_gather(fc1_cols, 'col', axis=1, tiled=True)  50.6 us
    all_gather x1, waiting for transfers between devices, per_device(): lax.all_gather(w_qkv, 'row', axis=1, tiled=True)  47.7 us
    dot_general x16, matrix products, exact_dot(): jnp.einsum(formula, left_side, right_side, precision=highest, preferred_e...  45 us
    all_gather x1, waiting for transfers between devices, per_device(): lax.all_gather(fc2_rows, 'col', axis=0, tiled=True)  38.8 us
    all_gather x1, blocking collectives, per_device(): lax.all_gather(w_proj, 'row', axis=1, tiled=True)  31.2 us
    all_gather x1, waiting for transfers between devices, per_device(): lax.all_gather(w_fc2, 'row', axis=1, tiled=True)  30 us
  transfers between devices with their start and end apart: 12, of which 10 were waited for; matrix products, arithmetic and copies ran while one was open for 11% of the time, Pallas kernels for 0%

commit v1 on v0

v1 whole, which is shorter than its diff:
```python
import jax
import jax.numpy as jnp
from jax import lax
from jax.sharding import PartitionSpec as P

D = 1024
H = 16
HD = 64
FF = 4096
BUF = 64
R = 16
NA = 8
SEQ = 320
BF = jnp.bfloat16
F32 = jnp.float32
BOTH = ("row", "col")


def norm_parts(values):
    row_mean = jnp.mean(values, axis=-1, keepdims=True)
    centered = values - row_mean
    variance = jnp.mean(centered * centered, axis=-1, keepdims=True)
    inverse = lax.rsqrt(variance + 1e-06)
    return (centered * inverse, inverse)


def norm_back(grad_normed, gain_row, unit_rows, inverse):
    scaled = grad_normed * gain_row
    first_mean = jnp.mean(scaled, axis=-1, keepdims=True)
    second_mean = jnp.mean(scaled * unit_rows, axis=-1, keepdims=True)
    return inverse * (scaled - first_mean - unit_rows * second_mean)


def gelu_slope(pre_gelu):
    cumulative = 0.5 * (1.0 + lax.erf(pre_gelu * 0.7071067811865476))
    return cumulative + pre_gelu * jnp.exp(-0.5 * pre_gelu * pre_gelu) * 0.3989422804014327


def dot(formula, left_side, right_side):
    return jnp.einsum(formula, left_side, right_side, preferred_element_type=F32)


def low(values):
    return values.astype(BF)


def exchange(block, axis, bit, rows, cols):
    stride = (1 << bit) * (cols if axis == "row" else 1)
    pairs = [(i, i ^ stride) for i in range(rows * cols)]
    return lax.ppermute(block, BOTH, pairs)


def joined(block, axis, bit, rows, cols, index, dim):
    other = exchange(block, axis, bit, rows, cols)
    is_high = ((index >> bit) & 1) == 1
    first = jnp.where(is_high, other, block)
    second = jnp.where(is_high, block, other)
    return jnp.stack([first, second], axis=dim)


def gather_blocks(shard, col_first):
    rows, cols = lax.axis_size("row"), lax.axis_size("col")
    row_bits = rows.bit_length() - 1
    col_bits = cols.bit_length() - 1
    row_index = lax.axis_index("row")
    order = [("row", b) for b in range(row_bits - 1, -1, -1)]
    wide = [("col", b) for b in range(col_bits - 1, 0, -1)]
    if col_first:
        order = order[:-1] + wide + order[-1:]
    else:
        order = order + wide
    order = order + [("col", 0)]
    held = [(0, shard)]
    depth = 0
    for axis, bit in order:
        if axis == "row":
            held = [
                (j, joined(block, axis, bit, rows, cols, row_index, depth)) for j, block in held
            ]
            depth += 1
            if bit == 0:
                held = [(j, block.reshape(-1, shard.shape[-1])) for j, block in held]
        else:
            held = held + [
                (j ^ (1 << bit), exchange(block, axis, bit, rows, cols)) for j, block in held
            ]
    return [block for _, block in sorted(held, key=lambda pair: pair[0])]


def gather_leading(block):
    rows, cols = lax.axis_size("row"), lax.axis_size("col")
    row_index, col_index = lax.axis_index("row"), lax.axis_index("col")
    depth = 0
    for axis, size, index in (("row", rows, row_index), ("col", cols, col_index)):
        for bit in range(size.bit_length() - 2, -1, -1):
            block = joined(block, axis, bit, rows, cols, index, depth)
            depth += 1
    return block.reshape((rows * cols,) + block.shape[depth:])


def sum_adapters(grads, owners):
    rows, cols = lax.axis_size("row"), lax.axis_size("col")
    devices = rows * cols
    width = grads.shape[-1]
    part = width // devices
    pieces = grads.reshape(R, devices, part).transpose(1, 0, 2)
    mine = lax.all_to_all(pieces, BOTH, split_axis=0, concat_axis=0, tiled=True)
    hot = (lax.broadcasted_iota(jnp.int32, (NA, devices), 0) == owners[None, :]).astype(BF)
    summed = low(dot("ad,drp->arp", hot, mine))
    whole = gather_leading(summed)
    return whole.transpose(1, 2, 0, 3).reshape(NA, R, width).astype(F32)


def place(parts, col_index):
    cols = len(parts)
    stacked = jnp.stack(parts, axis=-2)
    index = jnp.arange(cols)
    one_hot = (index[:, None] == (index[None, :] ^ col_index)).astype(stacked.dtype)
    picked = [
        sum(stacked[..., j, :] * one_hot[i, j] for j in range(cols)) for i in range(cols)
    ]
    return jnp.concatenate(picked, axis=-1)


def attention_pair(query_heads, key_heads, value_heads, key_open):
    def scores_of():
        raw_scores = dot("qhd,khd->hqk", query_heads, key_heads) * 0.125
        return jnp.where(key_open[None, None, :], raw_scores, -1e30)

    scores = scores_of()
    top_score = jnp.max(scores, axis=-1, keepdims=True)
    exponent = jnp.exp(scores - top_score)
    row_total = jnp.sum(exponent, axis=-1, keepdims=True)
    log_total = top_score + jnp.log(row_total)
    soft_low = (exponent / row_total).astype(BF)
    attended = dot("hqk,khd->qhd", soft_low, value_heads)

    def backward(grad_heads):
        soft_again = jnp.exp(scores_of() - log_total)
        grad_values = dot("hqk,qhd->khd", soft_again.astype(BF), grad_heads)
        grad_soft = dot("qhd,khd->hqk", grad_heads, value_heads)
        grad_scores = (
            soft_again * (grad_soft - jnp.sum(grad_soft * soft_again, axis=-1, keepdims=True))
        ).astype(BF)
        grad_queries = dot("hqk,khd->qhd", grad_scores, key_heads) * 0.125
        grad_keys = dot("hqk,qhd->khd", grad_scores, query_heads) * 0.125
        return (grad_queries, grad_keys, grad_values)

    return (attended, backward)


def per_device(
    tokens_in,
    grad_out,
    keep_mask,
    adapter_index,
    ln_gain,
    ln_shift,
    w_qkv,
    bias_qv,
    w_proj,
    w_fc1,
    bias_fc1,
    w_fc2,
    bias_out,
    qkv_down,
    qkv_up,
    proj_down,
    proj_up,
    fc1_down,
    fc1_up,
    fc2_down,
    fc2_up,
):
    rows, cols = lax.axis_size("row"), lax.axis_size("col")
    column = lax.axis_index("col")
    assert adapter_index.shape[0] == cols
    hid = D // cols
    ffn = FF // cols

    x_rows = lax.all_to_all(tokens_in, "col", split_axis=0, concat_axis=1, tiled=True)
    g_rows = lax.all_to_all(grad_out, "col", split_axis=0, concat_axis=1, tiled=True)

    shard_q = jnp.concatenate([w_qkv[0], w_qkv[1], w_qkv[2], w_proj.T], axis=1)
    w_q = gather_blocks(shard_q, True)
    w_1 = gather_blocks(w_fc1, False)
    w_2 = gather_blocks(w_fc2.T, True)
    bias_all = lax.all_gather(
        jnp.concatenate([bias_qv.reshape(-1), bias_fc1]), "col", axis=0, tiled=False
    )
    owners = lax.all_gather(adapter_index, "row", axis=0, tiled=True)

    mask_row = lax.dynamic_index_in_dim(keep_mask, column, 0, keepdims=False)
    keep_full = jnp.concatenate([jnp.ones((BUF,), jnp.int32), mask_row])
    key_open = keep_full > 0
    keep_rows = keep_full.reshape(SEQ, 1).astype(F32)
    adapter = lax.dynamic_index_in_dim(adapter_index, column, 0, keepdims=False)

    def mine(table):
        return lax.dynamic_index_in_dim(table, adapter, 0, keepdims=False)

    def block(table, j, width):
        return lax.dynamic_slice_in_dim(table, (column ^ j) * width, width, table.ndim - 1)

    qkv_down, qkv_up, proj_down, proj_up = mine(qkv_down), mine(qkv_up), mine(proj_down), mine(proj_up)
    fc1_down, fc1_up, fc2_down, fc2_up = mine(fc1_down), mine(fc1_up), mine(fc2_down), mine(fc2_up)
    bias_out = bias_out.astype(F32)

    def bias_of(j):
        return lax.dynamic_index_in_dim(bias_all, column ^ j, 0, keepdims=False).astype(F32)

    hidden = x_rows.astype(F32)
    unit_one, inverse_one = norm_parts(hidden)
    normed_one = low(unit_one * ln_gain[0] + ln_shift[0])
    latent_one = low(dot("td,rd->tr", normed_one, qkv_down))
    q_parts, k_parts, v_parts = [], [], []
    for j in range(cols):
        up = block(qkv_up, j, hid).reshape(R, 3 * hid)
        made = dot("td,de->te", normed_one, w_q[j][:, : 3 * hid]) + dot("tr,re->te", latent_one, up)
        bias = bias_of(j)
        q_parts.append(low(made[:, :hid] + bias[:hid]))
        k_parts.append(low(made[:, hid : 2 * hid]))
        v_parts.append(low(made[:, 2 * hid :] + bias[hid : 2 * hid]))
    heads = (SEQ, H, HD)
    q_all, k_all, v_all = (jnp.concatenate(p, axis=1) for p in (q_parts, k_parts, v_parts))
    attended_heads, attention_back = attention_pair(
        q_all.reshape(heads), k_all.reshape(heads), v_all.reshape(heads), key_open
    )
    attended = low(attended_heads.reshape(SEQ, D))
    proj_down_rel = jnp.concatenate([block(proj_down, j, hid) for j in range(cols)], axis=1)
    latent_two = low(dot("th,rh->tr", attended, proj_down_rel))
    branch = dot("tr,rd->td", latent_two, proj_up) + bias_out[0]
    for j in range(cols):
        branch = branch + dot("th,dh->td", attended[:, j * hid : (j + 1) * hid], w_q[j][:, 3 * hid :])
    middle = hidden + branch
    unit_two, inverse_two = norm_parts(middle)
    normed_two = low(unit_two * ln_gain[1] + ln_shift[1])
    latent_three = low(dot("td,rd->tr", normed_two, fc1_down))

    grad_result = g_rows.astype(F32) * keep_rows
    grad_result_low = low(grad_result)
    grad_latent_four = low(dot("td,rd->tr", grad_result_low, fc2_up))

    result = bias_out[1]
    grad_normed_two = 0.0
    latent_four = 0.0
    grad_latent_three = 0.0
    g_fc2_down, g_fc1_up = [], []
    for j in range(cols):
        up_1, down_2 = block(fc1_up, j, ffn), block(fc2_down, j, ffn)
        pre_gelu = (
            dot("td,df->tf", normed_two, w_1[j])
            + dot("tr,rf->tf", latent_three, up_1)
            + bias_of(j)[2 * hid :]
        )
        activated = low(jax.nn.gelu(pre_gelu, approximate=False))
        grad_act = dot("td,df->tf", grad_result_low, w_2[j]) + dot(
            "tr,rf->tf", grad_latent_four, down_2
        )
        grad_pre = low(grad_act * gelu_slope(pre_gelu))
        latent_four = latent_four + dot("tf,rf->tr", activated, down_2)
        grad_latent_three = grad_latent_three + dot("tf,rf->tr", grad_pre, up_1)
        result = result + dot("tf,df->td", activated, w_2[j])
        grad_normed_two = grad_normed_two + dot("tf,df->td", grad_pre, w_1[j])
        g_fc2_down.append(low(dot("tr,tf->rf", grad_latent_four, activated)))
        g_fc1_up.append(low(dot("tr,tf->rf", latent_three, grad_pre)))
    latent_four = low(latent_four)
    grad_latent_three = low(grad_latent_three)
    result = result + dot("tr,rd->td", latent_four, fc2_up)
    out_rows = low(keep_rows * (middle + result))
    layer_out = lax.all_to_all(out_rows, "col", split_axis=1, concat_axis=0, tiled=True)
    grad_normed_two = grad_normed_two + dot("tr,rd->td", grad_latent_three, fc1_down)
    grad_middle = grad_result + norm_back(grad_normed_two, ln_gain[1], unit_two, inverse_two)
    grad_branch = low(grad_middle)
    grad_latent_two = low(dot("td,rd->tr", grad_branch, proj_up))
    g_attended = []
    for j in range(cols):
        g_attended.append(
            low(
                dot("td,dh->th", grad_branch, w_q[j][:, 3 * hid :])
                + dot("tr,rh->th", grad_latent_two, block(proj_down, j, hid))
            )
        )
    g_attended = jnp.concatenate(g_attended, axis=1)
    g_proj_down = low(dot("tr,th->rh", grad_latent_two, attended))
    early = jnp.concatenate(
        [
            place([g_proj_down[:, j * hid : (j + 1) * hid] for j in range(cols)], column),
            low(dot("tr,td->rd", latent_two, grad_branch)),
            low(dot("tr,td->rd", grad_latent_three, normed_two)),
            place(g_fc1_up, column),
            place(g_fc2_down, column),
            low(dot("tr,td->rd", latent_four, grad_result_low)),
        ],
        axis=1,
    )
    early_sum = sum_adapters(early, owners)

    g_q, g_k, g_v = (low(g.reshape(SEQ, D)) for g in attention_back(g_attended.reshape(heads)))
    grad_latent_one = 0.0
    grad_normed_one = 0.0
    g_up = []
    for j in range(cols):
        up = block(qkv_up, j, hid).reshape(R, 3 * hid)
        g_j = jnp.concatenate([g[:, j * hid : (j + 1) * hid] for g in (g_q, g_k, g_v)], axis=1)
        grad_latent_one = grad_latent_one + dot("te,re->tr", g_j, up)
        grad_normed_one = grad_normed_one + dot("te,de->td", g_j, w_q[j][:, : 3 * hid])
        g_up.append(low(dot("tr,te->re", latent_one, g_j)).reshape(R, 3, hid))
    grad_latent_one = low(grad_latent_one)
    late = jnp.concatenate(
        [
            low(dot("tr,td->rd", grad_latent_one, normed_one)),
            place(g_up, column).reshape(R, 3 * D),
        ],
        axis=1,
    )
    late_sum = sum_adapters(late, owners)
    grad_normed_one = grad_normed_one + dot("tr,rd->td", grad_latent_one, qkv_down)
    grad_rows = low(grad_middle + norm_back(grad_normed_one, ln_gain[0], unit_one, inverse_one))
    grad_in = lax.all_to_all(grad_rows, "col", split_axis=1, concat_axis=0, tiled=True)

    return (
        layer_out,
        grad_in,
        late_sum[..., :D],
        late_sum[..., D:].reshape(NA, R, 3, D),
        early_sum[..., :D],
        early_sum[..., D : 2 * D],
        early_sum[..., 2 * D : 3 * D],
        early_sum[..., 3 * D : 3 * D + FF],
        early_sum[..., 3 * D + FF : 3 * D + 2 * FF],
        early_sum[..., 3 * D + 2 * FF :],
    )


def solution(mesh):
    return jax.shard_map(
        per_device,
        mesh=mesh,
        in_specs=(
            P("row", "col"),
            P("row", "col"),
            P("row", None),
            P("row"),
            P(),
            P(),
            P(None, "row", "col"),
            P(None, "col"),
            P("col", "row"),
            P("row", "col"),
            P("col"),
            P("col", "row"),
            P(),
            P(),
            P(),
            P(),
            P(),
            P(),
            P(),
            P(),
            P(),
        ),
        out_specs=(P("row", "col"), P("row", "col"), P(), P(), P(), P(), P(), P(), P(), P()),
        check_vma=False,
    )
```

time: 635 us -> 504 us (0.79)
  waiting for transfers between devices: 391 us -> 150 us
  other arithmetic: 11.5 us -> 69.4 us
  starting transfers between devices: 14.3 us -> 52.7 us
  matrix products: 107 us -> 144 us
  blocking collectives: 47.4 us -> 15.2 us
  local copies, waits for them, and re-layouts: 38.4 us -> 60.3 us
  between operations: 15.6 us -> 5.95 us
    all_gather x7 -> x0, waiting for transfers between devices: 218 us -> none  [the longest x1 50.6 us: per_device(): lax.all_gather(fc1_cols, 'col', axis=1, tiled=True)]
    psum x1 -> x0, waiting for transfers between devices: 139 us -> none  [per_device(): lax.psum((grads[0], grads[1], grads[2], grads[3], grads[4], grads[5], gra...]
    ppermute x0 -> x30, waiting for transfers between devices: none -> 126 us  [exchange(): return lax.ppermute(block, BOTH, pairs)]
    all_gather x3 -> x1, blocking collectives: 47.4 us -> 5.25 us  [per_device(): lax.all_gather(jnp.concatenate([bias_qv.reshape(-1), bias_fc1]), 'col', a...]
    dot_general x38 -> x94, matrix products: 107 us -> 144 us  [dot(): jnp.einsum(formula, left_side, right_side, preferred_element_type=F32)]
    ppermute x0 -> x30, starting transfers between devices: none -> 28.1 us  [exchange(): return lax.ppermute(block, BOTH, pairs)]
    unnamed x5 -> x14, other arithmetic: 0.7 us -> 25.5 us
    another operation x0 -> x39, other arithmetic: none -> 14.9 us  [joined(): return jnp.stack([first, second], axis=dim)]
  transfers between devices with their start and end apart: 12 -> 36, of which waited for: 10 -> 14; matrix products, arithmetic and copies ran while one was open for 11% -> 32% of each run, Pallas kernels for 0% -> 0%
where the time goes in v1:
time: 504 us; the launch traced here: 498 us
  waiting for transfers between devices  150 us (30%)
  matrix products  144 us (29%)
  other arithmetic  69.4 us (14%)
  local copies, waits for them, and re-layouts  60.3 us (12%)
  starting transfers between devices  52.7 us (10%)
  blocking collectives  15.2 us (3%)
  between operations  5.95 us (1%)
    dot_general x94, matrix products, dot(): jnp.einsum(formula, left_side, right_side, preferred_element_type=F32)  144 us
    ppermute x30, waiting for transfers between devices, exchange(): return lax.ppermute(block, BOTH, pairs)  126 us
    ppermute x30, starting transfers between devices, exchange(): return lax.ppermute(block, BOTH, pairs)  28.1 us
    unnamed x14, other arithmetic  25.5 us
    unnamed x264, local copies, waits for them, and re-layouts  22.4 us
    another operation x39, other arithmetic, joined(): return jnp.stack([first, second], axis=dim)  14.9 us
    all_to_all x1, waiting for transfers between devices, per_device(): lax.all_to_all(grad_rows, 'col', split_axis=1, concat_axis=0, tiled=True)  10.2 us
  transfers between devices with their start and end apart: 36, of which 14 were waited for; matrix products, arithmetic and copies ran while one was open for 32% of the time, Pallas kernels for 0%

profile of v1, /device:TPU:0, one launch (start us, length us, event | category | flops | bytes accessed | tf_op | source)
XLA Modules:
  0.0 497.6 jit_solution(16820488066109339706)
XLA Ops:
  0.7 4.4 all-to-all-start
  5.3 3.4 collective-permute-start
  8.9 2.9 collective-permute-start.7
  16.6 5.2 %all-gather.1 = bf16[4,1,1536]{2,1,0:T(2,128)(2,1)S(1)} all-gather(bf16[1,1,1536]{2,1,0:T(2,128)(2,1)S(1)} %reshape.336), channel_id=2, replica_groups=mesh['row'=8,'col'=4] {'col'}, dimensions={0}, use_global_device_ids=true | all-gather | bytes 15360 | tf_op jit(solution)/shard_map/all_gather | solution.py:188
  36.4 9.9 %all-reduce.1 = s32[32]{0:T(128)} all-reduce(s32[32]{0:T(128)S(1)} %dynamic-update-slice), channel_id=1, replica_groups=mesh['row'=8,'col'=4] {'row'}, use_global_device_ids=true, to_apply=%add.1 | all-reduce | flops 32 | bytes 256
  53.5 3.7 all-to-all-start.2
  59.4 7.8 %all-to-all-done.2 = bf16[4,320,256]{2,1,0:T(8,128)(2,1)S(1)} async-done(((bf16[4,320,256]{2,1,0:T(8,128)(2,1)}), bf16[4,320,256]{2,1,0:T(8,128)(2,1)S(1)}, u32[]{:S(2)}, u32[]{:S(2)}) %all-to-all-start.2) | async-done | bytes 655392 | tf_op jit(solution)/shard_map/all_to_all | solution.py:182
  90.8 19.7 %collective-permute-done.4 = bf16[2,2,128,1024]{3,2,1,0:T(8,128)(2,1)S(1)} collective-permute-done((bf16[2,2,128,1024]{3,2,1,0:T(8,128)(2,1)S(1)}, bf16[2,2,128,1024]{3,2,1,0:T(8,128)(2,1)S(1)}, u32[]{:S(2)}, u32[]{:S(2)}) %collective-permute-start.4) | collective-permute-done | bytes 1048608 | tf_op jit(solution)/shard_map/ppermute | solution.py:50
  111.4 18.5 %collective-permute-done.2 = bf16[2,2,128,1024]{3,2,1,0:T(8,128)(2,1)S(1)} collective-permute-done((bf16[2,2,128,1024]{3,2,1,0:T(8,128)(2,1)S(1)}, bf16[2,2,128,1024]{3,2,1,0:T(8,128)(2,1)S(1)}, u32[]{:S(2)}, u32[]{:S(2)}) %collective-permute-start.2) | collective-permute-done | bytes 1048608 | tf_op jit(solution)/shard_map/ppermute | solution.py:50
  134.3 18.1 %collective-permute-done.12 = bf16[2,2,128,1024]{3,2,1,0:T(8,128)(2,1)S(1)} collective-permute-done((bf16[2,2,128,1024]{3,2,1,0:T(8,128)(2,1)S(1)}, bf16[2,2,128,1024]{3,2,1,0:T(8,128)(2,1)S(1)}, u32[]{:S(2)}, u32[]{:S(2)}) %collective-permute-start.12) | collective-permute-done | bytes 1048608 | tf_op jit(solution)/shard_map/ppermute | solution.py:50
  154.5 20.4 %collective-permute-done.5 = bf16[2,2,128,1024]{3,2,1,0:T(8,128)(2,1)S(1)} collective-permute-done((bf16[2,2,128,1024]{3,2,1,0:T(8,128)(2,1)S(1)}, bf16[2,2,128,1024]{3,2,1,0:T(8,128)(2,1)S(1)}, u32[]{:S(2)}, u32[]{:S(2)}) %collective-permute-start.5) | collective-permute-done | bytes 1048608 | tf_op jit(solution)/shard_map/ppermute | solution.py:50
  178.1 18.0 %collective-permute-done.17 = bf16[2,2,128,1024]{3,2,1,0:T(8,128)(2,1)S(1)} collective-permute-done((bf16[2,2,128,1024]{3,2,1,0:T(8,128)(2,1)S(1)}, bf16[2,2,128,1024]{3,2,1,0:T(8,128)(2,1)S(1)}, u32[]{:S(2)}, u32[]{:S(2)}) %collective-permute-start.17) | collective-permute-done | bytes 1048608 | tf_op jit(solution)/shard_map/ppermute | solution.py:50
  198.7 3.5 convolution_add_fusion.3
  208.3 2.3 copy.167
  214.3 2.3 copy.166
  221.0 3.4 fusion.282
  238.2 5.6 %fusion.63 = (bf16[320,1024]{1,0:T(8,128)(2,1)S(1)}, f32[320,1024]{1,0:T(8,128)S(1)}) fusion(f32[1024]{0:T(1024)S(1)} %bitcast.536, f32[320,1024]{1,0:T(8,128)S(1)} %fusion.192, bf16[320,1024]{1,0:T(8,128)(2,1)S(1)} %add_convert_fusion.1, bf16[1024,1024]{1,0:T(8,128)(2,1)} %bitcast.62), kind=kOutput, calls=%fused_computation.105 | convolution fusion | flops 693043200 | bytes 6033408 | tf_op jit(solution)/shard_map/td,df->tf/dot_general | solution.py:40
  243.8 2.8 fusion.55
  247.9 5.7 %fusion.86 = (bf16[320,1024]{1,0:T(8,128)(2,1)S(1)}, bf16[320,1024]{1,0:T(8,128)(2,1)S(1)}) fusion(f32[320,1024]{1,0:T(8,128)S(1)} %copy-done.54, f32[1024]{0:T(1024)S(1)} %bitcast.535, f32[320,1024]{1,0:T(8,128)S(1)} %fusion.185, bf16[320,1024]{1,0:T(8,128)(2,1)S(1)} %add_convert_fusion.1, bf16[1024,1024]{1,0:T(8,128)(2,1)} %collective-permute-done.15), kind=kOutput, calls=%fused_computation.128 | convolution fusion | flops 696320000 | bytes 6688768 | tf_op jit(solution)/shard_map/td,df->tf/dot_general | solution.py:40
  255.7 5.3 %fusion.66 = (bf16[320,1024]{1,0:T(8,128)(2,1)S(1)}, f32[320,1024]{1,0:T(8,128)S(1)}) fusion(f32[1024]{0:T(1024)S(1)} %bitcast.534, f32[320,1024]{1,0:T(8,128)S(1)} %fusion.188, bf16[320,1024]{1,0:T(8,128)(2,1)S(1)} %add_convert_fusion.1, bf16[1024,1024]{1,0:T(8,128)(2,1)} %collective-permute-done.13), kind=kOutput, calls=%fused_computation.108 | convolution fusion | flops 693043200 | bytes 6033408 | tf_op jit(solution)/shard_map/td,df->tf/dot_general | solution.py:40
  261.1 2.8 fusion.54
  268.2 2.5 fusion.288
  270.6 2.5 fusion.289
  273.1 2.5 convolution_add_fusion.12
  275.6 2.5 convolution_add_fusion.4
  278.1 2.6 convolution_add_fusion.2
  280.7 2.5 convolution_add_fusion.1
  283.2 3.6 fusion.12
  286.8 6.8 %fusion.92 = (bf16[320,1024]{1,0:T(8,128)(2,1)S(1)}, bf16[320,1024]{1,0:T(8,128)(2,1)}) fusion(f32[320,1024]{1,0:T(8,128)S(1)} %convolution_add_fusion.1, f32[1024]{0:T(1024)S(1)} %bitcast.533, f32[320,1024]{1,0:T(8,128)S(1)} %fusion.182, bf16[320,1024]{1,0:T(8,128)(2,1)S(1)} %add_convert_fusion.1, bf16[1024,1024]{1,0:T(8,128)(2,1)} %collective-permute-done.18), kind=kOutput, calls=%fused_computation.134 | convolution fusion | flops 696320000 | bytes 6688768 | tf_op jit(solution)/shard_map/td,df->tf/dot_general | solution.py:40
  295.1 2.8 fusion.267
  307.5 5.9 %fusion.23 = bf16[16,64,320]{2,1,0:T(8,128)(2,1)} fusion(bf16[320,16,64]{0,2,1:T(8,128)(2,1)} %bitcast.483, f32[16,320,320]{1,2,0:T(8,128)} %copy-done.1, f32[16,320]{1,0:T(8,128)S(1)} %log_add_fusion), kind=kOutput, calls=%fused_computation.75 | convolution fusion | flops 213319680 | bytes 7884800 | tf_op jit(solution)/shard_map/hqk,qhd->khd/dot_general | solution.py:40
  313.3 8.0 %multiply_reduce_fusion = (f32[16,320]{1,0:T(8,128)S(1)}, f32[16,320,320]{1,2,0:T(8,128)}) fusion(f32[16,320,320]{1,2,0:T(8,128)} %copy-done.1, f32[16,320]{1,0:T(8,128)S(1)} %log_add_fusion, bf16[320,16,64]{0,2,1:T(8,128)(2,1)S(1)} %bitcast.484, bf16[320,16,64]{0,2,1:T(8,128)(2,1)S(1)} %bitcast.494), kind=kOutput, calls=%fused_computation.1 | convolution fusion | flops 214625280 | bytes 14458880 | tf_op jit(solution)/shard_map/qhd,khd->hqk/dot_general | solution.py:40
  321.3 7.3 %multiply_convert_fusion = bf16[16,320,320]{1,2,0:T(8,128)(2,1)S(1)} fusion(f32[16,320,320]{1,2,0:T(8,128)} %get-tuple-element.188, f32[16,320,320]{1,2,0:T(8,128)} %copy-done.1, f32[16,320]{1,0:T(8,128)S(1)} %get-tuple-element.187, f32[16,320]{1,0:T(8,128)S(1)} %log_add_fusion), kind=kLoop, calls=%fused_computation | loop fusion | flops 6553600 | bytes 16424960 | tf_op jit(solution)/shard_map/convert_element_type | solution.py:144
  328.6 2.5 multiply_convert_fusion.1
  345.1 2.3 fusion.166
  347.4 2.5 constant_dynamic-update-slice_fusion.11
  349.9 2.5 constant_dynamic-update-slice_fusion.10
  352.4 2.4 constant_dynamic-update-slice_fusion.9
  354.8 2.5 constant_dynamic-update-slice_fusion.8
  357.7 2.8 constant_dynamic-update-slice_fusion.7
  360.5 2.5 constant_dynamic-update-slice_fusion.6
  363.0 2.4 constant_dynamic-update-slice_fusion.5
  365.5 2.5 constant_dynamic-update-slice_fusion.4
  367.9 2.7 constant_dynamic-update-slice_fusion.3
  370.6 2.5 constant_dynamic-update-slice_fusion.2
  373.2 2.5 constant_dynamic-update-slice_fusion.1
  375.7 2.5 constant_dynamic-update-slice_fusion
  379.2 4.9 all-to-all-start.5
  384.1 9.2 %multiply_add_fusion.4 = (bf16[16,768]{1,0:T(8,128)(2,1)S(1)}, bf16[16,768]{1,0:T(8,128)(2,1)S(1)}, bf16[16,768]{1,0:T(8,128)(2,1)}, bf16[16,768]{1,0:T(8,128)(2,1)S(1)}) fusion(bf16[16,768]{1,0:T(8,128)(2,1)} %convolution_convert_fusion.16, bf16[16,768]{1,0:T(8,128)(2,1)} %convolution_convert_fusion.17, bf16[16,768]{1,0:T(8,128)(2,1)S(1)} %copy-done.103, ...), kind=kOutput, calls=%fused_computation.446 | convolution fusion | flops 9609216 | bytes 673816 | tf_op jit(solution)/shard_map/tr,te->re/dot_general | solution.py:40
  393.2 3.3 multiply_add_fusion.3
  397.4 3.1 convolution_add_fusion.19
  400.5 2.8 fusion.41
  409.3 2.7 collective-permute-start.25
  412.8 3.7 all-to-all-start.4
  418.4 6.3 %all-to-all-done.4 = bf16[32,16,128]{2,1,0:T(8,128)(2,1)S(1)} async-done(((bf16[32,16,128]{2,1,0:T(8,128)(2,1)}), bf16[32,16,128]{2,1,0:T(8,128)(2,1)S(1)}, u32[]{:S(2)}, u32[]{:S(2)}) %all-to-all-start.4) | async-done | bytes 131104 | tf_op jit(solution)/shard_map/all_to_all | solution.py:107
  424.7 4.2 all-to-all-start.1
  431.0 3.6 collective-permute-done.20
  434.8 6.7 %collective-permute-done.27 = bf16[2,2,8,16,384]{4,2,3,0,1:T(8,128)(2,1)S(1)} collective-permute-done((bf16[2,2,8,16,384]{4,2,3,0,1:T(8,128)(2,1)S(1)}, bf16[2,2,8,16,384]{4,2,3,0,1:T(8,128)(2,1)S(1)}, u32[]{:S(2)}, u32[]{:S(2)}) %collective-permute-start.27) | collective-permute-done | bytes 393248 | tf_op jit(solution)/shard_map/ppermute | solution.py:50
  444.3 4.3 collective-permute-done.22
  449.0 13.2 %collective-permute-done.28 = bf16[2,2,2,8,16,384]{5,3,4,0,1,2:T(8,128)(2,1)S(1)} collective-permute-done((bf16[2,2,2,8,16,384]{5,3,4,0,1,2:T(8,128)(2,1)S(1)}, bf16[2,2,2,8,16,384]{5,3,4,0,1,2:T(8,128)(2,1)S(1)}, u32[]{:S(2)}, u32[]{:S(2)}) %collective-permute-start.28) | collective-permute-done | bytes 786464 | tf_op jit(solution)/shard_map/ppermute | solution.py:50
  463.8 2.3 collective-permute-done.23
  468.5 3.8 all-to-all-start.3
  472.2 10.2 %all-to-all-done.3 = bf16[320,4,256]{2,0,1:T(8,128)(2,1)S(1)} async-done(((bf16[320,4,256]{2,0,1:T(8,128)(2,1)}), bf16[320,4,256]{2,0,1:T(8,128)(2,1)S(1)}, u32[]{:S(2)}, u32[]{:S(2)}) %all-to-all-start.3) | async-done | bytes 655392 | tf_op jit(solution)/shard_map/all_to_all | solution.py:320
  492.0 2.3 fusion.270
  (515 shorter events, 155.3 us)
Async XLA Ops:
  0.6 236.7 %copy-start = (bf16[8,16,4096]{2,1,0:T(8,128)(2,1)S(1)}, bf16[8,16,4096]{2,1,0:T(8,128)(2,1)}, u32[]{:S(2)}) copy-start(bf16[8,16,4096]{2,1,0:T(8,128)(2,1)} %param.39) | copy-start | bytes 3145732
  0.7 8.0 %copy-start.67 = (bf16[1024,128]{1,0:T(8,128)(2,1)S(1)}, bf16[1024,128]{1,0:T(8,128)(2,1)}, u32[]{:S(2)}) copy-start(bf16[1024,128]{1,0:T(8,128)(2,1)} %param.32) | copy-start | bytes 786436
  0.7 8.2 %copy-start.66 = (bf16[128,1024]{1,0:T(8,128)(2,1)S(1)}, bf16[128,1024]{1,0:T(8,128)(2,1)}, u32[]{:S(2)}) copy-start(bf16[128,1024]{1,0:T(8,128)(2,1)} %param.30) | copy-start | bytes 786436
  0.7 11.1 %copy-start.124 = (s32[4]{0:T(128)S(1)}, s32[4]{0:T(128)}, u32[]{:S(2)}) copy-start(s32[4]{0:T(128)} %param.24) | copy-start | bytes 52
  0.7 52.8 %all-to-all-start = ((bf16[4,320,256]{2,1,0:T(8,128)(2,1)}), bf16[4,320,256]{2,1,0:T(8,128)(2,1)S(1)}, u32[]{:S(2)}, u32[]{:S(2)}) async-start(bf16[4,320,256]{2,1,0:T(8,128)(2,1)} %bitcast.504), calls=%async_computation | async-start | bytes 1310720 | tf_op jit(solution)/shard_map/all_to_all | solution.py:181
  5.2 41.1 %copy-start.108 = (bf16[2,1024]{1,0:T(2,128)(2,1)S(1)}, bf16[2,1024]{1,0:T(2,128)(2,1)}, u32[]{:S(2)}) copy-start(bf16[2,1024]{1,0:T(2,128)(2,1)} %param.33) | copy-start | bytes 12292
  5.3 41.7 %collective-permute-start = (bf16[128,1024]{1,0:T(8,128)(2,1)S(1)}, bf16[128,1024]{1,0:T(8,128)(2,1)S(1)}, u32[]{:S(2)}, u32[]{:S(2)}) collective-permute-start(bf16[128,1024]{1,0:T(8,128)(2,1)S(1)} %pad_maximum_fusion.23), channel_id=1, source_target_pairs={{0,16},{1,17},{2,18},{3,19},{4,20},{5,21},{6,22},{7,23},{8,24},{9,... | collective-permute-start | bytes 786440 | tf_op jit(solution)/shard_map/ppermute | solution.py:50
  8.8 39.8 %collective-permute-start.10 = (bf16[128,1024]{1,0:T(8,128)(2,1)S(1)}, bf16[128,1024]{1,0:T(8,128)(2,1)S(1)}, u32[]{:S(2)}, u32[]{:S(2)}) collective-permute-start(bf16[128,1024]{1,0:T(8,128)(2,1)S(1)} %bitcast.503), channel_id=1, source_target_pairs={{0,16},{1,17},{2,18},{3,19},{4,20},{5,21},{6,22},{7,23},{8,24},{9,... | collective-permute-start | bytes 786440 | tf_op jit(solution)/shard_map/ppermute | solution.py:50
  8.9 39.7 %collective-permute-start.7 = (bf16[128,1024]{1,0:T(8,128)(2,1)S(1)}, bf16[128,1024]{1,0:T(8,128)(2,1)}, u32[]{:S(2)}, u32[]{:S(2)}) collective-permute-start(bf16[128,1024]{1,0:T(8,128)(2,1)S(1)} %copy-done.66), channel_id=1, source_target_pairs={{0,16},{1,17},{2,18},{3,19},{4,20},{5,21},{6,22},{7,23},{8,24},{9,... | collective-permute-start | bytes 786440 | tf_op jit(solution)/shard_map/ppermute | solution.py:50
  14.5 53.3 %copy-start.95 = (f32[320]{0:T(512)}, f32[320]{0:T(512)S(1)}, u32[]{:S(2)}) copy-start(f32[320]{0:T(512)S(1)} %pad_convert_fusion) | copy-start | bytes 3844
  48.0 35.1 %collective-permute-start.1 = (bf16[2,128,1024]{2,1,0:T(8,128)(2,1)}, bf16[2,128,1024]{2,1,0:T(8,128)(2,1)}, u32[]{:S(2)}, u32[]{:S(2)}) collective-permute-start(bf16[2,128,1024]{2,1,0:T(8,128)(2,1)} %pad_maximum_fusion.18), channel_id=1, source_target_pairs={{0,8},{1,9},{2,10},{3,11},{4,12},{5,13},{6,14},{7,15},{8,0},{9,1},... | collective-permute-start | bytes 1572872 | tf_op jit(solution)/shard_map/ppermute | solution.py:50
  50.6 29.1 %collective-permute-start.8 = (bf16[2,128,1024]{2,1,0:T(8,128)(2,1)}, bf16[2,128,1024]{2,1,0:T(8,128)(2,1)}, u32[]{:S(2)}, u32[]{:S(2)}) collective-permute-start(bf16[2,128,1024]{2,1,0:T(8,128)(2,1)} %pad_maximum_fusion.19), channel_id=1, source_target_pairs={{0,8},{1,9},{2,10},{3,11},{4,12},{5,13},{6,14},{7,15},{8,0},{9,1},... | collective-permute-start | bytes 1572872 | tf_op jit(solution)/shard_map/ppermute | solution.py:50
  52.9 33.6 %collective-permute-start.11 = (bf16[2,128,1024]{2,1,0:T(8,128)(2,1)}, bf16[2,128,1024]{2,1,0:T(8,128)(2,1)}, u32[]{:S(2)}, u32[]{:S(2)}) collective-permute-start(bf16[2,128,1024]{2,1,0:T(8,128)(2,1)} %pad_maximum_fusion.20), channel_id=1, source_target_pairs={{0,8},{1,9},{2,10},{3,11},{4,12},{5,13},{6,14},{7,15},{8,0},{9,1},... | collective-permute-start | bytes 1572872 | tf_op jit(solution)/shard_map/ppermute | solution.py:50
  53.5 13.7 %all-to-all-start.2 = ((bf16[4,320,256]{2,1,0:T(8,128)(2,1)}), bf16[4,320,256]{2,1,0:T(8,128)(2,1)S(1)}, u32[]{:S(2)}, u32[]{:S(2)}) async-start(bf16[4,320,256]{2,1,0:T(8,128)(2,1)} %bitcast.505), calls=%async_computation.2 | async-start | bytes 1310720 | tf_op jit(solution)/shard_map/all_to_all | solution.py:182
  57.4 21.6 %copy-start.92 = (f32[320]{0:T(512)}, f32[320]{0:T(512)S(1)}, u32[]{:S(2)}) copy-start(f32[320]{0:T(512)S(1)} %broadcast_multiply_fusion.5) | copy-start | bytes 3844
  59.4 19.6 %copy-start.2 = (f32[4,40,8,256]{3,2,0,1:T(8,128)}, f32[4,40,8,256]{3,2,0,1:T(8,128)S(1)}, u32[]{:S(2)}) copy-start(f32[4,40,8,256]{3,2,0,1:T(8,128)S(1)} %copy.202) | copy-start | bytes 3932164
  67.5 131.3 %copy-start.23 = (bf16[4,40,8,256]{3,2,0,1:T(8,128)(2,1)}, bf16[4,40,8,256]{3,2,0,1:T(8,128)(2,1)S(1)}, u32[]{:S(2)}) copy-start(bf16[4,40,8,256]{3,2,0,1:T(8,128)(2,1)S(1)} %copy.205) | copy-start | bytes 1966084
  78.9 11.5 %copy-start.64 = (bf16[320,16]{0,1:T(8,128)(2,1)}, bf16[320,16]{0,1:T(8,128)(2,1)S(1)}, u32[]{:S(2)}) copy-start(bf16[320,16]{0,1:T(8,128)(2,1)S(1)} %convolution_convert_fusion.23) | copy-start | bytes 30724
  79.3 125.7 %copy-start.5 = (bf16[320,1024]{1,0:T(8,128)(2,1)}, bf16[320,1024]{1,0:T(8,128)(2,1)S(1)}, u32[]{:S(2)}) copy-start(bf16[320,1024]{1,0:T(8,128)(2,1)S(1)} %add_convert_fusion.2) | copy-start | bytes 1966084
  81.3 30.0 %collective-permute-start.9 = (bf16[2,2,128,1024]{3,2,0,1:T(8,128)(2,1)S(1)}, bf16[2,2,128,1024]{3,2,0,1:T(8,128)(2,1)S(1)}, u32[]{:S(2)}, u32[]{:S(2)}) collective-permute-start(bf16[2,2,128,1024]{3,2,0,1:T(8,128)(2,1)S(1)} %pad_maximum_fusion.7), channel_id=1, source_target_pairs={{0,4},{1,5},{2,6},{3,7},{4,0},{5,1},{6,2},{7,3},{8,12},{9,13},{10,... | collective-permute-start | bytes 3145736 | tf_op jit(solution)/shard_map/ppermute | solution.py:50
  84.3 26.2 %collective-permute-start.4 = (bf16[2,2,128,1024]{3,2,1,0:T(8,128)(2,1)S(1)}, bf16[2,2,128,1024]{3,2,1,0:T(8,128)(2,1)S(1)}, u32[]{:S(2)}, u32[]{:S(2)}) collective-permute-start(bf16[2,2,128,1024]{3,2,1,0:T(8,128)(2,1)S(1)} %pad_maximum_fusion.6), channel_id=1, source_target_pairs={{0,2},{1,3},{2,0},{3,1},{4,6},{5,7},{6,4},{7,5},{8,10},{9,11},{10,... | collective-permute-start | bytes 3145736 | tf_op jit(solution)/shard_map/ppermute | solution.py:50
  85.3 44.6 %collective-permute-start.2 = (bf16[2,2,128,1024]{3,2,1,0:T(8,128)(2,1)S(1)}, bf16[2,2,128,1024]{3,2,1,0:T(8,128)(2,1)S(1)}, u32[]{:S(2)}, u32[]{:S(2)}) collective-permute-start(bf16[2,2,128,1024]{3,2,1,0:T(8,128)(2,1)S(1)} %pad_maximum_fusion.6), channel_id=1, source_target_pairs={{0,4},{1,5},{2,6},{3,7},{4,0},{5,1},{6,2},{7,3},{8,12},{9,13},{10,... | collective-permute-start | bytes 3145736 | tf_op jit(solution)/shard_map/ppermute | solution.py:50
  87.7 44.8 %collective-permute-start.16 = (bf16[2,2,128,1024]{3,2,1,0:T(8,128)(2,1)S(1)}, bf16[2,2,128,1024]{3,2,1,0:T(8,128)(2,1)S(1)}, u32[]{:S(2)}, u32[]{:S(2)}) collective-permute-start(bf16[2,2,128,1024]{3,2,1,0:T(8,128)(2,1)S(1)} %pad_maximum_fusion.8), channel_id=1, source_target_pairs={{0,2},{1,3},{2,0},{3,1},{4,6},{5,7},{6,4},{7,5},{8,10},{9,11},{10,... | collective-permute-start | bytes 3145736 | tf_op jit(solution)/shard_map/ppermute | solution.py:50
  89.3 63.1 %collective-permute-start.12 = (bf16[2,2,128,1024]{3,2,1,0:T(8,128)(2,1)S(1)}, bf16[2,2,128,1024]{3,2,1,0:T(8,128)(2,1)S(1)}, u32[]{:S(2)}, u32[]{:S(2)}) collective-permute-start(bf16[2,2,128,1024]{3,2,1,0:T(8,128)(2,1)S(1)} %pad_maximum_fusion.8), channel_id=1, source_target_pairs={{0,4},{1,5},{2,6},{3,7},{4,0},{5,1},{6,2},{7,3},{8,12},{9,13},{10,... | collective-permute-start | bytes 3145736 | tf_op jit(solution)/shard_map/ppermute | solution.py:50
  110.5 64.3 %collective-permute-start.5 = (bf16[2,2,128,1024]{3,2,1,0:T(8,128)(2,1)S(1)}, bf16[2,2,128,1024]{3,2,1,0:T(8,128)(2,1)S(1)}, u32[]{:S(2)}, u32[]{:S(2)}) collective-permute-start(bf16[2,2,128,1024]{3,2,1,0:T(8,128)(2,1)S(1)} %collective-permute-done.4), channel_id=1, source_target_pairs={{0,4},{1,5},{2,6},{3,7},{4,0},{5,1},{6,2},{7,3},{8,12},{9,13},{10,... | collective-permute-start | bytes 3145736 | tf_op jit(solution)/shard_map/ppermute | solution.py:50
  132.0 99.2 %copy-start.9 = (bf16[2,2,2,128,1024]{4,3,2,1,0:T(8,128)(2,1)}, bf16[2,2,2,128,1024]{4,3,2,1,0:T(8,128)(2,1)S(1)}, u32[]{:S(2)}) copy-start(bf16[2,2,2,128,1024]{4,3,2,1,0:T(8,128)(2,1)S(1)} %pad_maximum_fusion) | copy-start | bytes 6291460
  132.0 70.3 %collective-permute-start.3 = (bf16[1024,1024]{1,0:T(8,128)(2,1)S(1)}, bf16[1024,1024]{1,0:T(8,128)(2,1)S(1)}, u32[]{:S(2)}, u32[]{:S(2)}) collective-permute-start(bf16[1024,1024]{1,0:T(8,128)(2,1)S(1)} %bitcast.464), channel_id=1, source_target_pairs={{0,1},{1,0},{2,3},{3,2},{4,5},{5,4},{6,7},{7,6},{8,9},{9,8},{10,11... | collective-permute-start | bytes 6291464 | tf_op jit(solution)/shard_map/ppermute | solution.py:50
  132.1 123.6 %collective-permute-start.13 = (bf16[1024,1024]{1,0:T(8,128)(2,1)}, bf16[1024,1024]{1,0:T(8,128)(2,1)}, u32[]{:S(2)}, u32[]{:S(2)}) collective-permute-start(bf16[1024,1024]{1,0:T(8,128)(2,1)} %bitcast.62), channel_id=1, source_target_pairs={{0,1},{1,0},{2,3},{3,2},{4,5},{5,4},{6,7},{7,6},{8,9},{9,8},{10,11... | collective-permute-start | bytes 6291464 | tf_op jit(solution)/shard_map/ppermute | solution.py:50
  132.6 63.5 %collective-permute-start.17 = (bf16[2,2,128,1024]{3,2,1,0:T(8,128)(2,1)S(1)}, bf16[2,2,128,1024]{3,2,1,0:T(8,128)(2,1)S(1)}, u32[]{:S(2)}, u32[]{:S(2)}) collective-permute-start(bf16[2,2,128,1024]{3,2,1,0:T(8,128)(2,1)S(1)} %collective-permute-done.16), channel_id=1, source_target_pairs={{0,4},{1,5},{2,6},{3,7},{4,0},{5,1},{6,2},{7,3},{8,12},{9,13},{10,... | collective-permute-start | bytes 3145736 | tf_op jit(solution)/shard_map/ppermute | solution.py:50
  154.1 49.5 %collective-permute-start.15 = (bf16[1024,1024]{1,0:T(8,128)(2,1)}, bf16[1024,1024]{1,0:T(8,128)(2,1)}, u32[]{:S(2)}, u32[]{:S(2)}) collective-permute-start(bf16[1024,1024]{1,0:T(8,128)(2,1)} %bitcast.62), channel_id=1, source_target_pairs={{0,2},{1,3},{2,0},{3,1},{4,6},{5,7},{6,4},{7,5},{8,10},{9,11},{10,... | collective-permute-start | bytes 6291464 | tf_op jit(solution)/shard_map/ppermute | solution.py:50
  175.4 29.6 %collective-permute-start.6 = (bf16[1024,1024]{1,0:T(8,128)(2,1)S(1)}, bf16[1024,1024]{1,0:T(8,128)(2,1)S(1)}, u32[]{:S(2)}, u32[]{:S(2)}) collective-permute-start(bf16[1024,1024]{1,0:T(8,128)(2,1)S(1)} %bitcast.469), channel_id=1, source_target_pairs={{0,1},{1,0},{2,3},{3,2},{4,5},{5,4},{6,7},{7,6},{8,9},{9,8},{10,11... | collective-permute-start | bytes 6291464 | tf_op jit(solution)/shard_map/ppermute | solution.py:50
  196.1 65.0 %collective-permute-start.14 = (bf16[1024,1024]{1,0:T(8,128)(2,1)}, bf16[1024,1024]{1,0:T(8,128)(2,1)}, u32[]{:S(2)}, u32[]{:S(2)}) collective-permute-start(bf16[1024,1024]{1,0:T(8,128)(2,1)} %bitcast.74), channel_id=1, source_target_pairs={{0,1},{1,0},{2,3},{3,2},{4,5},{5,4},{6,7},{7,6},{8,9},{9,8},{10,11... | collective-permute-start | bytes 6291464 | tf_op jit(solution)/shard_map/ppermute | solution.py:50
  202.3 78.4 %collective-permute-start.19 = (bf16[1024,1024]{1,0:T(8,128)(2,1)}, bf16[1024,1024]{1,0:T(8,128)(2,1)}, u32[]{:S(2)}, u32[]{:S(2)}) collective-permute-start(bf16[1024,1024]{1,0:T(8,128)(2,1)} %bitcast.81), channel_id=1, source_target_pairs={{0,1},{1,0},{2,3},{3,2},{4,5},{5,4},{6,7},{7,6},{8,9},{9,8},{10,11... | collective-permute-start | bytes 6291464 | tf_op jit(solution)/shard_map/ppermute | solution.py:50
  203.6 83.1 %collective-permute-start.18 = (bf16[1024,1024]{1,0:T(8,128)(2,1)}, bf16[1024,1024]{1,0:T(8,128)(2,1)}, u32[]{:S(2)}, u32[]{:S(2)}) collective-permute-start(bf16[1024,1024]{1,0:T(8,128)(2,1)} %collective-permute-done.15), channel_id=1, source_target_pairs={{0,1},{1,0},{2,3},{3,2},{4,5},{5,4},{6,7},{7,6},{8,9},{9,8},{10,11... | collective-permute-start | bytes 6291464 | tf_op jit(solution)/shard_map/ppermute | solution.py:50
  236.2 50.5 %copy-start.28 = (bf16[320,1024]{1,0:T(8,128)(2,1)}, bf16[320,1024]{1,0:T(8,128)(2,1)S(1)}, u32[]{:S(2)}) copy-start(bf16[320,1024]{1,0:T(8,128)(2,1)S(1)} %add_convert_fusion.1) | copy-start | bytes 1966084
  332.4 6.7 %copy-start.74 = (bf16[320,256]{0,1:T(8,128)(2,1)}, bf16[320,256]{0,1:T(8,128)(2,1)S(1)}, u32[]{:S(2)}) copy-start(bf16[320,256]{0,1:T(8,128)(2,1)S(1)} %get-tuple-element.108) | copy-start | bytes 491524
  332.4 7.9 %copy-start.68 = (bf16[320,256]{0,1:T(8,128)(2,1)}, bf16[320,256]{0,1:T(8,128)(2,1)S(1)}, u32[]{:S(2)}) copy-start(bf16[320,256]{0,1:T(8,128)(2,1)S(1)} %get-tuple-element.107) | copy-start | bytes 491524
  332.5 6.6 %copy-start.76 = (bf16[320,256]{0,1:T(8,128)(2,1)}, bf16[320,256]{0,1:T(8,128)(2,1)S(1)}, u32[]{:S(2)}) copy-start(bf16[320,256]{0,1:T(8,128)(2,1)S(1)} %get-tuple-element.104) | copy-start | bytes 491524
  332.5 7.7 %copy-start.70 = (bf16[320,256]{0,1:T(8,128)(2,1)}, bf16[320,256]{0,1:T(8,128)(2,1)S(1)}, u32[]{:S(2)}) copy-start(bf16[320,256]{0,1:T(8,128)(2,1)S(1)} %get-tuple-element.103) | copy-start | bytes 491524
  332.5 7.9 %copy-start.57 = (bf16[320,256]{0,1:T(8,128)(2,1)}, bf16[320,256]{0,1:T(8,128)(2,1)S(1)}, u32[]{:S(2)}) copy-start(bf16[320,256]{0,1:T(8,128)(2,1)S(1)} %get-tuple-element.102) | copy-start | bytes 491524
  332.6 6.5 %copy-start.77 = (bf16[320,256]{0,1:T(8,128)(2,1)}, bf16[320,256]{0,1:T(8,128)(2,1)S(1)}, u32[]{:S(2)}) copy-start(bf16[320,256]{0,1:T(8,128)(2,1)S(1)} %get-tuple-element.100) | copy-start | bytes 491524
  332.7 7.6 %copy-start.72 = (bf16[320,256]{0,1:T(8,128)(2,1)}, bf16[320,256]{0,1:T(8,128)(2,1)S(1)}, u32[]{:S(2)}) copy-start(bf16[320,256]{0,1:T(8,128)(2,1)S(1)} %get-tuple-element.99) | copy-start | bytes 491524
  332.7 7.8 %copy-start.59 = (bf16[320,256]{0,1:T(8,128)(2,1)}, bf16[320,256]{0,1:T(8,128)(2,1)S(1)}, u32[]{:S(2)}) copy-start(bf16[320,256]{0,1:T(8,128)(2,1)S(1)} %get-tuple-element.98) | copy-start | bytes 491524
  345.1 12.4 %copy-start.29 = (bf16[320,1024]{1,0:T(8,128)(2,1)S(1)}, bf16[320,1024]{1,0:T(8,128)(2,1)}, u32[]{:S(2)}) copy-start(bf16[320,1024]{1,0:T(8,128)(2,1)} %copy-done.28) | copy-start | bytes 1966084
  345.1 12.6 %copy-start.27 = (bf16[320,1024]{1,0:T(8,128)(2,1)S(1)}, bf16[320,1024]{1,0:T(8,128)(2,1)}, u32[]{:S(2)}) copy-start(bf16[320,1024]{1,0:T(8,128)(2,1)} %copy-done.26) | copy-start | bytes 1966084
  357.7 20.4 %copy-start.22 = (bf16[320,1024]{1,0:T(8,128)(2,1)S(1)}, bf16[320,1024]{1,0:T(8,128)(2,1)}, u32[]{:S(2)}) copy-start(bf16[320,1024]{1,0:T(8,128)(2,1)} %multiply_convert_fusion.3) | copy-start | bytes 1966084
  373.2 10.9 %copy-start.58 = (bf16[320,256]{0,1:T(8,128)(2,1)S(1)}, bf16[320,256]{0,1:T(8,128)(2,1)}, u32[]{:S(2)}) copy-start(bf16[320,256]{0,1:T(8,128)(2,1)} %copy-done.57) | copy-start | bytes 491524
  373.2 10.9 %copy-start.103 = (bf16[16,768]{1,0:T(8,128)(2,1)S(1)}, bf16[16,768]{1,0:T(8,128)(2,1)}, u32[]{:S(2)}) copy-start(bf16[16,768]{1,0:T(8,128)(2,1)} %convolution_convert_fusion.18) | copy-start | bytes 73732
  379.2 18.2 %copy-start.75 = (bf16[320,256]{0,1:T(8,128)(2,1)S(1)}, bf16[320,256]{0,1:T(8,128)(2,1)}, u32[]{:S(2)}) copy-start(bf16[320,256]{0,1:T(8,128)(2,1)} %copy-done.74) | copy-start | bytes 491524
  379.2 30.0 %all-to-all-start.5 = ((bf16[32,16,384]{2,1,0:T(8,128)(2,1)}), bf16[32,16,384]{2,1,0:T(8,128)(2,1)S(1)}, u32[]{:S(2)}, u32[]{:S(2)}) async-start(bf16[32,16,384]{2,1,0:T(8,128)(2,1)} %bitcast.454), calls=%async_computation.5 | async-start | bytes 786432 | tf_op jit(solution)/shard_map/all_to_all | solution.py:107
  409.3 8.0 %collective-permute-start.25 = (bf16[8,16,384]{2,0,1:T(8,128)(2,1)S(1)}, bf16[8,16,384]{2,0,1:T(8,128)(2,1)S(1)}, u32[]{:S(2)}, u32[]{:S(2)}) collective-permute-start(bf16[8,16,384]{2,0,1:T(8,128)(2,1)S(1)} %convolution_convert_fusion), channel_id=1, source_target_pairs={{0,16},{1,17},{2,18},{3,19},{4,20},{5,21},{6,22},{7,23},{8,24},{9,... | collective-permute-start | bytes 294920 | tf_op jit(solution)/shard_map/ppermute | solution.py:50
  412.8 12.0 %all-to-all-start.4 = ((bf16[32,16,128]{2,1,0:T(8,128)(2,1)}), bf16[32,16,128]{2,1,0:T(8,128)(2,1)S(1)}, u32[]{:S(2)}, u32[]{:S(2)}) async-start(bf16[32,16,128]{2,1,0:T(8,128)(2,1)} %bitcast_bitcast_fusion.1), calls=%async_computation.4 | async-start | bytes 262144 | tf_op jit(solution)/shard_map/all_to_all | solution.py:107
  417.4 12.7 %collective-permute-start.26 = (bf16[2,8,16,384]{3,1,2,0:T(8,128)(2,1)S(1)}, bf16[2,8,16,384]{3,1,2,0:T(8,128)(2,1)S(1)}, u32[]{:S(2)}, u32[]{:S(2)}) collective-permute-start(bf16[2,8,16,384]{3,1,2,0:T(8,128)(2,1)S(1)} %pad_maximum_fusion.25), channel_id=1, source_target_pairs={{0,8},{1,9},{2,10},{3,11},{4,12},{5,13},{6,14},{7,15},{8,0},{9,1},... | collective-permute-start | bytes 589832 | tf_op jit(solution)/shard_map/ppermute | solution.py:50
  424.7 43.7 %all-to-all-start.1 = ((bf16[320,4,256]{2,0,1:T(8,128)(2,1)}), bf16[320,4,256]{2,0,1:T(8,128)(2,1)}, u32[]{:S(2)}, u32[]{:S(2)}) async-start(bf16[320,4,256]{2,0,1:T(8,128)(2,1)} %bitcast.452), calls=%async_computation.1 | async-start | bytes 1310720 | tf_op jit(solution)/shard_map/all_to_all | solution.py:271
  429.1 5.6 %collective-permute-start.20 = (bf16[8,16,128]{2,0,1:T(8,128)(2,1)S(1)}, bf16[8,16,128]{2,0,1:T(8,128)(2,1)S(1)}, u32[]{:S(2)}, u32[]{:S(2)}) collective-permute-start(bf16[8,16,128]{2,0,1:T(8,128)(2,1)S(1)} %convolution_convert_fusion.13), channel_id=1, source_target_pairs={{0,16},{1,17},{2,18},{3,19},{4,20},{5,21},{6,22},{7,23},{8,24},{9,... | collective-permute-start | bytes 98312 | tf_op jit(solution)/shard_map/ppermute | solution.py:50
  430.2 11.3 %collective-permute-start.27 = (bf16[2,2,8,16,384]{4,2,3,0,1:T(8,128)(2,1)S(1)}, bf16[2,2,8,16,384]{4,2,3,0,1:T(8,128)(2,1)S(1)}, u32[]{:S(2)}, u32[]{:S(2)}) collective-permute-start(bf16[2,2,8,16,384]{4,2,3,0,1:T(8,128)(2,1)S(1)} %pad_maximum_fusion.22), channel_id=1, source_target_pairs={{0,4},{1,5},{2,6},{3,7},{4,0},{5,1},{6,2},{7,3},{8,12},{9,13},{10,... | collective-permute-start | bytes 1179656 | tf_op jit(solution)/shard_map/ppermute | solution.py:50
  434.7 8.8 %collective-permute-start.21 = (bf16[2,8,16,128]{3,1,2,0:T(8,128)(2,1)S(1)}, bf16[2,8,16,128]{3,1,2,0:T(8,128)(2,1)S(1)}, u32[]{:S(2)}, u32[]{:S(2)}) collective-permute-start(bf16[2,8,16,128]{3,1,2,0:T(8,128)(2,1)S(1)} %pad_maximum_fusion.28), channel_id=1, source_target_pairs={{0,8},{1,9},{2,10},{3,11},{4,12},{5,13},{6,14},{7,15},{8,0},{9,1},... | collective-permute-start | bytes 196616 | tf_op jit(solution)/shard_map/ppermute | solution.py:50
  441.7 20.5 %collective-permute-start.28 = (bf16[2,2,2,8,16,384]{5,3,4,0,1,2:T(8,128)(2,1)S(1)}, bf16[2,2,2,8,16,384]{5,3,4,0,1,2:T(8,128)(2,1)S(1)}, u32[]{:S(2)}, u32[]{:S(2)}) collective-permute-start(bf16[2,2,2,8,16,384]{5,3,4,0,1,2:T(8,128)(2,1)S(1)} %pad_maximum_fusion.9), channel_id=1, source_target_pairs={{0,2},{1,3},{2,0},{3,1},{4,6},{5,7},{6,4},{7,5},{8,10},{9,11},{10,... | collective-permute-start | bytes 2359304 | tf_op jit(solution)/shard_map/ppermute | solution.py:50
  443.5 5.0 %collective-permute-start.22 = (bf16[2,2,8,16,128]{4,2,3,0,1:T(8,128)(2,1)S(1)}, bf16[2,2,8,16,128]{4,2,3,0,1:T(8,128)(2,1)S(1)}, u32[]{:S(2)}, u32[]{:S(2)}) collective-permute-start(bf16[2,2,8,16,128]{4,2,3,0,1:T(8,128)(2,1)S(1)} %pad_maximum_fusion.27), channel_id=1, source_target_pairs={{0,4},{1,5},{2,6},{3,7},{4,0},{5,1},{6,2},{7,3},{8,12},{9,13},{10,... | collective-permute-start | bytes 393224 | tf_op jit(solution)/shard_map/ppermute | solution.py:50
  448.6 17.6 %collective-permute-start.23 = (bf16[2,2,2,8,16,128]{5,3,4,0,1,2:T(8,128)(2,1)S(1)}, bf16[2,2,2,8,16,128]{5,3,4,0,1,2:T(8,128)(2,1)S(1)}, u32[]{:S(2)}, u32[]{:S(2)}) collective-permute-start(bf16[2,2,2,8,16,128]{5,3,4,0,1,2:T(8,128)(2,1)S(1)} %pad_maximum_fusion.24), channel_id=1, source_target_pairs={{0,2},{1,3},{2,0},{3,1},{4,6},{5,7},{6,4},{7,5},{8,10},{9,11},{10,... | collective-permute-start | bytes 786440 | tf_op jit(solution)/shard_map/ppermute | solution.py:50
  463.8 22.7 %collective-permute-start.29 = (bf16[2,2,2,2,8,16,384]{6,4,5,0,1,2,3:T(8,128)(2,1)}, bf16[2,2,2,2,8,16,384]{6,4,5,0,1,2,3:T(8,128)(2,1)}, u32[]{:S(2)}, u32[]{:S(2)}) collective-permute-start(bf16[2,2,2,2,8,16,384]{6,4,5,0,1,2,3:T(8,128)(2,1)} %pad_maximum_fusion.5), channel_id=1, source_target_pairs={{0,1},{1,0},{2,3},{3,2},{4,5},{5,4},{6,7},{7,6},{8,9},{9,8},{10,11... | collective-permute-start | bytes 4718600 | tf_op jit(solution)/shard_map/ppermute | solution.py:50
  467.1 15.3 %collective-permute-start.24 = (bf16[2,2,2,2,8,16,128]{6,4,5,0,1,2,3:T(8,128)(2,1)}, bf16[2,2,2,2,8,16,128]{6,4,5,0,1,2,3:T(8,128)(2,1)}, u32[]{:S(2)}, u32[]{:S(2)}) collective-permute-start(bf16[2,2,2,2,8,16,128]{6,4,5,0,1,2,3:T(8,128)(2,1)} %pad_maximum_fusion.21), channel_id=1, source_target_pairs={{0,1},{1,0},{2,3},{3,2},{4,5},{5,4},{6,7},{7,6},{8,9},{9,8},{10,11... | collective-permute-start | bytes 1572872 | tf_op jit(solution)/shard_map/ppermute | solution.py:50
  467.6 14.9 %copy-start.53 = (bf16[2,2,2,1,8,16,128]{6,4,5,0,1,2,3:T(8,128)(2,1)S(1)}, bf16[2,2,2,1,8,16,128]{6,4,5,0,1,2,3:T(8,128)(2,1)}, u32[]{:S(2)}) copy-start(bf16[2,2,2,1,8,16,128]{6,4,5,0,1,2,3:T(8,128)(2,1)} %copy-done.52) | copy-start | bytes 786436
  468.5 14.0 %all-to-all-start.3 = ((bf16[320,4,256]{2,0,1:T(8,128)(2,1)}), bf16[320,4,256]{2,0,1:T(8,128)(2,1)S(1)}, u32[]{:S(2)}, u32[]{:S(2)}) async-start(bf16[320,4,256]{2,0,1:T(8,128)(2,1)} %bitcast.451), calls=%async_computation.3 | async-start | bytes 1310720 | tf_op jit(solution)/shard_map/all_to_all | solution.py:320
  (97 other events, 227.6 us)

commit v2 on v0

v2 whole, which is shorter than its diff:
```python
import functools

import jax
import jax.numpy as jnp
from jax import lax
from jax.experimental import pallas as pl
from jax.experimental.pallas import tpu as pltpu
from jax.sharding import PartitionSpec as P

D = 1024
H = 16
HD = 64
FF = 4096
BUF = 64
R = 16
NA = 8
SEQ = 320
PAIR = 2 * HD
EXTRA = 16
EARLY = 4 * D + 2 * FF
LATE = 4 * D
BF = jnp.bfloat16
F32 = jnp.float32
BOTH = ("row", "col")
VMEM = pltpu.VMEM
NN = (((1,), (0,)), ((), ()))
NT = (((1,), (1,)), ((), ()))


def mm(left, right, dims=NN):
    return lax.dot_general(left, right, dims, preferred_element_type=F32)


def low(values):
    return values.astype(BF)


def norm_parts(values):
    row_mean = jnp.mean(values, axis=-1, keepdims=True)
    centered = values - row_mean
    variance = jnp.mean(centered * centered, axis=-1, keepdims=True)
    inverse = lax.rsqrt(variance + 1e-06)
    return (centered * inverse, inverse)


def norm_back(grad_normed, gain_row, unit_rows, inverse):
    scaled = grad_normed * gain_row
    first_mean = jnp.mean(scaled, axis=-1, keepdims=True)
    second_mean = jnp.mean(scaled * unit_rows, axis=-1, keepdims=True)
    return inverse * (scaled - first_mean - unit_rows * second_mean)


def call(kernel, outs, ins, spaces, scratch=(), flops=0, moved=0, aliases=None):
    return pl.pallas_call(
        kernel,
        out_shape=outs,
        in_specs=[pl.BlockSpec(memory_space=s) for s in spaces],
        out_specs=jax.tree.map(lambda _: pl.BlockSpec(memory_space=VMEM), outs),
        scratch_shapes=list(scratch),
        input_output_aliases=aliases or {},
        compiler_params=pltpu.CompilerParams(vmem_limit_bytes=56 << 20),
        cost_estimate=pl.CostEstimate(flops=flops, bytes_accessed=moved, transcendentals=0),
    )(*ins)


def sizes():
    return lax.axis_size("row"), lax.axis_size("col")


def swap(block, flip):
    rows, cols = sizes()
    pairs = []
    for i in range(rows * cols):
        row, col = flip(i // cols, i % cols)
        pairs.append((i, row * cols + col))
    return lax.ppermute(block, BOTH, pairs)


def bits_of(size):
    return size.bit_length() - 1


def stack_kernel(which, *refs):
    out = refs[-1]
    for m, ref in enumerate(refs[:-1]):
        out[which[0] ^ m] = ref[...]


def stacked(parts, index):
    shape = parts[0].shape
    flat = [p.reshape((-1, shape[-1])) for p in parts]
    out = jax.ShapeDtypeStruct((len(parts),) + flat[0].shape, flat[0].dtype)
    made = call(
        stack_kernel,
        out,
        [index.reshape(1).astype(jnp.int32)] + flat,
        [pltpu.SMEM] + [VMEM] * len(parts),
        moved=2 * len(parts) * flat[0].size * 2,
    )
    return made.reshape((len(parts),) + shape)


def group_join(block, axis, low_bit, width):
    parts = [block]
    for m in range(1, 1 << width):
        step = m << low_bit
        if axis == "row":
            parts.append(swap(block, lambda r, c: (r ^ step, c)))
        else:
            parts.append(swap(block, lambda r, c: (r, c ^ step)))
    index = (lax.axis_index(axis) >> low_bit) & ((1 << width) - 1)
    return stacked(parts, index)


def groups(top, bottom):
    out = []
    while top > bottom:
        width = min(2, top - bottom)
        out.append((top - width, width))
        top -= width
    return out


def early_groups(rows, cols):
    return [("row",) + g for g in groups(bits_of(rows), 1)] + [
        ("col",) + g for g in groups(bits_of(cols), 2)
    ]


def lead_table(rows, cols):
    table = [(0, 0)]
    for axis, bit, width in early_groups(rows, cols):
        shift = bit - (1 if axis == "row" else 2)
        new = []
        for value in range(1 << width):
            for high_col, high_row in table:
                if axis == "row":
                    new.append((high_col, high_row + (value << shift)))
                else:
                    new.append((high_col + (value << shift), high_row))
        table = new
    return table


def gather_pieces(shard):
    rows, cols = sizes()
    block = shard
    for axis, bit, width in early_groups(rows, cols):
        block = group_join(block, axis, bit, width)
    own = block.reshape((-1,) + shard.shape)

    def one(r, c):
        return (r, c ^ 2) if c % 2 == 0 else (r ^ 1, c)

    def two(r, c):
        return (r ^ 1, c) if c % 2 == 0 else (r, c ^ 2)

    def core(r, c):
        return (r, c ^ 1)

    first = swap(own, one)
    second = swap(own, two)
    both = swap(first, two)
    mine = [own, first, second, both]
    return mine + [swap(p, core) for p in mine]


def all_steps(rows, cols):
    return (
        [("row",) + g for g in groups(bits_of(rows), 1)]
        + [("row", 0, 1)]
        + [("col",) + g for g in groups(bits_of(cols), 1)]
        + [("col", 0, 1)]
    )


def all_table(rows, cols):
    table = [0]
    for axis, bit, width in all_steps(rows, cols):
        stride = (cols if axis == "row" else 1) << bit
        table = [old + value * stride for value in range(1 << width) for old in table]
    return table


def gather_leading(block):
    rows, cols = sizes()
    shape = block.shape
    for axis, bit, width in all_steps(rows, cols):
        block = group_join(block, axis, bit, width)
    return block.reshape((rows * cols,) + shape)


def gather_owners(adapter_index):
    rows, cols = sizes()
    index = lax.axis_index("row")
    block = adapter_index
    for low_bit, width in reversed(groups(bits_of(rows), 0)):
        parts = [block]
        for m in range(1, 1 << width):
            step = m << low_bit
            parts.append(swap(block, lambda r, c: (r ^ step, c)))
        here = (index >> low_bit) & ((1 << width) - 1)
        block = jnp.stack(parts)[jnp.arange(1 << width) ^ here]
    return block.reshape(-1)


class Weights:
    def __init__(self, sc, pieces, w, sems, lead, first_lane=0):
        core, low_row = sc[2], sc[3]
        self.copies = {}
        depth = pieces[0].shape[1]
        taken = pl.ds(first_lane, w.shape[2])
        for k, piece in enumerate(pieces):
            kind, away = k % 4, k // 4
            turn = (core + away) & 1
            x_rel = (0, 1 - turn, turn, 1)[kind]
            y_rel = (0, turn, 1 - turn, 1)[kind]
            for n, (high_col, high_row) in enumerate(lead):
                slot = high_col * 4 + x_rel * 2 + away
                row = (high_row * 2 + ((low_row + y_rel) & 1)) * depth
                copy = pltpu.make_async_copy(
                    piece.at[n, :, taken],
                    w.at[slot, pl.ds(pl.multiple_of(row, depth), depth), :],
                    sems.at[k, n],
                )
                self.copies[(k, n)] = copy

    def start(self):
        for copy in self.copies.values():
            copy.start()

    def wait(self):
        for copy in self.copies.values():
            copy.wait()


def column_of(sc, slot):
    return (slot // 4) * 4 + ((sc[1] & 3) ^ (slot & 3))


def weight_scratch(rows, cols, n):
    lead = len(lead_table(rows, cols))
    return [VMEM((cols, D, n), BF), pltpu.SemaphoreType.DMA((8, lead))]


def lanes(start, width):
    return pl.ds(pl.multiple_of(start, width), width)


def prep_kernel(wq, wp, w1, w2, out_q, out_a, out_b):
    hid = wq.shape[2]
    half = w1.shape[1] // 2
    for c in range(3):
        out_q[:, c * hid : (c + 1) * hid] = wq[c]
    out_q[:, 3 * hid :] = low(wp[...].astype(F32).T)
    out_a[:, :half] = w1[:, :half]
    out_b[:, :half] = w1[:, half:]
    out_a[:, half:] = low(w2[:half].astype(F32).T)
    out_b[:, half:] = low(w2[half:].astype(F32).T)


def tokens_of(ref, cols):
    return jnp.concatenate([ref[c, :SEQ, :] for c in range(cols)], axis=1).astype(F32)


def front_kernel(lead, cols, *refs):
    sc = refs[0]
    pieces = refs[1:9]
    (xa, closed, gain, shift, q_down, q_up, p_down, p_up, f_down, bias_out) = refs[9:19]
    (n1, lat1, q, k, v, lse, att, lat2, middle, n2, lat3) = refs[19:30]
    w, sems, hidden, branch = refs[30:]
    weights = Weights(sc, pieces, w, sems, lead)
    weights.start()
    a = sc[0]
    hid = D // cols
    x = tokens_of(xa, cols)
    hidden[...] = x
    unit, _ = norm_parts(x)
    n1[...] = low(unit * gain[0:1] + shift[0:1])
    lat1[...] = low(mm(n1[...], q_down[a], NT))
    weights.wait()

    def project(slot, _):
        block = column_of(sc, slot)
        up = jnp.concatenate([q_up[a, :, c, lanes(block * hid, hid)] for c in range(3)], axis=1)
        made = mm(n1[...], w[slot, :, : 3 * hid]) + mm(lat1[...], up)
        bias_q = xa[block, SEQ : SEQ + 1, :].astype(F32)
        bias_v = xa[block, SEQ + 1 : SEQ + 2, :].astype(F32)
        at = lanes(slot * hid, hid)
        q[:, at] = low(made[:, :hid] + bias_q) * jnp.asarray(0.125, BF)
        k[:, at] = low(made[:, hid : 2 * hid])
        v[:, at] = low(made[:, 2 * hid :] + bias_v)
        return 0

    lax.fori_loop(0, cols, project, 0)
    shut = closed[...] > 0.5
    left = lax.broadcasted_iota(jnp.int32, (1, PAIR), 1) < HD

    def attend(pair, _):
        at = lanes(pair * PAIR, PAIR)
        qp, kp, vp = q[:, at], k[:, at], v[:, at]
        v_t = low(vp.astype(F32).T)
        halves = []
        for h in range(2):
            masked = jnp.where(left == (h == 0), qp, jnp.zeros_like(qp))
            s = jnp.where(shut, -1e30, mm(kp, masked, NT))
            top = jnp.max(s, axis=0, keepdims=True)
            e = jnp.exp(s - top)
            total = jnp.sum(e, axis=0, keepdims=True)
            lse[pair, h : h + 1, :] = top + jnp.log(total)
            soft = low(e * (1.0 / total))
            halves.append(mm(v_t[h * HD : (h + 1) * HD], soft))
        att[:, at] = low(jnp.concatenate(halves, axis=0).T)
        return 0

    lax.fori_loop(0, H // 2, attend, 0)

    def down_two(slot, acc):
        block = column_of(sc, slot)
        return acc + mm(att[:, lanes(slot * hid, hid)], p_down[a, :, lanes(block * hid, hid)], NT)

    lat2[...] = low(lax.fori_loop(0, cols, down_two, jnp.zeros((SEQ, R), F32)))
    branch[...] = mm(lat2[...], p_up[a]) + bias_out[0:1].astype(F32)

    def out_proj(slot, _):
        branch[...] += mm(att[:, lanes(slot * hid, hid)], w[slot, :, 3 * hid :], NT)
        return 0

    lax.fori_loop(0, cols, out_proj, 0)
    mid = hidden[...] + branch[...]
    middle[...] = mid
    unit, _ = norm_parts(mid)
    n2[...] = low(unit * gain[1:2] + shift[1:2])
    lat3[...] = low(mm(n2[...], f_down[a], NT))


def ffn_steps(sc, part, cols, w, xa, n2, lat3, gr, glat4, up_1, down_2, acc, early):
    res, gn2, lat4, glat3 = acc
    a = sc[0]
    hid = D // cols
    ffn = FF // cols
    half = ffn // 2
    glat4_t = low(glat4.astype(F32).T)
    lat3_t = low(lat3[...].astype(F32).T)

    def step(slot, _):
        block = column_of(sc, slot)
        at = pl.ds(pl.multiple_of(block * ffn + part * half, half), half)
        bias = jnp.concatenate(
            [xa[block, SEQ + 2 + 2 * part + i : SEQ + 3 + 2 * part + i, :] for i in range(2)], axis=1
        ).astype(F32)
        up, down = up_1[a, :, at], down_2[a, :, at]
        w1, w2 = w[slot, :, :half], w[slot, :, half:]
        pre = mm(n2[...], w1) + mm(lat3[...], up) + bias
        back = mm(gr[...], w2) + mm(glat4, down)
        cumulative = 0.5 * (1.0 + lax.erf(pre * 0.7071067811865476))
        activated = low(pre * cumulative)
        slope = cumulative + pre * jnp.exp(-0.5 * pre * pre) * 0.3989422804014327
        grad_pre = low(back * slope)
        lat4[...] += mm(activated, down, NT)
        glat3[...] += mm(grad_pre, up, NT)
        res[...] += mm(activated, w2, NT)
        gn2[...] += mm(grad_pre, w1, NT)
        early[:, pl.ds(pl.multiple_of(3 * D + block * ffn + part * half, half), half)] = low(
            mm(lat3_t, grad_pre)
        )
        early[:, pl.ds(pl.multiple_of(3 * D + FF + block * ffn + part * half, half), half)] = low(
            mm(glat4_t, activated)
        )
        return 0

    lax.fori_loop(0, cols, step, 0)


def ffn_a_kernel(lead, cols, *refs):
    sc = refs[0]
    pieces = refs[1:9]
    xa, ga, keep, n2, lat3, up_1, down_2, up_2 = refs[9:17]
    res, gn2, lat4, glat3, gr, early = refs[17:23]
    w, sems = refs[23:]
    weights = Weights(sc, pieces, w, sems, lead)
    weights.start()
    gr[...] = low(
        jnp.concatenate([ga[c] for c in range(cols)], axis=1).astype(F32) * keep[...]
    )
    glat4 = low(mm(gr[...], up_2[sc[0]], NT))
    res[...] = jnp.zeros_like(res)
    gn2[...] = jnp.zeros_like(gn2)
    lat4[...] = jnp.zeros_like(lat4)
    glat3[...] = jnp.zeros_like(glat3)
    early[...] = jnp.zeros_like(early)
    weights.wait()
    ffn_steps(
        sc, 0, cols, w, xa, n2, lat3, gr, glat4, up_1, down_2, (res, gn2, lat4, glat3), early
    )


def ffn_b_kernel(lead, cols, *refs):
    sc = refs[0]
    pieces = refs[1:9]
    own_q = refs[9:17]
    (xa, keep, gain, n2, lat3, up_1, down_2, up_2, f_down, p_down, p_up, bias_out) = refs[17:29]
    (middle, att, lat2, gr, res_in, gn2_in, lat4_in, glat3_in, early_in) = refs[29:38]
    layer, gatt, gmid, early = refs[38:42]
    w, sems, wp, sems_p, res, gn2, lat4, glat3 = refs[42:]
    weights = Weights(sc, pieces, w, sems, lead)
    weights.start()
    proj = Weights(sc, own_q, wp, sems_p, lead, 3 * D // cols)
    proj.start()
    a = sc[0]
    hid = D // cols
    glat4 = low(mm(gr[...], up_2[a], NT))
    res[...] = res_in[...]
    gn2[...] = gn2_in[...]
    lat4[...] = lat4_in[...]
    glat3[...] = glat3_in[...]
    early[...] = early_in[...]
    weights.wait()
    ffn_steps(
        sc, 1, cols, w, xa, n2, lat3, gr, glat4, up_1, down_2, (res, gn2, lat4, glat3), early
    )
    mid = middle[...]
    lat4_low = low(lat4[...])
    out = low(
        keep[...] * (mid + res[...] + mm(lat4_low, up_2[a]) + bias_out[1:2].astype(F32))
    )
    for c in range(cols):
        layer[c] = out[:, c * hid : (c + 1) * hid]
    glat3_low = low(glat3[...])
    grad_normed = gn2[...] + mm(glat3_low, f_down[a])
    unit, inverse = norm_parts(mid)
    grad_middle = gr[...].astype(F32) + norm_back(grad_normed, gain[1:2], unit, inverse)
    gmid[...] = grad_middle
    gb = low(grad_middle)
    glat2 = low(mm(gb, p_up[a], NT))
    glat2_t = low(glat2.astype(F32).T)
    early[:, D : 2 * D] = low(mm(low(lat2[...].astype(F32).T), gb))
    early[:, 2 * D : 3 * D] = low(mm(low(glat3_low.astype(F32).T), n2[...]))
    early[:, 3 * D + 2 * FF :] = low(mm(low(lat4_low.astype(F32).T), gr[...]))
    proj.wait()

    def step(slot, _):
        block = column_of(sc, slot)
        here = lanes(slot * hid, hid)
        there = lanes(block * hid, hid)
        gatt[:, here] = low(mm(gb, wp[slot]) + mm(glat2, p_down[a, :, there]))
        early[:, there] = low(mm(glat2_t, att[:, here]))
        return 0

    lax.fori_loop(0, cols, step, 0)


def attention_back_kernel(cols, *refs):
    sc = refs[0]
    closed, q, k, v, lse, gatt, lat1, n1, q_up = refs[1:10]
    gq, gk, gv, glat1, late = refs[10:15]
    a = sc[0]
    hid = D // cols
    shut = closed[...] > 0.5
    left = lax.broadcasted_iota(jnp.int32, (1, PAIR), 1) < HD

    def attend(pair, _):
        at = lanes(pair * PAIR, PAIR)
        qp, kp, vp, gp = q[:, at], k[:, at], v[:, at], gatt[:, at]
        k_t = low(kp.astype(F32).T)
        by_q, by_k, by_v = [], [], []
        for h in range(2):
            mine = left == (h == 0)
            zero = jnp.zeros_like(qp)
            s = jnp.where(shut, -1e30, mm(kp, jnp.where(mine, qp, zero), NT))
            soft = jnp.exp(s - lse[pair, h : h + 1, :])
            grad_soft = mm(vp, jnp.where(mine, gp, zero), NT)
            total = jnp.sum(grad_soft * soft, axis=0, keepdims=True)
            grad_scores = low(soft * (grad_soft - total))
            by_v.append(mm(low(soft), gp))
            by_k.append(mm(grad_scores, qp))
            by_q.append(mm(k_t[h * HD : (h + 1) * HD], grad_scores))
        gq[:, at] = low(jnp.concatenate(by_q, axis=0).T * 0.125)
        gk[:, at] = low(jnp.where(left, by_k[0], by_k[1]))
        gv[:, at] = low(jnp.where(left, by_v[0], by_v[1]))
        return 0

    lax.fori_loop(0, H // 2, attend, 0)
    lat1_t = low(lat1[...].astype(F32).T)

    def step(slot, acc):
        block = column_of(sc, slot)
        here = lanes(slot * hid, hid)
        there = lanes(block * hid, hid)
        for c, g in enumerate((gq, gk, gv)):
            grad = g[:, here]
            acc = acc + mm(grad, q_up[a, :, c, there], NT)
            late[:, pl.ds(pl.multiple_of((c + 1) * D + block * hid, hid), hid)] = low(
                mm(lat1_t, grad)
            )
        return acc

    made = low(lax.fori_loop(0, cols, step, jnp.zeros((SEQ, R), F32)))
    glat1[...] = made
    late[:, :D] = low(mm(low(made.astype(F32).T), n1[...]))


def back_kernel(lead, cols, *refs):
    sc = refs[0]
    pieces = refs[1:9]
    xa, gain, gq, gk, gv, glat1, q_down, gmid = refs[9:17]
    out = refs[17]
    w, sems, acc = refs[18:]
    weights = Weights(sc, pieces, w, sems, lead)
    weights.start()
    hid = D // cols
    acc[...] = mm(glat1[...], q_down[sc[0]])
    x = tokens_of(xa, cols)
    unit, inverse = norm_parts(x)
    weights.wait()

    def step(slot, _):
        here = lanes(slot * hid, hid)
        grad = jnp.concatenate([gq[:, here], gk[:, here], gv[:, here]], axis=1)
        acc[...] += mm(grad, w[slot, :, : 3 * hid], NT)
        return 0

    lax.fori_loop(0, cols, step, 0)
    made = low(gmid[...] + norm_back(acc[...], gain[0:1], unit, inverse))
    for c in range(cols):
        out[c] = made[:, c * hid : (c + 1) * hid]


def sum_kernel(owners, mine, out, acc):
    acc[...] = jnp.zeros_like(acc)
    for d in range(mine.shape[0]):
        acc[owners[d]] += mine[d].astype(F32)
    out[...] = low(acc[...])


def spread_kernel(spans, part, table, whole, *outs):
    for b in range(whole.shape[0] * part // 128):
        lane = b * 128
        block = whole[table.index(lane // part), :, lane % part : lane % part + 128].astype(F32)
        for out, (start, width) in zip(outs, spans):
            if start <= lane < start + width:
                out[:, lane - start : lane - start + 128] = block


def sum_adapters(grads, owners, spans):
    rows, cols = sizes()
    devices = rows * cols
    width = grads.shape[-1]
    part = width // devices
    pieces = grads.reshape(R, devices, part).transpose(1, 0, 2)
    mine = lax.all_to_all(pieces, BOTH, split_axis=0, concat_axis=0, tiled=True)
    summed = call(
        sum_kernel,
        jax.ShapeDtypeStruct((NA, R, part), BF),
        [owners, mine],
        [pltpu.SMEM, VMEM],
        [VMEM((NA, R, part), F32)],
        moved=4 * mine.size,
    )
    whole = gather_leading(summed.reshape(NA * R, part))
    if part % 128 == 0:
        return call(
            functools.partial(spread_kernel, spans, part, all_table(rows, cols)),
            [jax.ShapeDtypeStruct((NA * R, n), F32) for _, n in spans],
            [whole],
            [VMEM],
            moved=6 * whole.size,
        )
    table = all_table(rows, cols)
    whole = whole[jnp.array([table.index(d) for d in range(devices)])]
    flat = jnp.swapaxes(whole, 0, 1).reshape(NA * R, width).astype(F32)
    return [flat[:, s : s + n] for s, n in spans]


def per_device(
    tokens_in,
    grad_out,
    keep_mask,
    adapter_index,
    ln_gain,
    ln_shift,
    w_qkv,
    bias_qv,
    w_proj,
    w_fc1,
    bias_fc1,
    w_fc2,
    bias_out,
    qkv_down,
    qkv_up,
    proj_down,
    proj_up,
    fc1_down,
    fc1_up,
    fc2_down,
    fc2_up,
):
    rows, cols = sizes()
    row, column = lax.axis_index("row"), lax.axis_index("col")
    assert adapter_index.shape[0] == cols and cols >= 4 and rows >= 2
    hid = D // cols
    n = 4 * hid
    blk = D // rows
    lead = lead_table(rows, cols)

    biases = jnp.concatenate(
        [bias_qv, bias_fc1.reshape(4, hid), jnp.zeros((EXTRA - 6, hid), BF)], axis=0
    )
    tokens = jnp.concatenate(
        [tokens_in.reshape(cols, SEQ, hid), jnp.broadcast_to(biases, (cols, EXTRA, hid))], axis=1
    )
    xa = lax.all_to_all(tokens, "col", split_axis=0, concat_axis=0, tiled=True)
    ga = lax.all_to_all(
        grad_out.reshape(cols, SEQ, hid), "col", split_axis=0, concat_axis=0, tiled=True
    )
    shard = jax.ShapeDtypeStruct((blk, n), BF)
    shard_q, shard_a, shard_b = call(
        prep_kernel, [shard] * 3, [w_qkv, w_proj, w_fc1, w_fc2], [VMEM] * 4, moved=12 * blk * n
    )
    pieces_q = gather_pieces(shard_q)
    pieces_a = gather_pieces(shard_a)
    pieces_b = gather_pieces(shard_b)
    owners = gather_owners(adapter_index)

    mask_row = lax.dynamic_index_in_dim(keep_mask, column, 0, keepdims=False)
    keep = jnp.concatenate([jnp.ones((BUF,), F32), mask_row.astype(F32)]).reshape(SEQ, 1)
    closed = 1.0 - keep
    adapter = lax.dynamic_index_in_dim(adapter_index, column, 0, keepdims=False)
    sc = jnp.stack([adapter, column, column % 2, row % 2]).astype(jnp.int32)

    def shaped(width, dtype, height=SEQ):
        return jax.ShapeDtypeStruct((height, width), dtype)

    big, small = shaped(D, BF), shaped(R, BF)
    scratch = weight_scratch(rows, cols, n)
    flops = 2 * SEQ * D * D
    any_space = [pl.ANY] * 8
    n1, lat1, q, k, v, lse, att, lat2, middle, n2, lat3 = call(
        functools.partial(front_kernel, lead, cols),
        [
            big,
            small,
            big,
            big,
            big,
            jax.ShapeDtypeStruct((H // 2, 2, SEQ), F32),
            big,
            small,
            shaped(D, F32),
            big,
            small,
        ],
        [sc, *pieces_q, xa, closed, ln_gain, ln_shift, qkv_down, qkv_up, proj_down, proj_up]
        + [fc1_down, bias_out],
        [pltpu.SMEM] + any_space + [VMEM] * 10,
        scratch + [VMEM((SEQ, D), F32), VMEM((SEQ, D), F32)],
        flops=5 * flops,
        moved=8 * D * D + 16 * SEQ * D,
    )
    wide = shaped(D, F32)
    thin = shaped(R, F32)
    res, gn2, lat4, glat3, gr, early = call(
        functools.partial(ffn_a_kernel, lead, cols),
        [wide, wide, thin, thin, big, shaped(EARLY, BF, R)],
        [sc, *pieces_a, xa, ga, keep, n2, lat3, fc1_up, fc2_down, fc2_up],
        [pltpu.SMEM] + any_space + [VMEM] * 8,
        scratch,
        flops=8 * flops,
        moved=8 * D * D + 16 * SEQ * D,
    )
    layer, gatt, gmid, early = call(
        functools.partial(ffn_b_kernel, lead, cols),
        [jax.ShapeDtypeStruct((cols, SEQ, hid), BF), big, wide, shaped(EARLY, BF, R)],
        [sc, *pieces_b, *pieces_q, xa, keep, ln_gain, n2, lat3, fc1_up, fc2_down, fc2_up]
        + [fc1_down, proj_down, proj_up, bias_out]
        + [middle, att, lat2, gr, res, gn2, lat4, glat3, early],
        [pltpu.SMEM] + any_space * 2 + [VMEM] * 21,
        scratch
        + [VMEM((cols, D, hid), BF), scratch[1]]
        + [VMEM((SEQ, D), F32), VMEM((SEQ, D), F32), VMEM((SEQ, R), F32), VMEM((SEQ, R), F32)],
        flops=10 * flops,
        moved=10 * D * D + 24 * SEQ * D,
    )
    layer = lax.all_to_all(layer, "col", split_axis=0, concat_axis=0, tiled=True)
    early_sum = sum_adapters(
        early,
        owners,
        ((0, D), (D, D), (2 * D, D), (3 * D, FF), (3 * D + FF, FF), (3 * D + 2 * FF, D)),
    )
    gq, gk, gv, glat1, late = call(
        functools.partial(attention_back_kernel, cols),
        [big, big, big, small, shaped(LATE, BF, R)],
        [sc, closed, q, k, v, lse, gatt, lat1, n1, qkv_up],
        [pltpu.SMEM] + [VMEM] * 9,
        flops=5 * flops,
        moved=16 * SEQ * D,
    )
    late_sum = sum_adapters(late, owners, ((0, D), (D, D), (2 * D, D), (3 * D, D)))
    grad_in = call(
        functools.partial(back_kernel, lead, cols),
        jax.ShapeDtypeStruct((cols, SEQ, hid), BF),
        [sc, *pieces_q, xa, ln_gain, gq, gk, gv, glat1, qkv_down, gmid],
        [pltpu.SMEM] + any_space + [VMEM] * 8,
        scratch + [VMEM((SEQ, D), F32)],
        flops=3 * flops,
        moved=8 * D * D + 8 * SEQ * D,
    )
    grad_in = lax.all_to_all(grad_in, "col", split_axis=0, concat_axis=0, tiled=True)

    def split(table, last=()):
        return table.reshape((NA, R) + last + (-1,))

    g_qkv_up = jnp.stack([split(t) for t in late_sum[1:]], axis=2)
    return (
        layer.reshape(cols * SEQ, hid),
        grad_in.reshape(cols * SEQ, hid),
        split(late_sum[0]),
        g_qkv_up,
        split(early_sum[0]),
        split(early_sum[1]),
        split(early_sum[2]),
        split(early_sum[3]),
        split(early_sum[4]),
        split(early_sum[5]),
    )


def solution(mesh):
    return jax.shard_map(
        per_device,
        mesh=mesh,
        in_specs=(
            P("row", "col"),
            P("row", "col"),
            P("row", None),
            P("row"),
            P(),
            P(),
            P(None, "row", "col"),
            P(None, "col"),
            P("col", "row"),
            P("row", "col"),
            P("col"),
            P("col", "row"),
            P(),
            P(),
            P(),
            P(),
            P(),
            P(),
            P(),
            P(),
            P(),
        ),
        out_specs=(P("row", "col"), P("row", "col"), P(), P(), P(), P(), P(), P(), P(), P()),
        check_vma=False,
    )
```

time: 635 us -> 387 us (0.61); the launches traced: 625 us -> 385 us
  waiting for transfers between devices: 391 us -> 153 us
  Pallas kernels: 0 us -> 119 us
  matrix products: 107 us -> 0 us
  starting transfers between devices: 14.3 us -> 84.4 us
  blocking collectives: 47.4 us -> 0 us
  local copies, waits for them, and re-layouts: 38.4 us -> 21.4 us
  between operations: 15.6 us -> 1.02 us
    all_gather x7 -> x0, waiting for transfers between devices: 218 us -> none  [the longest x1 50.6 us: per_device(): lax.all_gather(fc1_cols, 'col', axis=1, tiled=True)]
    ppermute x0 -> x46, waiting for transfers between devices: none -> 142 us  [swap(): return lax.ppermute(block, BOTH, pairs)]
    psum x1 -> x0, waiting for transfers between devices: 139 us -> none  [per_device(): lax.psum((grads[0], grads[1], grads[2], grads[3], grads[4], grads[5], gra...]
    pallas_call x0 -> x21, Pallas kernels: none -> 119 us  [call(): pl.pallas_call(kernel, out_shape=outs, in_specs=[pl.BlockSpec(memory_spac...]
    dot_general x38 -> x0, matrix products: 107 us -> none  [the longest x22 62.5 us: narrow_dot(): jnp.einsum(formula, left_side, right_side, preferred_element_type=jnp.flo...]
    ppermute x0 -> x46, starting transfers between devices: none -> 55.9 us  [swap(): return lax.ppermute(block, BOTH, pairs)]
    all_gather x3 -> x0, blocking collectives: 47.4 us -> none  [the longest x1 31.2 us: per_device(): lax.all_gather(w_proj, 'row', axis=1, tiled=True)]
    all_to_all x4 -> x6, waiting for transfers between devices: 31.1 us -> 11.2 us  [the longest x1 10.5 us: per_device(): lax.all_to_all(layer, 'col', split_axis=0, concat_axis=0, tiled=True)]
  transfers between devices with their start and end apart: 12 -> 52, of which waited for: 10 -> 23; matrix products, arithmetic and copies ran while one was open for 11% -> 4% of each run, Pallas kernels for 0% -> 20%
where the time goes in v2:
time: 387 us; the launch traced here: 385 us
  waiting for transfers between devices  153 us (40%)
  Pallas kernels  119 us (31%)
  starting transfers between devices  84.4 us (22%)
  local copies, waits for them, and re-layouts  21.4 us (6%)
  other arithmetic  6.73 us (2%)
    ppermute x46, waiting for transfers between devices, swap(): return lax.ppermute(block, BOTH, pairs)  142 us
    pallas_call x21, Pallas kernels, call(): pl.pallas_call(kernel, out_shape=outs, in_specs=[pl.BlockSpec(memory_spac...  119 us
    ppermute x46, starting transfers between devices, swap(): return lax.ppermute(block, BOTH, pairs)  55.9 us
    unnamed x83, local copies, waits for them, and re-layouts  15 us
    all_to_all x2, starting transfers between devices, sum_adapters(): mine = lax.all_to_all(pieces, BOTH, split_axis=0, concat_axis=0, tiled=True)  13.8 us
    all_to_all x1, waiting for transfers between devices, per_device(): lax.all_to_all(layer, 'col', split_axis=0, concat_axis=0, tiled=True)  10.5 us
  transfers between devices with their start and end apart: 52, of which 23 were waited for; matrix products, arithmetic and copies ran while one was open for 4% of the time, Pallas kernels for 20%

profile of v2, /device:TPU:0, one launch (start us, length us, event | category | flops | bytes accessed | tf_op | source)
XLA Modules:
  0.0 385.5 jit_solution(16432921819593522964)
XLA Ops:
  0.6 2.2 shard_map.276
  2.8 3.0 collective-permute-start.10
  5.8 2.6 collective-permute-start.11
  8.4 8.8 %collective-permute-done.10.refs_1_ = bf16[128,1024]{1,0:T(8,128)(2,1)S(1)} collective-permute-done((bf16[128,1024]{1,0:T(8,128)(2,1)}, bf16[128,1024]{1,0:T(8,128)(2,1)S(1)}, u32[]{:S(2)}, u32[]{:S(2)}) %collective-permute-start.10) | collective-permute-done | bytes 262176 | tf_op jit(solution)/shard_map/ppermute | solution.py:76
  17.2 10.2 %collective-permute-done.11.refs_2_ = bf16[128,1024]{1,0:T(8,128)(2,1)S(1)} collective-permute-done((bf16[128,1024]{1,0:T(8,128)(2,1)}, bf16[128,1024]{1,0:T(8,128)(2,1)S(1)}, u32[]{:S(2)}, u32[]{:S(2)}) %collective-permute-start.11) | collective-permute-done | bytes 262176 | tf_op jit(solution)/shard_map/ppermute | solution.py:76
  28.2 2.2 shard_map.278.refs_1_.refs_9_
  31.9 4.7 %collective-permute-start.20 = (bf16[128,1024]{1,0:T(8,128)(2,1)S(1)}, bf16[128,1024]{1,0:T(8,128)(2,1)S(1)}, u32[]{:S(2)}, u32[]{:S(2)}) collective-permute-start(bf16[128,1024]{1,0:T(8,128)(2,1)S(1)} %copy-done.17), channel_id=1, source_target_pairs={{0,8},{1,9},{2,10},{3,11},{4,12},{5,13},{6,14},{7,15},{8,0},{9,1},... | collective-permute-start | bytes 786440 | tf_op jit(solution)/shard_map/ppermute | solution.py:76
  40.6 5.1 %collective-permute-done.20.refs_1_ = bf16[128,1024]{1,0:T(8,128)(2,1)S(1)} collective-permute-done((bf16[128,1024]{1,0:T(8,128)(2,1)S(1)}, bf16[128,1024]{1,0:T(8,128)(2,1)S(1)}, u32[]{:S(2)}, u32[]{:S(2)}) %collective-permute-start.20) | collective-permute-done | bytes 262176 | tf_op jit(solution)/shard_map/ppermute | solution.py:76
  45.9 12.1 %collective-permute-done.21.refs_2_ = bf16[128,1024]{1,0:T(8,128)(2,1)S(1)} collective-permute-done((bf16[128,1024]{1,0:T(8,128)(2,1)S(1)}, bf16[128,1024]{1,0:T(8,128)(2,1)S(1)}, u32[]{:S(2)}, u32[]{:S(2)}) %collective-permute-start.21) | collective-permute-done | bytes 262176 | tf_op jit(solution)/shard_map/ppermute | solution.py:76
  58.0 2.5 collective-permute-start.2
  60.6 2.2 shard_map.280.refs_1_
  62.9 17.6 %collective-permute-done.1.refs_2_ = bf16[128,1024]{1,0:T(8,128)(2,1)S(1)} collective-permute-done((bf16[128,1024]{1,0:T(8,128)(2,1)S(1)}, bf16[128,1024]{1,0:T(8,128)(2,1)S(1)}, u32[]{:S(2)}, u32[]{:S(2)}) %collective-permute-start.1) | collective-permute-done | bytes 262176 | tf_op jit(solution)/shard_map/ppermute | solution.py:76
  82.5 2.6 shard_map.277.refs_1_
  85.7 1.5 collective-permute-start.4
  87.2 19.5 %collective-permute-done.23.refs_2_ = bf16[4,128,1024]{2,1,0:T(8,128)(2,1)S(1)} collective-permute-done((bf16[4,128,1024]{2,1,0:T(8,128)(2,1)}, bf16[4,128,1024]{2,1,0:T(8,128)(2,1)S(1)}, u32[]{:S(2)}, u32[]{:S(2)}) %collective-permute-start.23) | collective-permute-done | bytes 1048608 | tf_op jit(solution)/shard_map/ppermute | solution.py:76
  108.0 21.4 %collective-permute-done.3.refs_2_ = bf16[4,128,1024]{2,1,0:T(8,128)(2,1)} collective-permute-done((bf16[4,128,1024]{2,1,0:T(8,128)(2,1)}, bf16[4,128,1024]{2,1,0:T(8,128)(2,1)}, u32[]{:S(2)}, u32[]{:S(2)}) %collective-permute-start.3) | collective-permute-done | bytes 1048608 | tf_op jit(solution)/shard_map/ppermute | solution.py:76
  129.9 3.9 %collective-permute-done.15.refs_4_.refs_12_ = bf16[4,128,1024]{2,1,0:T(8,128)(2,1)} collective-permute-done((bf16[4,128,1024]{2,1,0:T(8,128)(2,1)S(1)}, bf16[4,128,1024]{2,1,0:T(8,128)(2,1)}, u32[]{:S(2)}, u32[]{:S(2)}) %collective-permute-start.15) | collective-permute-done | bytes 1048608 | tf_op jit(solution)/shard_map/ppermute | solution.py:76
  135.0 1.7 collective-permute-start.5
  137.9 2.0 pad_maximum_fusion.1
  139.9 3.5 all-to-all-start
  143.4 1.6 collective-permute-done.25.refs_4_
  146.8 9.5 %collective-permute-done.5.refs_4_ = bf16[4,128,1024]{2,1,0:T(8,128)(2,1)} collective-permute-done((bf16[4,128,1024]{2,1,0:T(8,128)(2,1)}, bf16[4,128,1024]{2,1,0:T(8,128)(2,1)}, u32[]{:S(2)}, u32[]{:S(2)}) %collective-permute-start.5) | collective-permute-done | bytes 1048608 | tf_op jit(solution)/shard_map/ppermute | solution.py:76
  156.2 4.6 %collective-permute-start.8 = (bf16[4,128,1024]{2,1,0:T(8,128)(2,1)}, bf16[4,128,1024]{2,1,0:T(8,128)(2,1)}, u32[]{:S(2)}, u32[]{:S(2)}) collective-permute-start(bf16[4,128,1024]{2,1,0:T(8,128)(2,1)} %copy-done.10), channel_id=1, source_target_pairs={{0,1},{1,0},{2,3},{3,2},{4,5},{5,4},{6,7},{7,6},{8,9},{9,8},{10,11... | collective-permute-start | bytes 3145736 | tf_op jit(solution)/shard_map/ppermute | solution.py:76
  162.8 4.3 %all-to-all-start.1 = ((bf16[4,320,256]{2,1,0:T(8,128)(2,1)}), bf16[4,320,256]{2,1,0:T(8,128)(2,1)S(1)}, u32[]{:S(2)}, u32[]{:S(2)}) async-start(bf16[4,320,256]{2,1,0:T(8,128)(2,1)} %bitcast.88), calls=%async_computation.1 | async-start | bytes 1310720 | tf_op jit(solution)/shard_map/all_to_all | solution.py:613
  167.9 2.8 copy.37.refs_14_.refs_9_
  172.7 20.8 %shard_map.279 = (bf16[320,1024]{1,0:T(8,128)(2,1)}, bf16[320,16]{1,0:T(8,128)(2,1)}, bf16[320,1024]{1,0:T(8,128)(2,1)}, bf16[320,1024]{1,0:T(8,128)(2,1)}, bf16...) custom-call(s32[4]{0:T(128)} %pad_add_fusion.2.refs_0_, ...), custom_call_target="tpu_custom_call" | custom-call | flops 3355443200 | bytes 13631488 | tf_op jit(solution)/shard_map/pallas_call | solution.py:54
  194.3 15.5 %shard_map.281 = (f32[320,1024]{1,0:T(8,128)}, f32[320,1024]{1,0:T(8,128)}, f32[320,16]{1,0:T(8,128)}, f32[320,16]{1,0:T(8,128)}, bf16[320,1024]{1,0:T(8,128)(2,1)}, /*index=5*/bf16[16,12288]{1,0:T(8,128)(2,1)}) custom-call(s32[4]{0:T(128)} %pad_add_fusion.2.refs_0_, bf16[4,128,1024]{2,1,0:T(8,128)(2,1)} %shard_map.280.refs_1_, ...), custom_call_target="tpu_custom_call" | custom-call | flops 5368709120 | bytes 13631488 | tf_op jit(solution)/shard_map/pallas_call | solution.py:54
  209.9 21.5 %shard_map.282 = (bf16[4,320,256]{2,1,0:T(8,128)(2,1)}, bf16[320,1024]{1,0:T(8,128)(2,1)}, f32[320,1024]{1,0:T(8,128)}, bf16[16,12288]{1,0:T(8,128)(2,1)}) custom-call(s32[4]{0:T(128)} %pad_add_fusion.2.refs_0_, bf16[4,128,1024]{2,1,0:T(8,128)(2,1)} %shard_map.277.refs_1_, bf16[4,128,1024]{2,1,0:T(8,128)(2,1)} %collective-permute-done.3.refs_2_, ...), custom_call_target="tpu_custom_call" | custom-call | flops 6710886400 | bytes 18350080 | tf_op jit(solution)/shard_map/pallas_call | solution.py:54
  231.4 1.8 copy.51
  233.2 7.3 %all-to-all-start.5 = ((bf16[32,16,384]{2,1,0:T(8,128)(2,1)}), bf16[32,16,384]{2,1,0:T(8,128)(2,1)S(1)}, u32[]{:S(2)}, u32[]{:S(2)}) async-start(bf16[32,16,384]{2,1,0:T(8,128)(2,1)} %bitcast.71), calls=%async_computation.5 | async-start | bytes 786432 | tf_op jit(solution)/shard_map/all_to_all | solution.py:551
  240.6 1.6 collective-permute-start.30
  242.2 1.9 collective-permute-done.30
  244.7 1.6 collective-permute-start.31
  246.4 2.4 collective-permute-start.32
  249.2 3.4 collective-permute-done.32
  256.1 1.8 shard_map.291
  258.9 3.4 collective-permute-start.42
  262.8 4.3 %collective-permute-done.41.refs_2_ = bf16[128,384]{1,0:T(8,128)(2,1)S(1)} collective-permute-done((bf16[128,384]{1,0:T(8,128)(2,1)}, bf16[128,384]{1,0:T(8,128)(2,1)S(1)}, u32[]{:S(2)}, u32[]{:S(2)}) %collective-permute-start.41) | collective-permute-done | bytes 98336 | tf_op jit(solution)/shard_map/ppermute | solution.py:76
  268.4 1.8 shard_map.292
  271.7 6.5 %collective-permute-done.43 = bf16[4,128,384]{2,1,0:T(8,128)(2,1)S(1)} collective-permute-done((bf16[4,128,384]{2,1,0:T(8,128)(2,1)}, bf16[4,128,384]{2,1,0:T(8,128)(2,1)S(1)}, u32[]{:S(2)}, u32[]{:S(2)}) %collective-permute-start.43) | collective-permute-done | bytes 393248 | tf_op jit(solution)/shard_map/ppermute | solution.py:76
  278.9 2.1 shard_map.293
  281.0 2.7 collective-permute-start.44
  283.7 13.2 %shard_map.283 = (bf16[320,1024]{1,0:T(8,128)(2,1)}, bf16[320,1024]{1,0:T(8,128)(2,1)}, bf16[320,1024]{1,0:T(8,128)(2,1)}, bf16[320,16]{1,0:T(8,128)(2,1)}, bf16[16,4096]{1,0:T(8,128)(2,1)}) custom-call(s32[4]{0:T(128)} %pad_add_fusion.2.refs_0_, f32[320,1]{1,0:T(8,128)} %sub.11.refs_10_.refs_1_, bf16[320,1024]{1,0:T(8,128)(2,1)} %get-tuple-element.64.refs_2_, ...), custom_call_target="tpu_custom_call" | custom-call | flops 3355443200 | bytes 5242880 | tf_op jit(solution)/shard_map/pallas_call | solution.py:54
  297.8 2.7 shard_map.294
  301.1 6.4 %all-to-all-start.4 = ((bf16[32,16,128]{2,1,0:T(8,128)(2,1)}), bf16[32,16,128]{2,1,0:T(8,128)(2,1)S(1)}, u32[]{:S(2)}, u32[]{:S(2)}) async-start(bf16[32,16,128]{2,1,0:T(8,128)(2,1)} %bitcast_bitcast_fusion.1), calls=%async_computation.4 | async-start | bytes 262144 | tf_op jit(solution)/shard_map/all_to_all | solution.py:551
  307.6 10.2 %shard_map.284 = bf16[4,320,256]{2,1,0:T(8,128)(2,1)} custom-call(s32[4]{0:T(128)} %pad_add_fusion.2.refs_0_, bf16[4,128,1024]{2,1,0:T(8,128)(2,1)} %shard_map.278.refs_1_.refs_9_, bf16[4,128,1024]{2,1,0:T(8,128)(2,1)} %copy-done.2, bf16[4,128,1024]{2,1,0:T(8,128)(2,1)} %copy-done.3, bf16[4,128,1024]{2,1,0:T(8,128)(2,1)} %collective-permute-done.15.refs_4_.refs_12_, ...), custom_call_target="tpu_custom_call" | custom-call | flops 2013265920 | bytes 11010048 | tf_op jit(solution)/shard_map/pallas_call | solution.py:54
  317.8 3.5 all-to-all-start.3
  321.4 1.6 shard_map.285
  323.0 1.8 collective-permute-start.34
  324.8 2.4 collective-permute-start.35
  327.4 3.0 collective-permute-done.35.refs_2_
  330.4 2.7 collective-permute-done.36.refs_3_
  336.7 3.7 collective-permute-done.37
  341.0 1.7 shard_map.287
  342.7 2.0 collective-permute-start.38
  344.7 4.6 %collective-permute-done.38 = bf16[2,4,128,128]{3,2,1,0:T(8,128)(2,1)S(1)} collective-permute-done((bf16[2,4,128,128]{3,2,1,0:T(8,128)(2,1)}, bf16[2,4,128,128]{3,2,1,0:T(8,128)(2,1)S(1)}, u32[]{:S(2)}, u32[]{:S(2)}) %collective-permute-start.38) | collective-permute-done | bytes 262176 | tf_op jit(solution)/shard_map/ppermute | solution.py:76
  350.0 1.9 shard_map.288
  351.9 3.5 all-to-all-start.2
  355.4 10.5 %all-to-all-done.2 = bf16[4,320,256]{2,1,0:T(8,128)(2,1)S(1)} async-done(((bf16[4,320,256]{2,1,0:T(8,128)(2,1)}), bf16[4,320,256]{2,1,0:T(8,128)(2,1)S(1)}, u32[]{:S(2)}, u32[]{:S(2)}) %all-to-all-start.2) | async-done | bytes 655392 | tf_op jit(solution)/shard_map/all_to_all | solution.py:684
  366.7 2.2 shard_map.289
  368.9 2.6 shard_map.290
  371.5 2.7 pad_maximum_fusion
  375.3 3.8 shard_map.295
  379.1 4.7 %shard_map.296 = (f32[128,1024]{1,0:T(8,128)}, f32[128,1024]{1,0:T(8,128)}, f32[128,1024]{1,0:T(8,128)}, f32[128,4096]{1,0:T(8,128)}, f32[128,4096]{1,0:T(8,128)}, /*index=5*/f32[128,1024]{1,0:T(8,128)}) custom-call(bf16[32,128,384]{2,1,0:T(8,128)(2,1)} %bitcast.72), custom_call_target="tpu_custom_call" | custom-call | bytes 9437184 | tf_op jit(solution)/shard_map/pallas_call | solution.py:54
  (168 shorter events, 40.5 us)
Async XLA Ops:
  2.8 29.1 %copy-start.17 = (bf16[128,1024]{1,0:T(8,128)(2,1)S(1)}, bf16[128,1024]{1,0:T(8,128)(2,1)}, u32[]{:S(2)}) copy-start(bf16[128,1024]{1,0:T(8,128)(2,1)} %get-tuple-element.56.refs_0_) | copy-start | bytes 786436
  2.8 42.9 %copy-start.16 = (bf16[128,1024]{1,0:T(8,128)(2,1)S(1)}, bf16[128,1024]{1,0:T(8,128)(2,1)}, u32[]{:S(2)}) copy-start(bf16[128,1024]{1,0:T(8,128)(2,1)} %get-tuple-element.49.refs_0_) | copy-start | bytes 786436
  2.8 14.4 %collective-permute-start.10 = (bf16[128,1024]{1,0:T(8,128)(2,1)}, bf16[128,1024]{1,0:T(8,128)(2,1)S(1)}, u32[]{:S(2)}, u32[]{:S(2)}) collective-permute-start(bf16[128,1024]{1,0:T(8,128)(2,1)} %get-tuple-element.50.refs_0_), channel_id=1, source_target_pairs={{0,8},{1,9},{2,10},{3,11},{4,12},{5,13},{6,14},{7,15},{8,0},{9,1},... | collective-permute-start | bytes 786440 | tf_op jit(solution)/shard_map/ppermute | solution.py:76
  5.8 21.6 %collective-permute-start.11 = (bf16[128,1024]{1,0:T(8,128)(2,1)}, bf16[128,1024]{1,0:T(8,128)(2,1)S(1)}, u32[]{:S(2)}, u32[]{:S(2)}) collective-permute-start(bf16[128,1024]{1,0:T(8,128)(2,1)} %get-tuple-element.50.refs_0_), channel_id=1, source_target_pairs={{0,16},{1,17},{2,18},{3,19},{4,20},{5,21},{6,22},{7,23},{8,24},{9,... | collective-permute-start | bytes 786440 | tf_op jit(solution)/shard_map/ppermute | solution.py:76
  8.4 19.0 %collective-permute-start.12 = (bf16[128,1024]{1,0:T(8,128)(2,1)}, bf16[128,1024]{1,0:T(8,128)(2,1)S(1)}, u32[]{:S(2)}, u32[]{:S(2)}) collective-permute-start(bf16[128,1024]{1,0:T(8,128)(2,1)} %get-tuple-element.50.refs_0_), channel_id=1, source_target_pairs={{0,24},{1,25},{2,26},{3,27},{4,28},{5,29},{6,30},{7,31},{8,16},{9,... | collective-permute-start | bytes 786440 | tf_op jit(solution)/shard_map/ppermute | solution.py:76
  30.4 32.4 %copy-start = (bf16[4,128,1024]{2,1,0:T(8,128)(2,1)S(1)}, bf16[4,128,1024]{2,1,0:T(8,128)(2,1)}, u32[]{:S(2)}) copy-start(bf16[4,128,1024]{2,1,0:T(8,128)(2,1)} %shard_map.278.refs_1_.refs_9_) | copy-start | bytes 3145732
  30.4 52.0 %collective-permute-start.13 = (bf16[4,128,1024]{2,1,0:T(8,128)(2,1)}, bf16[4,128,1024]{2,1,0:T(8,128)(2,1)S(1)}, u32[]{:S(2)}, u32[]{:S(2)}) collective-permute-start(bf16[4,128,1024]{2,1,0:T(8,128)(2,1)} %shard_map.278.refs_1_.refs_9_), channel_id=1, source_target_pairs={{0,2},{1,5},{2,0},{3,7},{4,6},{5,1},{6,4},{7,3},{8,10},{9,13},{10,... | collective-permute-start | bytes 3145736 | tf_op jit(solution)/shard_map/ppermute | solution.py:76
  31.9 13.7 %collective-permute-start.20 = (bf16[128,1024]{1,0:T(8,128)(2,1)S(1)}, bf16[128,1024]{1,0:T(8,128)(2,1)S(1)}, u32[]{:S(2)}, u32[]{:S(2)}) collective-permute-start(bf16[128,1024]{1,0:T(8,128)(2,1)S(1)} %copy-done.17), channel_id=1, source_target_pairs={{0,8},{1,9},{2,10},{3,11},{4,12},{5,13},{6,14},{7,15},{8,0},{9,1},... | collective-permute-start | bytes 786440 | tf_op jit(solution)/shard_map/ppermute | solution.py:76
  36.6 21.4 %collective-permute-start.21 = (bf16[128,1024]{1,0:T(8,128)(2,1)S(1)}, bf16[128,1024]{1,0:T(8,128)(2,1)S(1)}, u32[]{:S(2)}, u32[]{:S(2)}) collective-permute-start(bf16[128,1024]{1,0:T(8,128)(2,1)S(1)} %copy-done.17), channel_id=1, source_target_pairs={{0,16},{1,17},{2,18},{3,19},{4,20},{5,21},{6,22},{7,23},{8,24},{9,... | collective-permute-start | bytes 786440 | tf_op jit(solution)/shard_map/ppermute | solution.py:76
  37.6 20.4 %collective-permute-start.22 = (bf16[128,1024]{1,0:T(8,128)(2,1)S(1)}, bf16[128,1024]{1,0:T(8,128)(2,1)S(1)}, u32[]{:S(2)}, u32[]{:S(2)}) collective-permute-start(bf16[128,1024]{1,0:T(8,128)(2,1)S(1)} %copy-done.17), channel_id=1, source_target_pairs={{0,24},{1,25},{2,26},{3,27},{4,28},{5,29},{6,30},{7,31},{8,16},{9,... | collective-permute-start | bytes 786440 | tf_op jit(solution)/shard_map/ppermute | solution.py:76
  39.1 46.0 %collective-permute-start.14 = (bf16[4,128,1024]{2,1,0:T(8,128)(2,1)}, bf16[4,128,1024]{2,1,0:T(8,128)(2,1)S(1)}, u32[]{:S(2)}, u32[]{:S(2)}) collective-permute-start(bf16[4,128,1024]{2,1,0:T(8,128)(2,1)} %shard_map.278.refs_1_.refs_9_), channel_id=1, source_target_pairs={{0,4},{1,3},{2,6},{3,1},{4,0},{5,7},{6,2},{7,5},{8,12},{9,11},{10,... | collective-permute-start | bytes 3145736 | tf_op jit(solution)/shard_map/ppermute | solution.py:76
  45.7 14.9 %copy-start.21 = (bf16[128,1024]{1,0:T(8,128)(2,1)}, bf16[128,1024]{1,0:T(8,128)(2,1)S(1)}, u32[]{:S(2)}) copy-start(bf16[128,1024]{1,0:T(8,128)(2,1)S(1)} %collective-permute-done.20.refs_1_) | copy-start | bytes 786436
  45.7 17.1 %collective-permute-start = (bf16[128,1024]{1,0:T(8,128)(2,1)S(1)}, bf16[128,1024]{1,0:T(8,128)(2,1)S(1)}, u32[]{:S(2)}, u32[]{:S(2)}) collective-permute-start(bf16[128,1024]{1,0:T(8,128)(2,1)S(1)} %copy-done.16), channel_id=1, source_target_pairs={{0,8},{1,9},{2,10},{3,11},{4,12},{5,13},{6,14},{7,15},{8,0},{9,1},... | collective-permute-start | bytes 786440 | tf_op jit(solution)/shard_map/ppermute | solution.py:76
  58.0 22.5 %collective-permute-start.1 = (bf16[128,1024]{1,0:T(8,128)(2,1)S(1)}, bf16[128,1024]{1,0:T(8,128)(2,1)S(1)}, u32[]{:S(2)}, u32[]{:S(2)}) collective-permute-start(bf16[128,1024]{1,0:T(8,128)(2,1)S(1)} %copy-done.16), channel_id=1, source_target_pairs={{0,16},{1,17},{2,18},{3,19},{4,20},{5,21},{6,22},{7,23},{8,24},{9,... | collective-permute-start | bytes 786440 | tf_op jit(solution)/shard_map/ppermute | solution.py:76
  58.0 23.0 %collective-permute-start.2 = (bf16[128,1024]{1,0:T(8,128)(2,1)S(1)}, bf16[128,1024]{1,0:T(8,128)(2,1)S(1)}, u32[]{:S(2)}, u32[]{:S(2)}) collective-permute-start(bf16[128,1024]{1,0:T(8,128)(2,1)S(1)} %copy-done.16), channel_id=1, source_target_pairs={{0,24},{1,25},{2,26},{3,27},{4,28},{5,29},{6,30},{7,31},{8,16},{9,... | collective-permute-start | bytes 786440 | tf_op jit(solution)/shard_map/ppermute | solution.py:76
  62.8 75.0 %copy-start.36 = (bf16[1024]{0:T(1024)(128)(2,1)S(1)}, bf16[1024]{0:T(1024)(128)(2,1)}, u32[]{:S(2)}) copy-start(bf16[1024]{0:T(1024)(128)(2,1)} %param.31) | copy-start | bytes 6148
  62.8 75.1 %copy-start.37 = (bf16[2,256]{1,0:T(2,128)(2,1)S(1)}, bf16[2,256]{1,0:T(2,128)(2,1)}, u32[]{:S(2)}) copy-start(bf16[2,256]{1,0:T(2,128)(2,1)} %param.28) | copy-start | bytes 3076
  62.8 19.7 %copy-start.18 = (bf16[128,1024]{1,0:T(8,128)(2,1)}, bf16[128,1024]{1,0:T(8,128)(2,1)S(1)}, u32[]{:S(2)}) copy-start(bf16[128,1024]{1,0:T(8,128)(2,1)S(1)} %collective-permute-done.refs_1_) | copy-start | bytes 786436
  62.8 22.9 %collective-permute-start.16 = (bf16[4,128,1024]{2,1,0:T(8,128)(2,1)S(1)}, bf16[4,128,1024]{2,1,0:T(8,128)(2,1)S(1)}, u32[]{:S(2)}, u32[]{:S(2)}) collective-permute-start(bf16[4,128,1024]{2,1,0:T(8,128)(2,1)S(1)} %copy-done), channel_id=1, source_target_pairs={{0,1},{1,0},{2,3},{3,2},{4,5},{5,4},{6,7},{7,6},{8,9},{9,8},{10,11... | collective-permute-start | bytes 3145736 | tf_op jit(solution)/shard_map/ppermute | solution.py:76
  80.5 26.3 %collective-permute-start.23 = (bf16[4,128,1024]{2,1,0:T(8,128)(2,1)}, bf16[4,128,1024]{2,1,0:T(8,128)(2,1)S(1)}, u32[]{:S(2)}, u32[]{:S(2)}) collective-permute-start(bf16[4,128,1024]{2,1,0:T(8,128)(2,1)} %shard_map.280.refs_1_), channel_id=1, source_target_pairs={{0,2},{1,5},{2,0},{3,7},{4,6},{5,1},{6,4},{7,3},{8,10},{9,13},{10,... | collective-permute-start | bytes 3145736 | tf_op jit(solution)/shard_map/ppermute | solution.py:76
  81.1 26.4 %collective-permute-start.24 = (bf16[4,128,1024]{2,1,0:T(8,128)(2,1)}, bf16[4,128,1024]{2,1,0:T(8,128)(2,1)}, u32[]{:S(2)}, u32[]{:S(2)}) collective-permute-start(bf16[4,128,1024]{2,1,0:T(8,128)(2,1)} %shard_map.280.refs_1_), channel_id=1, source_target_pairs={{0,4},{1,3},{2,6},{3,1},{4,0},{5,7},{6,2},{7,5},{8,12},{9,11},{10,... | collective-permute-start | bytes 3145736 | tf_op jit(solution)/shard_map/ppermute | solution.py:76
  82.5 57.4 %copy-start.2 = (bf16[4,128,1024]{2,1,0:T(8,128)(2,1)}, bf16[4,128,1024]{2,1,0:T(8,128)(2,1)S(1)}, u32[]{:S(2)}) copy-start(bf16[4,128,1024]{2,1,0:T(8,128)(2,1)S(1)} %collective-permute-done.13.refs_2_.refs_10_) | copy-start | bytes 3145732
  82.5 25.3 %collective-permute-start.26 = (bf16[4,128,1024]{2,1,0:T(8,128)(2,1)}, bf16[4,128,1024]{2,1,0:T(8,128)(2,1)}, u32[]{:S(2)}, u32[]{:S(2)}) collective-permute-start(bf16[4,128,1024]{2,1,0:T(8,128)(2,1)} %shard_map.280.refs_1_), channel_id=1, source_target_pairs={{0,1},{1,0},{2,3},{3,2},{4,5},{5,4},{6,7},{7,6},{8,9},{9,8},{10,11... | collective-permute-start | bytes 3145736 | tf_op jit(solution)/shard_map/ppermute | solution.py:76
  85.1 61.1 %copy-start.7 = (bf16[4,128,1024]{2,1,0:T(8,128)(2,1)S(1)}, bf16[4,128,1024]{2,1,0:T(8,128)(2,1)}, u32[]{:S(2)}) copy-start(bf16[4,128,1024]{2,1,0:T(8,128)(2,1)} %shard_map.277.refs_1_) | copy-start | bytes 3145732
  85.1 76.5 %copy-start.38 = (s32[4]{0:T(128)S(1)}, s32[4]{0:T(128)}, u32[]{:S(2)}) copy-start(s32[4]{0:T(128)} %param.24) | copy-start | bytes 52
  85.1 77.7 %copy-start.3 = (bf16[4,128,1024]{2,1,0:T(8,128)(2,1)}, bf16[4,128,1024]{2,1,0:T(8,128)(2,1)S(1)}, u32[]{:S(2)}) copy-start(bf16[4,128,1024]{2,1,0:T(8,128)(2,1)S(1)} %collective-permute-done.14.refs_3_.refs_11_) | copy-start | bytes 3145732
  85.1 44.2 %collective-permute-start.3 = (bf16[4,128,1024]{2,1,0:T(8,128)(2,1)}, bf16[4,128,1024]{2,1,0:T(8,128)(2,1)}, u32[]{:S(2)}, u32[]{:S(2)}) collective-permute-start(bf16[4,128,1024]{2,1,0:T(8,128)(2,1)} %shard_map.277.refs_1_), channel_id=1, source_target_pairs={{0,2},{1,5},{2,0},{3,7},{4,6},{5,1},{6,4},{7,3},{8,10},{9,13},{10,... | collective-permute-start | bytes 3145736 | tf_op jit(solution)/shard_map/ppermute | solution.py:76
  85.7 51.0 %copy-start.4 = (bf16[4,128,1024]{2,1,0:T(8,128)(2,1)}, bf16[4,128,1024]{2,1,0:T(8,128)(2,1)S(1)}, u32[]{:S(2)}) copy-start(bf16[4,128,1024]{2,1,0:T(8,128)(2,1)S(1)} %collective-permute-done.16.refs_5_.refs_13_) | copy-start | bytes 3145732
  85.7 44.2 %collective-permute-start.4 = (bf16[4,128,1024]{2,1,0:T(8,128)(2,1)}, bf16[4,128,1024]{2,1,0:T(8,128)(2,1)S(1)}, u32[]{:S(2)}, u32[]{:S(2)}) collective-permute-start(bf16[4,128,1024]{2,1,0:T(8,128)(2,1)} %shard_map.277.refs_1_), channel_id=1, source_target_pairs={{0,4},{1,3},{2,6},{3,1},{4,0},{5,7},{6,2},{7,5},{8,12},{9,11},{10,... | collective-permute-start | bytes 3145736 | tf_op jit(solution)/shard_map/ppermute | solution.py:76
  106.8 27.0 %collective-permute-start.15 = (bf16[4,128,1024]{2,1,0:T(8,128)(2,1)S(1)}, bf16[4,128,1024]{2,1,0:T(8,128)(2,1)}, u32[]{:S(2)}, u32[]{:S(2)}) collective-permute-start(bf16[4,128,1024]{2,1,0:T(8,128)(2,1)S(1)} %collective-permute-done.13.refs_2_.refs_10_), channel_id=1, source_target_pairs={{0,4},{1,3},{2,6},{3,1},{4,0},{5,7},{6,2},{7,5},{8,12},{9,11},{10,... | collective-permute-start | bytes 3145736 | tf_op jit(solution)/shard_map/ppermute | solution.py:76
  107.5 27.5 %collective-permute-start.17 = (bf16[4,128,1024]{2,1,0:T(8,128)(2,1)S(1)}, bf16[4,128,1024]{2,1,0:T(8,128)(2,1)S(1)}, u32[]{:S(2)}, u32[]{:S(2)}) collective-permute-start(bf16[4,128,1024]{2,1,0:T(8,128)(2,1)S(1)} %collective-permute-done.13.refs_2_.refs_10_), channel_id=1, source_target_pairs={{0,1},{1,0},{2,3},{3,2},{4,5},{5,4},{6,7},{7,6},{8,9},{9,8},{10,11... | collective-permute-start | bytes 3145736 | tf_op jit(solution)/shard_map/ppermute | solution.py:76
  107.8 28.9 %collective-permute-start.18 = (bf16[4,128,1024]{2,1,0:T(8,128)(2,1)S(1)}, bf16[4,128,1024]{2,1,0:T(8,128)(2,1)S(1)}, u32[]{:S(2)}, u32[]{:S(2)}) collective-permute-start(bf16[4,128,1024]{2,1,0:T(8,128)(2,1)S(1)} %collective-permute-done.14.refs_3_.refs_11_), channel_id=1, source_target_pairs={{0,1},{1,0},{2,3},{3,2},{4,5},{5,4},{6,7},{7,6},{8,9},{9,8},{10,11... | collective-permute-start | bytes 3145736 | tf_op jit(solution)/shard_map/ppermute | solution.py:76
  129.4 15.6 %collective-permute-start.25 = (bf16[4,128,1024]{2,1,0:T(8,128)(2,1)}, bf16[4,128,1024]{2,1,0:T(8,128)(2,1)}, u32[]{:S(2)}, u32[]{:S(2)}) collective-permute-start(bf16[4,128,1024]{2,1,0:T(8,128)(2,1)} %copy-done.39), channel_id=1, source_target_pairs={{0,4},{1,3},{2,6},{3,1},{4,0},{5,7},{6,2},{7,5},{8,12},{9,11},{10,... | collective-permute-start | bytes 3145736 | tf_op jit(solution)/shard_map/ppermute | solution.py:76
  129.9 16.4 %collective-permute-start.27 = (bf16[4,128,1024]{2,1,0:T(8,128)(2,1)}, bf16[4,128,1024]{2,1,0:T(8,128)(2,1)}, u32[]{:S(2)}, u32[]{:S(2)}) collective-permute-start(bf16[4,128,1024]{2,1,0:T(8,128)(2,1)} %copy-done.39), channel_id=1, source_target_pairs={{0,1},{1,0},{2,3},{3,2},{4,5},{5,4},{6,7},{7,6},{8,9},{9,8},{10,11... | collective-permute-start | bytes 3145736 | tf_op jit(solution)/shard_map/ppermute | solution.py:76
  133.8 12.6 %collective-permute-start.28 = (bf16[4,128,1024]{2,1,0:T(8,128)(2,1)}, bf16[4,128,1024]{2,1,0:T(8,128)(2,1)}, u32[]{:S(2)}, u32[]{:S(2)}) collective-permute-start(bf16[4,128,1024]{2,1,0:T(8,128)(2,1)} %collective-permute-done.24.refs_3_), channel_id=1, source_target_pairs={{0,1},{1,0},{2,3},{3,2},{4,5},{5,4},{6,7},{7,6},{8,9},{9,8},{10,11... | collective-permute-start | bytes 3145736 | tf_op jit(solution)/shard_map/ppermute | solution.py:76
  135.0 21.2 %collective-permute-start.5 = (bf16[4,128,1024]{2,1,0:T(8,128)(2,1)}, bf16[4,128,1024]{2,1,0:T(8,128)(2,1)}, u32[]{:S(2)}, u32[]{:S(2)}) collective-permute-start(bf16[4,128,1024]{2,1,0:T(8,128)(2,1)} %collective-permute-done.3.refs_2_), channel_id=1, source_target_pairs={{0,4},{1,3},{2,6},{3,1},{4,0},{5,7},{6,2},{7,5},{8,12},{9,11},{10,... | collective-permute-start | bytes 3145736 | tf_op jit(solution)/shard_map/ppermute | solution.py:76
  137.7 23.2 %collective-permute-start.19 = (bf16[4,128,1024]{2,1,0:T(8,128)(2,1)}, bf16[4,128,1024]{2,1,0:T(8,128)(2,1)}, u32[]{:S(2)}, u32[]{:S(2)}) collective-permute-start(bf16[4,128,1024]{2,1,0:T(8,128)(2,1)} %collective-permute-done.15.refs_4_.refs_12_), channel_id=1, source_target_pairs={{0,1},{1,0},{2,3},{3,2},{4,5},{5,4},{6,7},{7,6},{8,9},{9,8},{10,11... | collective-permute-start | bytes 3145736 | tf_op jit(solution)/shard_map/ppermute | solution.py:76
  139.9 22.9 %all-to-all-start = ((bf16[4,336,256]{2,1,0:T(8,128)(2,1)}), bf16[4,336,256]{2,1,0:T(8,128)(2,1)S(1)}, u32[]{:S(2)}, u32[]{:S(2)}) async-start(bf16[4,336,256]{2,1,0:T(8,128)(2,1)} %pad_maximum_fusion.1), calls=%async_computation | async-start | bytes 1376256 | tf_op jit(solution)/shard_map/all_to_all | solution.py:612
  145.0 48.5 %collective-permute-start.29 = (bf16[4,128,1024]{2,1,0:T(8,128)(2,1)}, bf16[4,128,1024]{2,1,0:T(8,128)(2,1)}, u32[]{:S(2)}, u32[]{:S(2)}) collective-permute-start(bf16[4,128,1024]{2,1,0:T(8,128)(2,1)} %collective-permute-done.25.refs_4_), channel_id=1, source_target_pairs={{0,1},{1,0},{2,3},{3,2},{4,5},{5,4},{6,7},{7,6},{8,9},{9,8},{10,11... | collective-permute-start | bytes 3145736 | tf_op jit(solution)/shard_map/ppermute | solution.py:76
  146.2 63.6 %collective-permute-start.6 = (bf16[4,128,1024]{2,1,0:T(8,128)(2,1)S(1)}, bf16[4,128,1024]{2,1,0:T(8,128)(2,1)}, u32[]{:S(2)}, u32[]{:S(2)}) collective-permute-start(bf16[4,128,1024]{2,1,0:T(8,128)(2,1)S(1)} %copy-done.7), channel_id=1, source_target_pairs={{0,1},{1,0},{2,3},{3,2},{4,5},{5,4},{6,7},{7,6},{8,9},{9,8},{10,11... | collective-permute-start | bytes 3145736 | tf_op jit(solution)/shard_map/ppermute | solution.py:76
  146.3 63.6 %collective-permute-start.7 = (bf16[4,128,1024]{2,1,0:T(8,128)(2,1)}, bf16[4,128,1024]{2,1,0:T(8,128)(2,1)}, u32[]{:S(2)}, u32[]{:S(2)}) collective-permute-start(bf16[4,128,1024]{2,1,0:T(8,128)(2,1)} %collective-permute-done.3.refs_2_), channel_id=1, source_target_pairs={{0,1},{1,0},{2,3},{3,2},{4,5},{5,4},{6,7},{7,6},{8,9},{9,8},{10,11... | collective-permute-start | bytes 3145736 | tf_op jit(solution)/shard_map/ppermute | solution.py:76
  156.2 53.7 %collective-permute-start.8 = (bf16[4,128,1024]{2,1,0:T(8,128)(2,1)}, bf16[4,128,1024]{2,1,0:T(8,128)(2,1)}, u32[]{:S(2)}, u32[]{:S(2)}) collective-permute-start(bf16[4,128,1024]{2,1,0:T(8,128)(2,1)} %copy-done.10), channel_id=1, source_target_pairs={{0,1},{1,0},{2,3},{3,2},{4,5},{5,4},{6,7},{7,6},{8,9},{9,8},{10,11... | collective-permute-start | bytes 3145736 | tf_op jit(solution)/shard_map/ppermute | solution.py:76
  160.9 49.0 %collective-permute-start.9 = (bf16[4,128,1024]{2,1,0:T(8,128)(2,1)}, bf16[4,128,1024]{2,1,0:T(8,128)(2,1)}, u32[]{:S(2)}, u32[]{:S(2)}) collective-permute-start(bf16[4,128,1024]{2,1,0:T(8,128)(2,1)} %collective-permute-done.5.refs_4_), channel_id=1, source_target_pairs={{0,1},{1,0},{2,3},{3,2},{4,5},{5,4},{6,7},{7,6},{8,9},{9,8},{10,11... | collective-permute-start | bytes 3145736 | tf_op jit(solution)/shard_map/ppermute | solution.py:76
  162.8 30.7 %all-to-all-start.1 = ((bf16[4,320,256]{2,1,0:T(8,128)(2,1)}), bf16[4,320,256]{2,1,0:T(8,128)(2,1)S(1)}, u32[]{:S(2)}, u32[]{:S(2)}) async-start(bf16[4,320,256]{2,1,0:T(8,128)(2,1)} %bitcast.88), calls=%async_computation.1 | async-start | bytes 1310720 | tf_op jit(solution)/shard_map/all_to_all | solution.py:613
  233.2 22.2 %all-to-all-start.5 = ((bf16[32,16,384]{2,1,0:T(8,128)(2,1)}), bf16[32,16,384]{2,1,0:T(8,128)(2,1)S(1)}, u32[]{:S(2)}, u32[]{:S(2)}) async-start(bf16[32,16,384]{2,1,0:T(8,128)(2,1)} %bitcast.71), calls=%async_computation.5 | async-start | bytes 786432 | tf_op jit(solution)/shard_map/all_to_all | solution.py:551
  240.6 3.6 collective-permute-start.30
  244.7 4.5 %collective-permute-start.31 = (s32[2,4]{1,0:T(2,128)S(1)}, s32[2,4]{1,0:T(2,128)S(1)}, u32[]{:S(2)}, u32[]{:S(2)}) collective-permute-start(s32[2,4]{1,0:T(2,128)S(1)} %gather_fusion), channel_id=1, source_target_pairs={{0,8},{1,9},{2,10},{3,11},{4,12},{5,13},{6,14},{7,15},{8,0},{9,1},... | collective-permute-start | bytes 104 | tf_op jit(solution)/shard_map/ppermute | solution.py:76
  246.4 6.3 %collective-permute-start.32 = (s32[2,4]{1,0:T(2,128)S(1)}, s32[2,4]{1,0:T(2,128)S(1)}, u32[]{:S(2)}, u32[]{:S(2)}) collective-permute-start(s32[2,4]{1,0:T(2,128)S(1)} %gather_fusion), channel_id=1, source_target_pairs={{0,16},{1,17},{2,18},{3,19},{4,20},{5,21},{6,22},{7,23},{8,24},{9,... | collective-permute-start | bytes 104 | tf_op jit(solution)/shard_map/ppermute | solution.py:76
  248.8 5.4 %collective-permute-start.33 = (s32[2,4]{1,0:T(2,128)S(1)}, s32[2,4]{1,0:T(2,128)S(1)}, u32[]{:S(2)}, u32[]{:S(2)}) collective-permute-start(s32[2,4]{1,0:T(2,128)S(1)} %gather_fusion), channel_id=1, source_target_pairs={{0,24},{1,25},{2,26},{3,27},{4,28},{5,29},{6,30},{7,31},{8,16},{9,... | collective-permute-start | bytes 104 | tf_op jit(solution)/shard_map/ppermute | solution.py:76
  257.9 4.8 %collective-permute-start.40 = (bf16[128,384]{1,0:T(8,128)(2,1)}, bf16[128,384]{1,0:T(8,128)(2,1)S(1)}, u32[]{:S(2)}, u32[]{:S(2)}) collective-permute-start(bf16[128,384]{1,0:T(8,128)(2,1)} %bitcast.96), channel_id=1, source_target_pairs={{0,8},{1,9},{2,10},{3,11},{4,12},{5,13},{6,14},{7,15},{8,0},{9,1},... | collective-permute-start | bytes 294920 | tf_op jit(solution)/shard_map/ppermute | solution.py:76
  257.9 9.2 %collective-permute-start.41 = (bf16[128,384]{1,0:T(8,128)(2,1)}, bf16[128,384]{1,0:T(8,128)(2,1)S(1)}, u32[]{:S(2)}, u32[]{:S(2)}) collective-permute-start(bf16[128,384]{1,0:T(8,128)(2,1)} %bitcast.97), channel_id=1, source_target_pairs={{0,16},{1,17},{2,18},{3,19},{4,20},{5,21},{6,22},{7,23},{8,24},{9,... | collective-permute-start | bytes 294920 | tf_op jit(solution)/shard_map/ppermute | solution.py:76
  258.9 8.2 %collective-permute-start.42 = (bf16[128,384]{1,0:T(8,128)(2,1)}, bf16[128,384]{1,0:T(8,128)(2,1)S(1)}, u32[]{:S(2)}, u32[]{:S(2)}) collective-permute-start(bf16[128,384]{1,0:T(8,128)(2,1)} %bitcast.98), channel_id=1, source_target_pairs={{0,24},{1,25},{2,26},{3,27},{4,28},{5,29},{6,30},{7,31},{8,16},{9,... | collective-permute-start | bytes 294920 | tf_op jit(solution)/shard_map/ppermute | solution.py:76
  270.2 8.0 %collective-permute-start.43 = (bf16[4,128,384]{2,1,0:T(8,128)(2,1)}, bf16[4,128,384]{2,1,0:T(8,128)(2,1)S(1)}, u32[]{:S(2)}, u32[]{:S(2)}) collective-permute-start(bf16[4,128,384]{2,1,0:T(8,128)(2,1)} %shard_map.292), channel_id=1, source_target_pairs={{0,4},{1,5},{2,6},{3,7},{4,0},{5,1},{6,2},{7,3},{8,12},{9,13},{10,... | collective-permute-start | bytes 1179656 | tf_op jit(solution)/shard_map/ppermute | solution.py:76
  281.0 15.9 %collective-permute-start.44 = (bf16[2,4,128,384]{3,2,1,0:T(8,128)(2,1)}, bf16[2,4,128,384]{3,2,1,0:T(8,128)(2,1)S(1)}, u32[]{:S(2)}, u32[]{:S(2)}) collective-permute-start(bf16[2,4,128,384]{3,2,1,0:T(8,128)(2,1)} %bitcast.76), channel_id=1, source_target_pairs={{0,2},{1,3},{2,0},{3,1},{4,6},{5,7},{6,4},{7,5},{8,10},{9,11},{10,... | collective-permute-start | bytes 2359304 | tf_op jit(solution)/shard_map/ppermute | solution.py:76
  300.5 73.7 %collective-permute-start.45 = (bf16[2,2,4,128,384]{4,3,2,1,0:T(8,128)(2,1)}, bf16[2,2,4,128,384]{4,3,2,1,0:T(8,128)(2,1)S(1)}, u32[]{:S(2)}, u32[]{:S(2)}) collective-permute-start(bf16[2,2,4,128,384]{4,3,2,1,0:T(8,128)(2,1)} %bitcast.73), channel_id=1, source_target_pairs={{0,1},{1,0},{2,3},{3,2},{4,5},{5,4},{6,7},{7,6},{8,9},{9,8},{10,11... | collective-permute-start | bytes 4718600 | tf_op jit(solution)/shard_map/ppermute | solution.py:76
  301.1 16.7 %all-to-all-start.4 = ((bf16[32,16,128]{2,1,0:T(8,128)(2,1)}), bf16[32,16,128]{2,1,0:T(8,128)(2,1)S(1)}, u32[]{:S(2)}, u32[]{:S(2)}) async-start(bf16[32,16,128]{2,1,0:T(8,128)(2,1)} %bitcast_bitcast_fusion.1), calls=%async_computation.4 | async-start | bytes 262144 | tf_op jit(solution)/shard_map/all_to_all | solution.py:551
  317.8 34.0 %all-to-all-start.3 = ((bf16[4,320,256]{2,1,0:T(8,128)(2,1)}), bf16[4,320,256]{2,1,0:T(8,128)(2,1)S(1)}, u32[]{:S(2)}, u32[]{:S(2)}) async-start(bf16[4,320,256]{2,1,0:T(8,128)(2,1)} %shard_map.284), calls=%async_computation.3 | async-start | bytes 1310720 | tf_op jit(solution)/shard_map/all_to_all | solution.py:708
  323.0 4.4 %collective-permute-start.34 = (bf16[128,128]{1,0:T(8,128)(2,1)}, bf16[128,128]{1,0:T(8,128)(2,1)S(1)}, u32[]{:S(2)}, u32[]{:S(2)}) collective-permute-start(bf16[128,128]{1,0:T(8,128)(2,1)} %bitcast.102), channel_id=1, source_target_pairs={{0,8},{1,9},{2,10},{3,11},{4,12},{5,13},{6,14},{7,15},{8,0},{9,1},... | collective-permute-start | bytes 98312 | tf_op jit(solution)/shard_map/ppermute | solution.py:76
  324.8 5.6 %collective-permute-start.35 = (bf16[128,128]{1,0:T(8,128)(2,1)}, bf16[128,128]{1,0:T(8,128)(2,1)S(1)}, u32[]{:S(2)}, u32[]{:S(2)}) collective-permute-start(bf16[128,128]{1,0:T(8,128)(2,1)} %bitcast.103), channel_id=1, source_target_pairs={{0,16},{1,17},{2,18},{3,19},{4,20},{5,21},{6,22},{7,23},{8,24},{9,... | collective-permute-start | bytes 98312 | tf_op jit(solution)/shard_map/ppermute | solution.py:76
  327.2 5.9 %collective-permute-start.36 = (bf16[128,128]{1,0:T(8,128)(2,1)}, bf16[128,128]{1,0:T(8,128)(2,1)S(1)}, u32[]{:S(2)}, u32[]{:S(2)}) collective-permute-start(bf16[128,128]{1,0:T(8,128)(2,1)} %bitcast.104), channel_id=1, source_target_pairs={{0,24},{1,25},{2,26},{3,27},{4,28},{5,29},{6,30},{7,31},{8,16},{9,... | collective-permute-start | bytes 98312 | tf_op jit(solution)/shard_map/ppermute | solution.py:76
  335.2 5.2 %collective-permute-start.37 = (bf16[4,128,128]{2,1,0:T(8,128)(2,1)}, bf16[4,128,128]{2,1,0:T(8,128)(2,1)S(1)}, u32[]{:S(2)}, u32[]{:S(2)}) collective-permute-start(bf16[4,128,128]{2,1,0:T(8,128)(2,1)} %shard_map.286), channel_id=1, source_target_pairs={{0,4},{1,5},{2,6},{3,7},{4,0},{5,1},{6,2},{7,3},{8,12},{9,13},{10,... | collective-permute-start | bytes 393224 | tf_op jit(solution)/shard_map/ppermute | solution.py:76
  342.7 6.6 %collective-permute-start.38 = (bf16[2,4,128,128]{3,2,1,0:T(8,128)(2,1)}, bf16[2,4,128,128]{3,2,1,0:T(8,128)(2,1)S(1)}, u32[]{:S(2)}, u32[]{:S(2)}) collective-permute-start(bf16[2,4,128,128]{3,2,1,0:T(8,128)(2,1)} %bitcast.84), channel_id=1, source_target_pairs={{0,2},{1,3},{2,0},{3,1},{4,6},{5,7},{6,4},{7,5},{8,10},{9,11},{10,... | collective-permute-start | bytes 786440 | tf_op jit(solution)/shard_map/ppermute | solution.py:76
  351.9 14.0 %collective-permute-start.39 = (bf16[2,2,4,128,128]{4,3,2,1,0:T(8,128)(2,1)}, bf16[2,2,4,128,128]{4,3,2,1,0:T(8,128)(2,1)S(1)}, u32[]{:S(2)}, u32[]{:S(2)}) collective-permute-start(bf16[2,2,4,128,128]{4,3,2,1,0:T(8,128)(2,1)} %bitcast.80), channel_id=1, source_target_pairs={{0,1},{1,0},{2,3},{3,2},{4,5},{5,4},{6,7},{7,6},{8,9},{9,8},{10,11... | collective-permute-start | bytes 1572872 | tf_op jit(solution)/shard_map/ppermute | solution.py:76
  351.9 14.0 %all-to-all-start.2 = ((bf16[4,320,256]{2,1,0:T(8,128)(2,1)}), bf16[4,320,256]{2,1,0:T(8,128)(2,1)S(1)}, u32[]{:S(2)}, u32[]{:S(2)}) async-start(bf16[4,320,256]{2,1,0:T(8,128)(2,1)} %get-tuple-element.63), calls=%async_computation.2 | async-start | bytes 1310720 | tf_op jit(solution)/shard_map/all_to_all | solution.py:684
  (28 other events, 66.1 us)

commit v3 on v2

--- a/solution.py
+++ b/solution.py
@@ -17,8 +17,6 @@
 SEQ = 320
 PAIR = 2 * HD
 EXTRA = 16
-EARLY = 4 * D + 2 * FF
-LATE = 4 * D
 BF = jnp.bfloat16
 F32 = jnp.float32
 BOTH = ("row", "col")
@@ -50,16 +48,15 @@
     return inverse * (scaled - first_mean - unit_rows * second_mean)
 
 
-def call(kernel, outs, ins, spaces, scratch=(), flops=0, moved=0, aliases=None):
+def call(kernel, outs, ins, spaces, scratch=()):
     return pl.pallas_call(
         kernel,
         out_shape=outs,
         in_specs=[pl.BlockSpec(memory_space=s) for s in spaces],
         out_specs=jax.tree.map(lambda _: pl.BlockSpec(memory_space=VMEM), outs),
         scratch_shapes=list(scratch),
-        input_output_aliases=aliases or {},
         compiler_params=pltpu.CompilerParams(vmem_limit_bytes=56 << 20),
-        cost_estimate=pl.CostEstimate(flops=flops, bytes_accessed=moved, transcendentals=0),
+        cost_estimate=pl.CostEstimate(flops=0, bytes_accessed=0, transcendentals=0),
     )(*ins)
 
 
@@ -95,7 +92,6 @@
         out,
         [index.reshape(1).astype(jnp.int32)] + flat,
         [pltpu.SMEM] + [VMEM] * len(parts),
-        moved=2 * len(parts) * flat[0].size * 2,
     )
     return made.reshape((len(parts),) + shape)
 
@@ -142,27 +138,28 @@
     return table
 
 
-def gather_pieces(shard):
+def after(value, *others):
+    return lax.optimization_barrier((value,) + others)[0]
+
+
+def gather_high(shard):
     rows, cols = sizes()
     block = shard
     for axis, bit, width in early_groups(rows, cols):
         block = group_join(block, axis, bit, width)
-    own = block.reshape((-1,) + shard.shape)
-
-    def one(r, c):
-        return (r, c ^ 2) if c % 2 == 0 else (r ^ 1, c)
-
-    def two(r, c):
-        return (r ^ 1, c) if c % 2 == 0 else (r, c ^ 2)
-
-    def core(r, c):
-        return (r, c ^ 1)
-
-    first = swap(own, one)
-    second = swap(own, two)
-    both = swap(first, two)
-    mine = [own, first, second, both]
-    return mine + [swap(p, core) for p in mine]
+    return block.reshape((-1,) + shard.shape)
+
+
+def flip_one(r, c):
+    return (r, c ^ 2) if c % 2 == 0 else (r ^ 1, c)
+
+
+def flip_two(r, c):
+    return (r ^ 1, c) if c % 2 == 0 else (r, c ^ 2)
+
+
+def flip_core(r, c):
+    return (r, c ^ 1)
 
 
 def all_steps(rows, cols):
@@ -182,10 +179,12 @@
     return table
 
 
-def gather_leading(block):
+def gather_leading(block, waits):
     rows, cols = sizes()
     shape = block.shape
-    for axis, bit, width in all_steps(rows, cols):
+    for i, (axis, bit, width) in enumerate(all_steps(rows, cols)):
+        if i in waits:
+            block = after(block, *waits[i])
         block = group_join(block, axis, bit, width)
     return block.reshape((rows * cols,) + shape)
 
@@ -247,12 +246,15 @@
     return pl.ds(pl.multiple_of(start, width), width)
 
 
-def prep_kernel(wq, wp, w1, w2, out_q, out_a, out_b):
+def prep_q_kernel(wq, wp, out):
     hid = wq.shape[2]
+    for c in range(3):
+        out[:, c * hid : (c + 1) * hid] = wq[c]
+    out[:, 3 * hid :] = low(wp[...].astype(F32).T)
+
+
+def prep_f_kernel(w1, w2, out_a, out_b):
     half = w1.shape[1] // 2
-    for c in range(3):
-        out_q[:, c * hid : (c + 1) * hid] = wq[c]
-    out_q[:, 3 * hid :] = low(wp[...].astype(F32).T)
     out_a[:, :half] = w1[:, :half]
     out_b[:, :half] = w1[:, half:]
     out_a[:, half:] = low(w2[:half].astype(F32).T)
@@ -361,12 +363,8 @@
         glat3[...] += mm(grad_pre, up, NT)
         res[...] += mm(activated, w2, NT)
         gn2[...] += mm(grad_pre, w1, NT)
-        early[:, pl.ds(pl.multiple_of(3 * D + block * ffn + part * half, half), half)] = low(
-            mm(lat3_t, grad_pre)
-        )
-        early[:, pl.ds(pl.multiple_of(3 * D + FF + block * ffn + part * half, half), half)] = low(
-            mm(glat4_t, activated)
-        )
+        early[:, lanes(block * half, half)] = low(mm(lat3_t, grad_pre))
+        early[:, lanes(FF // 2 + block * half, half)] = low(mm(glat4_t, activated))
         return 0
 
     lax.fori_loop(0, cols, step, 0)
@@ -388,7 +386,6 @@
     gn2[...] = jnp.zeros_like(gn2)
     lat4[...] = jnp.zeros_like(lat4)
     glat3[...] = jnp.zeros_like(glat3)
-    early[...] = jnp.zeros_like(early)
     weights.wait()
     ffn_steps(
         sc, 0, cols, w, xa, n2, lat3, gr, glat4, up_1, down_2, (res, gn2, lat4, glat3), early
@@ -400,9 +397,9 @@
     pieces = refs[1:9]
     own_q = refs[9:17]
     (xa, keep, gain, n2, lat3, up_1, down_2, up_2, f_down, p_down, p_up, bias_out) = refs[17:29]
-    (middle, att, lat2, gr, res_in, gn2_in, lat4_in, glat3_in, early_in) = refs[29:38]
-    layer, gatt, gmid, early = refs[38:42]
-    w, sems, wp, sems_p, res, gn2, lat4, glat3 = refs[42:]
+    (middle, att, lat2, gr, res_in, gn2_in, lat4_in, glat3_in) = refs[29:37]
+    layer, gatt, gmid, early = refs[37:41]
+    w, sems, wp, sems_p, res, gn2, lat4, glat3 = refs[41:]
     weights = Weights(sc, pieces, w, sems, lead)
     weights.start()
     proj = Weights(sc, own_q, wp, sems_p, lead, 3 * D // cols)
@@ -414,7 +411,6 @@
     gn2[...] = gn2_in[...]
     lat4[...] = lat4_in[...]
     glat3[...] = glat3_in[...]
-    early[...] = early_in[...]
     weights.wait()
     ffn_steps(
         sc, 1, cols, w, xa, n2, lat3, gr, glat4, up_1, down_2, (res, gn2, lat4, glat3), early
@@ -434,9 +430,9 @@
     gb = low(grad_middle)
     glat2 = low(mm(gb, p_up[a], NT))
     glat2_t = low(glat2.astype(F32).T)
-    early[:, D : 2 * D] = low(mm(low(lat2[...].astype(F32).T), gb))
-    early[:, 2 * D : 3 * D] = low(mm(low(glat3_low.astype(F32).T), n2[...]))
-    early[:, 3 * D + 2 * FF :] = low(mm(low(lat4_low.astype(F32).T), gr[...]))
+    early[:, FF + D : FF + 2 * D] = low(mm(low(lat2[...].astype(F32).T), gb))
+    early[:, FF + 2 * D : FF + 3 * D] = low(mm(low(glat3_low.astype(F32).T), n2[...]))
+    early[:, FF + 3 * D :] = low(mm(low(lat4_low.astype(F32).T), gr[...]))
     proj.wait()
 
     def step(slot, _):
@@ -444,7 +440,7 @@
         here = lanes(slot * hid, hid)
         there = lanes(block * hid, hid)
         gatt[:, here] = low(mm(gb, wp[slot]) + mm(glat2, p_down[a, :, there]))
-        early[:, there] = low(mm(glat2_t, att[:, here]))
+        early[:, lanes(FF + block * hid, hid)] = low(mm(glat2_t, att[:, here]))
         return 0
 
     lax.fori_loop(0, cols, step, 0)
@@ -503,9 +499,9 @@
 def back_kernel(lead, cols, *refs):
     sc = refs[0]
     pieces = refs[1:9]
-    xa, gain, gq, gk, gv, glat1, q_down, gmid = refs[9:17]
-    out = refs[17]
-    w, sems, acc = refs[18:]
+    xa, gain, gq, gk, gv, glat1, q_down, gmid, layer = refs[9:18]
+    out = refs[18]
+    w, sems, acc = refs[19:]
     weights = Weights(sc, pieces, w, sems, lead)
     weights.start()
     hid = D // cols
@@ -523,53 +519,74 @@
     lax.fori_loop(0, cols, step, 0)
     made = low(gmid[...] + norm_back(acc[...], gain[0:1], unit, inverse))
     for c in range(cols):
-        out[c] = made[:, c * hid : (c + 1) * hid]
-
-
-def sum_kernel(owners, mine, out, acc):
+        out[c, :SEQ] = layer[c]
+        out[c, SEQ:] = made[:, c * hid : (c + 1) * hid]
+
+
+def sum_kernel(owners, *refs):
+    mines, out, acc = refs[:-2], refs[-2], refs[-1]
     acc[...] = jnp.zeros_like(acc)
-    for d in range(mine.shape[0]):
-        acc[owners[d]] += mine[d].astype(F32)
+    lane = 0
+    for mine in mines:
+        part = mine.shape[-1]
+        for d in range(mine.shape[0]):
+            acc[owners[d], :, lane : lane + part] += mine[d].astype(F32)
+        lane += part
     out[...] = low(acc[...])
 
 
-def spread_kernel(spans, part, table, whole, *outs):
-    for b in range(whole.shape[0] * part // 128):
-        lane = b * 128
-        block = whole[table.index(lane // part), :, lane % part : lane % part + 128].astype(F32)
-        for out, (start, width) in zip(outs, spans):
-            if start <= lane < start + width:
-                out[:, lane - start : lane - start + 128] = block
-
-
-def sum_adapters(grads, owners, spans):
+def spread_kernel(maps, parts, table, whole, *outs):
+    base = 0
+    for part, spans in zip(parts, maps):
+        for out, put, start, width in spans:
+            for lane in range(0, width, 128):
+                at = start + lane
+                here = base + at % part
+                block = whole[table.index(at // part), :, here : here + 128]
+                outs[out][:, put + lane : put + lane + 128] = block.astype(F32)
+        base += part
+
+
+def send_grads(grads):
     rows, cols = sizes()
     devices = rows * cols
-    width = grads.shape[-1]
-    part = width // devices
+    part = grads.shape[-1] // devices
     pieces = grads.reshape(R, devices, part).transpose(1, 0, 2)
-    mine = lax.all_to_all(pieces, BOTH, split_axis=0, concat_axis=0, tiled=True)
+    return lax.all_to_all(pieces, BOTH, split_axis=0, concat_axis=0, tiled=True)
+
+
+def sum_grads(mines, owners):
+    part = sum(m.shape[-1] for m in mines)
     summed = call(
         sum_kernel,
         jax.ShapeDtypeStruct((NA, R, part), BF),
-        [owners, mine],
-        [pltpu.SMEM, VMEM],
+        [owners, *mines],
+        [pltpu.SMEM] + [VMEM] * len(mines),
         [VMEM((NA, R, part), F32)],
-        moved=4 * mine.size,
-    )
-    whole = gather_leading(summed.reshape(NA * R, part))
-    if part % 128 == 0:
+    )
+    return summed.reshape(NA * R, part)
+
+
+def spread(whole, parts, maps, widths):
+    rows, cols = sizes()
+    devices = rows * cols
+    table = all_table(rows, cols)
+    if all(p % 128 == 0 for p in parts):
         return call(
-            functools.partial(spread_kernel, spans, part, all_table(rows, cols)),
-            [jax.ShapeDtypeStruct((NA * R, n), F32) for _, n in spans],
+            functools.partial(spread_kernel, maps, parts, table),
+            [jax.ShapeDtypeStruct((NA * R, n), F32) for n in widths],
             [whole],
             [VMEM],
-            moved=6 * whole.size,
         )
-    table = all_table(rows, cols)
-    whole = whole[jnp.array([table.index(d) for d in range(devices)])]
-    flat = jnp.swapaxes(whole, 0, 1).reshape(NA * R, width).astype(F32)
-    return [flat[:, s : s + n] for s, n in spans]
+    whole = whole[jnp.array([table.index(d) for d in range(devices)])].astype(F32)
+    found = [[] for _ in widths]
+    base = 0
+    for part, spans in zip(parts, maps):
+        flat = jnp.swapaxes(whole[:, :, base : base + part], 0, 1).reshape(NA * R, devices * part)
+        for out, put, start, width in spans:
+            found[out].append((put, flat[:, start : start + width]))
+        base += part
+    return [jnp.concatenate([x for _, x in sorted(f, key=lambda e: e[0])], axis=1) for f in found]
 
 
 def per_device(
@@ -614,13 +631,30 @@
         grad_out.reshape(cols, SEQ, hid), "col", split_axis=0, concat_axis=0, tiled=True
     )
     shard = jax.ShapeDtypeStruct((blk, n), BF)
-    shard_q, shard_a, shard_b = call(
-        prep_kernel, [shard] * 3, [w_qkv, w_proj, w_fc1, w_fc2], [VMEM] * 4, moved=12 * blk * n
-    )
-    pieces_q = gather_pieces(shard_q)
-    pieces_a = gather_pieces(shard_a)
-    pieces_b = gather_pieces(shard_b)
+    shard_q = call(prep_q_kernel, shard, [w_qkv, w_proj], [VMEM] * 2)
+    shard_a, shard_b = call(prep_f_kernel, [shard] * 2, [w_fc1, w_fc2], [VMEM] * 2)
     owners = gather_owners(adapter_index)
+    with jax.named_scope("q_high"):
+        own_q = gather_high(shard_q)
+    with jax.named_scope("fa_high"):
+        own_a = gather_high(after(shard_a, own_q))
+    with jax.named_scope("fb_high"):
+        own_b = gather_high(after(shard_b, own_a))
+    own_q = after(own_q, xa, owners)
+    with jax.named_scope("q_one"):
+        one_q = swap(own_q, flip_one)
+    with jax.named_scope("q_two"):
+        two_q = swap(own_q, flip_two)
+    own_a = after(own_a, one_q, two_q, ga)
+    with jax.named_scope("q_both"):
+        both_q = swap(one_q, flip_two)
+    with jax.named_scope("q_core"):
+        pieces_q = [own_q, one_q, two_q, both_q]
+        pieces_q = pieces_q + [swap(p, flip_core) for p in pieces_q]
+    with jax.named_scope("fa_one"):
+        one_a = swap(own_a, flip_one)
+    with jax.named_scope("fa_two"):
+        two_a = swap(own_a, flip_two)
 
     mask_row = lax.dynamic_index_in_dim(keep_mask, column, 0, keepdims=False)
     keep = jnp.concatenate([jnp.ones((BUF,), F32), mask_row.astype(F32)]).reshape(SEQ, 1)
@@ -633,7 +667,6 @@
 
     big, small = shaped(D, BF), shaped(R, BF)
     scratch = weight_scratch(rows, cols, n)
-    flops = 2 * SEQ * D * D
     any_space = [pl.ANY] * 8
     n1, lat1, q, k, v, lse, att, lat2, middle, n2, lat3 = call(
         functools.partial(front_kernel, lead, cols),
@@ -654,74 +687,102 @@
         + [fc1_down, bias_out],
         [pltpu.SMEM] + any_space + [VMEM] * 10,
         scratch + [VMEM((SEQ, D), F32), VMEM((SEQ, D), F32)],
-        flops=5 * flops,
-        moved=8 * D * D + 16 * SEQ * D,
-    )
+    )
+    with jax.named_scope("fa_both"):
+        both_a = swap(after(one_a, n1), flip_two)
+    with jax.named_scope("fa_core"):
+        pieces_a = [own_a, one_a, two_a, both_a]
+        pieces_a = pieces_a + [swap(p, flip_core) for p in pieces_a]
+    own_b = after(own_b, n1, one_a, two_a)
+    with jax.named_scope("fb_one"):
+        one_b = swap(own_b, flip_one)
+    with jax.named_scope("fb_two"):
+        two_b = swap(own_b, flip_two)
     wide = shaped(D, F32)
     thin = shaped(R, F32)
-    res, gn2, lat4, glat3, gr, early = call(
+    res, gn2, lat4, glat3, gr, early_a = call(
         functools.partial(ffn_a_kernel, lead, cols),
-        [wide, wide, thin, thin, big, shaped(EARLY, BF, R)],
+        [wide, wide, thin, thin, big, shaped(FF, BF, R)],
         [sc, *pieces_a, xa, ga, keep, n2, lat3, fc1_up, fc2_down, fc2_up],
         [pltpu.SMEM] + any_space + [VMEM] * 8,
         scratch,
-        flops=8 * flops,
-        moved=8 * D * D + 16 * SEQ * D,
-    )
-    layer, gatt, gmid, early = call(
+    )
+    with jax.named_scope("fb_both"):
+        both_b = swap(after(one_b, res), flip_two)
+    with jax.named_scope("grads_a_send"):
+        mine_a = send_grads(early_a)
+    with jax.named_scope("fb_core"):
+        pieces_b = [own_b, one_b, two_b, after(both_b, mine_a)]
+        pieces_b = pieces_b + [swap(p, flip_core) for p in pieces_b]
+    layer, gatt, gmid, early_b = call(
         functools.partial(ffn_b_kernel, lead, cols),
-        [jax.ShapeDtypeStruct((cols, SEQ, hid), BF), big, wide, shaped(EARLY, BF, R)],
+        [jax.ShapeDtypeStruct((cols, SEQ, hid), BF), big, wide, shaped(FF + 4 * D, BF, R)],
         [sc, *pieces_b, *pieces_q, xa, keep, ln_gain, n2, lat3, fc1_up, fc2_down, fc2_up]
         + [fc1_down, proj_down, proj_up, bias_out]
-        + [middle, att, lat2, gr, res, gn2, lat4, glat3, early],
-        [pltpu.SMEM] + any_space * 2 + [VMEM] * 21,
+        + [middle, att, lat2, gr, res, gn2, lat4, glat3],
+        [pltpu.SMEM] + any_space * 2 + [VMEM] * 20,
         scratch
         + [VMEM((cols, D, hid), BF), scratch[1]]
         + [VMEM((SEQ, D), F32), VMEM((SEQ, D), F32), VMEM((SEQ, R), F32), VMEM((SEQ, R), F32)],
-        flops=10 * flops,
-        moved=10 * D * D + 24 * SEQ * D,
-    )
-    layer = lax.all_to_all(layer, "col", split_axis=0, concat_axis=0, tiled=True)
-    early_sum = sum_adapters(
-        early,
-        owners,
-        ((0, D), (D, D), (2 * D, D), (3 * D, FF), (3 * D + FF, FF), (3 * D + 2 * FF, D)),
-    )
+    )
+    with jax.named_scope("grads_b_send"):
+        mine_b = send_grads(early_b)
     gq, gk, gv, glat1, late = call(
         functools.partial(attention_back_kernel, cols),
-        [big, big, big, small, shaped(LATE, BF, R)],
+        [big, big, big, small, shaped(4 * D, BF, R)],
         [sc, closed, q, k, v, lse, gatt, lat1, n1, qkv_up],
         [pltpu.SMEM] + [VMEM] * 9,
-        flops=5 * flops,
-        moved=16 * SEQ * D,
-    )
-    late_sum = sum_adapters(late, owners, ((0, D), (D, D), (2 * D, D), (3 * D, D)))
-    grad_in = call(
+    )
+    with jax.named_scope("grads_c_send"):
+        mine_c = send_grads(late)
+    with jax.named_scope("grads_b"):
+        part_b = sum_grads([mine_a, after(mine_b, late)], owners)
+    gmid = after(gmid, part_b)
+    sent = call(
         functools.partial(back_kernel, lead, cols),
-        jax.ShapeDtypeStruct((cols, SEQ, hid), BF),
-        [sc, *pieces_q, xa, ln_gain, gq, gk, gv, glat1, qkv_down, gmid],
-        [pltpu.SMEM] + any_space + [VMEM] * 8,
+        jax.ShapeDtypeStruct((cols, 2 * SEQ, hid), BF),
+        [sc, *pieces_q, xa, ln_gain, gq, gk, gv, glat1, qkv_down, gmid, layer],
+        [pltpu.SMEM] + any_space + [VMEM] * 9,
         scratch + [VMEM((SEQ, D), F32)],
-        flops=3 * flops,
-        moved=8 * D * D + 8 * SEQ * D,
-    )
-    grad_in = lax.all_to_all(grad_in, "col", split_axis=0, concat_axis=0, tiled=True)
+    )
+    with jax.named_scope("rows_out"):
+        rows_out = lax.all_to_all(sent, "col", split_axis=0, concat_axis=0, tiled=True)
+    layer, grad_in = rows_out[:, :SEQ], rows_out[:, SEQ:]
+    with jax.named_scope("grads_b"):
+        whole_b = gather_leading(part_b, {1: [sent, mine_c]})
+    with jax.named_scope("grads_c"):
+        whole_c = gather_leading(sum_grads([mine_c], owners), {})
+    half = FF // cols // 2
+    map_a, map_b = (
+        tuple(
+            (out, (2 * block + part) * half, base + block * half, half)
+            for out, base in ((0, 0), (1, FF // 2))
+            for block in range(cols)
+        )
+        for part in (0, 1)
+    )
+    map_b = map_b + tuple((2 + i, 0, FF + i * D, D) for i in range(4))
+    parts = [mine_a.shape[-1], mine_b.shape[-1]]
+    early_sum = spread(whole_b, parts, [map_a, map_b], [FF, FF, D, D, D, D])
+    map_c = tuple((i, 0, i * D, D) for i in range(4))
+    late_sum = spread(whole_c, [mine_c.shape[-1]], [map_c], [D] * 4)
 
     def split(table, last=()):
         return table.reshape((NA, R) + last + (-1,))
 
     g_qkv_up = jnp.stack([split(t) for t in late_sum[1:]], axis=2)
+    g_fc1_up, g_fc2_down, g_proj_down, g_proj_up, g_fc1_down, g_fc2_up = map(split, early_sum)
     return (
         layer.reshape(cols * SEQ, hid),
         grad_in.reshape(cols * SEQ, hid),
         split(late_sum[0]),
         g_qkv_up,
-        split(early_sum[0]),
-        split(early_sum[1]),
-        split(early_sum[2]),
-        split(early_sum[3]),
-        split(early_sum[4]),
-        split(early_sum[5]),
+        g_proj_down,
+        g_proj_up,
+        g_fc1_down,
+        g_fc1_up,
+        g_fc2_down,
+        g_fc2_up,
     )
 
 

time: 387 us -> 375 us (0.969)
  waiting for transfers between devices: 153 us -> 141 us
  starting transfers between devices: 84.4 us -> 79.4 us
    ppermute x46, waiting for transfers between devices: 142 us -> 133 us  [swap(): return lax.ppermute(block, BOTH, pairs)]
    ppermute x46, starting transfers between devices: 55.9 us -> 50.6 us  [swap(): return lax.ppermute(block, BOTH, pairs)]
    pallas_call x21 -> x22, Pallas kernels: 119 us -> 120 us  [call(): pl.pallas_call(kernel, out_shape=outs, in_specs=[pl.BlockSpec(memory_spac...]
    unnamed x83 -> x79, local copies, waits for them, and re-layouts: 15 us -> 14.5 us
  transfers between devices with their start and end apart: 52 -> 52, of which waited for: 23 -> 17; matrix products, arithmetic and copies ran while one was open for 4% -> 5% of each run, Pallas kernels for 20% -> 22%
where the time goes in v3:
time: 375 us; the launch traced here: 374 us
  waiting for transfers between devices  141 us (38%)
  Pallas kernels  120 us (32%)
  starting transfers between devices  79.4 us (21%)
  local copies, waits for them, and re-layouts  25.2 us (7%)
  other arithmetic  7.44 us (2%)
    ppermute x46, waiting for transfers between devices, swap(): return lax.ppermute(block, BOTH, pairs)  133 us
    pallas_call x22, Pallas kernels, call(): pl.pallas_call(kernel, out_shape=outs, in_specs=[pl.BlockSpec(memory_spac...  120 us
    ppermute x46, starting transfers between devices, swap(): return lax.ppermute(block, BOTH, pairs)  50.6 us
    all_to_all x3, starting transfers between devices, send_grads(): return lax.all_to_all(pieces, BOTH, split_axis=0, concat_axis=0, tiled=True)  17.6 us
    unnamed x79, local copies, waits for them, and re-layouts  14.5 us
  transfers between devices with their start and end apart: 52, of which 17 were waited for; matrix products, arithmetic and copies ran while one was open for 5% of the time, Pallas kernels for 22%

profile of v3, /device:TPU:0, one launch (start us, length us, event | category | flops | bytes accessed | tf_op | source)
XLA Modules:
  0.0 373.8 jit_solution(14269737815918162298)
XLA Ops:
  0.7 1.8 shard_map.276.refs_0_
  2.4 3.0 collective-permute-start
  5.4 2.6 collective-permute-start.1
  8.0 1.7 collective-permute-start.3
  11.3 2.0 pad_maximum_fusion.1
  13.3 3.5 all-to-all-start
  17.4 1.8 collective-permute-start.5
  19.2 2.0 collective-permute-start.6
  21.2 10.1 %collective-permute-done.5 = s32[2,4]{1,0:T(2,128)S(1)} collective-permute-done((s32[2,4]{1,0:T(2,128)S(1)}, s32[2,4]{1,0:T(2,128)S(1)}, u32[]{:S(2)}, u32[]{:S(2)}) %collective-permute-start.5) | collective-permute-done | bytes 64 | tf_op jit(solution)/shard_map/ppermute | solution.py:73
  31.3 3.6 collective-permute-done.4
  36.9 2.2 q_high.1.refs_1_.refs_9_
  42.3 23.3 %collective-permute-done.7.refs_2_.refs_10_ = bf16[4,128,1024]{2,1,0:T(8,128)(2,1)S(1)} collective-permute-done((bf16[4,128,1024]{2,1,0:T(8,128)(2,1)}, bf16[4,128,1024]{2,1,0:T(8,128)(2,1)S(1)}, u32[]{:S(2)}, u32[]{:S(2)}) %collective-permute-start.7) | collective-permute-done | bytes 1048608 | tf_op jit(solution)/shard_map/q_one/ppermute | solution.py:73
  65.6 4.2 %all-to-all-start.1 = ((bf16[4,320,256]{2,1,0:T(8,128)(2,1)}), bf16[4,320,256]{2,1,0:T(8,128)(2,1)}, u32[]{:S(2)}, u32[]{:S(2)}) async-start(bf16[4,320,256]{2,1,0:T(8,128)(2,1)} %bitcast.95), calls=%async_computation.1 | async-start | bytes 1310720 | tf_op jit(solution)/shard_map/all_to_all | solution.py:630
  69.7 1.9 shard_map.278
  71.7 3.0 collective-permute-start.15
  76.1 9.8 %collective-permute-done.14.refs_1_ = bf16[128,1024]{1,0:T(8,128)(2,1)S(1)} collective-permute-done((bf16[128,1024]{1,0:T(8,128)(2,1)}, bf16[128,1024]{1,0:T(8,128)(2,1)S(1)}, u32[]{:S(2)}, u32[]{:S(2)}) %collective-permute-start.14) | collective-permute-done | bytes 262176 | tf_op jit(solution)/shard_map/fa_high/ppermute | solution.py:73
  85.8 7.5 %collective-permute-done.15.refs_2_ = bf16[128,1024]{1,0:T(8,128)(2,1)S(1)} collective-permute-done((bf16[128,1024]{1,0:T(8,128)(2,1)}, bf16[128,1024]{1,0:T(8,128)(2,1)S(1)}, u32[]{:S(2)}, u32[]{:S(2)}) %collective-permute-start.15) | collective-permute-done | bytes 262176 | tf_op jit(solution)/shard_map/fa_high/ppermute | solution.py:73
  94.7 2.2 fa_high.1.refs_1_
  96.9 2.1 collective-permute-start.20
  101.2 2.8 copy.37.refs_14_.refs_9_
  105.2 2.1 collective-permute-start.21
  107.3 20.8 %shard_map.277 = (bf16[320,1024]{1,0:T(8,128)(2,1)}, bf16[320,16]{1,0:T(8,128)(2,1)}, bf16[320,1024]{1,0:T(8,128)(2,1)}, bf16[320,1024]{1,0:T(8,128)(2,1)}, bf16...) custom-call(s32[4]{0:T(128)} %pad_add_fusion.2.refs_0_, ...), custom_call_target="tpu_custom_call" | custom-call | tf_op jit(solution)/shard_map/pallas_call | solution.py:52
  128.2 4.8 %collective-permute-start.17 = (bf16[128,1024]{1,0:T(8,128)(2,1)S(1)}, bf16[128,1024]{1,0:T(8,128)(2,1)S(1)}, u32[]{:S(2)}, u32[]{:S(2)}) collective-permute-start(bf16[128,1024]{1,0:T(8,128)(2,1)S(1)} %copy-done.20), channel_id=1, source_target_pairs={{0,8},{1,9},{2,10},{3,11},{4,12},{5,13},{6,14},{7,15},{8,0},{9,1},... | collective-permute-start | bytes 786440 | tf_op jit(solution)/shard_map/fb_high/ppermute | solution.py:73
  135.4 7.5 %collective-permute-done.17.refs_1_ = bf16[128,1024]{1,0:T(8,128)(2,1)S(1)} collective-permute-done((bf16[128,1024]{1,0:T(8,128)(2,1)S(1)}, bf16[128,1024]{1,0:T(8,128)(2,1)S(1)}, u32[]{:S(2)}, u32[]{:S(2)}) %collective-permute-start.17) | collective-permute-done | bytes 262176 | tf_op jit(solution)/shard_map/fb_high/ppermute | solution.py:73
  142.9 11.4 %collective-permute-done.18.refs_2_ = bf16[128,1024]{1,0:T(8,128)(2,1)S(1)} collective-permute-done((bf16[128,1024]{1,0:T(8,128)(2,1)S(1)}, bf16[128,1024]{1,0:T(8,128)(2,1)S(1)}, u32[]{:S(2)}, u32[]{:S(2)}) %collective-permute-start.18) | collective-permute-done | bytes 262176 | tf_op jit(solution)/shard_map/fb_high/ppermute | solution.py:73
  155.9 2.3 fb_high.1.refs_1_
  159.3 1.9 collective-permute-start.23
  162.6 15.3 %shard_map.279 = (f32[320,1024]{1,0:T(8,128)}, f32[320,1024]{1,0:T(8,128)}, f32[320,16]{1,0:T(8,128)}, f32[320,16]{1,0:T(8,128)}, bf16[320,1024]{1,0:T(8,128)(2,1)}, /*index=5*/bf16[16,4096]{1,0:T(8,128)(2,1)}) custom-call(s32[4]{0:T(128)} %pad_add_fusion.2.refs_0_, bf16[4,128,1024]{2,1,0:T(8,128)(2,1)} %fa_high.1.refs_1_, ...), custom_call_target="tpu_custom_call" | custom-call | tf_op jit(solution)/shard_map/pallas_call | solution.py:52
  177.8 5.9 %collective-permute-done.22.refs_2_ = bf16[4,128,1024]{2,1,0:T(8,128)(2,1)S(1)} collective-permute-done((bf16[4,128,1024]{2,1,0:T(8,128)(2,1)}, bf16[4,128,1024]{2,1,0:T(8,128)(2,1)S(1)}, u32[]{:S(2)}, u32[]{:S(2)}) %collective-permute-start.22) | collective-permute-done | bytes 1048608 | tf_op jit(solution)/shard_map/fb_one/ppermute | solution.py:73
  186.0 6.8 %all-to-all-start.2 = ((bf16[32,16,128]{2,1,0:T(8,128)(2,1)}), bf16[32,16,128]{2,1,0:T(8,128)(2,1)S(1)}, u32[]{:S(2)}, u32[]{:S(2)}) async-start(bf16[32,16,128]{2,1,0:T(8,128)(2,1)} %bitcast_bitcast_fusion.2), calls=%async_computation.2 | async-start | bytes 262144 | tf_op jit(solution)/shard_map/grads_a_send/all_to_all | solution.py:555
  193.5 7.4 %all-to-all-done.2.refs_0_ = bf16[32,16,128]{2,1,0:T(8,128)(2,1)S(1)} async-done(((bf16[32,16,128]{2,1,0:T(8,128)(2,1)}), bf16[32,16,128]{2,1,0:T(8,128)(2,1)S(1)}, u32[]{:S(2)}, u32[]{:S(2)}) %all-to-all-start.2) | async-done | bytes 131104 | tf_op jit(solution)/shard_map/grads_a_send/all_to_all | solution.py:555
  201.1 2.6 collective-permute-done.33.refs_8_
  204.8 21.2 %shard_map.280 = (bf16[4,320,256]{2,1,0:T(8,128)(2,1)}, bf16[320,1024]{1,0:T(8,128)(2,1)}, f32[320,1024]{1,0:T(8,128)}, bf16[16,8192]{1,0:T(8,128)(2,1)}) custom-call(s32[4]{0:T(128)} %pad_add_fusion.2.refs_0_, bf16[4,128,1024]{2,1,0:T(8,128)(2,1)} %fb_high.1.refs_1_, bf16[4,128,1024]{2,1,0:T(8,128)(2,1)} %copy-done.7, bf16[4,128,1024]{2,1,0:T(8,128)(2,1)} %copy-done.8, ...), custom_call_target="tpu_custom_call" | custom-call | tf_op jit(solution)/shard_map/pallas_call | solution.py:52
  226.0 1.7 copy.54
  227.7 5.0 %all-to-all-start.3 = ((bf16[32,16,256]{2,1,0:T(8,128)(2,1)}), bf16[32,16,256]{2,1,0:T(8,128)(2,1)S(1)}, u32[]{:S(2)}, u32[]{:S(2)}) async-start(bf16[32,16,256]{2,1,0:T(8,128)(2,1)} %bitcast.78), calls=%async_computation.3 | async-start | bytes 524288 | tf_op jit(solution)/shard_map/grads_b_send/all_to_all | solution.py:555
  232.7 13.2 %shard_map.281 = (bf16[320,1024]{1,0:T(8,128)(2,1)}, bf16[320,1024]{1,0:T(8,128)(2,1)}, bf16[320,1024]{1,0:T(8,128)(2,1)}, bf16[320,16]{1,0:T(8,128)(2,1)}, bf16[16,4096]{1,0:T(8,128)(2,1)}) custom-call(s32[4]{0:T(128)} %pad_add_fusion.2.refs_0_, f32[320,1]{1,0:T(8,128)} %sub.11.refs_10_.refs_1_, bf16[320,1024]{1,0:T(8,128)(2,1)} %get-tuple-element.60.refs_2_, ...), custom_call_target="tpu_custom_call" | custom-call | tf_op jit(solution)/shard_map/pallas_call | solution.py:52
  245.8 1.6 bitcast_bitcast_fusion.1
  247.4 5.8 %all-to-all-start.5 = ((bf16[32,16,128]{2,1,0:T(8,128)(2,1)}), bf16[32,16,128]{2,1,0:T(8,128)(2,1)S(1)}, u32[]{:S(2)}, u32[]{:S(2)}) async-start(bf16[32,16,128]{2,1,0:T(8,128)(2,1)} %bitcast_bitcast_fusion.1), calls=%async_computation.5 | async-start | bytes 262144 | tf_op jit(solution)/shard_map/grads_c_send/all_to_all | solution.py:555
  253.3 1.9 grads_b.5
  255.2 1.8 collective-permute-start.40
  256.9 2.4 collective-permute-start.41
  259.5 10.6 %shard_map.282 = bf16[4,640,256]{2,1,0:T(8,128)(2,1)} custom-call(s32[4]{0:T(128)} %pad_add_fusion.2.refs_0_, bf16[4,128,1024]{2,1,0:T(8,128)(2,1)} %q_high.1.refs_1_.refs_9_, bf16[4,128,1024]{2,1,0:T(8,128)(2,1)} %copy-done.2, bf16[4,128,1024]{2,1,0:T(8,128)(2,1)} %collective-permute-done.8.refs_3_.refs_11_, ...), custom_call_target="tpu_custom_call" | custom-call | tf_op jit(solution)/shard_map/pallas_call | solution.py:52
  271.5 1.8 grads_b.6
  273.3 1.8 collective-permute-start.43
  275.1 8.9 %collective-permute-done.43 = bf16[4,128,384]{2,1,0:T(8,128)(2,1)S(1)} collective-permute-done((bf16[4,128,384]{2,1,0:T(8,128)(2,1)}, bf16[4,128,384]{2,1,0:T(8,128)(2,1)S(1)}, u32[]{:S(2)}, u32[]{:S(2)}) %collective-permute-start.43) | collective-permute-done | bytes 393248 | tf_op jit(solution)/shard_map/grads_b/ppermute | solution.py:73
  284.7 2.1 grads_b.7
  286.7 1.7 collective-permute-start.44
  288.4 16.5 %collective-permute-done.44 = bf16[2,4,128,384]{3,2,1,0:T(8,128)(2,1)S(1)} collective-permute-done((bf16[2,4,128,384]{3,2,1,0:T(8,128)(2,1)}, bf16[2,4,128,384]{3,2,1,0:T(8,128)(2,1)S(1)}, u32[]{:S(2)}, u32[]{:S(2)}) %collective-permute-start.44) | collective-permute-done | bytes 786464 | tf_op jit(solution)/shard_map/grads_b/ppermute | solution.py:73
  305.8 2.6 grads_b.8
  308.4 1.6 grads_c.5
  310.7 3.3 collective-permute-start.35
  314.5 2.5 collective-permute-done.35.refs_2_
  317.0 3.0 collective-permute-done.36.refs_3_
  323.6 3.5 all-to-all-start.4
  327.9 1.7 grads_c.7
  329.6 1.8 collective-permute-start.38
  331.4 18.5 %collective-permute-done.38 = bf16[2,4,128,128]{3,2,1,0:T(8,128)(2,1)S(1)} collective-permute-done((bf16[2,4,128,128]{3,2,1,0:T(8,128)(2,1)}, bf16[2,4,128,128]{3,2,1,0:T(8,128)(2,1)S(1)}, u32[]{:S(2)}, u32[]{:S(2)}) %collective-permute-start.38) | collective-permute-done | bytes 262176 | tf_op jit(solution)/shard_map/grads_c/ppermute | solution.py:73
  350.7 1.9 grads_c.8
  352.5 2.1 collective-permute-done.39
  355.4 2.2 grads_c.9
  357.7 2.6 shard_map.283
  360.3 2.7 pad_maximum_fusion
  365.2 3.8 %grads_b.9 = bf16[2,2048,384]{2,1,0:T(8,128)(2,1)} custom-call(s32[1]{0:T(128)} %bitcast.20.which, bf16[2048,384]{1,0:T(8,128)(2,1)} %bitcast.81, bf16[2048,384]{1,0:T(8,128)(2,1)} %bitcast.87), custom_call_target="tpu_custom_call" | custom-call | tf_op jit(solution)/shard_map/grads_b/pallas_call | solution.py:52
  369.0 4.8 %shard_map.284 = (f32[128,4096]{1,0:T(8,128)}, f32[128,4096]{1,0:T(8,128)}, f32[128,1024]{1,0:T(8,128)}, f32[128,1024]{1,0:T(8,128)}, f32[128,1024]{1,0:T(8,128)}, /*index=5*/f32[128,1024]{1,0:T(8,128)}) custom-call(bf16[32,128,384]{2,1,0:T(8,128)(2,1)} %bitcast.79), custom_call_target="tpu_custom_call" | custom-call | tf_op jit(solution)/shard_map/pallas_call | solution.py:52
  (167 shorter events, 36.4 us)
Async XLA Ops:
  0.6 16.2 %copy-start.38 = (s32[4]{0:T(128)S(1)}, s32[4]{0:T(128)}, u32[]{:S(2)}) copy-start(s32[4]{0:T(128)} %param.24) | copy-start | bytes 52
  2.4 33.7 %collective-permute-start = (bf16[128,1024]{1,0:T(8,128)(2,1)}, bf16[128,1024]{1,0:T(8,128)(2,1)S(1)}, u32[]{:S(2)}, u32[]{:S(2)}) collective-permute-start(bf16[128,1024]{1,0:T(8,128)(2,1)} %shard_map.276.refs_0_), channel_id=1, source_target_pairs={{0,8},{1,9},{2,10},{3,11},{4,12},{5,13},{6,14},{7,15},{8,0},{9,1},... | collective-permute-start | bytes 786440 | tf_op jit(solution)/shard_map/q_high/ppermute | solution.py:73
  5.4 30.6 %collective-permute-start.1 = (bf16[128,1024]{1,0:T(8,128)(2,1)}, bf16[128,1024]{1,0:T(8,128)(2,1)S(1)}, u32[]{:S(2)}, u32[]{:S(2)}) collective-permute-start(bf16[128,1024]{1,0:T(8,128)(2,1)} %shard_map.276.refs_0_), channel_id=1, source_target_pairs={{0,16},{1,17},{2,18},{3,19},{4,20},{5,21},{6,22},{7,23},{8,24},{9,... | collective-permute-start | bytes 786440 | tf_op jit(solution)/shard_map/q_high/ppermute | solution.py:73
  8.0 28.1 %collective-permute-start.2 = (bf16[128,1024]{1,0:T(8,128)(2,1)}, bf16[128,1024]{1,0:T(8,128)(2,1)S(1)}, u32[]{:S(2)}, u32[]{:S(2)}) collective-permute-start(bf16[128,1024]{1,0:T(8,128)(2,1)} %shard_map.276.refs_0_), channel_id=1, source_target_pairs={{0,24},{1,25},{2,26},{3,27},{4,28},{5,29},{6,30},{7,31},{8,16},{9,... | collective-permute-start | bytes 786440 | tf_op jit(solution)/shard_map/q_high/ppermute | solution.py:73
  8.0 8.8 %collective-permute-start.3 = (s32[4]{0:T(128)}, s32[4]{0:T(128)S(1)}, u32[]{:S(2)}, u32[]{:S(2)}) collective-permute-start(s32[4]{0:T(128)} %param.24), channel_id=1, source_target_pairs={{0,4},{1,5},{2,6},{3,7},{4,0},{5,1},{6,2},{7,3},{8,12},{9,13},{10,... | collective-permute-start | bytes 56 | tf_op jit(solution)/shard_map/ppermute | solution.py:73
  13.3 25.9 %all-to-all-start = ((bf16[4,336,256]{2,1,0:T(8,128)(2,1)}), bf16[4,336,256]{2,1,0:T(8,128)(2,1)S(1)}, u32[]{:S(2)}, u32[]{:S(2)}) async-start(bf16[4,336,256]{2,1,0:T(8,128)(2,1)} %pad_maximum_fusion.1), calls=%async_computation | async-start | bytes 1376256 | tf_op jit(solution)/shard_map/all_to_all | solution.py:629
  17.4 13.9 %collective-permute-start.5 = (s32[2,4]{1,0:T(2,128)S(1)}, s32[2,4]{1,0:T(2,128)S(1)}, u32[]{:S(2)}, u32[]{:S(2)}) collective-permute-start(s32[2,4]{1,0:T(2,128)S(1)} %gather_fusion), channel_id=1, source_target_pairs={{0,16},{1,17},{2,18},{3,19},{4,20},{5,21},{6,22},{7,23},{8,24},{9,... | collective-permute-start | bytes 104 | tf_op jit(solution)/shard_map/ppermute | solution.py:73
  19.2 12.1 %collective-permute-start.6 = (s32[2,4]{1,0:T(2,128)S(1)}, s32[2,4]{1,0:T(2,128)S(1)}, u32[]{:S(2)}, u32[]{:S(2)}) collective-permute-start(s32[2,4]{1,0:T(2,128)S(1)} %gather_fusion), channel_id=1, source_target_pairs={{0,24},{1,25},{2,26},{3,27},{4,28},{5,29},{6,30},{7,31},{8,16},{9,... | collective-permute-start | bytes 104 | tf_op jit(solution)/shard_map/ppermute | solution.py:73
  31.3 3.6 collective-permute-start.4
  39.2 46.6 %copy-start.1 = (bf16[4,128,1024]{2,1,0:T(8,128)(2,1)S(1)}, bf16[4,128,1024]{2,1,0:T(8,128)(2,1)}, u32[]{:S(2)}) copy-start(bf16[4,128,1024]{2,1,0:T(8,128)(2,1)} %q_high.1.refs_1_.refs_9_) | copy-start | bytes 3145732
  39.2 57.7 %copy-start = (bf16[4,336,256]{2,1,0:T(8,128)(2,1)}, bf16[4,336,256]{2,1,0:T(8,128)(2,1)S(1)}, u32[]{:S(2)}) copy-start(bf16[4,336,256]{2,1,0:T(8,128)(2,1)S(1)} %all-to-all-done.refs_9_.refs_17_) | copy-start | bytes 2064388
  39.2 26.4 %collective-permute-start.7 = (bf16[4,128,1024]{2,1,0:T(8,128)(2,1)}, bf16[4,128,1024]{2,1,0:T(8,128)(2,1)S(1)}, u32[]{:S(2)}, u32[]{:S(2)}) collective-permute-start(bf16[4,128,1024]{2,1,0:T(8,128)(2,1)} %q_high.1.refs_1_.refs_9_), channel_id=1, source_target_pairs={{0,2},{1,5},{2,0},{3,7},{4,6},{5,1},{6,4},{7,3},{8,10},{9,13},{10,... | collective-permute-start | bytes 3145736 | tf_op jit(solution)/shard_map/q_one/ppermute | solution.py:73
  40.8 52.5 %collective-permute-start.8 = (bf16[4,128,1024]{2,1,0:T(8,128)(2,1)}, bf16[4,128,1024]{2,1,0:T(8,128)(2,1)}, u32[]{:S(2)}, u32[]{:S(2)}) collective-permute-start(bf16[4,128,1024]{2,1,0:T(8,128)(2,1)} %q_high.1.refs_1_.refs_9_), channel_id=1, source_target_pairs={{0,4},{1,3},{2,6},{3,1},{4,0},{5,7},{6,2},{7,5},{8,12},{9,11},{10,... | collective-permute-start | bytes 3145736 | tf_op jit(solution)/shard_map/q_two/ppermute | solution.py:73
  65.6 31.4 %copy-start.2 = (bf16[4,128,1024]{2,1,0:T(8,128)(2,1)}, bf16[4,128,1024]{2,1,0:T(8,128)(2,1)S(1)}, u32[]{:S(2)}) copy-start(bf16[4,128,1024]{2,1,0:T(8,128)(2,1)S(1)} %collective-permute-done.7.refs_2_.refs_10_) | copy-start | bytes 3145732
  65.6 28.2 %collective-permute-start.9 = (bf16[4,128,1024]{2,1,0:T(8,128)(2,1)S(1)}, bf16[4,128,1024]{2,1,0:T(8,128)(2,1)}, u32[]{:S(2)}, u32[]{:S(2)}) collective-permute-start(bf16[4,128,1024]{2,1,0:T(8,128)(2,1)S(1)} %collective-permute-done.7.refs_2_.refs_10_), channel_id=1, source_target_pairs={{0,4},{1,3},{2,6},{3,1},{4,0},{5,7},{6,2},{7,5},{8,12},{9,11},{10,... | collective-permute-start | bytes 3145736 | tf_op jit(solution)/shard_map/q_both/ppermute | solution.py:73
  65.6 31.4 %all-to-all-start.1 = ((bf16[4,320,256]{2,1,0:T(8,128)(2,1)}), bf16[4,320,256]{2,1,0:T(8,128)(2,1)}, u32[]{:S(2)}, u32[]{:S(2)}) async-start(bf16[4,320,256]{2,1,0:T(8,128)(2,1)} %bitcast.95), calls=%async_computation.1 | async-start | bytes 1310720 | tf_op jit(solution)/shard_map/all_to_all | solution.py:630
  71.7 14.1 %collective-permute-start.14 = (bf16[128,1024]{1,0:T(8,128)(2,1)}, bf16[128,1024]{1,0:T(8,128)(2,1)S(1)}, u32[]{:S(2)}, u32[]{:S(2)}) collective-permute-start(bf16[128,1024]{1,0:T(8,128)(2,1)} %get-tuple-element.66.refs_0_), channel_id=1, source_target_pairs={{0,8},{1,9},{2,10},{3,11},{4,12},{5,13},{6,14},{7,15},{8,0},{9,1},... | collective-permute-start | bytes 786440 | tf_op jit(solution)/shard_map/fa_high/ppermute | solution.py:73
  71.7 21.6 %collective-permute-start.15 = (bf16[128,1024]{1,0:T(8,128)(2,1)}, bf16[128,1024]{1,0:T(8,128)(2,1)S(1)}, u32[]{:S(2)}, u32[]{:S(2)}) collective-permute-start(bf16[128,1024]{1,0:T(8,128)(2,1)} %get-tuple-element.66.refs_0_), channel_id=1, source_target_pairs={{0,16},{1,17},{2,18},{3,19},{4,20},{5,21},{6,22},{7,23},{8,24},{9,... | collective-permute-start | bytes 786440 | tf_op jit(solution)/shard_map/fa_high/ppermute | solution.py:73
  74.7 19.2 %collective-permute-start.16 = (bf16[128,1024]{1,0:T(8,128)(2,1)}, bf16[128,1024]{1,0:T(8,128)(2,1)S(1)}, u32[]{:S(2)}, u32[]{:S(2)}) collective-permute-start(bf16[128,1024]{1,0:T(8,128)(2,1)} %get-tuple-element.66.refs_0_), channel_id=1, source_target_pairs={{0,24},{1,25},{2,26},{3,27},{4,28},{5,29},{6,30},{7,31},{8,16},{9,... | collective-permute-start | bytes 786440 | tf_op jit(solution)/shard_map/fa_high/ppermute | solution.py:73
  85.8 19.4 %collective-permute-start.10 = (bf16[4,128,1024]{2,1,0:T(8,128)(2,1)S(1)}, bf16[4,128,1024]{2,1,0:T(8,128)(2,1)}, u32[]{:S(2)}, u32[]{:S(2)}) collective-permute-start(bf16[4,128,1024]{2,1,0:T(8,128)(2,1)S(1)} %copy-done.1), channel_id=1, source_target_pairs={{0,1},{1,0},{2,3},{3,2},{4,5},{5,4},{6,7},{7,6},{8,9},{9,8},{10,11... | collective-permute-start | bytes 3145736 | tf_op jit(solution)/shard_map/q_core/ppermute | solution.py:73
  93.3 14.0 %collective-permute-start.11 = (bf16[4,128,1024]{2,1,0:T(8,128)(2,1)S(1)}, bf16[4,128,1024]{2,1,0:T(8,128)(2,1)}, u32[]{:S(2)}, u32[]{:S(2)}) collective-permute-start(bf16[4,128,1024]{2,1,0:T(8,128)(2,1)S(1)} %collective-permute-done.7.refs_2_.refs_10_), channel_id=1, source_target_pairs={{0,1},{1,0},{2,3},{3,2},{4,5},{5,4},{6,7},{7,6},{8,9},{9,8},{10,11... | collective-permute-start | bytes 3145736 | tf_op jit(solution)/shard_map/q_core/ppermute | solution.py:73
  93.3 13.9 %collective-permute-start.12 = (bf16[4,128,1024]{2,1,0:T(8,128)(2,1)}, bf16[4,128,1024]{2,1,0:T(8,128)(2,1)}, u32[]{:S(2)}, u32[]{:S(2)}) collective-permute-start(bf16[4,128,1024]{2,1,0:T(8,128)(2,1)} %collective-permute-done.8.refs_3_.refs_11_), channel_id=1, source_target_pairs={{0,1},{1,0},{2,3},{3,2},{4,5},{5,4},{6,7},{7,6},{8,9},{9,8},{10,11... | collective-permute-start | bytes 3145736 | tf_op jit(solution)/shard_map/q_core/ppermute | solution.py:73
  93.8 13.4 %collective-permute-start.13 = (bf16[4,128,1024]{2,1,0:T(8,128)(2,1)}, bf16[4,128,1024]{2,1,0:T(8,128)(2,1)}, u32[]{:S(2)}, u32[]{:S(2)}) collective-permute-start(bf16[4,128,1024]{2,1,0:T(8,128)(2,1)} %collective-permute-done.9.refs_4_.refs_12_), channel_id=1, source_target_pairs={{0,1},{1,0},{2,3},{3,2},{4,5},{5,4},{6,7},{7,6},{8,9},{9,8},{10,11... | collective-permute-start | bytes 3145736 | tf_op jit(solution)/shard_map/q_core/ppermute | solution.py:73
  96.9 8.2 %copy-start.3 = (bf16[4,128,1024]{2,1,0:T(8,128)(2,1)S(1)}, bf16[4,128,1024]{2,1,0:T(8,128)(2,1)}, u32[]{:S(2)}) copy-start(bf16[4,128,1024]{2,1,0:T(8,128)(2,1)} %fa_high.1.refs_1_) | copy-start | bytes 3145732
  96.9 31.2 %collective-permute-start.20 = (bf16[4,128,1024]{2,1,0:T(8,128)(2,1)}, bf16[4,128,1024]{2,1,0:T(8,128)(2,1)}, u32[]{:S(2)}, u32[]{:S(2)}) collective-permute-start(bf16[4,128,1024]{2,1,0:T(8,128)(2,1)} %fa_high.1.refs_1_), channel_id=1, source_target_pairs={{0,2},{1,5},{2,0},{3,7},{4,6},{5,1},{6,4},{7,3},{8,10},{9,13},{10,... | collective-permute-start | bytes 3145736 | tf_op jit(solution)/shard_map/fa_one/ppermute | solution.py:73
  105.2 23.1 %copy-start.20 = (bf16[128,1024]{1,0:T(8,128)(2,1)S(1)}, bf16[128,1024]{1,0:T(8,128)(2,1)}, u32[]{:S(2)}) copy-start(bf16[128,1024]{1,0:T(8,128)(2,1)} %get-tuple-element.67.refs_0_) | copy-start | bytes 786436
  105.2 49.2 %collective-permute-start.21 = (bf16[4,128,1024]{2,1,0:T(8,128)(2,1)S(1)}, bf16[4,128,1024]{2,1,0:T(8,128)(2,1)S(1)}, u32[]{:S(2)}, u32[]{:S(2)}) collective-permute-start(bf16[4,128,1024]{2,1,0:T(8,128)(2,1)S(1)} %copy-done.3), channel_id=1, source_target_pairs={{0,4},{1,3},{2,6},{3,1},{4,0},{5,7},{6,2},{7,5},{8,12},{9,11},{10,... | collective-permute-start | bytes 3145736 | tf_op jit(solution)/shard_map/fa_two/ppermute | solution.py:73
  128.1 26.8 %collective-permute-start.24 = (bf16[4,128,1024]{2,1,0:T(8,128)(2,1)}, bf16[4,128,1024]{2,1,0:T(8,128)(2,1)S(1)}, u32[]{:S(2)}, u32[]{:S(2)}) collective-permute-start(bf16[4,128,1024]{2,1,0:T(8,128)(2,1)} %collective-permute-done.20.refs_2_), channel_id=1, source_target_pairs={{0,4},{1,3},{2,6},{3,1},{4,0},{5,7},{6,2},{7,5},{8,12},{9,11},{10,... | collective-permute-start | bytes 3145736 | tf_op jit(solution)/shard_map/fa_both/ppermute | solution.py:73
  128.2 14.7 %collective-permute-start.17 = (bf16[128,1024]{1,0:T(8,128)(2,1)S(1)}, bf16[128,1024]{1,0:T(8,128)(2,1)S(1)}, u32[]{:S(2)}, u32[]{:S(2)}) collective-permute-start(bf16[128,1024]{1,0:T(8,128)(2,1)S(1)} %copy-done.20), channel_id=1, source_target_pairs={{0,8},{1,9},{2,10},{3,11},{4,12},{5,13},{6,14},{7,15},{8,0},{9,1},... | collective-permute-start | bytes 786440 | tf_op jit(solution)/shard_map/fb_high/ppermute | solution.py:73
  133.0 21.4 %collective-permute-start.18 = (bf16[128,1024]{1,0:T(8,128)(2,1)S(1)}, bf16[128,1024]{1,0:T(8,128)(2,1)S(1)}, u32[]{:S(2)}, u32[]{:S(2)}) collective-permute-start(bf16[128,1024]{1,0:T(8,128)(2,1)S(1)} %copy-done.20), channel_id=1, source_target_pairs={{0,16},{1,17},{2,18},{3,19},{4,20},{5,21},{6,22},{7,23},{8,24},{9,... | collective-permute-start | bytes 786440 | tf_op jit(solution)/shard_map/fb_high/ppermute | solution.py:73
  133.9 21.0 %collective-permute-start.19 = (bf16[128,1024]{1,0:T(8,128)(2,1)S(1)}, bf16[128,1024]{1,0:T(8,128)(2,1)S(1)}, u32[]{:S(2)}, u32[]{:S(2)}) collective-permute-start(bf16[128,1024]{1,0:T(8,128)(2,1)S(1)} %copy-done.20), channel_id=1, source_target_pairs={{0,24},{1,25},{2,26},{3,27},{4,28},{5,29},{6,30},{7,31},{8,16},{9,... | collective-permute-start | bytes 786440 | tf_op jit(solution)/shard_map/fb_high/ppermute | solution.py:73
  142.9 12.0 %copy-start.25 = (bf16[128,1024]{1,0:T(8,128)(2,1)}, bf16[128,1024]{1,0:T(8,128)(2,1)S(1)}, u32[]{:S(2)}) copy-start(bf16[128,1024]{1,0:T(8,128)(2,1)S(1)} %collective-permute-done.17.refs_1_) | copy-start | bytes 786436
  142.9 16.4 %collective-permute-start.25 = (bf16[4,128,1024]{2,1,0:T(8,128)(2,1)S(1)}, bf16[4,128,1024]{2,1,0:T(8,128)(2,1)S(1)}, u32[]{:S(2)}, u32[]{:S(2)}) collective-permute-start(bf16[4,128,1024]{2,1,0:T(8,128)(2,1)S(1)} %copy-done.3), channel_id=1, source_target_pairs={{0,1},{1,0},{2,3},{3,2},{4,5},{5,4},{6,7},{7,6},{8,9},{9,8},{10,11... | collective-permute-start | bytes 3145736 | tf_op jit(solution)/shard_map/fa_core/ppermute | solution.py:73
  154.3 6.9 %collective-permute-start.26 = (bf16[4,128,1024]{2,1,0:T(8,128)(2,1)}, bf16[4,128,1024]{2,1,0:T(8,128)(2,1)S(1)}, u32[]{:S(2)}, u32[]{:S(2)}) collective-permute-start(bf16[4,128,1024]{2,1,0:T(8,128)(2,1)} %collective-permute-done.20.refs_2_), channel_id=1, source_target_pairs={{0,1},{1,0},{2,3},{3,2},{4,5},{5,4},{6,7},{7,6},{8,9},{9,8},{10,11... | collective-permute-start | bytes 3145736 | tf_op jit(solution)/shard_map/fa_core/ppermute | solution.py:73
  154.4 6.9 %collective-permute-start.27 = (bf16[4,128,1024]{2,1,0:T(8,128)(2,1)S(1)}, bf16[4,128,1024]{2,1,0:T(8,128)(2,1)S(1)}, u32[]{:S(2)}, u32[]{:S(2)}) collective-permute-start(bf16[4,128,1024]{2,1,0:T(8,128)(2,1)S(1)} %collective-permute-done.21.refs_3_), channel_id=1, source_target_pairs={{0,1},{1,0},{2,3},{3,2},{4,5},{5,4},{6,7},{7,6},{8,9},{9,8},{10,11... | collective-permute-start | bytes 3145736 | tf_op jit(solution)/shard_map/fa_core/ppermute | solution.py:73
  154.9 6.4 %collective-permute-start.28 = (bf16[4,128,1024]{2,1,0:T(8,128)(2,1)S(1)}, bf16[4,128,1024]{2,1,0:T(8,128)(2,1)}, u32[]{:S(2)}, u32[]{:S(2)}) collective-permute-start(bf16[4,128,1024]{2,1,0:T(8,128)(2,1)S(1)} %collective-permute-done.24.refs_4_), channel_id=1, source_target_pairs={{0,1},{1,0},{2,3},{3,2},{4,5},{5,4},{6,7},{7,6},{8,9},{9,8},{10,11... | collective-permute-start | bytes 3145736 | tf_op jit(solution)/shard_map/fa_core/ppermute | solution.py:73
  158.2 25.5 %collective-permute-start.22 = (bf16[4,128,1024]{2,1,0:T(8,128)(2,1)}, bf16[4,128,1024]{2,1,0:T(8,128)(2,1)S(1)}, u32[]{:S(2)}, u32[]{:S(2)}) collective-permute-start(bf16[4,128,1024]{2,1,0:T(8,128)(2,1)} %fb_high.1.refs_1_), channel_id=1, source_target_pairs={{0,2},{1,5},{2,0},{3,7},{4,6},{5,1},{6,4},{7,3},{8,10},{9,13},{10,... | collective-permute-start | bytes 3145736 | tf_op jit(solution)/shard_map/fb_one/ppermute | solution.py:73
  159.3 34.1 %collective-permute-start.23 = (bf16[4,128,1024]{2,1,0:T(8,128)(2,1)}, bf16[4,128,1024]{2,1,0:T(8,128)(2,1)S(1)}, u32[]{:S(2)}, u32[]{:S(2)}) collective-permute-start(bf16[4,128,1024]{2,1,0:T(8,128)(2,1)} %fb_high.1.refs_1_), channel_id=1, source_target_pairs={{0,4},{1,3},{2,6},{3,1},{4,0},{5,7},{6,2},{7,5},{8,12},{9,11},{10,... | collective-permute-start | bytes 3145736 | tf_op jit(solution)/shard_map/fb_two/ppermute | solution.py:73
  162.5 30.3 %copy-start.4 = (bf16[4,128,1024]{2,1,0:T(8,128)(2,1)S(1)}, bf16[4,128,1024]{2,1,0:T(8,128)(2,1)}, u32[]{:S(2)}) copy-start(bf16[4,128,1024]{2,1,0:T(8,128)(2,1)} %fb_high.1.refs_1_) | copy-start | bytes 3145732
  183.7 20.1 %copy-start.7 = (bf16[4,128,1024]{2,1,0:T(8,128)(2,1)}, bf16[4,128,1024]{2,1,0:T(8,128)(2,1)S(1)}, u32[]{:S(2)}) copy-start(bf16[4,128,1024]{2,1,0:T(8,128)(2,1)S(1)} %collective-permute-done.22.refs_2_) | copy-start | bytes 3145732
  183.7 17.2 %collective-permute-start.29 = (bf16[4,128,1024]{2,1,0:T(8,128)(2,1)S(1)}, bf16[4,128,1024]{2,1,0:T(8,128)(2,1)}, u32[]{:S(2)}, u32[]{:S(2)}) collective-permute-start(bf16[4,128,1024]{2,1,0:T(8,128)(2,1)S(1)} %collective-permute-done.22.refs_2_), channel_id=1, source_target_pairs={{0,4},{1,3},{2,6},{3,1},{4,0},{5,7},{6,2},{7,5},{8,12},{9,11},{10,... | collective-permute-start | bytes 3145736 | tf_op jit(solution)/shard_map/fb_both/ppermute | solution.py:73
  186.0 14.9 %all-to-all-start.2 = ((bf16[32,16,128]{2,1,0:T(8,128)(2,1)}), bf16[32,16,128]{2,1,0:T(8,128)(2,1)S(1)}, u32[]{:S(2)}, u32[]{:S(2)}) async-start(bf16[32,16,128]{2,1,0:T(8,128)(2,1)} %bitcast_bitcast_fusion.2), calls=%async_computation.2 | async-start | bytes 262144 | tf_op jit(solution)/shard_map/grads_a_send/all_to_all | solution.py:555
  192.9 8.3 %collective-permute-start.30 = (bf16[4,128,1024]{2,1,0:T(8,128)(2,1)S(1)}, bf16[4,128,1024]{2,1,0:T(8,128)(2,1)}, u32[]{:S(2)}, u32[]{:S(2)}) collective-permute-start(bf16[4,128,1024]{2,1,0:T(8,128)(2,1)S(1)} %copy-done.4), channel_id=1, source_target_pairs={{0,1},{1,0},{2,3},{3,2},{4,5},{5,4},{6,7},{7,6},{8,9},{9,8},{10,11... | collective-permute-start | bytes 3145736 | tf_op jit(solution)/shard_map/fb_core/ppermute | solution.py:73
  193.0 8.1 %collective-permute-start.31 = (bf16[4,128,1024]{2,1,0:T(8,128)(2,1)S(1)}, bf16[4,128,1024]{2,1,0:T(8,128)(2,1)}, u32[]{:S(2)}, u32[]{:S(2)}) collective-permute-start(bf16[4,128,1024]{2,1,0:T(8,128)(2,1)S(1)} %collective-permute-done.22.refs_2_), channel_id=1, source_target_pairs={{0,1},{1,0},{2,3},{3,2},{4,5},{5,4},{6,7},{7,6},{8,9},{9,8},{10,11... | collective-permute-start | bytes 3145736 | tf_op jit(solution)/shard_map/fb_core/ppermute | solution.py:73
  193.4 10.3 %copy-start.8 = (bf16[4,128,1024]{2,1,0:T(8,128)(2,1)}, bf16[4,128,1024]{2,1,0:T(8,128)(2,1)S(1)}, u32[]{:S(2)}) copy-start(bf16[4,128,1024]{2,1,0:T(8,128)(2,1)S(1)} %collective-permute-done.23.refs_3_) | copy-start | bytes 3145732
  193.4 7.7 %collective-permute-start.32 = (bf16[4,128,1024]{2,1,0:T(8,128)(2,1)S(1)}, bf16[4,128,1024]{2,1,0:T(8,128)(2,1)}, u32[]{:S(2)}, u32[]{:S(2)}) collective-permute-start(bf16[4,128,1024]{2,1,0:T(8,128)(2,1)S(1)} %collective-permute-done.23.refs_3_), channel_id=1, source_target_pairs={{0,1},{1,0},{2,3},{3,2},{4,5},{5,4},{6,7},{7,6},{8,9},{9,8},{10,11... | collective-permute-start | bytes 3145736 | tf_op jit(solution)/shard_map/fb_core/ppermute | solution.py:73
  200.9 25.1 %copy-start.17 = (bf16[32,16,128]{2,1,0:T(8,128)(2,1)}, bf16[32,16,128]{2,1,0:T(8,128)(2,1)S(1)}, u32[]{:S(2)}) copy-start(bf16[32,16,128]{2,1,0:T(8,128)(2,1)S(1)} %all-to-all-done.2.refs_0_) | copy-start | bytes 393220
  200.9 2.9 collective-permute-start.33
  227.7 19.7 %all-to-all-start.3 = ((bf16[32,16,256]{2,1,0:T(8,128)(2,1)}), bf16[32,16,256]{2,1,0:T(8,128)(2,1)S(1)}, u32[]{:S(2)}, u32[]{:S(2)}) async-start(bf16[32,16,256]{2,1,0:T(8,128)(2,1)} %bitcast.78), calls=%async_computation.3 | async-start | bytes 524288 | tf_op jit(solution)/shard_map/grads_b_send/all_to_all | solution.py:555
  247.4 25.9 %all-to-all-start.5 = ((bf16[32,16,128]{2,1,0:T(8,128)(2,1)}), bf16[32,16,128]{2,1,0:T(8,128)(2,1)S(1)}, u32[]{:S(2)}, u32[]{:S(2)}) async-start(bf16[32,16,128]{2,1,0:T(8,128)(2,1)} %bitcast_bitcast_fusion.1), calls=%async_computation.5 | async-start | bytes 262144 | tf_op jit(solution)/shard_map/grads_c_send/all_to_all | solution.py:555
  255.2 15.0 %collective-permute-start.40 = (bf16[128,384]{1,0:T(8,128)(2,1)}, bf16[128,384]{1,0:T(8,128)(2,1)S(1)}, u32[]{:S(2)}, u32[]{:S(2)}) collective-permute-start(bf16[128,384]{1,0:T(8,128)(2,1)} %bitcast.102), channel_id=1, source_target_pairs={{0,8},{1,9},{2,10},{3,11},{4,12},{5,13},{6,14},{7,15},{8,0},{9,1},... | collective-permute-start | bytes 294920 | tf_op jit(solution)/shard_map/grads_b/ppermute | solution.py:73
  256.9 13.2 %collective-permute-start.41 = (bf16[128,384]{1,0:T(8,128)(2,1)}, bf16[128,384]{1,0:T(8,128)(2,1)S(1)}, u32[]{:S(2)}, u32[]{:S(2)}) collective-permute-start(bf16[128,384]{1,0:T(8,128)(2,1)} %bitcast.103), channel_id=1, source_target_pairs={{0,16},{1,17},{2,18},{3,19},{4,20},{5,21},{6,22},{7,23},{8,24},{9,... | collective-permute-start | bytes 294920 | tf_op jit(solution)/shard_map/grads_b/ppermute | solution.py:73
  259.3 10.9 %collective-permute-start.42 = (bf16[128,384]{1,0:T(8,128)(2,1)}, bf16[128,384]{1,0:T(8,128)(2,1)S(1)}, u32[]{:S(2)}, u32[]{:S(2)}) collective-permute-start(bf16[128,384]{1,0:T(8,128)(2,1)} %bitcast.104), channel_id=1, source_target_pairs={{0,24},{1,25},{2,26},{3,27},{4,28},{5,29},{6,30},{7,31},{8,16},{9,... | collective-permute-start | bytes 294920 | tf_op jit(solution)/shard_map/grads_b/ppermute | solution.py:73
  273.3 35.1 %copy-start.18 = (bf16[32,16,128]{2,1,0:T(8,128)(2,1)}, bf16[32,16,128]{2,1,0:T(8,128)(2,1)S(1)}, u32[]{:S(2)}) copy-start(bf16[32,16,128]{2,1,0:T(8,128)(2,1)S(1)} %all-to-all-done.5.refs_0_) | copy-start | bytes 393220
  273.3 10.6 %collective-permute-start.43 = (bf16[4,128,384]{2,1,0:T(8,128)(2,1)}, bf16[4,128,384]{2,1,0:T(8,128)(2,1)S(1)}, u32[]{:S(2)}, u32[]{:S(2)}) collective-permute-start(bf16[4,128,384]{2,1,0:T(8,128)(2,1)} %grads_b.6), channel_id=1, source_target_pairs={{0,4},{1,5},{2,6},{3,7},{4,0},{5,1},{6,2},{7,3},{8,12},{9,13},{10,... | collective-permute-start | bytes 1179656 | tf_op jit(solution)/shard_map/grads_b/ppermute | solution.py:73
  286.7 18.1 %collective-permute-start.44 = (bf16[2,4,128,384]{3,2,1,0:T(8,128)(2,1)}, bf16[2,4,128,384]{3,2,1,0:T(8,128)(2,1)S(1)}, u32[]{:S(2)}, u32[]{:S(2)}) collective-permute-start(bf16[2,4,128,384]{3,2,1,0:T(8,128)(2,1)} %bitcast.83), channel_id=1, source_target_pairs={{0,2},{1,3},{2,0},{3,1},{4,6},{5,7},{6,4},{7,5},{8,10},{9,11},{10,... | collective-permute-start | bytes 2359304 | tf_op jit(solution)/shard_map/grads_b/ppermute | solution.py:73
  308.4 55.7 %collective-permute-start.45 = (bf16[2,2,4,128,384]{4,3,2,1,0:T(8,128)(2,1)}, bf16[2,2,4,128,384]{4,3,2,1,0:T(8,128)(2,1)S(1)}, u32[]{:S(2)}, u32[]{:S(2)}) collective-permute-start(bf16[2,2,4,128,384]{4,3,2,1,0:T(8,128)(2,1)} %bitcast.80), channel_id=1, source_target_pairs={{0,1},{1,0},{2,3},{3,2},{4,5},{5,4},{6,7},{7,6},{8,9},{9,8},{10,11... | collective-permute-start | bytes 4718600 | tf_op jit(solution)/shard_map/grads_b/ppermute | solution.py:73
  310.1 4.4 %collective-permute-start.34 = (bf16[128,128]{1,0:T(8,128)(2,1)}, bf16[128,128]{1,0:T(8,128)(2,1)S(1)}, u32[]{:S(2)}, u32[]{:S(2)}) collective-permute-start(bf16[128,128]{1,0:T(8,128)(2,1)} %bitcast.109), channel_id=1, source_target_pairs={{0,8},{1,9},{2,10},{3,11},{4,12},{5,13},{6,14},{7,15},{8,0},{9,1},... | collective-permute-start | bytes 98312 | tf_op jit(solution)/shard_map/grads_c/ppermute | solution.py:73
  310.7 6.3 %collective-permute-start.35 = (bf16[128,128]{1,0:T(8,128)(2,1)}, bf16[128,128]{1,0:T(8,128)(2,1)S(1)}, u32[]{:S(2)}, u32[]{:S(2)}) collective-permute-start(bf16[128,128]{1,0:T(8,128)(2,1)} %bitcast.110), channel_id=1, source_target_pairs={{0,16},{1,17},{2,18},{3,19},{4,20},{5,21},{6,22},{7,23},{8,24},{9,... | collective-permute-start | bytes 98312 | tf_op jit(solution)/shard_map/grads_c/ppermute | solution.py:73
  314.1 5.9 %collective-permute-start.36 = (bf16[128,128]{1,0:T(8,128)(2,1)}, bf16[128,128]{1,0:T(8,128)(2,1)S(1)}, u32[]{:S(2)}, u32[]{:S(2)}) collective-permute-start(bf16[128,128]{1,0:T(8,128)(2,1)} %bitcast.111), channel_id=1, source_target_pairs={{0,24},{1,25},{2,26},{3,27},{4,28},{5,29},{6,30},{7,31},{8,16},{9,... | collective-permute-start | bytes 98312 | tf_op jit(solution)/shard_map/grads_c/ppermute | solution.py:73
  322.1 5.2 %collective-permute-start.37 = (bf16[4,128,128]{2,1,0:T(8,128)(2,1)}, bf16[4,128,128]{2,1,0:T(8,128)(2,1)S(1)}, u32[]{:S(2)}, u32[]{:S(2)}) collective-permute-start(bf16[4,128,128]{2,1,0:T(8,128)(2,1)} %grads_c.6), channel_id=1, source_target_pairs={{0,4},{1,5},{2,6},{3,7},{4,0},{5,1},{6,2},{7,3},{8,12},{9,13},{10,... | collective-permute-start | bytes 393224 | tf_op jit(solution)/shard_map/grads_c/ppermute | solution.py:73
  323.6 39.4 %all-to-all-start.4 = ((bf16[4,640,256]{2,1,0:T(8,128)(2,1)}), bf16[4,640,256]{2,1,0:T(8,128)(2,1)S(1)}, u32[]{:S(2)}, u32[]{:S(2)}) async-start(bf16[4,640,256]{2,1,0:T(8,128)(2,1)} %shard_map.282), calls=%async_computation.4 | async-start | bytes 2621440 | tf_op jit(solution)/shard_map/rows_out/all_to_all | solution.py:749
  329.6 20.4 %collective-permute-start.38 = (bf16[2,4,128,128]{3,2,1,0:T(8,128)(2,1)}, bf16[2,4,128,128]{3,2,1,0:T(8,128)(2,1)S(1)}, u32[]{:S(2)}, u32[]{:S(2)}) collective-permute-start(bf16[2,4,128,128]{3,2,1,0:T(8,128)(2,1)} %bitcast.89), channel_id=1, source_target_pairs={{0,2},{1,3},{2,0},{3,1},{4,6},{5,7},{6,4},{7,5},{8,10},{9,11},{10,... | collective-permute-start | bytes 786440 | tf_op jit(solution)/shard_map/grads_c/ppermute | solution.py:73
  352.5 2.1 collective-permute-start.39
  (27 other events, 56.8 us)

commit v4 on v3

--- a/solution.py
+++ b/solution.py
@@ -17,6 +17,7 @@
 SEQ = 320
 PAIR = 2 * HD
 EXTRA = 16
+FRONT, FFN_A, FFN_B, ATT, BACK = 56, 56, 56, 56, 56
 BF = jnp.bfloat16
 F32 = jnp.float32
 BOTH = ("row", "col")
@@ -48,14 +49,14 @@
     return inverse * (scaled - first_mean - unit_rows * second_mean)
 
 
-def call(kernel, outs, ins, spaces, scratch=()):
+def call(kernel, outs, ins, spaces, scratch=(), out_space=VMEM, mib=4):
     return pl.pallas_call(
         kernel,
         out_shape=outs,
         in_specs=[pl.BlockSpec(memory_space=s) for s in spaces],
-        out_specs=jax.tree.map(lambda _: pl.BlockSpec(memory_space=VMEM), outs),
+        out_specs=jax.tree.map(lambda _: pl.BlockSpec(memory_space=out_space), outs),
         scratch_shapes=list(scratch),
-        compiler_params=pltpu.CompilerParams(vmem_limit_bytes=56 << 20),
+        compiler_params=pltpu.CompilerParams(vmem_limit_bytes=mib << 20),
         cost_estimate=pl.CostEstimate(flops=0, bytes_accessed=0, transcendentals=0),
     )(*ins)
 
@@ -78,9 +79,14 @@
 
 
 def stack_kernel(which, *refs):
-    out = refs[-1]
-    for m, ref in enumerate(refs[:-1]):
-        out[which[0] ^ m] = ref[...]
+    parts, out, sems = refs[:-2], refs[-2], refs[-1]
+    copies = [
+        pltpu.make_async_copy(ref, out.at[which[0] ^ m], sems.at[m]) for m, ref in enumerate(parts)
+    ]
+    for copy in copies:
+        copy.start()
+    for copy in copies:
+        copy.wait()
 
 
 def stacked(parts, index):
@@ -91,7 +97,8 @@
         stack_kernel,
         out,
         [index.reshape(1).astype(jnp.int32)] + flat,
-        [pltpu.SMEM] + [VMEM] * len(parts),
+        [pltpu.SMEM] + [pl.ANY] * len(parts),
+        [pltpu.SemaphoreType.DMA((len(parts),))],
     )
     return made.reshape((len(parts),) + shape)
 
@@ -105,7 +112,7 @@
         else:
             parts.append(swap(block, lambda r, c: (r, c ^ step)))
     index = (lax.axis_index(axis) >> low_bit) & ((1 << width) - 1)
-    return stacked(parts, index)
+    return stacked(parts, index), parts
 
 
 def groups(top, bottom):
@@ -142,12 +149,42 @@
     return lax.optimization_barrier((value,) + others)[0]
 
 
+def after_all(values, *others):
+    return lax.optimization_barrier(tuple(values) + others)[: len(values)]
+
+
 def gather_high(shard):
     rows, cols = sizes()
-    block = shard
+    block, parts = shard, []
     for axis, bit, width in early_groups(rows, cols):
-        block = group_join(block, axis, bit, width)
-    return block.reshape((-1,) + shard.shape)
+        block, parts = group_join(block, axis, bit, width)
+    return block.reshape((-1,) + shard.shape), parts[1:]
+
+
+def lane_join_kernel(*refs):
+    parts, out, sems = refs[:-2], refs[-2], refs[-1]
+    copies, lane = [], 0
+    for i, part in enumerate(parts):
+        width = part.shape[-1]
+        copies.append(pltpu.make_async_copy(part, out.at[:, :, lane : lane + width], sems.at[i]))
+        lane += width
+    for copy in copies:
+        copy.start()
+    for copy in copies:
+        copy.wait()
+
+
+def lane_join(*parts):
+    if any(p.shape[-1] % 128 for p in parts):
+        return jnp.concatenate(parts, axis=-1)
+    shape = parts[0].shape[:-1] + (sum(p.shape[-1] for p in parts),)
+    return call(
+        lane_join_kernel,
+        jax.ShapeDtypeStruct(shape, parts[0].dtype),
+        parts,
+        [pl.ANY] * len(parts),
+        [pltpu.SemaphoreType.DMA((len(parts),))],
+    )
 
 
 def flip_one(r, c):
@@ -162,74 +199,40 @@
     return (r, c ^ 1)
 
 
-def all_steps(rows, cols):
-    return (
-        [("row",) + g for g in groups(bits_of(rows), 1)]
-        + [("row", 0, 1)]
-        + [("col",) + g for g in groups(bits_of(cols), 1)]
-        + [("col", 0, 1)]
-    )
-
-
-def all_table(rows, cols):
-    table = [0]
-    for axis, bit, width in all_steps(rows, cols):
-        stride = (cols if axis == "row" else 1) << bit
-        table = [old + value * stride for value in range(1 << width) for old in table]
-    return table
-
-
-def gather_leading(block, waits):
-    rows, cols = sizes()
-    shape = block.shape
-    for i, (axis, bit, width) in enumerate(all_steps(rows, cols)):
-        if i in waits:
-            block = after(block, *waits[i])
-        block = group_join(block, axis, bit, width)
-    return block.reshape((rows * cols,) + shape)
-
-
-def gather_owners(adapter_index):
-    rows, cols = sizes()
-    index = lax.axis_index("row")
-    block = adapter_index
-    for low_bit, width in reversed(groups(bits_of(rows), 0)):
-        parts = [block]
-        for m in range(1, 1 << width):
-            step = m << low_bit
-            parts.append(swap(block, lambda r, c: (r ^ step, c)))
-        here = (index >> low_bit) & ((1 << width) - 1)
-        block = jnp.stack(parts)[jnp.arange(1 << width) ^ here]
-    return block.reshape(-1)
+def with_cores(pieces):
+    return pieces + [swap(p, flip_core) for p in pieces]
+
+
+def piece_place(sc, k):
+    kind, away = k % 4, k // 4
+    turn = (sc[2] + away) & 1
+    return (0, 1 - turn, turn, 1)[kind], (0, turn, 1 - turn, 1)[kind], away
 
 
 class Weights:
     def __init__(self, sc, pieces, w, sems, lead, first_lane=0):
-        core, low_row = sc[2], sc[3]
-        self.copies = {}
+        self.copies = []
         depth = pieces[0].shape[1]
         taken = pl.ds(first_lane, w.shape[2])
         for k, piece in enumerate(pieces):
-            kind, away = k % 4, k // 4
-            turn = (core + away) & 1
-            x_rel = (0, 1 - turn, turn, 1)[kind]
-            y_rel = (0, turn, 1 - turn, 1)[kind]
+            x_rel, y_rel, away = piece_place(sc, k)
             for n, (high_col, high_row) in enumerate(lead):
                 slot = high_col * 4 + x_rel * 2 + away
-                row = (high_row * 2 + ((low_row + y_rel) & 1)) * depth
-                copy = pltpu.make_async_copy(
-                    piece.at[n, :, taken],
-                    w.at[slot, pl.ds(pl.multiple_of(row, depth), depth), :],
-                    sems.at[k, n],
+                row = (high_row * 2 + ((sc[3] + y_rel) & 1)) * depth
+                self.copies.append(
+                    pltpu.make_async_copy(
+                        piece.at[n, :, taken],
+                        w.at[slot, pl.ds(pl.multiple_of(row, depth), depth), :],
+                        sems.at[k, n],
+                    )
                 )
-                self.copies[(k, n)] = copy
 
     def start(self):
-        for copy in self.copies.values():
+        for copy in self.copies:
             copy.start()
 
     def wait(self):
-        for copy in self.copies.values():
+        for copy in self.copies:
             copy.wait()
 
 
@@ -240,6 +243,12 @@
 def weight_scratch(rows, cols, n):
     lead = len(lead_table(rows, cols))
     return [VMEM((cols, D, n), BF), pltpu.SemaphoreType.DMA((8, lead))]
+
+
+def put(ref, start, value, lane=0):
+    part = ref.shape[-1] - lane
+    for i in range(value.shape[-1] // part):
+        ref[start // part + i, :R, lane:] = value[:, i * part : (i + 1) * part]
 
 
 def lanes(start, width):
@@ -253,7 +262,21 @@
     out[:, 3 * hid :] = low(wp[...].astype(F32).T)
 
 
-def prep_f_kernel(w1, w2, out_a, out_b):
+def prep_rows_kernel(tokens, grads, bias_qv, bias_f, out):
+    cols, seq = out.shape[0], tokens.shape[1]
+    for c in range(cols):
+        out[c, :seq] = tokens[c]
+        out[c, seq : 2 * seq] = grads[c]
+        out[c, 2 * seq : 2 * seq + 2] = bias_qv[...]
+        out[c, 2 * seq + 2 : 2 * seq + 6] = bias_f[...]
+
+
+def prep_f_kernel(sc, mask, w1, w2, out_a, out_b, keep, closed):
+    row = mask[pl.ds(sc[1], 1), :].astype(F32)
+    row = jnp.concatenate([jnp.ones((1, BUF), F32), row], axis=1)
+    column = jnp.broadcast_to(row, (8, SEQ)).T[:, :1]
+    keep[...] = column
+    closed[...] = 1.0 - column
     half = w1.shape[1] // 2
     out_a[:, :half] = w1[:, :half]
     out_b[:, :half] = w1[:, half:]
@@ -284,10 +307,10 @@
 
     def project(slot, _):
         block = column_of(sc, slot)
-        up = jnp.concatenate([q_up[a, :, c, lanes(block * hid, hid)] for c in range(3)], axis=1)
+        up = jnp.concatenate([q_up[c, :, lanes(block * hid, hid)] for c in range(3)], axis=1)
         made = mm(n1[...], w[slot, :, : 3 * hid]) + mm(lat1[...], up)
-        bias_q = xa[block, SEQ : SEQ + 1, :].astype(F32)
-        bias_v = xa[block, SEQ + 1 : SEQ + 2, :].astype(F32)
+        bias_q = xa[block, 2 * SEQ : 2 * SEQ + 1, :].astype(F32)
+        bias_v = xa[block, 2 * SEQ + 1 : 2 * SEQ + 2, :].astype(F32)
         at = lanes(slot * hid, hid)
         q[:, at] = low(made[:, :hid] + bias_q) * jnp.asarray(0.125, BF)
         k[:, at] = low(made[:, hid : 2 * hid])
@@ -336,7 +359,7 @@
     lat3[...] = low(mm(n2[...], f_down[a], NT))
 
 
-def ffn_steps(sc, part, cols, w, xa, n2, lat3, gr, glat4, up_1, down_2, acc, early):
+def ffn_steps(sc, part, cols, w, xa, n2, lat3, gr, glat4, up_1, down_2, acc, early, lane=0):
     res, gn2, lat4, glat3 = acc
     a = sc[0]
     hid = D // cols
@@ -349,7 +372,8 @@
         block = column_of(sc, slot)
         at = pl.ds(pl.multiple_of(block * ffn + part * half, half), half)
         bias = jnp.concatenate(
-            [xa[block, SEQ + 2 + 2 * part + i : SEQ + 3 + 2 * part + i, :] for i in range(2)], axis=1
+            [xa[block, 2 * SEQ + 2 + 2 * part + i : 2 * SEQ + 3 + 2 * part + i, :] for i in range(2)],
+            axis=1,
         ).astype(F32)
         up, down = up_1[a, :, at], down_2[a, :, at]
         w1, w2 = w[slot, :, :half], w[slot, :, half:]
@@ -363,8 +387,8 @@
         glat3[...] += mm(grad_pre, up, NT)
         res[...] += mm(activated, w2, NT)
         gn2[...] += mm(grad_pre, w1, NT)
-        early[:, lanes(block * half, half)] = low(mm(lat3_t, grad_pre))
-        early[:, lanes(FF // 2 + block * half, half)] = low(mm(glat4_t, activated))
+        put(early, block * half, low(mm(lat3_t, grad_pre)), lane)
+        put(early, FF // 2 + block * half, low(mm(glat4_t, activated)), lane)
         return 0
 
     lax.fori_loop(0, cols, step, 0)
@@ -373,13 +397,13 @@
 def ffn_a_kernel(lead, cols, *refs):
     sc = refs[0]
     pieces = refs[1:9]
-    xa, ga, keep, n2, lat3, up_1, down_2, up_2 = refs[9:17]
-    res, gn2, lat4, glat3, gr, early = refs[17:23]
-    w, sems = refs[23:]
+    xa, keep, n2, lat3, up_1, down_2, up_2 = refs[9:16]
+    res, gn2, lat4, glat3, gr, early = refs[16:22]
+    w, sems = refs[22:]
     weights = Weights(sc, pieces, w, sems, lead)
     weights.start()
     gr[...] = low(
-        jnp.concatenate([ga[c] for c in range(cols)], axis=1).astype(F32) * keep[...]
+        jnp.concatenate([xa[c, SEQ : 2 * SEQ] for c in range(cols)], axis=1).astype(F32) * keep[...]
     )
     glat4 = low(mm(gr[...], up_2[sc[0]], NT))
     res[...] = jnp.zeros_like(res)
@@ -397,9 +421,12 @@
     pieces = refs[1:9]
     own_q = refs[9:17]
     (xa, keep, gain, n2, lat3, up_1, down_2, up_2, f_down, p_down, p_up, bias_out) = refs[17:29]
-    (middle, att, lat2, gr, res_in, gn2_in, lat4_in, glat3_in) = refs[29:37]
-    layer, gatt, gmid, early = refs[37:41]
-    w, sems, wp, sems_p, res, gn2, lat4, glat3 = refs[41:]
+    (middle, att, lat2, gr, res_in, gn2_in, lat4_in, glat3_in, early_in) = refs[29:38]
+    layer, gatt, gmid, early = refs[38:42]
+    w, sems, wp, sems_p, res, gn2, lat4, glat3 = refs[42:]
+    lane = early_in.shape[-1]
+    early[:, :R, :lane] = early_in[...]
+    early[:, R:] = low(jnp.full((early.shape[0], R, early.shape[2]), sc[0], F32))
     weights = Weights(sc, pieces, w, sems, lead)
     weights.start()
     proj = Weights(sc, own_q, wp, sems_p, lead, 3 * D // cols)
@@ -413,7 +440,7 @@
     glat3[...] = glat3_in[...]
     weights.wait()
     ffn_steps(
-        sc, 1, cols, w, xa, n2, lat3, gr, glat4, up_1, down_2, (res, gn2, lat4, glat3), early
+        sc, 1, cols, w, xa, n2, lat3, gr, glat4, up_1, down_2, (res, gn2, lat4, glat3), early, lane
     )
     mid = middle[...]
     lat4_low = low(lat4[...])
@@ -430,9 +457,9 @@
     gb = low(grad_middle)
     glat2 = low(mm(gb, p_up[a], NT))
     glat2_t = low(glat2.astype(F32).T)
-    early[:, FF + D : FF + 2 * D] = low(mm(low(lat2[...].astype(F32).T), gb))
-    early[:, FF + 2 * D : FF + 3 * D] = low(mm(low(glat3_low.astype(F32).T), n2[...]))
-    early[:, FF + 3 * D :] = low(mm(low(lat4_low.astype(F32).T), gr[...]))
+    put(early, FF + D, low(mm(low(lat2[...].astype(F32).T), gb)), lane)
+    put(early, FF + 2 * D, low(mm(low(glat3_low.astype(F32).T), n2[...])), lane)
+    put(early, FF + 3 * D, low(mm(low(lat4_low.astype(F32).T), gr[...])), lane)
     proj.wait()
 
     def step(slot, _):
@@ -440,7 +467,7 @@
         here = lanes(slot * hid, hid)
         there = lanes(block * hid, hid)
         gatt[:, here] = low(mm(gb, wp[slot]) + mm(glat2, p_down[a, :, there]))
-        early[:, lanes(FF + block * hid, hid)] = low(mm(glat2_t, att[:, here]))
+        put(early, FF + block * hid, low(mm(glat2_t, att[:, here])), lane)
         return 0
 
     lax.fori_loop(0, cols, step, 0)
@@ -485,15 +512,13 @@
         there = lanes(block * hid, hid)
         for c, g in enumerate((gq, gk, gv)):
             grad = g[:, here]
-            acc = acc + mm(grad, q_up[a, :, c, there], NT)
-            late[:, pl.ds(pl.multiple_of((c + 1) * D + block * hid, hid), hid)] = low(
-                mm(lat1_t, grad)
-            )
+            acc = acc + mm(grad, q_up[c, :, there], NT)
+            put(late, (c + 1) * D + block * hid, low(mm(lat1_t, grad)))
         return acc
 
     made = low(lax.fori_loop(0, cols, step, jnp.zeros((SEQ, R), F32)))
     glat1[...] = made
-    late[:, :D] = low(mm(low(made.astype(F32).T), n1[...]))
+    put(late, 0, low(mm(low(made.astype(F32).T), n1[...])))
 
 
 def back_kernel(lead, cols, *refs):
@@ -530,29 +555,68 @@
     for mine in mines:
         part = mine.shape[-1]
         for d in range(mine.shape[0]):
-            acc[owners[d], :, lane : lane + part] += mine[d].astype(F32)
+            acc[owners[d], :, lane : lane + part] += mine[d, :R].astype(F32)
         lane += part
     out[...] = low(acc[...])
 
 
-def spread_kernel(maps, parts, table, whole, *outs):
+def spread_kernel(lead, cols, parts, maps, *refs):
+    sc, pieces = refs[0], refs[1:9]
+    count = (len(refs) - 11) // 2
+    outs, whole, made = refs[9 : 9 + count], refs[9 + count], refs[10 + count : 10 + 2 * count]
+    sems_in, sems_out = refs[10 + 2 * count :]
+    copies = []
+    for k, piece in enumerate(pieces):
+        x_rel, y_rel, away = piece_place(sc, k)
+        for n, (high_col, high_row) in enumerate(lead):
+            row = high_row * 2 + ((sc[3] + y_rel) & 1)
+            col = high_col * 4 + ((sc[1] & 3) ^ (x_rel * 2 + away))
+            copies.append(
+                pltpu.make_async_copy(piece.at[n], whole.at[row * cols + col], sems_in.at[k, n])
+            )
+    for copy in copies:
+        copy.start()
+    for copy in copies:
+        copy.wait()
+    found = [[] for _ in outs]
     base = 0
     for part, spans in zip(parts, maps):
-        for out, put, start, width in spans:
+        for out, section, there, start, width in spans:
             for lane in range(0, width, 128):
                 at = start + lane
-                here = base + at % part
-                block = whole[table.index(at // part), :, here : here + 128]
-                outs[out][:, put + lane : put + lane + 128] = block.astype(F32)
+                found[out].append((section, there + lane, at // part, base + at % part))
         base += part
+    leaving = []
+    for i, (out, buffer) in enumerate(zip(outs, made)):
+        for section, there, device, here in found[i]:
+            block = whole[device, :, here : here + 128].astype(F32)
+            if section is None:
+                buffer[:, there : there + 128] = block
+            else:
+                buffer[:, section, :, there : there + 128] = block.reshape(NA, R, 128)
+        leaving.append(pltpu.make_async_copy(buffer, out, sems_out.at[i]))
+        leaving[-1].start()
+    for copy in leaving:
+        copy.wait()
+
+
+def place_kernel(lead, cols, *refs):
+    sc, pieces, out, sems = refs[0], refs[1:9], refs[9], refs[10]
+    copies = []
+    for k, piece in enumerate(pieces):
+        x_rel, y_rel, away = piece_place(sc, k)
+        for n, (high_col, high_row) in enumerate(lead):
+            row = high_row * 2 + ((sc[3] + y_rel) & 1)
+            col = high_col * 4 + ((sc[1] & 3) ^ (x_rel * 2 + away))
+            copies.append(pltpu.make_async_copy(piece.at[n], out.at[row * cols + col], sems.at[k, n]))
+    for copy in copies:
+        copy.start()
+    for copy in copies:
+        copy.wait()
 
 
 def send_grads(grads):
-    rows, cols = sizes()
-    devices = rows * cols
-    part = grads.shape[-1] // devices
-    pieces = grads.reshape(R, devices, part).transpose(1, 0, 2)
-    return lax.all_to_all(pieces, BOTH, split_axis=0, concat_axis=0, tiled=True)
+    return lax.all_to_all(grads, BOTH, split_axis=0, concat_axis=0, tiled=True)
 
 
 def sum_grads(mines, owners):
@@ -567,26 +631,47 @@
     return summed.reshape(NA * R, part)
 
 
-def spread(whole, parts, maps, widths):
+def spread(sc, pieces, parts, maps, shapes):
     rows, cols = sizes()
     devices = rows * cols
-    table = all_table(rows, cols)
+    lead = lead_table(rows, cols)
+    arrivals = pltpu.SemaphoreType.DMA((8, len(lead)))
+    whole = (devices, NA * R, sum(parts))
+    ins, spaces = [sc, *pieces], [pltpu.SMEM] + [pl.ANY] * 8
     if all(p % 128 == 0 for p in parts):
         return call(
-            functools.partial(spread_kernel, maps, parts, table),
-            [jax.ShapeDtypeStruct((NA * R, n), F32) for n in widths],
-            [whole],
-            [VMEM],
+            functools.partial(spread_kernel, lead, cols, parts, maps),
+            [jax.ShapeDtypeStruct(x, F32) for x in shapes],
+            ins,
+            spaces,
+            [VMEM(whole, BF)]
+            + [VMEM(x, F32) for x in shapes]
+            + [arrivals, pltpu.SemaphoreType.DMA((len(shapes),))],
+            pl.ANY,
+            56,
         )
-    whole = whole[jnp.array([table.index(d) for d in range(devices)])].astype(F32)
-    found = [[] for _ in widths]
+    whole = call(
+        functools.partial(place_kernel, lead, cols),
+        jax.ShapeDtypeStruct(whole, BF),
+        ins,
+        spaces,
+        [arrivals],
+    )
+    found = [[] for _ in shapes]
     base = 0
     for part, spans in zip(parts, maps):
         flat = jnp.swapaxes(whole[:, :, base : base + part], 0, 1).reshape(NA * R, devices * part)
-        for out, put, start, width in spans:
-            found[out].append((put, flat[:, start : start + width]))
+        for out, section, there, start, width in spans:
+            found[out].append((section or 0, there, flat[:, start : start + width].astype(F32)))
         base += part
-    return [jnp.concatenate([x for _, x in sorted(f, key=lambda e: e[0])], axis=1) for f in found]
+    return [
+        (
+            jnp.concatenate([x for _, _, x in sorted(f, key=lambda e: e[:2])], axis=1)
+            if len(shape) == 2
+            else jnp.stack([x.reshape(NA, R, -1) for _, _, x in sorted(f, key=lambda e: e[:2])], 1)
+        )
+        for f, shape in zip(found, shapes)
+    ]
 
 
 def per_device(
@@ -620,47 +705,51 @@
     blk = D // rows
     lead = lead_table(rows, cols)
 
-    biases = jnp.concatenate(
-        [bias_qv, bias_fc1.reshape(4, hid), jnp.zeros((EXTRA - 6, hid), BF)], axis=0
-    )
-    tokens = jnp.concatenate(
-        [tokens_in.reshape(cols, SEQ, hid), jnp.broadcast_to(biases, (cols, EXTRA, hid))], axis=1
-    )
-    xa = lax.all_to_all(tokens, "col", split_axis=0, concat_axis=0, tiled=True)
-    ga = lax.all_to_all(
-        grad_out.reshape(cols, SEQ, hid), "col", split_axis=0, concat_axis=0, tiled=True
-    )
     shard = jax.ShapeDtypeStruct((blk, n), BF)
     shard_q = call(prep_q_kernel, shard, [w_qkv, w_proj], [VMEM] * 2)
-    shard_a, shard_b = call(prep_f_kernel, [shard] * 2, [w_fc1, w_fc2], [VMEM] * 2)
-    owners = gather_owners(adapter_index)
     with jax.named_scope("q_high"):
-        own_q = gather_high(shard_q)
-    with jax.named_scope("fa_high"):
-        own_a = gather_high(after(shard_a, own_q))
-    with jax.named_scope("fb_high"):
-        own_b = gather_high(after(shard_b, own_a))
-    own_q = after(own_q, xa, owners)
+        own_q, came_q = gather_high(shard_q)
+    rows_in = call(
+        prep_rows_kernel,
+        jax.ShapeDtypeStruct((cols, 2 * SEQ + EXTRA, hid), BF),
+        [after(tokens_in, shard_q).reshape(cols, SEQ, hid), grad_out.reshape(cols, SEQ, hid), bias_qv]
+        + [bias_fc1.reshape(4, hid)],
+        [VMEM] * 4,
+    )
+    xa = lax.all_to_all(rows_in, "col", split_axis=0, concat_axis=0, tiled=True)
+    adapter = lax.dynamic_index_in_dim(adapter_index, column, 0, keepdims=False)
+    sc = jnp.stack([adapter, column, column % 2, row % 2]).astype(jnp.int32)
+    up_qkv = jnp.swapaxes(lax.dynamic_index_in_dim(qkv_up, adapter, 0, keepdims=False), 0, 1)
+    shard_a, shard_b, keep, closed = call(
+        prep_f_kernel,
+        [shard] * 2 + [jax.ShapeDtypeStruct((SEQ, 1), F32)] * 2,
+        [sc, keep_mask, w_fc1, w_fc2],
+        [pltpu.SMEM] + [VMEM] * 3,
+    )
+
+    own_q, shard_a, shard_b = after_all(
+        (own_q, shard_a, shard_b), xa, keep, closed, sc, up_qkv, *came_q
+    )
     with jax.named_scope("q_one"):
         one_q = swap(own_q, flip_one)
     with jax.named_scope("q_two"):
         two_q = swap(own_q, flip_two)
-    own_a = after(own_a, one_q, two_q, ga)
+    with jax.named_scope("fa_high"):
+        own_a, came_a = gather_high(shard_a)
+    own_q, one_q, two_q = after_all((own_q, one_q, two_q), *came_a)
     with jax.named_scope("q_both"):
         both_q = swap(one_q, flip_two)
     with jax.named_scope("q_core"):
-        pieces_q = [own_q, one_q, two_q, both_q]
-        pieces_q = pieces_q + [swap(p, flip_core) for p in pieces_q]
+        away_q = [swap(p, flip_core) for p in (own_q, one_q, two_q)]
+    both_q, own_a, shard_b = after_all((both_q, own_a, shard_b), *away_q)
+    with jax.named_scope("q_core"):
+        pieces_q = [own_q, one_q, two_q, both_q] + away_q + [swap(both_q, flip_core)]
     with jax.named_scope("fa_one"):
         one_a = swap(own_a, flip_one)
     with jax.named_scope("fa_two"):
         two_a = swap(own_a, flip_two)
-
-    mask_row = lax.dynamic_index_in_dim(keep_mask, column, 0, keepdims=False)
-    keep = jnp.concatenate([jnp.ones((BUF,), F32), mask_row.astype(F32)]).reshape(SEQ, 1)
-    closed = 1.0 - keep
-    adapter = lax.dynamic_index_in_dim(adapter_index, column, 0, keepdims=False)
-    sc = jnp.stack([adapter, column, column % 2, row % 2]).astype(jnp.int32)
+    with jax.named_scope("fb_high"):
+        own_b, came_b = gather_high(shard_b)
 
     def shaped(width, dtype, height=SEQ):
         return jax.ShapeDtypeStruct((height, width), dtype)
@@ -683,17 +772,21 @@
             big,
             small,
         ],
-        [sc, *pieces_q, xa, closed, ln_gain, ln_shift, qkv_down, qkv_up, proj_down, proj_up]
+        [sc, *pieces_q, xa, closed, ln_gain, ln_shift, qkv_down, up_qkv, proj_down]
+        + [proj_up]
         + [fc1_down, bias_out],
         [pltpu.SMEM] + any_space + [VMEM] * 10,
         scratch + [VMEM((SEQ, D), F32), VMEM((SEQ, D), F32)],
-    )
+        mib=FRONT,
+    )
+    own_a, one_a, two_a = after_all((own_a, one_a, two_a), n1, *came_b)
     with jax.named_scope("fa_both"):
-        both_a = swap(after(one_a, n1), flip_two)
+        both_a = swap(one_a, flip_two)
     with jax.named_scope("fa_core"):
-        pieces_a = [own_a, one_a, two_a, both_a]
-        pieces_a = pieces_a + [swap(p, flip_core) for p in pieces_a]
-    own_b = after(own_b, n1, one_a, two_a)
+        away_a = [swap(p, flip_core) for p in (own_a, one_a, two_a)]
+    both_a, own_b = after_all((both_a, own_b), *away_a)
+    with jax.named_scope("fa_core"):
+        pieces_a = [own_a, one_a, two_a, both_a] + away_a + [swap(both_a, flip_core)]
     with jax.named_scope("fb_one"):
         one_b = swap(own_b, flip_one)
     with jax.named_scope("fb_two"):
@@ -702,41 +795,45 @@
     thin = shaped(R, F32)
     res, gn2, lat4, glat3, gr, early_a = call(
         functools.partial(ffn_a_kernel, lead, cols),
-        [wide, wide, thin, thin, big, shaped(FF, BF, R)],
-        [sc, *pieces_a, xa, ga, keep, n2, lat3, fc1_up, fc2_down, fc2_up],
-        [pltpu.SMEM] + any_space + [VMEM] * 8,
+        [wide, wide, thin, thin, big, jax.ShapeDtypeStruct((rows * cols, R, FF // (rows * cols)), BF)],
+        [sc, *pieces_a, xa, keep, n2, lat3, fc1_up, fc2_down, fc2_up],
+        [pltpu.SMEM] + any_space + [VMEM] * 7,
         scratch,
-    )
+        mib=FFN_A,
+    )
+    own_b, one_b, two_b = after_all((own_b, one_b, two_b), res)
     with jax.named_scope("fb_both"):
-        both_b = swap(after(one_b, res), flip_two)
-    with jax.named_scope("grads_a_send"):
-        mine_a = send_grads(early_a)
+        both_b = swap(one_b, flip_two)
     with jax.named_scope("fb_core"):
-        pieces_b = [own_b, one_b, two_b, after(both_b, mine_a)]
-        pieces_b = pieces_b + [swap(p, flip_core) for p in pieces_b]
-    layer, gatt, gmid, early_b = call(
+        away_b = [swap(p, flip_core) for p in (own_b, one_b, two_b)]
+        pieces_b = [own_b, one_b, two_b, both_b] + away_b + [swap(both_b, flip_core)]
+    layer, gatt, gmid, grads_b = call(
         functools.partial(ffn_b_kernel, lead, cols),
-        [jax.ShapeDtypeStruct((cols, SEQ, hid), BF), big, wide, shaped(FF + 4 * D, BF, R)],
+        [jax.ShapeDtypeStruct((cols, SEQ, hid), BF), big, wide]
+        + [jax.ShapeDtypeStruct((rows * cols, 2 * R, 12 * D // (rows * cols)), BF)],
         [sc, *pieces_b, *pieces_q, xa, keep, ln_gain, n2, lat3, fc1_up, fc2_down, fc2_up]
         + [fc1_down, proj_down, proj_up, bias_out]
-        + [middle, att, lat2, gr, res, gn2, lat4, glat3],
-        [pltpu.SMEM] + any_space * 2 + [VMEM] * 20,
+        + [middle, att, lat2, gr, res, gn2, lat4, glat3, early_a],
+        [pltpu.SMEM] + any_space * 2 + [VMEM] * 21,
         scratch
         + [VMEM((cols, D, hid), BF), scratch[1]]
         + [VMEM((SEQ, D), F32), VMEM((SEQ, D), F32), VMEM((SEQ, R), F32), VMEM((SEQ, R), F32)],
+        mib=FFN_B,
     )
     with jax.named_scope("grads_b_send"):
-        mine_b = send_grads(early_b)
+        mine_b = send_grads(grads_b)
+        owners = mine_b[:, R, 0].astype(jnp.int32)
     gq, gk, gv, glat1, late = call(
         functools.partial(attention_back_kernel, cols),
-        [big, big, big, small, shaped(4 * D, BF, R)],
-        [sc, closed, q, k, v, lse, gatt, lat1, n1, qkv_up],
+        [big, big, big, small, jax.ShapeDtypeStruct((rows * cols, R, 4 * D // (rows * cols)), BF)],
+        [sc, closed, q, k, v, lse, gatt, lat1, n1, up_qkv],
         [pltpu.SMEM] + [VMEM] * 9,
+        mib=ATT,
     )
     with jax.named_scope("grads_c_send"):
         mine_c = send_grads(late)
     with jax.named_scope("grads_b"):
-        part_b = sum_grads([mine_a, after(mine_b, late)], owners)
+        part_b = sum_grads([after(mine_b, late)], owners)
     gmid = after(gmid, part_b)
     sent = call(
         functools.partial(back_kernel, lead, cols),
@@ -744,39 +841,44 @@
         [sc, *pieces_q, xa, ln_gain, gq, gk, gv, glat1, qkv_down, gmid, layer],
         [pltpu.SMEM] + any_space + [VMEM] * 9,
         scratch + [VMEM((SEQ, D), F32)],
-    )
+        mib=BACK,
+    )
+    with jax.named_scope("grads"):
+        own_b, _ = gather_high(part_b)
+        own_c, _ = gather_high(after(sum_grads([mine_c], owners), sent))
+        own = lane_join(own_b, own_c)
+        one, two = swap(own, flip_one), swap(own, flip_two)
+        both = swap(after(one, two), flip_two)
+        pieces = with_cores([own, one, two, both])
+        half = FF // cols // 2
+        map_a, map_b = (
+            tuple(
+                (out, None, (2 * block + part) * half, base + block * half, half)
+                for out, base in ((0, 0), (1, FF // 2))
+                for block in range(cols)
+            )
+            for part in (0, 1)
+        )
+        map_b = map_b + tuple((2 + i, None, 0, FF + i * D, D) for i in range(4))
+        map_c = ((6, None, 0, 0, D),) + tuple((7, c, 0, (c + 1) * D, D) for c in range(3))
+        parts = [early_a.shape[-1], mine_b.shape[-1] - early_a.shape[-1], mine_c.shape[-1]]
+        shapes = [(NA * R, FF)] * 2 + [(NA * R, D)] * 5 + [(NA, 3, R, D)]
+        sums = spread(sc, pieces, parts, [map_a, map_b, map_c], shapes)
+
     with jax.named_scope("rows_out"):
+        sent = after(sent, both)
         rows_out = lax.all_to_all(sent, "col", split_axis=0, concat_axis=0, tiled=True)
     layer, grad_in = rows_out[:, :SEQ], rows_out[:, SEQ:]
-    with jax.named_scope("grads_b"):
-        whole_b = gather_leading(part_b, {1: [sent, mine_c]})
-    with jax.named_scope("grads_c"):
-        whole_c = gather_leading(sum_grads([mine_c], owners), {})
-    half = FF // cols // 2
-    map_a, map_b = (
-        tuple(
-            (out, (2 * block + part) * half, base + block * half, half)
-            for out, base in ((0, 0), (1, FF // 2))
-            for block in range(cols)
-        )
-        for part in (0, 1)
-    )
-    map_b = map_b + tuple((2 + i, 0, FF + i * D, D) for i in range(4))
-    parts = [mine_a.shape[-1], mine_b.shape[-1]]
-    early_sum = spread(whole_b, parts, [map_a, map_b], [FF, FF, D, D, D, D])
-    map_c = tuple((i, 0, i * D, D) for i in range(4))
-    late_sum = spread(whole_c, [mine_c.shape[-1]], [map_c], [D] * 4)
-
-    def split(table, last=()):
-        return table.reshape((NA, R) + last + (-1,))
-
-    g_qkv_up = jnp.stack([split(t) for t in late_sum[1:]], axis=2)
-    g_fc1_up, g_fc2_down, g_proj_down, g_proj_up, g_fc1_down, g_fc2_up = map(split, early_sum)
+
+    def split(table):
+        return table.reshape((NA, R) + table.shape[1:])
+
+    g_fc1_up, g_fc2_down, g_proj_down, g_proj_up, g_fc1_down, g_fc2_up = map(split, sums[:6])
     return (
         layer.reshape(cols * SEQ, hid),
         grad_in.reshape(cols * SEQ, hid),
-        split(late_sum[0]),
-        g_qkv_up,
+        split(sums[6]),
+        jnp.swapaxes(sums[7], 1, 2),
         g_proj_down,
         g_proj_up,
         g_fc1_down,

time: 375 us -> 293 us (0.78)
  starting transfers between devices: 79.4 us -> 51.5 us
  Pallas kernels: 120 us -> 93.5 us
  local copies, waits for them, and re-layouts: 25.2 us -> 13.1 us
  waiting for transfers between devices: 141 us -> 130 us
  other arithmetic: 7.44 us -> 1.38 us
    pallas_call x22 -> x17, Pallas kernels: 120 us -> 93.5 us  [call(): pl.pallas_call(kernel, out_shape=outs, in_specs=[pl.BlockSpec(memory_spac...]
    ppermute x46 -> x43, waiting for transfers between devices: 133 us -> 116 us  [swap(): return lax.ppermute(block, BOTH, pairs)]
    all_to_all x5 -> x3, starting transfers between devices: 25.3 us -> 10.9 us  [the longest x2 6.48 us: send_grads(): return lax.all_to_all(grads, BOTH, split_axis=0, concat_axis=0, tiled=True)]
    ppermute x46 -> x43, starting transfers between devices: 50.6 us -> 37 us  [swap(): return lax.ppermute(block, BOTH, pairs)]
    unnamed x79 -> x86, local copies, waits for them, and re-layouts: 14.5 us -> 9.95 us
    all_to_all x1, waiting for transfers between devices: 0.01 us -> 4.12 us  [per_device(): lax.all_to_all(sent, 'col', split_axis=0, concat_axis=0, tiled=True)]
    all_to_all x5 -> x3, waiting for transfers between devices: 7.39 us -> 10 us  [the longest x2 10 us: send_grads(): return lax.all_to_all(grads, BOTH, split_axis=0, concat_axis=0, tiled=True)]
  transfers between devices with their start and end apart: 52 -> 47, of which waited for: 17 -> 26; matrix products, arithmetic and copies ran while one was open for 5% -> 1% of each run, Pallas kernels for 22% -> 24%
where the time goes in v4:
time: 293 us
  waiting for transfers between devices  130 us (44%)
  Pallas kernels  93.5 us (32%)
  starting transfers between devices  51.5 us (18%)
  local copies, waits for them, and re-layouts  13.1 us (4%)
  between operations  3.13 us (1%)
    ppermute x43, waiting for transfers between devices, swap(): return lax.ppermute(block, BOTH, pairs)  116 us
    pallas_call x17, Pallas kernels, call(): pl.pallas_call(kernel, out_shape=outs, in_specs=[pl.BlockSpec(memory_spac...  93.5 us
    ppermute x43, starting transfers between devices, swap(): return lax.ppermute(block, BOTH, pairs)  37 us
    all_to_all x2, waiting for transfers between devices, send_grads(): return lax.all_to_all(grads, BOTH, split_axis=0, concat_axis=0, tiled=True)  10 us
    unnamed x86, local copies, waits for them, and re-layouts  9.95 us
    all_to_all x2, starting transfers between devices, send_grads(): return lax.all_to_all(grads, BOTH, split_axis=0, concat_axis=0, tiled=True)  6.48 us
  transfers between devices with their start and end apart: 47, of which 26 were waited for; matrix products, arithmetic and copies ran while one was open for 1% of the time, Pallas kernels for 24%

profile of v4, /device:TPU:0, one launch (start us, length us, event | category | flops | bytes accessed | tf_op | source)
XLA Modules:
  0.0 292.6 jit_solution(5175144905055748950)
XLA Ops:
  1.4 0.9 copy-done.12
  2.4 0.8 copy-done.13
  3.3 1.1 copy-done.7
  4.4 1.1 copy-done.8
  6.2 1.2 shard_map.278
  7.3 4.4 %all-to-all-start = ((bf16[4,656,256]{2,1,0:T(8,128)(2,1)}), bf16[4,656,256]{2,1,0:T(8,128)(2,1)}, u32[]{:S(2)}, u32[]{:S(2)}) async-start(bf16[4,656,256]{2,1,0:T(8,128)(2,1)} %shard_map.278), calls=%async_computation | async-start | bytes 2686976 | tf_op jit(solution)/shard_map/all_to_all | solution.py:719
  11.8 5.1 %collective-permute-start.2 = (bf16[128,1024]{1,0:T(8,128)(2,1)S(1)}, bf16[128,1024]{1,0:T(8,128)(2,1)S(1)}, u32[]{:S(2)}, u32[]{:S(2)}) collective-permute-start(bf16[128,1024]{1,0:T(8,128)(2,1)S(1)} %shard_map.276.refs_0_), channel_id=1, source_target_pairs={{0,24},{1,25},{2,26},{3,27},{4,28},{5,29},{6,30},{7,31},{8,16},{9,... | collective-permute-start | bytes 786440 | tf_op jit(solution)/shard_map/q_high/ppermute | solution.py:74
  20.8 0.8 shard_map.277
  23.0 1.2 collective-permute-done.2.refs_3_
  24.2 15.6 %collective-permute-done.1.refs_2_ = bf16[128,1024]{1,0:T(8,128)(2,1)S(1)} collective-permute-done((bf16[128,1024]{1,0:T(8,128)(2,1)S(1)}, bf16[128,1024]{1,0:T(8,128)(2,1)S(1)}, u32[]{:S(2)}, u32[]{:S(2)}) %collective-permute-start.1) | collective-permute-done | bytes 262176 | tf_op jit(solution)/shard_map/q_high/ppermute | solution.py:74
  39.9 1.6 collective-permute-start.4
  41.5 1.7 collective-permute-start.3
  43.2 2.5 collective-permute-start.7
  45.7 1.9 collective-permute-start.5
  47.6 6.8 %collective-permute-done.7.refs_3_ = bf16[128,1024]{1,0:T(8,128)(2,1)S(1)} collective-permute-done((bf16[128,1024]{1,0:T(8,128)(2,1)S(1)}, bf16[128,1024]{1,0:T(8,128)(2,1)S(1)}, u32[]{:S(2)}, u32[]{:S(2)}) %collective-permute-start.7) | collective-permute-done | bytes 262176 | tf_op jit(solution)/shard_map/fa_high/ppermute | solution.py:74
  54.3 11.8 %collective-permute-done.6.refs_2_ = bf16[128,1024]{1,0:T(8,128)(2,1)S(1)} collective-permute-done((bf16[128,1024]{1,0:T(8,128)(2,1)S(1)}, bf16[128,1024]{1,0:T(8,128)(2,1)S(1)}, u32[]{:S(2)}, u32[]{:S(2)}) %collective-permute-start.6) | collective-permute-done | bytes 262176 | tf_op jit(solution)/shard_map/fa_high/ppermute | solution.py:74
  66.8 1.2 collective-permute-start.8
  68.1 0.8 collective-permute-done.9.refs_5_.refs_13_
  68.9 1.5 collective-permute-done.11.refs_7_.refs_15_
  70.4 1.5 collective-permute-done.10.refs_6_.refs_14_
  71.9 9.7 %collective-permute-done.8.refs_4_.refs_12_ = bf16[4,128,1024]{2,1,0:T(8,128)(2,1)S(1)} collective-permute-done((bf16[4,128,1024]{2,1,0:T(8,128)(2,1)S(1)}, bf16[4,128,1024]{2,1,0:T(8,128)(2,1)S(1)}, u32[]{:S(2)}, u32[]{:S(2)}) %collective-permute-start.8) | collective-permute-done | bytes 1048608 | tf_op jit(solution)/shard_map/q_both/ppermute | solution.py:74
  81.6 1.2 collective-permute-start.14
  83.3 2.5 collective-permute-start.17
  85.9 2.0 collective-permute-start.15
  87.9 20.7 %shard_map.279 = (bf16[320,1024]{1,0:T(8,128)(2,1)}, bf16[320,16]{1,0:T(8,128)(2,1)}, bf16[320,1024]{1,0:T(8,128)(2,1)}, bf16[320,1024]{1,0:T(8,128)(2,1)}, bf16...) custom-call(s32[4]{0:T(128)} %copy-done.14, ...), custom_call_target="tpu_custom_call" | custom-call | tf_op jit(solution)/shard_map/pallas_call | solution.py:53
  109.3 0.9 collective-permute-start.18
  110.3 1.8 collective-permute-done.19.refs_5_
  112.1 1.0 collective-permute-done.21.refs_7_
  113.1 1.5 collective-permute-done.20.refs_6_
  114.6 9.7 %collective-permute-done.18.refs_4_ = bf16[4,128,1024]{2,1,0:T(8,128)(2,1)S(1)} collective-permute-done((bf16[4,128,1024]{2,1,0:T(8,128)(2,1)}, bf16[4,128,1024]{2,1,0:T(8,128)(2,1)S(1)}, u32[]{:S(2)}, u32[]{:S(2)}) %collective-permute-start.18) | collective-permute-done | bytes 1048608 | tf_op jit(solution)/shard_map/fa_both/ppermute | solution.py:74
  124.3 1.0 copy-done.32
  125.3 0.9 collective-permute-start.23
  126.1 1.4 collective-permute-start.22
  127.6 1.0 copy-done.35
  128.6 15.5 %shard_map.280 = (f32[320,1024]{1,0:T(8,128)}, f32[320,1024]{1,0:T(8,128)}, f32[320,16]{1,0:T(8,128)}, f32[320,16]{1,0:T(8,128)}, bf16[320,1024]{1,0:T(8,128)(2,1)}, /*index=5*/bf16[32,16,128]{2,1,0:T(8,128)(2,1)}) custom-call(s32[4]{0:T(128)} %copy-done.14, bf16[4,128,1024]{2,1,0:T(8,128)(2,1)} %copy-done.3, ...), custom_call_target="tpu_custom_call" | custom-call | tf_op jit(solution)/shard_map/pallas_call | solution.py:53
  144.1 6.9 %collective-permute-done.23.refs_3_ = bf16[4,128,1024]{2,1,0:T(8,128)(2,1)S(1)} collective-permute-done((bf16[4,128,1024]{2,1,0:T(8,128)(2,1)S(1)}, bf16[4,128,1024]{2,1,0:T(8,128)(2,1)S(1)}, u32[]{:S(2)}, u32[]{:S(2)}) %collective-permute-start.23) | collective-permute-done | bytes 1048608 | tf_op jit(solution)/shard_map/fb_two/ppermute | solution.py:74
  151.0 0.9 collective-permute-start.25
  152.5 13.4 %collective-permute-done.25.refs_4_ = bf16[4,128,1024]{2,1,0:T(8,128)(2,1)S(1)} collective-permute-done((bf16[4,128,1024]{2,1,0:T(8,128)(2,1)S(1)}, bf16[4,128,1024]{2,1,0:T(8,128)(2,1)S(1)}, u32[]{:S(2)}, u32[]{:S(2)}) %collective-permute-start.25) | collective-permute-done | bytes 1048608 | tf_op jit(solution)/shard_map/fb_both/ppermute | solution.py:74
  166.0 2.6 collective-permute-done.29.refs_8_
  168.6 1.0 copy-done.34
  169.6 22.0 %shard_map.281 = (bf16[4,320,256]{2,1,0:T(8,128)(2,1)}, bf16[320,1024]{1,0:T(8,128)(2,1)}, f32[320,1024]{1,0:T(8,128)}, bf16[32,32,384]{2,1,0:T(8,128)(2,1)}) custom-call(s32[4]{0:T(128)} %copy-done.14, bf16[4,128,1024]{2,1,0:T(8,128)(2,1)} %copy-done.4, bf16[4,128,1024]{2,1,0:T(8,128)(2,1)} %copy-done.25, bf16[4,128,1024]{2,1,0:T(8,128)(2,1)} %copy-done.24, ...), custom_call_target="tpu_custom_call" | custom-call | tf_op jit(solution)/shard_map/pallas_call | solution.py:53
  191.6 2.9 all-to-all-start.1
  194.5 13.0 %shard_map.282 = (bf16[320,1024]{1,0:T(8,128)(2,1)}, bf16[320,1024]{1,0:T(8,128)(2,1)}, bf16[320,1024]{1,0:T(8,128)(2,1)}, bf16[320,16]{1,0:T(8,128)(2,1)}, bf16[32,16,128]{2,1,0:T(8,128)(2,1)}) custom-call(s32[4]{0:T(128)} %copy-done.14, f32[320,1]{1,0:T(8,128)} %copy-done.9, bf16[320,1024]{1,0:T(8,128)(2,1)} %get-tuple-element.83.refs_2_, ...), custom_call_target="tpu_custom_call" | custom-call | tf_op jit(solution)/shard_map/pallas_call | solution.py:53
  207.5 7.6 %all-to-all-done.1.refs_0_ = bf16[32,32,384]{2,1,0:T(8,128)(2,1)S(1)} async-done(((bf16[32,32,384]{2,1,0:T(8,128)(2,1)}), bf16[32,32,384]{2,1,0:T(8,128)(2,1)S(1)}, u32[]{:S(2)}, u32[]{:S(2)}) %all-to-all-start.1) | async-done | bytes 786464 | tf_op jit(solution)/shard_map/grads_b_send/all_to_all | solution.py:619
  215.1 3.6 %all-to-all-start.2 = ((bf16[32,16,128]{2,1,0:T(8,128)(2,1)}), bf16[32,16,128]{2,1,0:T(8,128)(2,1)S(1)}, u32[]{:S(2)}, u32[]{:S(2)}) async-start(bf16[32,16,128]{2,1,0:T(8,128)(2,1)} %get-tuple-element.117), calls=%async_computation.2 | async-start | bytes 262144 | tf_op jit(solution)/shard_map/grads_c_send/all_to_all | solution.py:619
  220.1 3.7 %collective-permute-start.32 = (bf16[128,384]{1,0:T(8,128)(2,1)S(1)}, bf16[128,384]{1,0:T(8,128)(2,1)S(1)}, u32[]{:S(2)}, u32[]{:S(2)}) collective-permute-start(bf16[128,384]{1,0:T(8,128)(2,1)S(1)} %bitcast.25), channel_id=1, source_target_pairs={{0,24},{1,25},{2,26},{3,27},{4,28},{5,29},{6,30},{7,31},{8,16},{9,... | collective-permute-start | bytes 294920 | tf_op jit(solution)/shard_map/grads/ppermute | solution.py:74
  224.6 2.4 all-to-all-done.2.refs_0_
  227.7 10.7 %shard_map.283 = bf16[4,640,256]{2,1,0:T(8,128)(2,1)} custom-call(s32[4]{0:T(128)} %copy-done.14, bf16[4,128,1024]{2,1,0:T(8,128)(2,1)} %copy-done.2, bf16[4,128,1024]{2,1,0:T(8,128)(2,1)} %copy-done.18, bf16[4,128,1024]{2,1,0:T(8,128)(2,1)} %copy-done.17, bf16[4,128,1024]{2,1,0:T(8,128)(2,1)} %copy-done.22, bf16[4,128,1024]{2,1,0:T(8,128)(2,1)} %copy-done.19, ...), custom_call_target="tpu_custom_call" | custom-call | tf_op jit(solution)/shard_map/pallas_call | solution.py:53
  238.4 1.4 collective-permute-start.35
  239.8 0.9 collective-permute-start.34
  240.7 3.8 %collective-permute-done.35.refs_3_ = bf16[128,128]{1,0:T(8,128)(2,1)S(1)} collective-permute-done((bf16[128,128]{1,0:T(8,128)(2,1)S(1)}, bf16[128,128]{1,0:T(8,128)(2,1)S(1)}, u32[]{:S(2)}, u32[]{:S(2)}) %collective-permute-start.35) | collective-permute-done | bytes 32800 | tf_op jit(solution)/shard_map/grads/ppermute | solution.py:74
  244.4 0.8 collective-permute-done.34.refs_2_
  245.2 3.1 %collective-permute-done.33.refs_1_ = bf16[128,128]{1,0:T(8,128)(2,1)S(1)} collective-permute-done((bf16[128,128]{1,0:T(8,128)(2,1)S(1)}, bf16[128,128]{1,0:T(8,128)(2,1)S(1)}, u32[]{:S(2)}, u32[]{:S(2)}) %collective-permute-start.33) | collective-permute-done | bytes 32800 | tf_op jit(solution)/shard_map/grads/ppermute | solution.py:74
  249.8 1.0 collective-permute-start.36
  250.8 10.5 %collective-permute-done.37.refs_3_ = bf16[4,128,512]{2,1,0:T(8,128)(2,1)S(1)} collective-permute-done((bf16[4,128,512]{2,1,0:T(8,128)(2,1)S(1)}, bf16[4,128,512]{2,1,0:T(8,128)(2,1)S(1)}, u32[]{:S(2)}, u32[]{:S(2)}) %collective-permute-start.37) | collective-permute-done | bytes 524320 | tf_op jit(solution)/shard_map/grads/ppermute | solution.py:74
  261.3 0.9 collective-permute-start.38
  262.2 8.4 %collective-permute-done.38.refs_4_ = bf16[4,128,512]{2,1,0:T(8,128)(2,1)} collective-permute-done((bf16[4,128,512]{2,1,0:T(8,128)(2,1)S(1)}, bf16[4,128,512]{2,1,0:T(8,128)(2,1)}, u32[]{:S(2)}, u32[]{:S(2)}) %collective-permute-start.38) | collective-permute-done | bytes 524320 | tf_op jit(solution)/shard_map/grads/ppermute | solution.py:74
  270.6 3.5 %all-to-all-start.3 = ((bf16[4,640,256]{2,1,0:T(8,128)(2,1)}), bf16[4,640,256]{2,1,0:T(8,128)(2,1)S(1)}, u32[]{:S(2)}, u32[]{:S(2)}) async-start(bf16[4,640,256]{2,1,0:T(8,128)(2,1)} %shard_map.283), calls=%async_computation.3 | async-start | bytes 2621440 | tf_op jit(solution)/shard_map/rows_out/all_to_all | solution.py:870
  275.3 1.2 collective-permute-done.39.refs_5_
  276.5 1.5 collective-permute-done.41.refs_7_
  279.6 0.8 copy-done.41
  280.4 6.9 %grads.9 = (f32[128,4096]{1,0:T(8,128)}, f32[128,4096]{1,0:T(8,128)}, f32[128,1024]{1,0:T(8,128)}, f32[128,1024]{1,0:T(8,128)}, f32[128,1024]{1,0:T(8,128)}, /*i...) custom-call(s32[4]{0:T(128)} %copy-done.14, bf16[4,128,512]{2,1,0:T(8,128)(2,1)} %copy-done.5, ...), custom_call_target="tpu_custom_call" | custom-call | tf_op jit(solution)/shard_map/grads/pallas_call | solution.py:53
  287.3 4.1 %all-to-all-done.3 = bf16[4,640,256]{2,1,0:T(8,128)(2,1)S(1)} async-done(((bf16[4,640,256]{2,1,0:T(8,128)(2,1)}), bf16[4,640,256]{2,1,0:T(8,128)(2,1)S(1)}, u32[]{:S(2)}, u32[]{:S(2)}) %all-to-all-start.3) | async-done | bytes 1310752 | tf_op jit(solution)/shard_map/rows_out/all_to_all | solution.py:870
  291.4 1.1 fusion.1
  (139 shorter events, 14.7 us)
Async XLA Ops:
  0.6 21.7 %copy-start = (bf16[8,16,3,1024]{3,1,2,0:T(8,128)(2,1)S(1)}, bf16[8,16,3,1024]{3,1,2,0:T(8,128)(2,1)}, u32[]{:S(2)}) copy-start(bf16[8,16,3,1024]{3,1,2,0:T(8,128)(2,1)} %param.35) | copy-start | bytes 2359300
  7.3 13.5 %copy-start.15 = (s32[4,256]{1,0:T(4,128)S(1)}, s32[4,256]{1,0:T(4,128)}, u32[]{:S(2)}) copy-start(s32[4,256]{1,0:T(4,128)} %mask.1) | copy-start | bytes 12292
  7.3 32.6 %all-to-all-start = ((bf16[4,656,256]{2,1,0:T(8,128)(2,1)}), bf16[4,656,256]{2,1,0:T(8,128)(2,1)}, u32[]{:S(2)}, u32[]{:S(2)}) async-start(bf16[4,656,256]{2,1,0:T(8,128)(2,1)} %shard_map.278), calls=%async_computation | async-start | bytes 2686976 | tf_op jit(solution)/shard_map/all_to_all | solution.py:719
  11.8 12.4 %collective-permute-start.2 = (bf16[128,1024]{1,0:T(8,128)(2,1)S(1)}, bf16[128,1024]{1,0:T(8,128)(2,1)S(1)}, u32[]{:S(2)}, u32[]{:S(2)}) collective-permute-start(bf16[128,1024]{1,0:T(8,128)(2,1)S(1)} %shard_map.276.refs_0_), channel_id=1, source_target_pairs={{0,24},{1,25},{2,26},{3,27},{4,28},{5,29},{6,30},{7,31},{8,16},{9,... | collective-permute-start | bytes 786440 | tf_op jit(solution)/shard_map/q_high/ppermute | solution.py:74
  16.9 22.8 %collective-permute-start.1 = (bf16[128,1024]{1,0:T(8,128)(2,1)S(1)}, bf16[128,1024]{1,0:T(8,128)(2,1)S(1)}, u32[]{:S(2)}, u32[]{:S(2)}) collective-permute-start(bf16[128,1024]{1,0:T(8,128)(2,1)S(1)} %shard_map.276.refs_0_), channel_id=1, source_target_pairs={{0,16},{1,17},{2,18},{3,19},{4,20},{5,21},{6,22},{7,23},{8,24},{9,... | collective-permute-start | bytes 786440 | tf_op jit(solution)/shard_map/q_high/ppermute | solution.py:74
  16.9 22.8 %collective-permute-start = (bf16[128,1024]{1,0:T(8,128)(2,1)S(1)}, bf16[128,1024]{1,0:T(8,128)(2,1)S(1)}, u32[]{:S(2)}, u32[]{:S(2)}) collective-permute-start(bf16[128,1024]{1,0:T(8,128)(2,1)S(1)} %shard_map.276.refs_0_), channel_id=1, source_target_pairs={{0,8},{1,9},{2,10},{3,11},{4,12},{5,13},{6,14},{7,15},{8,0},{9,1},... | collective-permute-start | bytes 786440 | tf_op jit(solution)/shard_map/q_high/ppermute | solution.py:74
  20.8 19.1 %copy-start.14 = (s32[4]{0:T(128)}, s32[4]{0:T(128)S(1)}, u32[]{:S(2)}) copy-start(s32[4]{0:T(128)S(1)} %pad_add_fusion.sc.refs_0_) | copy-start | bytes 52
  22.3 17.4 %copy-start.9 = (f32[320,1]{1,0:T(8,128)}, f32[320,1]{1,0:T(8,128)S(1)}, u32[]{:S(2)}) copy-start(f32[320,1]{1,0:T(8,128)S(1)} %get-tuple-element.75.refs_10_.refs_1_) | copy-start | bytes 3844
  39.9 47.9 %copy-start.2 = (bf16[4,128,1024]{2,1,0:T(8,128)(2,1)}, bf16[4,128,1024]{2,1,0:T(8,128)(2,1)S(1)}, u32[]{:S(2)}) copy-start(bf16[4,128,1024]{2,1,0:T(8,128)(2,1)S(1)} %q_high.1.refs_1_.refs_9_) | copy-start | bytes 3145732
  39.9 26.2 %collective-permute-start.4 = (bf16[4,128,1024]{2,1,0:T(8,128)(2,1)S(1)}, bf16[4,128,1024]{2,1,0:T(8,128)(2,1)S(1)}, u32[]{:S(2)}, u32[]{:S(2)}) collective-permute-start(bf16[4,128,1024]{2,1,0:T(8,128)(2,1)S(1)} %q_high.1.refs_1_.refs_9_), channel_id=1, source_target_pairs={{0,4},{1,3},{2,6},{3,1},{4,0},{5,7},{6,2},{7,5},{8,12},{9,11},{10,... | collective-permute-start | bytes 3145736 | tf_op jit(solution)/shard_map/q_two/ppermute | solution.py:74
  41.5 24.6 %collective-permute-start.3 = (bf16[4,128,1024]{2,1,0:T(8,128)(2,1)S(1)}, bf16[4,128,1024]{2,1,0:T(8,128)(2,1)S(1)}, u32[]{:S(2)}, u32[]{:S(2)}) collective-permute-start(bf16[4,128,1024]{2,1,0:T(8,128)(2,1)S(1)} %q_high.1.refs_1_.refs_9_), channel_id=1, source_target_pairs={{0,2},{1,5},{2,0},{3,7},{4,6},{5,1},{6,4},{7,3},{8,10},{9,13},{10,... | collective-permute-start | bytes 3145736 | tf_op jit(solution)/shard_map/q_one/ppermute | solution.py:74
  43.2 11.1 %collective-permute-start.7 = (bf16[128,1024]{1,0:T(8,128)(2,1)S(1)}, bf16[128,1024]{1,0:T(8,128)(2,1)S(1)}, u32[]{:S(2)}, u32[]{:S(2)}) collective-permute-start(bf16[128,1024]{1,0:T(8,128)(2,1)S(1)} %get-tuple-element.77.refs_0_), channel_id=1, source_target_pairs={{0,24},{1,25},{2,26},{3,27},{4,28},{5,29},{6,30},{7,31},{8,16},{9,... | collective-permute-start | bytes 786440 | tf_op jit(solution)/shard_map/fa_high/ppermute | solution.py:74
  45.7 20.4 %collective-permute-start.6 = (bf16[128,1024]{1,0:T(8,128)(2,1)S(1)}, bf16[128,1024]{1,0:T(8,128)(2,1)S(1)}, u32[]{:S(2)}, u32[]{:S(2)}) collective-permute-start(bf16[128,1024]{1,0:T(8,128)(2,1)S(1)} %get-tuple-element.77.refs_0_), channel_id=1, source_target_pairs={{0,16},{1,17},{2,18},{3,19},{4,20},{5,21},{6,22},{7,23},{8,24},{9,... | collective-permute-start | bytes 786440 | tf_op jit(solution)/shard_map/fa_high/ppermute | solution.py:74
  45.7 20.4 %collective-permute-start.5 = (bf16[128,1024]{1,0:T(8,128)(2,1)S(1)}, bf16[128,1024]{1,0:T(8,128)(2,1)S(1)}, u32[]{:S(2)}, u32[]{:S(2)}) collective-permute-start(bf16[128,1024]{1,0:T(8,128)(2,1)S(1)} %get-tuple-element.77.refs_0_), channel_id=1, source_target_pairs={{0,8},{1,9},{2,10},{3,11},{4,12},{5,13},{6,14},{7,15},{8,0},{9,1},... | collective-permute-start | bytes 786440 | tf_op jit(solution)/shard_map/fa_high/ppermute | solution.py:74
  66.1 21.7 %copy-start.17 = (bf16[4,128,1024]{2,1,0:T(8,128)(2,1)}, bf16[4,128,1024]{2,1,0:T(8,128)(2,1)S(1)}, u32[]{:S(2)}) copy-start(bf16[4,128,1024]{2,1,0:T(8,128)(2,1)S(1)} %collective-permute-done.4.refs_3_.refs_11_) | copy-start | bytes 3145732
  66.1 21.7 %copy-start.18 = (bf16[4,128,1024]{2,1,0:T(8,128)(2,1)}, bf16[4,128,1024]{2,1,0:T(8,128)(2,1)S(1)}, u32[]{:S(2)}) copy-start(bf16[4,128,1024]{2,1,0:T(8,128)(2,1)S(1)} %collective-permute-done.3.refs_2_.refs_10_) | copy-start | bytes 3145732
  66.1 2.7 collective-permute-start.9
  66.2 4.1 %collective-permute-start.11 = (bf16[4,128,1024]{2,1,0:T(8,128)(2,1)S(1)}, bf16[4,128,1024]{2,1,0:T(8,128)(2,1)S(1)}, u32[]{:S(2)}, u32[]{:S(2)}) collective-permute-start(bf16[4,128,1024]{2,1,0:T(8,128)(2,1)S(1)} %collective-permute-done.4.refs_3_.refs_11_), channel_id=1, source_target_pairs={{0,1},{1,0},{2,3},{3,2},{4,5},{5,4},{6,7},{7,6},{8,9},{9,8},{10,11... | collective-permute-start | bytes 3145736 | tf_op jit(solution)/shard_map/q_core/ppermute | solution.py:74
  66.7 5.1 %collective-permute-start.10 = (bf16[4,128,1024]{2,1,0:T(8,128)(2,1)S(1)}, bf16[4,128,1024]{2,1,0:T(8,128)(2,1)S(1)}, u32[]{:S(2)}, u32[]{:S(2)}) collective-permute-start(bf16[4,128,1024]{2,1,0:T(8,128)(2,1)S(1)} %collective-permute-done.3.refs_2_.refs_10_), channel_id=1, source_target_pairs={{0,1},{1,0},{2,3},{3,2},{4,5},{5,4},{6,7},{7,6},{8,9},{9,8},{10,11... | collective-permute-start | bytes 3145736 | tf_op jit(solution)/shard_map/q_core/ppermute | solution.py:74
  66.8 14.8 %collective-permute-start.8 = (bf16[4,128,1024]{2,1,0:T(8,128)(2,1)S(1)}, bf16[4,128,1024]{2,1,0:T(8,128)(2,1)S(1)}, u32[]{:S(2)}, u32[]{:S(2)}) collective-permute-start(bf16[4,128,1024]{2,1,0:T(8,128)(2,1)S(1)} %collective-permute-done.3.refs_2_.refs_10_), channel_id=1, source_target_pairs={{0,4},{1,3},{2,6},{3,1},{4,0},{5,7},{6,2},{7,5},{8,12},{9,11},{10,... | collective-permute-start | bytes 3145736 | tf_op jit(solution)/shard_map/q_both/ppermute | solution.py:74
  68.1 40.5 %copy-start.3 = (bf16[4,128,1024]{2,1,0:T(8,128)(2,1)}, bf16[4,128,1024]{2,1,0:T(8,128)(2,1)S(1)}, u32[]{:S(2)}) copy-start(bf16[4,128,1024]{2,1,0:T(8,128)(2,1)S(1)} %fa_high.1.refs_1_) | copy-start | bytes 3145732
  68.9 19.0 %copy-start.19 = (bf16[4,128,1024]{2,1,0:T(8,128)(2,1)}, bf16[4,128,1024]{2,1,0:T(8,128)(2,1)S(1)}, u32[]{:S(2)}) copy-start(bf16[4,128,1024]{2,1,0:T(8,128)(2,1)S(1)} %collective-permute-done.9.refs_5_.refs_13_) | copy-start | bytes 3145732
  70.4 15.5 %copy-start.20 = (bf16[4,128,1024]{2,1,0:T(8,128)(2,1)}, bf16[4,128,1024]{2,1,0:T(8,128)(2,1)S(1)}, u32[]{:S(2)}) copy-start(bf16[4,128,1024]{2,1,0:T(8,128)(2,1)S(1)} %collective-permute-done.11.refs_7_.refs_15_) | copy-start | bytes 3145732
  71.9 14.0 %copy-start.21 = (bf16[4,128,1024]{2,1,0:T(8,128)(2,1)}, bf16[4,128,1024]{2,1,0:T(8,128)(2,1)S(1)}, u32[]{:S(2)}) copy-start(bf16[4,128,1024]{2,1,0:T(8,128)(2,1)S(1)} %collective-permute-done.10.refs_6_.refs_14_) | copy-start | bytes 3145732
  81.6 4.2 %collective-permute-start.12 = (bf16[4,128,1024]{2,1,0:T(8,128)(2,1)S(1)}, bf16[4,128,1024]{2,1,0:T(8,128)(2,1)S(1)}, u32[]{:S(2)}, u32[]{:S(2)}) collective-permute-start(bf16[4,128,1024]{2,1,0:T(8,128)(2,1)S(1)} %collective-permute-done.8.refs_4_.refs_12_), channel_id=1, source_target_pairs={{0,1},{1,0},{2,3},{3,2},{4,5},{5,4},{6,7},{7,6},{8,9},{9,8},{10,11... | collective-permute-start | bytes 3145736 | tf_op jit(solution)/shard_map/q_core/ppermute | solution.py:74
  81.6 27.0 %collective-permute-start.14 = (bf16[4,128,1024]{2,1,0:T(8,128)(2,1)S(1)}, bf16[4,128,1024]{2,1,0:T(8,128)(2,1)}, u32[]{:S(2)}, u32[]{:S(2)}) collective-permute-start(bf16[4,128,1024]{2,1,0:T(8,128)(2,1)S(1)} %fa_high.1.refs_1_), channel_id=1, source_target_pairs={{0,4},{1,3},{2,6},{3,1},{4,0},{5,7},{6,2},{7,5},{8,12},{9,11},{10,... | collective-permute-start | bytes 3145736 | tf_op jit(solution)/shard_map/fa_two/ppermute | solution.py:74
  82.7 25.9 %collective-permute-start.13 = (bf16[4,128,1024]{2,1,0:T(8,128)(2,1)S(1)}, bf16[4,128,1024]{2,1,0:T(8,128)(2,1)}, u32[]{:S(2)}, u32[]{:S(2)}) collective-permute-start(bf16[4,128,1024]{2,1,0:T(8,128)(2,1)S(1)} %fa_high.1.refs_1_), channel_id=1, source_target_pairs={{0,2},{1,5},{2,0},{3,7},{4,6},{5,1},{6,4},{7,3},{8,10},{9,13},{10,... | collective-permute-start | bytes 3145736 | tf_op jit(solution)/shard_map/fa_one/ppermute | solution.py:74
  83.3 25.2 %collective-permute-start.17 = (bf16[128,1024]{1,0:T(8,128)(2,1)S(1)}, bf16[128,1024]{1,0:T(8,128)(2,1)S(1)}, u32[]{:S(2)}, u32[]{:S(2)}) collective-permute-start(bf16[128,1024]{1,0:T(8,128)(2,1)S(1)} %get-tuple-element.89.refs_0_), channel_id=1, source_target_pairs={{0,24},{1,25},{2,26},{3,27},{4,28},{5,29},{6,30},{7,31},{8,16},{9,... | collective-permute-start | bytes 786440 | tf_op jit(solution)/shard_map/fb_high/ppermute | solution.py:74
  85.8 22.7 %collective-permute-start.16 = (bf16[128,1024]{1,0:T(8,128)(2,1)S(1)}, bf16[128,1024]{1,0:T(8,128)(2,1)S(1)}, u32[]{:S(2)}, u32[]{:S(2)}) collective-permute-start(bf16[128,1024]{1,0:T(8,128)(2,1)S(1)} %get-tuple-element.89.refs_0_), channel_id=1, source_target_pairs={{0,16},{1,17},{2,18},{3,19},{4,20},{5,21},{6,22},{7,23},{8,24},{9,... | collective-permute-start | bytes 786440 | tf_op jit(solution)/shard_map/fb_high/ppermute | solution.py:74
  85.9 22.7 %collective-permute-start.15 = (bf16[128,1024]{1,0:T(8,128)(2,1)S(1)}, bf16[128,1024]{1,0:T(8,128)(2,1)S(1)}, u32[]{:S(2)}, u32[]{:S(2)}) collective-permute-start(bf16[128,1024]{1,0:T(8,128)(2,1)S(1)} %get-tuple-element.89.refs_0_), channel_id=1, source_target_pairs={{0,8},{1,9},{2,10},{3,11},{4,12},{5,13},{6,14},{7,15},{8,0},{9,1},... | collective-permute-start | bytes 786440 | tf_op jit(solution)/shard_map/fb_high/ppermute | solution.py:74
  108.6 3.4 %collective-permute-start.19 = (bf16[4,128,1024]{2,1,0:T(8,128)(2,1)S(1)}, bf16[4,128,1024]{2,1,0:T(8,128)(2,1)S(1)}, u32[]{:S(2)}, u32[]{:S(2)}) collective-permute-start(bf16[4,128,1024]{2,1,0:T(8,128)(2,1)S(1)} %fa_high.1.refs_1_), channel_id=1, source_target_pairs={{0,1},{1,0},{2,3},{3,2},{4,5},{5,4},{6,7},{7,6},{8,9},{9,8},{10,11... | collective-permute-start | bytes 3145736 | tf_op jit(solution)/shard_map/fa_core/ppermute | solution.py:74
  108.7 4.4 %collective-permute-start.21 = (bf16[4,128,1024]{2,1,0:T(8,128)(2,1)}, bf16[4,128,1024]{2,1,0:T(8,128)(2,1)S(1)}, u32[]{:S(2)}, u32[]{:S(2)}) collective-permute-start(bf16[4,128,1024]{2,1,0:T(8,128)(2,1)} %collective-permute-done.14.refs_3_), channel_id=1, source_target_pairs={{0,1},{1,0},{2,3},{3,2},{4,5},{5,4},{6,7},{7,6},{8,9},{9,8},{10,11... | collective-permute-start | bytes 3145736 | tf_op jit(solution)/shard_map/fa_core/ppermute | solution.py:74
  109.2 5.4 %collective-permute-start.20 = (bf16[4,128,1024]{2,1,0:T(8,128)(2,1)}, bf16[4,128,1024]{2,1,0:T(8,128)(2,1)S(1)}, u32[]{:S(2)}, u32[]{:S(2)}) collective-permute-start(bf16[4,128,1024]{2,1,0:T(8,128)(2,1)} %collective-permute-done.13.refs_2_), channel_id=1, source_target_pairs={{0,1},{1,0},{2,3},{3,2},{4,5},{5,4},{6,7},{7,6},{8,9},{9,8},{10,11... | collective-permute-start | bytes 3145736 | tf_op jit(solution)/shard_map/fa_core/ppermute | solution.py:74
  109.3 15.0 %collective-permute-start.18 = (bf16[4,128,1024]{2,1,0:T(8,128)(2,1)}, bf16[4,128,1024]{2,1,0:T(8,128)(2,1)S(1)}, u32[]{:S(2)}, u32[]{:S(2)}) collective-permute-start(bf16[4,128,1024]{2,1,0:T(8,128)(2,1)} %collective-permute-done.13.refs_2_), channel_id=1, source_target_pairs={{0,4},{1,3},{2,6},{3,1},{4,0},{5,7},{6,2},{7,5},{8,12},{9,11},{10,... | collective-permute-start | bytes 3145736 | tf_op jit(solution)/shard_map/fa_both/ppermute | solution.py:74
  110.3 41.7 %copy-start.4 = (bf16[4,128,1024]{2,1,0:T(8,128)(2,1)}, bf16[4,128,1024]{2,1,0:T(8,128)(2,1)S(1)}, u32[]{:S(2)}) copy-start(bf16[4,128,1024]{2,1,0:T(8,128)(2,1)S(1)} %fb_high.1.refs_1_) | copy-start | bytes 3145732
  112.0 15.5 %copy-start.26 = (bf16[4,128,1024]{2,1,0:T(8,128)(2,1)}, bf16[4,128,1024]{2,1,0:T(8,128)(2,1)S(1)}, u32[]{:S(2)}) copy-start(bf16[4,128,1024]{2,1,0:T(8,128)(2,1)S(1)} %collective-permute-done.19.refs_5_) | copy-start | bytes 3145732
  113.0 14.5 %copy-start.28 = (bf16[4,128,1024]{2,1,0:T(8,128)(2,1)}, bf16[4,128,1024]{2,1,0:T(8,128)(2,1)S(1)}, u32[]{:S(2)}) copy-start(bf16[4,128,1024]{2,1,0:T(8,128)(2,1)S(1)} %collective-permute-done.21.refs_7_) | copy-start | bytes 3145732
  124.3 3.3 %collective-permute-start.24 = (bf16[4,128,1024]{2,1,0:T(8,128)(2,1)S(1)}, bf16[4,128,1024]{2,1,0:T(8,128)(2,1)S(1)}, u32[]{:S(2)}, u32[]{:S(2)}) collective-permute-start(bf16[4,128,1024]{2,1,0:T(8,128)(2,1)S(1)} %collective-permute-done.18.refs_4_), channel_id=1, source_target_pairs={{0,1},{1,0},{2,3},{3,2},{4,5},{5,4},{6,7},{7,6},{8,9},{9,8},{10,11... | collective-permute-start | bytes 3145736 | tf_op jit(solution)/shard_map/fa_core/ppermute | solution.py:74
  125.3 25.8 %collective-permute-start.23 = (bf16[4,128,1024]{2,1,0:T(8,128)(2,1)S(1)}, bf16[4,128,1024]{2,1,0:T(8,128)(2,1)S(1)}, u32[]{:S(2)}, u32[]{:S(2)}) collective-permute-start(bf16[4,128,1024]{2,1,0:T(8,128)(2,1)S(1)} %fb_high.1.refs_1_), channel_id=1, source_target_pairs={{0,4},{1,3},{2,6},{3,1},{4,0},{5,7},{6,2},{7,5},{8,12},{9,11},{10,... | collective-permute-start | bytes 3145736 | tf_op jit(solution)/shard_map/fb_two/ppermute | solution.py:74
  126.1 24.9 %collective-permute-start.22 = (bf16[4,128,1024]{2,1,0:T(8,128)(2,1)S(1)}, bf16[4,128,1024]{2,1,0:T(8,128)(2,1)S(1)}, u32[]{:S(2)}, u32[]{:S(2)}) collective-permute-start(bf16[4,128,1024]{2,1,0:T(8,128)(2,1)S(1)} %fb_high.1.refs_1_), channel_id=1, source_target_pairs={{0,2},{1,5},{2,0},{3,7},{4,6},{5,1},{6,4},{7,3},{8,10},{9,13},{10,... | collective-permute-start | bytes 3145736 | tf_op jit(solution)/shard_map/fb_one/ppermute | solution.py:74
  151.0 18.5 %copy-start.24 = (bf16[4,128,1024]{2,1,0:T(8,128)(2,1)}, bf16[4,128,1024]{2,1,0:T(8,128)(2,1)S(1)}, u32[]{:S(2)}) copy-start(bf16[4,128,1024]{2,1,0:T(8,128)(2,1)S(1)} %collective-permute-done.23.refs_3_) | copy-start | bytes 3145732
  151.0 18.5 %copy-start.25 = (bf16[4,128,1024]{2,1,0:T(8,128)(2,1)}, bf16[4,128,1024]{2,1,0:T(8,128)(2,1)S(1)}, u32[]{:S(2)}) copy-start(bf16[4,128,1024]{2,1,0:T(8,128)(2,1)S(1)} %collective-permute-done.22.refs_2_) | copy-start | bytes 3145732
  151.0 14.9 %collective-permute-start.25 = (bf16[4,128,1024]{2,1,0:T(8,128)(2,1)S(1)}, bf16[4,128,1024]{2,1,0:T(8,128)(2,1)S(1)}, u32[]{:S(2)}, u32[]{:S(2)}) collective-permute-start(bf16[4,128,1024]{2,1,0:T(8,128)(2,1)S(1)} %collective-permute-done.22.refs_2_), channel_id=1, source_target_pairs={{0,4},{1,3},{2,6},{3,1},{4,0},{5,7},{6,2},{7,5},{8,12},{9,11},{10,... | collective-permute-start | bytes 3145736 | tf_op jit(solution)/shard_map/fb_both/ppermute | solution.py:74
  152.0 14.0 %collective-permute-start.27 = (bf16[4,128,1024]{2,1,0:T(8,128)(2,1)S(1)}, bf16[4,128,1024]{2,1,0:T(8,128)(2,1)S(1)}, u32[]{:S(2)}, u32[]{:S(2)}) collective-permute-start(bf16[4,128,1024]{2,1,0:T(8,128)(2,1)S(1)} %collective-permute-done.22.refs_2_), channel_id=1, source_target_pairs={{0,1},{1,0},{2,3},{3,2},{4,5},{5,4},{6,7},{7,6},{8,9},{9,8},{10,11... | collective-permute-start | bytes 3145736 | tf_op jit(solution)/shard_map/fb_core/ppermute | solution.py:74
  152.0 13.9 %collective-permute-start.26 = (bf16[4,128,1024]{2,1,0:T(8,128)(2,1)S(1)}, bf16[4,128,1024]{2,1,0:T(8,128)(2,1)S(1)}, u32[]{:S(2)}, u32[]{:S(2)}) collective-permute-start(bf16[4,128,1024]{2,1,0:T(8,128)(2,1)S(1)} %fb_high.1.refs_1_), channel_id=1, source_target_pairs={{0,1},{1,0},{2,3},{3,2},{4,5},{5,4},{6,7},{7,6},{8,9},{9,8},{10,11... | collective-permute-start | bytes 3145736 | tf_op jit(solution)/shard_map/fb_core/ppermute | solution.py:74
  152.5 13.4 %collective-permute-start.28 = (bf16[4,128,1024]{2,1,0:T(8,128)(2,1)S(1)}, bf16[4,128,1024]{2,1,0:T(8,128)(2,1)S(1)}, u32[]{:S(2)}, u32[]{:S(2)}) collective-permute-start(bf16[4,128,1024]{2,1,0:T(8,128)(2,1)S(1)} %collective-permute-done.23.refs_3_), channel_id=1, source_target_pairs={{0,1},{1,0},{2,3},{3,2},{4,5},{5,4},{6,7},{7,6},{8,9},{9,8},{10,11... | collective-permute-start | bytes 3145736 | tf_op jit(solution)/shard_map/fb_core/ppermute | solution.py:74
  165.9 2.7 collective-permute-start.29
  191.6 23.5 %all-to-all-start.1 = ((bf16[32,32,384]{2,1,0:T(8,128)(2,1)}), bf16[32,32,384]{2,1,0:T(8,128)(2,1)S(1)}, u32[]{:S(2)}, u32[]{:S(2)}) async-start(bf16[32,32,384]{2,1,0:T(8,128)(2,1)} %get-tuple-element.116), calls=%async_computation.1 | async-start | bytes 1572864 | tf_op jit(solution)/shard_map/grads_b_send/all_to_all | solution.py:619
  215.1 11.9 %all-to-all-start.2 = ((bf16[32,16,128]{2,1,0:T(8,128)(2,1)}), bf16[32,16,128]{2,1,0:T(8,128)(2,1)S(1)}, u32[]{:S(2)}, u32[]{:S(2)}) async-start(bf16[32,16,128]{2,1,0:T(8,128)(2,1)} %get-tuple-element.117), calls=%async_computation.2 | async-start | bytes 262144 | tf_op jit(solution)/shard_map/grads_c_send/all_to_all | solution.py:619
  220.1 28.4 %collective-permute-start.32 = (bf16[128,384]{1,0:T(8,128)(2,1)S(1)}, bf16[128,384]{1,0:T(8,128)(2,1)S(1)}, u32[]{:S(2)}, u32[]{:S(2)}) collective-permute-start(bf16[128,384]{1,0:T(8,128)(2,1)S(1)} %bitcast.25), channel_id=1, source_target_pairs={{0,24},{1,25},{2,26},{3,27},{4,28},{5,29},{6,30},{7,31},{8,16},{9,... | collective-permute-start | bytes 294920 | tf_op jit(solution)/shard_map/grads/ppermute | solution.py:74
  223.8 24.7 %collective-permute-start.31 = (bf16[128,384]{1,0:T(8,128)(2,1)S(1)}, bf16[128,384]{1,0:T(8,128)(2,1)S(1)}, u32[]{:S(2)}, u32[]{:S(2)}) collective-permute-start(bf16[128,384]{1,0:T(8,128)(2,1)S(1)} %bitcast.26), channel_id=1, source_target_pairs={{0,16},{1,17},{2,18},{3,19},{4,20},{5,21},{6,22},{7,23},{8,24},{9,... | collective-permute-start | bytes 294920 | tf_op jit(solution)/shard_map/grads/ppermute | solution.py:74
  223.8 24.7 %collective-permute-start.30 = (bf16[128,384]{1,0:T(8,128)(2,1)S(1)}, bf16[128,384]{1,0:T(8,128)(2,1)S(1)}, u32[]{:S(2)}, u32[]{:S(2)}) collective-permute-start(bf16[128,384]{1,0:T(8,128)(2,1)S(1)} %bitcast.27), channel_id=1, source_target_pairs={{0,8},{1,9},{2,10},{3,11},{4,12},{5,13},{6,14},{7,15},{8,0},{9,1},... | collective-permute-start | bytes 294920 | tf_op jit(solution)/shard_map/grads/ppermute | solution.py:74
  238.4 6.0 %collective-permute-start.35 = (bf16[128,128]{1,0:T(8,128)(2,1)S(1)}, bf16[128,128]{1,0:T(8,128)(2,1)S(1)}, u32[]{:S(2)}, u32[]{:S(2)}) collective-permute-start(bf16[128,128]{1,0:T(8,128)(2,1)S(1)} %bitcast.29), channel_id=1, source_target_pairs={{0,24},{1,25},{2,26},{3,27},{4,28},{5,29},{6,30},{7,31},{8,16},{9,... | collective-permute-start | bytes 98312 | tf_op jit(solution)/shard_map/grads/ppermute | solution.py:74
  239.8 5.5 %collective-permute-start.34 = (bf16[128,128]{1,0:T(8,128)(2,1)S(1)}, bf16[128,128]{1,0:T(8,128)(2,1)S(1)}, u32[]{:S(2)}, u32[]{:S(2)}) collective-permute-start(bf16[128,128]{1,0:T(8,128)(2,1)S(1)} %bitcast.30), channel_id=1, source_target_pairs={{0,16},{1,17},{2,18},{3,19},{4,20},{5,21},{6,22},{7,23},{8,24},{9,... | collective-permute-start | bytes 98312 | tf_op jit(solution)/shard_map/grads/ppermute | solution.py:74
  244.4 3.9 %collective-permute-start.33 = (bf16[128,128]{1,0:T(8,128)(2,1)S(1)}, bf16[128,128]{1,0:T(8,128)(2,1)S(1)}, u32[]{:S(2)}, u32[]{:S(2)}) collective-permute-start(bf16[128,128]{1,0:T(8,128)(2,1)S(1)} %bitcast.31), channel_id=1, source_target_pairs={{0,8},{1,9},{2,10},{3,11},{4,12},{5,13},{6,14},{7,15},{8,0},{9,1},... | collective-permute-start | bytes 98312 | tf_op jit(solution)/shard_map/grads/ppermute | solution.py:74
  249.2 24.9 %copy-start.5 = (bf16[4,128,512]{2,1,0:T(8,128)(2,1)}, bf16[4,128,512]{2,1,0:T(8,128)(2,1)S(1)}, u32[]{:S(2)}) copy-start(bf16[4,128,512]{2,1,0:T(8,128)(2,1)S(1)} %grads.8.refs_1_) | copy-start | bytes 1572868
  249.2 12.0 %collective-permute-start.37 = (bf16[4,128,512]{2,1,0:T(8,128)(2,1)S(1)}, bf16[4,128,512]{2,1,0:T(8,128)(2,1)S(1)}, u32[]{:S(2)}, u32[]{:S(2)}) collective-permute-start(bf16[4,128,512]{2,1,0:T(8,128)(2,1)S(1)} %grads.8.refs_1_), channel_id=1, source_target_pairs={{0,4},{1,3},{2,6},{3,1},{4,0},{5,7},{6,2},{7,5},{8,12},{9,11},{10,... | collective-permute-start | bytes 1572872 | tf_op jit(solution)/shard_map/grads/ppermute | solution.py:74
  249.8 11.4 %collective-permute-start.36 = (bf16[4,128,512]{2,1,0:T(8,128)(2,1)S(1)}, bf16[4,128,512]{2,1,0:T(8,128)(2,1)S(1)}, u32[]{:S(2)}, u32[]{:S(2)}) collective-permute-start(bf16[4,128,512]{2,1,0:T(8,128)(2,1)S(1)} %grads.8.refs_1_), channel_id=1, source_target_pairs={{0,2},{1,5},{2,0},{3,7},{4,6},{5,1},{6,4},{7,3},{8,10},{9,13},{10,... | collective-permute-start | bytes 1572872 | tf_op jit(solution)/shard_map/grads/ppermute | solution.py:74
  261.3 9.3 %collective-permute-start.38 = (bf16[4,128,512]{2,1,0:T(8,128)(2,1)S(1)}, bf16[4,128,512]{2,1,0:T(8,128)(2,1)}, u32[]{:S(2)}, u32[]{:S(2)}) collective-permute-start(bf16[4,128,512]{2,1,0:T(8,128)(2,1)S(1)} %collective-permute-done.36.refs_2_), channel_id=1, source_target_pairs={{0,4},{1,3},{2,6},{3,1},{4,0},{5,7},{6,2},{7,5},{8,12},{9,11},{10,... | collective-permute-start | bytes 1572872 | tf_op jit(solution)/shard_map/grads/ppermute | solution.py:74
  270.6 20.8 %all-to-all-start.3 = ((bf16[4,640,256]{2,1,0:T(8,128)(2,1)}), bf16[4,640,256]{2,1,0:T(8,128)(2,1)S(1)}, u32[]{:S(2)}, u32[]{:S(2)}) async-start(bf16[4,640,256]{2,1,0:T(8,128)(2,1)} %shard_map.283), calls=%async_computation.3 | async-start | bytes 2621440 | tf_op jit(solution)/shard_map/rows_out/all_to_all | solution.py:870
  274.2 2.3 collective-permute-start.39
  274.6 3.4 %collective-permute-start.41 = (bf16[4,128,512]{2,1,0:T(8,128)(2,1)S(1)}, bf16[4,128,512]{2,1,0:T(8,128)(2,1)S(1)}, u32[]{:S(2)}, u32[]{:S(2)}) collective-permute-start(bf16[4,128,512]{2,1,0:T(8,128)(2,1)S(1)} %collective-permute-done.37.refs_3_), channel_id=1, source_target_pairs={{0,1},{1,0},{2,3},{3,2},{4,5},{5,4},{6,7},{7,6},{8,9},{9,8},{10,11... | collective-permute-start | bytes 1572872 | tf_op jit(solution)/shard_map/grads/ppermute | solution.py:74
  274.8 4.0 %collective-permute-start.40 = (bf16[4,128,512]{2,1,0:T(8,128)(2,1)S(1)}, bf16[4,128,512]{2,1,0:T(8,128)(2,1)S(1)}, u32[]{:S(2)}, u32[]{:S(2)}) collective-permute-start(bf16[4,128,512]{2,1,0:T(8,128)(2,1)S(1)} %collective-permute-done.36.refs_2_), channel_id=1, source_target_pairs={{0,1},{1,0},{2,3},{3,2},{4,5},{5,4},{6,7},{7,6},{8,9},{9,8},{10,11... | collective-permute-start | bytes 1572872 | tf_op jit(solution)/shard_map/grads/ppermute | solution.py:74
  275.2 3.6 %collective-permute-start.42 = (bf16[4,128,512]{2,1,0:T(8,128)(2,1)}, bf16[4,128,512]{2,1,0:T(8,128)(2,1)S(1)}, u32[]{:S(2)}, u32[]{:S(2)}) collective-permute-start(bf16[4,128,512]{2,1,0:T(8,128)(2,1)} %collective-permute-done.38.refs_4_), channel_id=1, source_target_pairs={{0,1},{1,0},{2,3},{3,2},{4,5},{5,4},{6,7},{7,6},{8,9},{9,8},{10,11... | collective-permute-start | bytes 1572872 | tf_op jit(solution)/shard_map/grads/ppermute | solution.py:74
  (26 other events, 123.0 us)

commit v5 on v4

--- a/solution.py
+++ b/solution.py
@@ -17,6 +17,7 @@
 SEQ = 320
 PAIR = 2 * HD
 EXTRA = 16
+OWNER = 128
 FRONT, FFN_A, FFN_B, ATT, BACK = 56, 56, 56, 56, 56
 BF = jnp.bfloat16
 F32 = jnp.float32
@@ -245,10 +246,11 @@
     return [VMEM((cols, D, n), BF), pltpu.SemaphoreType.DMA((8, lead))]
 
 
-def put(ref, start, value, lane=0):
-    part = ref.shape[-1] - lane
+def put(ref, start, value, lane=0, spare=0):
+    end = ref.shape[-1] - spare
+    part = end - lane
     for i in range(value.shape[-1] // part):
-        ref[start // part + i, :R, lane:] = value[:, i * part : (i + 1) * part]
+        ref[start // part + i, :, lane:end] = value[:, i * part : (i + 1) * part]
 
 
 def lanes(start, width):
@@ -359,7 +361,7 @@
     lat3[...] = low(mm(n2[...], f_down[a], NT))
 
 
-def ffn_steps(sc, part, cols, w, xa, n2, lat3, gr, glat4, up_1, down_2, acc, early, lane=0):
+def ffn_steps(sc, part, cols, w, xa, n2, lat3, gr, glat4, up_1, down_2, acc, early, lane=0, spare=0):
     res, gn2, lat4, glat3 = acc
     a = sc[0]
     hid = D // cols
@@ -387,8 +389,8 @@
         glat3[...] += mm(grad_pre, up, NT)
         res[...] += mm(activated, w2, NT)
         gn2[...] += mm(grad_pre, w1, NT)
-        put(early, block * half, low(mm(lat3_t, grad_pre)), lane)
-        put(early, FF // 2 + block * half, low(mm(glat4_t, activated)), lane)
+        put(early, block * half, low(mm(lat3_t, grad_pre)), lane, spare)
+        put(early, FF // 2 + block * half, low(mm(glat4_t, activated)), lane, spare)
         return 0
 
     lax.fori_loop(0, cols, step, 0)
@@ -425,8 +427,8 @@
     layer, gatt, gmid, early = refs[38:42]
     w, sems, wp, sems_p, res, gn2, lat4, glat3 = refs[42:]
     lane = early_in.shape[-1]
-    early[:, :R, :lane] = early_in[...]
-    early[:, R:] = low(jnp.full((early.shape[0], R, early.shape[2]), sc[0], F32))
+    early[:, :, :lane] = early_in[...]
+    early[:, :, early.shape[2] - OWNER :] = low(jnp.full((early.shape[0], R, OWNER), sc[0], F32))
     weights = Weights(sc, pieces, w, sems, lead)
     weights.start()
     proj = Weights(sc, own_q, wp, sems_p, lead, 3 * D // cols)
@@ -440,7 +442,7 @@
     glat3[...] = glat3_in[...]
     weights.wait()
     ffn_steps(
-        sc, 1, cols, w, xa, n2, lat3, gr, glat4, up_1, down_2, (res, gn2, lat4, glat3), early, lane
+        sc, 1, cols, w, xa, n2, lat3, gr, glat4, up_1, down_2, (res, gn2, lat4, glat3), early, lane, OWNER
     )
     mid = middle[...]
     lat4_low = low(lat4[...])
@@ -457,9 +459,9 @@
     gb = low(grad_middle)
     glat2 = low(mm(gb, p_up[a], NT))
     glat2_t = low(glat2.astype(F32).T)
-    put(early, FF + D, low(mm(low(lat2[...].astype(F32).T), gb)), lane)
-    put(early, FF + 2 * D, low(mm(low(glat3_low.astype(F32).T), n2[...])), lane)
-    put(early, FF + 3 * D, low(mm(low(lat4_low.astype(F32).T), gr[...])), lane)
+    put(early, FF + D, low(mm(low(lat2[...].astype(F32).T), gb)), lane, OWNER)
+    put(early, FF + 2 * D, low(mm(low(glat3_low.astype(F32).T), n2[...])), lane, OWNER)
+    put(early, FF + 3 * D, low(mm(low(lat4_low.astype(F32).T), gr[...])), lane, OWNER)
     proj.wait()
 
     def step(slot, _):
@@ -467,7 +469,7 @@
         here = lanes(slot * hid, hid)
         there = lanes(block * hid, hid)
         gatt[:, here] = low(mm(gb, wp[slot]) + mm(glat2, p_down[a, :, there]))
-        put(early, FF + block * hid, low(mm(glat2_t, att[:, here])), lane)
+        put(early, FF + block * hid, low(mm(glat2_t, att[:, here])), lane, OWNER)
         return 0
 
     lax.fori_loop(0, cols, step, 0)
@@ -548,15 +550,10 @@
         out[c, SEQ:] = made[:, c * hid : (c + 1) * hid]
 
 
-def sum_kernel(owners, *refs):
-    mines, out, acc = refs[:-2], refs[-2], refs[-1]
+def sum_kernel(owners, mine, out, acc):
     acc[...] = jnp.zeros_like(acc)
-    lane = 0
-    for mine in mines:
-        part = mine.shape[-1]
-        for d in range(mine.shape[0]):
-            acc[owners[d], :, lane : lane + part] += mine[d, :R].astype(F32)
-        lane += part
+    for d in range(mine.shape[0]):
+        acc[owners[d]] += mine[d, :, : acc.shape[2]].astype(F32)
     out[...] = low(acc[...])
 
 
@@ -619,13 +616,12 @@
     return lax.all_to_all(grads, BOTH, split_axis=0, concat_axis=0, tiled=True)
 
 
-def sum_grads(mines, owners):
-    part = sum(m.shape[-1] for m in mines)
+def sum_grads(mine, owners, part):
     summed = call(
         sum_kernel,
         jax.ShapeDtypeStruct((NA, R, part), BF),
-        [owners, *mines],
-        [pltpu.SMEM] + [VMEM] * len(mines),
+        [owners, mine],
+        [pltpu.SMEM, VMEM],
         [VMEM((NA, R, part), F32)],
     )
     return summed.reshape(NA * R, part)
@@ -706,7 +702,7 @@
     lead = lead_table(rows, cols)
 
     shard = jax.ShapeDtypeStruct((blk, n), BF)
-    shard_q = call(prep_q_kernel, shard, [w_qkv, w_proj], [VMEM] * 2)
+    shard_q = call(prep_q_kernel, shard, [w_qkv, w_proj], [VMEM] * 2, mib=56)
     with jax.named_scope("q_high"):
         own_q, came_q = gather_high(shard_q)
     rows_in = call(
@@ -715,6 +711,7 @@
         [after(tokens_in, shard_q).reshape(cols, SEQ, hid), grad_out.reshape(cols, SEQ, hid), bias_qv]
         + [bias_fc1.reshape(4, hid)],
         [VMEM] * 4,
+        mib=56,
     )
     xa = lax.all_to_all(rows_in, "col", split_axis=0, concat_axis=0, tiled=True)
     adapter = lax.dynamic_index_in_dim(adapter_index, column, 0, keepdims=False)
@@ -810,7 +807,7 @@
     layer, gatt, gmid, grads_b = call(
         functools.partial(ffn_b_kernel, lead, cols),
         [jax.ShapeDtypeStruct((cols, SEQ, hid), BF), big, wide]
-        + [jax.ShapeDtypeStruct((rows * cols, 2 * R, 12 * D // (rows * cols)), BF)],
+        + [jax.ShapeDtypeStruct((rows * cols, R, 12 * D // (rows * cols) + OWNER), BF)],
         [sc, *pieces_b, *pieces_q, xa, keep, ln_gain, n2, lat3, fc1_up, fc2_down, fc2_up]
         + [fc1_down, proj_down, proj_up, bias_out]
         + [middle, att, lat2, gr, res, gn2, lat4, glat3, early_a],
@@ -822,7 +819,7 @@
     )
     with jax.named_scope("grads_b_send"):
         mine_b = send_grads(grads_b)
-        owners = mine_b[:, R, 0].astype(jnp.int32)
+        owners = mine_b[:, 0, mine_b.shape[2] - 1].astype(jnp.int32)
     gq, gk, gv, glat1, late = call(
         functools.partial(attention_back_kernel, cols),
         [big, big, big, small, jax.ShapeDtypeStruct((rows * cols, R, 4 * D // (rows * cols)), BF)],
@@ -833,8 +830,10 @@
     with jax.named_scope("grads_c_send"):
         mine_c = send_grads(late)
     with jax.named_scope("grads_b"):
-        part_b = sum_grads([after(mine_b, late)], owners)
-    gmid = after(gmid, part_b)
+        own_b, _ = gather_high(sum_grads(after(mine_b, late), owners, mine_b.shape[2] - OWNER))
+        own_c, _ = gather_high(sum_grads(mine_c, owners, mine_c.shape[2]))
+        own = lane_join(own_b, own_c)
+    gmid = after(gmid, own)
     sent = call(
         functools.partial(back_kernel, lead, cols),
         jax.ShapeDtypeStruct((cols, 2 * SEQ, hid), BF),
@@ -844,11 +843,8 @@
         mib=BACK,
     )
     with jax.named_scope("grads"):
-        own_b, _ = gather_high(part_b)
-        own_c, _ = gather_high(after(sum_grads([mine_c], owners), sent))
-        own = lane_join(own_b, own_c)
         one, two = swap(own, flip_one), swap(own, flip_two)
-        both = swap(after(one, two), flip_two)
+        both = swap(after(one, two, sent), flip_two)
         pieces = with_cores([own, one, two, both])
         half = FF // cols // 2
         map_a, map_b = (
@@ -861,7 +857,7 @@
         )
         map_b = map_b + tuple((2 + i, None, 0, FF + i * D, D) for i in range(4))
         map_c = ((6, None, 0, 0, D),) + tuple((7, c, 0, (c + 1) * D, D) for c in range(3))
-        parts = [early_a.shape[-1], mine_b.shape[-1] - early_a.shape[-1], mine_c.shape[-1]]
+        parts = [early_a.shape[-1], mine_b.shape[-1] - early_a.shape[-1] - OWNER, mine_c.shape[-1]]
         shapes = [(NA * R, FF)] * 2 + [(NA * R, D)] * 5 + [(NA, 3, R, D)]
         sums = spread(sc, pieces, parts, [map_a, map_b, map_c], shapes)
 

time: 293 us -> 279 us (0.952)
  waiting for transfers between devices: 130 us -> 112 us
  starting transfers between devices: 51.5 us -> 55.9 us
  local copies, waits for them, and re-layouts: 13.1 us -> 9.15 us
    ppermute x43, waiting for transfers between devices: 116 us -> 103 us  [swap(): return lax.ppermute(block, BOTH, pairs)]
    all_to_all x2, waiting for transfers between devices: 10 us -> 4.89 us  [send_grads(): return lax.all_to_all(grads, BOTH, split_axis=0, concat_axis=0, tiled=True)]
    ppermute x43, starting transfers between devices: 37 us -> 41.8 us  [swap(): return lax.ppermute(block, BOTH, pairs)]
    unnamed x86 -> x78, local copies, waits for them, and re-layouts: 9.95 us -> 5.41 us
  transfers between devices with their start and end apart: 47 -> 47, of which waited for: 26 -> 25; matrix products, arithmetic and copies ran while one was open for 1% -> 1% of each run, Pallas kernels for 24% -> 25%
where the time goes in v5:
time: 279 us; the launch traced here: 278 us
  waiting for transfers between devices  112 us (40%)
  Pallas kernels  96.2 us (34%)
  starting transfers between devices  55.9 us (20%)
  local copies, waits for them, and re-layouts  9.15 us (3%)
  between operations  3.13 us (1%)
    ppermute x43, waiting for transfers between devices, swap(): return lax.ppermute(block, BOTH, pairs)  103 us
    pallas_call x17, Pallas kernels, call(): pl.pallas_call(kernel, out_shape=outs, in_specs=[pl.BlockSpec(memory_spac...  96.2 us
    ppermute x43, starting transfers between devices, swap(): return lax.ppermute(block, BOTH, pairs)  41.8 us
    all_to_all x2, starting transfers between devices, send_grads(): return lax.all_to_all(grads, BOTH, split_axis=0, concat_axis=0, tiled=True)  6.13 us
  transfers between devices with their start and end apart: 47, of which 25 were waited for; matrix products, arithmetic and copies ran while one was open for 1% of the time, Pallas kernels for 25%

profile of v5, /device:TPU:0, one launch (start us, length us, event | category | flops | bytes accessed | tf_op | source)
XLA Modules:
  0.0 278.0 jit_solution(4425153071435346779)
XLA Ops:
  0.7 1.3 reshape.74.bias_f
  2.0 1.7 shard_map.276.refs_0_
  3.7 2.4 shard_map.278
  6.2 4.4 %all-to-all-start = ((bf16[4,656,256]{2,1,0:T(8,128)(2,1)}), bf16[4,656,256]{2,1,0:T(8,128)(2,1)}, u32[]{:S(2)}, u32[]{:S(2)}) async-start(bf16[4,656,256]{2,1,0:T(8,128)(2,1)} %shard_map.278), calls=%async_computation | async-start | bytes 2686976 | tf_op jit(solution)/shard_map/all_to_all | solution.py:716
  10.7 5.1 %collective-permute-start.2 = (bf16[128,1024]{1,0:T(8,128)(2,1)S(1)}, bf16[128,1024]{1,0:T(8,128)(2,1)S(1)}, u32[]{:S(2)}, u32[]{:S(2)}) collective-permute-start(bf16[128,1024]{1,0:T(8,128)(2,1)S(1)} %copy-done.6), channel_id=1, source_target_pairs={{0,24},{1,25},{2,26},{3,27},{4,28},{5,29},{6,30},{7,31},{8,16},{9,... | collective-permute-start | bytes 786440 | tf_op jit(solution)/shard_map/q_high/ppermute | solution.py:75
  19.7 0.8 shard_map.277
  21.9 1.2 collective-permute-done.2.refs_3_
  23.1 15.6 %collective-permute-done.1.refs_2_ = bf16[128,1024]{1,0:T(8,128)(2,1)S(1)} collective-permute-done((bf16[128,1024]{1,0:T(8,128)(2,1)S(1)}, bf16[128,1024]{1,0:T(8,128)(2,1)S(1)}, u32[]{:S(2)}, u32[]{:S(2)}) %collective-permute-start.1) | collective-permute-done | bytes 262176 | tf_op jit(solution)/shard_map/q_high/ppermute | solution.py:75
  38.8 1.6 collective-permute-start.4
  40.4 1.7 collective-permute-start.3
  42.1 2.5 collective-permute-start.7
  44.5 1.9 collective-permute-start.5
  46.4 6.8 %collective-permute-done.7.refs_3_ = bf16[128,1024]{1,0:T(8,128)(2,1)S(1)} collective-permute-done((bf16[128,1024]{1,0:T(8,128)(2,1)S(1)}, bf16[128,1024]{1,0:T(8,128)(2,1)S(1)}, u32[]{:S(2)}, u32[]{:S(2)}) %collective-permute-start.7) | collective-permute-done | bytes 262176 | tf_op jit(solution)/shard_map/fa_high/ppermute | solution.py:75
  53.2 11.8 %collective-permute-done.6.refs_2_ = bf16[128,1024]{1,0:T(8,128)(2,1)S(1)} collective-permute-done((bf16[128,1024]{1,0:T(8,128)(2,1)S(1)}, bf16[128,1024]{1,0:T(8,128)(2,1)S(1)}, u32[]{:S(2)}, u32[]{:S(2)}) %collective-permute-start.6) | collective-permute-done | bytes 262176 | tf_op jit(solution)/shard_map/fa_high/ppermute | solution.py:75
  65.7 1.2 collective-permute-start.8
  67.0 0.8 collective-permute-done.9.refs_5_.refs_13_
  67.7 1.5 collective-permute-done.11.refs_7_.refs_15_
  69.2 1.5 collective-permute-done.10.refs_6_.refs_14_
  70.7 9.7 %collective-permute-done.8.refs_4_.refs_12_ = bf16[4,128,1024]{2,1,0:T(8,128)(2,1)S(1)} collective-permute-done((bf16[4,128,1024]{2,1,0:T(8,128)(2,1)S(1)}, bf16[4,128,1024]{2,1,0:T(8,128)(2,1)S(1)}, u32[]{:S(2)}, u32[]{:S(2)}) %collective-permute-start.8) | collective-permute-done | bytes 1048608 | tf_op jit(solution)/shard_map/q_both/ppermute | solution.py:75
  80.5 1.2 collective-permute-start.14
  82.2 2.5 collective-permute-start.17
  84.7 2.0 collective-permute-start.15
  86.7 20.7 %shard_map.279 = (bf16[320,1024]{1,0:T(8,128)(2,1)}, bf16[320,16]{1,0:T(8,128)(2,1)}, bf16[320,1024]{1,0:T(8,128)(2,1)}, bf16[320,1024]{1,0:T(8,128)(2,1)}, bf16...) custom-call(s32[4]{0:T(128)} %copy-done.11, ...), custom_call_target="tpu_custom_call" | custom-call | tf_op jit(solution)/shard_map/pallas_call | solution.py:54
  108.1 0.9 collective-permute-start.18
  109.2 1.8 collective-permute-done.19.refs_5_
  110.9 1.0 collective-permute-done.21.refs_7_
  111.9 1.5 collective-permute-done.20.refs_6_
  113.4 9.7 %collective-permute-done.18.refs_4_ = bf16[4,128,1024]{2,1,0:T(8,128)(2,1)S(1)} collective-permute-done((bf16[4,128,1024]{2,1,0:T(8,128)(2,1)}, bf16[4,128,1024]{2,1,0:T(8,128)(2,1)S(1)}, u32[]{:S(2)}, u32[]{:S(2)}) %collective-permute-start.18) | collective-permute-done | bytes 1048608 | tf_op jit(solution)/shard_map/fa_both/ppermute | solution.py:75
  123.2 1.0 copy-done.28
  124.1 0.9 collective-permute-start.23
  125.0 1.4 collective-permute-start.22
  126.5 1.0 copy-done.31
  127.5 15.5 %shard_map.280 = (f32[320,1024]{1,0:T(8,128)}, f32[320,1024]{1,0:T(8,128)}, f32[320,16]{1,0:T(8,128)}, f32[320,16]{1,0:T(8,128)}, bf16[320,1024]{1,0:T(8,128)(2,1)}, /*index=5*/bf16[32,16,128]{2,1,0:T(8,128)(2,1)}) custom-call(s32[4]{0:T(128)} %copy-done.11, bf16[4,128,1024]{2,1,0:T(8,128)(2,1)} %copy-done.3, ...), custom_call_target="tpu_custom_call" | custom-call | tf_op jit(solution)/shard_map/pallas_call | solution.py:54
  143.0 7.0 %collective-permute-done.23.refs_3_ = bf16[4,128,1024]{2,1,0:T(8,128)(2,1)S(1)} collective-permute-done((bf16[4,128,1024]{2,1,0:T(8,128)(2,1)S(1)}, bf16[4,128,1024]{2,1,0:T(8,128)(2,1)S(1)}, u32[]{:S(2)}, u32[]{:S(2)}) %collective-permute-start.23) | collective-permute-done | bytes 1048608 | tf_op jit(solution)/shard_map/fb_two/ppermute | solution.py:75
  149.9 0.9 collective-permute-start.25
  151.4 13.4 %collective-permute-done.25.refs_4_ = bf16[4,128,1024]{2,1,0:T(8,128)(2,1)S(1)} collective-permute-done((bf16[4,128,1024]{2,1,0:T(8,128)(2,1)S(1)}, bf16[4,128,1024]{2,1,0:T(8,128)(2,1)S(1)}, u32[]{:S(2)}, u32[]{:S(2)}) %collective-permute-start.25) | collective-permute-done | bytes 1048608 | tf_op jit(solution)/shard_map/fb_both/ppermute | solution.py:75
  164.9 2.6 collective-permute-done.29.refs_8_
  167.5 1.0 copy-done.30
  168.5 21.8 %shard_map.281 = (bf16[4,320,256]{2,1,0:T(8,128)(2,1)}, bf16[320,1024]{1,0:T(8,128)(2,1)}, f32[320,1024]{1,0:T(8,128)}, bf16[32,16,512]{2,1,0:T(8,128)(2,1)}) custom-call(s32[4]{0:T(128)} %copy-done.11, bf16[4,128,1024]{2,1,0:T(8,128)(2,1)} %copy-done.4, bf16[4,128,1024]{2,1,0:T(8,128)(2,1)} %copy-done.21, bf16[4,128,1024]{2,1,0:T(8,128)(2,1)} %copy-done.20, ...), custom_call_target="tpu_custom_call" | custom-call | tf_op jit(solution)/shard_map/pallas_call | solution.py:54
  190.4 2.9 %all-to-all-start.1 = ((bf16[32,16,512]{2,1,0:T(8,128)(2,1)}), bf16[32,16,512]{2,1,0:T(8,128)(2,1)S(1)}, u32[]{:S(2)}, u32[]{:S(2)}) async-start(bf16[32,16,512]{2,1,0:T(8,128)(2,1)} %get-tuple-element.115), calls=%async_computation.1 | async-start | bytes 1048576 | tf_op jit(solution)/shard_map/grads_b_send/all_to_all | solution.py:616
  193.3 13.0 %shard_map.282 = (bf16[320,1024]{1,0:T(8,128)(2,1)}, bf16[320,1024]{1,0:T(8,128)(2,1)}, bf16[320,1024]{1,0:T(8,128)(2,1)}, bf16[320,16]{1,0:T(8,128)(2,1)}, bf16[32,16,128]{2,1,0:T(8,128)(2,1)}) custom-call(s32[4]{0:T(128)} %copy-done.11, f32[320,1]{1,0:T(8,128)} %copy-done.8, bf16[320,1024]{1,0:T(8,128)(2,1)} %get-tuple-element.82.refs_2_, ...), custom_call_target="tpu_custom_call" | custom-call | tf_op jit(solution)/shard_map/pallas_call | solution.py:54
  206.2 2.6 all-to-all-done.1.mine
  208.8 3.3 %all-to-all-start.2 = ((bf16[32,16,128]{2,1,0:T(8,128)(2,1)}), bf16[32,16,128]{2,1,0:T(8,128)(2,1)S(1)}, u32[]{:S(2)}, u32[]{:S(2)}) async-start(bf16[32,16,128]{2,1,0:T(8,128)(2,1)} %get-tuple-element.116), calls=%async_computation.2 | async-start | bytes 262144 | tf_op jit(solution)/shard_map/grads_c_send/all_to_all | solution.py:616
  212.8 0.7 grads_b.5
  213.6 3.7 %collective-permute-start.32 = (bf16[128,384]{1,0:T(8,128)(2,1)S(1)}, bf16[128,384]{1,0:T(8,128)(2,1)S(1)}, u32[]{:S(2)}, u32[]{:S(2)}) collective-permute-start(bf16[128,384]{1,0:T(8,128)(2,1)S(1)} %bitcast.23), channel_id=1, source_target_pairs={{0,24},{1,25},{2,26},{3,27},{4,28},{5,29},{6,30},{7,31},{8,16},{9,... | collective-permute-start | bytes 294920 | tf_op jit(solution)/shard_map/grads_b/ppermute | solution.py:75
  217.2 0.8 collective-permute-start.30
  218.0 2.3 all-to-all-done.2.mine
  221.0 1.4 collective-permute-start.35
  222.4 0.9 collective-permute-start.34
  223.3 3.9 %collective-permute-done.35.refs_3_ = bf16[128,128]{1,0:T(8,128)(2,1)S(1)} collective-permute-done((bf16[128,128]{1,0:T(8,128)(2,1)S(1)}, bf16[128,128]{1,0:T(8,128)(2,1)S(1)}, u32[]{:S(2)}, u32[]{:S(2)}) %collective-permute-start.35) | collective-permute-done | bytes 32800 | tf_op jit(solution)/shard_map/grads_b/ppermute | solution.py:75
  227.1 2.7 collective-permute-start.33
  229.9 1.9 collective-permute-done.33.refs_1_
  232.6 1.6 collective-permute-start.37
  234.2 1.5 collective-permute-start.36
  235.7 10.7 %shard_map.283 = bf16[4,640,256]{2,1,0:T(8,128)(2,1)} custom-call(s32[4]{0:T(128)} %copy-done.11, bf16[4,128,1024]{2,1,0:T(8,128)(2,1)} %copy-done.2, bf16[4,128,1024]{2,1,0:T(8,128)(2,1)} %copy-done.14, bf16[4,128,1024]{2,1,0:T(8,128)(2,1)} %copy-done.13, bf16[4,128,1024]{2,1,0:T(8,128)(2,1)} %copy-done.18, bf16[4,128,1024]{2,1,0:T(8,128)(2,1)} %copy-done.15, ...), custom_call_target="tpu_custom_call" | custom-call | tf_op jit(solution)/shard_map/pallas_call | solution.py:54
  246.7 1.5 collective-permute-start.38
  248.3 7.8 %collective-permute-done.38.refs_4_ = bf16[4,128,512]{2,1,0:T(8,128)(2,1)} collective-permute-done((bf16[4,128,512]{2,1,0:T(8,128)(2,1)S(1)}, bf16[4,128,512]{2,1,0:T(8,128)(2,1)}, u32[]{:S(2)}, u32[]{:S(2)}) %collective-permute-start.38) | collective-permute-done | bytes 524320 | tf_op jit(solution)/shard_map/grads/ppermute | solution.py:75
  256.1 3.5 %all-to-all-start.3 = ((bf16[4,640,256]{2,1,0:T(8,128)(2,1)}), bf16[4,640,256]{2,1,0:T(8,128)(2,1)S(1)}, u32[]{:S(2)}, u32[]{:S(2)}) async-start(bf16[4,640,256]{2,1,0:T(8,128)(2,1)} %shard_map.283), calls=%async_computation.3 | async-start | bytes 2621440 | tf_op jit(solution)/shard_map/rows_out/all_to_all | solution.py:866
  260.7 1.2 collective-permute-done.39.refs_5_
  262.0 1.5 collective-permute-done.41.refs_7_
  265.0 0.8 copy-done.37
  265.8 6.9 %grads.1 = (f32[128,4096]{1,0:T(8,128)}, f32[128,4096]{1,0:T(8,128)}, f32[128,1024]{1,0:T(8,128)}, f32[128,1024]{1,0:T(8,128)}, f32[128,1024]{1,0:T(8,128)}, /*i...) custom-call(s32[4]{0:T(128)} %copy-done.11, bf16[4,128,512]{2,1,0:T(8,128)(2,1)} %copy-done.5, ...), custom_call_target="tpu_custom_call" | custom-call | tf_op jit(solution)/shard_map/grads/pallas_call | solution.py:54
  272.7 4.1 %all-to-all-done.3 = bf16[4,640,256]{2,1,0:T(8,128)(2,1)S(1)} async-done(((bf16[4,640,256]{2,1,0:T(8,128)(2,1)}), bf16[4,640,256]{2,1,0:T(8,128)(2,1)S(1)}, u32[]{:S(2)}, u32[]{:S(2)}) %all-to-all-start.3) | async-done | bytes 1310752 | tf_op jit(solution)/shard_map/rows_out/all_to_all | solution.py:866
  276.8 1.1 fusion.1
  (131 shorter events, 11.4 us)
Async XLA Ops:
  0.6 20.6 %copy-start = (bf16[8,16,3,1024]{3,1,2,0:T(8,128)(2,1)S(1)}, bf16[8,16,3,1024]{3,1,2,0:T(8,128)(2,1)}, u32[]{:S(2)}) copy-start(bf16[8,16,3,1024]{3,1,2,0:T(8,128)(2,1)} %param.35) | copy-start | bytes 2359300
  6.2 13.5 %copy-start.10 = (bf16[1024,128]{1,0:T(8,128)(2,1)S(1)}, bf16[1024,128]{1,0:T(8,128)(2,1)}, u32[]{:S(2)}) copy-start(bf16[1024,128]{1,0:T(8,128)(2,1)} %w2.1) | copy-start | bytes 786436
  6.2 32.6 %all-to-all-start = ((bf16[4,656,256]{2,1,0:T(8,128)(2,1)}), bf16[4,656,256]{2,1,0:T(8,128)(2,1)}, u32[]{:S(2)}, u32[]{:S(2)}) async-start(bf16[4,656,256]{2,1,0:T(8,128)(2,1)} %shard_map.278), calls=%async_computation | async-start | bytes 2686976 | tf_op jit(solution)/shard_map/all_to_all | solution.py:716
  10.7 12.4 %collective-permute-start.2 = (bf16[128,1024]{1,0:T(8,128)(2,1)S(1)}, bf16[128,1024]{1,0:T(8,128)(2,1)S(1)}, u32[]{:S(2)}, u32[]{:S(2)}) collective-permute-start(bf16[128,1024]{1,0:T(8,128)(2,1)S(1)} %copy-done.6), channel_id=1, source_target_pairs={{0,24},{1,25},{2,26},{3,27},{4,28},{5,29},{6,30},{7,31},{8,16},{9,... | collective-permute-start | bytes 786440 | tf_op jit(solution)/shard_map/q_high/ppermute | solution.py:75
  15.8 22.8 %collective-permute-start.1 = (bf16[128,1024]{1,0:T(8,128)(2,1)S(1)}, bf16[128,1024]{1,0:T(8,128)(2,1)S(1)}, u32[]{:S(2)}, u32[]{:S(2)}) collective-permute-start(bf16[128,1024]{1,0:T(8,128)(2,1)S(1)} %copy-done.6), channel_id=1, source_target_pairs={{0,16},{1,17},{2,18},{3,19},{4,20},{5,21},{6,22},{7,23},{8,24},{9,... | collective-permute-start | bytes 786440 | tf_op jit(solution)/shard_map/q_high/ppermute | solution.py:75
  15.8 22.8 %collective-permute-start = (bf16[128,1024]{1,0:T(8,128)(2,1)S(1)}, bf16[128,1024]{1,0:T(8,128)(2,1)S(1)}, u32[]{:S(2)}, u32[]{:S(2)}) collective-permute-start(bf16[128,1024]{1,0:T(8,128)(2,1)S(1)} %copy-done.6), channel_id=1, source_target_pairs={{0,8},{1,9},{2,10},{3,11},{4,12},{5,13},{6,14},{7,15},{8,0},{9,1},... | collective-permute-start | bytes 786440 | tf_op jit(solution)/shard_map/q_high/ppermute | solution.py:75
  19.7 19.1 %copy-start.11 = (s32[4]{0:T(128)}, s32[4]{0:T(128)S(1)}, u32[]{:S(2)}) copy-start(s32[4]{0:T(128)S(1)} %pad_add_fusion.sc.refs_0_) | copy-start | bytes 52
  21.2 17.4 %copy-start.8 = (f32[320,1]{1,0:T(8,128)}, f32[320,1]{1,0:T(8,128)S(1)}, u32[]{:S(2)}) copy-start(f32[320,1]{1,0:T(8,128)S(1)} %get-tuple-element.74.refs_10_.refs_1_) | copy-start | bytes 3844
  38.8 47.9 %copy-start.2 = (bf16[4,128,1024]{2,1,0:T(8,128)(2,1)}, bf16[4,128,1024]{2,1,0:T(8,128)(2,1)S(1)}, u32[]{:S(2)}) copy-start(bf16[4,128,1024]{2,1,0:T(8,128)(2,1)S(1)} %q_high.1.refs_1_.refs_9_) | copy-start | bytes 3145732
  38.8 26.2 %collective-permute-start.4 = (bf16[4,128,1024]{2,1,0:T(8,128)(2,1)S(1)}, bf16[4,128,1024]{2,1,0:T(8,128)(2,1)S(1)}, u32[]{:S(2)}, u32[]{:S(2)}) collective-permute-start(bf16[4,128,1024]{2,1,0:T(8,128)(2,1)S(1)} %q_high.1.refs_1_.refs_9_), channel_id=1, source_target_pairs={{0,4},{1,3},{2,6},{3,1},{4,0},{5,7},{6,2},{7,5},{8,12},{9,11},{10,... | collective-permute-start | bytes 3145736 | tf_op jit(solution)/shard_map/q_two/ppermute | solution.py:75
  40.4 24.6 %collective-permute-start.3 = (bf16[4,128,1024]{2,1,0:T(8,128)(2,1)S(1)}, bf16[4,128,1024]{2,1,0:T(8,128)(2,1)S(1)}, u32[]{:S(2)}, u32[]{:S(2)}) collective-permute-start(bf16[4,128,1024]{2,1,0:T(8,128)(2,1)S(1)} %q_high.1.refs_1_.refs_9_), channel_id=1, source_target_pairs={{0,2},{1,5},{2,0},{3,7},{4,6},{5,1},{6,4},{7,3},{8,10},{9,13},{10,... | collective-permute-start | bytes 3145736 | tf_op jit(solution)/shard_map/q_one/ppermute | solution.py:75
  42.1 11.1 %collective-permute-start.7 = (bf16[128,1024]{1,0:T(8,128)(2,1)S(1)}, bf16[128,1024]{1,0:T(8,128)(2,1)S(1)}, u32[]{:S(2)}, u32[]{:S(2)}) collective-permute-start(bf16[128,1024]{1,0:T(8,128)(2,1)S(1)} %get-tuple-element.76.refs_0_), channel_id=1, source_target_pairs={{0,24},{1,25},{2,26},{3,27},{4,28},{5,29},{6,30},{7,31},{8,16},{9,... | collective-permute-start | bytes 786440 | tf_op jit(solution)/shard_map/fa_high/ppermute | solution.py:75
  44.5 20.4 %collective-permute-start.6 = (bf16[128,1024]{1,0:T(8,128)(2,1)S(1)}, bf16[128,1024]{1,0:T(8,128)(2,1)S(1)}, u32[]{:S(2)}, u32[]{:S(2)}) collective-permute-start(bf16[128,1024]{1,0:T(8,128)(2,1)S(1)} %get-tuple-element.76.refs_0_), channel_id=1, source_target_pairs={{0,16},{1,17},{2,18},{3,19},{4,20},{5,21},{6,22},{7,23},{8,24},{9,... | collective-permute-start | bytes 786440 | tf_op jit(solution)/shard_map/fa_high/ppermute | solution.py:75
  44.5 20.4 %collective-permute-start.5 = (bf16[128,1024]{1,0:T(8,128)(2,1)S(1)}, bf16[128,1024]{1,0:T(8,128)(2,1)S(1)}, u32[]{:S(2)}, u32[]{:S(2)}) collective-permute-start(bf16[128,1024]{1,0:T(8,128)(2,1)S(1)} %get-tuple-element.76.refs_0_), channel_id=1, source_target_pairs={{0,8},{1,9},{2,10},{3,11},{4,12},{5,13},{6,14},{7,15},{8,0},{9,1},... | collective-permute-start | bytes 786440 | tf_op jit(solution)/shard_map/fa_high/ppermute | solution.py:75
  65.0 21.7 %copy-start.13 = (bf16[4,128,1024]{2,1,0:T(8,128)(2,1)}, bf16[4,128,1024]{2,1,0:T(8,128)(2,1)S(1)}, u32[]{:S(2)}) copy-start(bf16[4,128,1024]{2,1,0:T(8,128)(2,1)S(1)} %collective-permute-done.4.refs_3_.refs_11_) | copy-start | bytes 3145732
  65.0 21.7 %copy-start.14 = (bf16[4,128,1024]{2,1,0:T(8,128)(2,1)}, bf16[4,128,1024]{2,1,0:T(8,128)(2,1)S(1)}, u32[]{:S(2)}) copy-start(bf16[4,128,1024]{2,1,0:T(8,128)(2,1)S(1)} %collective-permute-done.3.refs_2_.refs_10_) | copy-start | bytes 3145732
  65.0 2.7 collective-permute-start.9
  65.1 4.1 %collective-permute-start.11 = (bf16[4,128,1024]{2,1,0:T(8,128)(2,1)S(1)}, bf16[4,128,1024]{2,1,0:T(8,128)(2,1)S(1)}, u32[]{:S(2)}, u32[]{:S(2)}) collective-permute-start(bf16[4,128,1024]{2,1,0:T(8,128)(2,1)S(1)} %collective-permute-done.4.refs_3_.refs_11_), channel_id=1, source_target_pairs={{0,1},{1,0},{2,3},{3,2},{4,5},{5,4},{6,7},{7,6},{8,9},{9,8},{10,11... | collective-permute-start | bytes 3145736 | tf_op jit(solution)/shard_map/q_core/ppermute | solution.py:75
  65.6 5.1 %collective-permute-start.10 = (bf16[4,128,1024]{2,1,0:T(8,128)(2,1)S(1)}, bf16[4,128,1024]{2,1,0:T(8,128)(2,1)S(1)}, u32[]{:S(2)}, u32[]{:S(2)}) collective-permute-start(bf16[4,128,1024]{2,1,0:T(8,128)(2,1)S(1)} %collective-permute-done.3.refs_2_.refs_10_), channel_id=1, source_target_pairs={{0,1},{1,0},{2,3},{3,2},{4,5},{5,4},{6,7},{7,6},{8,9},{9,8},{10,11... | collective-permute-start | bytes 3145736 | tf_op jit(solution)/shard_map/q_core/ppermute | solution.py:75
  65.7 14.8 %collective-permute-start.8 = (bf16[4,128,1024]{2,1,0:T(8,128)(2,1)S(1)}, bf16[4,128,1024]{2,1,0:T(8,128)(2,1)S(1)}, u32[]{:S(2)}, u32[]{:S(2)}) collective-permute-start(bf16[4,128,1024]{2,1,0:T(8,128)(2,1)S(1)} %collective-permute-done.3.refs_2_.refs_10_), channel_id=1, source_target_pairs={{0,4},{1,3},{2,6},{3,1},{4,0},{5,7},{6,2},{7,5},{8,12},{9,11},{10,... | collective-permute-start | bytes 3145736 | tf_op jit(solution)/shard_map/q_both/ppermute | solution.py:75
  66.9 40.5 %copy-start.3 = (bf16[4,128,1024]{2,1,0:T(8,128)(2,1)}, bf16[4,128,1024]{2,1,0:T(8,128)(2,1)S(1)}, u32[]{:S(2)}) copy-start(bf16[4,128,1024]{2,1,0:T(8,128)(2,1)S(1)} %fa_high.1.refs_1_) | copy-start | bytes 3145732
  67.7 19.0 %copy-start.15 = (bf16[4,128,1024]{2,1,0:T(8,128)(2,1)}, bf16[4,128,1024]{2,1,0:T(8,128)(2,1)S(1)}, u32[]{:S(2)}) copy-start(bf16[4,128,1024]{2,1,0:T(8,128)(2,1)S(1)} %collective-permute-done.9.refs_5_.refs_13_) | copy-start | bytes 3145732
  69.2 15.5 %copy-start.16 = (bf16[4,128,1024]{2,1,0:T(8,128)(2,1)}, bf16[4,128,1024]{2,1,0:T(8,128)(2,1)S(1)}, u32[]{:S(2)}) copy-start(bf16[4,128,1024]{2,1,0:T(8,128)(2,1)S(1)} %collective-permute-done.11.refs_7_.refs_15_) | copy-start | bytes 3145732
  70.7 14.0 %copy-start.17 = (bf16[4,128,1024]{2,1,0:T(8,128)(2,1)}, bf16[4,128,1024]{2,1,0:T(8,128)(2,1)S(1)}, u32[]{:S(2)}) copy-start(bf16[4,128,1024]{2,1,0:T(8,128)(2,1)S(1)} %collective-permute-done.10.refs_6_.refs_14_) | copy-start | bytes 3145732
  80.5 4.2 %collective-permute-start.12 = (bf16[4,128,1024]{2,1,0:T(8,128)(2,1)S(1)}, bf16[4,128,1024]{2,1,0:T(8,128)(2,1)S(1)}, u32[]{:S(2)}, u32[]{:S(2)}) collective-permute-start(bf16[4,128,1024]{2,1,0:T(8,128)(2,1)S(1)} %collective-permute-done.8.refs_4_.refs_12_), channel_id=1, source_target_pairs={{0,1},{1,0},{2,3},{3,2},{4,5},{5,4},{6,7},{7,6},{8,9},{9,8},{10,11... | collective-permute-start | bytes 3145736 | tf_op jit(solution)/shard_map/q_core/ppermute | solution.py:75
  80.5 27.0 %collective-permute-start.14 = (bf16[4,128,1024]{2,1,0:T(8,128)(2,1)S(1)}, bf16[4,128,1024]{2,1,0:T(8,128)(2,1)}, u32[]{:S(2)}, u32[]{:S(2)}) collective-permute-start(bf16[4,128,1024]{2,1,0:T(8,128)(2,1)S(1)} %fa_high.1.refs_1_), channel_id=1, source_target_pairs={{0,4},{1,3},{2,6},{3,1},{4,0},{5,7},{6,2},{7,5},{8,12},{9,11},{10,... | collective-permute-start | bytes 3145736 | tf_op jit(solution)/shard_map/fa_two/ppermute | solution.py:75
  81.6 25.8 %collective-permute-start.13 = (bf16[4,128,1024]{2,1,0:T(8,128)(2,1)S(1)}, bf16[4,128,1024]{2,1,0:T(8,128)(2,1)}, u32[]{:S(2)}, u32[]{:S(2)}) collective-permute-start(bf16[4,128,1024]{2,1,0:T(8,128)(2,1)S(1)} %fa_high.1.refs_1_), channel_id=1, source_target_pairs={{0,2},{1,5},{2,0},{3,7},{4,6},{5,1},{6,4},{7,3},{8,10},{9,13},{10,... | collective-permute-start | bytes 3145736 | tf_op jit(solution)/shard_map/fa_one/ppermute | solution.py:75
  82.2 25.2 %collective-permute-start.17 = (bf16[128,1024]{1,0:T(8,128)(2,1)S(1)}, bf16[128,1024]{1,0:T(8,128)(2,1)S(1)}, u32[]{:S(2)}, u32[]{:S(2)}) collective-permute-start(bf16[128,1024]{1,0:T(8,128)(2,1)S(1)} %get-tuple-element.88.refs_0_), channel_id=1, source_target_pairs={{0,24},{1,25},{2,26},{3,27},{4,28},{5,29},{6,30},{7,31},{8,16},{9,... | collective-permute-start | bytes 786440 | tf_op jit(solution)/shard_map/fb_high/ppermute | solution.py:75
  84.7 22.7 %collective-permute-start.16 = (bf16[128,1024]{1,0:T(8,128)(2,1)S(1)}, bf16[128,1024]{1,0:T(8,128)(2,1)S(1)}, u32[]{:S(2)}, u32[]{:S(2)}) collective-permute-start(bf16[128,1024]{1,0:T(8,128)(2,1)S(1)} %get-tuple-element.88.refs_0_), channel_id=1, source_target_pairs={{0,16},{1,17},{2,18},{3,19},{4,20},{5,21},{6,22},{7,23},{8,24},{9,... | collective-permute-start | bytes 786440 | tf_op jit(solution)/shard_map/fb_high/ppermute | solution.py:75
  84.7 22.7 %collective-permute-start.15 = (bf16[128,1024]{1,0:T(8,128)(2,1)S(1)}, bf16[128,1024]{1,0:T(8,128)(2,1)S(1)}, u32[]{:S(2)}, u32[]{:S(2)}) collective-permute-start(bf16[128,1024]{1,0:T(8,128)(2,1)S(1)} %get-tuple-element.88.refs_0_), channel_id=1, source_target_pairs={{0,8},{1,9},{2,10},{3,11},{4,12},{5,13},{6,14},{7,15},{8,0},{9,1},... | collective-permute-start | bytes 786440 | tf_op jit(solution)/shard_map/fb_high/ppermute | solution.py:75
  107.5 3.4 %collective-permute-start.19 = (bf16[4,128,1024]{2,1,0:T(8,128)(2,1)S(1)}, bf16[4,128,1024]{2,1,0:T(8,128)(2,1)S(1)}, u32[]{:S(2)}, u32[]{:S(2)}) collective-permute-start(bf16[4,128,1024]{2,1,0:T(8,128)(2,1)S(1)} %fa_high.1.refs_1_), channel_id=1, source_target_pairs={{0,1},{1,0},{2,3},{3,2},{4,5},{5,4},{6,7},{7,6},{8,9},{9,8},{10,11... | collective-permute-start | bytes 3145736 | tf_op jit(solution)/shard_map/fa_core/ppermute | solution.py:75
  107.6 4.4 %collective-permute-start.21 = (bf16[4,128,1024]{2,1,0:T(8,128)(2,1)}, bf16[4,128,1024]{2,1,0:T(8,128)(2,1)S(1)}, u32[]{:S(2)}, u32[]{:S(2)}) collective-permute-start(bf16[4,128,1024]{2,1,0:T(8,128)(2,1)} %collective-permute-done.14.refs_3_), channel_id=1, source_target_pairs={{0,1},{1,0},{2,3},{3,2},{4,5},{5,4},{6,7},{7,6},{8,9},{9,8},{10,11... | collective-permute-start | bytes 3145736 | tf_op jit(solution)/shard_map/fa_core/ppermute | solution.py:75
  108.1 5.4 %collective-permute-start.20 = (bf16[4,128,1024]{2,1,0:T(8,128)(2,1)}, bf16[4,128,1024]{2,1,0:T(8,128)(2,1)S(1)}, u32[]{:S(2)}, u32[]{:S(2)}) collective-permute-start(bf16[4,128,1024]{2,1,0:T(8,128)(2,1)} %collective-permute-done.13.refs_2_), channel_id=1, source_target_pairs={{0,1},{1,0},{2,3},{3,2},{4,5},{5,4},{6,7},{7,6},{8,9},{9,8},{10,11... | collective-permute-start | bytes 3145736 | tf_op jit(solution)/shard_map/fa_core/ppermute | solution.py:75
  108.1 15.0 %collective-permute-start.18 = (bf16[4,128,1024]{2,1,0:T(8,128)(2,1)}, bf16[4,128,1024]{2,1,0:T(8,128)(2,1)S(1)}, u32[]{:S(2)}, u32[]{:S(2)}) collective-permute-start(bf16[4,128,1024]{2,1,0:T(8,128)(2,1)} %collective-permute-done.13.refs_2_), channel_id=1, source_target_pairs={{0,4},{1,3},{2,6},{3,1},{4,0},{5,7},{6,2},{7,5},{8,12},{9,11},{10,... | collective-permute-start | bytes 3145736 | tf_op jit(solution)/shard_map/fa_both/ppermute | solution.py:75
  109.1 41.7 %copy-start.4 = (bf16[4,128,1024]{2,1,0:T(8,128)(2,1)}, bf16[4,128,1024]{2,1,0:T(8,128)(2,1)S(1)}, u32[]{:S(2)}) copy-start(bf16[4,128,1024]{2,1,0:T(8,128)(2,1)S(1)} %fb_high.1.refs_1_) | copy-start | bytes 3145732
  110.9 15.5 %copy-start.22 = (bf16[4,128,1024]{2,1,0:T(8,128)(2,1)}, bf16[4,128,1024]{2,1,0:T(8,128)(2,1)S(1)}, u32[]{:S(2)}) copy-start(bf16[4,128,1024]{2,1,0:T(8,128)(2,1)S(1)} %collective-permute-done.19.refs_5_) | copy-start | bytes 3145732
  111.9 14.5 %copy-start.24 = (bf16[4,128,1024]{2,1,0:T(8,128)(2,1)}, bf16[4,128,1024]{2,1,0:T(8,128)(2,1)S(1)}, u32[]{:S(2)}) copy-start(bf16[4,128,1024]{2,1,0:T(8,128)(2,1)S(1)} %collective-permute-done.21.refs_7_) | copy-start | bytes 3145732
  123.2 3.3 %collective-permute-start.24 = (bf16[4,128,1024]{2,1,0:T(8,128)(2,1)S(1)}, bf16[4,128,1024]{2,1,0:T(8,128)(2,1)S(1)}, u32[]{:S(2)}, u32[]{:S(2)}) collective-permute-start(bf16[4,128,1024]{2,1,0:T(8,128)(2,1)S(1)} %collective-permute-done.18.refs_4_), channel_id=1, source_target_pairs={{0,1},{1,0},{2,3},{3,2},{4,5},{5,4},{6,7},{7,6},{8,9},{9,8},{10,11... | collective-permute-start | bytes 3145736 | tf_op jit(solution)/shard_map/fa_core/ppermute | solution.py:75
  124.1 25.8 %collective-permute-start.23 = (bf16[4,128,1024]{2,1,0:T(8,128)(2,1)S(1)}, bf16[4,128,1024]{2,1,0:T(8,128)(2,1)S(1)}, u32[]{:S(2)}, u32[]{:S(2)}) collective-permute-start(bf16[4,128,1024]{2,1,0:T(8,128)(2,1)S(1)} %fb_high.1.refs_1_), channel_id=1, source_target_pairs={{0,4},{1,3},{2,6},{3,1},{4,0},{5,7},{6,2},{7,5},{8,12},{9,11},{10,... | collective-permute-start | bytes 3145736 | tf_op jit(solution)/shard_map/fb_two/ppermute | solution.py:75
  125.0 24.9 %collective-permute-start.22 = (bf16[4,128,1024]{2,1,0:T(8,128)(2,1)S(1)}, bf16[4,128,1024]{2,1,0:T(8,128)(2,1)S(1)}, u32[]{:S(2)}, u32[]{:S(2)}) collective-permute-start(bf16[4,128,1024]{2,1,0:T(8,128)(2,1)S(1)} %fb_high.1.refs_1_), channel_id=1, source_target_pairs={{0,2},{1,5},{2,0},{3,7},{4,6},{5,1},{6,4},{7,3},{8,10},{9,13},{10,... | collective-permute-start | bytes 3145736 | tf_op jit(solution)/shard_map/fb_one/ppermute | solution.py:75
  149.9 18.5 %copy-start.20 = (bf16[4,128,1024]{2,1,0:T(8,128)(2,1)}, bf16[4,128,1024]{2,1,0:T(8,128)(2,1)S(1)}, u32[]{:S(2)}) copy-start(bf16[4,128,1024]{2,1,0:T(8,128)(2,1)S(1)} %collective-permute-done.23.refs_3_) | copy-start | bytes 3145732
  149.9 18.5 %copy-start.21 = (bf16[4,128,1024]{2,1,0:T(8,128)(2,1)}, bf16[4,128,1024]{2,1,0:T(8,128)(2,1)S(1)}, u32[]{:S(2)}) copy-start(bf16[4,128,1024]{2,1,0:T(8,128)(2,1)S(1)} %collective-permute-done.22.refs_2_) | copy-start | bytes 3145732
  149.9 14.9 %collective-permute-start.25 = (bf16[4,128,1024]{2,1,0:T(8,128)(2,1)S(1)}, bf16[4,128,1024]{2,1,0:T(8,128)(2,1)S(1)}, u32[]{:S(2)}, u32[]{:S(2)}) collective-permute-start(bf16[4,128,1024]{2,1,0:T(8,128)(2,1)S(1)} %collective-permute-done.22.refs_2_), channel_id=1, source_target_pairs={{0,4},{1,3},{2,6},{3,1},{4,0},{5,7},{6,2},{7,5},{8,12},{9,11},{10,... | collective-permute-start | bytes 3145736 | tf_op jit(solution)/shard_map/fb_both/ppermute | solution.py:75
  150.9 14.0 %collective-permute-start.27 = (bf16[4,128,1024]{2,1,0:T(8,128)(2,1)S(1)}, bf16[4,128,1024]{2,1,0:T(8,128)(2,1)S(1)}, u32[]{:S(2)}, u32[]{:S(2)}) collective-permute-start(bf16[4,128,1024]{2,1,0:T(8,128)(2,1)S(1)} %collective-permute-done.22.refs_2_), channel_id=1, source_target_pairs={{0,1},{1,0},{2,3},{3,2},{4,5},{5,4},{6,7},{7,6},{8,9},{9,8},{10,11... | collective-permute-start | bytes 3145736 | tf_op jit(solution)/shard_map/fb_core/ppermute | solution.py:75
  150.9 13.9 %collective-permute-start.26 = (bf16[4,128,1024]{2,1,0:T(8,128)(2,1)S(1)}, bf16[4,128,1024]{2,1,0:T(8,128)(2,1)S(1)}, u32[]{:S(2)}, u32[]{:S(2)}) collective-permute-start(bf16[4,128,1024]{2,1,0:T(8,128)(2,1)S(1)} %fb_high.1.refs_1_), channel_id=1, source_target_pairs={{0,1},{1,0},{2,3},{3,2},{4,5},{5,4},{6,7},{7,6},{8,9},{9,8},{10,11... | collective-permute-start | bytes 3145736 | tf_op jit(solution)/shard_map/fb_core/ppermute | solution.py:75
  151.4 13.4 %collective-permute-start.28 = (bf16[4,128,1024]{2,1,0:T(8,128)(2,1)S(1)}, bf16[4,128,1024]{2,1,0:T(8,128)(2,1)S(1)}, u32[]{:S(2)}, u32[]{:S(2)}) collective-permute-start(bf16[4,128,1024]{2,1,0:T(8,128)(2,1)S(1)} %collective-permute-done.23.refs_3_), channel_id=1, source_target_pairs={{0,1},{1,0},{2,3},{3,2},{4,5},{5,4},{6,7},{7,6},{8,9},{9,8},{10,11... | collective-permute-start | bytes 3145736 | tf_op jit(solution)/shard_map/fb_core/ppermute | solution.py:75
  164.8 2.7 collective-permute-start.29
  190.4 18.4 %all-to-all-start.1 = ((bf16[32,16,512]{2,1,0:T(8,128)(2,1)}), bf16[32,16,512]{2,1,0:T(8,128)(2,1)S(1)}, u32[]{:S(2)}, u32[]{:S(2)}) async-start(bf16[32,16,512]{2,1,0:T(8,128)(2,1)} %get-tuple-element.115), calls=%async_computation.1 | async-start | bytes 1048576 | tf_op jit(solution)/shard_map/grads_b_send/all_to_all | solution.py:616
  208.8 11.5 %all-to-all-start.2 = ((bf16[32,16,128]{2,1,0:T(8,128)(2,1)}), bf16[32,16,128]{2,1,0:T(8,128)(2,1)S(1)}, u32[]{:S(2)}, u32[]{:S(2)}) async-start(bf16[32,16,128]{2,1,0:T(8,128)(2,1)} %get-tuple-element.116), calls=%async_computation.2 | async-start | bytes 262144 | tf_op jit(solution)/shard_map/grads_c_send/all_to_all | solution.py:616
  213.6 18.4 %collective-permute-start.32 = (bf16[128,384]{1,0:T(8,128)(2,1)S(1)}, bf16[128,384]{1,0:T(8,128)(2,1)S(1)}, u32[]{:S(2)}, u32[]{:S(2)}) collective-permute-start(bf16[128,384]{1,0:T(8,128)(2,1)S(1)} %bitcast.23), channel_id=1, source_target_pairs={{0,24},{1,25},{2,26},{3,27},{4,28},{5,29},{6,30},{7,31},{8,16},{9,... | collective-permute-start | bytes 294920 | tf_op jit(solution)/shard_map/grads_b/ppermute | solution.py:75
  217.2 14.7 %collective-permute-start.31 = (bf16[128,384]{1,0:T(8,128)(2,1)S(1)}, bf16[128,384]{1,0:T(8,128)(2,1)S(1)}, u32[]{:S(2)}, u32[]{:S(2)}) collective-permute-start(bf16[128,384]{1,0:T(8,128)(2,1)S(1)} %bitcast.24), channel_id=1, source_target_pairs={{0,16},{1,17},{2,18},{3,19},{4,20},{5,21},{6,22},{7,23},{8,24},{9,... | collective-permute-start | bytes 294920 | tf_op jit(solution)/shard_map/grads_b/ppermute | solution.py:75
  217.2 14.7 %collective-permute-start.30 = (bf16[128,384]{1,0:T(8,128)(2,1)S(1)}, bf16[128,384]{1,0:T(8,128)(2,1)S(1)}, u32[]{:S(2)}, u32[]{:S(2)}) collective-permute-start(bf16[128,384]{1,0:T(8,128)(2,1)S(1)} %bitcast.25), channel_id=1, source_target_pairs={{0,8},{1,9},{2,10},{3,11},{4,12},{5,13},{6,14},{7,15},{8,0},{9,1},... | collective-permute-start | bytes 294920 | tf_op jit(solution)/shard_map/grads_b/ppermute | solution.py:75
  221.0 6.1 %collective-permute-start.35 = (bf16[128,128]{1,0:T(8,128)(2,1)S(1)}, bf16[128,128]{1,0:T(8,128)(2,1)S(1)}, u32[]{:S(2)}, u32[]{:S(2)}) collective-permute-start(bf16[128,128]{1,0:T(8,128)(2,1)S(1)} %bitcast.27), channel_id=1, source_target_pairs={{0,24},{1,25},{2,26},{3,27},{4,28},{5,29},{6,30},{7,31},{8,16},{9,... | collective-permute-start | bytes 98312 | tf_op jit(solution)/shard_map/grads_b/ppermute | solution.py:75
  222.4 7.5 %collective-permute-start.34 = (bf16[128,128]{1,0:T(8,128)(2,1)S(1)}, bf16[128,128]{1,0:T(8,128)(2,1)S(1)}, u32[]{:S(2)}, u32[]{:S(2)}) collective-permute-start(bf16[128,128]{1,0:T(8,128)(2,1)S(1)} %bitcast.28), channel_id=1, source_target_pairs={{0,16},{1,17},{2,18},{3,19},{4,20},{5,21},{6,22},{7,23},{8,24},{9,... | collective-permute-start | bytes 98312 | tf_op jit(solution)/shard_map/grads_b/ppermute | solution.py:75
  227.1 4.6 %collective-permute-start.33 = (bf16[128,128]{1,0:T(8,128)(2,1)S(1)}, bf16[128,128]{1,0:T(8,128)(2,1)S(1)}, u32[]{:S(2)}, u32[]{:S(2)}) collective-permute-start(bf16[128,128]{1,0:T(8,128)(2,1)S(1)} %bitcast.29), channel_id=1, source_target_pairs={{0,8},{1,9},{2,10},{3,11},{4,12},{5,13},{6,14},{7,15},{8,0},{9,1},... | collective-permute-start | bytes 98312 | tf_op jit(solution)/shard_map/grads_b/ppermute | solution.py:75
  232.6 27.0 %copy-start.5 = (bf16[4,128,512]{2,1,0:T(8,128)(2,1)}, bf16[4,128,512]{2,1,0:T(8,128)(2,1)S(1)}, u32[]{:S(2)}) copy-start(bf16[4,128,512]{2,1,0:T(8,128)(2,1)S(1)} %grads_b.9.refs_1_) | copy-start | bytes 1572868
  232.6 14.1 %collective-permute-start.37 = (bf16[4,128,512]{2,1,0:T(8,128)(2,1)S(1)}, bf16[4,128,512]{2,1,0:T(8,128)(2,1)S(1)}, u32[]{:S(2)}, u32[]{:S(2)}) collective-permute-start(bf16[4,128,512]{2,1,0:T(8,128)(2,1)S(1)} %grads_b.9.refs_1_), channel_id=1, source_target_pairs={{0,4},{1,3},{2,6},{3,1},{4,0},{5,7},{6,2},{7,5},{8,12},{9,11},{10,... | collective-permute-start | bytes 1572872 | tf_op jit(solution)/shard_map/grads/ppermute | solution.py:75
  234.2 12.5 %collective-permute-start.36 = (bf16[4,128,512]{2,1,0:T(8,128)(2,1)S(1)}, bf16[4,128,512]{2,1,0:T(8,128)(2,1)S(1)}, u32[]{:S(2)}, u32[]{:S(2)}) collective-permute-start(bf16[4,128,512]{2,1,0:T(8,128)(2,1)S(1)} %grads_b.9.refs_1_), channel_id=1, source_target_pairs={{0,2},{1,5},{2,0},{3,7},{4,6},{5,1},{6,4},{7,3},{8,10},{9,13},{10,... | collective-permute-start | bytes 1572872 | tf_op jit(solution)/shard_map/grads/ppermute | solution.py:75
  246.7 9.3 %collective-permute-start.38 = (bf16[4,128,512]{2,1,0:T(8,128)(2,1)S(1)}, bf16[4,128,512]{2,1,0:T(8,128)(2,1)}, u32[]{:S(2)}, u32[]{:S(2)}) collective-permute-start(bf16[4,128,512]{2,1,0:T(8,128)(2,1)S(1)} %collective-permute-done.36.refs_2_), channel_id=1, source_target_pairs={{0,4},{1,3},{2,6},{3,1},{4,0},{5,7},{6,2},{7,5},{8,12},{9,11},{10,... | collective-permute-start | bytes 1572872 | tf_op jit(solution)/shard_map/grads/ppermute | solution.py:75
  256.1 20.8 %all-to-all-start.3 = ((bf16[4,640,256]{2,1,0:T(8,128)(2,1)}), bf16[4,640,256]{2,1,0:T(8,128)(2,1)S(1)}, u32[]{:S(2)}, u32[]{:S(2)}) async-start(bf16[4,640,256]{2,1,0:T(8,128)(2,1)} %shard_map.283), calls=%async_computation.3 | async-start | bytes 2621440 | tf_op jit(solution)/shard_map/rows_out/all_to_all | solution.py:866
  259.6 2.3 collective-permute-start.39
  260.1 3.4 %collective-permute-start.41 = (bf16[4,128,512]{2,1,0:T(8,128)(2,1)S(1)}, bf16[4,128,512]{2,1,0:T(8,128)(2,1)S(1)}, u32[]{:S(2)}, u32[]{:S(2)}) collective-permute-start(bf16[4,128,512]{2,1,0:T(8,128)(2,1)S(1)} %collective-permute-done.37.refs_3_), channel_id=1, source_target_pairs={{0,1},{1,0},{2,3},{3,2},{4,5},{5,4},{6,7},{7,6},{8,9},{9,8},{10,11... | collective-permute-start | bytes 1572872 | tf_op jit(solution)/shard_map/grads/ppermute | solution.py:75
  260.2 4.0 %collective-permute-start.40 = (bf16[4,128,512]{2,1,0:T(8,128)(2,1)S(1)}, bf16[4,128,512]{2,1,0:T(8,128)(2,1)S(1)}, u32[]{:S(2)}, u32[]{:S(2)}) collective-permute-start(bf16[4,128,512]{2,1,0:T(8,128)(2,1)S(1)} %collective-permute-done.36.refs_2_), channel_id=1, source_target_pairs={{0,1},{1,0},{2,3},{3,2},{4,5},{5,4},{6,7},{7,6},{8,9},{9,8},{10,11... | collective-permute-start | bytes 1572872 | tf_op jit(solution)/shard_map/grads/ppermute | solution.py:75
  260.6 3.6 %collective-permute-start.42 = (bf16[4,128,512]{2,1,0:T(8,128)(2,1)}, bf16[4,128,512]{2,1,0:T(8,128)(2,1)S(1)}, u32[]{:S(2)}, u32[]{:S(2)}) collective-permute-start(bf16[4,128,512]{2,1,0:T(8,128)(2,1)} %collective-permute-done.38.refs_4_), channel_id=1, source_target_pairs={{0,1},{1,0},{2,3},{3,2},{4,5},{5,4},{6,7},{7,6},{8,9},{9,8},{10,11... | collective-permute-start | bytes 1572872 | tf_op jit(solution)/shard_map/grads/ppermute | solution.py:75
  (22 other events, 123.1 us)

commit v6 on v5

--- a/solution.py
+++ b/solution.py
@@ -18,6 +18,7 @@
 PAIR = 2 * HD
 EXTRA = 16
 OWNER = 128
+SPREAD = 56
 FRONT, FFN_A, FFN_B, ATT, BACK = 56, 56, 56, 56, 56
 BF = jnp.bfloat16
 F32 = jnp.float32
@@ -232,9 +233,23 @@
         for copy in self.copies:
             copy.start()
 
-    def wait(self):
-        for copy in self.copies:
+    def wait(self, away=None):
+        half = len(self.copies) // 2
+        for copy in self.copies if away is None else self.copies[away * half : (away + 1) * half]:
             copy.wait()
+
+    def slot(self, i, cols):
+        half = cols // 2
+
+        @pl.when(i == 0)
+        def _():
+            self.wait(0)
+
+        @pl.when(i == half)
+        def _():
+            self.wait(1)
+
+        return lax.rem(i, half) * 2 + i // half
 
 
 def column_of(sc, slot):
@@ -257,20 +272,18 @@
     return pl.ds(pl.multiple_of(start, width), width)
 
 
-def prep_q_kernel(wq, wp, out):
+def prep_q_kernel(tokens, grads, bias_qv, bias_f, wq, wp, rows, out):
     hid = wq.shape[2]
+    seq = tokens.shape[1]
+    for c in range(tokens.shape[0]):
+        rows[c, :seq] = tokens[c]
+        rows[c, seq : 2 * seq] = grads[c]
+        rows[c, 2 * seq : 2 * seq + 2] = bias_qv[...]
+        for i in range(4):
+            rows[c, 2 * seq + 2 + i : 2 * seq + 3 + i] = bias_f[:, i * hid : (i + 1) * hid]
     for c in range(3):
         out[:, c * hid : (c + 1) * hid] = wq[c]
     out[:, 3 * hid :] = low(wp[...].astype(F32).T)
-
-
-def prep_rows_kernel(tokens, grads, bias_qv, bias_f, out):
-    cols, seq = out.shape[0], tokens.shape[1]
-    for c in range(cols):
-        out[c, :seq] = tokens[c]
-        out[c, seq : 2 * seq] = grads[c]
-        out[c, 2 * seq : 2 * seq + 2] = bias_qv[...]
-        out[c, 2 * seq + 2 : 2 * seq + 6] = bias_f[...]
 
 
 def prep_f_kernel(sc, mask, w1, w2, out_a, out_b, keep, closed):
@@ -286,8 +299,30 @@
     out_b[:, half:] = low(w2[half:].astype(F32).T)
 
 
-def tokens_of(ref, cols):
-    return jnp.concatenate([ref[c, :SEQ, :] for c in range(cols)], axis=1).astype(F32)
+def fetch(sems, *pairs):
+    copies = [pltpu.make_async_copy(src, dst, sems.at[i]) for i, (src, dst) in enumerate(pairs)]
+    for copy in copies:
+        copy.start()
+    return copies
+
+
+def rows_at(xa, start, height):
+    return xa.at[:, pl.ds(start, height), :]
+
+
+def across(ref, cols):
+    return jnp.concatenate([ref[c] for c in range(cols)], axis=1).astype(F32)
+
+
+def both_heads(pair):
+    left = lax.broadcasted_iota(jnp.int32, (1, PAIR), 1) < HD
+    zero = jnp.zeros_like(pair)
+    return jnp.concatenate([jnp.where(left, pair, zero), jnp.where(left, zero, pair)], axis=0)
+
+
+def own_heads(made, scale=1.0):
+    both = jnp.concatenate([made[:HD, :SEQ], made[HD:, SEQ:]], axis=0)
+    return low(both.T * scale)
 
 
 def front_kernel(lead, cols, *refs):
@@ -295,24 +330,36 @@
     pieces = refs[1:9]
     (xa, closed, gain, shift, q_down, q_up, p_down, p_up, f_down, bias_out) = refs[9:19]
     (n1, lat1, q, k, v, lse, att, lat2, middle, n2, lat3) = refs[19:30]
-    w, sems, hidden, branch = refs[30:]
+    w, sems, hidden, branch, xs, bs, row_qd, row_pd, row_pu, row_fd, sems_f = refs[30:]
+    a = sc[0]
+    hid = D // cols
+    first = fetch(
+        sems_f,
+        (rows_at(xa, 0, SEQ), xs),
+        (q_down.at[a], row_qd),
+        (rows_at(xa, 2 * SEQ, EXTRA), bs),
+        (p_down.at[a], row_pd),
+        (p_up.at[a], row_pu),
+        (f_down.at[a], row_fd),
+    )
     weights = Weights(sc, pieces, w, sems, lead)
     weights.start()
-    a = sc[0]
-    hid = D // cols
-    x = tokens_of(xa, cols)
+    first[0].wait()
+    x = across(xs, cols)
     hidden[...] = x
     unit, _ = norm_parts(x)
     n1[...] = low(unit * gain[0:1] + shift[0:1])
-    lat1[...] = low(mm(n1[...], q_down[a], NT))
-    weights.wait()
-
-    def project(slot, _):
+    for copy in first[1:]:
+        copy.wait()
+    lat1[...] = low(mm(n1[...], row_qd[...], NT))
+
+    def project(i, _):
+        slot = weights.slot(i, cols)
         block = column_of(sc, slot)
         up = jnp.concatenate([q_up[c, :, lanes(block * hid, hid)] for c in range(3)], axis=1)
         made = mm(n1[...], w[slot, :, : 3 * hid]) + mm(lat1[...], up)
-        bias_q = xa[block, 2 * SEQ : 2 * SEQ + 1, :].astype(F32)
-        bias_v = xa[block, 2 * SEQ + 1 : 2 * SEQ + 2, :].astype(F32)
+        bias_q = bs[block, 0:1, :].astype(F32)
+        bias_v = bs[block, 1:2, :].astype(F32)
         at = lanes(slot * hid, hid)
         q[:, at] = low(made[:, :hid] + bias_q) * jnp.asarray(0.125, BF)
         k[:, at] = low(made[:, hid : 2 * hid])
@@ -321,33 +368,26 @@
 
     lax.fori_loop(0, cols, project, 0)
     shut = closed[...] > 0.5
-    left = lax.broadcasted_iota(jnp.int32, (1, PAIR), 1) < HD
 
     def attend(pair, _):
         at = lanes(pair * PAIR, PAIR)
-        qp, kp, vp = q[:, at], k[:, at], v[:, at]
-        v_t = low(vp.astype(F32).T)
-        halves = []
-        for h in range(2):
-            masked = jnp.where(left == (h == 0), qp, jnp.zeros_like(qp))
-            s = jnp.where(shut, -1e30, mm(kp, masked, NT))
-            top = jnp.max(s, axis=0, keepdims=True)
-            e = jnp.exp(s - top)
-            total = jnp.sum(e, axis=0, keepdims=True)
-            lse[pair, h : h + 1, :] = top + jnp.log(total)
-            soft = low(e * (1.0 / total))
-            halves.append(mm(v_t[h * HD : (h + 1) * HD], soft))
-        att[:, at] = low(jnp.concatenate(halves, axis=0).T)
+        v_t = low(v[:, at].astype(F32).T)
+        s = jnp.where(shut, -1e30, mm(k[:, at], both_heads(q[:, at]), NT))
+        top = jnp.max(s, axis=0, keepdims=True)
+        e = jnp.exp(s - top)
+        total = jnp.sum(e, axis=0, keepdims=True)
+        lse[pair] = top + jnp.log(total)
+        att[:, at] = own_heads(mm(v_t, low(e * (1.0 / total))))
         return 0
 
-    lax.fori_loop(0, H // 2, attend, 0)
+    lax.fori_loop(0, H // 2, attend, 0, unroll=4)
 
     def down_two(slot, acc):
         block = column_of(sc, slot)
-        return acc + mm(att[:, lanes(slot * hid, hid)], p_down[a, :, lanes(block * hid, hid)], NT)
+        return acc + mm(att[:, lanes(slot * hid, hid)], row_pd[:, lanes(block * hid, hid)], NT)
 
     lat2[...] = low(lax.fori_loop(0, cols, down_two, jnp.zeros((SEQ, R), F32)))
-    branch[...] = mm(lat2[...], p_up[a]) + bias_out[0:1].astype(F32)
+    branch[...] = mm(lat2[...], row_pu[...]) + bias_out[0:1].astype(F32)
 
     def out_proj(slot, _):
         branch[...] += mm(att[:, lanes(slot * hid, hid)], w[slot, :, 3 * hid :], NT)
@@ -358,26 +398,25 @@
     middle[...] = mid
     unit, _ = norm_parts(mid)
     n2[...] = low(unit * gain[1:2] + shift[1:2])
-    lat3[...] = low(mm(n2[...], f_down[a], NT))
-
-
-def ffn_steps(sc, part, cols, w, xa, n2, lat3, gr, glat4, up_1, down_2, acc, early, lane=0, spare=0):
+    lat3[...] = low(mm(n2[...], row_fd[...], NT))
+
+
+def ffn_steps(weights, sc, part, cols, w, bs, n2, lat3, gr, glat4, up_1, down_2, acc, early, lane=0, spare=0):
     res, gn2, lat4, glat3 = acc
-    a = sc[0]
     hid = D // cols
     ffn = FF // cols
     half = ffn // 2
     glat4_t = low(glat4.astype(F32).T)
     lat3_t = low(lat3[...].astype(F32).T)
 
-    def step(slot, _):
+    def step(i, _):
+        slot = weights.slot(i, cols)
         block = column_of(sc, slot)
         at = pl.ds(pl.multiple_of(block * ffn + part * half, half), half)
         bias = jnp.concatenate(
-            [xa[block, 2 * SEQ + 2 + 2 * part + i : 2 * SEQ + 3 + 2 * part + i, :] for i in range(2)],
-            axis=1,
+            [bs[block, 2 + 2 * part + i : 3 + 2 * part + i, :] for i in range(2)], axis=1
         ).astype(F32)
-        up, down = up_1[a, :, at], down_2[a, :, at]
+        up, down = up_1[:, at], down_2[:, at]
         w1, w2 = w[slot, :, :half], w[slot, :, half:]
         pre = mm(n2[...], w1) + mm(lat3[...], up) + bias
         back = mm(gr[...], w2) + mm(glat4, down)
@@ -401,20 +440,29 @@
     pieces = refs[1:9]
     xa, keep, n2, lat3, up_1, down_2, up_2 = refs[9:16]
     res, gn2, lat4, glat3, gr, early = refs[16:22]
-    w, sems = refs[22:]
+    w, sems, gs, bs, row_u1, row_d2, row_u2, sems_f = refs[22:]
+    a = sc[0]
+    first = fetch(
+        sems_f,
+        (rows_at(xa, SEQ, SEQ), gs),
+        (up_2.at[a], row_u2),
+        (rows_at(xa, 2 * SEQ, EXTRA), bs),
+        (up_1.at[a], row_u1),
+        (down_2.at[a], row_d2),
+    )
     weights = Weights(sc, pieces, w, sems, lead)
     weights.start()
-    gr[...] = low(
-        jnp.concatenate([xa[c, SEQ : 2 * SEQ] for c in range(cols)], axis=1).astype(F32) * keep[...]
-    )
-    glat4 = low(mm(gr[...], up_2[sc[0]], NT))
+    first[0].wait()
+    gr[...] = low(across(gs, cols) * keep[...])
+    for copy in first[1:]:
+        copy.wait()
+    glat4 = low(mm(gr[...], row_u2[...], NT))
     res[...] = jnp.zeros_like(res)
     gn2[...] = jnp.zeros_like(gn2)
     lat4[...] = jnp.zeros_like(lat4)
     glat3[...] = jnp.zeros_like(glat3)
-    weights.wait()
     ffn_steps(
-        sc, 0, cols, w, xa, n2, lat3, gr, glat4, up_1, down_2, (res, gn2, lat4, glat3), early
+        weights, sc, 0, cols, w, bs, n2, lat3, gr, glat4, row_u1, row_d2, (res, gn2, lat4, glat3), early
     )
 
 
@@ -425,39 +473,63 @@
     (xa, keep, gain, n2, lat3, up_1, down_2, up_2, f_down, p_down, p_up, bias_out) = refs[17:29]
     (middle, att, lat2, gr, res_in, gn2_in, lat4_in, glat3_in, early_in) = refs[29:38]
     layer, gatt, gmid, early = refs[38:42]
-    w, sems, wp, sems_p, res, gn2, lat4, glat3 = refs[42:]
+    w, sems, wp, sems_p, res, gn2, lat4, glat3 = refs[42:50]
+    bs, row_u1, row_d2, row_u2, row_fd, row_pd, row_pu, mid_s, att_s, res_s, gn2_s, early_s = refs[50:62]
+    sems_f = refs[62]
     lane = early_in.shape[-1]
-    early[:, :, :lane] = early_in[...]
+    a = sc[0]
+    first = fetch(
+        sems_f,
+        (up_2.at[a], row_u2),
+        (rows_at(xa, 2 * SEQ, EXTRA), bs),
+        (up_1.at[a], row_u1),
+        (down_2.at[a], row_d2),
+    )
     early[:, :, early.shape[2] - OWNER :] = low(jnp.full((early.shape[0], R, OWNER), sc[0], F32))
     weights = Weights(sc, pieces, w, sems, lead)
     weights.start()
     proj = Weights(sc, own_q, wp, sems_p, lead, 3 * D // cols)
+    last = fetch(
+        sems_f.at[pl.ds(4, 8)],
+        (res_in, res_s),
+        (middle, mid_s),
+        (gn2_in, gn2_s),
+        (f_down.at[a], row_fd),
+        (p_up.at[a], row_pu),
+        (p_down.at[a], row_pd),
+        (att, att_s),
+        (early_in, early_s),
+    )
     proj.start()
-    a = sc[0]
     hid = D // cols
-    glat4 = low(mm(gr[...], up_2[a], NT))
-    res[...] = res_in[...]
-    gn2[...] = gn2_in[...]
+    for copy in first:
+        copy.wait()
+    glat4 = low(mm(gr[...], row_u2[...], NT))
+    res[...] = jnp.zeros_like(res)
+    gn2[...] = jnp.zeros_like(gn2)
     lat4[...] = lat4_in[...]
     glat3[...] = glat3_in[...]
-    weights.wait()
     ffn_steps(
-        sc, 1, cols, w, xa, n2, lat3, gr, glat4, up_1, down_2, (res, gn2, lat4, glat3), early, lane, OWNER
-    )
-    mid = middle[...]
+        weights, sc, 1, cols, w, bs, n2, lat3, gr, glat4, row_u1, row_d2, (res, gn2, lat4, glat3), early, lane, OWNER
+    )
+    for copy in last:
+        copy.wait()
+    early[:, :, :lane] = early_s[...]
+    mid = mid_s[...]
     lat4_low = low(lat4[...])
     out = low(
-        keep[...] * (mid + res[...] + mm(lat4_low, up_2[a]) + bias_out[1:2].astype(F32))
+        keep[...]
+        * (mid + (res_s[...] + res[...]) + mm(lat4_low, row_u2[...]) + bias_out[1:2].astype(F32))
     )
     for c in range(cols):
         layer[c] = out[:, c * hid : (c + 1) * hid]
     glat3_low = low(glat3[...])
-    grad_normed = gn2[...] + mm(glat3_low, f_down[a])
+    grad_normed = gn2_s[...] + gn2[...] + mm(glat3_low, row_fd[...])
     unit, inverse = norm_parts(mid)
     grad_middle = gr[...].astype(F32) + norm_back(grad_normed, gain[1:2], unit, inverse)
     gmid[...] = grad_middle
     gb = low(grad_middle)
-    glat2 = low(mm(gb, p_up[a], NT))
+    glat2 = low(mm(gb, row_pu[...], NT))
     glat2_t = low(glat2.astype(F32).T)
     put(early, FF + D, low(mm(low(lat2[...].astype(F32).T), gb)), lane, OWNER)
     put(early, FF + 2 * D, low(mm(low(glat3_low.astype(F32).T), n2[...])), lane, OWNER)
@@ -468,8 +540,8 @@
         block = column_of(sc, slot)
         here = lanes(slot * hid, hid)
         there = lanes(block * hid, hid)
-        gatt[:, here] = low(mm(gb, wp[slot]) + mm(glat2, p_down[a, :, there]))
-        put(early, FF + block * hid, low(mm(glat2_t, att[:, here])), lane, OWNER)
+        gatt[:, here] = low(mm(gb, wp[slot]) + mm(glat2, row_pd[:, there]))
+        put(early, FF + block * hid, low(mm(glat2_t, att_s[:, here])), lane, OWNER)
         return 0
 
     lax.fori_loop(0, cols, step, 0)
@@ -482,30 +554,23 @@
     a = sc[0]
     hid = D // cols
     shut = closed[...] > 0.5
-    left = lax.broadcasted_iota(jnp.int32, (1, PAIR), 1) < HD
 
     def attend(pair, _):
         at = lanes(pair * PAIR, PAIR)
-        qp, kp, vp, gp = q[:, at], k[:, at], v[:, at], gatt[:, at]
+        kp = k[:, at]
         k_t = low(kp.astype(F32).T)
-        by_q, by_k, by_v = [], [], []
-        for h in range(2):
-            mine = left == (h == 0)
-            zero = jnp.zeros_like(qp)
-            s = jnp.where(shut, -1e30, mm(kp, jnp.where(mine, qp, zero), NT))
-            soft = jnp.exp(s - lse[pair, h : h + 1, :])
-            grad_soft = mm(vp, jnp.where(mine, gp, zero), NT)
-            total = jnp.sum(grad_soft * soft, axis=0, keepdims=True)
-            grad_scores = low(soft * (grad_soft - total))
-            by_v.append(mm(low(soft), gp))
-            by_k.append(mm(grad_scores, qp))
-            by_q.append(mm(k_t[h * HD : (h + 1) * HD], grad_scores))
-        gq[:, at] = low(jnp.concatenate(by_q, axis=0).T * 0.125)
-        gk[:, at] = low(jnp.where(left, by_k[0], by_k[1]))
-        gv[:, at] = low(jnp.where(left, by_v[0], by_v[1]))
+        q_both, g_both = both_heads(q[:, at]), both_heads(gatt[:, at])
+        s = jnp.where(shut, -1e30, mm(kp, q_both, NT))
+        soft = jnp.exp(s - lse[pair])
+        grad_soft = mm(v[:, at], g_both, NT)
+        total = jnp.sum(grad_soft * soft, axis=0, keepdims=True)
+        grad_scores = low(soft * (grad_soft - total))
+        gq[:, at] = own_heads(mm(k_t, grad_scores), 0.125)
+        gk[:, at] = low(mm(grad_scores, q_both))
+        gv[:, at] = low(mm(low(soft), g_both))
         return 0
 
-    lax.fori_loop(0, H // 2, attend, 0)
+    lax.fori_loop(0, H // 2, attend, 0, unroll=4)
     lat1_t = low(lat1[...].astype(F32).T)
 
     def step(slot, acc):
@@ -528,25 +593,33 @@
     pieces = refs[1:9]
     xa, gain, gq, gk, gv, glat1, q_down, gmid, layer = refs[9:18]
     out = refs[18]
-    w, sems, acc = refs[19:]
+    w, sems, acc, xs, row_qd, gmid_s, sems_f = refs[19:]
+    first = fetch(
+        sems_f,
+        (rows_at(xa, 0, SEQ), xs),
+        (q_down.at[sc[0]], row_qd),
+        (gmid, gmid_s),
+        (layer, rows_at(out, 0, SEQ)),
+    )
     weights = Weights(sc, pieces, w, sems, lead)
     weights.start()
     hid = D // cols
-    acc[...] = mm(glat1[...], q_down[sc[0]])
-    x = tokens_of(xa, cols)
+    for copy in first:
+        copy.wait()
+    acc[...] = mm(glat1[...], row_qd[...])
+    x = across(xs, cols)
     unit, inverse = norm_parts(x)
-    weights.wait()
-
-    def step(slot, _):
+
+    def step(i, _):
+        slot = weights.slot(i, cols)
         here = lanes(slot * hid, hid)
         grad = jnp.concatenate([gq[:, here], gk[:, here], gv[:, here]], axis=1)
         acc[...] += mm(grad, w[slot, :, : 3 * hid], NT)
         return 0
 
     lax.fori_loop(0, cols, step, 0)
-    made = low(gmid[...] + norm_back(acc[...], gain[0:1], unit, inverse))
+    made = low(gmid_s[...] + norm_back(acc[...], gain[0:1], unit, inverse))
     for c in range(cols):
-        out[c, :SEQ] = layer[c]
         out[c, SEQ:] = made[:, c * hid : (c + 1) * hid]
 
 
@@ -644,7 +717,7 @@
             + [VMEM(x, F32) for x in shapes]
             + [arrivals, pltpu.SemaphoreType.DMA((len(shapes),))],
             pl.ANY,
-            56,
+            SPREAD,
         )
     whole = call(
         functools.partial(place_kernel, lead, cols),
@@ -702,17 +775,16 @@
     lead = lead_table(rows, cols)
 
     shard = jax.ShapeDtypeStruct((blk, n), BF)
-    shard_q = call(prep_q_kernel, shard, [w_qkv, w_proj], [VMEM] * 2, mib=56)
+    rows_in, shard_q = call(
+        prep_q_kernel,
+        [jax.ShapeDtypeStruct((cols, 2 * SEQ + EXTRA, hid), BF), shard],
+        [tokens_in.reshape(cols, SEQ, hid), grad_out.reshape(cols, SEQ, hid), bias_qv]
+        + [bias_fc1.reshape(1, n), w_qkv, w_proj],
+        [VMEM] * 6,
+        mib=56,
+    )
     with jax.named_scope("q_high"):
         own_q, came_q = gather_high(shard_q)
-    rows_in = call(
-        prep_rows_kernel,
-        jax.ShapeDtypeStruct((cols, 2 * SEQ + EXTRA, hid), BF),
-        [after(tokens_in, shard_q).reshape(cols, SEQ, hid), grad_out.reshape(cols, SEQ, hid), bias_qv]
-        + [bias_fc1.reshape(4, hid)],
-        [VMEM] * 4,
-        mib=56,
-    )
     xa = lax.all_to_all(rows_in, "col", split_axis=0, concat_axis=0, tiled=True)
     adapter = lax.dynamic_index_in_dim(adapter_index, column, 0, keepdims=False)
     sc = jnp.stack([adapter, column, column % 2, row % 2]).astype(jnp.int32)
@@ -738,7 +810,7 @@
         both_q = swap(one_q, flip_two)
     with jax.named_scope("q_core"):
         away_q = [swap(p, flip_core) for p in (own_q, one_q, two_q)]
-    both_q, own_a, shard_b = after_all((both_q, own_a, shard_b), *away_q)
+    own_a, shard_b = after_all((own_a, shard_b), *away_q)
     with jax.named_scope("q_core"):
         pieces_q = [own_q, one_q, two_q, both_q] + away_q + [swap(both_q, flip_core)]
     with jax.named_scope("fa_one"):
@@ -753,6 +825,7 @@
 
     big, small = shaped(D, BF), shaped(R, BF)
     scratch = weight_scratch(rows, cols, n)
+    rows_space, bias_space = VMEM((cols, SEQ, hid), BF), VMEM((cols, EXTRA, hid), BF)
     any_space = [pl.ANY] * 8
     n1, lat1, q, k, v, lse, att, lat2, middle, n2, lat3 = call(
         functools.partial(front_kernel, lead, cols),
@@ -762,7 +835,7 @@
             big,
             big,
             big,
-            jax.ShapeDtypeStruct((H // 2, 2, SEQ), F32),
+            jax.ShapeDtypeStruct((H // 2, 1, 2 * SEQ), F32),
             big,
             small,
             shaped(D, F32),
@@ -772,8 +845,11 @@
         [sc, *pieces_q, xa, closed, ln_gain, ln_shift, qkv_down, up_qkv, proj_down]
         + [proj_up]
         + [fc1_down, bias_out],
-        [pltpu.SMEM] + any_space + [VMEM] * 10,
-        scratch + [VMEM((SEQ, D), F32), VMEM((SEQ, D), F32)],
+        [pltpu.SMEM] + any_space + [pl.ANY] + [VMEM] * 3 + [pl.ANY, VMEM] + [pl.ANY] * 3 + [VMEM],
+        scratch
+        + [VMEM((SEQ, D), F32), VMEM((SEQ, D), F32), rows_space, bias_space]
+        + [VMEM((R, D), BF)] * 4
+        + [pltpu.SemaphoreType.DMA((6,))],
         mib=FRONT,
     )
     own_a, one_a, two_a = after_all((own_a, one_a, two_a), n1, *came_b)
@@ -781,7 +857,7 @@
         both_a = swap(one_a, flip_two)
     with jax.named_scope("fa_core"):
         away_a = [swap(p, flip_core) for p in (own_a, one_a, two_a)]
-    both_a, own_b = after_all((both_a, own_b), *away_a)
+    own_b = after(own_b, *away_a)
     with jax.named_scope("fa_core"):
         pieces_a = [own_a, one_a, two_a, both_a] + away_a + [swap(both_a, flip_core)]
     with jax.named_scope("fb_one"):
@@ -794,8 +870,10 @@
         functools.partial(ffn_a_kernel, lead, cols),
         [wide, wide, thin, thin, big, jax.ShapeDtypeStruct((rows * cols, R, FF // (rows * cols)), BF)],
         [sc, *pieces_a, xa, keep, n2, lat3, fc1_up, fc2_down, fc2_up],
-        [pltpu.SMEM] + any_space + [VMEM] * 7,
-        scratch,
+        [pltpu.SMEM] + any_space + [pl.ANY] + [VMEM] * 3 + [pl.ANY] * 3,
+        scratch
+        + [rows_space, bias_space, VMEM((R, FF), BF), VMEM((R, FF), BF), VMEM((R, D), BF)]
+        + [pltpu.SemaphoreType.DMA((5,))],
         mib=FFN_A,
     )
     own_b, one_b, two_b = after_all((own_b, one_b, two_b), res)
@@ -811,10 +889,18 @@
         [sc, *pieces_b, *pieces_q, xa, keep, ln_gain, n2, lat3, fc1_up, fc2_down, fc2_up]
         + [fc1_down, proj_down, proj_up, bias_out]
         + [middle, att, lat2, gr, res, gn2, lat4, glat3, early_a],
-        [pltpu.SMEM] + any_space * 2 + [VMEM] * 21,
+        [pltpu.SMEM]
+        + any_space * 2
+        + [pl.ANY, VMEM, VMEM, VMEM, VMEM]
+        + [pl.ANY] * 6
+        + [VMEM, pl.ANY, pl.ANY, VMEM, VMEM, pl.ANY, pl.ANY, VMEM, VMEM, pl.ANY],
         scratch
         + [VMEM((cols, D, hid), BF), scratch[1]]
-        + [VMEM((SEQ, D), F32), VMEM((SEQ, D), F32), VMEM((SEQ, R), F32), VMEM((SEQ, R), F32)],
+        + [VMEM((SEQ, D), F32), VMEM((SEQ, D), F32), VMEM((SEQ, R), F32), VMEM((SEQ, R), F32)]
+        + [bias_space, VMEM((R, FF), BF), VMEM((R, FF), BF)]
+        + [VMEM((R, D), BF)] * 4
+        + [VMEM((SEQ, D), F32), VMEM((SEQ, D), BF), VMEM((SEQ, D), F32), VMEM((SEQ, D), F32)]
+        + [VMEM(early_a.shape, BF), pltpu.SemaphoreType.DMA((12,))],
         mib=FFN_B,
     )
     with jax.named_scope("grads_b_send"):
@@ -838,13 +924,16 @@
         functools.partial(back_kernel, lead, cols),
         jax.ShapeDtypeStruct((cols, 2 * SEQ, hid), BF),
         [sc, *pieces_q, xa, ln_gain, gq, gk, gv, glat1, qkv_down, gmid, layer],
-        [pltpu.SMEM] + any_space + [VMEM] * 9,
-        scratch + [VMEM((SEQ, D), F32)],
+        [pltpu.SMEM] + any_space + [pl.ANY] + [VMEM] * 5 + [pl.ANY] * 3,
+        scratch
+        + [VMEM((SEQ, D), F32), rows_space, VMEM((R, D), BF), VMEM((SEQ, D), F32)]
+        + [pltpu.SemaphoreType.DMA((4,))],
         mib=BACK,
     )
     with jax.named_scope("grads"):
         one, two = swap(own, flip_one), swap(own, flip_two)
-        both = swap(after(one, two, sent), flip_two)
+        own, one, two = after_all((own, one, two), sent)
+        both = swap(one, flip_two)
         pieces = with_cores([own, one, two, both])
         half = FF // cols // 2
         map_a, map_b = (
@@ -862,7 +951,7 @@
         sums = spread(sc, pieces, parts, [map_a, map_b, map_c], shapes)
 
     with jax.named_scope("rows_out"):
-        sent = after(sent, both)
+        sent = after(sent, pieces[4])
         rows_out = lax.all_to_all(sent, "col", split_axis=0, concat_axis=0, tiled=True)
     layer, grad_in = rows_out[:, :SEQ], rows_out[:, SEQ:]
 

time: 279 us -> 265 us (0.950)
  Pallas kernels: 96.2 us -> 87.3 us
  waiting for transfers between devices: 112 us -> 106 us
    pallas_call x17 -> x16, Pallas kernels: 96.2 us -> 87.3 us  [call(): pl.pallas_call(kernel, out_shape=outs, in_specs=[pl.BlockSpec(memory_spac...]
    ppermute x43, waiting for transfers between devices: 103 us -> 95.9 us  [swap(): return lax.ppermute(block, BOTH, pairs)]
  transfers between devices with their start and end apart: 47 -> 47, of which waited for: 25 -> 21; matrix products, arithmetic and copies ran while one was open for 1% -> 1% of each run, Pallas kernels for 25% -> 25%
where the time goes in v6:
time: 265 us; the launch traced here: 264 us
  waiting for transfers between devices  106 us (40%)
  Pallas kernels  87.3 us (33%)
  starting transfers between devices  56.4 us (21%)
  local copies, waits for them, and re-layouts  9.06 us (3%)
  between operations  3.18 us (1%)
    ppermute x43, waiting for transfers between devices, swap(): return lax.ppermute(block, BOTH, pairs)  95.9 us
    pallas_call x16, Pallas kernels, call(): pl.pallas_call(kernel, out_shape=outs, in_specs=[pl.BlockSpec(memory_spac...  87.3 us
    ppermute x43, starting transfers between devices, swap(): return lax.ppermute(block, BOTH, pairs)  41.8 us
    all_to_all x2, waiting for transfers between devices, send_grads(): return lax.all_to_all(grads, BOTH, split_axis=0, concat_axis=0, tiled=True)  7.03 us
    all_to_all x2, starting transfers between devices, send_grads(): return lax.all_to_all(grads, BOTH, split_axis=0, concat_axis=0, tiled=True)  6.66 us
    unnamed x74, local copies, waits for them, and re-layouts  5.35 us
  transfers between devices with their start and end apart: 47, of which 21 were waited for; matrix products, arithmetic and copies ran while one was open for 1% of the time, Pallas kernels for 25%

profile of v6, /device:TPU:0, one launch (start us, length us, event | category | flops | bytes accessed | tf_op | source)
XLA Modules:
  0.0 263.9 jit_solution(14173393728884338039)
XLA Ops:
  0.7 1.4 reshape.74.bias_f
  2.0 2.6 shard_map.276
  4.6 4.4 %all-to-all-start = ((bf16[4,656,256]{2,1,0:T(8,128)(2,1)}), bf16[4,656,256]{2,1,0:T(8,128)(2,1)}, u32[]{:S(2)}, u32[]{:S(2)}) async-start(bf16[4,656,256]{2,1,0:T(8,128)(2,1)} %get-tuple-element.74), calls=%async_computation | async-start | bytes 2686976 | tf_op jit(solution)/shard_map/all_to_all | solution.py:788
  9.1 5.1 %collective-permute-start.2 = (bf16[128,1024]{1,0:T(8,128)(2,1)S(1)}, bf16[128,1024]{1,0:T(8,128)(2,1)S(1)}, u32[]{:S(2)}, u32[]{:S(2)}) collective-permute-start(bf16[128,1024]{1,0:T(8,128)(2,1)S(1)} %copy-done.8), channel_id=1, source_target_pairs={{0,24},{1,25},{2,26},{3,27},{4,28},{5,29},{6,30},{7,31},{8,16},{9,... | collective-permute-start | bytes 786440 | tf_op jit(solution)/shard_map/q_high/ppermute | solution.py:76
  14.2 0.6 collective-permute-start
  17.4 0.7 pad_add_fusion.sc.refs_0_
  18.2 0.8 shard_map.277
  19.0 0.7 copy-done.6
  19.7 0.7 copy-done.7
  20.3 0.6 dynamic-slice_bitcast_fusion.refs_14_.refs_9_
  21.5 15.6 %collective-permute-done.1.refs_2_ = bf16[128,1024]{1,0:T(8,128)(2,1)S(1)} collective-permute-done((bf16[128,1024]{1,0:T(8,128)(2,1)S(1)}, bf16[128,1024]{1,0:T(8,128)(2,1)S(1)}, u32[]{:S(2)}, u32[]{:S(2)}) %collective-permute-start.1) | collective-permute-done | bytes 262176 | tf_op jit(solution)/shard_map/q_high/ppermute | solution.py:76
  37.2 1.6 collective-permute-start.4
  38.8 1.7 collective-permute-start.3
  40.5 2.5 collective-permute-start.7
  43.0 1.9 collective-permute-start.5
  44.9 6.8 %collective-permute-done.7.refs_3_ = bf16[128,1024]{1,0:T(8,128)(2,1)S(1)} collective-permute-done((bf16[128,1024]{1,0:T(8,128)(2,1)S(1)}, bf16[128,1024]{1,0:T(8,128)(2,1)S(1)}, u32[]{:S(2)}, u32[]{:S(2)}) %collective-permute-start.7) | collective-permute-done | bytes 262176 | tf_op jit(solution)/shard_map/fa_high/ppermute | solution.py:76
  51.6 11.8 %collective-permute-done.6.refs_2_ = bf16[128,1024]{1,0:T(8,128)(2,1)S(1)} collective-permute-done((bf16[128,1024]{1,0:T(8,128)(2,1)S(1)}, bf16[128,1024]{1,0:T(8,128)(2,1)S(1)}, u32[]{:S(2)}, u32[]{:S(2)}) %collective-permute-start.6) | collective-permute-done | bytes 262176 | tf_op jit(solution)/shard_map/fa_high/ppermute | solution.py:76
  63.4 1.2 collective-permute-start.8
  65.2 13.1 %collective-permute-done.8.refs_4_.refs_12_ = bf16[4,128,1024]{2,1,0:T(8,128)(2,1)S(1)} collective-permute-done((bf16[4,128,1024]{2,1,0:T(8,128)(2,1)S(1)}, bf16[4,128,1024]{2,1,0:T(8,128)(2,1)S(1)}, u32[]{:S(2)}, u32[]{:S(2)}) %collective-permute-start.8) | collective-permute-done | bytes 1048608 | tf_op jit(solution)/shard_map/q_both/ppermute | solution.py:76
  78.5 1.2 collective-permute-start.17
  80.3 2.5 collective-permute-start.15
  82.9 1.0 copy-done.19
  83.9 1.9 collective-permute-start.13
  85.8 18.0 %shard_map.278 = (bf16[320,1024]{1,0:T(8,128)(2,1)}, bf16[320,16]{1,0:T(8,128)(2,1)}, bf16[320,1024]{1,0:T(8,128)(2,1)}, bf16[320,1024]{1,0:T(8,128)(2,1)}, bf16...) custom-call(s32[4]{0:T(128)} %copy-done.11, ...), custom_call_target="tpu_custom_call" | custom-call | tf_op jit(solution)/shard_map/pallas_call | solution.py:55
  103.8 0.7 collective-permute-done.14.refs_2_
  104.6 1.2 collective-permute-start.23
  106.4 13.2 %collective-permute-done.23.refs_4_ = bf16[4,128,1024]{2,1,0:T(8,128)(2,1)S(1)} collective-permute-done((bf16[4,128,1024]{2,1,0:T(8,128)(2,1)}, bf16[4,128,1024]{2,1,0:T(8,128)(2,1)S(1)}, u32[]{:S(2)}, u32[]{:S(2)}) %collective-permute-start.23) | collective-permute-done | bytes 1048608 | tf_op jit(solution)/shard_map/fa_both/ppermute | solution.py:76
  119.6 1.2 collective-permute-start.22
  120.9 0.7 collective-permute-start.21
  121.6 0.7 collective-permute-done.24.refs_8_
  122.2 1.0 copy-done.30
  123.3 15.4 %shard_map.279 = (f32[320,1024]{1,0:T(8,128)}, f32[320,1024]{1,0:T(8,128)}, f32[320,16]{1,0:T(8,128)}, f32[320,16]{1,0:T(8,128)}, bf16[320,1024]{1,0:T(8,128)(2,1)}, /*index=5*/bf16[32,16,128]{2,1,0:T(8,128)(2,1)}) custom-call(s32[4]{0:T(128)} %copy-done.11, bf16[4,128,1024]{2,1,0:T(8,128)(2,1)} %copy-done.3, ...), custom_call_target="tpu_custom_call" | custom-call | tf_op jit(solution)/shard_map/pallas_call | solution.py:55
  138.7 6.5 %collective-permute-done.22.refs_3_ = bf16[4,128,1024]{2,1,0:T(8,128)(2,1)S(1)} collective-permute-done((bf16[4,128,1024]{2,1,0:T(8,128)(2,1)S(1)}, bf16[4,128,1024]{2,1,0:T(8,128)(2,1)S(1)}, u32[]{:S(2)}, u32[]{:S(2)}) %collective-permute-start.22) | collective-permute-done | bytes 1048608 | tf_op jit(solution)/shard_map/fb_two/ppermute | solution.py:76
  145.3 1.7 collective-permute-start.25
  147.4 12.6 %collective-permute-done.25.refs_4_ = bf16[4,128,1024]{2,1,0:T(8,128)(2,1)S(1)} collective-permute-done((bf16[4,128,1024]{2,1,0:T(8,128)(2,1)S(1)}, bf16[4,128,1024]{2,1,0:T(8,128)(2,1)S(1)}, u32[]{:S(2)}, u32[]{:S(2)}) %collective-permute-start.25) | collective-permute-done | bytes 1048608 | tf_op jit(solution)/shard_map/fb_both/ppermute | solution.py:76
  160.1 2.6 collective-permute-done.29.refs_8_
  162.7 1.0 copy-done.29
  163.8 19.2 %shard_map.280 = (bf16[4,320,256]{2,1,0:T(8,128)(2,1)}, bf16[320,1024]{1,0:T(8,128)(2,1)}, f32[320,1024]{1,0:T(8,128)}, bf16[32,16,512]{2,1,0:T(8,128)(2,1)}) custom-call(s32[4]{0:T(128)} %copy-done.11, bf16[4,128,1024]{2,1,0:T(8,128)(2,1)} %copy-done.4, bf16[4,128,1024]{2,1,0:T(8,128)(2,1)} %copy-done.21, bf16[4,128,1024]{2,1,0:T(8,128)(2,1)} %copy-done.20, ...), custom_call_target="tpu_custom_call" | custom-call | tf_op jit(solution)/shard_map/pallas_call | solution.py:55
  183.0 3.6 %all-to-all-start.1 = ((bf16[32,16,512]{2,1,0:T(8,128)(2,1)}), bf16[32,16,512]{2,1,0:T(8,128)(2,1)S(1)}, u32[]{:S(2)}, u32[]{:S(2)}) async-start(bf16[32,16,512]{2,1,0:T(8,128)(2,1)} %get-tuple-element.115), calls=%async_computation.1 | async-start | bytes 1048576 | tf_op jit(solution)/shard_map/grads_b_send/all_to_all | solution.py:689
  186.6 10.8 %shard_map.281 = (bf16[320,1024]{1,0:T(8,128)(2,1)}, bf16[320,1024]{1,0:T(8,128)(2,1)}, bf16[320,1024]{1,0:T(8,128)(2,1)}, bf16[320,16]{1,0:T(8,128)(2,1)}, bf16[32,16,128]{2,1,0:T(8,128)(2,1)}) custom-call(s32[4]{0:T(128)} %copy-done.11, f32[320,1]{1,0:T(8,128)} %copy-done.7, bf16[320,1024]{1,0:T(8,128)(2,1)} %get-tuple-element.82.refs_2_, ...), custom_call_target="tpu_custom_call" | custom-call | tf_op jit(solution)/shard_map/pallas_call | solution.py:55
  197.4 4.7 %all-to-all-done.1.mine = bf16[32,16,512]{2,1,0:T(8,128)(2,1)S(1)} async-done(((bf16[32,16,512]{2,1,0:T(8,128)(2,1)}), bf16[32,16,512]{2,1,0:T(8,128)(2,1)S(1)}, u32[]{:S(2)}, u32[]{:S(2)}) %all-to-all-start.1) | async-done | bytes 524320 | tf_op jit(solution)/shard_map/grads_b_send/all_to_all | solution.py:689
  202.1 3.1 %all-to-all-start.2 = ((bf16[32,16,128]{2,1,0:T(8,128)(2,1)}), bf16[32,16,128]{2,1,0:T(8,128)(2,1)S(1)}, u32[]{:S(2)}, u32[]{:S(2)}) async-start(bf16[32,16,128]{2,1,0:T(8,128)(2,1)} %get-tuple-element.116), calls=%async_computation.2 | async-start | bytes 262144 | tf_op jit(solution)/shard_map/grads_c_send/all_to_all | solution.py:689
  205.2 0.7 fusion.owners
  205.9 0.7 grads_b.5
  206.7 3.7 %collective-permute-start.32 = (bf16[128,384]{1,0:T(8,128)(2,1)S(1)}, bf16[128,384]{1,0:T(8,128)(2,1)S(1)}, u32[]{:S(2)}, u32[]{:S(2)}) collective-permute-start(bf16[128,384]{1,0:T(8,128)(2,1)S(1)} %bitcast.23), channel_id=1, source_target_pairs={{0,24},{1,25},{2,26},{3,27},{4,28},{5,29},{6,30},{7,31},{8,16},{9,... | collective-permute-start | bytes 294920 | tf_op jit(solution)/shard_map/grads_b/ppermute | solution.py:76
  210.4 0.8 collective-permute-start.30
  211.1 2.3 all-to-all-done.2.mine
  213.4 0.7 grads_b.7
  214.1 1.4 collective-permute-start.35
  215.5 0.9 collective-permute-start.34
  216.4 3.9 %collective-permute-done.35.refs_3_ = bf16[128,128]{1,0:T(8,128)(2,1)S(1)} collective-permute-done((bf16[128,128]{1,0:T(8,128)(2,1)S(1)}, bf16[128,128]{1,0:T(8,128)(2,1)S(1)}, u32[]{:S(2)}, u32[]{:S(2)}) %collective-permute-start.35) | collective-permute-done | bytes 32800 | tf_op jit(solution)/shard_map/grads_b/ppermute | solution.py:76
  220.3 2.7 %collective-permute-start.33 = (bf16[128,128]{1,0:T(8,128)(2,1)S(1)}, bf16[128,128]{1,0:T(8,128)(2,1)S(1)}, u32[]{:S(2)}, u32[]{:S(2)}) collective-permute-start(bf16[128,128]{1,0:T(8,128)(2,1)S(1)} %bitcast.29), channel_id=1, source_target_pairs={{0,8},{1,9},{2,10},{3,11},{4,12},{5,13},{6,14},{7,15},{8,0},{9,1},... | collective-permute-start | bytes 98312 | tf_op jit(solution)/shard_map/grads_b/ppermute | solution.py:76
  223.0 1.9 collective-permute-done.33.refs_1_
  225.8 1.6 collective-permute-start.37
  227.3 1.5 collective-permute-start.36
  228.8 11.0 %shard_map.282 = bf16[4,640,256]{2,1,0:T(8,128)(2,1)} custom-call(s32[4]{0:T(128)} %copy-done.11, bf16[4,128,1024]{2,1,0:T(8,128)(2,1)} %copy-done.2, bf16[4,128,1024]{2,1,0:T(8,128)(2,1)} %copy-done.14, bf16[4,128,1024]{2,1,0:T(8,128)(2,1)} %copy-done.13, bf16[4,128,1024]{2,1,0:T(8,128)(2,1)} %copy-done.15, bf16[4,128,1024]{2,1,0:T(8,128)(2,1)} %copy-done.16, ...), custom_call_target="tpu_custom_call" | custom-call | tf_op jit(solution)/shard_map/pallas_call | solution.py:55
  239.9 1.5 collective-permute-start.39
  242.0 3.5 %all-to-all-start.3 = ((bf16[4,640,256]{2,1,0:T(8,128)(2,1)}), bf16[4,640,256]{2,1,0:T(8,128)(2,1)S(1)}, u32[]{:S(2)}, u32[]{:S(2)}) async-start(bf16[4,640,256]{2,1,0:T(8,128)(2,1)} %shard_map.282), calls=%async_computation.3 | async-start | bytes 2621440 | tf_op jit(solution)/shard_map/rows_out/all_to_all | solution.py:955
  246.1 3.2 %collective-permute-done.39.refs_4_ = bf16[4,128,512]{2,1,0:T(8,128)(2,1)} collective-permute-done((bf16[4,128,512]{2,1,0:T(8,128)(2,1)S(1)}, bf16[4,128,512]{2,1,0:T(8,128)(2,1)}, u32[]{:S(2)}, u32[]{:S(2)}) %collective-permute-start.39) | collective-permute-done | bytes 524320 | tf_op jit(solution)/shard_map/grads/ppermute | solution.py:76
  249.3 2.1 collective-permute-done.42.refs_8_
  251.4 0.8 copy-done.35
  252.2 6.9 %grads.1 = (f32[128,4096]{1,0:T(8,128)}, f32[128,4096]{1,0:T(8,128)}, f32[128,1024]{1,0:T(8,128)}, f32[128,1024]{1,0:T(8,128)}, f32[128,1024]{1,0:T(8,128)}, /*i...) custom-call(s32[4]{0:T(128)} %copy-done.11, bf16[4,128,512]{2,1,0:T(8,128)(2,1)} %copy-done.5, ...), custom_call_target="tpu_custom_call" | custom-call | tf_op jit(solution)/shard_map/grads/pallas_call | solution.py:55
  259.2 3.6 %all-to-all-done.3 = bf16[4,640,256]{2,1,0:T(8,128)(2,1)S(1)} async-done(((bf16[4,640,256]{2,1,0:T(8,128)(2,1)}), bf16[4,640,256]{2,1,0:T(8,128)(2,1)S(1)}, u32[]{:S(2)}, u32[]{:S(2)}) %all-to-all-start.3) | async-done | bytes 1310752 | tf_op jit(solution)/shard_map/rows_out/all_to_all | solution.py:955
  262.8 1.1 fusion.1
  (126 shorter events, 6.1 us)
Async XLA Ops:
  0.6 19.7 %copy-start = (bf16[8,16,3,1024]{3,1,2,0:T(8,128)(2,1)S(1)}, bf16[8,16,3,1024]{3,1,2,0:T(8,128)(2,1)}, u32[]{:S(2)}) copy-start(bf16[8,16,3,1024]{3,1,2,0:T(8,128)(2,1)} %param.35) | copy-start | bytes 2359300
  4.6 10.2 %copy-start.36 = (s32[4]{0:T(128)S(1)}, s32[4]{0:T(128)}, u32[]{:S(2)}) copy-start(s32[4]{0:T(128)} %param.24) | copy-start | bytes 52
  4.6 13.5 %copy-start.9 = (bf16[128,1024]{1,0:T(8,128)(2,1)S(1)}, bf16[128,1024]{1,0:T(8,128)(2,1)}, u32[]{:S(2)}) copy-start(bf16[128,1024]{1,0:T(8,128)(2,1)} %w1.1) | copy-start | bytes 786436
  4.6 13.5 %copy-start.10 = (bf16[1024,128]{1,0:T(8,128)(2,1)S(1)}, bf16[1024,128]{1,0:T(8,128)(2,1)}, u32[]{:S(2)}) copy-start(bf16[1024,128]{1,0:T(8,128)(2,1)} %w2.1) | copy-start | bytes 786436
  4.6 13.5 %copy-start.12 = (s32[4,256]{1,0:T(4,128)S(1)}, s32[4,256]{1,0:T(4,128)}, u32[]{:S(2)}) copy-start(s32[4,256]{1,0:T(4,128)} %mask.1) | copy-start | bytes 12292
  4.6 32.6 %all-to-all-start = ((bf16[4,656,256]{2,1,0:T(8,128)(2,1)}), bf16[4,656,256]{2,1,0:T(8,128)(2,1)}, u32[]{:S(2)}, u32[]{:S(2)}) async-start(bf16[4,656,256]{2,1,0:T(8,128)(2,1)} %get-tuple-element.74), calls=%async_computation | async-start | bytes 2686976 | tf_op jit(solution)/shard_map/all_to_all | solution.py:788
  9.1 12.4 %collective-permute-start.2 = (bf16[128,1024]{1,0:T(8,128)(2,1)S(1)}, bf16[128,1024]{1,0:T(8,128)(2,1)S(1)}, u32[]{:S(2)}, u32[]{:S(2)}) collective-permute-start(bf16[128,1024]{1,0:T(8,128)(2,1)S(1)} %copy-done.8), channel_id=1, source_target_pairs={{0,24},{1,25},{2,26},{3,27},{4,28},{5,29},{6,30},{7,31},{8,16},{9,... | collective-permute-start | bytes 786440 | tf_op jit(solution)/shard_map/q_high/ppermute | solution.py:76
  14.2 22.8 %collective-permute-start.1 = (bf16[128,1024]{1,0:T(8,128)(2,1)S(1)}, bf16[128,1024]{1,0:T(8,128)(2,1)S(1)}, u32[]{:S(2)}, u32[]{:S(2)}) collective-permute-start(bf16[128,1024]{1,0:T(8,128)(2,1)S(1)} %copy-done.8), channel_id=1, source_target_pairs={{0,16},{1,17},{2,18},{3,19},{4,20},{5,21},{6,22},{7,23},{8,24},{9,... | collective-permute-start | bytes 786440 | tf_op jit(solution)/shard_map/q_high/ppermute | solution.py:76
  14.2 22.8 %collective-permute-start = (bf16[128,1024]{1,0:T(8,128)(2,1)S(1)}, bf16[128,1024]{1,0:T(8,128)(2,1)S(1)}, u32[]{:S(2)}, u32[]{:S(2)}) collective-permute-start(bf16[128,1024]{1,0:T(8,128)(2,1)S(1)} %copy-done.8), channel_id=1, source_target_pairs={{0,8},{1,9},{2,10},{3,11},{4,12},{5,13},{6,14},{7,15},{8,0},{9,1},... | collective-permute-start | bytes 786440 | tf_op jit(solution)/shard_map/q_high/ppermute | solution.py:76
  18.1 19.1 %copy-start.11 = (s32[4]{0:T(128)}, s32[4]{0:T(128)S(1)}, u32[]{:S(2)}) copy-start(s32[4]{0:T(128)S(1)} %pad_add_fusion.sc.refs_0_) | copy-start | bytes 52
  37.2 48.6 %copy-start.2 = (bf16[4,128,1024]{2,1,0:T(8,128)(2,1)}, bf16[4,128,1024]{2,1,0:T(8,128)(2,1)S(1)}, u32[]{:S(2)}) copy-start(bf16[4,128,1024]{2,1,0:T(8,128)(2,1)S(1)} %q_high.1.refs_1_.refs_9_) | copy-start | bytes 3145732
  37.2 26.2 %collective-permute-start.4 = (bf16[4,128,1024]{2,1,0:T(8,128)(2,1)S(1)}, bf16[4,128,1024]{2,1,0:T(8,128)(2,1)S(1)}, u32[]{:S(2)}, u32[]{:S(2)}) collective-permute-start(bf16[4,128,1024]{2,1,0:T(8,128)(2,1)S(1)} %q_high.1.refs_1_.refs_9_), channel_id=1, source_target_pairs={{0,4},{1,3},{2,6},{3,1},{4,0},{5,7},{6,2},{7,5},{8,12},{9,11},{10,... | collective-permute-start | bytes 3145736 | tf_op jit(solution)/shard_map/q_two/ppermute | solution.py:76
  38.8 24.6 %collective-permute-start.3 = (bf16[4,128,1024]{2,1,0:T(8,128)(2,1)S(1)}, bf16[4,128,1024]{2,1,0:T(8,128)(2,1)S(1)}, u32[]{:S(2)}, u32[]{:S(2)}) collective-permute-start(bf16[4,128,1024]{2,1,0:T(8,128)(2,1)S(1)} %q_high.1.refs_1_.refs_9_), channel_id=1, source_target_pairs={{0,2},{1,5},{2,0},{3,7},{4,6},{5,1},{6,4},{7,3},{8,10},{9,13},{10,... | collective-permute-start | bytes 3145736 | tf_op jit(solution)/shard_map/q_one/ppermute | solution.py:76
  40.5 11.1 %collective-permute-start.7 = (bf16[128,1024]{1,0:T(8,128)(2,1)S(1)}, bf16[128,1024]{1,0:T(8,128)(2,1)S(1)}, u32[]{:S(2)}, u32[]{:S(2)}) collective-permute-start(bf16[128,1024]{1,0:T(8,128)(2,1)S(1)} %get-tuple-element.78.refs_0_), channel_id=1, source_target_pairs={{0,24},{1,25},{2,26},{3,27},{4,28},{5,29},{6,30},{7,31},{8,16},{9,... | collective-permute-start | bytes 786440 | tf_op jit(solution)/shard_map/fa_high/ppermute | solution.py:76
  43.0 20.4 %collective-permute-start.6 = (bf16[128,1024]{1,0:T(8,128)(2,1)S(1)}, bf16[128,1024]{1,0:T(8,128)(2,1)S(1)}, u32[]{:S(2)}, u32[]{:S(2)}) collective-permute-start(bf16[128,1024]{1,0:T(8,128)(2,1)S(1)} %get-tuple-element.78.refs_0_), channel_id=1, source_target_pairs={{0,16},{1,17},{2,18},{3,19},{4,20},{5,21},{6,22},{7,23},{8,24},{9,... | collective-permute-start | bytes 786440 | tf_op jit(solution)/shard_map/fa_high/ppermute | solution.py:76
  43.0 20.4 %collective-permute-start.5 = (bf16[128,1024]{1,0:T(8,128)(2,1)S(1)}, bf16[128,1024]{1,0:T(8,128)(2,1)S(1)}, u32[]{:S(2)}, u32[]{:S(2)}) collective-permute-start(bf16[128,1024]{1,0:T(8,128)(2,1)S(1)} %get-tuple-element.78.refs_0_), channel_id=1, source_target_pairs={{0,8},{1,9},{2,10},{3,11},{4,12},{5,13},{6,14},{7,15},{8,0},{9,1},... | collective-permute-start | bytes 786440 | tf_op jit(solution)/shard_map/fa_high/ppermute | solution.py:76
  63.4 22.4 %copy-start.13 = (bf16[4,128,1024]{2,1,0:T(8,128)(2,1)}, bf16[4,128,1024]{2,1,0:T(8,128)(2,1)S(1)}, u32[]{:S(2)}) copy-start(bf16[4,128,1024]{2,1,0:T(8,128)(2,1)S(1)} %collective-permute-done.4.refs_3_.refs_11_) | copy-start | bytes 3145732
  63.4 22.4 %copy-start.14 = (bf16[4,128,1024]{2,1,0:T(8,128)(2,1)}, bf16[4,128,1024]{2,1,0:T(8,128)(2,1)S(1)}, u32[]{:S(2)}) copy-start(bf16[4,128,1024]{2,1,0:T(8,128)(2,1)S(1)} %collective-permute-done.3.refs_2_.refs_10_) | copy-start | bytes 3145732
  63.4 14.9 %collective-permute-start.8 = (bf16[4,128,1024]{2,1,0:T(8,128)(2,1)S(1)}, bf16[4,128,1024]{2,1,0:T(8,128)(2,1)S(1)}, u32[]{:S(2)}, u32[]{:S(2)}) collective-permute-start(bf16[4,128,1024]{2,1,0:T(8,128)(2,1)S(1)} %collective-permute-done.3.refs_2_.refs_10_), channel_id=1, source_target_pairs={{0,4},{1,3},{2,6},{3,1},{4,0},{5,7},{6,2},{7,5},{8,12},{9,11},{10,... | collective-permute-start | bytes 3145736 | tf_op jit(solution)/shard_map/q_both/ppermute | solution.py:76
  64.7 13.8 %collective-permute-start.9 = (bf16[4,128,1024]{2,1,0:T(8,128)(2,1)S(1)}, bf16[4,128,1024]{2,1,0:T(8,128)(2,1)S(1)}, u32[]{:S(2)}, u32[]{:S(2)}) collective-permute-start(bf16[4,128,1024]{2,1,0:T(8,128)(2,1)S(1)} %q_high.1.refs_1_.refs_9_), channel_id=1, source_target_pairs={{0,1},{1,0},{2,3},{3,2},{4,5},{5,4},{6,7},{7,6},{8,9},{9,8},{10,11... | collective-permute-start | bytes 3145736 | tf_op jit(solution)/shard_map/q_core/ppermute | solution.py:76
  64.7 13.8 %collective-permute-start.11 = (bf16[4,128,1024]{2,1,0:T(8,128)(2,1)S(1)}, bf16[4,128,1024]{2,1,0:T(8,128)(2,1)S(1)}, u32[]{:S(2)}, u32[]{:S(2)}) collective-permute-start(bf16[4,128,1024]{2,1,0:T(8,128)(2,1)S(1)} %collective-permute-done.4.refs_3_.refs_11_), channel_id=1, source_target_pairs={{0,1},{1,0},{2,3},{3,2},{4,5},{5,4},{6,7},{7,6},{8,9},{9,8},{10,11... | collective-permute-start | bytes 3145736 | tf_op jit(solution)/shard_map/q_core/ppermute | solution.py:76
  65.2 13.3 %collective-permute-start.10 = (bf16[4,128,1024]{2,1,0:T(8,128)(2,1)S(1)}, bf16[4,128,1024]{2,1,0:T(8,128)(2,1)S(1)}, u32[]{:S(2)}, u32[]{:S(2)}) collective-permute-start(bf16[4,128,1024]{2,1,0:T(8,128)(2,1)S(1)} %collective-permute-done.3.refs_2_.refs_10_), channel_id=1, source_target_pairs={{0,1},{1,0},{2,3},{3,2},{4,5},{5,4},{6,7},{7,6},{8,9},{9,8},{10,11... | collective-permute-start | bytes 3145736 | tf_op jit(solution)/shard_map/q_core/ppermute | solution.py:76
  78.3 4.5 %collective-permute-start.12 = (bf16[4,128,1024]{2,1,0:T(8,128)(2,1)S(1)}, bf16[4,128,1024]{2,1,0:T(8,128)(2,1)S(1)}, u32[]{:S(2)}, u32[]{:S(2)}) collective-permute-start(bf16[4,128,1024]{2,1,0:T(8,128)(2,1)S(1)} %collective-permute-done.8.refs_4_.refs_12_), channel_id=1, source_target_pairs={{0,1},{1,0},{2,3},{3,2},{4,5},{5,4},{6,7},{7,6},{8,9},{9,8},{10,11... | collective-permute-start | bytes 3145736 | tf_op jit(solution)/shard_map/q_core/ppermute | solution.py:76
  78.4 27.3 %copy-start.3 = (bf16[4,128,1024]{2,1,0:T(8,128)(2,1)}, bf16[4,128,1024]{2,1,0:T(8,128)(2,1)S(1)}, u32[]{:S(2)}) copy-start(bf16[4,128,1024]{2,1,0:T(8,128)(2,1)S(1)} %fa_high.1.refs_1_) | copy-start | bytes 3145732
  78.5 26.1 %collective-permute-start.17 = (bf16[4,128,1024]{2,1,0:T(8,128)(2,1)S(1)}, bf16[4,128,1024]{2,1,0:T(8,128)(2,1)}, u32[]{:S(2)}, u32[]{:S(2)}) collective-permute-start(bf16[4,128,1024]{2,1,0:T(8,128)(2,1)S(1)} %fa_high.1.refs_1_), channel_id=1, source_target_pairs={{0,4},{1,3},{2,6},{3,1},{4,0},{5,7},{6,2},{7,5},{8,12},{9,11},{10,... | collective-permute-start | bytes 3145736 | tf_op jit(solution)/shard_map/fa_two/ppermute | solution.py:76
  79.7 24.8 %collective-permute-start.16 = (bf16[4,128,1024]{2,1,0:T(8,128)(2,1)S(1)}, bf16[4,128,1024]{2,1,0:T(8,128)(2,1)}, u32[]{:S(2)}, u32[]{:S(2)}) collective-permute-start(bf16[4,128,1024]{2,1,0:T(8,128)(2,1)S(1)} %fa_high.1.refs_1_), channel_id=1, source_target_pairs={{0,2},{1,5},{2,0},{3,7},{4,6},{5,1},{6,4},{7,3},{8,10},{9,13},{10,... | collective-permute-start | bytes 3145736 | tf_op jit(solution)/shard_map/fa_one/ppermute | solution.py:76
  80.3 23.4 %collective-permute-start.15 = (bf16[128,1024]{1,0:T(8,128)(2,1)S(1)}, bf16[128,1024]{1,0:T(8,128)(2,1)S(1)}, u32[]{:S(2)}, u32[]{:S(2)}) collective-permute-start(bf16[128,1024]{1,0:T(8,128)(2,1)S(1)} %get-tuple-element.87.refs_0_), channel_id=1, source_target_pairs={{0,24},{1,25},{2,26},{3,27},{4,28},{5,29},{6,30},{7,31},{8,16},{9,... | collective-permute-start | bytes 786440 | tf_op jit(solution)/shard_map/fb_high/ppermute | solution.py:76
  82.8 21.6 %collective-permute-start.14 = (bf16[128,1024]{1,0:T(8,128)(2,1)S(1)}, bf16[128,1024]{1,0:T(8,128)(2,1)S(1)}, u32[]{:S(2)}, u32[]{:S(2)}) collective-permute-start(bf16[128,1024]{1,0:T(8,128)(2,1)S(1)} %get-tuple-element.87.refs_0_), channel_id=1, source_target_pairs={{0,16},{1,17},{2,18},{3,19},{4,20},{5,21},{6,22},{7,23},{8,24},{9,... | collective-permute-start | bytes 786440 | tf_op jit(solution)/shard_map/fb_high/ppermute | solution.py:76
  83.9 20.5 %collective-permute-start.13 = (bf16[128,1024]{1,0:T(8,128)(2,1)S(1)}, bf16[128,1024]{1,0:T(8,128)(2,1)S(1)}, u32[]{:S(2)}, u32[]{:S(2)}) collective-permute-start(bf16[128,1024]{1,0:T(8,128)(2,1)S(1)} %get-tuple-element.87.refs_0_), channel_id=1, source_target_pairs={{0,8},{1,9},{2,10},{3,11},{4,12},{5,13},{6,14},{7,15},{8,0},{9,1},... | collective-permute-start | bytes 786440 | tf_op jit(solution)/shard_map/fb_high/ppermute | solution.py:76
  104.6 15.0 %collective-permute-start.23 = (bf16[4,128,1024]{2,1,0:T(8,128)(2,1)}, bf16[4,128,1024]{2,1,0:T(8,128)(2,1)S(1)}, u32[]{:S(2)}, u32[]{:S(2)}) collective-permute-start(bf16[4,128,1024]{2,1,0:T(8,128)(2,1)} %collective-permute-done.16.refs_2_), channel_id=1, source_target_pairs={{0,4},{1,3},{2,6},{3,1},{4,0},{5,7},{6,2},{7,5},{8,12},{9,11},{10,... | collective-permute-start | bytes 3145736 | tf_op jit(solution)/shard_map/fa_both/ppermute | solution.py:76
  105.7 13.9 %collective-permute-start.18 = (bf16[4,128,1024]{2,1,0:T(8,128)(2,1)S(1)}, bf16[4,128,1024]{2,1,0:T(8,128)(2,1)S(1)}, u32[]{:S(2)}, u32[]{:S(2)}) collective-permute-start(bf16[4,128,1024]{2,1,0:T(8,128)(2,1)S(1)} %fa_high.1.refs_1_), channel_id=1, source_target_pairs={{0,1},{1,0},{2,3},{3,2},{4,5},{5,4},{6,7},{7,6},{8,9},{9,8},{10,11... | collective-permute-start | bytes 3145736 | tf_op jit(solution)/shard_map/fa_core/ppermute | solution.py:76
  105.7 13.9 %collective-permute-start.20 = (bf16[4,128,1024]{2,1,0:T(8,128)(2,1)}, bf16[4,128,1024]{2,1,0:T(8,128)(2,1)S(1)}, u32[]{:S(2)}, u32[]{:S(2)}) collective-permute-start(bf16[4,128,1024]{2,1,0:T(8,128)(2,1)} %collective-permute-done.17.refs_3_), channel_id=1, source_target_pairs={{0,1},{1,0},{2,3},{3,2},{4,5},{5,4},{6,7},{7,6},{8,9},{9,8},{10,11... | collective-permute-start | bytes 3145736 | tf_op jit(solution)/shard_map/fa_core/ppermute | solution.py:76
  106.2 13.4 %collective-permute-start.19 = (bf16[4,128,1024]{2,1,0:T(8,128)(2,1)}, bf16[4,128,1024]{2,1,0:T(8,128)(2,1)}, u32[]{:S(2)}, u32[]{:S(2)}) collective-permute-start(bf16[4,128,1024]{2,1,0:T(8,128)(2,1)} %collective-permute-done.16.refs_2_), channel_id=1, source_target_pairs={{0,1},{1,0},{2,3},{3,2},{4,5},{5,4},{6,7},{7,6},{8,9},{9,8},{10,11... | collective-permute-start | bytes 3145736 | tf_op jit(solution)/shard_map/fa_core/ppermute | solution.py:76
  106.4 40.6 %copy-start.4 = (bf16[4,128,1024]{2,1,0:T(8,128)(2,1)}, bf16[4,128,1024]{2,1,0:T(8,128)(2,1)S(1)}, u32[]{:S(2)}) copy-start(bf16[4,128,1024]{2,1,0:T(8,128)(2,1)S(1)} %fb_high.1.refs_1_) | copy-start | bytes 3145732
  119.6 2.7 %collective-permute-start.24 = (bf16[4,128,1024]{2,1,0:T(8,128)(2,1)S(1)}, bf16[4,128,1024]{2,1,0:T(8,128)(2,1)S(1)}, u32[]{:S(2)}, u32[]{:S(2)}) collective-permute-start(bf16[4,128,1024]{2,1,0:T(8,128)(2,1)S(1)} %collective-permute-done.23.refs_4_), channel_id=1, source_target_pairs={{0,1},{1,0},{2,3},{3,2},{4,5},{5,4},{6,7},{7,6},{8,9},{9,8},{10,11... | collective-permute-start | bytes 3145736 | tf_op jit(solution)/shard_map/fa_core/ppermute | solution.py:76
  119.6 25.5 %collective-permute-start.22 = (bf16[4,128,1024]{2,1,0:T(8,128)(2,1)S(1)}, bf16[4,128,1024]{2,1,0:T(8,128)(2,1)S(1)}, u32[]{:S(2)}, u32[]{:S(2)}) collective-permute-start(bf16[4,128,1024]{2,1,0:T(8,128)(2,1)S(1)} %fb_high.1.refs_1_), channel_id=1, source_target_pairs={{0,4},{1,3},{2,6},{3,1},{4,0},{5,7},{6,2},{7,5},{8,12},{9,11},{10,... | collective-permute-start | bytes 3145736 | tf_op jit(solution)/shard_map/fb_two/ppermute | solution.py:76
  120.9 24.4 %collective-permute-start.21 = (bf16[4,128,1024]{2,1,0:T(8,128)(2,1)S(1)}, bf16[4,128,1024]{2,1,0:T(8,128)(2,1)S(1)}, u32[]{:S(2)}, u32[]{:S(2)}) collective-permute-start(bf16[4,128,1024]{2,1,0:T(8,128)(2,1)S(1)} %fb_high.1.refs_1_), channel_id=1, source_target_pairs={{0,2},{1,5},{2,0},{3,7},{4,6},{5,1},{6,4},{7,3},{8,10},{9,13},{10,... | collective-permute-start | bytes 3145736 | tf_op jit(solution)/shard_map/fb_one/ppermute | solution.py:76
  145.2 18.6 %copy-start.20 = (bf16[4,128,1024]{2,1,0:T(8,128)(2,1)}, bf16[4,128,1024]{2,1,0:T(8,128)(2,1)S(1)}, u32[]{:S(2)}) copy-start(bf16[4,128,1024]{2,1,0:T(8,128)(2,1)S(1)} %collective-permute-done.22.refs_3_) | copy-start | bytes 3145732
  145.3 18.5 %copy-start.21 = (bf16[4,128,1024]{2,1,0:T(8,128)(2,1)}, bf16[4,128,1024]{2,1,0:T(8,128)(2,1)S(1)}, u32[]{:S(2)}) copy-start(bf16[4,128,1024]{2,1,0:T(8,128)(2,1)S(1)} %collective-permute-done.21.refs_2_) | copy-start | bytes 3145732
  145.3 14.8 %collective-permute-start.25 = (bf16[4,128,1024]{2,1,0:T(8,128)(2,1)S(1)}, bf16[4,128,1024]{2,1,0:T(8,128)(2,1)S(1)}, u32[]{:S(2)}, u32[]{:S(2)}) collective-permute-start(bf16[4,128,1024]{2,1,0:T(8,128)(2,1)S(1)} %collective-permute-done.21.refs_2_), channel_id=1, source_target_pairs={{0,4},{1,3},{2,6},{3,1},{4,0},{5,7},{6,2},{7,5},{8,12},{9,11},{10,... | collective-permute-start | bytes 3145736 | tf_op jit(solution)/shard_map/fb_both/ppermute | solution.py:76
  146.9 13.2 %collective-permute-start.27 = (bf16[4,128,1024]{2,1,0:T(8,128)(2,1)S(1)}, bf16[4,128,1024]{2,1,0:T(8,128)(2,1)S(1)}, u32[]{:S(2)}, u32[]{:S(2)}) collective-permute-start(bf16[4,128,1024]{2,1,0:T(8,128)(2,1)S(1)} %collective-permute-done.21.refs_2_), channel_id=1, source_target_pairs={{0,1},{1,0},{2,3},{3,2},{4,5},{5,4},{6,7},{7,6},{8,9},{9,8},{10,11... | collective-permute-start | bytes 3145736 | tf_op jit(solution)/shard_map/fb_core/ppermute | solution.py:76
  146.9 13.1 %collective-permute-start.26 = (bf16[4,128,1024]{2,1,0:T(8,128)(2,1)S(1)}, bf16[4,128,1024]{2,1,0:T(8,128)(2,1)S(1)}, u32[]{:S(2)}, u32[]{:S(2)}) collective-permute-start(bf16[4,128,1024]{2,1,0:T(8,128)(2,1)S(1)} %fb_high.1.refs_1_), channel_id=1, source_target_pairs={{0,1},{1,0},{2,3},{3,2},{4,5},{5,4},{6,7},{7,6},{8,9},{9,8},{10,11... | collective-permute-start | bytes 3145736 | tf_op jit(solution)/shard_map/fb_core/ppermute | solution.py:76
  147.4 12.7 %collective-permute-start.28 = (bf16[4,128,1024]{2,1,0:T(8,128)(2,1)S(1)}, bf16[4,128,1024]{2,1,0:T(8,128)(2,1)S(1)}, u32[]{:S(2)}, u32[]{:S(2)}) collective-permute-start(bf16[4,128,1024]{2,1,0:T(8,128)(2,1)S(1)} %collective-permute-done.22.refs_3_), channel_id=1, source_target_pairs={{0,1},{1,0},{2,3},{3,2},{4,5},{5,4},{6,7},{7,6},{8,9},{9,8},{10,11... | collective-permute-start | bytes 3145736 | tf_op jit(solution)/shard_map/fb_core/ppermute | solution.py:76
  160.1 2.7 %collective-permute-start.29 = (bf16[4,128,1024]{2,1,0:T(8,128)(2,1)S(1)}, bf16[4,128,1024]{2,1,0:T(8,128)(2,1)S(1)}, u32[]{:S(2)}, u32[]{:S(2)}) collective-permute-start(bf16[4,128,1024]{2,1,0:T(8,128)(2,1)S(1)} %collective-permute-done.25.refs_4_), channel_id=1, source_target_pairs={{0,1},{1,0},{2,3},{3,2},{4,5},{5,4},{6,7},{7,6},{8,9},{9,8},{10,11... | collective-permute-start | bytes 3145736 | tf_op jit(solution)/shard_map/fb_core/ppermute | solution.py:76
  183.0 19.1 %all-to-all-start.1 = ((bf16[32,16,512]{2,1,0:T(8,128)(2,1)}), bf16[32,16,512]{2,1,0:T(8,128)(2,1)S(1)}, u32[]{:S(2)}, u32[]{:S(2)}) async-start(bf16[32,16,512]{2,1,0:T(8,128)(2,1)} %get-tuple-element.115), calls=%async_computation.1 | async-start | bytes 1048576 | tf_op jit(solution)/shard_map/grads_b_send/all_to_all | solution.py:689
  202.1 11.3 %all-to-all-start.2 = ((bf16[32,16,128]{2,1,0:T(8,128)(2,1)}), bf16[32,16,128]{2,1,0:T(8,128)(2,1)S(1)}, u32[]{:S(2)}, u32[]{:S(2)}) async-start(bf16[32,16,128]{2,1,0:T(8,128)(2,1)} %get-tuple-element.116), calls=%async_computation.2 | async-start | bytes 262144 | tf_op jit(solution)/shard_map/grads_c_send/all_to_all | solution.py:689
  206.7 18.4 %collective-permute-start.32 = (bf16[128,384]{1,0:T(8,128)(2,1)S(1)}, bf16[128,384]{1,0:T(8,128)(2,1)S(1)}, u32[]{:S(2)}, u32[]{:S(2)}) collective-permute-start(bf16[128,384]{1,0:T(8,128)(2,1)S(1)} %bitcast.23), channel_id=1, source_target_pairs={{0,24},{1,25},{2,26},{3,27},{4,28},{5,29},{6,30},{7,31},{8,16},{9,... | collective-permute-start | bytes 294920 | tf_op jit(solution)/shard_map/grads_b/ppermute | solution.py:76
  210.4 14.7 %collective-permute-start.31 = (bf16[128,384]{1,0:T(8,128)(2,1)S(1)}, bf16[128,384]{1,0:T(8,128)(2,1)S(1)}, u32[]{:S(2)}, u32[]{:S(2)}) collective-permute-start(bf16[128,384]{1,0:T(8,128)(2,1)S(1)} %bitcast.24), channel_id=1, source_target_pairs={{0,16},{1,17},{2,18},{3,19},{4,20},{5,21},{6,22},{7,23},{8,24},{9,... | collective-permute-start | bytes 294920 | tf_op jit(solution)/shard_map/grads_b/ppermute | solution.py:76
  210.4 14.7 %collective-permute-start.30 = (bf16[128,384]{1,0:T(8,128)(2,1)S(1)}, bf16[128,384]{1,0:T(8,128)(2,1)S(1)}, u32[]{:S(2)}, u32[]{:S(2)}) collective-permute-start(bf16[128,384]{1,0:T(8,128)(2,1)S(1)} %bitcast.25), channel_id=1, source_target_pairs={{0,8},{1,9},{2,10},{3,11},{4,12},{5,13},{6,14},{7,15},{8,0},{9,1},... | collective-permute-start | bytes 294920 | tf_op jit(solution)/shard_map/grads_b/ppermute | solution.py:76
  214.1 6.1 %collective-permute-start.35 = (bf16[128,128]{1,0:T(8,128)(2,1)S(1)}, bf16[128,128]{1,0:T(8,128)(2,1)S(1)}, u32[]{:S(2)}, u32[]{:S(2)}) collective-permute-start(bf16[128,128]{1,0:T(8,128)(2,1)S(1)} %bitcast.27), channel_id=1, source_target_pairs={{0,24},{1,25},{2,26},{3,27},{4,28},{5,29},{6,30},{7,31},{8,16},{9,... | collective-permute-start | bytes 98312 | tf_op jit(solution)/shard_map/grads_b/ppermute | solution.py:76
  215.5 7.5 %collective-permute-start.34 = (bf16[128,128]{1,0:T(8,128)(2,1)S(1)}, bf16[128,128]{1,0:T(8,128)(2,1)S(1)}, u32[]{:S(2)}, u32[]{:S(2)}) collective-permute-start(bf16[128,128]{1,0:T(8,128)(2,1)S(1)} %bitcast.28), channel_id=1, source_target_pairs={{0,16},{1,17},{2,18},{3,19},{4,20},{5,21},{6,22},{7,23},{8,24},{9,... | collective-permute-start | bytes 98312 | tf_op jit(solution)/shard_map/grads_b/ppermute | solution.py:76
  220.3 4.6 %collective-permute-start.33 = (bf16[128,128]{1,0:T(8,128)(2,1)S(1)}, bf16[128,128]{1,0:T(8,128)(2,1)S(1)}, u32[]{:S(2)}, u32[]{:S(2)}) collective-permute-start(bf16[128,128]{1,0:T(8,128)(2,1)S(1)} %bitcast.29), channel_id=1, source_target_pairs={{0,8},{1,9},{2,10},{3,11},{4,12},{5,13},{6,14},{7,15},{8,0},{9,1},... | collective-permute-start | bytes 98312 | tf_op jit(solution)/shard_map/grads_b/ppermute | solution.py:76
  225.8 14.1 %copy-start.5 = (bf16[4,128,512]{2,1,0:T(8,128)(2,1)}, bf16[4,128,512]{2,1,0:T(8,128)(2,1)S(1)}, u32[]{:S(2)}) copy-start(bf16[4,128,512]{2,1,0:T(8,128)(2,1)S(1)} %grads_b.9.refs_1_) | copy-start | bytes 1572868
  225.8 14.1 %collective-permute-start.37 = (bf16[4,128,512]{2,1,0:T(8,128)(2,1)S(1)}, bf16[4,128,512]{2,1,0:T(8,128)(2,1)S(1)}, u32[]{:S(2)}, u32[]{:S(2)}) collective-permute-start(bf16[4,128,512]{2,1,0:T(8,128)(2,1)S(1)} %grads_b.9.refs_1_), channel_id=1, source_target_pairs={{0,4},{1,3},{2,6},{3,1},{4,0},{5,7},{6,2},{7,5},{8,12},{9,11},{10,... | collective-permute-start | bytes 1572872 | tf_op jit(solution)/shard_map/grads/ppermute | solution.py:76
  227.3 12.5 %collective-permute-start.36 = (bf16[4,128,512]{2,1,0:T(8,128)(2,1)S(1)}, bf16[4,128,512]{2,1,0:T(8,128)(2,1)S(1)}, u32[]{:S(2)}, u32[]{:S(2)}) collective-permute-start(bf16[4,128,512]{2,1,0:T(8,128)(2,1)S(1)} %grads_b.9.refs_1_), channel_id=1, source_target_pairs={{0,2},{1,5},{2,0},{3,7},{4,6},{5,1},{6,4},{7,3},{8,10},{9,13},{10,... | collective-permute-start | bytes 1572872 | tf_op jit(solution)/shard_map/grads/ppermute | solution.py:76
  239.8 6.2 %copy-start.31 = (bf16[4,128,512]{2,1,0:T(8,128)(2,1)}, bf16[4,128,512]{2,1,0:T(8,128)(2,1)S(1)}, u32[]{:S(2)}) copy-start(bf16[4,128,512]{2,1,0:T(8,128)(2,1)S(1)} %collective-permute-done.37.refs_3_) | copy-start | bytes 1572868
  239.8 5.7 %copy-start.32 = (bf16[4,128,512]{2,1,0:T(8,128)(2,1)}, bf16[4,128,512]{2,1,0:T(8,128)(2,1)S(1)}, u32[]{:S(2)}) copy-start(bf16[4,128,512]{2,1,0:T(8,128)(2,1)S(1)} %collective-permute-done.36.refs_2_) | copy-start | bytes 1572868
  239.9 2.1 collective-permute-start.38
  239.9 9.4 %collective-permute-start.39 = (bf16[4,128,512]{2,1,0:T(8,128)(2,1)S(1)}, bf16[4,128,512]{2,1,0:T(8,128)(2,1)}, u32[]{:S(2)}, u32[]{:S(2)}) collective-permute-start(bf16[4,128,512]{2,1,0:T(8,128)(2,1)S(1)} %collective-permute-done.36.refs_2_), channel_id=1, source_target_pairs={{0,4},{1,3},{2,6},{3,1},{4,0},{5,7},{6,2},{7,5},{8,12},{9,11},{10,... | collective-permute-start | bytes 1572872 | tf_op jit(solution)/shard_map/grads/ppermute | solution.py:76
  242.0 20.8 %all-to-all-start.3 = ((bf16[4,640,256]{2,1,0:T(8,128)(2,1)}), bf16[4,640,256]{2,1,0:T(8,128)(2,1)S(1)}, u32[]{:S(2)}, u32[]{:S(2)}) async-start(bf16[4,640,256]{2,1,0:T(8,128)(2,1)} %shard_map.282), calls=%async_computation.3 | async-start | bytes 2621440 | tf_op jit(solution)/shard_map/rows_out/all_to_all | solution.py:955
  245.5 3.8 %collective-permute-start.40 = (bf16[4,128,512]{2,1,0:T(8,128)(2,1)S(1)}, bf16[4,128,512]{2,1,0:T(8,128)(2,1)S(1)}, u32[]{:S(2)}, u32[]{:S(2)}) collective-permute-start(bf16[4,128,512]{2,1,0:T(8,128)(2,1)S(1)} %collective-permute-done.36.refs_2_), channel_id=1, source_target_pairs={{0,1},{1,0},{2,3},{3,2},{4,5},{5,4},{6,7},{7,6},{8,9},{9,8},{10,11... | collective-permute-start | bytes 1572872 | tf_op jit(solution)/shard_map/grads/ppermute | solution.py:76
  246.0 3.3 %collective-permute-start.41 = (bf16[4,128,512]{2,1,0:T(8,128)(2,1)S(1)}, bf16[4,128,512]{2,1,0:T(8,128)(2,1)S(1)}, u32[]{:S(2)}, u32[]{:S(2)}) collective-permute-start(bf16[4,128,512]{2,1,0:T(8,128)(2,1)S(1)} %collective-permute-done.37.refs_3_), channel_id=1, source_target_pairs={{0,1},{1,0},{2,3},{3,2},{4,5},{5,4},{6,7},{7,6},{8,9},{9,8},{10,11... | collective-permute-start | bytes 1572872 | tf_op jit(solution)/shard_map/grads/ppermute | solution.py:76
  249.3 2.1 collective-permute-start.42
  252.2 11.6 %copy-start.1 = (bf16[8,16,3,1024]{3,1,2,0:T(8,128)(2,1)S(1)}, bf16[8,16,3,1024]{3,1,2,0:T(8,128)(2,1)}, u32[]{:S(2)}) copy-start(bf16[8,16,3,1024]{3,1,2,0:T(8,128)(2,1)} %param.35) | copy-start | bytes 2359300
  (20 other events, 57.1 us)

commit v7 on v6

--- a/solution.py
+++ b/solution.py
@@ -17,7 +17,6 @@
 SEQ = 320
 PAIR = 2 * HD
 EXTRA = 16
-OWNER = 128
 SPREAD = 56
 FRONT, FFN_A, FFN_B, ATT, BACK = 56, 56, 56, 56, 56
 BF = jnp.bfloat16
@@ -117,24 +116,24 @@
     return stacked(parts, index), parts
 
 
-def groups(top, bottom):
+def groups(top, bottom, most):
     out = []
     while top > bottom:
-        width = min(2, top - bottom)
+        width = min(most, top - bottom)
         out.append((top - width, width))
         top -= width
     return out
 
 
-def early_groups(rows, cols):
-    return [("row",) + g for g in groups(bits_of(rows), 1)] + [
-        ("col",) + g for g in groups(bits_of(cols), 2)
+def early_groups(rows, cols, most):
+    return [("row",) + g for g in groups(bits_of(rows), 1, most)] + [
+        ("col",) + g for g in groups(bits_of(cols), 2, most)
     ]
 
 
-def lead_table(rows, cols):
+def lead_table(rows, cols, most=2):
     table = [(0, 0)]
-    for axis, bit, width in early_groups(rows, cols):
+    for axis, bit, width in early_groups(rows, cols, most):
         shift = bit - (1 if axis == "row" else 2)
         new = []
         for value in range(1 << width):
@@ -155,20 +154,22 @@
     return lax.optimization_barrier(tuple(values) + others)[: len(values)]
 
 
-def gather_high(shard):
+def gather_high(shard, most=2):
     rows, cols = sizes()
     block, parts = shard, []
-    for axis, bit, width in early_groups(rows, cols):
+    for axis, bit, width in early_groups(rows, cols, most):
         block, parts = group_join(block, axis, bit, width)
     return block.reshape((-1,) + shard.shape), parts[1:]
 
 
-def lane_join_kernel(*refs):
+def lane_join_kernel(orders, *refs):
     parts, out, sems = refs[:-2], refs[-2], refs[-1]
     copies, lane = [], 0
-    for i, part in enumerate(parts):
+    for i, (part, order) in enumerate(zip(parts, orders)):
         width = part.shape[-1]
-        copies.append(pltpu.make_async_copy(part, out.at[:, :, lane : lane + width], sems.at[i]))
+        for n, put_at in enumerate(order):
+            target = out.at[put_at, :, lane : lane + width]
+            copies.append(pltpu.make_async_copy(part.at[n], target, sems.at[i, n]))
         lane += width
     for copy in copies:
         copy.start()
@@ -176,16 +177,17 @@
         copy.wait()
 
 
-def lane_join(*parts):
+def lane_join(parts, orders):
     if any(p.shape[-1] % 128 for p in parts):
-        return jnp.concatenate(parts, axis=-1)
+        placed = [p[jnp.array(sorted(range(len(o)), key=o.index))] for p, o in zip(parts, orders)]
+        return jnp.concatenate(placed, axis=-1)
     shape = parts[0].shape[:-1] + (sum(p.shape[-1] for p in parts),)
     return call(
-        lane_join_kernel,
+        functools.partial(lane_join_kernel, orders),
         jax.ShapeDtypeStruct(shape, parts[0].dtype),
         parts,
         [pl.ANY] * len(parts),
-        [pltpu.SemaphoreType.DMA((len(parts),))],
+        [pltpu.SemaphoreType.DMA((len(parts), shape[0]))],
     )
 
 
@@ -203,6 +205,15 @@
 
 def with_cores(pieces):
     return pieces + [swap(p, flip_core) for p in pieces]
+
+
+def owner_parts(block, bit):
+    step = 1 << bit
+    return [block, swap(block, lambda r, c: (r ^ step, c))]
+
+
+def owner_stack(parts, bit):
+    return jnp.stack(parts)[jnp.arange(2) ^ ((lax.axis_index("row") >> bit) & 1)]
 
 
 def piece_place(sc, k):
@@ -261,11 +272,10 @@
     return [VMEM((cols, D, n), BF), pltpu.SemaphoreType.DMA((8, lead))]
 
 
-def put(ref, start, value, lane=0, spare=0):
-    end = ref.shape[-1] - spare
-    part = end - lane
+def put(ref, start, value, lane=0):
+    part = ref.shape[-1] - lane
     for i in range(value.shape[-1] // part):
-        ref[start // part + i, :, lane:end] = value[:, i * part : (i + 1) * part]
+        ref[start // part + i, :, lane:] = value[:, i * part : (i + 1) * part]
 
 
 def lanes(start, width):
@@ -401,7 +411,7 @@
     lat3[...] = low(mm(n2[...], row_fd[...], NT))
 
 
-def ffn_steps(weights, sc, part, cols, w, bs, n2, lat3, gr, glat4, up_1, down_2, acc, early, lane=0, spare=0):
+def ffn_steps(weights, sc, part, cols, w, bs, n2, lat3, gr, glat4, up_1, down_2, acc, early, lane=0):
     res, gn2, lat4, glat3 = acc
     hid = D // cols
     ffn = FF // cols
@@ -428,8 +438,8 @@
         glat3[...] += mm(grad_pre, up, NT)
         res[...] += mm(activated, w2, NT)
         gn2[...] += mm(grad_pre, w1, NT)
-        put(early, block * half, low(mm(lat3_t, grad_pre)), lane, spare)
-        put(early, FF // 2 + block * half, low(mm(glat4_t, activated)), lane, spare)
+        put(early, block * half, low(mm(lat3_t, grad_pre)), lane)
+        put(early, FF // 2 + block * half, low(mm(glat4_t, activated)), lane)
         return 0
 
     lax.fori_loop(0, cols, step, 0)
@@ -485,7 +495,6 @@
         (up_1.at[a], row_u1),
         (down_2.at[a], row_d2),
     )
-    early[:, :, early.shape[2] - OWNER :] = low(jnp.full((early.shape[0], R, OWNER), sc[0], F32))
     weights = Weights(sc, pieces, w, sems, lead)
     weights.start()
     proj = Weights(sc, own_q, wp, sems_p, lead, 3 * D // cols)
@@ -510,7 +519,7 @@
     lat4[...] = lat4_in[...]
     glat3[...] = glat3_in[...]
     ffn_steps(
-        weights, sc, 1, cols, w, bs, n2, lat3, gr, glat4, row_u1, row_d2, (res, gn2, lat4, glat3), early, lane, OWNER
+        weights, sc, 1, cols, w, bs, n2, lat3, gr, glat4, row_u1, row_d2, (res, gn2, lat4, glat3), early, lane
     )
     for copy in last:
         copy.wait()
@@ -531,9 +540,9 @@
     gb = low(grad_middle)
     glat2 = low(mm(gb, row_pu[...], NT))
     glat2_t = low(glat2.astype(F32).T)
-    put(early, FF + D, low(mm(low(lat2[...].astype(F32).T), gb)), lane, OWNER)
-    put(early, FF + 2 * D, low(mm(low(glat3_low.astype(F32).T), n2[...])), lane, OWNER)
-    put(early, FF + 3 * D, low(mm(low(lat4_low.astype(F32).T), gr[...])), lane, OWNER)
+    put(early, FF + D, low(mm(low(lat2[...].astype(F32).T), gb)), lane)
+    put(early, FF + 2 * D, low(mm(low(glat3_low.astype(F32).T), n2[...])), lane)
+    put(early, FF + 3 * D, low(mm(low(lat4_low.astype(F32).T), gr[...])), lane)
     proj.wait()
 
     def step(slot, _):
@@ -541,7 +550,7 @@
         here = lanes(slot * hid, hid)
         there = lanes(block * hid, hid)
         gatt[:, here] = low(mm(gb, wp[slot]) + mm(glat2, row_pd[:, there]))
-        put(early, FF + block * hid, low(mm(glat2_t, att_s[:, here])), lane, OWNER)
+        put(early, FF + block * hid, low(mm(glat2_t, att_s[:, here])), lane)
         return 0
 
     lax.fori_loop(0, cols, step, 0)
@@ -853,11 +862,16 @@
         mib=FRONT,
     )
     own_a, one_a, two_a = after_all((own_a, one_a, two_a), n1, *came_b)
+    bits = list(reversed(range(bits_of(rows))))
+    owners = after(adapter_index, n1)
+    for bit in bits[:-1]:
+        owners = owner_stack(owner_parts(owners, bit), bit)
     with jax.named_scope("fa_both"):
         both_a = swap(one_a, flip_two)
     with jax.named_scope("fa_core"):
         away_a = [swap(p, flip_core) for p in (own_a, one_a, two_a)]
-    own_b = after(own_b, *away_a)
+    own_b, owners = after_all((own_b, owners), *away_a)
+    owners = owner_parts(owners, 0)
     with jax.named_scope("fa_core"):
         pieces_a = [own_a, one_a, two_a, both_a] + away_a + [swap(both_a, flip_core)]
     with jax.named_scope("fb_one"):
@@ -876,7 +890,8 @@
         + [pltpu.SemaphoreType.DMA((5,))],
         mib=FFN_A,
     )
-    own_b, one_b, two_b = after_all((own_b, one_b, two_b), res)
+    own_b, one_b, two_b, *owners = after_all((own_b, one_b, two_b, *owners), res)
+    owners = owner_stack(owners, 0).transpose(tuple(bits) + (len(bits),)).reshape(-1)
     with jax.named_scope("fb_both"):
         both_b = swap(one_b, flip_two)
     with jax.named_scope("fb_core"):
@@ -885,7 +900,7 @@
     layer, gatt, gmid, grads_b = call(
         functools.partial(ffn_b_kernel, lead, cols),
         [jax.ShapeDtypeStruct((cols, SEQ, hid), BF), big, wide]
-        + [jax.ShapeDtypeStruct((rows * cols, R, 12 * D // (rows * cols) + OWNER), BF)],
+        + [jax.ShapeDtypeStruct((rows * cols, R, 12 * D // (rows * cols)), BF)],
         [sc, *pieces_b, *pieces_q, xa, keep, ln_gain, n2, lat3, fc1_up, fc2_down, fc2_up]
         + [fc1_down, proj_down, proj_up, bias_out]
         + [middle, att, lat2, gr, res, gn2, lat4, glat3, early_a],
@@ -905,7 +920,6 @@
     )
     with jax.named_scope("grads_b_send"):
         mine_b = send_grads(grads_b)
-        owners = mine_b[:, 0, mine_b.shape[2] - 1].astype(jnp.int32)
     gq, gk, gv, glat1, late = call(
         functools.partial(attention_back_kernel, cols),
         [big, big, big, small, jax.ShapeDtypeStruct((rows * cols, R, 4 * D // (rows * cols)), BF)],
@@ -916,9 +930,12 @@
     with jax.named_scope("grads_c_send"):
         mine_c = send_grads(late)
     with jax.named_scope("grads_b"):
-        own_b, _ = gather_high(sum_grads(after(mine_b, late), owners, mine_b.shape[2] - OWNER))
+        own_b, _ = gather_high(
+            sum_grads(after(mine_b, late), owners, mine_b.shape[2]), 1
+        )
         own_c, _ = gather_high(sum_grads(mine_c, owners, mine_c.shape[2]))
-        own = lane_join(own_b, own_c)
+        order_b = tuple(lead.index(place) for place in lead_table(rows, cols, 1))
+        own = lane_join([own_b, own_c], [order_b, tuple(range(len(lead)))])
     gmid = after(gmid, own)
     sent = call(
         functools.partial(back_kernel, lead, cols),
@@ -946,7 +963,7 @@
         )
         map_b = map_b + tuple((2 + i, None, 0, FF + i * D, D) for i in range(4))
         map_c = ((6, None, 0, 0, D),) + tuple((7, c, 0, (c + 1) * D, D) for c in range(3))
-        parts = [early_a.shape[-1], mine_b.shape[-1] - early_a.shape[-1] - OWNER, mine_c.shape[-1]]
+        parts = [early_a.shape[-1], mine_b.shape[-1] - early_a.shape[-1], mine_c.shape[-1]]
         shapes = [(NA * R, FF)] * 2 + [(NA * R, D)] * 5 + [(NA, 3, R, D)]
         sums = spread(sc, pieces, parts, [map_a, map_b, map_c], shapes)
 

time: 265 us -> 261 us (0.985)
  starting transfers between devices: 56.4 us -> 52.4 us
    ppermute x43 -> x45, starting transfers between devices: 41.8 us -> 37 us  [swap(): return lax.ppermute(block, BOTH, pairs)]
    unnamed x74 -> x66, local copies, waits for them, and re-layouts: 5.35 us -> 4.33 us
    ppermute x43 -> x45, waiting for transfers between devices: 95.9 us -> 96.2 us  [swap(): return lax.ppermute(block, BOTH, pairs)]
    pallas_call x16 -> x17, Pallas kernels: 87.3 us -> 87.6 us  [call(): pl.pallas_call(kernel, out_shape=outs, in_specs=[pl.BlockSpec(memory_spac...]
  transfers between devices with their start and end apart: 47 -> 49, of which waited for: 21 -> 24; matrix products, arithmetic and copies ran while one was open for 1% -> 1% of each run, Pallas kernels for 25% -> 25%
where the time goes in v7:
time: 261 us
  waiting for transfers between devices  107 us (41%)
  Pallas kernels  87.6 us (34%)
  starting transfers between devices  52.4 us (20%)
  local copies, waits for them, and re-layouts  9.83 us (4%)
  between operations  3.19 us (1%)
    ppermute x45, waiting for transfers between devices, swap(): return lax.ppermute(block, BOTH, pairs)  96.2 us
    pallas_call x17, Pallas kernels, call(): pl.pallas_call(kernel, out_shape=outs, in_specs=[pl.BlockSpec(memory_spac...  87.6 us
    ppermute x45, starting transfers between devices, swap(): return lax.ppermute(block, BOTH, pairs)  37 us
    all_to_all x2, starting transfers between devices, send_grads(): return lax.all_to_all(grads, BOTH, split_axis=0, concat_axis=0, tiled=True)  7.34 us
    all_to_all x2, waiting for transfers between devices, send_grads(): return lax.all_to_all(grads, BOTH, split_axis=0, concat_axis=0, tiled=True)  7.15 us
  transfers between devices with their start and end apart: 49, of which 24 were waited for; matrix products, arithmetic and copies ran while one was open for 1% of the time, Pallas kernels for 25%

profile of v7, /device:TPU:0, one launch (start us, length us, event | category | flops | bytes accessed | tf_op | source)
XLA Modules:
  0.0 260.7 jit_solution(7487863809234582057)
XLA Ops:
  0.7 1.4 reshape.137.bias_f
  2.0 2.6 shard_map.276
  4.6 4.4 %all-to-all-start = ((bf16[4,656,256]{2,1,0:T(8,128)(2,1)}), bf16[4,656,256]{2,1,0:T(8,128)(2,1)}, u32[]{:S(2)}, u32[]{:S(2)}) async-start(bf16[4,656,256]{2,1,0:T(8,128)(2,1)} %get-tuple-element.78), calls=%async_computation | async-start | bytes 2686976 | tf_op jit(solution)/shard_map/all_to_all | solution.py:797
  9.1 5.1 %collective-permute-start.2 = (bf16[128,1024]{1,0:T(8,128)(2,1)S(1)}, bf16[128,1024]{1,0:T(8,128)(2,1)S(1)}, u32[]{:S(2)}, u32[]{:S(2)}) collective-permute-start(bf16[128,1024]{1,0:T(8,128)(2,1)S(1)} %copy-done.8), channel_id=1, source_target_pairs={{0,24},{1,25},{2,26},{3,27},{4,28},{5,29},{6,30},{7,31},{8,16},{9,... | collective-permute-start | bytes 786440 | tf_op jit(solution)/shard_map/q_high/ppermute | solution.py:75
  14.2 0.6 collective-permute-start
  17.4 0.7 pad_add_fusion.3.sc.refs_0_
  18.2 0.8 shard_map.277
  19.0 0.7 copy-done.6
  19.7 0.7 copy-done.7
  20.3 0.6 dynamic-slice_bitcast_fusion.refs_14_.refs_9_
  21.5 15.6 %collective-permute-done.1.refs_2_ = bf16[128,1024]{1,0:T(8,128)(2,1)S(1)} collective-permute-done((bf16[128,1024]{1,0:T(8,128)(2,1)S(1)}, bf16[128,1024]{1,0:T(8,128)(2,1)S(1)}, u32[]{:S(2)}, u32[]{:S(2)}) %collective-permute-start.1) | collective-permute-done | bytes 262176 | tf_op jit(solution)/shard_map/q_high/ppermute | solution.py:75
  37.2 1.6 collective-permute-start.4
  38.8 1.7 collective-permute-start.3
  40.5 2.5 collective-permute-start.7
  43.0 1.9 collective-permute-start.5
  44.9 6.8 %collective-permute-done.7.refs_3_ = bf16[128,1024]{1,0:T(8,128)(2,1)S(1)} collective-permute-done((bf16[128,1024]{1,0:T(8,128)(2,1)S(1)}, bf16[128,1024]{1,0:T(8,128)(2,1)S(1)}, u32[]{:S(2)}, u32[]{:S(2)}) %collective-permute-start.7) | collective-permute-done | bytes 262176 | tf_op jit(solution)/shard_map/fa_high/ppermute | solution.py:75
  51.6 11.8 %collective-permute-done.6.refs_2_ = bf16[128,1024]{1,0:T(8,128)(2,1)S(1)} collective-permute-done((bf16[128,1024]{1,0:T(8,128)(2,1)S(1)}, bf16[128,1024]{1,0:T(8,128)(2,1)S(1)}, u32[]{:S(2)}, u32[]{:S(2)}) %collective-permute-start.6) | collective-permute-done | bytes 262176 | tf_op jit(solution)/shard_map/fa_high/ppermute | solution.py:75
  63.4 1.2 collective-permute-start.8
  65.2 13.1 %collective-permute-done.8.refs_4_.refs_12_ = bf16[4,128,1024]{2,1,0:T(8,128)(2,1)S(1)} collective-permute-done((bf16[4,128,1024]{2,1,0:T(8,128)(2,1)S(1)}, bf16[4,128,1024]{2,1,0:T(8,128)(2,1)S(1)}, u32[]{:S(2)}, u32[]{:S(2)}) %collective-permute-start.8) | collective-permute-done | bytes 1048608 | tf_op jit(solution)/shard_map/q_both/ppermute | solution.py:75
  78.5 1.2 collective-permute-start.19
  80.3 2.5 collective-permute-start.15
  82.8 1.0 copy-done.19
  83.9 1.9 collective-permute-start.13
  85.8 18.0 %shard_map.278 = (bf16[320,1024]{1,0:T(8,128)(2,1)}, bf16[320,16]{1,0:T(8,128)(2,1)}, bf16[320,1024]{1,0:T(8,128)(2,1)}, bf16[320,1024]{1,0:T(8,128)(2,1)}, bf16...) custom-call(s32[4]{0:T(128)} %copy-done.11, ...), custom_call_target="tpu_custom_call" | custom-call | tf_op jit(solution)/shard_map/pallas_call | solution.py:54
  103.8 0.7 collective-permute-done.14.refs_2_
  104.6 1.2 collective-permute-start.26
  106.5 4.4 %collective-permute-done.16 = s32[4]{0:T(128)S(1)} collective-permute-done((s32[4]{0:T(128)S(1)}, s32[4]{0:T(128)S(1)}, u32[]{:S(2)}, u32[]{:S(2)}) %collective-permute-start.16) | collective-permute-done | bytes 48 | tf_op jit(solution)/shard_map/ppermute | solution.py:75
  111.7 3.4 %collective-permute-done.17 = s32[2,4]{1,0:T(2,128)S(1)} collective-permute-done((s32[2,4]{1,0:T(2,128)S(1)}, s32[2,4]{1,0:T(2,128)S(1)}, u32[]{:S(2)}, u32[]{:S(2)}) %collective-permute-start.17) | collective-permute-done | bytes 64 | tf_op jit(solution)/shard_map/ppermute | solution.py:75
  115.1 4.6 %collective-permute-done.26.refs_4_ = bf16[4,128,1024]{2,1,0:T(8,128)(2,1)} collective-permute-done((bf16[4,128,1024]{2,1,0:T(8,128)(2,1)}, bf16[4,128,1024]{2,1,0:T(8,128)(2,1)}, u32[]{:S(2)}, u32[]{:S(2)}) %collective-permute-start.26) | collective-permute-done | bytes 1048608 | tf_op jit(solution)/shard_map/fa_both/ppermute | solution.py:75
  120.3 1.2 collective-permute-start.24
  121.5 0.7 collective-permute-start.23
  122.2 1.5 collective-permute-start.25
  123.7 15.4 %shard_map.279 = (f32[320,1024]{1,0:T(8,128)}, f32[320,1024]{1,0:T(8,128)}, f32[320,16]{1,0:T(8,128)}, f32[320,16]{1,0:T(8,128)}, bf16[320,1024]{1,0:T(8,128)(2,1)}, /*index=5*/bf16[32,16,128]{2,1,0:T(8,128)(2,1)}) custom-call(s32[4]{0:T(128)} %copy-done.11, bf16[4,128,1024]{2,1,0:T(8,128)(2,1)} %copy-done.3, ...), custom_call_target="tpu_custom_call" | custom-call | tf_op jit(solution)/shard_map/pallas_call | solution.py:54
  139.1 6.7 %collective-permute-done.25 = s32[2,2,4]{2,1,0:T(2,128)S(1)} collective-permute-done((s32[2,2,4]{2,1,0:T(2,128)S(1)}, s32[2,2,4]{2,1,0:T(2,128)S(1)}, u32[]{:S(2)}, u32[]{:S(2)}) %collective-permute-start.25) | collective-permute-done | bytes 96 | tf_op jit(solution)/shard_map/ppermute | solution.py:75
  145.9 1.7 collective-permute-start.28
  148.2 12.6 %collective-permute-done.28.refs_4_ = bf16[4,128,1024]{2,1,0:T(8,128)(2,1)S(1)} collective-permute-done((bf16[4,128,1024]{2,1,0:T(8,128)(2,1)S(1)}, bf16[4,128,1024]{2,1,0:T(8,128)(2,1)S(1)}, u32[]{:S(2)}, u32[]{:S(2)}) %collective-permute-start.28) | collective-permute-done | bytes 1048608 | tf_op jit(solution)/shard_map/fb_both/ppermute | solution.py:75
  160.8 2.6 collective-permute-done.32.refs_8_
  163.4 1.0 copy-done.26
  164.4 19.2 %shard_map.280 = (bf16[4,320,256]{2,1,0:T(8,128)(2,1)}, bf16[320,1024]{1,0:T(8,128)(2,1)}, f32[320,1024]{1,0:T(8,128)}, bf16[32,16,384]{2,1,0:T(8,128)(2,1)}) custom-call(s32[4]{0:T(128)} %copy-done.11, bf16[4,128,1024]{2,1,0:T(8,128)(2,1)} %copy-done.4, bf16[4,128,1024]{2,1,0:T(8,128)(2,1)} %copy-done.21, bf16[4,128,1024]{2,1,0:T(8,128)(2,1)} %copy-done.20, ...), custom_call_target="tpu_custom_call" | custom-call | tf_op jit(solution)/shard_map/pallas_call | solution.py:54
  183.6 3.6 %all-to-all-start.1 = ((bf16[32,16,384]{2,1,0:T(8,128)(2,1)}), bf16[32,16,384]{2,1,0:T(8,128)(2,1)S(1)}, u32[]{:S(2)}, u32[]{:S(2)}) async-start(bf16[32,16,384]{2,1,0:T(8,128)(2,1)} %get-tuple-element.123), calls=%async_computation.1 | async-start | bytes 786432 | tf_op jit(solution)/shard_map/grads_b_send/all_to_all | solution.py:698
  188.0 10.8 %shard_map.281 = (bf16[320,1024]{1,0:T(8,128)(2,1)}, bf16[320,1024]{1,0:T(8,128)(2,1)}, bf16[320,1024]{1,0:T(8,128)(2,1)}, bf16[320,16]{1,0:T(8,128)(2,1)}, bf16[32,16,128]{2,1,0:T(8,128)(2,1)}) custom-call(s32[4]{0:T(128)} %copy-done.11, f32[320,1]{1,0:T(8,128)} %copy-done.7, bf16[320,1024]{1,0:T(8,128)(2,1)} %get-tuple-element.86.refs_2_, ...), custom_call_target="tpu_custom_call" | custom-call | tf_op jit(solution)/shard_map/pallas_call | solution.py:54
  198.8 1.6 all-to-all-done.1.mine
  200.4 0.7 grads_b.6
  201.2 1.1 collective-permute-start.33
  202.3 3.7 %all-to-all-start.2 = ((bf16[32,16,128]{2,1,0:T(8,128)(2,1)}), bf16[32,16,128]{2,1,0:T(8,128)(2,1)S(1)}, u32[]{:S(2)}, u32[]{:S(2)}) async-start(bf16[32,16,128]{2,1,0:T(8,128)(2,1)} %get-tuple-element.124), calls=%async_computation.2 | async-start | bytes 262144 | tf_op jit(solution)/shard_map/grads_c_send/all_to_all | solution.py:698
  206.0 2.4 collective-permute-done.33.refs_1_
  208.7 5.5 %all-to-all-done.2.mine = bf16[32,16,128]{2,1,0:T(8,128)(2,1)S(1)} async-done(((bf16[32,16,128]{2,1,0:T(8,128)(2,1)}), bf16[32,16,128]{2,1,0:T(8,128)(2,1)S(1)}, u32[]{:S(2)}, u32[]{:S(2)}) %all-to-all-start.2) | async-done | bytes 131104 | tf_op jit(solution)/shard_map/grads_c_send/all_to_all | solution.py:698
  214.3 0.7 grads_b.9
  215.0 1.4 collective-permute-start.37
  216.3 0.9 collective-permute-start.36
  217.2 2.2 collective-permute-start.35
  219.4 1.6 collective-permute-done.37.refs_3_
  221.0 0.8 collective-permute-done.36.refs_2_
  223.3 0.9 collective-permute-start.38
  224.2 11.0 %shard_map.282 = bf16[4,640,256]{2,1,0:T(8,128)(2,1)} custom-call(s32[4]{0:T(128)} %copy-done.11, bf16[4,128,1024]{2,1,0:T(8,128)(2,1)} %copy-done.2, bf16[4,128,1024]{2,1,0:T(8,128)(2,1)} %copy-done.14, bf16[4,128,1024]{2,1,0:T(8,128)(2,1)} %copy-done.13, bf16[4,128,1024]{2,1,0:T(8,128)(2,1)} %copy-done.15, bf16[4,128,1024]{2,1,0:T(8,128)(2,1)} %copy-done.16, ...), custom_call_target="tpu_custom_call" | custom-call | tf_op jit(solution)/shard_map/pallas_call | solution.py:54
  235.2 1.5 collective-permute-done.39.refs_3_
  237.1 1.7 collective-permute-done.40.refs_5_
  238.8 3.5 %all-to-all-start.3 = ((bf16[4,640,256]{2,1,0:T(8,128)(2,1)}), bf16[4,640,256]{2,1,0:T(8,128)(2,1)S(1)}, u32[]{:S(2)}, u32[]{:S(2)}) async-start(bf16[4,640,256]{2,1,0:T(8,128)(2,1)} %shard_map.282), calls=%async_computation.3 | async-start | bytes 2621440 | tf_op jit(solution)/shard_map/rows_out/all_to_all | solution.py:972
  242.9 3.2 %collective-permute-done.41.refs_4_ = bf16[4,128,512]{2,1,0:T(8,128)(2,1)} collective-permute-done((bf16[4,128,512]{2,1,0:T(8,128)(2,1)S(1)}, bf16[4,128,512]{2,1,0:T(8,128)(2,1)}, u32[]{:S(2)}, u32[]{:S(2)}) %collective-permute-start.41) | collective-permute-done | bytes 524320 | tf_op jit(solution)/shard_map/grads/ppermute | solution.py:75
  246.1 2.1 collective-permute-done.44.refs_8_
  248.2 0.8 copy-done.31
  249.0 6.9 %grads.1 = (f32[128,4096]{1,0:T(8,128)}, f32[128,4096]{1,0:T(8,128)}, f32[128,1024]{1,0:T(8,128)}, f32[128,1024]{1,0:T(8,128)}, f32[128,1024]{1,0:T(8,128)}, /*i...) custom-call(s32[4]{0:T(128)} %copy-done.11, bf16[4,128,512]{2,1,0:T(8,128)(2,1)} %copy-done.5, ...), custom_call_target="tpu_custom_call" | custom-call | tf_op jit(solution)/shard_map/grads/pallas_call | solution.py:54
  256.0 3.6 %all-to-all-done.3 = bf16[4,640,256]{2,1,0:T(8,128)(2,1)S(1)} async-done(((bf16[4,640,256]{2,1,0:T(8,128)(2,1)}), bf16[4,640,256]{2,1,0:T(8,128)(2,1)S(1)}, u32[]{:S(2)}, u32[]{:S(2)}) %all-to-all-start.3) | async-done | bytes 1310752 | tf_op jit(solution)/shard_map/rows_out/all_to_all | solution.py:972
  259.5 1.1 fusion.3
  (136 shorter events, 8.9 us)
Async XLA Ops:
  0.6 19.7 %copy-start = (bf16[8,16,3,1024]{3,1,2,0:T(8,128)(2,1)S(1)}, bf16[8,16,3,1024]{3,1,2,0:T(8,128)(2,1)}, u32[]{:S(2)}) copy-start(bf16[8,16,3,1024]{3,1,2,0:T(8,128)(2,1)} %param.35) | copy-start | bytes 2359300
  4.6 10.2 %copy-start.32 = (s32[4]{0:T(128)S(1)}, s32[4]{0:T(128)}, u32[]{:S(2)}) copy-start(s32[4]{0:T(128)} %param.24) | copy-start | bytes 52
  4.6 13.5 %copy-start.9 = (bf16[128,1024]{1,0:T(8,128)(2,1)S(1)}, bf16[128,1024]{1,0:T(8,128)(2,1)}, u32[]{:S(2)}) copy-start(bf16[128,1024]{1,0:T(8,128)(2,1)} %w1.1) | copy-start | bytes 786436
  4.6 13.5 %copy-start.10 = (bf16[1024,128]{1,0:T(8,128)(2,1)S(1)}, bf16[1024,128]{1,0:T(8,128)(2,1)}, u32[]{:S(2)}) copy-start(bf16[1024,128]{1,0:T(8,128)(2,1)} %w2.1) | copy-start | bytes 786436
  4.6 13.5 %copy-start.12 = (s32[4,256]{1,0:T(4,128)S(1)}, s32[4,256]{1,0:T(4,128)}, u32[]{:S(2)}) copy-start(s32[4,256]{1,0:T(4,128)} %mask.1) | copy-start | bytes 12292
  4.6 32.6 %all-to-all-start = ((bf16[4,656,256]{2,1,0:T(8,128)(2,1)}), bf16[4,656,256]{2,1,0:T(8,128)(2,1)}, u32[]{:S(2)}, u32[]{:S(2)}) async-start(bf16[4,656,256]{2,1,0:T(8,128)(2,1)} %get-tuple-element.78), calls=%async_computation | async-start | bytes 2686976 | tf_op jit(solution)/shard_map/all_to_all | solution.py:797
  9.1 12.4 %collective-permute-start.2 = (bf16[128,1024]{1,0:T(8,128)(2,1)S(1)}, bf16[128,1024]{1,0:T(8,128)(2,1)S(1)}, u32[]{:S(2)}, u32[]{:S(2)}) collective-permute-start(bf16[128,1024]{1,0:T(8,128)(2,1)S(1)} %copy-done.8), channel_id=1, source_target_pairs={{0,24},{1,25},{2,26},{3,27},{4,28},{5,29},{6,30},{7,31},{8,16},{9,... | collective-permute-start | bytes 786440 | tf_op jit(solution)/shard_map/q_high/ppermute | solution.py:75
  14.2 22.8 %collective-permute-start.1 = (bf16[128,1024]{1,0:T(8,128)(2,1)S(1)}, bf16[128,1024]{1,0:T(8,128)(2,1)S(1)}, u32[]{:S(2)}, u32[]{:S(2)}) collective-permute-start(bf16[128,1024]{1,0:T(8,128)(2,1)S(1)} %copy-done.8), channel_id=1, source_target_pairs={{0,16},{1,17},{2,18},{3,19},{4,20},{5,21},{6,22},{7,23},{8,24},{9,... | collective-permute-start | bytes 786440 | tf_op jit(solution)/shard_map/q_high/ppermute | solution.py:75
  14.2 22.8 %collective-permute-start = (bf16[128,1024]{1,0:T(8,128)(2,1)S(1)}, bf16[128,1024]{1,0:T(8,128)(2,1)S(1)}, u32[]{:S(2)}, u32[]{:S(2)}) collective-permute-start(bf16[128,1024]{1,0:T(8,128)(2,1)S(1)} %copy-done.8), channel_id=1, source_target_pairs={{0,8},{1,9},{2,10},{3,11},{4,12},{5,13},{6,14},{7,15},{8,0},{9,1},... | collective-permute-start | bytes 786440 | tf_op jit(solution)/shard_map/q_high/ppermute | solution.py:75
  18.1 19.1 %copy-start.11 = (s32[4]{0:T(128)}, s32[4]{0:T(128)S(1)}, u32[]{:S(2)}) copy-start(s32[4]{0:T(128)S(1)} %pad_add_fusion.3.sc.refs_0_) | copy-start | bytes 52
  37.2 48.6 %copy-start.2 = (bf16[4,128,1024]{2,1,0:T(8,128)(2,1)}, bf16[4,128,1024]{2,1,0:T(8,128)(2,1)S(1)}, u32[]{:S(2)}) copy-start(bf16[4,128,1024]{2,1,0:T(8,128)(2,1)S(1)} %q_high.1.refs_1_.refs_9_) | copy-start | bytes 3145732
  37.2 26.2 %collective-permute-start.4 = (bf16[4,128,1024]{2,1,0:T(8,128)(2,1)S(1)}, bf16[4,128,1024]{2,1,0:T(8,128)(2,1)S(1)}, u32[]{:S(2)}, u32[]{:S(2)}) collective-permute-start(bf16[4,128,1024]{2,1,0:T(8,128)(2,1)S(1)} %q_high.1.refs_1_.refs_9_), channel_id=1, source_target_pairs={{0,4},{1,3},{2,6},{3,1},{4,0},{5,7},{6,2},{7,5},{8,12},{9,11},{10,... | collective-permute-start | bytes 3145736 | tf_op jit(solution)/shard_map/q_two/ppermute | solution.py:75
  38.8 24.6 %collective-permute-start.3 = (bf16[4,128,1024]{2,1,0:T(8,128)(2,1)S(1)}, bf16[4,128,1024]{2,1,0:T(8,128)(2,1)S(1)}, u32[]{:S(2)}, u32[]{:S(2)}) collective-permute-start(bf16[4,128,1024]{2,1,0:T(8,128)(2,1)S(1)} %q_high.1.refs_1_.refs_9_), channel_id=1, source_target_pairs={{0,2},{1,5},{2,0},{3,7},{4,6},{5,1},{6,4},{7,3},{8,10},{9,13},{10,... | collective-permute-start | bytes 3145736 | tf_op jit(solution)/shard_map/q_one/ppermute | solution.py:75
  40.5 11.1 %collective-permute-start.7 = (bf16[128,1024]{1,0:T(8,128)(2,1)S(1)}, bf16[128,1024]{1,0:T(8,128)(2,1)S(1)}, u32[]{:S(2)}, u32[]{:S(2)}) collective-permute-start(bf16[128,1024]{1,0:T(8,128)(2,1)S(1)} %get-tuple-element.82.refs_0_), channel_id=1, source_target_pairs={{0,24},{1,25},{2,26},{3,27},{4,28},{5,29},{6,30},{7,31},{8,16},{9,... | collective-permute-start | bytes 786440 | tf_op jit(solution)/shard_map/fa_high/ppermute | solution.py:75
  43.0 20.4 %collective-permute-start.6 = (bf16[128,1024]{1,0:T(8,128)(2,1)S(1)}, bf16[128,1024]{1,0:T(8,128)(2,1)S(1)}, u32[]{:S(2)}, u32[]{:S(2)}) collective-permute-start(bf16[128,1024]{1,0:T(8,128)(2,1)S(1)} %get-tuple-element.82.refs_0_), channel_id=1, source_target_pairs={{0,16},{1,17},{2,18},{3,19},{4,20},{5,21},{6,22},{7,23},{8,24},{9,... | collective-permute-start | bytes 786440 | tf_op jit(solution)/shard_map/fa_high/ppermute | solution.py:75
  43.0 20.4 %collective-permute-start.5 = (bf16[128,1024]{1,0:T(8,128)(2,1)S(1)}, bf16[128,1024]{1,0:T(8,128)(2,1)S(1)}, u32[]{:S(2)}, u32[]{:S(2)}) collective-permute-start(bf16[128,1024]{1,0:T(8,128)(2,1)S(1)} %get-tuple-element.82.refs_0_), channel_id=1, source_target_pairs={{0,8},{1,9},{2,10},{3,11},{4,12},{5,13},{6,14},{7,15},{8,0},{9,1},... | collective-permute-start | bytes 786440 | tf_op jit(solution)/shard_map/fa_high/ppermute | solution.py:75
  63.4 22.4 %copy-start.13 = (bf16[4,128,1024]{2,1,0:T(8,128)(2,1)}, bf16[4,128,1024]{2,1,0:T(8,128)(2,1)S(1)}, u32[]{:S(2)}) copy-start(bf16[4,128,1024]{2,1,0:T(8,128)(2,1)S(1)} %collective-permute-done.4.refs_3_.refs_11_) | copy-start | bytes 3145732
  63.4 22.4 %copy-start.14 = (bf16[4,128,1024]{2,1,0:T(8,128)(2,1)}, bf16[4,128,1024]{2,1,0:T(8,128)(2,1)S(1)}, u32[]{:S(2)}) copy-start(bf16[4,128,1024]{2,1,0:T(8,128)(2,1)S(1)} %collective-permute-done.3.refs_2_.refs_10_) | copy-start | bytes 3145732
  63.4 14.9 %collective-permute-start.8 = (bf16[4,128,1024]{2,1,0:T(8,128)(2,1)S(1)}, bf16[4,128,1024]{2,1,0:T(8,128)(2,1)S(1)}, u32[]{:S(2)}, u32[]{:S(2)}) collective-permute-start(bf16[4,128,1024]{2,1,0:T(8,128)(2,1)S(1)} %collective-permute-done.3.refs_2_.refs_10_), channel_id=1, source_target_pairs={{0,4},{1,3},{2,6},{3,1},{4,0},{5,7},{6,2},{7,5},{8,12},{9,11},{10,... | collective-permute-start | bytes 3145736 | tf_op jit(solution)/shard_map/q_both/ppermute | solution.py:75
  64.7 13.8 %collective-permute-start.9 = (bf16[4,128,1024]{2,1,0:T(8,128)(2,1)S(1)}, bf16[4,128,1024]{2,1,0:T(8,128)(2,1)S(1)}, u32[]{:S(2)}, u32[]{:S(2)}) collective-permute-start(bf16[4,128,1024]{2,1,0:T(8,128)(2,1)S(1)} %q_high.1.refs_1_.refs_9_), channel_id=1, source_target_pairs={{0,1},{1,0},{2,3},{3,2},{4,5},{5,4},{6,7},{7,6},{8,9},{9,8},{10,11... | collective-permute-start | bytes 3145736 | tf_op jit(solution)/shard_map/q_core/ppermute | solution.py:75
  64.7 13.8 %collective-permute-start.11 = (bf16[4,128,1024]{2,1,0:T(8,128)(2,1)S(1)}, bf16[4,128,1024]{2,1,0:T(8,128)(2,1)S(1)}, u32[]{:S(2)}, u32[]{:S(2)}) collective-permute-start(bf16[4,128,1024]{2,1,0:T(8,128)(2,1)S(1)} %collective-permute-done.4.refs_3_.refs_11_), channel_id=1, source_target_pairs={{0,1},{1,0},{2,3},{3,2},{4,5},{5,4},{6,7},{7,6},{8,9},{9,8},{10,11... | collective-permute-start | bytes 3145736 | tf_op jit(solution)/shard_map/q_core/ppermute | solution.py:75
  65.2 13.3 %collective-permute-start.10 = (bf16[4,128,1024]{2,1,0:T(8,128)(2,1)S(1)}, bf16[4,128,1024]{2,1,0:T(8,128)(2,1)S(1)}, u32[]{:S(2)}, u32[]{:S(2)}) collective-permute-start(bf16[4,128,1024]{2,1,0:T(8,128)(2,1)S(1)} %collective-permute-done.3.refs_2_.refs_10_), channel_id=1, source_target_pairs={{0,1},{1,0},{2,3},{3,2},{4,5},{5,4},{6,7},{7,6},{8,9},{9,8},{10,11... | collective-permute-start | bytes 3145736 | tf_op jit(solution)/shard_map/q_core/ppermute | solution.py:75
  78.3 4.5 %collective-permute-start.12 = (bf16[4,128,1024]{2,1,0:T(8,128)(2,1)S(1)}, bf16[4,128,1024]{2,1,0:T(8,128)(2,1)S(1)}, u32[]{:S(2)}, u32[]{:S(2)}) collective-permute-start(bf16[4,128,1024]{2,1,0:T(8,128)(2,1)S(1)} %collective-permute-done.8.refs_4_.refs_12_), channel_id=1, source_target_pairs={{0,1},{1,0},{2,3},{3,2},{4,5},{5,4},{6,7},{7,6},{8,9},{9,8},{10,11... | collective-permute-start | bytes 3145736 | tf_op jit(solution)/shard_map/q_core/ppermute | solution.py:75
  78.4 27.3 %copy-start.3 = (bf16[4,128,1024]{2,1,0:T(8,128)(2,1)}, bf16[4,128,1024]{2,1,0:T(8,128)(2,1)S(1)}, u32[]{:S(2)}) copy-start(bf16[4,128,1024]{2,1,0:T(8,128)(2,1)S(1)} %fa_high.1.refs_1_) | copy-start | bytes 3145732
  78.5 26.1 %collective-permute-start.19 = (bf16[4,128,1024]{2,1,0:T(8,128)(2,1)S(1)}, bf16[4,128,1024]{2,1,0:T(8,128)(2,1)}, u32[]{:S(2)}, u32[]{:S(2)}) collective-permute-start(bf16[4,128,1024]{2,1,0:T(8,128)(2,1)S(1)} %fa_high.1.refs_1_), channel_id=1, source_target_pairs={{0,4},{1,3},{2,6},{3,1},{4,0},{5,7},{6,2},{7,5},{8,12},{9,11},{10,... | collective-permute-start | bytes 3145736 | tf_op jit(solution)/shard_map/fa_two/ppermute | solution.py:75
  79.7 24.8 %collective-permute-start.18 = (bf16[4,128,1024]{2,1,0:T(8,128)(2,1)S(1)}, bf16[4,128,1024]{2,1,0:T(8,128)(2,1)}, u32[]{:S(2)}, u32[]{:S(2)}) collective-permute-start(bf16[4,128,1024]{2,1,0:T(8,128)(2,1)S(1)} %fa_high.1.refs_1_), channel_id=1, source_target_pairs={{0,2},{1,5},{2,0},{3,7},{4,6},{5,1},{6,4},{7,3},{8,10},{9,13},{10,... | collective-permute-start | bytes 3145736 | tf_op jit(solution)/shard_map/fa_one/ppermute | solution.py:75
  80.3 23.4 %collective-permute-start.15 = (bf16[128,1024]{1,0:T(8,128)(2,1)S(1)}, bf16[128,1024]{1,0:T(8,128)(2,1)S(1)}, u32[]{:S(2)}, u32[]{:S(2)}) collective-permute-start(bf16[128,1024]{1,0:T(8,128)(2,1)S(1)} %get-tuple-element.91.refs_0_), channel_id=1, source_target_pairs={{0,24},{1,25},{2,26},{3,27},{4,28},{5,29},{6,30},{7,31},{8,16},{9,... | collective-permute-start | bytes 786440 | tf_op jit(solution)/shard_map/fb_high/ppermute | solution.py:75
  82.8 21.6 %collective-permute-start.14 = (bf16[128,1024]{1,0:T(8,128)(2,1)S(1)}, bf16[128,1024]{1,0:T(8,128)(2,1)S(1)}, u32[]{:S(2)}, u32[]{:S(2)}) collective-permute-start(bf16[128,1024]{1,0:T(8,128)(2,1)S(1)} %get-tuple-element.91.refs_0_), channel_id=1, source_target_pairs={{0,16},{1,17},{2,18},{3,19},{4,20},{5,21},{6,22},{7,23},{8,24},{9,... | collective-permute-start | bytes 786440 | tf_op jit(solution)/shard_map/fb_high/ppermute | solution.py:75
  83.9 20.6 %collective-permute-start.13 = (bf16[128,1024]{1,0:T(8,128)(2,1)S(1)}, bf16[128,1024]{1,0:T(8,128)(2,1)S(1)}, u32[]{:S(2)}, u32[]{:S(2)}) collective-permute-start(bf16[128,1024]{1,0:T(8,128)(2,1)S(1)} %get-tuple-element.91.refs_0_), channel_id=1, source_target_pairs={{0,8},{1,9},{2,10},{3,11},{4,12},{5,13},{6,14},{7,15},{8,0},{9,1},... | collective-permute-start | bytes 786440 | tf_op jit(solution)/shard_map/fb_high/ppermute | solution.py:75
  104.6 15.1 %collective-permute-start.26 = (bf16[4,128,1024]{2,1,0:T(8,128)(2,1)}, bf16[4,128,1024]{2,1,0:T(8,128)(2,1)}, u32[]{:S(2)}, u32[]{:S(2)}) collective-permute-start(bf16[4,128,1024]{2,1,0:T(8,128)(2,1)} %collective-permute-done.18.refs_2_), channel_id=1, source_target_pairs={{0,4},{1,3},{2,6},{3,1},{4,0},{5,7},{6,2},{7,5},{8,12},{9,11},{10,... | collective-permute-start | bytes 3145736 | tf_op jit(solution)/shard_map/fa_both/ppermute | solution.py:75
  105.7 14.5 %collective-permute-start.20 = (bf16[4,128,1024]{2,1,0:T(8,128)(2,1)S(1)}, bf16[4,128,1024]{2,1,0:T(8,128)(2,1)}, u32[]{:S(2)}, u32[]{:S(2)}) collective-permute-start(bf16[4,128,1024]{2,1,0:T(8,128)(2,1)S(1)} %fa_high.1.refs_1_), channel_id=1, source_target_pairs={{0,1},{1,0},{2,3},{3,2},{4,5},{5,4},{6,7},{7,6},{8,9},{9,8},{10,11... | collective-permute-start | bytes 3145736 | tf_op jit(solution)/shard_map/fa_core/ppermute | solution.py:75
  105.7 14.5 %collective-permute-start.22 = (bf16[4,128,1024]{2,1,0:T(8,128)(2,1)}, bf16[4,128,1024]{2,1,0:T(8,128)(2,1)}, u32[]{:S(2)}, u32[]{:S(2)}) collective-permute-start(bf16[4,128,1024]{2,1,0:T(8,128)(2,1)} %collective-permute-done.19.refs_3_), channel_id=1, source_target_pairs={{0,1},{1,0},{2,3},{3,2},{4,5},{5,4},{6,7},{7,6},{8,9},{9,8},{10,11... | collective-permute-start | bytes 3145736 | tf_op jit(solution)/shard_map/fa_core/ppermute | solution.py:75
  106.2 14.0 %collective-permute-start.21 = (bf16[4,128,1024]{2,1,0:T(8,128)(2,1)}, bf16[4,128,1024]{2,1,0:T(8,128)(2,1)}, u32[]{:S(2)}, u32[]{:S(2)}) collective-permute-start(bf16[4,128,1024]{2,1,0:T(8,128)(2,1)} %collective-permute-done.18.refs_2_), channel_id=1, source_target_pairs={{0,1},{1,0},{2,3},{3,2},{4,5},{5,4},{6,7},{7,6},{8,9},{9,8},{10,11... | collective-permute-start | bytes 3145736 | tf_op jit(solution)/shard_map/fa_core/ppermute | solution.py:75
  106.4 41.2 %copy-start.4 = (bf16[4,128,1024]{2,1,0:T(8,128)(2,1)}, bf16[4,128,1024]{2,1,0:T(8,128)(2,1)S(1)}, u32[]{:S(2)}) copy-start(bf16[4,128,1024]{2,1,0:T(8,128)(2,1)S(1)} %fb_high.1.refs_1_) | copy-start | bytes 3145732
  106.4 4.5 %collective-permute-start.16 = (s32[4]{0:T(128)S(1)}, s32[4]{0:T(128)S(1)}, u32[]{:S(2)}, u32[]{:S(2)}) collective-permute-start(s32[4]{0:T(128)S(1)} %copy-done.32), channel_id=1, source_target_pairs={{0,16},{1,17},{2,18},{3,19},{4,20},{5,21},{6,22},{7,23},{8,24},{9,... | collective-permute-start | bytes 56 | tf_op jit(solution)/shard_map/ppermute | solution.py:75
  111.5 3.6 %collective-permute-start.17 = (s32[2,4]{1,0:T(2,128)S(1)}, s32[2,4]{1,0:T(2,128)S(1)}, u32[]{:S(2)}, u32[]{:S(2)}) collective-permute-start(s32[2,4]{1,0:T(2,128)S(1)} %gather_fusion), channel_id=1, source_target_pairs={{0,8},{1,9},{2,10},{3,11},{4,12},{5,13},{6,14},{7,15},{8,0},{9,1},... | collective-permute-start | bytes 104 | tf_op jit(solution)/shard_map/ppermute | solution.py:75
  119.7 4.1 %collective-permute-start.27 = (bf16[4,128,1024]{2,1,0:T(8,128)(2,1)}, bf16[4,128,1024]{2,1,0:T(8,128)(2,1)}, u32[]{:S(2)}, u32[]{:S(2)}) collective-permute-start(bf16[4,128,1024]{2,1,0:T(8,128)(2,1)} %collective-permute-done.26.refs_4_), channel_id=1, source_target_pairs={{0,1},{1,0},{2,3},{3,2},{4,5},{5,4},{6,7},{7,6},{8,9},{9,8},{10,11... | collective-permute-start | bytes 3145736 | tf_op jit(solution)/shard_map/fa_core/ppermute | solution.py:75
  120.3 25.6 %collective-permute-start.24 = (bf16[4,128,1024]{2,1,0:T(8,128)(2,1)S(1)}, bf16[4,128,1024]{2,1,0:T(8,128)(2,1)S(1)}, u32[]{:S(2)}, u32[]{:S(2)}) collective-permute-start(bf16[4,128,1024]{2,1,0:T(8,128)(2,1)S(1)} %fb_high.1.refs_1_), channel_id=1, source_target_pairs={{0,4},{1,3},{2,6},{3,1},{4,0},{5,7},{6,2},{7,5},{8,12},{9,11},{10,... | collective-permute-start | bytes 3145736 | tf_op jit(solution)/shard_map/fb_two/ppermute | solution.py:75
  121.5 24.4 %collective-permute-start.23 = (bf16[4,128,1024]{2,1,0:T(8,128)(2,1)S(1)}, bf16[4,128,1024]{2,1,0:T(8,128)(2,1)S(1)}, u32[]{:S(2)}, u32[]{:S(2)}) collective-permute-start(bf16[4,128,1024]{2,1,0:T(8,128)(2,1)S(1)} %fb_high.1.refs_1_), channel_id=1, source_target_pairs={{0,2},{1,5},{2,0},{3,7},{4,6},{5,1},{6,4},{7,3},{8,10},{9,13},{10,... | collective-permute-start | bytes 3145736 | tf_op jit(solution)/shard_map/fb_one/ppermute | solution.py:75
  122.2 23.6 %collective-permute-start.25 = (s32[2,2,4]{2,1,0:T(2,128)S(1)}, s32[2,2,4]{2,1,0:T(2,128)S(1)}, u32[]{:S(2)}, u32[]{:S(2)}) collective-permute-start(s32[2,2,4]{2,1,0:T(2,128)S(1)} %gather_fusion.1), channel_id=1, source_target_pairs={{0,4},{1,5},{2,6},{3,7},{4,0},{5,1},{6,2},{7,3},{8,12},{9,13},{10,... | collective-permute-start | bytes 200 | tf_op jit(solution)/shard_map/ppermute | solution.py:75
  145.9 18.6 %copy-start.20 = (bf16[4,128,1024]{2,1,0:T(8,128)(2,1)}, bf16[4,128,1024]{2,1,0:T(8,128)(2,1)S(1)}, u32[]{:S(2)}) copy-start(bf16[4,128,1024]{2,1,0:T(8,128)(2,1)S(1)} %collective-permute-done.24.refs_3_) | copy-start | bytes 3145732
  145.9 18.5 %copy-start.21 = (bf16[4,128,1024]{2,1,0:T(8,128)(2,1)}, bf16[4,128,1024]{2,1,0:T(8,128)(2,1)S(1)}, u32[]{:S(2)}) copy-start(bf16[4,128,1024]{2,1,0:T(8,128)(2,1)S(1)} %collective-permute-done.23.refs_2_) | copy-start | bytes 3145732
  145.9 14.8 %collective-permute-start.28 = (bf16[4,128,1024]{2,1,0:T(8,128)(2,1)S(1)}, bf16[4,128,1024]{2,1,0:T(8,128)(2,1)S(1)}, u32[]{:S(2)}, u32[]{:S(2)}) collective-permute-start(bf16[4,128,1024]{2,1,0:T(8,128)(2,1)S(1)} %collective-permute-done.23.refs_2_), channel_id=1, source_target_pairs={{0,4},{1,3},{2,6},{3,1},{4,0},{5,7},{6,2},{7,5},{8,12},{9,11},{10,... | collective-permute-start | bytes 3145736 | tf_op jit(solution)/shard_map/fb_both/ppermute | solution.py:75
  147.6 13.1 %collective-permute-start.30 = (bf16[4,128,1024]{2,1,0:T(8,128)(2,1)S(1)}, bf16[4,128,1024]{2,1,0:T(8,128)(2,1)S(1)}, u32[]{:S(2)}, u32[]{:S(2)}) collective-permute-start(bf16[4,128,1024]{2,1,0:T(8,128)(2,1)S(1)} %collective-permute-done.23.refs_2_), channel_id=1, source_target_pairs={{0,1},{1,0},{2,3},{3,2},{4,5},{5,4},{6,7},{7,6},{8,9},{9,8},{10,11... | collective-permute-start | bytes 3145736 | tf_op jit(solution)/shard_map/fb_core/ppermute | solution.py:75
  147.6 13.1 %collective-permute-start.29 = (bf16[4,128,1024]{2,1,0:T(8,128)(2,1)S(1)}, bf16[4,128,1024]{2,1,0:T(8,128)(2,1)S(1)}, u32[]{:S(2)}, u32[]{:S(2)}) collective-permute-start(bf16[4,128,1024]{2,1,0:T(8,128)(2,1)S(1)} %fb_high.1.refs_1_), channel_id=1, source_target_pairs={{0,1},{1,0},{2,3},{3,2},{4,5},{5,4},{6,7},{7,6},{8,9},{9,8},{10,11... | collective-permute-start | bytes 3145736 | tf_op jit(solution)/shard_map/fb_core/ppermute | solution.py:75
  148.2 12.6 %collective-permute-start.31 = (bf16[4,128,1024]{2,1,0:T(8,128)(2,1)S(1)}, bf16[4,128,1024]{2,1,0:T(8,128)(2,1)S(1)}, u32[]{:S(2)}, u32[]{:S(2)}) collective-permute-start(bf16[4,128,1024]{2,1,0:T(8,128)(2,1)S(1)} %collective-permute-done.24.refs_3_), channel_id=1, source_target_pairs={{0,1},{1,0},{2,3},{3,2},{4,5},{5,4},{6,7},{7,6},{8,9},{9,8},{10,11... | collective-permute-start | bytes 3145736 | tf_op jit(solution)/shard_map/fb_core/ppermute | solution.py:75
  160.7 2.7 %collective-permute-start.32 = (bf16[4,128,1024]{2,1,0:T(8,128)(2,1)S(1)}, bf16[4,128,1024]{2,1,0:T(8,128)(2,1)S(1)}, u32[]{:S(2)}, u32[]{:S(2)}) collective-permute-start(bf16[4,128,1024]{2,1,0:T(8,128)(2,1)S(1)} %collective-permute-done.28.refs_4_), channel_id=1, source_target_pairs={{0,1},{1,0},{2,3},{3,2},{4,5},{5,4},{6,7},{7,6},{8,9},{9,8},{10,11... | collective-permute-start | bytes 3145736 | tf_op jit(solution)/shard_map/fb_core/ppermute | solution.py:75
  183.6 16.8 %all-to-all-start.1 = ((bf16[32,16,384]{2,1,0:T(8,128)(2,1)}), bf16[32,16,384]{2,1,0:T(8,128)(2,1)S(1)}, u32[]{:S(2)}, u32[]{:S(2)}) async-start(bf16[32,16,384]{2,1,0:T(8,128)(2,1)} %get-tuple-element.123), calls=%async_computation.1 | async-start | bytes 786432 | tf_op jit(solution)/shard_map/grads_b_send/all_to_all | solution.py:698
  201.2 7.3 %collective-permute-start.33 = (bf16[128,384]{1,0:T(8,128)(2,1)S(1)}, bf16[128,384]{1,0:T(8,128)(2,1)S(1)}, u32[]{:S(2)}, u32[]{:S(2)}) collective-permute-start(bf16[128,384]{1,0:T(8,128)(2,1)S(1)} %bitcast.43), channel_id=1, source_target_pairs={{0,16},{1,17},{2,18},{3,19},{4,20},{5,21},{6,22},{7,23},{8,24},{9,... | collective-permute-start | bytes 294920 | tf_op jit(solution)/shard_map/grads_b/ppermute | solution.py:75
  202.3 12.0 %all-to-all-start.2 = ((bf16[32,16,128]{2,1,0:T(8,128)(2,1)}), bf16[32,16,128]{2,1,0:T(8,128)(2,1)S(1)}, u32[]{:S(2)}, u32[]{:S(2)}) async-start(bf16[32,16,128]{2,1,0:T(8,128)(2,1)} %get-tuple-element.124), calls=%async_computation.2 | async-start | bytes 262144 | tf_op jit(solution)/shard_map/grads_c_send/all_to_all | solution.py:698
  208.7 13.3 %collective-permute-start.34 = (bf16[2,128,384]{2,1,0:T(8,128)(2,1)S(1)}, bf16[2,128,384]{2,1,0:T(8,128)(2,1)S(1)}, u32[]{:S(2)}, u32[]{:S(2)}) collective-permute-start(bf16[2,128,384]{2,1,0:T(8,128)(2,1)S(1)} %grads_b.7), channel_id=1, source_target_pairs={{0,8},{1,9},{2,10},{3,11},{4,12},{5,13},{6,14},{7,15},{8,0},{9,1},... | collective-permute-start | bytes 589832 | tf_op jit(solution)/shard_map/grads_b/ppermute | solution.py:75
  215.0 6.0 %collective-permute-start.37 = (bf16[128,128]{1,0:T(8,128)(2,1)S(1)}, bf16[128,128]{1,0:T(8,128)(2,1)S(1)}, u32[]{:S(2)}, u32[]{:S(2)}) collective-permute-start(bf16[128,128]{1,0:T(8,128)(2,1)S(1)} %bitcast.46), channel_id=1, source_target_pairs={{0,24},{1,25},{2,26},{3,27},{4,28},{5,29},{6,30},{7,31},{8,16},{9,... | collective-permute-start | bytes 98312 | tf_op jit(solution)/shard_map/grads_b/ppermute | solution.py:75
  216.3 5.5 %collective-permute-start.36 = (bf16[128,128]{1,0:T(8,128)(2,1)S(1)}, bf16[128,128]{1,0:T(8,128)(2,1)S(1)}, u32[]{:S(2)}, u32[]{:S(2)}) collective-permute-start(bf16[128,128]{1,0:T(8,128)(2,1)S(1)} %bitcast.47), channel_id=1, source_target_pairs={{0,16},{1,17},{2,18},{3,19},{4,20},{5,21},{6,22},{7,23},{8,24},{9,... | collective-permute-start | bytes 98312 | tf_op jit(solution)/shard_map/grads_b/ppermute | solution.py:75
  217.2 4.6 %collective-permute-start.35 = (bf16[128,128]{1,0:T(8,128)(2,1)S(1)}, bf16[128,128]{1,0:T(8,128)(2,1)S(1)}, u32[]{:S(2)}, u32[]{:S(2)}) collective-permute-start(bf16[128,128]{1,0:T(8,128)(2,1)S(1)} %bitcast.48), channel_id=1, source_target_pairs={{0,8},{1,9},{2,10},{3,11},{4,12},{5,13},{6,14},{7,15},{8,0},{9,1},... | collective-permute-start | bytes 98312 | tf_op jit(solution)/shard_map/grads_b/ppermute | solution.py:75
  222.7 13.9 %copy-start.5 = (bf16[4,128,512]{2,1,0:T(8,128)(2,1)}, bf16[4,128,512]{2,1,0:T(8,128)(2,1)S(1)}, u32[]{:S(2)}) copy-start(bf16[4,128,512]{2,1,0:T(8,128)(2,1)S(1)} %grads_b.11.refs_1_) | copy-start | bytes 1572868
  222.7 13.9 %collective-permute-start.39 = (bf16[4,128,512]{2,1,0:T(8,128)(2,1)S(1)}, bf16[4,128,512]{2,1,0:T(8,128)(2,1)S(1)}, u32[]{:S(2)}, u32[]{:S(2)}) collective-permute-start(bf16[4,128,512]{2,1,0:T(8,128)(2,1)S(1)} %grads_b.11.refs_1_), channel_id=1, source_target_pairs={{0,4},{1,3},{2,6},{3,1},{4,0},{5,7},{6,2},{7,5},{8,12},{9,11},{10,... | collective-permute-start | bytes 1572872 | tf_op jit(solution)/shard_map/grads/ppermute | solution.py:75
  223.3 13.4 %collective-permute-start.38 = (bf16[4,128,512]{2,1,0:T(8,128)(2,1)S(1)}, bf16[4,128,512]{2,1,0:T(8,128)(2,1)S(1)}, u32[]{:S(2)}, u32[]{:S(2)}) collective-permute-start(bf16[4,128,512]{2,1,0:T(8,128)(2,1)S(1)} %grads_b.11.refs_1_), channel_id=1, source_target_pairs={{0,2},{1,5},{2,0},{3,7},{4,6},{5,1},{6,4},{7,3},{8,10},{9,13},{10,... | collective-permute-start | bytes 1572872 | tf_op jit(solution)/shard_map/grads/ppermute | solution.py:75
  236.6 2.1 collective-permute-start.40
  236.7 9.4 %collective-permute-start.41 = (bf16[4,128,512]{2,1,0:T(8,128)(2,1)S(1)}, bf16[4,128,512]{2,1,0:T(8,128)(2,1)}, u32[]{:S(2)}, u32[]{:S(2)}) collective-permute-start(bf16[4,128,512]{2,1,0:T(8,128)(2,1)S(1)} %collective-permute-done.38.refs_2_), channel_id=1, source_target_pairs={{0,4},{1,3},{2,6},{3,1},{4,0},{5,7},{6,2},{7,5},{8,12},{9,11},{10,... | collective-permute-start | bytes 1572872 | tf_op jit(solution)/shard_map/grads/ppermute | solution.py:75
  238.8 20.8 %all-to-all-start.3 = ((bf16[4,640,256]{2,1,0:T(8,128)(2,1)}), bf16[4,640,256]{2,1,0:T(8,128)(2,1)S(1)}, u32[]{:S(2)}, u32[]{:S(2)}) async-start(bf16[4,640,256]{2,1,0:T(8,128)(2,1)} %shard_map.282), calls=%async_computation.3 | async-start | bytes 2621440 | tf_op jit(solution)/shard_map/rows_out/all_to_all | solution.py:972
  242.3 3.8 %collective-permute-start.42 = (bf16[4,128,512]{2,1,0:T(8,128)(2,1)S(1)}, bf16[4,128,512]{2,1,0:T(8,128)(2,1)S(1)}, u32[]{:S(2)}, u32[]{:S(2)}) collective-permute-start(bf16[4,128,512]{2,1,0:T(8,128)(2,1)S(1)} %collective-permute-done.38.refs_2_), channel_id=1, source_target_pairs={{0,1},{1,0},{2,3},{3,2},{4,5},{5,4},{6,7},{7,6},{8,9},{9,8},{10,11... | collective-permute-start | bytes 1572872 | tf_op jit(solution)/shard_map/grads/ppermute | solution.py:75
  242.8 3.3 %collective-permute-start.43 = (bf16[4,128,512]{2,1,0:T(8,128)(2,1)S(1)}, bf16[4,128,512]{2,1,0:T(8,128)(2,1)S(1)}, u32[]{:S(2)}, u32[]{:S(2)}) collective-permute-start(bf16[4,128,512]{2,1,0:T(8,128)(2,1)S(1)} %collective-permute-done.39.refs_3_), channel_id=1, source_target_pairs={{0,1},{1,0},{2,3},{3,2},{4,5},{5,4},{6,7},{7,6},{8,9},{9,8},{10,11... | collective-permute-start | bytes 1572872 | tf_op jit(solution)/shard_map/grads/ppermute | solution.py:75
  246.1 2.1 collective-permute-start.44
  249.0 11.6 %copy-start.1 = (bf16[8,16,3,1024]{3,1,2,0:T(8,128)(2,1)S(1)}, bf16[8,16,3,1024]{3,1,2,0:T(8,128)(2,1)}, u32[]{:S(2)}) copy-start(bf16[8,16,3,1024]{3,1,2,0:T(8,128)(2,1)} %param.35) | copy-start | bytes 2359300
  (18 other events, 61.8 us)

commit v8 on v7

--- a/solution.py
+++ b/solution.py
@@ -290,7 +290,7 @@
         rows[c, seq : 2 * seq] = grads[c]
         rows[c, 2 * seq : 2 * seq + 2] = bias_qv[...]
         for i in range(4):
-            rows[c, 2 * seq + 2 + i : 2 * seq + 3 + i] = bias_f[:, i * hid : (i + 1) * hid]
+            rows[c, 2 * seq + 2 + i, :] = bias_f[pl.ds(i * hid, hid)]
     for c in range(3):
         out[:, c * hid : (c + 1) * hid] = wq[c]
     out[:, 3 * hid :] = low(wp[...].astype(F32).T)
@@ -788,7 +788,7 @@
         prep_q_kernel,
         [jax.ShapeDtypeStruct((cols, 2 * SEQ + EXTRA, hid), BF), shard],
         [tokens_in.reshape(cols, SEQ, hid), grad_out.reshape(cols, SEQ, hid), bias_qv]
-        + [bias_fc1.reshape(1, n), w_qkv, w_proj],
+        + [bias_fc1, w_qkv, w_proj],
         [VMEM] * 6,
         mib=56,
     )

time: 261 us -> 260 us (level)
  no operation moved by 1% of the time
where the time goes in v8:
time: 260 us; the launch traced here: 259 us
  waiting for transfers between devices  107 us (41%)
  Pallas kernels  87.6 us (34%)
  starting transfers between devices  52.4 us (20%)
  local copies, waits for them, and re-layouts  8.48 us (3%)
  between operations  3.19 us (1%)
    ppermute x45, waiting for transfers between devices, swap(): return lax.ppermute(block, BOTH, pairs)  96.2 us
    pallas_call x17, Pallas kernels, call(): pl.pallas_call(kernel, out_shape=outs, in_specs=[pl.BlockSpec(memory_spac...  87.6 us
    ppermute x45, starting transfers between devices, swap(): return lax.ppermute(block, BOTH, pairs)  37 us
    all_to_all x2, starting transfers between devices, send_grads(): return lax.all_to_all(grads, BOTH, split_axis=0, concat_axis=0, tiled=True)  7.35 us
    all_to_all x2, waiting for transfers between devices, send_grads(): return lax.all_to_all(grads, BOTH, split_axis=0, concat_axis=0, tiled=True)  7.15 us
  transfers between devices with their start and end apart: 49, of which 24 were waited for; matrix products, arithmetic and copies ran while one was open for 1% of the time, Pallas kernels for 25%

profile of v8, /device:TPU:0, one launch (start us, length us, event | category | flops | bytes accessed | tf_op | source)
XLA Modules:
  0.0 259.4 jit_solution(18327927666474596304)
XLA Ops:
  0.7 2.7 %shard_map.276 = (bf16[4,656,256]{2,1,0:T(8,128)(2,1)}, bf16[128,1024]{1,0:T(8,128)(2,1)}) custom-call(bf16[4,320,256]{2,1,0:T(8,128)(2,1)} %bitcast.52, bf16[4,320,256]{2,1,0:T(8,128)(2,1)} %bitcast.53, bf16[2,256]{1,0:T(2,128)(2,1)} %bias_qv.1, bf16[1024]{0:T(1024)(128)(2,1)} %bias_f.1, bf16[3,128,256]{2,1,0:T(8,128)(2,1)} %wq.1, bf16[256,128]{1,0:T(8,128)(2,1)} %wp.1), custom_call_target="tpu_custom_call" | custom-call | tf_op jit(solution)/shard_map/pallas_call | solution.py:54
  3.4 4.4 %all-to-all-start = ((bf16[4,656,256]{2,1,0:T(8,128)(2,1)}), bf16[4,656,256]{2,1,0:T(8,128)(2,1)}, u32[]{:S(2)}, u32[]{:S(2)}) async-start(bf16[4,656,256]{2,1,0:T(8,128)(2,1)} %get-tuple-element.78), calls=%async_computation | async-start | bytes 2686976 | tf_op jit(solution)/shard_map/all_to_all | solution.py:797
  7.8 5.1 %collective-permute-start.2 = (bf16[128,1024]{1,0:T(8,128)(2,1)S(1)}, bf16[128,1024]{1,0:T(8,128)(2,1)S(1)}, u32[]{:S(2)}, u32[]{:S(2)}) collective-permute-start(bf16[128,1024]{1,0:T(8,128)(2,1)S(1)} %copy-done.8), channel_id=1, source_target_pairs={{0,24},{1,25},{2,26},{3,27},{4,28},{5,29},{6,30},{7,31},{8,16},{9,... | collective-permute-start | bytes 786440 | tf_op jit(solution)/shard_map/q_high/ppermute | solution.py:75
  13.0 0.6 collective-permute-start
  16.1 0.7 pad_add_fusion.3.sc.refs_0_
  16.9 0.8 shard_map.277
  17.7 0.7 copy-done.6
  18.4 0.7 copy-done.7
  19.0 0.6 dynamic-slice_bitcast_fusion.refs_14_.refs_9_
  20.2 15.6 %collective-permute-done.1.refs_2_ = bf16[128,1024]{1,0:T(8,128)(2,1)S(1)} collective-permute-done((bf16[128,1024]{1,0:T(8,128)(2,1)S(1)}, bf16[128,1024]{1,0:T(8,128)(2,1)S(1)}, u32[]{:S(2)}, u32[]{:S(2)}) %collective-permute-start.1) | collective-permute-done | bytes 262176 | tf_op jit(solution)/shard_map/q_high/ppermute | solution.py:75
  36.0 1.6 collective-permute-start.4
  37.5 1.7 collective-permute-start.3
  39.2 2.5 collective-permute-start.7
  41.7 1.9 collective-permute-start.5
  43.6 6.8 %collective-permute-done.7.refs_3_ = bf16[128,1024]{1,0:T(8,128)(2,1)S(1)} collective-permute-done((bf16[128,1024]{1,0:T(8,128)(2,1)S(1)}, bf16[128,1024]{1,0:T(8,128)(2,1)S(1)}, u32[]{:S(2)}, u32[]{:S(2)}) %collective-permute-start.7) | collective-permute-done | bytes 262176 | tf_op jit(solution)/shard_map/fa_high/ppermute | solution.py:75
  50.4 11.8 %collective-permute-done.6.refs_2_ = bf16[128,1024]{1,0:T(8,128)(2,1)S(1)} collective-permute-done((bf16[128,1024]{1,0:T(8,128)(2,1)S(1)}, bf16[128,1024]{1,0:T(8,128)(2,1)S(1)}, u32[]{:S(2)}, u32[]{:S(2)}) %collective-permute-start.6) | collective-permute-done | bytes 262176 | tf_op jit(solution)/shard_map/fa_high/ppermute | solution.py:75
  62.2 1.2 collective-permute-start.8
  63.9 13.1 %collective-permute-done.8.refs_4_.refs_12_ = bf16[4,128,1024]{2,1,0:T(8,128)(2,1)S(1)} collective-permute-done((bf16[4,128,1024]{2,1,0:T(8,128)(2,1)S(1)}, bf16[4,128,1024]{2,1,0:T(8,128)(2,1)S(1)}, u32[]{:S(2)}, u32[]{:S(2)}) %collective-permute-start.8) | collective-permute-done | bytes 1048608 | tf_op jit(solution)/shard_map/q_both/ppermute | solution.py:75
  77.2 1.2 collective-permute-start.19
  78.5 0.6 collective-permute-start.18
  79.0 2.5 collective-permute-start.15
  81.6 1.0 copy-done.19
  82.6 1.9 collective-permute-start.13
  84.5 18.0 %shard_map.278 = (bf16[320,1024]{1,0:T(8,128)(2,1)}, bf16[320,16]{1,0:T(8,128)(2,1)}, bf16[320,1024]{1,0:T(8,128)(2,1)}, bf16[320,1024]{1,0:T(8,128)(2,1)}, bf16...) custom-call(s32[4]{0:T(128)} %copy-done.11, ...), custom_call_target="tpu_custom_call" | custom-call | tf_op jit(solution)/shard_map/pallas_call | solution.py:54
  102.5 0.7 collective-permute-done.14.refs_2_
  103.3 1.2 collective-permute-start.26
  105.2 4.4 %collective-permute-done.16 = s32[4]{0:T(128)S(1)} collective-permute-done((s32[4]{0:T(128)S(1)}, s32[4]{0:T(128)S(1)}, u32[]{:S(2)}, u32[]{:S(2)}) %collective-permute-start.16) | collective-permute-done | bytes 48 | tf_op jit(solution)/shard_map/ppermute | solution.py:75
  110.4 3.4 %collective-permute-done.17 = s32[2,4]{1,0:T(2,128)S(1)} collective-permute-done((s32[2,4]{1,0:T(2,128)S(1)}, s32[2,4]{1,0:T(2,128)S(1)}, u32[]{:S(2)}, u32[]{:S(2)}) %collective-permute-start.17) | collective-permute-done | bytes 64 | tf_op jit(solution)/shard_map/ppermute | solution.py:75
  113.9 4.6 %collective-permute-done.26.refs_4_ = bf16[4,128,1024]{2,1,0:T(8,128)(2,1)} collective-permute-done((bf16[4,128,1024]{2,1,0:T(8,128)(2,1)}, bf16[4,128,1024]{2,1,0:T(8,128)(2,1)}, u32[]{:S(2)}, u32[]{:S(2)}) %collective-permute-start.26) | collective-permute-done | bytes 1048608 | tf_op jit(solution)/shard_map/fa_both/ppermute | solution.py:75
  119.0 1.2 collective-permute-start.24
  120.2 0.7 collective-permute-start.23
  120.9 1.5 collective-permute-start.25
  122.5 15.4 %shard_map.279 = (f32[320,1024]{1,0:T(8,128)}, f32[320,1024]{1,0:T(8,128)}, f32[320,16]{1,0:T(8,128)}, f32[320,16]{1,0:T(8,128)}, bf16[320,1024]{1,0:T(8,128)(2,1)}, /*index=5*/bf16[32,16,128]{2,1,0:T(8,128)(2,1)}) custom-call(s32[4]{0:T(128)} %copy-done.11, bf16[4,128,1024]{2,1,0:T(8,128)(2,1)} %copy-done.3, ...), custom_call_target="tpu_custom_call" | custom-call | tf_op jit(solution)/shard_map/pallas_call | solution.py:54
  137.9 6.7 %collective-permute-done.25 = s32[2,2,4]{2,1,0:T(2,128)S(1)} collective-permute-done((s32[2,2,4]{2,1,0:T(2,128)S(1)}, s32[2,2,4]{2,1,0:T(2,128)S(1)}, u32[]{:S(2)}, u32[]{:S(2)}) %collective-permute-start.25) | collective-permute-done | bytes 96 | tf_op jit(solution)/shard_map/ppermute | solution.py:75
  144.6 1.7 collective-permute-start.28
  146.9 12.6 %collective-permute-done.28.refs_4_ = bf16[4,128,1024]{2,1,0:T(8,128)(2,1)S(1)} collective-permute-done((bf16[4,128,1024]{2,1,0:T(8,128)(2,1)S(1)}, bf16[4,128,1024]{2,1,0:T(8,128)(2,1)S(1)}, u32[]{:S(2)}, u32[]{:S(2)}) %collective-permute-start.28) | collective-permute-done | bytes 1048608 | tf_op jit(solution)/shard_map/fb_both/ppermute | solution.py:75
  159.5 2.6 %collective-permute-done.32.refs_8_ = bf16[4,128,1024]{2,1,0:T(8,128)(2,1)S(1)} collective-permute-done((bf16[4,128,1024]{2,1,0:T(8,128)(2,1)S(1)}, bf16[4,128,1024]{2,1,0:T(8,128)(2,1)S(1)}, u32[]{:S(2)}, u32[]{:S(2)}) %collective-permute-start.32) | collective-permute-done | bytes 1048608 | tf_op jit(solution)/shard_map/fb_core/ppermute | solution.py:75
  162.1 1.0 copy-done.26
  163.2 19.2 %shard_map.280 = (bf16[4,320,256]{2,1,0:T(8,128)(2,1)}, bf16[320,1024]{1,0:T(8,128)(2,1)}, f32[320,1024]{1,0:T(8,128)}, bf16[32,16,384]{2,1,0:T(8,128)(2,1)}) custom-call(s32[4]{0:T(128)} %copy-done.11, bf16[4,128,1024]{2,1,0:T(8,128)(2,1)} %copy-done.4, bf16[4,128,1024]{2,1,0:T(8,128)(2,1)} %copy-done.21, bf16[4,128,1024]{2,1,0:T(8,128)(2,1)} %copy-done.20, ...), custom_call_target="tpu_custom_call" | custom-call | tf_op jit(solution)/shard_map/pallas_call | solution.py:54
  182.3 3.6 %all-to-all-start.1 = ((bf16[32,16,384]{2,1,0:T(8,128)(2,1)}), bf16[32,16,384]{2,1,0:T(8,128)(2,1)S(1)}, u32[]{:S(2)}, u32[]{:S(2)}) async-start(bf16[32,16,384]{2,1,0:T(8,128)(2,1)} %get-tuple-element.123), calls=%async_computation.1 | async-start | bytes 786432 | tf_op jit(solution)/shard_map/grads_b_send/all_to_all | solution.py:698
  186.7 10.8 %shard_map.281 = (bf16[320,1024]{1,0:T(8,128)(2,1)}, bf16[320,1024]{1,0:T(8,128)(2,1)}, bf16[320,1024]{1,0:T(8,128)(2,1)}, bf16[320,16]{1,0:T(8,128)(2,1)}, bf16[32,16,128]{2,1,0:T(8,128)(2,1)}) custom-call(s32[4]{0:T(128)} %copy-done.11, f32[320,1]{1,0:T(8,128)} %copy-done.7, bf16[320,1024]{1,0:T(8,128)(2,1)} %get-tuple-element.86.refs_2_, ...), custom_call_target="tpu_custom_call" | custom-call | tf_op jit(solution)/shard_map/pallas_call | solution.py:54
  197.5 1.6 all-to-all-done.1.mine
  199.2 0.7 grads_b.6
  199.9 1.1 collective-permute-start.33
  201.0 3.7 %all-to-all-start.2 = ((bf16[32,16,128]{2,1,0:T(8,128)(2,1)}), bf16[32,16,128]{2,1,0:T(8,128)(2,1)S(1)}, u32[]{:S(2)}, u32[]{:S(2)}) async-start(bf16[32,16,128]{2,1,0:T(8,128)(2,1)} %get-tuple-element.124), calls=%async_computation.2 | async-start | bytes 262144 | tf_op jit(solution)/shard_map/grads_c_send/all_to_all | solution.py:698
  204.7 2.4 collective-permute-done.33.refs_1_
  207.5 5.5 %all-to-all-done.2.mine = bf16[32,16,128]{2,1,0:T(8,128)(2,1)S(1)} async-done(((bf16[32,16,128]{2,1,0:T(8,128)(2,1)}), bf16[32,16,128]{2,1,0:T(8,128)(2,1)S(1)}, u32[]{:S(2)}, u32[]{:S(2)}) %all-to-all-start.2) | async-done | bytes 131104 | tf_op jit(solution)/shard_map/grads_c_send/all_to_all | solution.py:698
  213.0 0.7 grads_b.9
  213.7 1.4 collective-permute-start.37
  215.0 0.9 collective-permute-start.36
  215.9 2.2 collective-permute-start.35
  218.1 1.6 collective-permute-done.37.refs_3_
  219.7 0.8 collective-permute-done.36.refs_2_
  222.0 0.9 collective-permute-start.38
  222.9 11.0 %shard_map.282 = bf16[4,640,256]{2,1,0:T(8,128)(2,1)} custom-call(s32[4]{0:T(128)} %copy-done.11, bf16[4,128,1024]{2,1,0:T(8,128)(2,1)} %copy-done.2, bf16[4,128,1024]{2,1,0:T(8,128)(2,1)} %copy-done.14, bf16[4,128,1024]{2,1,0:T(8,128)(2,1)} %copy-done.13, bf16[4,128,1024]{2,1,0:T(8,128)(2,1)} %copy-done.15, bf16[4,128,1024]{2,1,0:T(8,128)(2,1)} %copy-done.16, ...), custom_call_target="tpu_custom_call" | custom-call | tf_op jit(solution)/shard_map/pallas_call | solution.py:54
  233.9 1.5 collective-permute-done.39.refs_3_
  235.8 1.7 collective-permute-done.40.refs_5_
  237.5 3.5 %all-to-all-start.3 = ((bf16[4,640,256]{2,1,0:T(8,128)(2,1)}), bf16[4,640,256]{2,1,0:T(8,128)(2,1)S(1)}, u32[]{:S(2)}, u32[]{:S(2)}) async-start(bf16[4,640,256]{2,1,0:T(8,128)(2,1)} %shard_map.282), calls=%async_computation.3 | async-start | bytes 2621440 | tf_op jit(solution)/shard_map/rows_out/all_to_all | solution.py:972
  241.6 3.2 %collective-permute-done.41.refs_4_ = bf16[4,128,512]{2,1,0:T(8,128)(2,1)} collective-permute-done((bf16[4,128,512]{2,1,0:T(8,128)(2,1)S(1)}, bf16[4,128,512]{2,1,0:T(8,128)(2,1)}, u32[]{:S(2)}, u32[]{:S(2)}) %collective-permute-start.41) | collective-permute-done | bytes 524320 | tf_op jit(solution)/shard_map/grads/ppermute | solution.py:75
  244.8 2.1 collective-permute-done.44.refs_8_
  246.9 0.8 copy-done.31
  247.8 6.9 %grads.1 = (f32[128,4096]{1,0:T(8,128)}, f32[128,4096]{1,0:T(8,128)}, f32[128,1024]{1,0:T(8,128)}, f32[128,1024]{1,0:T(8,128)}, f32[128,1024]{1,0:T(8,128)}, /*i...) custom-call(s32[4]{0:T(128)} %copy-done.11, bf16[4,128,512]{2,1,0:T(8,128)(2,1)} %copy-done.5, ...), custom_call_target="tpu_custom_call" | custom-call | tf_op jit(solution)/shard_map/grads/pallas_call | solution.py:54
  254.7 3.6 %all-to-all-done.3 = bf16[4,640,256]{2,1,0:T(8,128)(2,1)S(1)} async-done(((bf16[4,640,256]{2,1,0:T(8,128)(2,1)}), bf16[4,640,256]{2,1,0:T(8,128)(2,1)S(1)}, u32[]{:S(2)}, u32[]{:S(2)}) %all-to-all-start.3) | async-done | bytes 1310752 | tf_op jit(solution)/shard_map/rows_out/all_to_all | solution.py:972
  258.3 1.1 fusion.3
  (135 shorter events, 8.3 us)
Async XLA Ops:
  0.6 18.4 %copy-start = (bf16[8,16,3,1024]{3,1,2,0:T(8,128)(2,1)S(1)}, bf16[8,16,3,1024]{3,1,2,0:T(8,128)(2,1)}, u32[]{:S(2)}) copy-start(bf16[8,16,3,1024]{3,1,2,0:T(8,128)(2,1)} %param.35) | copy-start | bytes 2359300
  3.3 10.2 %copy-start.32 = (s32[4]{0:T(128)S(1)}, s32[4]{0:T(128)}, u32[]{:S(2)}) copy-start(s32[4]{0:T(128)} %param.24) | copy-start | bytes 52
  3.3 13.5 %copy-start.9 = (bf16[128,1024]{1,0:T(8,128)(2,1)S(1)}, bf16[128,1024]{1,0:T(8,128)(2,1)}, u32[]{:S(2)}) copy-start(bf16[128,1024]{1,0:T(8,128)(2,1)} %w1.1) | copy-start | bytes 786436
  3.3 13.5 %copy-start.10 = (bf16[1024,128]{1,0:T(8,128)(2,1)S(1)}, bf16[1024,128]{1,0:T(8,128)(2,1)}, u32[]{:S(2)}) copy-start(bf16[1024,128]{1,0:T(8,128)(2,1)} %w2.1) | copy-start | bytes 786436
  3.4 13.5 %copy-start.12 = (s32[4,256]{1,0:T(4,128)S(1)}, s32[4,256]{1,0:T(4,128)}, u32[]{:S(2)}) copy-start(s32[4,256]{1,0:T(4,128)} %mask.1) | copy-start | bytes 12292
  3.4 32.6 %all-to-all-start = ((bf16[4,656,256]{2,1,0:T(8,128)(2,1)}), bf16[4,656,256]{2,1,0:T(8,128)(2,1)}, u32[]{:S(2)}, u32[]{:S(2)}) async-start(bf16[4,656,256]{2,1,0:T(8,128)(2,1)} %get-tuple-element.78), calls=%async_computation | async-start | bytes 2686976 | tf_op jit(solution)/shard_map/all_to_all | solution.py:797
  7.8 12.4 %collective-permute-start.2 = (bf16[128,1024]{1,0:T(8,128)(2,1)S(1)}, bf16[128,1024]{1,0:T(8,128)(2,1)S(1)}, u32[]{:S(2)}, u32[]{:S(2)}) collective-permute-start(bf16[128,1024]{1,0:T(8,128)(2,1)S(1)} %copy-done.8), channel_id=1, source_target_pairs={{0,24},{1,25},{2,26},{3,27},{4,28},{5,29},{6,30},{7,31},{8,16},{9,... | collective-permute-start | bytes 786440 | tf_op jit(solution)/shard_map/q_high/ppermute | solution.py:75
  13.0 22.8 %collective-permute-start.1 = (bf16[128,1024]{1,0:T(8,128)(2,1)S(1)}, bf16[128,1024]{1,0:T(8,128)(2,1)S(1)}, u32[]{:S(2)}, u32[]{:S(2)}) collective-permute-start(bf16[128,1024]{1,0:T(8,128)(2,1)S(1)} %copy-done.8), channel_id=1, source_target_pairs={{0,16},{1,17},{2,18},{3,19},{4,20},{5,21},{6,22},{7,23},{8,24},{9,... | collective-permute-start | bytes 786440 | tf_op jit(solution)/shard_map/q_high/ppermute | solution.py:75
  13.0 22.8 %collective-permute-start = (bf16[128,1024]{1,0:T(8,128)(2,1)S(1)}, bf16[128,1024]{1,0:T(8,128)(2,1)S(1)}, u32[]{:S(2)}, u32[]{:S(2)}) collective-permute-start(bf16[128,1024]{1,0:T(8,128)(2,1)S(1)} %copy-done.8), channel_id=1, source_target_pairs={{0,8},{1,9},{2,10},{3,11},{4,12},{5,13},{6,14},{7,15},{8,0},{9,1},... | collective-permute-start | bytes 786440 | tf_op jit(solution)/shard_map/q_high/ppermute | solution.py:75
  16.9 19.1 %copy-start.11 = (s32[4]{0:T(128)}, s32[4]{0:T(128)S(1)}, u32[]{:S(2)}) copy-start(s32[4]{0:T(128)S(1)} %pad_add_fusion.3.sc.refs_0_) | copy-start | bytes 52
  35.9 48.6 %copy-start.2 = (bf16[4,128,1024]{2,1,0:T(8,128)(2,1)}, bf16[4,128,1024]{2,1,0:T(8,128)(2,1)S(1)}, u32[]{:S(2)}) copy-start(bf16[4,128,1024]{2,1,0:T(8,128)(2,1)S(1)} %q_high.1.refs_1_.refs_9_) | copy-start | bytes 3145732
  36.0 26.2 %collective-permute-start.4 = (bf16[4,128,1024]{2,1,0:T(8,128)(2,1)S(1)}, bf16[4,128,1024]{2,1,0:T(8,128)(2,1)S(1)}, u32[]{:S(2)}, u32[]{:S(2)}) collective-permute-start(bf16[4,128,1024]{2,1,0:T(8,128)(2,1)S(1)} %q_high.1.refs_1_.refs_9_), channel_id=1, source_target_pairs={{0,4},{1,3},{2,6},{3,1},{4,0},{5,7},{6,2},{7,5},{8,12},{9,11},{10,... | collective-permute-start | bytes 3145736 | tf_op jit(solution)/shard_map/q_two/ppermute | solution.py:75
  37.5 24.6 %collective-permute-start.3 = (bf16[4,128,1024]{2,1,0:T(8,128)(2,1)S(1)}, bf16[4,128,1024]{2,1,0:T(8,128)(2,1)S(1)}, u32[]{:S(2)}, u32[]{:S(2)}) collective-permute-start(bf16[4,128,1024]{2,1,0:T(8,128)(2,1)S(1)} %q_high.1.refs_1_.refs_9_), channel_id=1, source_target_pairs={{0,2},{1,5},{2,0},{3,7},{4,6},{5,1},{6,4},{7,3},{8,10},{9,13},{10,... | collective-permute-start | bytes 3145736 | tf_op jit(solution)/shard_map/q_one/ppermute | solution.py:75
  39.2 11.1 %collective-permute-start.7 = (bf16[128,1024]{1,0:T(8,128)(2,1)S(1)}, bf16[128,1024]{1,0:T(8,128)(2,1)S(1)}, u32[]{:S(2)}, u32[]{:S(2)}) collective-permute-start(bf16[128,1024]{1,0:T(8,128)(2,1)S(1)} %get-tuple-element.82.refs_0_), channel_id=1, source_target_pairs={{0,24},{1,25},{2,26},{3,27},{4,28},{5,29},{6,30},{7,31},{8,16},{9,... | collective-permute-start | bytes 786440 | tf_op jit(solution)/shard_map/fa_high/ppermute | solution.py:75
  41.7 20.4 %collective-permute-start.6 = (bf16[128,1024]{1,0:T(8,128)(2,1)S(1)}, bf16[128,1024]{1,0:T(8,128)(2,1)S(1)}, u32[]{:S(2)}, u32[]{:S(2)}) collective-permute-start(bf16[128,1024]{1,0:T(8,128)(2,1)S(1)} %get-tuple-element.82.refs_0_), channel_id=1, source_target_pairs={{0,16},{1,17},{2,18},{3,19},{4,20},{5,21},{6,22},{7,23},{8,24},{9,... | collective-permute-start | bytes 786440 | tf_op jit(solution)/shard_map/fa_high/ppermute | solution.py:75
  41.7 20.4 %collective-permute-start.5 = (bf16[128,1024]{1,0:T(8,128)(2,1)S(1)}, bf16[128,1024]{1,0:T(8,128)(2,1)S(1)}, u32[]{:S(2)}, u32[]{:S(2)}) collective-permute-start(bf16[128,1024]{1,0:T(8,128)(2,1)S(1)} %get-tuple-element.82.refs_0_), channel_id=1, source_target_pairs={{0,8},{1,9},{2,10},{3,11},{4,12},{5,13},{6,14},{7,15},{8,0},{9,1},... | collective-permute-start | bytes 786440 | tf_op jit(solution)/shard_map/fa_high/ppermute | solution.py:75
  62.1 22.4 %copy-start.13 = (bf16[4,128,1024]{2,1,0:T(8,128)(2,1)}, bf16[4,128,1024]{2,1,0:T(8,128)(2,1)S(1)}, u32[]{:S(2)}) copy-start(bf16[4,128,1024]{2,1,0:T(8,128)(2,1)S(1)} %collective-permute-done.4.refs_3_.refs_11_) | copy-start | bytes 3145732
  62.2 22.4 %copy-start.14 = (bf16[4,128,1024]{2,1,0:T(8,128)(2,1)}, bf16[4,128,1024]{2,1,0:T(8,128)(2,1)S(1)}, u32[]{:S(2)}) copy-start(bf16[4,128,1024]{2,1,0:T(8,128)(2,1)S(1)} %collective-permute-done.3.refs_2_.refs_10_) | copy-start | bytes 3145732
  62.2 14.9 %collective-permute-start.8 = (bf16[4,128,1024]{2,1,0:T(8,128)(2,1)S(1)}, bf16[4,128,1024]{2,1,0:T(8,128)(2,1)S(1)}, u32[]{:S(2)}, u32[]{:S(2)}) collective-permute-start(bf16[4,128,1024]{2,1,0:T(8,128)(2,1)S(1)} %collective-permute-done.3.refs_2_.refs_10_), channel_id=1, source_target_pairs={{0,4},{1,3},{2,6},{3,1},{4,0},{5,7},{6,2},{7,5},{8,12},{9,11},{10,... | collective-permute-start | bytes 3145736 | tf_op jit(solution)/shard_map/q_both/ppermute | solution.py:75
  63.4 13.8 %collective-permute-start.9 = (bf16[4,128,1024]{2,1,0:T(8,128)(2,1)S(1)}, bf16[4,128,1024]{2,1,0:T(8,128)(2,1)S(1)}, u32[]{:S(2)}, u32[]{:S(2)}) collective-permute-start(bf16[4,128,1024]{2,1,0:T(8,128)(2,1)S(1)} %q_high.1.refs_1_.refs_9_), channel_id=1, source_target_pairs={{0,1},{1,0},{2,3},{3,2},{4,5},{5,4},{6,7},{7,6},{8,9},{9,8},{10,11... | collective-permute-start | bytes 3145736 | tf_op jit(solution)/shard_map/q_core/ppermute | solution.py:75
  63.4 13.8 %collective-permute-start.11 = (bf16[4,128,1024]{2,1,0:T(8,128)(2,1)S(1)}, bf16[4,128,1024]{2,1,0:T(8,128)(2,1)S(1)}, u32[]{:S(2)}, u32[]{:S(2)}) collective-permute-start(bf16[4,128,1024]{2,1,0:T(8,128)(2,1)S(1)} %collective-permute-done.4.refs_3_.refs_11_), channel_id=1, source_target_pairs={{0,1},{1,0},{2,3},{3,2},{4,5},{5,4},{6,7},{7,6},{8,9},{9,8},{10,11... | collective-permute-start | bytes 3145736 | tf_op jit(solution)/shard_map/q_core/ppermute | solution.py:75
  63.9 13.3 %collective-permute-start.10 = (bf16[4,128,1024]{2,1,0:T(8,128)(2,1)S(1)}, bf16[4,128,1024]{2,1,0:T(8,128)(2,1)S(1)}, u32[]{:S(2)}, u32[]{:S(2)}) collective-permute-start(bf16[4,128,1024]{2,1,0:T(8,128)(2,1)S(1)} %collective-permute-done.3.refs_2_.refs_10_), channel_id=1, source_target_pairs={{0,1},{1,0},{2,3},{3,2},{4,5},{5,4},{6,7},{7,6},{8,9},{9,8},{10,11... | collective-permute-start | bytes 3145736 | tf_op jit(solution)/shard_map/q_core/ppermute | solution.py:75
  77.0 4.5 %collective-permute-start.12 = (bf16[4,128,1024]{2,1,0:T(8,128)(2,1)S(1)}, bf16[4,128,1024]{2,1,0:T(8,128)(2,1)S(1)}, u32[]{:S(2)}, u32[]{:S(2)}) collective-permute-start(bf16[4,128,1024]{2,1,0:T(8,128)(2,1)S(1)} %collective-permute-done.8.refs_4_.refs_12_), channel_id=1, source_target_pairs={{0,1},{1,0},{2,3},{3,2},{4,5},{5,4},{6,7},{7,6},{8,9},{9,8},{10,11... | collective-permute-start | bytes 3145736 | tf_op jit(solution)/shard_map/q_core/ppermute | solution.py:75
  77.2 27.3 %copy-start.3 = (bf16[4,128,1024]{2,1,0:T(8,128)(2,1)}, bf16[4,128,1024]{2,1,0:T(8,128)(2,1)S(1)}, u32[]{:S(2)}) copy-start(bf16[4,128,1024]{2,1,0:T(8,128)(2,1)S(1)} %fa_high.1.refs_1_) | copy-start | bytes 3145732
  77.2 26.1 %collective-permute-start.19 = (bf16[4,128,1024]{2,1,0:T(8,128)(2,1)S(1)}, bf16[4,128,1024]{2,1,0:T(8,128)(2,1)}, u32[]{:S(2)}, u32[]{:S(2)}) collective-permute-start(bf16[4,128,1024]{2,1,0:T(8,128)(2,1)S(1)} %fa_high.1.refs_1_), channel_id=1, source_target_pairs={{0,4},{1,3},{2,6},{3,1},{4,0},{5,7},{6,2},{7,5},{8,12},{9,11},{10,... | collective-permute-start | bytes 3145736 | tf_op jit(solution)/shard_map/fa_two/ppermute | solution.py:75
  78.5 24.8 %collective-permute-start.18 = (bf16[4,128,1024]{2,1,0:T(8,128)(2,1)S(1)}, bf16[4,128,1024]{2,1,0:T(8,128)(2,1)}, u32[]{:S(2)}, u32[]{:S(2)}) collective-permute-start(bf16[4,128,1024]{2,1,0:T(8,128)(2,1)S(1)} %fa_high.1.refs_1_), channel_id=1, source_target_pairs={{0,2},{1,5},{2,0},{3,7},{4,6},{5,1},{6,4},{7,3},{8,10},{9,13},{10,... | collective-permute-start | bytes 3145736 | tf_op jit(solution)/shard_map/fa_one/ppermute | solution.py:75
  79.0 23.4 %collective-permute-start.15 = (bf16[128,1024]{1,0:T(8,128)(2,1)S(1)}, bf16[128,1024]{1,0:T(8,128)(2,1)S(1)}, u32[]{:S(2)}, u32[]{:S(2)}) collective-permute-start(bf16[128,1024]{1,0:T(8,128)(2,1)S(1)} %get-tuple-element.91.refs_0_), channel_id=1, source_target_pairs={{0,24},{1,25},{2,26},{3,27},{4,28},{5,29},{6,30},{7,31},{8,16},{9,... | collective-permute-start | bytes 786440 | tf_op jit(solution)/shard_map/fb_high/ppermute | solution.py:75
  81.5 21.6 %collective-permute-start.14 = (bf16[128,1024]{1,0:T(8,128)(2,1)S(1)}, bf16[128,1024]{1,0:T(8,128)(2,1)S(1)}, u32[]{:S(2)}, u32[]{:S(2)}) collective-permute-start(bf16[128,1024]{1,0:T(8,128)(2,1)S(1)} %get-tuple-element.91.refs_0_), channel_id=1, source_target_pairs={{0,16},{1,17},{2,18},{3,19},{4,20},{5,21},{6,22},{7,23},{8,24},{9,... | collective-permute-start | bytes 786440 | tf_op jit(solution)/shard_map/fb_high/ppermute | solution.py:75
  82.6 20.6 %collective-permute-start.13 = (bf16[128,1024]{1,0:T(8,128)(2,1)S(1)}, bf16[128,1024]{1,0:T(8,128)(2,1)S(1)}, u32[]{:S(2)}, u32[]{:S(2)}) collective-permute-start(bf16[128,1024]{1,0:T(8,128)(2,1)S(1)} %get-tuple-element.91.refs_0_), channel_id=1, source_target_pairs={{0,8},{1,9},{2,10},{3,11},{4,12},{5,13},{6,14},{7,15},{8,0},{9,1},... | collective-permute-start | bytes 786440 | tf_op jit(solution)/shard_map/fb_high/ppermute | solution.py:75
  103.3 15.1 %collective-permute-start.26 = (bf16[4,128,1024]{2,1,0:T(8,128)(2,1)}, bf16[4,128,1024]{2,1,0:T(8,128)(2,1)}, u32[]{:S(2)}, u32[]{:S(2)}) collective-permute-start(bf16[4,128,1024]{2,1,0:T(8,128)(2,1)} %collective-permute-done.18.refs_2_), channel_id=1, source_target_pairs={{0,4},{1,3},{2,6},{3,1},{4,0},{5,7},{6,2},{7,5},{8,12},{9,11},{10,... | collective-permute-start | bytes 3145736 | tf_op jit(solution)/shard_map/fa_both/ppermute | solution.py:75
  104.5 14.5 %collective-permute-start.20 = (bf16[4,128,1024]{2,1,0:T(8,128)(2,1)S(1)}, bf16[4,128,1024]{2,1,0:T(8,128)(2,1)}, u32[]{:S(2)}, u32[]{:S(2)}) collective-permute-start(bf16[4,128,1024]{2,1,0:T(8,128)(2,1)S(1)} %fa_high.1.refs_1_), channel_id=1, source_target_pairs={{0,1},{1,0},{2,3},{3,2},{4,5},{5,4},{6,7},{7,6},{8,9},{9,8},{10,11... | collective-permute-start | bytes 3145736 | tf_op jit(solution)/shard_map/fa_core/ppermute | solution.py:75
  104.5 14.5 %collective-permute-start.22 = (bf16[4,128,1024]{2,1,0:T(8,128)(2,1)}, bf16[4,128,1024]{2,1,0:T(8,128)(2,1)}, u32[]{:S(2)}, u32[]{:S(2)}) collective-permute-start(bf16[4,128,1024]{2,1,0:T(8,128)(2,1)} %collective-permute-done.19.refs_3_), channel_id=1, source_target_pairs={{0,1},{1,0},{2,3},{3,2},{4,5},{5,4},{6,7},{7,6},{8,9},{9,8},{10,11... | collective-permute-start | bytes 3145736 | tf_op jit(solution)/shard_map/fa_core/ppermute | solution.py:75
  105.0 14.0 %collective-permute-start.21 = (bf16[4,128,1024]{2,1,0:T(8,128)(2,1)}, bf16[4,128,1024]{2,1,0:T(8,128)(2,1)}, u32[]{:S(2)}, u32[]{:S(2)}) collective-permute-start(bf16[4,128,1024]{2,1,0:T(8,128)(2,1)} %collective-permute-done.18.refs_2_), channel_id=1, source_target_pairs={{0,1},{1,0},{2,3},{3,2},{4,5},{5,4},{6,7},{7,6},{8,9},{9,8},{10,11... | collective-permute-start | bytes 3145736 | tf_op jit(solution)/shard_map/fa_core/ppermute | solution.py:75
  105.1 41.2 %copy-start.4 = (bf16[4,128,1024]{2,1,0:T(8,128)(2,1)}, bf16[4,128,1024]{2,1,0:T(8,128)(2,1)S(1)}, u32[]{:S(2)}) copy-start(bf16[4,128,1024]{2,1,0:T(8,128)(2,1)S(1)} %fb_high.1.refs_1_) | copy-start | bytes 3145732
  105.1 4.5 %collective-permute-start.16 = (s32[4]{0:T(128)S(1)}, s32[4]{0:T(128)S(1)}, u32[]{:S(2)}, u32[]{:S(2)}) collective-permute-start(s32[4]{0:T(128)S(1)} %copy-done.32), channel_id=1, source_target_pairs={{0,16},{1,17},{2,18},{3,19},{4,20},{5,21},{6,22},{7,23},{8,24},{9,... | collective-permute-start | bytes 56 | tf_op jit(solution)/shard_map/ppermute | solution.py:75
  110.2 3.6 %collective-permute-start.17 = (s32[2,4]{1,0:T(2,128)S(1)}, s32[2,4]{1,0:T(2,128)S(1)}, u32[]{:S(2)}, u32[]{:S(2)}) collective-permute-start(s32[2,4]{1,0:T(2,128)S(1)} %gather_fusion), channel_id=1, source_target_pairs={{0,8},{1,9},{2,10},{3,11},{4,12},{5,13},{6,14},{7,15},{8,0},{9,1},... | collective-permute-start | bytes 104 | tf_op jit(solution)/shard_map/ppermute | solution.py:75
  118.4 4.1 %collective-permute-start.27 = (bf16[4,128,1024]{2,1,0:T(8,128)(2,1)}, bf16[4,128,1024]{2,1,0:T(8,128)(2,1)}, u32[]{:S(2)}, u32[]{:S(2)}) collective-permute-start(bf16[4,128,1024]{2,1,0:T(8,128)(2,1)} %collective-permute-done.26.refs_4_), channel_id=1, source_target_pairs={{0,1},{1,0},{2,3},{3,2},{4,5},{5,4},{6,7},{7,6},{8,9},{9,8},{10,11... | collective-permute-start | bytes 3145736 | tf_op jit(solution)/shard_map/fa_core/ppermute | solution.py:75
  119.0 25.6 %collective-permute-start.24 = (bf16[4,128,1024]{2,1,0:T(8,128)(2,1)S(1)}, bf16[4,128,1024]{2,1,0:T(8,128)(2,1)S(1)}, u32[]{:S(2)}, u32[]{:S(2)}) collective-permute-start(bf16[4,128,1024]{2,1,0:T(8,128)(2,1)S(1)} %fb_high.1.refs_1_), channel_id=1, source_target_pairs={{0,4},{1,3},{2,6},{3,1},{4,0},{5,7},{6,2},{7,5},{8,12},{9,11},{10,... | collective-permute-start | bytes 3145736 | tf_op jit(solution)/shard_map/fb_two/ppermute | solution.py:75
  120.2 24.4 %collective-permute-start.23 = (bf16[4,128,1024]{2,1,0:T(8,128)(2,1)S(1)}, bf16[4,128,1024]{2,1,0:T(8,128)(2,1)S(1)}, u32[]{:S(2)}, u32[]{:S(2)}) collective-permute-start(bf16[4,128,1024]{2,1,0:T(8,128)(2,1)S(1)} %fb_high.1.refs_1_), channel_id=1, source_target_pairs={{0,2},{1,5},{2,0},{3,7},{4,6},{5,1},{6,4},{7,3},{8,10},{9,13},{10,... | collective-permute-start | bytes 3145736 | tf_op jit(solution)/shard_map/fb_one/ppermute | solution.py:75
  120.9 23.6 %collective-permute-start.25 = (s32[2,2,4]{2,1,0:T(2,128)S(1)}, s32[2,2,4]{2,1,0:T(2,128)S(1)}, u32[]{:S(2)}, u32[]{:S(2)}) collective-permute-start(s32[2,2,4]{2,1,0:T(2,128)S(1)} %gather_fusion.1), channel_id=1, source_target_pairs={{0,4},{1,5},{2,6},{3,7},{4,0},{5,1},{6,2},{7,3},{8,12},{9,13},{10,... | collective-permute-start | bytes 200 | tf_op jit(solution)/shard_map/ppermute | solution.py:75
  144.6 18.6 %copy-start.20 = (bf16[4,128,1024]{2,1,0:T(8,128)(2,1)}, bf16[4,128,1024]{2,1,0:T(8,128)(2,1)S(1)}, u32[]{:S(2)}) copy-start(bf16[4,128,1024]{2,1,0:T(8,128)(2,1)S(1)} %collective-permute-done.24.refs_3_) | copy-start | bytes 3145732
  144.6 18.5 %copy-start.21 = (bf16[4,128,1024]{2,1,0:T(8,128)(2,1)}, bf16[4,128,1024]{2,1,0:T(8,128)(2,1)S(1)}, u32[]{:S(2)}) copy-start(bf16[4,128,1024]{2,1,0:T(8,128)(2,1)S(1)} %collective-permute-done.23.refs_2_) | copy-start | bytes 3145732
  144.6 14.8 %collective-permute-start.28 = (bf16[4,128,1024]{2,1,0:T(8,128)(2,1)S(1)}, bf16[4,128,1024]{2,1,0:T(8,128)(2,1)S(1)}, u32[]{:S(2)}, u32[]{:S(2)}) collective-permute-start(bf16[4,128,1024]{2,1,0:T(8,128)(2,1)S(1)} %collective-permute-done.23.refs_2_), channel_id=1, source_target_pairs={{0,4},{1,3},{2,6},{3,1},{4,0},{5,7},{6,2},{7,5},{8,12},{9,11},{10,... | collective-permute-start | bytes 3145736 | tf_op jit(solution)/shard_map/fb_both/ppermute | solution.py:75
  146.4 13.1 %collective-permute-start.30 = (bf16[4,128,1024]{2,1,0:T(8,128)(2,1)S(1)}, bf16[4,128,1024]{2,1,0:T(8,128)(2,1)S(1)}, u32[]{:S(2)}, u32[]{:S(2)}) collective-permute-start(bf16[4,128,1024]{2,1,0:T(8,128)(2,1)S(1)} %collective-permute-done.23.refs_2_), channel_id=1, source_target_pairs={{0,1},{1,0},{2,3},{3,2},{4,5},{5,4},{6,7},{7,6},{8,9},{9,8},{10,11... | collective-permute-start | bytes 3145736 | tf_op jit(solution)/shard_map/fb_core/ppermute | solution.py:75
  146.4 13.1 %collective-permute-start.29 = (bf16[4,128,1024]{2,1,0:T(8,128)(2,1)S(1)}, bf16[4,128,1024]{2,1,0:T(8,128)(2,1)S(1)}, u32[]{:S(2)}, u32[]{:S(2)}) collective-permute-start(bf16[4,128,1024]{2,1,0:T(8,128)(2,1)S(1)} %fb_high.1.refs_1_), channel_id=1, source_target_pairs={{0,1},{1,0},{2,3},{3,2},{4,5},{5,4},{6,7},{7,6},{8,9},{9,8},{10,11... | collective-permute-start | bytes 3145736 | tf_op jit(solution)/shard_map/fb_core/ppermute | solution.py:75
  146.9 12.6 %collective-permute-start.31 = (bf16[4,128,1024]{2,1,0:T(8,128)(2,1)S(1)}, bf16[4,128,1024]{2,1,0:T(8,128)(2,1)S(1)}, u32[]{:S(2)}, u32[]{:S(2)}) collective-permute-start(bf16[4,128,1024]{2,1,0:T(8,128)(2,1)S(1)} %collective-permute-done.24.refs_3_), channel_id=1, source_target_pairs={{0,1},{1,0},{2,3},{3,2},{4,5},{5,4},{6,7},{7,6},{8,9},{9,8},{10,11... | collective-permute-start | bytes 3145736 | tf_op jit(solution)/shard_map/fb_core/ppermute | solution.py:75
  159.5 2.7 %collective-permute-start.32 = (bf16[4,128,1024]{2,1,0:T(8,128)(2,1)S(1)}, bf16[4,128,1024]{2,1,0:T(8,128)(2,1)S(1)}, u32[]{:S(2)}, u32[]{:S(2)}) collective-permute-start(bf16[4,128,1024]{2,1,0:T(8,128)(2,1)S(1)} %collective-permute-done.28.refs_4_), channel_id=1, source_target_pairs={{0,1},{1,0},{2,3},{3,2},{4,5},{5,4},{6,7},{7,6},{8,9},{9,8},{10,11... | collective-permute-start | bytes 3145736 | tf_op jit(solution)/shard_map/fb_core/ppermute | solution.py:75
  182.3 16.8 %all-to-all-start.1 = ((bf16[32,16,384]{2,1,0:T(8,128)(2,1)}), bf16[32,16,384]{2,1,0:T(8,128)(2,1)S(1)}, u32[]{:S(2)}, u32[]{:S(2)}) async-start(bf16[32,16,384]{2,1,0:T(8,128)(2,1)} %get-tuple-element.123), calls=%async_computation.1 | async-start | bytes 786432 | tf_op jit(solution)/shard_map/grads_b_send/all_to_all | solution.py:698
  199.9 7.3 %collective-permute-start.33 = (bf16[128,384]{1,0:T(8,128)(2,1)S(1)}, bf16[128,384]{1,0:T(8,128)(2,1)S(1)}, u32[]{:S(2)}, u32[]{:S(2)}) collective-permute-start(bf16[128,384]{1,0:T(8,128)(2,1)S(1)} %bitcast.43), channel_id=1, source_target_pairs={{0,16},{1,17},{2,18},{3,19},{4,20},{5,21},{6,22},{7,23},{8,24},{9,... | collective-permute-start | bytes 294920 | tf_op jit(solution)/shard_map/grads_b/ppermute | solution.py:75
  201.0 12.0 %all-to-all-start.2 = ((bf16[32,16,128]{2,1,0:T(8,128)(2,1)}), bf16[32,16,128]{2,1,0:T(8,128)(2,1)S(1)}, u32[]{:S(2)}, u32[]{:S(2)}) async-start(bf16[32,16,128]{2,1,0:T(8,128)(2,1)} %get-tuple-element.124), calls=%async_computation.2 | async-start | bytes 262144 | tf_op jit(solution)/shard_map/grads_c_send/all_to_all | solution.py:698
  207.4 13.3 %collective-permute-start.34 = (bf16[2,128,384]{2,1,0:T(8,128)(2,1)S(1)}, bf16[2,128,384]{2,1,0:T(8,128)(2,1)S(1)}, u32[]{:S(2)}, u32[]{:S(2)}) collective-permute-start(bf16[2,128,384]{2,1,0:T(8,128)(2,1)S(1)} %grads_b.7), channel_id=1, source_target_pairs={{0,8},{1,9},{2,10},{3,11},{4,12},{5,13},{6,14},{7,15},{8,0},{9,1},... | collective-permute-start | bytes 589832 | tf_op jit(solution)/shard_map/grads_b/ppermute | solution.py:75
  213.7 6.0 %collective-permute-start.37 = (bf16[128,128]{1,0:T(8,128)(2,1)S(1)}, bf16[128,128]{1,0:T(8,128)(2,1)S(1)}, u32[]{:S(2)}, u32[]{:S(2)}) collective-permute-start(bf16[128,128]{1,0:T(8,128)(2,1)S(1)} %bitcast.46), channel_id=1, source_target_pairs={{0,24},{1,25},{2,26},{3,27},{4,28},{5,29},{6,30},{7,31},{8,16},{9,... | collective-permute-start | bytes 98312 | tf_op jit(solution)/shard_map/grads_b/ppermute | solution.py:75
  215.0 5.5 %collective-permute-start.36 = (bf16[128,128]{1,0:T(8,128)(2,1)S(1)}, bf16[128,128]{1,0:T(8,128)(2,1)S(1)}, u32[]{:S(2)}, u32[]{:S(2)}) collective-permute-start(bf16[128,128]{1,0:T(8,128)(2,1)S(1)} %bitcast.47), channel_id=1, source_target_pairs={{0,16},{1,17},{2,18},{3,19},{4,20},{5,21},{6,22},{7,23},{8,24},{9,... | collective-permute-start | bytes 98312 | tf_op jit(solution)/shard_map/grads_b/ppermute | solution.py:75
  215.9 4.6 %collective-permute-start.35 = (bf16[128,128]{1,0:T(8,128)(2,1)S(1)}, bf16[128,128]{1,0:T(8,128)(2,1)S(1)}, u32[]{:S(2)}, u32[]{:S(2)}) collective-permute-start(bf16[128,128]{1,0:T(8,128)(2,1)S(1)} %bitcast.48), channel_id=1, source_target_pairs={{0,8},{1,9},{2,10},{3,11},{4,12},{5,13},{6,14},{7,15},{8,0},{9,1},... | collective-permute-start | bytes 98312 | tf_op jit(solution)/shard_map/grads_b/ppermute | solution.py:75
  221.4 13.9 %copy-start.5 = (bf16[4,128,512]{2,1,0:T(8,128)(2,1)}, bf16[4,128,512]{2,1,0:T(8,128)(2,1)S(1)}, u32[]{:S(2)}) copy-start(bf16[4,128,512]{2,1,0:T(8,128)(2,1)S(1)} %grads_b.11.refs_1_) | copy-start | bytes 1572868
  221.4 13.9 %collective-permute-start.39 = (bf16[4,128,512]{2,1,0:T(8,128)(2,1)S(1)}, bf16[4,128,512]{2,1,0:T(8,128)(2,1)S(1)}, u32[]{:S(2)}, u32[]{:S(2)}) collective-permute-start(bf16[4,128,512]{2,1,0:T(8,128)(2,1)S(1)} %grads_b.11.refs_1_), channel_id=1, source_target_pairs={{0,4},{1,3},{2,6},{3,1},{4,0},{5,7},{6,2},{7,5},{8,12},{9,11},{10,... | collective-permute-start | bytes 1572872 | tf_op jit(solution)/shard_map/grads/ppermute | solution.py:75
  222.0 13.4 %collective-permute-start.38 = (bf16[4,128,512]{2,1,0:T(8,128)(2,1)S(1)}, bf16[4,128,512]{2,1,0:T(8,128)(2,1)S(1)}, u32[]{:S(2)}, u32[]{:S(2)}) collective-permute-start(bf16[4,128,512]{2,1,0:T(8,128)(2,1)S(1)} %grads_b.11.refs_1_), channel_id=1, source_target_pairs={{0,2},{1,5},{2,0},{3,7},{4,6},{5,1},{6,4},{7,3},{8,10},{9,13},{10,... | collective-permute-start | bytes 1572872 | tf_op jit(solution)/shard_map/grads/ppermute | solution.py:75
  235.4 2.1 collective-permute-start.40
  235.4 9.4 %collective-permute-start.41 = (bf16[4,128,512]{2,1,0:T(8,128)(2,1)S(1)}, bf16[4,128,512]{2,1,0:T(8,128)(2,1)}, u32[]{:S(2)}, u32[]{:S(2)}) collective-permute-start(bf16[4,128,512]{2,1,0:T(8,128)(2,1)S(1)} %collective-permute-done.38.refs_2_), channel_id=1, source_target_pairs={{0,4},{1,3},{2,6},{3,1},{4,0},{5,7},{6,2},{7,5},{8,12},{9,11},{10,... | collective-permute-start | bytes 1572872 | tf_op jit(solution)/shard_map/grads/ppermute | solution.py:75
  237.5 20.8 %all-to-all-start.3 = ((bf16[4,640,256]{2,1,0:T(8,128)(2,1)}), bf16[4,640,256]{2,1,0:T(8,128)(2,1)S(1)}, u32[]{:S(2)}, u32[]{:S(2)}) async-start(bf16[4,640,256]{2,1,0:T(8,128)(2,1)} %shard_map.282), calls=%async_computation.3 | async-start | bytes 2621440 | tf_op jit(solution)/shard_map/rows_out/all_to_all | solution.py:972
  241.0 3.8 %collective-permute-start.42 = (bf16[4,128,512]{2,1,0:T(8,128)(2,1)S(1)}, bf16[4,128,512]{2,1,0:T(8,128)(2,1)S(1)}, u32[]{:S(2)}, u32[]{:S(2)}) collective-permute-start(bf16[4,128,512]{2,1,0:T(8,128)(2,1)S(1)} %collective-permute-done.38.refs_2_), channel_id=1, source_target_pairs={{0,1},{1,0},{2,3},{3,2},{4,5},{5,4},{6,7},{7,6},{8,9},{9,8},{10,11... | collective-permute-start | bytes 1572872 | tf_op jit(solution)/shard_map/grads/ppermute | solution.py:75
  241.5 3.3 %collective-permute-start.43 = (bf16[4,128,512]{2,1,0:T(8,128)(2,1)S(1)}, bf16[4,128,512]{2,1,0:T(8,128)(2,1)S(1)}, u32[]{:S(2)}, u32[]{:S(2)}) collective-permute-start(bf16[4,128,512]{2,1,0:T(8,128)(2,1)S(1)} %collective-permute-done.39.refs_3_), channel_id=1, source_target_pairs={{0,1},{1,0},{2,3},{3,2},{4,5},{5,4},{6,7},{7,6},{8,9},{9,8},{10,11... | collective-permute-start | bytes 1572872 | tf_op jit(solution)/shard_map/grads/ppermute | solution.py:75
  244.8 2.1 collective-permute-start.44
  247.8 11.6 %copy-start.1 = (bf16[8,16,3,1024]{3,1,2,0:T(8,128)(2,1)S(1)}, bf16[8,16,3,1024]{3,1,2,0:T(8,128)(2,1)}, u32[]{:S(2)}) copy-start(bf16[8,16,3,1024]{3,1,2,0:T(8,128)(2,1)} %param.35) | copy-start | bytes 2359300
  (18 other events, 61.8 us)

commit v9 on v8

--- a/solution.py
+++ b/solution.py
@@ -90,7 +90,7 @@
         copy.wait()
 
 
-def stacked(parts, index):
+def stacked(parts, index, out_space=VMEM):
     shape = parts[0].shape
     flat = [p.reshape((-1, shape[-1])) for p in parts]
     out = jax.ShapeDtypeStruct((len(parts),) + flat[0].shape, flat[0].dtype)
@@ -100,6 +100,7 @@
         [index.reshape(1).astype(jnp.int32)] + flat,
         [pltpu.SMEM] + [pl.ANY] * len(parts),
         [pltpu.SemaphoreType.DMA((len(parts),))],
+        out_space,
     )
     return made.reshape((len(parts),) + shape)
 
@@ -152,6 +153,13 @@
 
 def after_all(values, *others):
     return lax.optimization_barrier(tuple(values) + others)[: len(values)]
+
+
+def exchange_rows(parts):
+    came = [parts[0]]
+    for j in range(1, len(parts)):
+        came.append(swap(parts[j], lambda r, c: (r, c ^ j)))
+    return came
 
 
 def gather_high(shard, most=2):
@@ -314,6 +322,13 @@
     for copy in copies:
         copy.start()
     return copies
+
+
+def to_columns(sc, made, buffer, outs):
+    hid = outs[0].shape[-1]
+    buffer[...] = made
+    for j, out in enumerate(outs):
+        out[...] = buffer[:, lanes((sc[1] ^ j) * hid, hid)]
 
 
 def rows_at(xa, start, height):
@@ -482,10 +497,12 @@
     own_q = refs[9:17]
     (xa, keep, gain, n2, lat3, up_1, down_2, up_2, f_down, p_down, p_up, bias_out) = refs[17:29]
     (middle, att, lat2, gr, res_in, gn2_in, lat4_in, glat3_in, early_in) = refs[29:38]
-    layer, gatt, gmid, early = refs[38:42]
+    layer, refs = refs[38 : 38 + cols], refs[:38] + refs[38 + cols :]
+    gatt, gmid, early = refs[38:41]
+    refs = refs[:41] + (None,) + refs[41:]
     w, sems, wp, sems_p, res, gn2, lat4, glat3 = refs[42:50]
     bs, row_u1, row_d2, row_u2, row_fd, row_pd, row_pu, mid_s, att_s, res_s, gn2_s, early_s = refs[50:62]
-    sems_f = refs[62]
+    sems_f, out_s = refs[62:]
     lane = early_in.shape[-1]
     a = sc[0]
     first = fetch(
@@ -530,8 +547,7 @@
         keep[...]
         * (mid + (res_s[...] + res[...]) + mm(lat4_low, row_u2[...]) + bias_out[1:2].astype(F32))
     )
-    for c in range(cols):
-        layer[c] = out[:, c * hid : (c + 1) * hid]
+    to_columns(sc, out, out_s, layer)
     glat3_low = low(glat3[...])
     grad_normed = gn2_s[...] + gn2[...] + mm(glat3_low, row_fd[...])
     unit, inverse = norm_parts(mid)
@@ -600,15 +616,14 @@
 def back_kernel(lead, cols, *refs):
     sc = refs[0]
     pieces = refs[1:9]
-    xa, gain, gq, gk, gv, glat1, q_down, gmid, layer = refs[9:18]
-    out = refs[18]
-    w, sems, acc, xs, row_qd, gmid_s, sems_f = refs[19:]
+    xa, gain, gq, gk, gv, glat1, q_down, gmid = refs[9:17]
+    outs = refs[17 : 17 + cols]
+    w, sems, acc, xs, row_qd, gmid_s, sems_f, out_s = refs[17 + cols :]
     first = fetch(
         sems_f,
         (rows_at(xa, 0, SEQ), xs),
         (q_down.at[sc[0]], row_qd),
         (gmid, gmid_s),
-        (layer, rows_at(out, 0, SEQ)),
     )
     weights = Weights(sc, pieces, w, sems, lead)
     weights.start()
@@ -628,8 +643,7 @@
 
     lax.fori_loop(0, cols, step, 0)
     made = low(gmid_s[...] + norm_back(acc[...], gain[0:1], unit, inverse))
-    for c in range(cols):
-        out[c, SEQ:] = made[:, c * hid : (c + 1) * hid]
+    to_columns(sc, made, out_s, outs)
 
 
 def sum_kernel(owners, mine, out, acc):
@@ -897,9 +911,9 @@
     with jax.named_scope("fb_core"):
         away_b = [swap(p, flip_core) for p in (own_b, one_b, two_b)]
         pieces_b = [own_b, one_b, two_b, both_b] + away_b + [swap(both_b, flip_core)]
-    layer, gatt, gmid, grads_b = call(
+    *layer, gatt, gmid, grads_b = call(
         functools.partial(ffn_b_kernel, lead, cols),
-        [jax.ShapeDtypeStruct((cols, SEQ, hid), BF), big, wide]
+        [shaped(hid, BF)] * cols + [big, wide]
         + [jax.ShapeDtypeStruct((rows * cols, R, 12 * D // (rows * cols)), BF)],
         [sc, *pieces_b, *pieces_q, xa, keep, ln_gain, n2, lat3, fc1_up, fc2_down, fc2_up]
         + [fc1_down, proj_down, proj_up, bias_out]
@@ -915,11 +929,13 @@
         + [bias_space, VMEM((R, FF), BF), VMEM((R, FF), BF)]
         + [VMEM((R, D), BF)] * 4
         + [VMEM((SEQ, D), F32), VMEM((SEQ, D), BF), VMEM((SEQ, D), F32), VMEM((SEQ, D), F32)]
-        + [VMEM(early_a.shape, BF), pltpu.SemaphoreType.DMA((12,))],
+        + [VMEM(early_a.shape, BF), pltpu.SemaphoreType.DMA((12,)), VMEM((SEQ, D), BF)],
         mib=FFN_B,
     )
     with jax.named_scope("grads_b_send"):
         mine_b = send_grads(grads_b)
+    with jax.named_scope("layer_out"):
+        layer = exchange_rows(layer)
     gq, gk, gv, glat1, late = call(
         functools.partial(attention_back_kernel, cols),
         [big, big, big, small, jax.ShapeDtypeStruct((rows * cols, R, 4 * D // (rows * cols)), BF)],
@@ -931,7 +947,7 @@
         mine_c = send_grads(late)
     with jax.named_scope("grads_b"):
         own_b, _ = gather_high(
-            sum_grads(after(mine_b, late), owners, mine_b.shape[2]), 1
+            sum_grads(after(mine_b, late, *layer), owners, mine_b.shape[2]), 1
         )
         own_c, _ = gather_high(sum_grads(mine_c, owners, mine_c.shape[2]))
         order_b = tuple(lead.index(place) for place in lead_table(rows, cols, 1))
@@ -939,19 +955,22 @@
     gmid = after(gmid, own)
     sent = call(
         functools.partial(back_kernel, lead, cols),
-        jax.ShapeDtypeStruct((cols, 2 * SEQ, hid), BF),
-        [sc, *pieces_q, xa, ln_gain, gq, gk, gv, glat1, qkv_down, gmid, layer],
-        [pltpu.SMEM] + any_space + [pl.ANY] + [VMEM] * 5 + [pl.ANY] * 3,
+        [shaped(hid, BF)] * cols,
+        [sc, *pieces_q, xa, ln_gain, gq, gk, gv, glat1, qkv_down, gmid],
+        [pltpu.SMEM] + any_space + [pl.ANY] + [VMEM] * 5 + [pl.ANY] * 2,
         scratch
         + [VMEM((SEQ, D), F32), rows_space, VMEM((R, D), BF), VMEM((SEQ, D), F32)]
-        + [pltpu.SemaphoreType.DMA((4,))],
+        + [pltpu.SemaphoreType.DMA((3,)), VMEM((SEQ, D), BF)],
         mib=BACK,
     )
     with jax.named_scope("grads"):
         one, two = swap(own, flip_one), swap(own, flip_two)
-        own, one, two = after_all((own, one, two), sent)
+        own, one, two = after_all((own, one, two), *sent)
+        layer_out = stacked(after_all(layer, one, two), column, pl.ANY)
         both = swap(one, flip_two)
-        pieces = with_cores([own, one, two, both])
+        away = [swap(p, flip_core) for p in (own, one, two)]
+        both = after(both, layer_out)
+        pieces = [own, one, two, both] + away + [swap(both, flip_core)]
         half = FF // cols // 2
         map_a, map_b = (
             tuple(
@@ -968,16 +987,15 @@
         sums = spread(sc, pieces, parts, [map_a, map_b, map_c], shapes)
 
     with jax.named_scope("rows_out"):
-        sent = after(sent, pieces[4])
-        rows_out = lax.all_to_all(sent, "col", split_axis=0, concat_axis=0, tiled=True)
-    layer, grad_in = rows_out[:, :SEQ], rows_out[:, SEQ:]
+        grad_rows = exchange_rows(after_all(sent, *away))
+        grad_in = stacked(after_all(grad_rows, sums[0]), column, pl.ANY)
 
     def split(table):
         return table.reshape((NA, R) + table.shape[1:])
 
     g_fc1_up, g_fc2_down, g_proj_down, g_proj_up, g_fc1_down, g_fc2_up = map(split, sums[:6])
     return (
-        layer.reshape(cols * SEQ, hid),
+        layer_out.reshape(cols * SEQ, hid),
         grad_in.reshape(cols * SEQ, hid),
         split(sums[6]),
         jnp.swapaxes(sums[7], 1, 2),

time: 260 us -> 258 us (level)
  waiting for transfers between devices: 107 us -> 101 us
  starting transfers between devices: 52.4 us -> 55.3 us
    ppermute x45 -> x51, starting transfers between devices: 37 us -> 43.3 us  [swap(): return lax.ppermute(block, BOTH, pairs)]
    all_to_all x1 -> x0, waiting for transfers between devices: 3.58 us -> none  [per_device(): lax.all_to_all(sent, 'col', split_axis=0, concat_axis=0, tiled=True)]
    all_to_all x1 -> x0, starting transfers between devices: 3.54 us -> none  [per_device(): lax.all_to_all(sent, 'col', split_axis=0, concat_axis=0, tiled=True)]
    pallas_call x17 -> x19, Pallas kernels: 87.6 us -> 89.1 us  [call(): pl.pallas_call(kernel, out_shape=outs, in_specs=[pl.BlockSpec(memory_spac...]
    ppermute x45 -> x51, waiting for transfers between devices: 96.2 us -> 96.2 us  [swap(): return lax.ppermute(block, BOTH, pairs)]
  transfers between devices with their start and end apart: 49 -> 54, of which waited for: 24 -> 22; matrix products, arithmetic and copies ran while one was open for 1% -> 1% of each run, Pallas kernels for 25% -> 25%
where the time goes in v9:
time: 258 us; the launch traced here: 257 us
  waiting for transfers between devices  101 us (39%)
  Pallas kernels  89.1 us (35%)
  starting transfers between devices  55.3 us (21%)
  local copies, waits for them, and re-layouts  7.26 us (3%)
  between operations  3.45 us (1%)
    ppermute x51, waiting for transfers between devices, swap(): return lax.ppermute(block, BOTH, pairs)  96.2 us
    pallas_call x19, Pallas kernels, call(): pl.pallas_call(kernel, out_shape=outs, in_specs=[pl.BlockSpec(memory_spac...  89.1 us
    ppermute x51, starting transfers between devices, swap(): return lax.ppermute(block, BOTH, pairs)  43.3 us
    all_to_all x2, starting transfers between devices, send_grads(): return lax.all_to_all(grads, BOTH, split_axis=0, concat_axis=0, tiled=True)  7.56 us
    all_to_all x2, waiting for transfers between devices, send_grads(): return lax.all_to_all(grads, BOTH, split_axis=0, concat_axis=0, tiled=True)  5.21 us
  transfers between devices with their start and end apart: 54, of which 22 were waited for; matrix products, arithmetic and copies ran while one was open for 1% of the time, Pallas kernels for 25%

profile of v9, /device:TPU:0, one launch (start us, length us, event | category | flops | bytes accessed | tf_op | source)
XLA Modules:
  0.0 257.3 jit_solution(17089339518565659047)
XLA Ops:
  0.7 2.7 %shard_map.276 = (bf16[4,656,256]{2,1,0:T(8,128)(2,1)}, bf16[128,1024]{1,0:T(8,128)(2,1)}) custom-call(bf16[4,320,256]{2,1,0:T(8,128)(2,1)} %bitcast.50, bf16[4,320,256]{2,1,0:T(8,128)(2,1)} %bitcast.51, bf16[2,256]{1,0:T(2,128)(2,1)} %bias_qv.1, bf16[1024]{0:T(1024)(128)(2,1)} %bias_f.1, bf16[3,128,256]{2,1,0:T(8,128)(2,1)} %wq.1, bf16[256,128]{1,0:T(8,128)(2,1)} %wp.1), custom_call_target="tpu_custom_call" | custom-call | tf_op jit(solution)/shard_map/pallas_call | solution.py:54
  3.4 4.4 %all-to-all-start = ((bf16[4,656,256]{2,1,0:T(8,128)(2,1)}), bf16[4,656,256]{2,1,0:T(8,128)(2,1)}, u32[]{:S(2)}, u32[]{:S(2)}) async-start(bf16[4,656,256]{2,1,0:T(8,128)(2,1)} %get-tuple-element.97), calls=%async_computation | async-start | bytes 2686976 | tf_op jit(solution)/shard_map/all_to_all | solution.py:811
  7.8 5.1 %collective-permute-start.2 = (bf16[128,1024]{1,0:T(8,128)(2,1)S(1)}, bf16[128,1024]{1,0:T(8,128)(2,1)S(1)}, u32[]{:S(2)}, u32[]{:S(2)}) collective-permute-start(bf16[128,1024]{1,0:T(8,128)(2,1)S(1)} %copy-done.8), channel_id=1, source_target_pairs={{0,24},{1,25},{2,26},{3,27},{4,28},{5,29},{6,30},{7,31},{8,16},{9,... | collective-permute-start | bytes 786440 | tf_op jit(solution)/shard_map/q_high/ppermute | solution.py:75
  13.0 0.6 collective-permute-start
  13.6 0.6 dynamic_slice.8
  16.1 0.7 pad_add_fusion.3.sc.refs_0_
  16.9 0.8 shard_map.277
  17.7 0.7 copy-done.6
  18.4 0.7 copy-done.7
  19.1 0.6 dynamic-slice_bitcast_fusion.refs_14_.refs_9_
  20.3 15.6 %collective-permute-done.1.refs_2_ = bf16[128,1024]{1,0:T(8,128)(2,1)S(1)} collective-permute-done((bf16[128,1024]{1,0:T(8,128)(2,1)S(1)}, bf16[128,1024]{1,0:T(8,128)(2,1)S(1)}, u32[]{:S(2)}, u32[]{:S(2)}) %collective-permute-start.1) | collective-permute-done | bytes 262176 | tf_op jit(solution)/shard_map/q_high/ppermute | solution.py:75
  36.0 1.6 collective-permute-start.7
  37.6 1.7 collective-permute-start.6
  39.2 2.5 collective-permute-start.5
  41.7 1.9 collective-permute-start.3
  43.6 6.8 %collective-permute-done.5.refs_3_ = bf16[128,1024]{1,0:T(8,128)(2,1)S(1)} collective-permute-done((bf16[128,1024]{1,0:T(8,128)(2,1)S(1)}, bf16[128,1024]{1,0:T(8,128)(2,1)S(1)}, u32[]{:S(2)}, u32[]{:S(2)}) %collective-permute-start.5) | collective-permute-done | bytes 262176 | tf_op jit(solution)/shard_map/fa_high/ppermute | solution.py:75
  50.4 11.8 %collective-permute-done.4.refs_2_ = bf16[128,1024]{1,0:T(8,128)(2,1)S(1)} collective-permute-done((bf16[128,1024]{1,0:T(8,128)(2,1)S(1)}, bf16[128,1024]{1,0:T(8,128)(2,1)S(1)}, u32[]{:S(2)}, u32[]{:S(2)}) %collective-permute-start.4) | collective-permute-done | bytes 262176 | tf_op jit(solution)/shard_map/fa_high/ppermute | solution.py:75
  62.2 1.2 collective-permute-start.14
  63.9 13.1 %collective-permute-done.14.refs_4_.refs_12_ = bf16[4,128,1024]{2,1,0:T(8,128)(2,1)S(1)} collective-permute-done((bf16[4,128,1024]{2,1,0:T(8,128)(2,1)S(1)}, bf16[4,128,1024]{2,1,0:T(8,128)(2,1)S(1)}, u32[]{:S(2)}, u32[]{:S(2)}) %collective-permute-start.14) | collective-permute-done | bytes 1048608 | tf_op jit(solution)/shard_map/q_both/ppermute | solution.py:75
  77.2 1.2 collective-permute-start.19
  78.5 0.6 collective-permute-start.18
  79.1 2.5 collective-permute-start.13
  81.6 1.0 copy-done.21
  82.6 1.9 collective-permute-start.11
  84.5 18.0 %shard_map.278 = (bf16[320,1024]{1,0:T(8,128)(2,1)}, bf16[320,16]{1,0:T(8,128)(2,1)}, bf16[320,1024]{1,0:T(8,128)(2,1)}, bf16[320,1024]{1,0:T(8,128)(2,1)}, bf16...) custom-call(s32[4]{0:T(128)} %copy-done.13, ...), custom_call_target="tpu_custom_call" | custom-call | tf_op jit(solution)/shard_map/pallas_call | solution.py:54
  102.5 0.7 collective-permute-done.12.refs_2_
  103.3 1.2 collective-permute-start.26
  105.2 4.4 %collective-permute-done.16 = s32[4]{0:T(128)S(1)} collective-permute-done((s32[4]{0:T(128)S(1)}, s32[4]{0:T(128)S(1)}, u32[]{:S(2)}, u32[]{:S(2)}) %collective-permute-start.16) | collective-permute-done | bytes 48 | tf_op jit(solution)/shard_map/ppermute | solution.py:75
  110.4 3.4 %collective-permute-done.17 = s32[2,4]{1,0:T(2,128)S(1)} collective-permute-done((s32[2,4]{1,0:T(2,128)S(1)}, s32[2,4]{1,0:T(2,128)S(1)}, u32[]{:S(2)}, u32[]{:S(2)}) %collective-permute-start.17) | collective-permute-done | bytes 64 | tf_op jit(solution)/shard_map/ppermute | solution.py:75
  113.9 4.6 %collective-permute-done.26.refs_4_ = bf16[4,128,1024]{2,1,0:T(8,128)(2,1)} collective-permute-done((bf16[4,128,1024]{2,1,0:T(8,128)(2,1)}, bf16[4,128,1024]{2,1,0:T(8,128)(2,1)}, u32[]{:S(2)}, u32[]{:S(2)}) %collective-permute-start.26) | collective-permute-done | bytes 1048608 | tf_op jit(solution)/shard_map/fa_both/ppermute | solution.py:75
  119.0 1.2 collective-permute-start.24
  120.2 0.7 collective-permute-start.23
  121.0 1.5 collective-permute-start.25
  122.5 15.4 %shard_map.279 = (f32[320,1024]{1,0:T(8,128)}, f32[320,1024]{1,0:T(8,128)}, f32[320,16]{1,0:T(8,128)}, f32[320,16]{1,0:T(8,128)}, bf16[320,1024]{1,0:T(8,128)(2,1)}, /*index=5*/bf16[32,16,128]{2,1,0:T(8,128)(2,1)}) custom-call(s32[4]{0:T(128)} %copy-done.13, bf16[4,128,1024]{2,1,0:T(8,128)(2,1)} %copy-done.3, ...), custom_call_target="tpu_custom_call" | custom-call | tf_op jit(solution)/shard_map/pallas_call | solution.py:54
  137.9 6.7 %collective-permute-done.25 = s32[2,2,4]{2,1,0:T(2,128)S(1)} collective-permute-done((s32[2,2,4]{2,1,0:T(2,128)S(1)}, s32[2,2,4]{2,1,0:T(2,128)S(1)}, u32[]{:S(2)}, u32[]{:S(2)}) %collective-permute-start.25) | collective-permute-done | bytes 96 | tf_op jit(solution)/shard_map/ppermute | solution.py:75
  144.7 1.7 collective-permute-start.28
  146.9 12.6 %collective-permute-done.28.refs_4_ = bf16[4,128,1024]{2,1,0:T(8,128)(2,1)S(1)} collective-permute-done((bf16[4,128,1024]{2,1,0:T(8,128)(2,1)S(1)}, bf16[4,128,1024]{2,1,0:T(8,128)(2,1)S(1)}, u32[]{:S(2)}, u32[]{:S(2)}) %collective-permute-start.28) | collective-permute-done | bytes 1048608 | tf_op jit(solution)/shard_map/fb_both/ppermute | solution.py:75
  159.5 2.6 %collective-permute-done.32.refs_8_ = bf16[4,128,1024]{2,1,0:T(8,128)(2,1)S(1)} collective-permute-done((bf16[4,128,1024]{2,1,0:T(8,128)(2,1)S(1)}, bf16[4,128,1024]{2,1,0:T(8,128)(2,1)S(1)}, u32[]{:S(2)}, u32[]{:S(2)}) %collective-permute-start.32) | collective-permute-done | bytes 1048608 | tf_op jit(solution)/shard_map/fb_core/ppermute | solution.py:75
  162.1 1.0 copy-done.28
  163.2 19.1 %shard_map.280 = (bf16[320,256]{1,0:T(8,128)(2,1)}, bf16[320,256]{1,0:T(8,128)(2,1)}, bf16[320,256]{1,0:T(8,128)(2,1)}, bf16[320,256]{1,0:T(8,128)(2,1)}, bf16[3...) custom-call(s32[4]{0:T(128)} %copy-done.13, bf16[4,128,1024]{2,1,0:T(8,128)(2,1)} %copy-done.4, ...), custom_call_target="tpu_custom_call" | custom-call | tf_op jit(solution)/shard_map/pallas_call | solution.py:54
  182.3 3.6 %all-to-all-start.1 = ((bf16[32,16,384]{2,1,0:T(8,128)(2,1)}), bf16[32,16,384]{2,1,0:T(8,128)(2,1)S(1)}, u32[]{:S(2)}, u32[]{:S(2)}) async-start(bf16[32,16,384]{2,1,0:T(8,128)(2,1)} %get-tuple-element.135), calls=%async_computation.1 | async-start | bytes 786432 | tf_op jit(solution)/shard_map/grads_b_send/all_to_all | solution.py:712
  186.2 1.7 collective-permute-start.34
  188.6 10.8 %shard_map.281 = (bf16[320,1024]{1,0:T(8,128)(2,1)}, bf16[320,1024]{1,0:T(8,128)(2,1)}, bf16[320,1024]{1,0:T(8,128)(2,1)}, bf16[320,16]{1,0:T(8,128)(2,1)}, bf16[32,16,128]{2,1,0:T(8,128)(2,1)}) custom-call(s32[4]{0:T(128)} %copy-done.13, f32[320,1]{1,0:T(8,128)} %copy-done.7, bf16[320,1024]{1,0:T(8,128)(2,1)} %get-tuple-element.136.refs_2_, ...), custom_call_target="tpu_custom_call" | custom-call | tf_op jit(solution)/shard_map/pallas_call | solution.py:54
  199.5 0.7 grads_b.6
  200.2 2.6 %collective-permute-start.36 = (bf16[128,384]{1,0:T(8,128)(2,1)S(1)}, bf16[128,384]{1,0:T(8,128)(2,1)S(1)}, u32[]{:S(2)}, u32[]{:S(2)}) collective-permute-start(bf16[128,384]{1,0:T(8,128)(2,1)S(1)} %bitcast.43), channel_id=1, source_target_pairs={{0,16},{1,17},{2,18},{3,19},{4,20},{5,21},{6,22},{7,23},{8,24},{9,... | collective-permute-start | bytes 294920 | tf_op jit(solution)/shard_map/grads_b/ppermute | solution.py:75
  202.8 3.9 %all-to-all-start.2 = ((bf16[32,16,128]{2,1,0:T(8,128)(2,1)}), bf16[32,16,128]{2,1,0:T(8,128)(2,1)S(1)}, u32[]{:S(2)}, u32[]{:S(2)}) async-start(bf16[32,16,128]{2,1,0:T(8,128)(2,1)} %get-tuple-element.142), calls=%async_computation.2 | async-start | bytes 262144 | tf_op jit(solution)/shard_map/grads_c_send/all_to_all | solution.py:712
  206.8 1.6 collective-permute-done.36.refs_1_
  208.6 0.9 collective-permute-start.37
  209.6 5.2 %all-to-all-done.2.mine = bf16[32,16,128]{2,1,0:T(8,128)(2,1)S(1)} async-done(((bf16[32,16,128]{2,1,0:T(8,128)(2,1)}), bf16[32,16,128]{2,1,0:T(8,128)(2,1)S(1)}, u32[]{:S(2)}, u32[]{:S(2)}) %all-to-all-start.2) | async-done | bytes 131104 | tf_op jit(solution)/shard_map/grads_c_send/all_to_all | solution.py:712
  214.8 0.7 grads_b.9
  215.5 1.5 collective-permute-start.40
  217.0 0.7 collective-permute-start.39
  217.7 2.3 collective-permute-start.38
  220.0 1.6 collective-permute-done.40.refs_3_
  223.1 0.7 collective-permute-start.42
  223.8 0.8 collective-permute-start.41
  224.6 10.7 %shard_map.282 = (bf16[320,256]{1,0:T(8,128)(2,1)}, bf16[320,256]{1,0:T(8,128)(2,1)}, bf16[320,256]{1,0:T(8,128)(2,1)}, bf16[320,256]{1,0:T(8,128)(2,1)}) custom-call(s32[4]{0:T(128)} %copy-done.13, bf16[4,128,1024]{2,1,0:T(8,128)(2,1)} %copy-done.2, bf16[4,128,1024]{2,1,0:T(8,128)(2,1)} %copy-done.16, bf16[4,128,1024]{2,1,0:T(8,128)(2,1)} %copy-done.15, ...), custom_call_target="tpu_custom_call" | custom-call | tf_op jit(solution)/shard_map/pallas_call | solution.py:54
  235.4 1.8 collective-permute-done.42.refs_3_
  238.0 0.9 grads.2
  238.9 7.5 %collective-permute-done.49.refs_4_ = bf16[4,128,512]{2,1,0:T(8,128)(2,1)S(1)} collective-permute-done((bf16[4,128,512]{2,1,0:T(8,128)(2,1)S(1)}, bf16[4,128,512]{2,1,0:T(8,128)(2,1)S(1)}, u32[]{:S(2)}, u32[]{:S(2)}) %collective-permute-start.49) | collective-permute-done | bytes 524320 | tf_op jit(solution)/shard_map/grads/ppermute | solution.py:75
  247.0 0.9 collective-permute-start.47
  248.5 0.8 copy-done.35
  249.3 6.9 %grads.3 = (f32[128,4096]{1,0:T(8,128)}, f32[128,4096]{1,0:T(8,128)}, f32[128,1024]{1,0:T(8,128)}, f32[128,1024]{1,0:T(8,128)}, f32[128,1024]{1,0:T(8,128)}, /*i...) custom-call(s32[4]{0:T(128)} %copy-done.13, bf16[4,128,512]{2,1,0:T(8,128)(2,1)} %copy-done.5, ...), custom_call_target="tpu_custom_call" | custom-call | tf_op jit(solution)/shard_map/grads/pallas_call | solution.py:54
  256.3 0.9 rows_out.1
  (154 shorter events, 9.1 us)
Async XLA Ops:
  0.6 18.4 %copy-start = (bf16[8,16,3,1024]{3,1,2,0:T(8,128)(2,1)S(1)}, bf16[8,16,3,1024]{3,1,2,0:T(8,128)(2,1)}, u32[]{:S(2)}) copy-start(bf16[8,16,3,1024]{3,1,2,0:T(8,128)(2,1)} %param.35) | copy-start | bytes 2359300
  3.4 32.6 %all-to-all-start = ((bf16[4,656,256]{2,1,0:T(8,128)(2,1)}), bf16[4,656,256]{2,1,0:T(8,128)(2,1)}, u32[]{:S(2)}, u32[]{:S(2)}) async-start(bf16[4,656,256]{2,1,0:T(8,128)(2,1)} %get-tuple-element.97), calls=%async_computation | async-start | bytes 2686976 | tf_op jit(solution)/shard_map/all_to_all | solution.py:811
  7.8 12.4 %collective-permute-start.2 = (bf16[128,1024]{1,0:T(8,128)(2,1)S(1)}, bf16[128,1024]{1,0:T(8,128)(2,1)S(1)}, u32[]{:S(2)}, u32[]{:S(2)}) collective-permute-start(bf16[128,1024]{1,0:T(8,128)(2,1)S(1)} %copy-done.8), channel_id=1, source_target_pairs={{0,24},{1,25},{2,26},{3,27},{4,28},{5,29},{6,30},{7,31},{8,16},{9,... | collective-permute-start | bytes 786440 | tf_op jit(solution)/shard_map/q_high/ppermute | solution.py:75
  13.0 22.8 %collective-permute-start.1 = (bf16[128,1024]{1,0:T(8,128)(2,1)S(1)}, bf16[128,1024]{1,0:T(8,128)(2,1)S(1)}, u32[]{:S(2)}, u32[]{:S(2)}) collective-permute-start(bf16[128,1024]{1,0:T(8,128)(2,1)S(1)} %copy-done.8), channel_id=1, source_target_pairs={{0,16},{1,17},{2,18},{3,19},{4,20},{5,21},{6,22},{7,23},{8,24},{9,... | collective-permute-start | bytes 786440 | tf_op jit(solution)/shard_map/q_high/ppermute | solution.py:75
  13.0 22.8 %collective-permute-start = (bf16[128,1024]{1,0:T(8,128)(2,1)S(1)}, bf16[128,1024]{1,0:T(8,128)(2,1)S(1)}, u32[]{:S(2)}, u32[]{:S(2)}) collective-permute-start(bf16[128,1024]{1,0:T(8,128)(2,1)S(1)} %copy-done.8), channel_id=1, source_target_pairs={{0,8},{1,9},{2,10},{3,11},{4,12},{5,13},{6,14},{7,15},{8,0},{9,1},... | collective-permute-start | bytes 786440 | tf_op jit(solution)/shard_map/q_high/ppermute | solution.py:75
  16.9 19.1 %copy-start.13 = (s32[4]{0:T(128)}, s32[4]{0:T(128)S(1)}, u32[]{:S(2)}) copy-start(s32[4]{0:T(128)S(1)} %pad_add_fusion.3.sc.refs_0_) | copy-start | bytes 52
  36.0 48.5 %copy-start.2 = (bf16[4,128,1024]{2,1,0:T(8,128)(2,1)}, bf16[4,128,1024]{2,1,0:T(8,128)(2,1)S(1)}, u32[]{:S(2)}) copy-start(bf16[4,128,1024]{2,1,0:T(8,128)(2,1)S(1)} %q_high.1.refs_1_.refs_9_) | copy-start | bytes 3145732
  36.0 26.2 %collective-permute-start.7 = (bf16[4,128,1024]{2,1,0:T(8,128)(2,1)S(1)}, bf16[4,128,1024]{2,1,0:T(8,128)(2,1)S(1)}, u32[]{:S(2)}, u32[]{:S(2)}) collective-permute-start(bf16[4,128,1024]{2,1,0:T(8,128)(2,1)S(1)} %q_high.1.refs_1_.refs_9_), channel_id=1, source_target_pairs={{0,4},{1,3},{2,6},{3,1},{4,0},{5,7},{6,2},{7,5},{8,12},{9,11},{10,... | collective-permute-start | bytes 3145736 | tf_op jit(solution)/shard_map/q_two/ppermute | solution.py:75
  37.6 24.6 %collective-permute-start.6 = (bf16[4,128,1024]{2,1,0:T(8,128)(2,1)S(1)}, bf16[4,128,1024]{2,1,0:T(8,128)(2,1)S(1)}, u32[]{:S(2)}, u32[]{:S(2)}) collective-permute-start(bf16[4,128,1024]{2,1,0:T(8,128)(2,1)S(1)} %q_high.1.refs_1_.refs_9_), channel_id=1, source_target_pairs={{0,2},{1,5},{2,0},{3,7},{4,6},{5,1},{6,4},{7,3},{8,10},{9,13},{10,... | collective-permute-start | bytes 3145736 | tf_op jit(solution)/shard_map/q_one/ppermute | solution.py:75
  39.2 11.1 %collective-permute-start.5 = (bf16[128,1024]{1,0:T(8,128)(2,1)S(1)}, bf16[128,1024]{1,0:T(8,128)(2,1)S(1)}, u32[]{:S(2)}, u32[]{:S(2)}) collective-permute-start(bf16[128,1024]{1,0:T(8,128)(2,1)S(1)} %get-tuple-element.100.refs_0_), channel_id=1, source_target_pairs={{0,24},{1,25},{2,26},{3,27},{4,28},{5,29},{6,30},{7,31},{8,16},{9,... | collective-permute-start | bytes 786440 | tf_op jit(solution)/shard_map/fa_high/ppermute | solution.py:75
  41.7 20.4 %collective-permute-start.4 = (bf16[128,1024]{1,0:T(8,128)(2,1)S(1)}, bf16[128,1024]{1,0:T(8,128)(2,1)S(1)}, u32[]{:S(2)}, u32[]{:S(2)}) collective-permute-start(bf16[128,1024]{1,0:T(8,128)(2,1)S(1)} %get-tuple-element.100.refs_0_), channel_id=1, source_target_pairs={{0,16},{1,17},{2,18},{3,19},{4,20},{5,21},{6,22},{7,23},{8,24},{9,... | collective-permute-start | bytes 786440 | tf_op jit(solution)/shard_map/fa_high/ppermute | solution.py:75
  41.7 20.4 %collective-permute-start.3 = (bf16[128,1024]{1,0:T(8,128)(2,1)S(1)}, bf16[128,1024]{1,0:T(8,128)(2,1)S(1)}, u32[]{:S(2)}, u32[]{:S(2)}) collective-permute-start(bf16[128,1024]{1,0:T(8,128)(2,1)S(1)} %get-tuple-element.100.refs_0_), channel_id=1, source_target_pairs={{0,8},{1,9},{2,10},{3,11},{4,12},{5,13},{6,14},{7,15},{8,0},{9,1},... | collective-permute-start | bytes 786440 | tf_op jit(solution)/shard_map/fa_high/ppermute | solution.py:75
  62.2 22.3 %copy-start.15 = (bf16[4,128,1024]{2,1,0:T(8,128)(2,1)}, bf16[4,128,1024]{2,1,0:T(8,128)(2,1)S(1)}, u32[]{:S(2)}) copy-start(bf16[4,128,1024]{2,1,0:T(8,128)(2,1)S(1)} %collective-permute-done.7.refs_3_.refs_11_) | copy-start | bytes 3145732
  62.2 22.3 %copy-start.16 = (bf16[4,128,1024]{2,1,0:T(8,128)(2,1)}, bf16[4,128,1024]{2,1,0:T(8,128)(2,1)S(1)}, u32[]{:S(2)}) copy-start(bf16[4,128,1024]{2,1,0:T(8,128)(2,1)S(1)} %collective-permute-done.6.refs_2_.refs_10_) | copy-start | bytes 3145732
  62.2 14.9 %collective-permute-start.14 = (bf16[4,128,1024]{2,1,0:T(8,128)(2,1)S(1)}, bf16[4,128,1024]{2,1,0:T(8,128)(2,1)S(1)}, u32[]{:S(2)}, u32[]{:S(2)}) collective-permute-start(bf16[4,128,1024]{2,1,0:T(8,128)(2,1)S(1)} %collective-permute-done.6.refs_2_.refs_10_), channel_id=1, source_target_pairs={{0,4},{1,3},{2,6},{3,1},{4,0},{5,7},{6,2},{7,5},{8,12},{9,11},{10,... | collective-permute-start | bytes 3145736 | tf_op jit(solution)/shard_map/q_both/ppermute | solution.py:75
  63.4 13.8 %collective-permute-start.8 = (bf16[4,128,1024]{2,1,0:T(8,128)(2,1)S(1)}, bf16[4,128,1024]{2,1,0:T(8,128)(2,1)S(1)}, u32[]{:S(2)}, u32[]{:S(2)}) collective-permute-start(bf16[4,128,1024]{2,1,0:T(8,128)(2,1)S(1)} %q_high.1.refs_1_.refs_9_), channel_id=1, source_target_pairs={{0,1},{1,0},{2,3},{3,2},{4,5},{5,4},{6,7},{7,6},{8,9},{9,8},{10,11... | collective-permute-start | bytes 3145736 | tf_op jit(solution)/shard_map/q_core/ppermute | solution.py:75
  63.4 13.8 %collective-permute-start.10 = (bf16[4,128,1024]{2,1,0:T(8,128)(2,1)S(1)}, bf16[4,128,1024]{2,1,0:T(8,128)(2,1)S(1)}, u32[]{:S(2)}, u32[]{:S(2)}) collective-permute-start(bf16[4,128,1024]{2,1,0:T(8,128)(2,1)S(1)} %collective-permute-done.7.refs_3_.refs_11_), channel_id=1, source_target_pairs={{0,1},{1,0},{2,3},{3,2},{4,5},{5,4},{6,7},{7,6},{8,9},{9,8},{10,11... | collective-permute-start | bytes 3145736 | tf_op jit(solution)/shard_map/q_core/ppermute | solution.py:75
  63.9 13.3 %collective-permute-start.9 = (bf16[4,128,1024]{2,1,0:T(8,128)(2,1)S(1)}, bf16[4,128,1024]{2,1,0:T(8,128)(2,1)S(1)}, u32[]{:S(2)}, u32[]{:S(2)}) collective-permute-start(bf16[4,128,1024]{2,1,0:T(8,128)(2,1)S(1)} %collective-permute-done.6.refs_2_.refs_10_), channel_id=1, source_target_pairs={{0,1},{1,0},{2,3},{3,2},{4,5},{5,4},{6,7},{7,6},{8,9},{9,8},{10,11... | collective-permute-start | bytes 3145736 | tf_op jit(solution)/shard_map/q_core/ppermute | solution.py:75
  77.0 4.5 %collective-permute-start.15 = (bf16[4,128,1024]{2,1,0:T(8,128)(2,1)S(1)}, bf16[4,128,1024]{2,1,0:T(8,128)(2,1)S(1)}, u32[]{:S(2)}, u32[]{:S(2)}) collective-permute-start(bf16[4,128,1024]{2,1,0:T(8,128)(2,1)S(1)} %collective-permute-done.14.refs_4_.refs_12_), channel_id=1, source_target_pairs={{0,1},{1,0},{2,3},{3,2},{4,5},{5,4},{6,7},{7,6},{8,9},{9,8},{10,11... | collective-permute-start | bytes 3145736 | tf_op jit(solution)/shard_map/q_core/ppermute | solution.py:75
  77.2 27.3 %copy-start.3 = (bf16[4,128,1024]{2,1,0:T(8,128)(2,1)}, bf16[4,128,1024]{2,1,0:T(8,128)(2,1)S(1)}, u32[]{:S(2)}) copy-start(bf16[4,128,1024]{2,1,0:T(8,128)(2,1)S(1)} %fa_high.1.refs_1_) | copy-start | bytes 3145732
  77.2 26.1 %collective-permute-start.19 = (bf16[4,128,1024]{2,1,0:T(8,128)(2,1)S(1)}, bf16[4,128,1024]{2,1,0:T(8,128)(2,1)}, u32[]{:S(2)}, u32[]{:S(2)}) collective-permute-start(bf16[4,128,1024]{2,1,0:T(8,128)(2,1)S(1)} %fa_high.1.refs_1_), channel_id=1, source_target_pairs={{0,4},{1,3},{2,6},{3,1},{4,0},{5,7},{6,2},{7,5},{8,12},{9,11},{10,... | collective-permute-start | bytes 3145736 | tf_op jit(solution)/shard_map/fa_two/ppermute | solution.py:75
  78.5 24.8 %collective-permute-start.18 = (bf16[4,128,1024]{2,1,0:T(8,128)(2,1)S(1)}, bf16[4,128,1024]{2,1,0:T(8,128)(2,1)}, u32[]{:S(2)}, u32[]{:S(2)}) collective-permute-start(bf16[4,128,1024]{2,1,0:T(8,128)(2,1)S(1)} %fa_high.1.refs_1_), channel_id=1, source_target_pairs={{0,2},{1,5},{2,0},{3,7},{4,6},{5,1},{6,4},{7,3},{8,10},{9,13},{10,... | collective-permute-start | bytes 3145736 | tf_op jit(solution)/shard_map/fa_one/ppermute | solution.py:75
  79.1 23.4 %collective-permute-start.13 = (bf16[128,1024]{1,0:T(8,128)(2,1)S(1)}, bf16[128,1024]{1,0:T(8,128)(2,1)S(1)}, u32[]{:S(2)}, u32[]{:S(2)}) collective-permute-start(bf16[128,1024]{1,0:T(8,128)(2,1)S(1)} %get-tuple-element.106.refs_0_), channel_id=1, source_target_pairs={{0,24},{1,25},{2,26},{3,27},{4,28},{5,29},{6,30},{7,31},{8,16},{9,... | collective-permute-start | bytes 786440 | tf_op jit(solution)/shard_map/fb_high/ppermute | solution.py:75
  81.5 21.6 %collective-permute-start.12 = (bf16[128,1024]{1,0:T(8,128)(2,1)S(1)}, bf16[128,1024]{1,0:T(8,128)(2,1)S(1)}, u32[]{:S(2)}, u32[]{:S(2)}) collective-permute-start(bf16[128,1024]{1,0:T(8,128)(2,1)S(1)} %get-tuple-element.106.refs_0_), channel_id=1, source_target_pairs={{0,16},{1,17},{2,18},{3,19},{4,20},{5,21},{6,22},{7,23},{8,24},{9,... | collective-permute-start | bytes 786440 | tf_op jit(solution)/shard_map/fb_high/ppermute | solution.py:75
  82.6 20.6 %collective-permute-start.11 = (bf16[128,1024]{1,0:T(8,128)(2,1)S(1)}, bf16[128,1024]{1,0:T(8,128)(2,1)S(1)}, u32[]{:S(2)}, u32[]{:S(2)}) collective-permute-start(bf16[128,1024]{1,0:T(8,128)(2,1)S(1)} %get-tuple-element.106.refs_0_), channel_id=1, source_target_pairs={{0,8},{1,9},{2,10},{3,11},{4,12},{5,13},{6,14},{7,15},{8,0},{9,1},... | collective-permute-start | bytes 786440 | tf_op jit(solution)/shard_map/fb_high/ppermute | solution.py:75
  103.3 15.1 %collective-permute-start.26 = (bf16[4,128,1024]{2,1,0:T(8,128)(2,1)}, bf16[4,128,1024]{2,1,0:T(8,128)(2,1)}, u32[]{:S(2)}, u32[]{:S(2)}) collective-permute-start(bf16[4,128,1024]{2,1,0:T(8,128)(2,1)} %collective-permute-done.18.refs_2_), channel_id=1, source_target_pairs={{0,4},{1,3},{2,6},{3,1},{4,0},{5,7},{6,2},{7,5},{8,12},{9,11},{10,... | collective-permute-start | bytes 3145736 | tf_op jit(solution)/shard_map/fa_both/ppermute | solution.py:75
  104.5 14.5 %collective-permute-start.20 = (bf16[4,128,1024]{2,1,0:T(8,128)(2,1)S(1)}, bf16[4,128,1024]{2,1,0:T(8,128)(2,1)}, u32[]{:S(2)}, u32[]{:S(2)}) collective-permute-start(bf16[4,128,1024]{2,1,0:T(8,128)(2,1)S(1)} %fa_high.1.refs_1_), channel_id=1, source_target_pairs={{0,1},{1,0},{2,3},{3,2},{4,5},{5,4},{6,7},{7,6},{8,9},{9,8},{10,11... | collective-permute-start | bytes 3145736 | tf_op jit(solution)/shard_map/fa_core/ppermute | solution.py:75
  104.5 14.5 %collective-permute-start.22 = (bf16[4,128,1024]{2,1,0:T(8,128)(2,1)}, bf16[4,128,1024]{2,1,0:T(8,128)(2,1)}, u32[]{:S(2)}, u32[]{:S(2)}) collective-permute-start(bf16[4,128,1024]{2,1,0:T(8,128)(2,1)} %collective-permute-done.19.refs_3_), channel_id=1, source_target_pairs={{0,1},{1,0},{2,3},{3,2},{4,5},{5,4},{6,7},{7,6},{8,9},{9,8},{10,11... | collective-permute-start | bytes 3145736 | tf_op jit(solution)/shard_map/fa_core/ppermute | solution.py:75
  105.0 14.0 %collective-permute-start.21 = (bf16[4,128,1024]{2,1,0:T(8,128)(2,1)}, bf16[4,128,1024]{2,1,0:T(8,128)(2,1)}, u32[]{:S(2)}, u32[]{:S(2)}) collective-permute-start(bf16[4,128,1024]{2,1,0:T(8,128)(2,1)} %collective-permute-done.18.refs_2_), channel_id=1, source_target_pairs={{0,1},{1,0},{2,3},{3,2},{4,5},{5,4},{6,7},{7,6},{8,9},{9,8},{10,11... | collective-permute-start | bytes 3145736 | tf_op jit(solution)/shard_map/fa_core/ppermute | solution.py:75
  105.2 41.2 %copy-start.4 = (bf16[4,128,1024]{2,1,0:T(8,128)(2,1)}, bf16[4,128,1024]{2,1,0:T(8,128)(2,1)S(1)}, u32[]{:S(2)}) copy-start(bf16[4,128,1024]{2,1,0:T(8,128)(2,1)S(1)} %fb_high.1.refs_1_) | copy-start | bytes 3145732
  105.2 4.5 %collective-permute-start.16 = (s32[4]{0:T(128)S(1)}, s32[4]{0:T(128)S(1)}, u32[]{:S(2)}, u32[]{:S(2)}) collective-permute-start(s32[4]{0:T(128)S(1)} %copy-done.36), channel_id=1, source_target_pairs={{0,16},{1,17},{2,18},{3,19},{4,20},{5,21},{6,22},{7,23},{8,24},{9,... | collective-permute-start | bytes 56 | tf_op jit(solution)/shard_map/ppermute | solution.py:75
  110.2 3.6 %collective-permute-start.17 = (s32[2,4]{1,0:T(2,128)S(1)}, s32[2,4]{1,0:T(2,128)S(1)}, u32[]{:S(2)}, u32[]{:S(2)}) collective-permute-start(s32[2,4]{1,0:T(2,128)S(1)} %gather_fusion), channel_id=1, source_target_pairs={{0,8},{1,9},{2,10},{3,11},{4,12},{5,13},{6,14},{7,15},{8,0},{9,1},... | collective-permute-start | bytes 104 | tf_op jit(solution)/shard_map/ppermute | solution.py:75
  118.4 4.1 %collective-permute-start.27 = (bf16[4,128,1024]{2,1,0:T(8,128)(2,1)}, bf16[4,128,1024]{2,1,0:T(8,128)(2,1)}, u32[]{:S(2)}, u32[]{:S(2)}) collective-permute-start(bf16[4,128,1024]{2,1,0:T(8,128)(2,1)} %collective-permute-done.26.refs_4_), channel_id=1, source_target_pairs={{0,1},{1,0},{2,3},{3,2},{4,5},{5,4},{6,7},{7,6},{8,9},{9,8},{10,11... | collective-permute-start | bytes 3145736 | tf_op jit(solution)/shard_map/fa_core/ppermute | solution.py:75
  119.0 25.6 %collective-permute-start.24 = (bf16[4,128,1024]{2,1,0:T(8,128)(2,1)S(1)}, bf16[4,128,1024]{2,1,0:T(8,128)(2,1)S(1)}, u32[]{:S(2)}, u32[]{:S(2)}) collective-permute-start(bf16[4,128,1024]{2,1,0:T(8,128)(2,1)S(1)} %fb_high.1.refs_1_), channel_id=1, source_target_pairs={{0,4},{1,3},{2,6},{3,1},{4,0},{5,7},{6,2},{7,5},{8,12},{9,11},{10,... | collective-permute-start | bytes 3145736 | tf_op jit(solution)/shard_map/fb_two/ppermute | solution.py:75
  120.2 24.4 %collective-permute-start.23 = (bf16[4,128,1024]{2,1,0:T(8,128)(2,1)S(1)}, bf16[4,128,1024]{2,1,0:T(8,128)(2,1)S(1)}, u32[]{:S(2)}, u32[]{:S(2)}) collective-permute-start(bf16[4,128,1024]{2,1,0:T(8,128)(2,1)S(1)} %fb_high.1.refs_1_), channel_id=1, source_target_pairs={{0,2},{1,5},{2,0},{3,7},{4,6},{5,1},{6,4},{7,3},{8,10},{9,13},{10,... | collective-permute-start | bytes 3145736 | tf_op jit(solution)/shard_map/fb_one/ppermute | solution.py:75
  121.0 23.6 %collective-permute-start.25 = (s32[2,2,4]{2,1,0:T(2,128)S(1)}, s32[2,2,4]{2,1,0:T(2,128)S(1)}, u32[]{:S(2)}, u32[]{:S(2)}) collective-permute-start(s32[2,2,4]{2,1,0:T(2,128)S(1)} %gather_fusion.1), channel_id=1, source_target_pairs={{0,4},{1,5},{2,6},{3,7},{4,0},{5,1},{6,2},{7,3},{8,12},{9,13},{10,... | collective-permute-start | bytes 200 | tf_op jit(solution)/shard_map/ppermute | solution.py:75
  144.6 18.5 %copy-start.22 = (bf16[4,128,1024]{2,1,0:T(8,128)(2,1)}, bf16[4,128,1024]{2,1,0:T(8,128)(2,1)S(1)}, u32[]{:S(2)}) copy-start(bf16[4,128,1024]{2,1,0:T(8,128)(2,1)S(1)} %collective-permute-done.24.refs_3_) | copy-start | bytes 3145732
  144.7 18.5 %copy-start.23 = (bf16[4,128,1024]{2,1,0:T(8,128)(2,1)}, bf16[4,128,1024]{2,1,0:T(8,128)(2,1)S(1)}, u32[]{:S(2)}) copy-start(bf16[4,128,1024]{2,1,0:T(8,128)(2,1)S(1)} %collective-permute-done.23.refs_2_) | copy-start | bytes 3145732
  144.7 14.8 %collective-permute-start.28 = (bf16[4,128,1024]{2,1,0:T(8,128)(2,1)S(1)}, bf16[4,128,1024]{2,1,0:T(8,128)(2,1)S(1)}, u32[]{:S(2)}, u32[]{:S(2)}) collective-permute-start(bf16[4,128,1024]{2,1,0:T(8,128)(2,1)S(1)} %collective-permute-done.23.refs_2_), channel_id=1, source_target_pairs={{0,4},{1,3},{2,6},{3,1},{4,0},{5,7},{6,2},{7,5},{8,12},{9,11},{10,... | collective-permute-start | bytes 3145736 | tf_op jit(solution)/shard_map/fb_both/ppermute | solution.py:75
  146.4 13.1 %collective-permute-start.30 = (bf16[4,128,1024]{2,1,0:T(8,128)(2,1)S(1)}, bf16[4,128,1024]{2,1,0:T(8,128)(2,1)S(1)}, u32[]{:S(2)}, u32[]{:S(2)}) collective-permute-start(bf16[4,128,1024]{2,1,0:T(8,128)(2,1)S(1)} %collective-permute-done.23.refs_2_), channel_id=1, source_target_pairs={{0,1},{1,0},{2,3},{3,2},{4,5},{5,4},{6,7},{7,6},{8,9},{9,8},{10,11... | collective-permute-start | bytes 3145736 | tf_op jit(solution)/shard_map/fb_core/ppermute | solution.py:75
  146.4 13.1 %collective-permute-start.29 = (bf16[4,128,1024]{2,1,0:T(8,128)(2,1)S(1)}, bf16[4,128,1024]{2,1,0:T(8,128)(2,1)S(1)}, u32[]{:S(2)}, u32[]{:S(2)}) collective-permute-start(bf16[4,128,1024]{2,1,0:T(8,128)(2,1)S(1)} %fb_high.1.refs_1_), channel_id=1, source_target_pairs={{0,1},{1,0},{2,3},{3,2},{4,5},{5,4},{6,7},{7,6},{8,9},{9,8},{10,11... | collective-permute-start | bytes 3145736 | tf_op jit(solution)/shard_map/fb_core/ppermute | solution.py:75
  146.9 12.6 %collective-permute-start.31 = (bf16[4,128,1024]{2,1,0:T(8,128)(2,1)S(1)}, bf16[4,128,1024]{2,1,0:T(8,128)(2,1)S(1)}, u32[]{:S(2)}, u32[]{:S(2)}) collective-permute-start(bf16[4,128,1024]{2,1,0:T(8,128)(2,1)S(1)} %collective-permute-done.24.refs_3_), channel_id=1, source_target_pairs={{0,1},{1,0},{2,3},{3,2},{4,5},{5,4},{6,7},{7,6},{8,9},{9,8},{10,11... | collective-permute-start | bytes 3145736 | tf_op jit(solution)/shard_map/fb_core/ppermute | solution.py:75
  159.5 2.7 %collective-permute-start.32 = (bf16[4,128,1024]{2,1,0:T(8,128)(2,1)S(1)}, bf16[4,128,1024]{2,1,0:T(8,128)(2,1)S(1)}, u32[]{:S(2)}, u32[]{:S(2)}) collective-permute-start(bf16[4,128,1024]{2,1,0:T(8,128)(2,1)S(1)} %collective-permute-done.28.refs_4_), channel_id=1, source_target_pairs={{0,1},{1,0},{2,3},{3,2},{4,5},{5,4},{6,7},{7,6},{8,9},{9,8},{10,11... | collective-permute-start | bytes 3145736 | tf_op jit(solution)/shard_map/fb_core/ppermute | solution.py:75
  182.3 17.2 %all-to-all-start.1 = ((bf16[32,16,384]{2,1,0:T(8,128)(2,1)}), bf16[32,16,384]{2,1,0:T(8,128)(2,1)S(1)}, u32[]{:S(2)}, u32[]{:S(2)}) async-start(bf16[32,16,384]{2,1,0:T(8,128)(2,1)} %get-tuple-element.135), calls=%async_computation.1 | async-start | bytes 786432 | tf_op jit(solution)/shard_map/grads_b_send/all_to_all | solution.py:712
  185.9 13.5 %collective-permute-start.33 = (bf16[320,256]{1,0:T(8,128)(2,1)}, bf16[320,256]{1,0:T(8,128)(2,1)S(1)}, u32[]{:S(2)}, u32[]{:S(2)}) collective-permute-start(bf16[320,256]{1,0:T(8,128)(2,1)} %get-tuple-element.130), channel_id=1, source_target_pairs={{0,1},{1,0},{2,3},{3,2},{4,5},{5,4},{6,7},{7,6},{8,9},{9,8},{10,11... | collective-permute-start | bytes 491528 | tf_op jit(solution)/shard_map/layer_out/ppermute | solution.py:75
  186.2 13.2 %collective-permute-start.34 = (bf16[320,256]{1,0:T(8,128)(2,1)}, bf16[320,256]{1,0:T(8,128)(2,1)S(1)}, u32[]{:S(2)}, u32[]{:S(2)}) collective-permute-start(bf16[320,256]{1,0:T(8,128)(2,1)} %get-tuple-element.131), channel_id=1, source_target_pairs={{0,2},{1,3},{2,0},{3,1},{4,6},{5,7},{6,4},{7,5},{8,10},{9,11},{10,... | collective-permute-start | bytes 491528 | tf_op jit(solution)/shard_map/layer_out/ppermute | solution.py:75
  187.9 11.6 %collective-permute-start.35 = (bf16[320,256]{1,0:T(8,128)(2,1)}, bf16[320,256]{1,0:T(8,128)(2,1)S(1)}, u32[]{:S(2)}, u32[]{:S(2)}) collective-permute-start(bf16[320,256]{1,0:T(8,128)(2,1)} %get-tuple-element.132), channel_id=1, source_target_pairs={{0,3},{1,2},{2,1},{3,0},{4,7},{5,6},{6,5},{7,4},{8,11},{9,10},{10,... | collective-permute-start | bytes 491528 | tf_op jit(solution)/shard_map/layer_out/ppermute | solution.py:75
  200.2 8.2 %collective-permute-start.36 = (bf16[128,384]{1,0:T(8,128)(2,1)S(1)}, bf16[128,384]{1,0:T(8,128)(2,1)S(1)}, u32[]{:S(2)}, u32[]{:S(2)}) collective-permute-start(bf16[128,384]{1,0:T(8,128)(2,1)S(1)} %bitcast.43), channel_id=1, source_target_pairs={{0,16},{1,17},{2,18},{3,19},{4,20},{5,21},{6,22},{7,23},{8,24},{9,... | collective-permute-start | bytes 294920 | tf_op jit(solution)/shard_map/grads_b/ppermute | solution.py:75
  202.8 12.0 %all-to-all-start.2 = ((bf16[32,16,128]{2,1,0:T(8,128)(2,1)}), bf16[32,16,128]{2,1,0:T(8,128)(2,1)S(1)}, u32[]{:S(2)}, u32[]{:S(2)}) async-start(bf16[32,16,128]{2,1,0:T(8,128)(2,1)} %get-tuple-element.142), calls=%async_computation.2 | async-start | bytes 262144 | tf_op jit(solution)/shard_map/grads_c_send/all_to_all | solution.py:712
  208.6 13.7 %collective-permute-start.37 = (bf16[2,128,384]{2,1,0:T(8,128)(2,1)S(1)}, bf16[2,128,384]{2,1,0:T(8,128)(2,1)S(1)}, u32[]{:S(2)}, u32[]{:S(2)}) collective-permute-start(bf16[2,128,384]{2,1,0:T(8,128)(2,1)S(1)} %grads_b.7), channel_id=1, source_target_pairs={{0,8},{1,9},{2,10},{3,11},{4,12},{5,13},{6,14},{7,15},{8,0},{9,1},... | collective-permute-start | bytes 589832 | tf_op jit(solution)/shard_map/grads_b/ppermute | solution.py:75
  215.5 6.1 %collective-permute-start.40 = (bf16[128,128]{1,0:T(8,128)(2,1)S(1)}, bf16[128,128]{1,0:T(8,128)(2,1)S(1)}, u32[]{:S(2)}, u32[]{:S(2)}) collective-permute-start(bf16[128,128]{1,0:T(8,128)(2,1)S(1)} %bitcast.46), channel_id=1, source_target_pairs={{0,24},{1,25},{2,26},{3,27},{4,28},{5,29},{6,30},{7,31},{8,16},{9,... | collective-permute-start | bytes 98312 | tf_op jit(solution)/shard_map/grads_b/ppermute | solution.py:75
  217.0 5.1 %collective-permute-start.39 = (bf16[128,128]{1,0:T(8,128)(2,1)S(1)}, bf16[128,128]{1,0:T(8,128)(2,1)S(1)}, u32[]{:S(2)}, u32[]{:S(2)}) collective-permute-start(bf16[128,128]{1,0:T(8,128)(2,1)S(1)} %bitcast.47), channel_id=1, source_target_pairs={{0,16},{1,17},{2,18},{3,19},{4,20},{5,21},{6,22},{7,23},{8,24},{9,... | collective-permute-start | bytes 98312 | tf_op jit(solution)/shard_map/grads_b/ppermute | solution.py:75
  217.7 4.5 %collective-permute-start.38 = (bf16[128,128]{1,0:T(8,128)(2,1)S(1)}, bf16[128,128]{1,0:T(8,128)(2,1)S(1)}, u32[]{:S(2)}, u32[]{:S(2)}) collective-permute-start(bf16[128,128]{1,0:T(8,128)(2,1)S(1)} %bitcast.48), channel_id=1, source_target_pairs={{0,8},{1,9},{2,10},{3,11},{4,12},{5,13},{6,14},{7,15},{8,0},{9,1},... | collective-permute-start | bytes 98312 | tf_op jit(solution)/shard_map/grads_b/ppermute | solution.py:75
  223.1 14.0 %collective-permute-start.42 = (bf16[4,128,512]{2,1,0:T(8,128)(2,1)S(1)}, bf16[4,128,512]{2,1,0:T(8,128)(2,1)S(1)}, u32[]{:S(2)}, u32[]{:S(2)}) collective-permute-start(bf16[4,128,512]{2,1,0:T(8,128)(2,1)S(1)} %grads_b.11.refs_1_), channel_id=1, source_target_pairs={{0,4},{1,3},{2,6},{3,1},{4,0},{5,7},{6,2},{7,5},{8,12},{9,11},{10,... | collective-permute-start | bytes 1572872 | tf_op jit(solution)/shard_map/grads/ppermute | solution.py:75
  223.8 13.3 %collective-permute-start.41 = (bf16[4,128,512]{2,1,0:T(8,128)(2,1)S(1)}, bf16[4,128,512]{2,1,0:T(8,128)(2,1)S(1)}, u32[]{:S(2)}, u32[]{:S(2)}) collective-permute-start(bf16[4,128,512]{2,1,0:T(8,128)(2,1)S(1)} %grads_b.11.refs_1_), channel_id=1, source_target_pairs={{0,2},{1,5},{2,0},{3,7},{4,6},{5,1},{6,4},{7,3},{8,10},{9,13},{10,... | collective-permute-start | bytes 1572872 | tf_op jit(solution)/shard_map/grads/ppermute | solution.py:75
  237.1 9.2 %collective-permute-start.49 = (bf16[4,128,512]{2,1,0:T(8,128)(2,1)S(1)}, bf16[4,128,512]{2,1,0:T(8,128)(2,1)S(1)}, u32[]{:S(2)}, u32[]{:S(2)}) collective-permute-start(bf16[4,128,512]{2,1,0:T(8,128)(2,1)S(1)} %collective-permute-done.41.refs_2_), channel_id=1, source_target_pairs={{0,4},{1,3},{2,6},{3,1},{4,0},{5,7},{6,2},{7,5},{8,12},{9,11},{10,... | collective-permute-start | bytes 1572872 | tf_op jit(solution)/shard_map/grads/ppermute | solution.py:75
  237.5 8.9 %collective-permute-start.43 = (bf16[4,128,512]{2,1,0:T(8,128)(2,1)S(1)}, bf16[4,128,512]{2,1,0:T(8,128)(2,1)S(1)}, u32[]{:S(2)}, u32[]{:S(2)}) collective-permute-start(bf16[4,128,512]{2,1,0:T(8,128)(2,1)S(1)} %grads_b.11.refs_1_), channel_id=1, source_target_pairs={{0,1},{1,0},{2,3},{3,2},{4,5},{5,4},{6,7},{7,6},{8,9},{9,8},{10,11... | collective-permute-start | bytes 1572872 | tf_op jit(solution)/shard_map/grads/ppermute | solution.py:75
  237.5 8.9 %collective-permute-start.45 = (bf16[4,128,512]{2,1,0:T(8,128)(2,1)S(1)}, bf16[4,128,512]{2,1,0:T(8,128)(2,1)S(1)}, u32[]{:S(2)}, u32[]{:S(2)}) collective-permute-start(bf16[4,128,512]{2,1,0:T(8,128)(2,1)S(1)} %collective-permute-done.42.refs_3_), channel_id=1, source_target_pairs={{0,1},{1,0},{2,3},{3,2},{4,5},{5,4},{6,7},{7,6},{8,9},{9,8},{10,11... | collective-permute-start | bytes 1572872 | tf_op jit(solution)/shard_map/grads/ppermute | solution.py:75
  238.0 8.4 %collective-permute-start.44 = (bf16[4,128,512]{2,1,0:T(8,128)(2,1)S(1)}, bf16[4,128,512]{2,1,0:T(8,128)(2,1)S(1)}, u32[]{:S(2)}, u32[]{:S(2)}) collective-permute-start(bf16[4,128,512]{2,1,0:T(8,128)(2,1)S(1)} %collective-permute-done.41.refs_2_), channel_id=1, source_target_pairs={{0,1},{1,0},{2,3},{3,2},{4,5},{5,4},{6,7},{7,6},{8,9},{9,8},{10,11... | collective-permute-start | bytes 1572872 | tf_op jit(solution)/shard_map/grads/ppermute | solution.py:75
  238.9 17.3 %copy-start.12 = (bf16[320,256]{1,0:T(8,128)(2,1)S(1)}, bf16[320,256]{1,0:T(8,128)(2,1)}, u32[]{:S(2)}) copy-start(bf16[320,256]{1,0:T(8,128)(2,1)} %get-tuple-element.167.refs_0_) | copy-start | bytes 491524
  246.4 2.0 collective-permute-start.50
  246.4 9.8 %collective-permute-start.46 = (bf16[320,256]{1,0:T(8,128)(2,1)}, bf16[320,256]{1,0:T(8,128)(2,1)S(1)}, u32[]{:S(2)}, u32[]{:S(2)}) collective-permute-start(bf16[320,256]{1,0:T(8,128)(2,1)} %get-tuple-element.162), channel_id=1, source_target_pairs={{0,1},{1,0},{2,3},{3,2},{4,5},{5,4},{6,7},{7,6},{8,9},{9,8},{10,11... | collective-permute-start | bytes 491528 | tf_op jit(solution)/shard_map/rows_out/ppermute | solution.py:75
  247.0 9.2 %collective-permute-start.47 = (bf16[320,256]{1,0:T(8,128)(2,1)}, bf16[320,256]{1,0:T(8,128)(2,1)S(1)}, u32[]{:S(2)}, u32[]{:S(2)}) collective-permute-start(bf16[320,256]{1,0:T(8,128)(2,1)} %get-tuple-element.163), channel_id=1, source_target_pairs={{0,2},{1,3},{2,0},{3,1},{4,6},{5,7},{6,4},{7,5},{8,10},{9,11},{10,... | collective-permute-start | bytes 491528 | tf_op jit(solution)/shard_map/rows_out/ppermute | solution.py:75
  247.9 8.4 %collective-permute-start.48 = (bf16[320,256]{1,0:T(8,128)(2,1)}, bf16[320,256]{1,0:T(8,128)(2,1)S(1)}, u32[]{:S(2)}, u32[]{:S(2)}) collective-permute-start(bf16[320,256]{1,0:T(8,128)(2,1)} %get-tuple-element.164), channel_id=1, source_target_pairs={{0,3},{1,2},{2,1},{3,0},{4,7},{5,6},{6,5},{7,4},{8,11},{9,10},{10,... | collective-permute-start | bytes 491528 | tf_op jit(solution)/shard_map/rows_out/ppermute | solution.py:75
  (27 other events, 162.8 us)

commit v10 on v9

--- a/solution.py
+++ b/solution.py
@@ -910,7 +910,7 @@
         both_b = swap(one_b, flip_two)
     with jax.named_scope("fb_core"):
         away_b = [swap(p, flip_core) for p in (own_b, one_b, two_b)]
-        pieces_b = [own_b, one_b, two_b, both_b] + away_b + [swap(both_b, flip_core)]
+        pieces_b = [own_b, one_b, two_b, both_b] + away_b + [swap(after(both_b, owners), flip_core)]
     *layer, gatt, gmid, grads_b = call(
         functools.partial(ffn_b_kernel, lead, cols),
         [shaped(hid, BF)] * cols + [big, wide]

time: 258 us -> 257 us (level)
  no operation moved by 1% of the time
where the time goes in v10:
time: 257 us; the launch traced here: 256 us
  waiting for transfers between devices  100 us (39%)
  Pallas kernels  88.9 us (35%)
  starting transfers between devices  55.6 us (22%)
  local copies, waits for them, and re-layouts  7.22 us (3%)
  between operations  3.43 us (1%)
    ppermute x51, waiting for transfers between devices, swap(): return lax.ppermute(block, BOTH, pairs)  96.3 us
    pallas_call x19, Pallas kernels, call(): pl.pallas_call(kernel, out_shape=outs, in_specs=[pl.BlockSpec(memory_spac...  88.9 us
    ppermute x51, starting transfers between devices, swap(): return lax.ppermute(block, BOTH, pairs)  44.3 us
    all_to_all x2, starting transfers between devices, send_grads(): return lax.all_to_all(grads, BOTH, split_axis=0, concat_axis=0, tiled=True)  6.88 us
  transfers between devices with their start and end apart: 54, of which 22 were waited for; matrix products, arithmetic and copies ran while one was open for 1% of the time, Pallas kernels for 25%

profile of v10, /device:TPU:0, one launch (start us, length us, event | category | flops | bytes accessed | tf_op | source)
XLA Modules:
  0.0 256.3 jit_solution(9513104100221105232)
XLA Ops:
  0.7 2.7 %shard_map.276 = (bf16[4,656,256]{2,1,0:T(8,128)(2,1)}, bf16[128,1024]{1,0:T(8,128)(2,1)}) custom-call(bf16[4,320,256]{2,1,0:T(8,128)(2,1)} %bitcast.50, bf16[4,320,256]{2,1,0:T(8,128)(2,1)} %bitcast.51, bf16[2,256]{1,0:T(2,128)(2,1)} %bias_qv.1, bf16[1024]{0:T(1024)(128)(2,1)} %bias_f.1, bf16[3,128,256]{2,1,0:T(8,128)(2,1)} %wq.1, bf16[256,128]{1,0:T(8,128)(2,1)} %wp.1), custom_call_target="tpu_custom_call" | custom-call | tf_op jit(solution)/shard_map/pallas_call | solution.py:54
  3.4 4.4 %all-to-all-start = ((bf16[4,656,256]{2,1,0:T(8,128)(2,1)}), bf16[4,656,256]{2,1,0:T(8,128)(2,1)}, u32[]{:S(2)}, u32[]{:S(2)}) async-start(bf16[4,656,256]{2,1,0:T(8,128)(2,1)} %get-tuple-element.98), calls=%async_computation | async-start | bytes 2686976 | tf_op jit(solution)/shard_map/all_to_all | solution.py:811
  7.8 5.1 %collective-permute-start.2 = (bf16[128,1024]{1,0:T(8,128)(2,1)S(1)}, bf16[128,1024]{1,0:T(8,128)(2,1)S(1)}, u32[]{:S(2)}, u32[]{:S(2)}) collective-permute-start(bf16[128,1024]{1,0:T(8,128)(2,1)S(1)} %copy-done.8), channel_id=1, source_target_pairs={{0,24},{1,25},{2,26},{3,27},{4,28},{5,29},{6,30},{7,31},{8,16},{9,... | collective-permute-start | bytes 786440 | tf_op jit(solution)/shard_map/q_high/ppermute | solution.py:75
  13.0 0.6 collective-permute-start
  16.1 0.7 pad_add_fusion.3.sc.refs_0_
  16.9 0.8 shard_map.277
  17.7 0.7 copy-done.6
  18.4 0.7 copy-done.7
  19.0 0.6 dynamic-slice_bitcast_fusion.refs_14_.refs_9_
  20.2 15.6 %collective-permute-done.1.refs_2_ = bf16[128,1024]{1,0:T(8,128)(2,1)S(1)} collective-permute-done((bf16[128,1024]{1,0:T(8,128)(2,1)S(1)}, bf16[128,1024]{1,0:T(8,128)(2,1)S(1)}, u32[]{:S(2)}, u32[]{:S(2)}) %collective-permute-start.1) | collective-permute-done | bytes 262176 | tf_op jit(solution)/shard_map/q_high/ppermute | solution.py:75
  36.0 1.6 collective-permute-start.7
  37.5 1.7 collective-permute-start.6
  39.2 2.5 collective-permute-start.5
  41.7 1.9 collective-permute-start.3
  43.6 6.8 %collective-permute-done.5.refs_3_ = bf16[128,1024]{1,0:T(8,128)(2,1)S(1)} collective-permute-done((bf16[128,1024]{1,0:T(8,128)(2,1)S(1)}, bf16[128,1024]{1,0:T(8,128)(2,1)S(1)}, u32[]{:S(2)}, u32[]{:S(2)}) %collective-permute-start.5) | collective-permute-done | bytes 262176 | tf_op jit(solution)/shard_map/fa_high/ppermute | solution.py:75
  50.4 11.8 %collective-permute-done.4.refs_2_ = bf16[128,1024]{1,0:T(8,128)(2,1)S(1)} collective-permute-done((bf16[128,1024]{1,0:T(8,128)(2,1)S(1)}, bf16[128,1024]{1,0:T(8,128)(2,1)S(1)}, u32[]{:S(2)}, u32[]{:S(2)}) %collective-permute-start.4) | collective-permute-done | bytes 262176 | tf_op jit(solution)/shard_map/fa_high/ppermute | solution.py:75
  62.2 1.2 collective-permute-start.14
  63.9 13.1 %collective-permute-done.14.refs_4_.refs_12_ = bf16[4,128,1024]{2,1,0:T(8,128)(2,1)S(1)} collective-permute-done((bf16[4,128,1024]{2,1,0:T(8,128)(2,1)S(1)}, bf16[4,128,1024]{2,1,0:T(8,128)(2,1)S(1)}, u32[]{:S(2)}, u32[]{:S(2)}) %collective-permute-start.14) | collective-permute-done | bytes 1048608 | tf_op jit(solution)/shard_map/q_both/ppermute | solution.py:75
  77.2 1.2 collective-permute-start.19
  78.5 0.6 collective-permute-start.18
  79.1 2.5 collective-permute-start.13
  81.6 1.0 copy-done.21
  82.5 1.9 collective-permute-start.11
  84.5 18.0 %shard_map.278 = (bf16[320,1024]{1,0:T(8,128)(2,1)}, bf16[320,16]{1,0:T(8,128)(2,1)}, bf16[320,1024]{1,0:T(8,128)(2,1)}, bf16[320,1024]{1,0:T(8,128)(2,1)}, bf16...) custom-call(s32[4]{0:T(128)} %copy-done.13, ...), custom_call_target="tpu_custom_call" | custom-call | tf_op jit(solution)/shard_map/pallas_call | solution.py:54
  102.4 0.7 collective-permute-done.12.refs_2_
  103.3 1.2 collective-permute-start.26
  105.2 4.4 %collective-permute-done.16 = s32[4]{0:T(128)S(1)} collective-permute-done((s32[4]{0:T(128)S(1)}, s32[4]{0:T(128)S(1)}, u32[]{:S(2)}, u32[]{:S(2)}) %collective-permute-start.16) | collective-permute-done | bytes 48 | tf_op jit(solution)/shard_map/ppermute | solution.py:75
  110.4 3.4 %collective-permute-done.17 = s32[2,4]{1,0:T(2,128)S(1)} collective-permute-done((s32[2,4]{1,0:T(2,128)S(1)}, s32[2,4]{1,0:T(2,128)S(1)}, u32[]{:S(2)}, u32[]{:S(2)}) %collective-permute-start.17) | collective-permute-done | bytes 64 | tf_op jit(solution)/shard_map/ppermute | solution.py:75
  113.9 4.6 %collective-permute-done.26.refs_4_ = bf16[4,128,1024]{2,1,0:T(8,128)(2,1)} collective-permute-done((bf16[4,128,1024]{2,1,0:T(8,128)(2,1)}, bf16[4,128,1024]{2,1,0:T(8,128)(2,1)}, u32[]{:S(2)}, u32[]{:S(2)}) %collective-permute-start.26) | collective-permute-done | bytes 1048608 | tf_op jit(solution)/shard_map/fa_both/ppermute | solution.py:75
  119.0 1.2 collective-permute-start.24
  120.2 0.7 collective-permute-start.23
  120.9 1.5 collective-permute-start.25
  122.5 15.4 %shard_map.279 = (f32[320,1024]{1,0:T(8,128)}, f32[320,1024]{1,0:T(8,128)}, f32[320,16]{1,0:T(8,128)}, f32[320,16]{1,0:T(8,128)}, bf16[320,1024]{1,0:T(8,128)(2,1)}, /*index=5*/bf16[32,16,128]{2,1,0:T(8,128)(2,1)}) custom-call(s32[4]{0:T(128)} %copy-done.13, bf16[4,128,1024]{2,1,0:T(8,128)(2,1)} %copy-done.3, ...), custom_call_target="tpu_custom_call" | custom-call | tf_op jit(solution)/shard_map/pallas_call | solution.py:54
  137.9 6.7 %collective-permute-done.25 = s32[2,2,4]{2,1,0:T(2,128)S(1)} collective-permute-done((s32[2,2,4]{2,1,0:T(2,128)S(1)}, s32[2,2,4]{2,1,0:T(2,128)S(1)}, u32[]{:S(2)}, u32[]{:S(2)}) %collective-permute-start.25) | collective-permute-done | bytes 96 | tf_op jit(solution)/shard_map/ppermute | solution.py:75
  144.6 1.7 collective-permute-start.28
  147.8 11.8 %collective-permute-done.28.refs_4_ = bf16[4,128,1024]{2,1,0:T(8,128)(2,1)} collective-permute-done((bf16[4,128,1024]{2,1,0:T(8,128)(2,1)S(1)}, bf16[4,128,1024]{2,1,0:T(8,128)(2,1)}, u32[]{:S(2)}, u32[]{:S(2)}) %collective-permute-start.28) | collective-permute-done | bytes 1048608 | tf_op jit(solution)/shard_map/fb_both/ppermute | solution.py:75
  159.6 2.8 %collective-permute-done.32.refs_8_ = bf16[4,128,1024]{2,1,0:T(8,128)(2,1)S(1)} collective-permute-done((bf16[4,128,1024]{2,1,0:T(8,128)(2,1)}, bf16[4,128,1024]{2,1,0:T(8,128)(2,1)S(1)}, u32[]{:S(2)}, u32[]{:S(2)}) %collective-permute-start.32) | collective-permute-done | bytes 1048608 | tf_op jit(solution)/shard_map/fb_core/ppermute | solution.py:75
  162.5 1.0 copy-done.26
  163.4 19.0 %shard_map.280 = (bf16[320,256]{1,0:T(8,128)(2,1)}, bf16[320,256]{1,0:T(8,128)(2,1)}, bf16[320,256]{1,0:T(8,128)(2,1)}, bf16[320,256]{1,0:T(8,128)(2,1)}, bf16[3...) custom-call(s32[4]{0:T(128)} %copy-done.13, bf16[4,128,1024]{2,1,0:T(8,128)(2,1)} %copy-done.4, ...), custom_call_target="tpu_custom_call" | custom-call | tf_op jit(solution)/shard_map/pallas_call | solution.py:54
  182.4 3.6 %all-to-all-start.1 = ((bf16[32,16,384]{2,1,0:T(8,128)(2,1)}), bf16[32,16,384]{2,1,0:T(8,128)(2,1)S(1)}, u32[]{:S(2)}, u32[]{:S(2)}) async-start(bf16[32,16,384]{2,1,0:T(8,128)(2,1)} %get-tuple-element.137), calls=%async_computation.1 | async-start | bytes 786432 | tf_op jit(solution)/shard_map/grads_b_send/all_to_all | solution.py:712
  186.4 1.7 collective-permute-start.34
  188.1 10.8 %shard_map.281 = (bf16[320,1024]{1,0:T(8,128)(2,1)}, bf16[320,1024]{1,0:T(8,128)(2,1)}, bf16[320,1024]{1,0:T(8,128)(2,1)}, bf16[320,16]{1,0:T(8,128)(2,1)}, bf16[32,16,128]{2,1,0:T(8,128)(2,1)}) custom-call(s32[4]{0:T(128)} %copy-done.13, f32[320,1]{1,0:T(8,128)} %copy-done.7, bf16[320,1024]{1,0:T(8,128)(2,1)} %get-tuple-element.138.refs_2_, ...), custom_call_target="tpu_custom_call" | custom-call | tf_op jit(solution)/shard_map/pallas_call | solution.py:54
  198.9 0.8 collective-permute-done.35.refs_3_
  199.6 0.7 grads_b.6
  200.4 2.6 %collective-permute-start.36 = (bf16[128,384]{1,0:T(8,128)(2,1)S(1)}, bf16[128,384]{1,0:T(8,128)(2,1)S(1)}, u32[]{:S(2)}, u32[]{:S(2)}) collective-permute-start(bf16[128,384]{1,0:T(8,128)(2,1)S(1)} %bitcast.43), channel_id=1, source_target_pairs={{0,16},{1,17},{2,18},{3,19},{4,20},{5,21},{6,22},{7,23},{8,24},{9,... | collective-permute-start | bytes 294920 | tf_op jit(solution)/shard_map/grads_b/ppermute | solution.py:75
  203.0 3.3 %all-to-all-start.2 = ((bf16[32,16,128]{2,1,0:T(8,128)(2,1)}), bf16[32,16,128]{2,1,0:T(8,128)(2,1)S(1)}, u32[]{:S(2)}, u32[]{:S(2)}) async-start(bf16[32,16,128]{2,1,0:T(8,128)(2,1)} %get-tuple-element.144), calls=%async_computation.2 | async-start | bytes 262144 | tf_op jit(solution)/shard_map/grads_c_send/all_to_all | solution.py:712
  206.3 2.2 collective-permute-done.36.refs_1_
  208.8 1.5 collective-permute-start.37
  210.2 4.0 %all-to-all-done.2.mine = bf16[32,16,128]{2,1,0:T(8,128)(2,1)S(1)} async-done(((bf16[32,16,128]{2,1,0:T(8,128)(2,1)}), bf16[32,16,128]{2,1,0:T(8,128)(2,1)S(1)}, u32[]{:S(2)}, u32[]{:S(2)}) %all-to-all-start.2) | async-done | bytes 131104 | tf_op jit(solution)/shard_map/grads_c_send/all_to_all | solution.py:712
  214.3 0.7 grads_b.9
  215.0 1.5 collective-permute-start.40
  216.4 0.7 collective-permute-start.39
  217.1 2.3 collective-permute-start.38
  219.4 1.6 collective-permute-done.40.refs_3_
  222.6 0.7 collective-permute-start.42
  223.3 0.9 collective-permute-start.41
  224.2 10.7 %shard_map.282 = (bf16[320,256]{1,0:T(8,128)(2,1)}, bf16[320,256]{1,0:T(8,128)(2,1)}, bf16[320,256]{1,0:T(8,128)(2,1)}, bf16[320,256]{1,0:T(8,128)(2,1)}) custom-call(s32[4]{0:T(128)} %copy-done.13, bf16[4,128,1024]{2,1,0:T(8,128)(2,1)} %copy-done.2, bf16[4,128,1024]{2,1,0:T(8,128)(2,1)} %copy-done.16, bf16[4,128,1024]{2,1,0:T(8,128)(2,1)} %copy-done.15, ...), custom_call_target="tpu_custom_call" | custom-call | tf_op jit(solution)/shard_map/pallas_call | solution.py:54
  234.9 1.2 collective-permute-done.42.refs_3_
  237.2 0.9 grads.2
  238.1 7.3 %collective-permute-done.49.refs_4_ = bf16[4,128,512]{2,1,0:T(8,128)(2,1)S(1)} collective-permute-done((bf16[4,128,512]{2,1,0:T(8,128)(2,1)S(1)}, bf16[4,128,512]{2,1,0:T(8,128)(2,1)S(1)}, u32[]{:S(2)}, u32[]{:S(2)}) %collective-permute-start.49) | collective-permute-done | bytes 524320 | tf_op jit(solution)/shard_map/grads/ppermute | solution.py:75
  246.0 1.3 collective-permute-start.47
  247.5 0.8 copy-done.33
  248.3 6.9 %grads.3 = (f32[128,4096]{1,0:T(8,128)}, f32[128,4096]{1,0:T(8,128)}, f32[128,1024]{1,0:T(8,128)}, f32[128,1024]{1,0:T(8,128)}, f32[128,1024]{1,0:T(8,128)}, /*i...) custom-call(s32[4]{0:T(128)} %copy-done.13, bf16[4,128,512]{2,1,0:T(8,128)(2,1)} %copy-done.5, ...), custom_call_target="tpu_custom_call" | custom-call | tf_op jit(solution)/shard_map/grads/pallas_call | solution.py:54
  255.3 0.9 rows_out.1
  (150 shorter events, 9.6 us)
Async XLA Ops:
  0.6 18.4 %copy-start = (bf16[8,16,3,1024]{3,1,2,0:T(8,128)(2,1)S(1)}, bf16[8,16,3,1024]{3,1,2,0:T(8,128)(2,1)}, u32[]{:S(2)}) copy-start(bf16[8,16,3,1024]{3,1,2,0:T(8,128)(2,1)} %param.35) | copy-start | bytes 2359300
  3.4 32.6 %all-to-all-start = ((bf16[4,656,256]{2,1,0:T(8,128)(2,1)}), bf16[4,656,256]{2,1,0:T(8,128)(2,1)}, u32[]{:S(2)}, u32[]{:S(2)}) async-start(bf16[4,656,256]{2,1,0:T(8,128)(2,1)} %get-tuple-element.98), calls=%async_computation | async-start | bytes 2686976 | tf_op jit(solution)/shard_map/all_to_all | solution.py:811
  7.8 12.4 %collective-permute-start.2 = (bf16[128,1024]{1,0:T(8,128)(2,1)S(1)}, bf16[128,1024]{1,0:T(8,128)(2,1)S(1)}, u32[]{:S(2)}, u32[]{:S(2)}) collective-permute-start(bf16[128,1024]{1,0:T(8,128)(2,1)S(1)} %copy-done.8), channel_id=1, source_target_pairs={{0,24},{1,25},{2,26},{3,27},{4,28},{5,29},{6,30},{7,31},{8,16},{9,... | collective-permute-start | bytes 786440 | tf_op jit(solution)/shard_map/q_high/ppermute | solution.py:75
  13.0 22.8 %collective-permute-start.1 = (bf16[128,1024]{1,0:T(8,128)(2,1)S(1)}, bf16[128,1024]{1,0:T(8,128)(2,1)S(1)}, u32[]{:S(2)}, u32[]{:S(2)}) collective-permute-start(bf16[128,1024]{1,0:T(8,128)(2,1)S(1)} %copy-done.8), channel_id=1, source_target_pairs={{0,16},{1,17},{2,18},{3,19},{4,20},{5,21},{6,22},{7,23},{8,24},{9,... | collective-permute-start | bytes 786440 | tf_op jit(solution)/shard_map/q_high/ppermute | solution.py:75
  13.0 22.8 %collective-permute-start = (bf16[128,1024]{1,0:T(8,128)(2,1)S(1)}, bf16[128,1024]{1,0:T(8,128)(2,1)S(1)}, u32[]{:S(2)}, u32[]{:S(2)}) collective-permute-start(bf16[128,1024]{1,0:T(8,128)(2,1)S(1)} %copy-done.8), channel_id=1, source_target_pairs={{0,8},{1,9},{2,10},{3,11},{4,12},{5,13},{6,14},{7,15},{8,0},{9,1},... | collective-permute-start | bytes 786440 | tf_op jit(solution)/shard_map/q_high/ppermute | solution.py:75
  16.9 19.1 %copy-start.13 = (s32[4]{0:T(128)}, s32[4]{0:T(128)S(1)}, u32[]{:S(2)}) copy-start(s32[4]{0:T(128)S(1)} %pad_add_fusion.3.sc.refs_0_) | copy-start | bytes 52
  35.9 48.5 %copy-start.2 = (bf16[4,128,1024]{2,1,0:T(8,128)(2,1)}, bf16[4,128,1024]{2,1,0:T(8,128)(2,1)S(1)}, u32[]{:S(2)}) copy-start(bf16[4,128,1024]{2,1,0:T(8,128)(2,1)S(1)} %q_high.1.refs_1_.refs_9_) | copy-start | bytes 3145732
  36.0 26.2 %collective-permute-start.7 = (bf16[4,128,1024]{2,1,0:T(8,128)(2,1)S(1)}, bf16[4,128,1024]{2,1,0:T(8,128)(2,1)S(1)}, u32[]{:S(2)}, u32[]{:S(2)}) collective-permute-start(bf16[4,128,1024]{2,1,0:T(8,128)(2,1)S(1)} %q_high.1.refs_1_.refs_9_), channel_id=1, source_target_pairs={{0,4},{1,3},{2,6},{3,1},{4,0},{5,7},{6,2},{7,5},{8,12},{9,11},{10,... | collective-permute-start | bytes 3145736 | tf_op jit(solution)/shard_map/q_two/ppermute | solution.py:75
  37.5 24.6 %collective-permute-start.6 = (bf16[4,128,1024]{2,1,0:T(8,128)(2,1)S(1)}, bf16[4,128,1024]{2,1,0:T(8,128)(2,1)S(1)}, u32[]{:S(2)}, u32[]{:S(2)}) collective-permute-start(bf16[4,128,1024]{2,1,0:T(8,128)(2,1)S(1)} %q_high.1.refs_1_.refs_9_), channel_id=1, source_target_pairs={{0,2},{1,5},{2,0},{3,7},{4,6},{5,1},{6,4},{7,3},{8,10},{9,13},{10,... | collective-permute-start | bytes 3145736 | tf_op jit(solution)/shard_map/q_one/ppermute | solution.py:75
  39.2 11.1 %collective-permute-start.5 = (bf16[128,1024]{1,0:T(8,128)(2,1)S(1)}, bf16[128,1024]{1,0:T(8,128)(2,1)S(1)}, u32[]{:S(2)}, u32[]{:S(2)}) collective-permute-start(bf16[128,1024]{1,0:T(8,128)(2,1)S(1)} %get-tuple-element.101.refs_0_), channel_id=1, source_target_pairs={{0,24},{1,25},{2,26},{3,27},{4,28},{5,29},{6,30},{7,31},{8,16},{9,... | collective-permute-start | bytes 786440 | tf_op jit(solution)/shard_map/fa_high/ppermute | solution.py:75
  41.7 20.4 %collective-permute-start.4 = (bf16[128,1024]{1,0:T(8,128)(2,1)S(1)}, bf16[128,1024]{1,0:T(8,128)(2,1)S(1)}, u32[]{:S(2)}, u32[]{:S(2)}) collective-permute-start(bf16[128,1024]{1,0:T(8,128)(2,1)S(1)} %get-tuple-element.101.refs_0_), channel_id=1, source_target_pairs={{0,16},{1,17},{2,18},{3,19},{4,20},{5,21},{6,22},{7,23},{8,24},{9,... | collective-permute-start | bytes 786440 | tf_op jit(solution)/shard_map/fa_high/ppermute | solution.py:75
  41.7 20.4 %collective-permute-start.3 = (bf16[128,1024]{1,0:T(8,128)(2,1)S(1)}, bf16[128,1024]{1,0:T(8,128)(2,1)S(1)}, u32[]{:S(2)}, u32[]{:S(2)}) collective-permute-start(bf16[128,1024]{1,0:T(8,128)(2,1)S(1)} %get-tuple-element.101.refs_0_), channel_id=1, source_target_pairs={{0,8},{1,9},{2,10},{3,11},{4,12},{5,13},{6,14},{7,15},{8,0},{9,1},... | collective-permute-start | bytes 786440 | tf_op jit(solution)/shard_map/fa_high/ppermute | solution.py:75
  62.1 22.3 %copy-start.15 = (bf16[4,128,1024]{2,1,0:T(8,128)(2,1)}, bf16[4,128,1024]{2,1,0:T(8,128)(2,1)S(1)}, u32[]{:S(2)}) copy-start(bf16[4,128,1024]{2,1,0:T(8,128)(2,1)S(1)} %collective-permute-done.7.refs_3_.refs_11_) | copy-start | bytes 3145732
  62.2 22.3 %copy-start.16 = (bf16[4,128,1024]{2,1,0:T(8,128)(2,1)}, bf16[4,128,1024]{2,1,0:T(8,128)(2,1)S(1)}, u32[]{:S(2)}) copy-start(bf16[4,128,1024]{2,1,0:T(8,128)(2,1)S(1)} %collective-permute-done.6.refs_2_.refs_10_) | copy-start | bytes 3145732
  62.2 14.9 %collective-permute-start.14 = (bf16[4,128,1024]{2,1,0:T(8,128)(2,1)S(1)}, bf16[4,128,1024]{2,1,0:T(8,128)(2,1)S(1)}, u32[]{:S(2)}, u32[]{:S(2)}) collective-permute-start(bf16[4,128,1024]{2,1,0:T(8,128)(2,1)S(1)} %collective-permute-done.6.refs_2_.refs_10_), channel_id=1, source_target_pairs={{0,4},{1,3},{2,6},{3,1},{4,0},{5,7},{6,2},{7,5},{8,12},{9,11},{10,... | collective-permute-start | bytes 3145736 | tf_op jit(solution)/shard_map/q_both/ppermute | solution.py:75
  63.4 13.8 %collective-permute-start.8 = (bf16[4,128,1024]{2,1,0:T(8,128)(2,1)S(1)}, bf16[4,128,1024]{2,1,0:T(8,128)(2,1)S(1)}, u32[]{:S(2)}, u32[]{:S(2)}) collective-permute-start(bf16[4,128,1024]{2,1,0:T(8,128)(2,1)S(1)} %q_high.1.refs_1_.refs_9_), channel_id=1, source_target_pairs={{0,1},{1,0},{2,3},{3,2},{4,5},{5,4},{6,7},{7,6},{8,9},{9,8},{10,11... | collective-permute-start | bytes 3145736 | tf_op jit(solution)/shard_map/q_core/ppermute | solution.py:75
  63.4 13.8 %collective-permute-start.10 = (bf16[4,128,1024]{2,1,0:T(8,128)(2,1)S(1)}, bf16[4,128,1024]{2,1,0:T(8,128)(2,1)S(1)}, u32[]{:S(2)}, u32[]{:S(2)}) collective-permute-start(bf16[4,128,1024]{2,1,0:T(8,128)(2,1)S(1)} %collective-permute-done.7.refs_3_.refs_11_), channel_id=1, source_target_pairs={{0,1},{1,0},{2,3},{3,2},{4,5},{5,4},{6,7},{7,6},{8,9},{9,8},{10,11... | collective-permute-start | bytes 3145736 | tf_op jit(solution)/shard_map/q_core/ppermute | solution.py:75
  63.9 13.3 %collective-permute-start.9 = (bf16[4,128,1024]{2,1,0:T(8,128)(2,1)S(1)}, bf16[4,128,1024]{2,1,0:T(8,128)(2,1)S(1)}, u32[]{:S(2)}, u32[]{:S(2)}) collective-permute-start(bf16[4,128,1024]{2,1,0:T(8,128)(2,1)S(1)} %collective-permute-done.6.refs_2_.refs_10_), channel_id=1, source_target_pairs={{0,1},{1,0},{2,3},{3,2},{4,5},{5,4},{6,7},{7,6},{8,9},{9,8},{10,11... | collective-permute-start | bytes 3145736 | tf_op jit(solution)/shard_map/q_core/ppermute | solution.py:75
  77.0 4.5 %collective-permute-start.15 = (bf16[4,128,1024]{2,1,0:T(8,128)(2,1)S(1)}, bf16[4,128,1024]{2,1,0:T(8,128)(2,1)S(1)}, u32[]{:S(2)}, u32[]{:S(2)}) collective-permute-start(bf16[4,128,1024]{2,1,0:T(8,128)(2,1)S(1)} %collective-permute-done.14.refs_4_.refs_12_), channel_id=1, source_target_pairs={{0,1},{1,0},{2,3},{3,2},{4,5},{5,4},{6,7},{7,6},{8,9},{9,8},{10,11... | collective-permute-start | bytes 3145736 | tf_op jit(solution)/shard_map/q_core/ppermute | solution.py:75
  77.2 27.3 %copy-start.3 = (bf16[4,128,1024]{2,1,0:T(8,128)(2,1)}, bf16[4,128,1024]{2,1,0:T(8,128)(2,1)S(1)}, u32[]{:S(2)}) copy-start(bf16[4,128,1024]{2,1,0:T(8,128)(2,1)S(1)} %fa_high.1.refs_1_) | copy-start | bytes 3145732
  77.2 26.1 %collective-permute-start.19 = (bf16[4,128,1024]{2,1,0:T(8,128)(2,1)S(1)}, bf16[4,128,1024]{2,1,0:T(8,128)(2,1)}, u32[]{:S(2)}, u32[]{:S(2)}) collective-permute-start(bf16[4,128,1024]{2,1,0:T(8,128)(2,1)S(1)} %fa_high.1.refs_1_), channel_id=1, source_target_pairs={{0,4},{1,3},{2,6},{3,1},{4,0},{5,7},{6,2},{7,5},{8,12},{9,11},{10,... | collective-permute-start | bytes 3145736 | tf_op jit(solution)/shard_map/fa_two/ppermute | solution.py:75
  78.5 24.8 %collective-permute-start.18 = (bf16[4,128,1024]{2,1,0:T(8,128)(2,1)S(1)}, bf16[4,128,1024]{2,1,0:T(8,128)(2,1)}, u32[]{:S(2)}, u32[]{:S(2)}) collective-permute-start(bf16[4,128,1024]{2,1,0:T(8,128)(2,1)S(1)} %fa_high.1.refs_1_), channel_id=1, source_target_pairs={{0,2},{1,5},{2,0},{3,7},{4,6},{5,1},{6,4},{7,3},{8,10},{9,13},{10,... | collective-permute-start | bytes 3145736 | tf_op jit(solution)/shard_map/fa_one/ppermute | solution.py:75
  79.1 23.4 %collective-permute-start.13 = (bf16[128,1024]{1,0:T(8,128)(2,1)S(1)}, bf16[128,1024]{1,0:T(8,128)(2,1)S(1)}, u32[]{:S(2)}, u32[]{:S(2)}) collective-permute-start(bf16[128,1024]{1,0:T(8,128)(2,1)S(1)} %get-tuple-element.107.refs_0_), channel_id=1, source_target_pairs={{0,24},{1,25},{2,26},{3,27},{4,28},{5,29},{6,30},{7,31},{8,16},{9,... | collective-permute-start | bytes 786440 | tf_op jit(solution)/shard_map/fb_high/ppermute | solution.py:75
  81.5 21.6 %collective-permute-start.12 = (bf16[128,1024]{1,0:T(8,128)(2,1)S(1)}, bf16[128,1024]{1,0:T(8,128)(2,1)S(1)}, u32[]{:S(2)}, u32[]{:S(2)}) collective-permute-start(bf16[128,1024]{1,0:T(8,128)(2,1)S(1)} %get-tuple-element.107.refs_0_), channel_id=1, source_target_pairs={{0,16},{1,17},{2,18},{3,19},{4,20},{5,21},{6,22},{7,23},{8,24},{9,... | collective-permute-start | bytes 786440 | tf_op jit(solution)/shard_map/fb_high/ppermute | solution.py:75
  82.5 20.6 %collective-permute-start.11 = (bf16[128,1024]{1,0:T(8,128)(2,1)S(1)}, bf16[128,1024]{1,0:T(8,128)(2,1)S(1)}, u32[]{:S(2)}, u32[]{:S(2)}) collective-permute-start(bf16[128,1024]{1,0:T(8,128)(2,1)S(1)} %get-tuple-element.107.refs_0_), channel_id=1, source_target_pairs={{0,8},{1,9},{2,10},{3,11},{4,12},{5,13},{6,14},{7,15},{8,0},{9,1},... | collective-permute-start | bytes 786440 | tf_op jit(solution)/shard_map/fb_high/ppermute | solution.py:75
  103.3 15.1 %collective-permute-start.26 = (bf16[4,128,1024]{2,1,0:T(8,128)(2,1)}, bf16[4,128,1024]{2,1,0:T(8,128)(2,1)}, u32[]{:S(2)}, u32[]{:S(2)}) collective-permute-start(bf16[4,128,1024]{2,1,0:T(8,128)(2,1)} %collective-permute-done.18.refs_2_), channel_id=1, source_target_pairs={{0,4},{1,3},{2,6},{3,1},{4,0},{5,7},{6,2},{7,5},{8,12},{9,11},{10,... | collective-permute-start | bytes 3145736 | tf_op jit(solution)/shard_map/fa_both/ppermute | solution.py:75
  104.5 14.5 %collective-permute-start.20 = (bf16[4,128,1024]{2,1,0:T(8,128)(2,1)S(1)}, bf16[4,128,1024]{2,1,0:T(8,128)(2,1)}, u32[]{:S(2)}, u32[]{:S(2)}) collective-permute-start(bf16[4,128,1024]{2,1,0:T(8,128)(2,1)S(1)} %fa_high.1.refs_1_), channel_id=1, source_target_pairs={{0,1},{1,0},{2,3},{3,2},{4,5},{5,4},{6,7},{7,6},{8,9},{9,8},{10,11... | collective-permute-start | bytes 3145736 | tf_op jit(solution)/shard_map/fa_core/ppermute | solution.py:75
  104.5 14.5 %collective-permute-start.22 = (bf16[4,128,1024]{2,1,0:T(8,128)(2,1)}, bf16[4,128,1024]{2,1,0:T(8,128)(2,1)}, u32[]{:S(2)}, u32[]{:S(2)}) collective-permute-start(bf16[4,128,1024]{2,1,0:T(8,128)(2,1)} %collective-permute-done.19.refs_3_), channel_id=1, source_target_pairs={{0,1},{1,0},{2,3},{3,2},{4,5},{5,4},{6,7},{7,6},{8,9},{9,8},{10,11... | collective-permute-start | bytes 3145736 | tf_op jit(solution)/shard_map/fa_core/ppermute | solution.py:75
  105.0 14.0 %collective-permute-start.21 = (bf16[4,128,1024]{2,1,0:T(8,128)(2,1)}, bf16[4,128,1024]{2,1,0:T(8,128)(2,1)}, u32[]{:S(2)}, u32[]{:S(2)}) collective-permute-start(bf16[4,128,1024]{2,1,0:T(8,128)(2,1)} %collective-permute-done.18.refs_2_), channel_id=1, source_target_pairs={{0,1},{1,0},{2,3},{3,2},{4,5},{5,4},{6,7},{7,6},{8,9},{9,8},{10,11... | collective-permute-start | bytes 3145736 | tf_op jit(solution)/shard_map/fa_core/ppermute | solution.py:75
  105.1 42.0 %copy-start.4 = (bf16[4,128,1024]{2,1,0:T(8,128)(2,1)}, bf16[4,128,1024]{2,1,0:T(8,128)(2,1)S(1)}, u32[]{:S(2)}) copy-start(bf16[4,128,1024]{2,1,0:T(8,128)(2,1)S(1)} %fb_high.1.refs_1_) | copy-start | bytes 3145732
  105.2 4.5 %collective-permute-start.16 = (s32[4]{0:T(128)S(1)}, s32[4]{0:T(128)S(1)}, u32[]{:S(2)}, u32[]{:S(2)}) collective-permute-start(s32[4]{0:T(128)S(1)} %copy-done.34), channel_id=1, source_target_pairs={{0,16},{1,17},{2,18},{3,19},{4,20},{5,21},{6,22},{7,23},{8,24},{9,... | collective-permute-start | bytes 56 | tf_op jit(solution)/shard_map/ppermute | solution.py:75
  110.2 3.6 %collective-permute-start.17 = (s32[2,4]{1,0:T(2,128)S(1)}, s32[2,4]{1,0:T(2,128)S(1)}, u32[]{:S(2)}, u32[]{:S(2)}) collective-permute-start(s32[2,4]{1,0:T(2,128)S(1)} %gather_fusion), channel_id=1, source_target_pairs={{0,8},{1,9},{2,10},{3,11},{4,12},{5,13},{6,14},{7,15},{8,0},{9,1},... | collective-permute-start | bytes 104 | tf_op jit(solution)/shard_map/ppermute | solution.py:75
  118.4 4.1 %collective-permute-start.27 = (bf16[4,128,1024]{2,1,0:T(8,128)(2,1)}, bf16[4,128,1024]{2,1,0:T(8,128)(2,1)}, u32[]{:S(2)}, u32[]{:S(2)}) collective-permute-start(bf16[4,128,1024]{2,1,0:T(8,128)(2,1)} %collective-permute-done.26.refs_4_), channel_id=1, source_target_pairs={{0,1},{1,0},{2,3},{3,2},{4,5},{5,4},{6,7},{7,6},{8,9},{9,8},{10,11... | collective-permute-start | bytes 3145736 | tf_op jit(solution)/shard_map/fa_core/ppermute | solution.py:75
  119.0 25.6 %collective-permute-start.24 = (bf16[4,128,1024]{2,1,0:T(8,128)(2,1)S(1)}, bf16[4,128,1024]{2,1,0:T(8,128)(2,1)S(1)}, u32[]{:S(2)}, u32[]{:S(2)}) collective-permute-start(bf16[4,128,1024]{2,1,0:T(8,128)(2,1)S(1)} %fb_high.1.refs_1_), channel_id=1, source_target_pairs={{0,4},{1,3},{2,6},{3,1},{4,0},{5,7},{6,2},{7,5},{8,12},{9,11},{10,... | collective-permute-start | bytes 3145736 | tf_op jit(solution)/shard_map/fb_two/ppermute | solution.py:75
  120.2 24.4 %collective-permute-start.23 = (bf16[4,128,1024]{2,1,0:T(8,128)(2,1)S(1)}, bf16[4,128,1024]{2,1,0:T(8,128)(2,1)S(1)}, u32[]{:S(2)}, u32[]{:S(2)}) collective-permute-start(bf16[4,128,1024]{2,1,0:T(8,128)(2,1)S(1)} %fb_high.1.refs_1_), channel_id=1, source_target_pairs={{0,2},{1,5},{2,0},{3,7},{4,6},{5,1},{6,4},{7,3},{8,10},{9,13},{10,... | collective-permute-start | bytes 3145736 | tf_op jit(solution)/shard_map/fb_one/ppermute | solution.py:75
  120.9 23.6 %collective-permute-start.25 = (s32[2,2,4]{2,1,0:T(2,128)S(1)}, s32[2,2,4]{2,1,0:T(2,128)S(1)}, u32[]{:S(2)}, u32[]{:S(2)}) collective-permute-start(s32[2,2,4]{2,1,0:T(2,128)S(1)} %gather_fusion.1), channel_id=1, source_target_pairs={{0,4},{1,5},{2,6},{3,7},{4,0},{5,1},{6,2},{7,3},{8,12},{9,13},{10,... | collective-permute-start | bytes 200 | tf_op jit(solution)/shard_map/ppermute | solution.py:75
  144.6 17.9 %copy-start.22 = (bf16[4,128,1024]{2,1,0:T(8,128)(2,1)}, bf16[4,128,1024]{2,1,0:T(8,128)(2,1)S(1)}, u32[]{:S(2)}) copy-start(bf16[4,128,1024]{2,1,0:T(8,128)(2,1)S(1)} %collective-permute-done.24.refs_3_) | copy-start | bytes 3145732
  144.6 17.8 %copy-start.23 = (bf16[4,128,1024]{2,1,0:T(8,128)(2,1)}, bf16[4,128,1024]{2,1,0:T(8,128)(2,1)S(1)}, u32[]{:S(2)}) copy-start(bf16[4,128,1024]{2,1,0:T(8,128)(2,1)S(1)} %collective-permute-done.23.refs_2_) | copy-start | bytes 3145732
  144.6 14.9 %collective-permute-start.28 = (bf16[4,128,1024]{2,1,0:T(8,128)(2,1)S(1)}, bf16[4,128,1024]{2,1,0:T(8,128)(2,1)}, u32[]{:S(2)}, u32[]{:S(2)}) collective-permute-start(bf16[4,128,1024]{2,1,0:T(8,128)(2,1)S(1)} %collective-permute-done.23.refs_2_), channel_id=1, source_target_pairs={{0,4},{1,3},{2,6},{3,1},{4,0},{5,7},{6,2},{7,5},{8,12},{9,11},{10,... | collective-permute-start | bytes 3145736 | tf_op jit(solution)/shard_map/fb_both/ppermute | solution.py:75
  146.4 13.2 %collective-permute-start.30 = (bf16[4,128,1024]{2,1,0:T(8,128)(2,1)S(1)}, bf16[4,128,1024]{2,1,0:T(8,128)(2,1)}, u32[]{:S(2)}, u32[]{:S(2)}) collective-permute-start(bf16[4,128,1024]{2,1,0:T(8,128)(2,1)S(1)} %collective-permute-done.23.refs_2_), channel_id=1, source_target_pairs={{0,1},{1,0},{2,3},{3,2},{4,5},{5,4},{6,7},{7,6},{8,9},{9,8},{10,11... | collective-permute-start | bytes 3145736 | tf_op jit(solution)/shard_map/fb_core/ppermute | solution.py:75
  147.1 12.4 %collective-permute-start.29 = (bf16[4,128,1024]{2,1,0:T(8,128)(2,1)S(1)}, bf16[4,128,1024]{2,1,0:T(8,128)(2,1)S(1)}, u32[]{:S(2)}, u32[]{:S(2)}) collective-permute-start(bf16[4,128,1024]{2,1,0:T(8,128)(2,1)S(1)} %fb_high.1.refs_1_), channel_id=1, source_target_pairs={{0,1},{1,0},{2,3},{3,2},{4,5},{5,4},{6,7},{7,6},{8,9},{9,8},{10,11... | collective-permute-start | bytes 3145736 | tf_op jit(solution)/shard_map/fb_core/ppermute | solution.py:75
  147.7 11.9 %collective-permute-start.31 = (bf16[4,128,1024]{2,1,0:T(8,128)(2,1)S(1)}, bf16[4,128,1024]{2,1,0:T(8,128)(2,1)S(1)}, u32[]{:S(2)}, u32[]{:S(2)}) collective-permute-start(bf16[4,128,1024]{2,1,0:T(8,128)(2,1)S(1)} %collective-permute-done.24.refs_3_), channel_id=1, source_target_pairs={{0,1},{1,0},{2,3},{3,2},{4,5},{5,4},{6,7},{7,6},{8,9},{9,8},{10,11... | collective-permute-start | bytes 3145736 | tf_op jit(solution)/shard_map/fb_core/ppermute | solution.py:75
  159.6 2.9 %collective-permute-start.32 = (bf16[4,128,1024]{2,1,0:T(8,128)(2,1)}, bf16[4,128,1024]{2,1,0:T(8,128)(2,1)S(1)}, u32[]{:S(2)}, u32[]{:S(2)}) collective-permute-start(bf16[4,128,1024]{2,1,0:T(8,128)(2,1)} %collective-permute-done.28.refs_4_), channel_id=1, source_target_pairs={{0,1},{1,0},{2,3},{3,2},{4,5},{5,4},{6,7},{7,6},{8,9},{9,8},{10,11... | collective-permute-start | bytes 3145736 | tf_op jit(solution)/shard_map/fb_core/ppermute | solution.py:75
  182.4 17.2 %all-to-all-start.1 = ((bf16[32,16,384]{2,1,0:T(8,128)(2,1)}), bf16[32,16,384]{2,1,0:T(8,128)(2,1)S(1)}, u32[]{:S(2)}, u32[]{:S(2)}) async-start(bf16[32,16,384]{2,1,0:T(8,128)(2,1)} %get-tuple-element.137), calls=%async_computation.1 | async-start | bytes 786432 | tf_op jit(solution)/shard_map/grads_b_send/all_to_all | solution.py:712
  186.1 12.8 %collective-permute-start.33 = (bf16[320,256]{1,0:T(8,128)(2,1)}, bf16[320,256]{1,0:T(8,128)(2,1)S(1)}, u32[]{:S(2)}, u32[]{:S(2)}) collective-permute-start(bf16[320,256]{1,0:T(8,128)(2,1)} %get-tuple-element.134), channel_id=1, source_target_pairs={{0,1},{1,0},{2,3},{3,2},{4,5},{5,4},{6,7},{7,6},{8,9},{9,8},{10,11... | collective-permute-start | bytes 491528 | tf_op jit(solution)/shard_map/layer_out/ppermute | solution.py:75
  186.4 12.5 %collective-permute-start.34 = (bf16[320,256]{1,0:T(8,128)(2,1)}, bf16[320,256]{1,0:T(8,128)(2,1)S(1)}, u32[]{:S(2)}, u32[]{:S(2)}) collective-permute-start(bf16[320,256]{1,0:T(8,128)(2,1)} %get-tuple-element.135), channel_id=1, source_target_pairs={{0,2},{1,3},{2,0},{3,1},{4,6},{5,7},{6,4},{7,5},{8,10},{9,11},{10,... | collective-permute-start | bytes 491528 | tf_op jit(solution)/shard_map/layer_out/ppermute | solution.py:75
  188.1 11.6 %collective-permute-start.35 = (bf16[320,256]{1,0:T(8,128)(2,1)}, bf16[320,256]{1,0:T(8,128)(2,1)S(1)}, u32[]{:S(2)}, u32[]{:S(2)}) collective-permute-start(bf16[320,256]{1,0:T(8,128)(2,1)} %get-tuple-element.136), channel_id=1, source_target_pairs={{0,3},{1,2},{2,1},{3,0},{4,7},{5,6},{6,5},{7,4},{8,11},{9,10},{10,... | collective-permute-start | bytes 491528 | tf_op jit(solution)/shard_map/layer_out/ppermute | solution.py:75
  200.4 8.1 %collective-permute-start.36 = (bf16[128,384]{1,0:T(8,128)(2,1)S(1)}, bf16[128,384]{1,0:T(8,128)(2,1)S(1)}, u32[]{:S(2)}, u32[]{:S(2)}) collective-permute-start(bf16[128,384]{1,0:T(8,128)(2,1)S(1)} %bitcast.43), channel_id=1, source_target_pairs={{0,16},{1,17},{2,18},{3,19},{4,20},{5,21},{6,22},{7,23},{8,24},{9,... | collective-permute-start | bytes 294920 | tf_op jit(solution)/shard_map/grads_b/ppermute | solution.py:75
  203.0 11.3 %all-to-all-start.2 = ((bf16[32,16,128]{2,1,0:T(8,128)(2,1)}), bf16[32,16,128]{2,1,0:T(8,128)(2,1)S(1)}, u32[]{:S(2)}, u32[]{:S(2)}) async-start(bf16[32,16,128]{2,1,0:T(8,128)(2,1)} %get-tuple-element.144), calls=%async_computation.2 | async-start | bytes 262144 | tf_op jit(solution)/shard_map/grads_c_send/all_to_all | solution.py:712
  208.8 13.1 %collective-permute-start.37 = (bf16[2,128,384]{2,1,0:T(8,128)(2,1)S(1)}, bf16[2,128,384]{2,1,0:T(8,128)(2,1)S(1)}, u32[]{:S(2)}, u32[]{:S(2)}) collective-permute-start(bf16[2,128,384]{2,1,0:T(8,128)(2,1)S(1)} %grads_b.7), channel_id=1, source_target_pairs={{0,8},{1,9},{2,10},{3,11},{4,12},{5,13},{6,14},{7,15},{8,0},{9,1},... | collective-permute-start | bytes 589832 | tf_op jit(solution)/shard_map/grads_b/ppermute | solution.py:75
  215.0 6.1 %collective-permute-start.40 = (bf16[128,128]{1,0:T(8,128)(2,1)S(1)}, bf16[128,128]{1,0:T(8,128)(2,1)S(1)}, u32[]{:S(2)}, u32[]{:S(2)}) collective-permute-start(bf16[128,128]{1,0:T(8,128)(2,1)S(1)} %bitcast.46), channel_id=1, source_target_pairs={{0,24},{1,25},{2,26},{3,27},{4,28},{5,29},{6,30},{7,31},{8,16},{9,... | collective-permute-start | bytes 98312 | tf_op jit(solution)/shard_map/grads_b/ppermute | solution.py:75
  216.4 5.1 %collective-permute-start.39 = (bf16[128,128]{1,0:T(8,128)(2,1)S(1)}, bf16[128,128]{1,0:T(8,128)(2,1)S(1)}, u32[]{:S(2)}, u32[]{:S(2)}) collective-permute-start(bf16[128,128]{1,0:T(8,128)(2,1)S(1)} %bitcast.47), channel_id=1, source_target_pairs={{0,16},{1,17},{2,18},{3,19},{4,20},{5,21},{6,22},{7,23},{8,24},{9,... | collective-permute-start | bytes 98312 | tf_op jit(solution)/shard_map/grads_b/ppermute | solution.py:75
  217.1 4.5 %collective-permute-start.38 = (bf16[128,128]{1,0:T(8,128)(2,1)S(1)}, bf16[128,128]{1,0:T(8,128)(2,1)S(1)}, u32[]{:S(2)}, u32[]{:S(2)}) collective-permute-start(bf16[128,128]{1,0:T(8,128)(2,1)S(1)} %bitcast.48), channel_id=1, source_target_pairs={{0,8},{1,9},{2,10},{3,11},{4,12},{5,13},{6,14},{7,15},{8,0},{9,1},... | collective-permute-start | bytes 98312 | tf_op jit(solution)/shard_map/grads_b/ppermute | solution.py:75
  222.6 13.6 %collective-permute-start.42 = (bf16[4,128,512]{2,1,0:T(8,128)(2,1)S(1)}, bf16[4,128,512]{2,1,0:T(8,128)(2,1)S(1)}, u32[]{:S(2)}, u32[]{:S(2)}) collective-permute-start(bf16[4,128,512]{2,1,0:T(8,128)(2,1)S(1)} %grads_b.11.refs_1_), channel_id=1, source_target_pairs={{0,4},{1,3},{2,6},{3,1},{4,0},{5,7},{6,2},{7,5},{8,12},{9,11},{10,... | collective-permute-start | bytes 1572872 | tf_op jit(solution)/shard_map/grads/ppermute | solution.py:75
  223.3 12.9 %collective-permute-start.41 = (bf16[4,128,512]{2,1,0:T(8,128)(2,1)S(1)}, bf16[4,128,512]{2,1,0:T(8,128)(2,1)S(1)}, u32[]{:S(2)}, u32[]{:S(2)}) collective-permute-start(bf16[4,128,512]{2,1,0:T(8,128)(2,1)S(1)} %grads_b.11.refs_1_), channel_id=1, source_target_pairs={{0,2},{1,5},{2,0},{3,7},{4,6},{5,1},{6,4},{7,3},{8,10},{9,13},{10,... | collective-permute-start | bytes 1572872 | tf_op jit(solution)/shard_map/grads/ppermute | solution.py:75
  236.1 9.2 %collective-permute-start.49 = (bf16[4,128,512]{2,1,0:T(8,128)(2,1)S(1)}, bf16[4,128,512]{2,1,0:T(8,128)(2,1)S(1)}, u32[]{:S(2)}, u32[]{:S(2)}) collective-permute-start(bf16[4,128,512]{2,1,0:T(8,128)(2,1)S(1)} %collective-permute-done.41.refs_2_), channel_id=1, source_target_pairs={{0,4},{1,3},{2,6},{3,1},{4,0},{5,7},{6,2},{7,5},{8,12},{9,11},{10,... | collective-permute-start | bytes 1572872 | tf_op jit(solution)/shard_map/grads/ppermute | solution.py:75
  236.5 8.9 %collective-permute-start.43 = (bf16[4,128,512]{2,1,0:T(8,128)(2,1)S(1)}, bf16[4,128,512]{2,1,0:T(8,128)(2,1)S(1)}, u32[]{:S(2)}, u32[]{:S(2)}) collective-permute-start(bf16[4,128,512]{2,1,0:T(8,128)(2,1)S(1)} %grads_b.11.refs_1_), channel_id=1, source_target_pairs={{0,1},{1,0},{2,3},{3,2},{4,5},{5,4},{6,7},{7,6},{8,9},{9,8},{10,11... | collective-permute-start | bytes 1572872 | tf_op jit(solution)/shard_map/grads/ppermute | solution.py:75
  236.7 8.7 %collective-permute-start.45 = (bf16[4,128,512]{2,1,0:T(8,128)(2,1)S(1)}, bf16[4,128,512]{2,1,0:T(8,128)(2,1)S(1)}, u32[]{:S(2)}, u32[]{:S(2)}) collective-permute-start(bf16[4,128,512]{2,1,0:T(8,128)(2,1)S(1)} %collective-permute-done.42.refs_3_), channel_id=1, source_target_pairs={{0,1},{1,0},{2,3},{3,2},{4,5},{5,4},{6,7},{7,6},{8,9},{9,8},{10,11... | collective-permute-start | bytes 1572872 | tf_op jit(solution)/shard_map/grads/ppermute | solution.py:75
  237.0 8.4 %collective-permute-start.44 = (bf16[4,128,512]{2,1,0:T(8,128)(2,1)S(1)}, bf16[4,128,512]{2,1,0:T(8,128)(2,1)S(1)}, u32[]{:S(2)}, u32[]{:S(2)}) collective-permute-start(bf16[4,128,512]{2,1,0:T(8,128)(2,1)S(1)} %collective-permute-done.41.refs_2_), channel_id=1, source_target_pairs={{0,1},{1,0},{2,3},{3,2},{4,5},{5,4},{6,7},{7,6},{8,9},{9,8},{10,11... | collective-permute-start | bytes 1572872 | tf_op jit(solution)/shard_map/grads/ppermute | solution.py:75
  238.1 17.2 %copy-start.12 = (bf16[320,256]{1,0:T(8,128)(2,1)S(1)}, bf16[320,256]{1,0:T(8,128)(2,1)}, u32[]{:S(2)}) copy-start(bf16[320,256]{1,0:T(8,128)(2,1)} %get-tuple-element.169.refs_0_) | copy-start | bytes 491524
  245.4 2.0 collective-permute-start.50
  245.4 9.8 %collective-permute-start.46 = (bf16[320,256]{1,0:T(8,128)(2,1)}, bf16[320,256]{1,0:T(8,128)(2,1)S(1)}, u32[]{:S(2)}, u32[]{:S(2)}) collective-permute-start(bf16[320,256]{1,0:T(8,128)(2,1)} %get-tuple-element.164), channel_id=1, source_target_pairs={{0,1},{1,0},{2,3},{3,2},{4,5},{5,4},{6,7},{7,6},{8,9},{9,8},{10,11... | collective-permute-start | bytes 491528 | tf_op jit(solution)/shard_map/rows_out/ppermute | solution.py:75
  246.0 9.2 %collective-permute-start.47 = (bf16[320,256]{1,0:T(8,128)(2,1)}, bf16[320,256]{1,0:T(8,128)(2,1)S(1)}, u32[]{:S(2)}, u32[]{:S(2)}) collective-permute-start(bf16[320,256]{1,0:T(8,128)(2,1)} %get-tuple-element.165), channel_id=1, source_target_pairs={{0,2},{1,3},{2,0},{3,1},{4,6},{5,7},{6,4},{7,5},{8,10},{9,11},{10,... | collective-permute-start | bytes 491528 | tf_op jit(solution)/shard_map/rows_out/ppermute | solution.py:75
  247.3 7.9 %collective-permute-start.48 = (bf16[320,256]{1,0:T(8,128)(2,1)}, bf16[320,256]{1,0:T(8,128)(2,1)S(1)}, u32[]{:S(2)}, u32[]{:S(2)}) collective-permute-start(bf16[320,256]{1,0:T(8,128)(2,1)} %get-tuple-element.166), channel_id=1, source_target_pairs={{0,3},{1,2},{2,1},{3,0},{4,7},{5,6},{6,5},{7,4},{8,11},{9,10},{10,... | collective-permute-start | bytes 491528 | tf_op jit(solution)/shard_map/rows_out/ppermute | solution.py:75
  (25 other events, 154.1 us)

commit v11 on v10

--- a/solution.py
+++ b/solution.py
@@ -457,7 +457,7 @@
         put(early, FF // 2 + block * half, low(mm(glat4_t, activated)), lane)
         return 0
 
-    lax.fori_loop(0, cols, step, 0)
+    lax.fori_loop(0, cols, step, 0, unroll=2)
 
 
 def ffn_a_kernel(lead, cols, *refs):
@@ -569,7 +569,8 @@
         put(early, FF + block * hid, low(mm(glat2_t, att_s[:, here])), lane)
         return 0
 
-    lax.fori_loop(0, cols, step, 0)
+    for slot in range(cols):
+        step(slot, 0)
 
 
 def attention_back_kernel(cols, *refs):
@@ -608,7 +609,10 @@
             put(late, (c + 1) * D + block * hid, low(mm(lat1_t, grad)))
         return acc
 
-    made = low(lax.fori_loop(0, cols, step, jnp.zeros((SEQ, R), F32)))
+    made = jnp.zeros((SEQ, R), F32)
+    for slot in range(cols):
+        made = step(slot, made)
+    made = low(made)
     glat1[...] = made
     put(late, 0, low(mm(low(made.astype(F32).T), n1[...])))
 

time: 257 us -> 256 us (level)
  transfers between devices with their start and end apart: 54 -> 54, of which waited for: 22 -> 21; matrix products, arithmetic and copies ran while one was open for 1% -> 1% of each run, Pallas kernels for 25% -> 25%
where the time goes in v11:
time: 256 us
  waiting for transfers between devices  101 us (39%)
  Pallas kernels  87 us (34%)
  starting transfers between devices  55.9 us (22%)
  local copies, waits for them, and re-layouts  7.22 us (3%)
  between operations  3.43 us (1%)
    ppermute x51, waiting for transfers between devices, swap(): return lax.ppermute(block, BOTH, pairs)  97.5 us
    pallas_call x19, Pallas kernels, call(): pl.pallas_call(kernel, out_shape=outs, in_specs=[pl.BlockSpec(memory_spac...  87 us
    ppermute x51, starting transfers between devices, swap(): return lax.ppermute(block, BOTH, pairs)  44.8 us
    all_to_all x2, starting transfers between devices, send_grads(): return lax.all_to_all(grads, BOTH, split_axis=0, concat_axis=0, tiled=True)  6.59 us
  transfers between devices with their start and end apart: 54, of which 21 were waited for; matrix products, arithmetic and copies ran while one was open for 1% of the time, Pallas kernels for 25%

profile of v11, /device:TPU:0, one launch (start us, length us, event | category | flops | bytes accessed | tf_op | source)
XLA Modules:
  0.0 255.7 jit_solution(16636876877751389134)
XLA Ops:
  0.7 2.7 %shard_map.276 = (bf16[4,656,256]{2,1,0:T(8,128)(2,1)}, bf16[128,1024]{1,0:T(8,128)(2,1)}) custom-call(bf16[4,320,256]{2,1,0:T(8,128)(2,1)} %bitcast.50, bf16[4,320,256]{2,1,0:T(8,128)(2,1)} %bitcast.51, bf16[2,256]{1,0:T(2,128)(2,1)} %bias_qv.1, bf16[1024]{0:T(1024)(128)(2,1)} %bias_f.1, bf16[3,128,256]{2,1,0:T(8,128)(2,1)} %wq.1, bf16[256,128]{1,0:T(8,128)(2,1)} %wp.1), custom_call_target="tpu_custom_call" | custom-call | tf_op jit(solution)/shard_map/pallas_call | solution.py:54
  3.4 4.4 %all-to-all-start = ((bf16[4,656,256]{2,1,0:T(8,128)(2,1)}), bf16[4,656,256]{2,1,0:T(8,128)(2,1)}, u32[]{:S(2)}, u32[]{:S(2)}) async-start(bf16[4,656,256]{2,1,0:T(8,128)(2,1)} %get-tuple-element.98), calls=%async_computation | async-start | bytes 2686976 | tf_op jit(solution)/shard_map/all_to_all | solution.py:815
  7.8 5.1 %collective-permute-start.2 = (bf16[128,1024]{1,0:T(8,128)(2,1)S(1)}, bf16[128,1024]{1,0:T(8,128)(2,1)S(1)}, u32[]{:S(2)}, u32[]{:S(2)}) collective-permute-start(bf16[128,1024]{1,0:T(8,128)(2,1)S(1)} %copy-done.8), channel_id=1, source_target_pairs={{0,24},{1,25},{2,26},{3,27},{4,28},{5,29},{6,30},{7,31},{8,16},{9,... | collective-permute-start | bytes 786440 | tf_op jit(solution)/shard_map/q_high/ppermute | solution.py:75
  13.0 0.6 collective-permute-start
  16.1 0.7 pad_add_fusion.3.sc.refs_0_
  16.9 0.8 shard_map.277
  17.7 0.7 copy-done.6
  18.4 0.7 copy-done.7
  19.0 0.6 dynamic-slice_bitcast_fusion.refs_14_.refs_9_
  20.2 15.6 %collective-permute-done.1.refs_2_ = bf16[128,1024]{1,0:T(8,128)(2,1)S(1)} collective-permute-done((bf16[128,1024]{1,0:T(8,128)(2,1)S(1)}, bf16[128,1024]{1,0:T(8,128)(2,1)S(1)}, u32[]{:S(2)}, u32[]{:S(2)}) %collective-permute-start.1) | collective-permute-done | bytes 262176 | tf_op jit(solution)/shard_map/q_high/ppermute | solution.py:75
  36.0 1.6 collective-permute-start.7
  37.5 1.7 collective-permute-start.6
  39.2 2.5 collective-permute-start.5
  41.7 1.9 collective-permute-start.3
  43.6 6.8 %collective-permute-done.5.refs_3_ = bf16[128,1024]{1,0:T(8,128)(2,1)S(1)} collective-permute-done((bf16[128,1024]{1,0:T(8,128)(2,1)S(1)}, bf16[128,1024]{1,0:T(8,128)(2,1)S(1)}, u32[]{:S(2)}, u32[]{:S(2)}) %collective-permute-start.5) | collective-permute-done | bytes 262176 | tf_op jit(solution)/shard_map/fa_high/ppermute | solution.py:75
  50.4 11.8 %collective-permute-done.4.refs_2_ = bf16[128,1024]{1,0:T(8,128)(2,1)S(1)} collective-permute-done((bf16[128,1024]{1,0:T(8,128)(2,1)S(1)}, bf16[128,1024]{1,0:T(8,128)(2,1)S(1)}, u32[]{:S(2)}, u32[]{:S(2)}) %collective-permute-start.4) | collective-permute-done | bytes 262176 | tf_op jit(solution)/shard_map/fa_high/ppermute | solution.py:75
  62.2 1.2 collective-permute-start.14
  63.9 13.1 %collective-permute-done.14.refs_4_.refs_12_ = bf16[4,128,1024]{2,1,0:T(8,128)(2,1)S(1)} collective-permute-done((bf16[4,128,1024]{2,1,0:T(8,128)(2,1)S(1)}, bf16[4,128,1024]{2,1,0:T(8,128)(2,1)S(1)}, u32[]{:S(2)}, u32[]{:S(2)}) %collective-permute-start.14) | collective-permute-done | bytes 1048608 | tf_op jit(solution)/shard_map/q_both/ppermute | solution.py:75
  77.2 1.2 collective-permute-start.19
  78.5 0.6 collective-permute-start.18
  79.1 2.5 collective-permute-start.13
  81.6 1.0 copy-done.21
  82.5 1.9 collective-permute-start.11
  84.5 18.0 %shard_map.278 = (bf16[320,1024]{1,0:T(8,128)(2,1)}, bf16[320,16]{1,0:T(8,128)(2,1)}, bf16[320,1024]{1,0:T(8,128)(2,1)}, bf16[320,1024]{1,0:T(8,128)(2,1)}, bf16...) custom-call(s32[4]{0:T(128)} %copy-done.13, ...), custom_call_target="tpu_custom_call" | custom-call | tf_op jit(solution)/shard_map/pallas_call | solution.py:54
  102.4 0.7 collective-permute-done.12.refs_2_
  103.3 1.2 collective-permute-start.26
  105.2 4.4 %collective-permute-done.16 = s32[4]{0:T(128)S(1)} collective-permute-done((s32[4]{0:T(128)S(1)}, s32[4]{0:T(128)S(1)}, u32[]{:S(2)}, u32[]{:S(2)}) %collective-permute-start.16) | collective-permute-done | bytes 48 | tf_op jit(solution)/shard_map/ppermute | solution.py:75
  110.4 3.4 %collective-permute-done.17 = s32[2,4]{1,0:T(2,128)S(1)} collective-permute-done((s32[2,4]{1,0:T(2,128)S(1)}, s32[2,4]{1,0:T(2,128)S(1)}, u32[]{:S(2)}, u32[]{:S(2)}) %collective-permute-start.17) | collective-permute-done | bytes 64 | tf_op jit(solution)/shard_map/ppermute | solution.py:75
  113.9 4.6 %collective-permute-done.26.refs_4_ = bf16[4,128,1024]{2,1,0:T(8,128)(2,1)} collective-permute-done((bf16[4,128,1024]{2,1,0:T(8,128)(2,1)}, bf16[4,128,1024]{2,1,0:T(8,128)(2,1)}, u32[]{:S(2)}, u32[]{:S(2)}) %collective-permute-start.26) | collective-permute-done | bytes 1048608 | tf_op jit(solution)/shard_map/fa_both/ppermute | solution.py:75
  119.0 1.2 collective-permute-start.24
  120.2 0.7 collective-permute-start.23
  120.9 1.5 collective-permute-start.25
  122.5 15.2 %shard_map.279 = (f32[320,1024]{1,0:T(8,128)}, f32[320,1024]{1,0:T(8,128)}, f32[320,16]{1,0:T(8,128)}, f32[320,16]{1,0:T(8,128)}, bf16[320,1024]{1,0:T(8,128)(2,1)}, /*index=5*/bf16[32,16,128]{2,1,0:T(8,128)(2,1)}) custom-call(s32[4]{0:T(128)} %copy-done.13, bf16[4,128,1024]{2,1,0:T(8,128)(2,1)} %copy-done.3, ...), custom_call_target="tpu_custom_call" | custom-call | tf_op jit(solution)/shard_map/pallas_call | solution.py:54
  137.7 6.9 %collective-permute-done.25 = s32[2,2,4]{2,1,0:T(2,128)S(1)} collective-permute-done((s32[2,2,4]{2,1,0:T(2,128)S(1)}, s32[2,2,4]{2,1,0:T(2,128)S(1)}, u32[]{:S(2)}, u32[]{:S(2)}) %collective-permute-start.25) | collective-permute-done | bytes 96 | tf_op jit(solution)/shard_map/ppermute | solution.py:75
  144.6 1.7 collective-permute-start.28
  147.8 11.8 %collective-permute-done.28.refs_4_ = bf16[4,128,1024]{2,1,0:T(8,128)(2,1)} collective-permute-done((bf16[4,128,1024]{2,1,0:T(8,128)(2,1)S(1)}, bf16[4,128,1024]{2,1,0:T(8,128)(2,1)}, u32[]{:S(2)}, u32[]{:S(2)}) %collective-permute-start.28) | collective-permute-done | bytes 1048608 | tf_op jit(solution)/shard_map/fb_both/ppermute | solution.py:75
  159.6 2.8 %collective-permute-done.32.refs_8_ = bf16[4,128,1024]{2,1,0:T(8,128)(2,1)S(1)} collective-permute-done((bf16[4,128,1024]{2,1,0:T(8,128)(2,1)}, bf16[4,128,1024]{2,1,0:T(8,128)(2,1)S(1)}, u32[]{:S(2)}, u32[]{:S(2)}) %collective-permute-start.32) | collective-permute-done | bytes 1048608 | tf_op jit(solution)/shard_map/fb_core/ppermute | solution.py:75
  162.5 1.0 copy-done.26
  163.4 17.9 %shard_map.280 = (bf16[320,256]{1,0:T(8,128)(2,1)}, bf16[320,256]{1,0:T(8,128)(2,1)}, bf16[320,256]{1,0:T(8,128)(2,1)}, bf16[320,256]{1,0:T(8,128)(2,1)}, bf16[3...) custom-call(s32[4]{0:T(128)} %copy-done.13, bf16[4,128,1024]{2,1,0:T(8,128)(2,1)} %copy-done.4, ...), custom_call_target="tpu_custom_call" | custom-call | tf_op jit(solution)/shard_map/pallas_call | solution.py:54
  181.3 3.6 %all-to-all-start.1 = ((bf16[32,16,384]{2,1,0:T(8,128)(2,1)}), bf16[32,16,384]{2,1,0:T(8,128)(2,1)S(1)}, u32[]{:S(2)}, u32[]{:S(2)}) async-start(bf16[32,16,384]{2,1,0:T(8,128)(2,1)} %get-tuple-element.137), calls=%async_computation.1 | async-start | bytes 786432 | tf_op jit(solution)/shard_map/grads_b_send/all_to_all | solution.py:716
  185.3 1.7 collective-permute-start.34
  187.0 10.2 %shard_map.281 = (bf16[320,1024]{1,0:T(8,128)(2,1)}, bf16[320,1024]{1,0:T(8,128)(2,1)}, bf16[320,1024]{1,0:T(8,128)(2,1)}, bf16[320,16]{1,0:T(8,128)(2,1)}, bf16[32,16,128]{2,1,0:T(8,128)(2,1)}) custom-call(s32[4]{0:T(128)} %copy-done.13, f32[320,1]{1,0:T(8,128)} %copy-done.7, bf16[320,1024]{1,0:T(8,128)(2,1)} %get-tuple-element.138.refs_2_, ...), custom_call_target="tpu_custom_call" | custom-call | tf_op jit(solution)/shard_map/pallas_call | solution.py:54
  197.2 1.4 collective-permute-done.35.refs_3_
  198.5 0.7 grads_b.6
  199.3 2.6 %collective-permute-start.36 = (bf16[128,384]{1,0:T(8,128)(2,1)S(1)}, bf16[128,384]{1,0:T(8,128)(2,1)S(1)}, u32[]{:S(2)}, u32[]{:S(2)}) collective-permute-start(bf16[128,384]{1,0:T(8,128)(2,1)S(1)} %bitcast.43), channel_id=1, source_target_pairs={{0,16},{1,17},{2,18},{3,19},{4,20},{5,21},{6,22},{7,23},{8,24},{9,... | collective-permute-start | bytes 294920 | tf_op jit(solution)/shard_map/grads_b/ppermute | solution.py:75
  201.9 3.0 %all-to-all-start.2 = ((bf16[32,16,128]{2,1,0:T(8,128)(2,1)}), bf16[32,16,128]{2,1,0:T(8,128)(2,1)S(1)}, u32[]{:S(2)}, u32[]{:S(2)}) async-start(bf16[32,16,128]{2,1,0:T(8,128)(2,1)} %get-tuple-element.144), calls=%async_computation.2 | async-start | bytes 262144 | tf_op jit(solution)/shard_map/grads_c_send/all_to_all | solution.py:716
  204.9 2.5 collective-permute-done.36.refs_1_
  207.7 1.6 collective-permute-start.37
  209.3 3.9 %all-to-all-done.2.mine = bf16[32,16,128]{2,1,0:T(8,128)(2,1)S(1)} async-done(((bf16[32,16,128]{2,1,0:T(8,128)(2,1)}), bf16[32,16,128]{2,1,0:T(8,128)(2,1)S(1)}, u32[]{:S(2)}, u32[]{:S(2)}) %all-to-all-start.2) | async-done | bytes 131104 | tf_op jit(solution)/shard_map/grads_c_send/all_to_all | solution.py:716
  213.1 0.7 grads_b.9
  213.8 1.4 collective-permute-start.40
  215.2 0.9 collective-permute-start.39
  216.1 2.2 collective-permute-start.38
  218.3 1.6 collective-permute-done.40.refs_3_
  219.9 0.8 collective-permute-done.39.refs_2_
  222.2 1.0 collective-permute-start.41
  223.2 10.7 %shard_map.282 = (bf16[320,256]{1,0:T(8,128)(2,1)}, bf16[320,256]{1,0:T(8,128)(2,1)}, bf16[320,256]{1,0:T(8,128)(2,1)}, bf16[320,256]{1,0:T(8,128)(2,1)}) custom-call(s32[4]{0:T(128)} %copy-done.13, bf16[4,128,1024]{2,1,0:T(8,128)(2,1)} %copy-done.2, bf16[4,128,1024]{2,1,0:T(8,128)(2,1)} %copy-done.16, bf16[4,128,1024]{2,1,0:T(8,128)(2,1)} %copy-done.15, ...), custom_call_target="tpu_custom_call" | custom-call | tf_op jit(solution)/shard_map/pallas_call | solution.py:54
  233.9 1.6 collective-permute-done.42.refs_3_
  236.9 0.9 grads.2
  237.8 6.9 %collective-permute-done.49.refs_4_ = bf16[4,128,512]{2,1,0:T(8,128)(2,1)S(1)} collective-permute-done((bf16[4,128,512]{2,1,0:T(8,128)(2,1)S(1)}, bf16[4,128,512]{2,1,0:T(8,128)(2,1)S(1)}, u32[]{:S(2)}, u32[]{:S(2)}) %collective-permute-start.49) | collective-permute-done | bytes 524320 | tf_op jit(solution)/shard_map/grads/ppermute | solution.py:75
  245.3 1.3 collective-permute-start.47
  246.8 0.8 copy-done.33
  247.6 6.9 %grads.3 = (f32[128,4096]{1,0:T(8,128)}, f32[128,4096]{1,0:T(8,128)}, f32[128,1024]{1,0:T(8,128)}, f32[128,1024]{1,0:T(8,128)}, f32[128,1024]{1,0:T(8,128)}, /*i...) custom-call(s32[4]{0:T(128)} %copy-done.13, bf16[4,128,512]{2,1,0:T(8,128)(2,1)} %copy-done.5, ...), custom_call_target="tpu_custom_call" | custom-call | tf_op jit(solution)/shard_map/grads/pallas_call | solution.py:54
  254.6 0.9 rows_out.1
  (150 shorter events, 9.9 us)
Async XLA Ops:
  0.6 18.4 %copy-start = (bf16[8,16,3,1024]{3,1,2,0:T(8,128)(2,1)S(1)}, bf16[8,16,3,1024]{3,1,2,0:T(8,128)(2,1)}, u32[]{:S(2)}) copy-start(bf16[8,16,3,1024]{3,1,2,0:T(8,128)(2,1)} %param.35) | copy-start | bytes 2359300
  3.4 32.6 %all-to-all-start = ((bf16[4,656,256]{2,1,0:T(8,128)(2,1)}), bf16[4,656,256]{2,1,0:T(8,128)(2,1)}, u32[]{:S(2)}, u32[]{:S(2)}) async-start(bf16[4,656,256]{2,1,0:T(8,128)(2,1)} %get-tuple-element.98), calls=%async_computation | async-start | bytes 2686976 | tf_op jit(solution)/shard_map/all_to_all | solution.py:815
  7.8 12.4 %collective-permute-start.2 = (bf16[128,1024]{1,0:T(8,128)(2,1)S(1)}, bf16[128,1024]{1,0:T(8,128)(2,1)S(1)}, u32[]{:S(2)}, u32[]{:S(2)}) collective-permute-start(bf16[128,1024]{1,0:T(8,128)(2,1)S(1)} %copy-done.8), channel_id=1, source_target_pairs={{0,24},{1,25},{2,26},{3,27},{4,28},{5,29},{6,30},{7,31},{8,16},{9,... | collective-permute-start | bytes 786440 | tf_op jit(solution)/shard_map/q_high/ppermute | solution.py:75
  13.0 22.8 %collective-permute-start.1 = (bf16[128,1024]{1,0:T(8,128)(2,1)S(1)}, bf16[128,1024]{1,0:T(8,128)(2,1)S(1)}, u32[]{:S(2)}, u32[]{:S(2)}) collective-permute-start(bf16[128,1024]{1,0:T(8,128)(2,1)S(1)} %copy-done.8), channel_id=1, source_target_pairs={{0,16},{1,17},{2,18},{3,19},{4,20},{5,21},{6,22},{7,23},{8,24},{9,... | collective-permute-start | bytes 786440 | tf_op jit(solution)/shard_map/q_high/ppermute | solution.py:75
  13.0 22.8 %collective-permute-start = (bf16[128,1024]{1,0:T(8,128)(2,1)S(1)}, bf16[128,1024]{1,0:T(8,128)(2,1)S(1)}, u32[]{:S(2)}, u32[]{:S(2)}) collective-permute-start(bf16[128,1024]{1,0:T(8,128)(2,1)S(1)} %copy-done.8), channel_id=1, source_target_pairs={{0,8},{1,9},{2,10},{3,11},{4,12},{5,13},{6,14},{7,15},{8,0},{9,1},... | collective-permute-start | bytes 786440 | tf_op jit(solution)/shard_map/q_high/ppermute | solution.py:75
  16.9 19.1 %copy-start.13 = (s32[4]{0:T(128)}, s32[4]{0:T(128)S(1)}, u32[]{:S(2)}) copy-start(s32[4]{0:T(128)S(1)} %pad_add_fusion.3.sc.refs_0_) | copy-start | bytes 52
  35.9 48.5 %copy-start.2 = (bf16[4,128,1024]{2,1,0:T(8,128)(2,1)}, bf16[4,128,1024]{2,1,0:T(8,128)(2,1)S(1)}, u32[]{:S(2)}) copy-start(bf16[4,128,1024]{2,1,0:T(8,128)(2,1)S(1)} %q_high.1.refs_1_.refs_9_) | copy-start | bytes 3145732
  36.0 26.2 %collective-permute-start.7 = (bf16[4,128,1024]{2,1,0:T(8,128)(2,1)S(1)}, bf16[4,128,1024]{2,1,0:T(8,128)(2,1)S(1)}, u32[]{:S(2)}, u32[]{:S(2)}) collective-permute-start(bf16[4,128,1024]{2,1,0:T(8,128)(2,1)S(1)} %q_high.1.refs_1_.refs_9_), channel_id=1, source_target_pairs={{0,4},{1,3},{2,6},{3,1},{4,0},{5,7},{6,2},{7,5},{8,12},{9,11},{10,... | collective-permute-start | bytes 3145736 | tf_op jit(solution)/shard_map/q_two/ppermute | solution.py:75
  37.5 24.6 %collective-permute-start.6 = (bf16[4,128,1024]{2,1,0:T(8,128)(2,1)S(1)}, bf16[4,128,1024]{2,1,0:T(8,128)(2,1)S(1)}, u32[]{:S(2)}, u32[]{:S(2)}) collective-permute-start(bf16[4,128,1024]{2,1,0:T(8,128)(2,1)S(1)} %q_high.1.refs_1_.refs_9_), channel_id=1, source_target_pairs={{0,2},{1,5},{2,0},{3,7},{4,6},{5,1},{6,4},{7,3},{8,10},{9,13},{10,... | collective-permute-start | bytes 3145736 | tf_op jit(solution)/shard_map/q_one/ppermute | solution.py:75
  39.2 11.1 %collective-permute-start.5 = (bf16[128,1024]{1,0:T(8,128)(2,1)S(1)}, bf16[128,1024]{1,0:T(8,128)(2,1)S(1)}, u32[]{:S(2)}, u32[]{:S(2)}) collective-permute-start(bf16[128,1024]{1,0:T(8,128)(2,1)S(1)} %get-tuple-element.101.refs_0_), channel_id=1, source_target_pairs={{0,24},{1,25},{2,26},{3,27},{4,28},{5,29},{6,30},{7,31},{8,16},{9,... | collective-permute-start | bytes 786440 | tf_op jit(solution)/shard_map/fa_high/ppermute | solution.py:75
  41.7 20.4 %collective-permute-start.4 = (bf16[128,1024]{1,0:T(8,128)(2,1)S(1)}, bf16[128,1024]{1,0:T(8,128)(2,1)S(1)}, u32[]{:S(2)}, u32[]{:S(2)}) collective-permute-start(bf16[128,1024]{1,0:T(8,128)(2,1)S(1)} %get-tuple-element.101.refs_0_), channel_id=1, source_target_pairs={{0,16},{1,17},{2,18},{3,19},{4,20},{5,21},{6,22},{7,23},{8,24},{9,... | collective-permute-start | bytes 786440 | tf_op jit(solution)/shard_map/fa_high/ppermute | solution.py:75
  41.7 20.4 %collective-permute-start.3 = (bf16[128,1024]{1,0:T(8,128)(2,1)S(1)}, bf16[128,1024]{1,0:T(8,128)(2,1)S(1)}, u32[]{:S(2)}, u32[]{:S(2)}) collective-permute-start(bf16[128,1024]{1,0:T(8,128)(2,1)S(1)} %get-tuple-element.101.refs_0_), channel_id=1, source_target_pairs={{0,8},{1,9},{2,10},{3,11},{4,12},{5,13},{6,14},{7,15},{8,0},{9,1},... | collective-permute-start | bytes 786440 | tf_op jit(solution)/shard_map/fa_high/ppermute | solution.py:75
  62.1 22.3 %copy-start.15 = (bf16[4,128,1024]{2,1,0:T(8,128)(2,1)}, bf16[4,128,1024]{2,1,0:T(8,128)(2,1)S(1)}, u32[]{:S(2)}) copy-start(bf16[4,128,1024]{2,1,0:T(8,128)(2,1)S(1)} %collective-permute-done.7.refs_3_.refs_11_) | copy-start | bytes 3145732
  62.2 22.3 %copy-start.16 = (bf16[4,128,1024]{2,1,0:T(8,128)(2,1)}, bf16[4,128,1024]{2,1,0:T(8,128)(2,1)S(1)}, u32[]{:S(2)}) copy-start(bf16[4,128,1024]{2,1,0:T(8,128)(2,1)S(1)} %collective-permute-done.6.refs_2_.refs_10_) | copy-start | bytes 3145732
  62.2 14.9 %collective-permute-start.14 = (bf16[4,128,1024]{2,1,0:T(8,128)(2,1)S(1)}, bf16[4,128,1024]{2,1,0:T(8,128)(2,1)S(1)}, u32[]{:S(2)}, u32[]{:S(2)}) collective-permute-start(bf16[4,128,1024]{2,1,0:T(8,128)(2,1)S(1)} %collective-permute-done.6.refs_2_.refs_10_), channel_id=1, source_target_pairs={{0,4},{1,3},{2,6},{3,1},{4,0},{5,7},{6,2},{7,5},{8,12},{9,11},{10,... | collective-permute-start | bytes 3145736 | tf_op jit(solution)/shard_map/q_both/ppermute | solution.py:75
  63.4 13.8 %collective-permute-start.8 = (bf16[4,128,1024]{2,1,0:T(8,128)(2,1)S(1)}, bf16[4,128,1024]{2,1,0:T(8,128)(2,1)S(1)}, u32[]{:S(2)}, u32[]{:S(2)}) collective-permute-start(bf16[4,128,1024]{2,1,0:T(8,128)(2,1)S(1)} %q_high.1.refs_1_.refs_9_), channel_id=1, source_target_pairs={{0,1},{1,0},{2,3},{3,2},{4,5},{5,4},{6,7},{7,6},{8,9},{9,8},{10,11... | collective-permute-start | bytes 3145736 | tf_op jit(solution)/shard_map/q_core/ppermute | solution.py:75
  63.4 13.8 %collective-permute-start.10 = (bf16[4,128,1024]{2,1,0:T(8,128)(2,1)S(1)}, bf16[4,128,1024]{2,1,0:T(8,128)(2,1)S(1)}, u32[]{:S(2)}, u32[]{:S(2)}) collective-permute-start(bf16[4,128,1024]{2,1,0:T(8,128)(2,1)S(1)} %collective-permute-done.7.refs_3_.refs_11_), channel_id=1, source_target_pairs={{0,1},{1,0},{2,3},{3,2},{4,5},{5,4},{6,7},{7,6},{8,9},{9,8},{10,11... | collective-permute-start | bytes 3145736 | tf_op jit(solution)/shard_map/q_core/ppermute | solution.py:75
  63.9 13.3 %collective-permute-start.9 = (bf16[4,128,1024]{2,1,0:T(8,128)(2,1)S(1)}, bf16[4,128,1024]{2,1,0:T(8,128)(2,1)S(1)}, u32[]{:S(2)}, u32[]{:S(2)}) collective-permute-start(bf16[4,128,1024]{2,1,0:T(8,128)(2,1)S(1)} %collective-permute-done.6.refs_2_.refs_10_), channel_id=1, source_target_pairs={{0,1},{1,0},{2,3},{3,2},{4,5},{5,4},{6,7},{7,6},{8,9},{9,8},{10,11... | collective-permute-start | bytes 3145736 | tf_op jit(solution)/shard_map/q_core/ppermute | solution.py:75
  77.0 4.5 %collective-permute-start.15 = (bf16[4,128,1024]{2,1,0:T(8,128)(2,1)S(1)}, bf16[4,128,1024]{2,1,0:T(8,128)(2,1)S(1)}, u32[]{:S(2)}, u32[]{:S(2)}) collective-permute-start(bf16[4,128,1024]{2,1,0:T(8,128)(2,1)S(1)} %collective-permute-done.14.refs_4_.refs_12_), channel_id=1, source_target_pairs={{0,1},{1,0},{2,3},{3,2},{4,5},{5,4},{6,7},{7,6},{8,9},{9,8},{10,11... | collective-permute-start | bytes 3145736 | tf_op jit(solution)/shard_map/q_core/ppermute | solution.py:75
  77.2 27.3 %copy-start.3 = (bf16[4,128,1024]{2,1,0:T(8,128)(2,1)}, bf16[4,128,1024]{2,1,0:T(8,128)(2,1)S(1)}, u32[]{:S(2)}) copy-start(bf16[4,128,1024]{2,1,0:T(8,128)(2,1)S(1)} %fa_high.1.refs_1_) | copy-start | bytes 3145732
  77.2 26.1 %collective-permute-start.19 = (bf16[4,128,1024]{2,1,0:T(8,128)(2,1)S(1)}, bf16[4,128,1024]{2,1,0:T(8,128)(2,1)}, u32[]{:S(2)}, u32[]{:S(2)}) collective-permute-start(bf16[4,128,1024]{2,1,0:T(8,128)(2,1)S(1)} %fa_high.1.refs_1_), channel_id=1, source_target_pairs={{0,4},{1,3},{2,6},{3,1},{4,0},{5,7},{6,2},{7,5},{8,12},{9,11},{10,... | collective-permute-start | bytes 3145736 | tf_op jit(solution)/shard_map/fa_two/ppermute | solution.py:75
  78.5 24.8 %collective-permute-start.18 = (bf16[4,128,1024]{2,1,0:T(8,128)(2,1)S(1)}, bf16[4,128,1024]{2,1,0:T(8,128)(2,1)}, u32[]{:S(2)}, u32[]{:S(2)}) collective-permute-start(bf16[4,128,1024]{2,1,0:T(8,128)(2,1)S(1)} %fa_high.1.refs_1_), channel_id=1, source_target_pairs={{0,2},{1,5},{2,0},{3,7},{4,6},{5,1},{6,4},{7,3},{8,10},{9,13},{10,... | collective-permute-start | bytes 3145736 | tf_op jit(solution)/shard_map/fa_one/ppermute | solution.py:75
  79.1 23.4 %collective-permute-start.13 = (bf16[128,1024]{1,0:T(8,128)(2,1)S(1)}, bf16[128,1024]{1,0:T(8,128)(2,1)S(1)}, u32[]{:S(2)}, u32[]{:S(2)}) collective-permute-start(bf16[128,1024]{1,0:T(8,128)(2,1)S(1)} %get-tuple-element.107.refs_0_), channel_id=1, source_target_pairs={{0,24},{1,25},{2,26},{3,27},{4,28},{5,29},{6,30},{7,31},{8,16},{9,... | collective-permute-start | bytes 786440 | tf_op jit(solution)/shard_map/fb_high/ppermute | solution.py:75
  81.5 21.6 %collective-permute-start.12 = (bf16[128,1024]{1,0:T(8,128)(2,1)S(1)}, bf16[128,1024]{1,0:T(8,128)(2,1)S(1)}, u32[]{:S(2)}, u32[]{:S(2)}) collective-permute-start(bf16[128,1024]{1,0:T(8,128)(2,1)S(1)} %get-tuple-element.107.refs_0_), channel_id=1, source_target_pairs={{0,16},{1,17},{2,18},{3,19},{4,20},{5,21},{6,22},{7,23},{8,24},{9,... | collective-permute-start | bytes 786440 | tf_op jit(solution)/shard_map/fb_high/ppermute | solution.py:75
  82.5 20.6 %collective-permute-start.11 = (bf16[128,1024]{1,0:T(8,128)(2,1)S(1)}, bf16[128,1024]{1,0:T(8,128)(2,1)S(1)}, u32[]{:S(2)}, u32[]{:S(2)}) collective-permute-start(bf16[128,1024]{1,0:T(8,128)(2,1)S(1)} %get-tuple-element.107.refs_0_), channel_id=1, source_target_pairs={{0,8},{1,9},{2,10},{3,11},{4,12},{5,13},{6,14},{7,15},{8,0},{9,1},... | collective-permute-start | bytes 786440 | tf_op jit(solution)/shard_map/fb_high/ppermute | solution.py:75
  103.3 15.1 %collective-permute-start.26 = (bf16[4,128,1024]{2,1,0:T(8,128)(2,1)}, bf16[4,128,1024]{2,1,0:T(8,128)(2,1)}, u32[]{:S(2)}, u32[]{:S(2)}) collective-permute-start(bf16[4,128,1024]{2,1,0:T(8,128)(2,1)} %collective-permute-done.18.refs_2_), channel_id=1, source_target_pairs={{0,4},{1,3},{2,6},{3,1},{4,0},{5,7},{6,2},{7,5},{8,12},{9,11},{10,... | collective-permute-start | bytes 3145736 | tf_op jit(solution)/shard_map/fa_both/ppermute | solution.py:75
  104.5 14.5 %collective-permute-start.20 = (bf16[4,128,1024]{2,1,0:T(8,128)(2,1)S(1)}, bf16[4,128,1024]{2,1,0:T(8,128)(2,1)}, u32[]{:S(2)}, u32[]{:S(2)}) collective-permute-start(bf16[4,128,1024]{2,1,0:T(8,128)(2,1)S(1)} %fa_high.1.refs_1_), channel_id=1, source_target_pairs={{0,1},{1,0},{2,3},{3,2},{4,5},{5,4},{6,7},{7,6},{8,9},{9,8},{10,11... | collective-permute-start | bytes 3145736 | tf_op jit(solution)/shard_map/fa_core/ppermute | solution.py:75
  104.5 14.5 %collective-permute-start.22 = (bf16[4,128,1024]{2,1,0:T(8,128)(2,1)}, bf16[4,128,1024]{2,1,0:T(8,128)(2,1)}, u32[]{:S(2)}, u32[]{:S(2)}) collective-permute-start(bf16[4,128,1024]{2,1,0:T(8,128)(2,1)} %collective-permute-done.19.refs_3_), channel_id=1, source_target_pairs={{0,1},{1,0},{2,3},{3,2},{4,5},{5,4},{6,7},{7,6},{8,9},{9,8},{10,11... | collective-permute-start | bytes 3145736 | tf_op jit(solution)/shard_map/fa_core/ppermute | solution.py:75
  105.0 14.0 %collective-permute-start.21 = (bf16[4,128,1024]{2,1,0:T(8,128)(2,1)}, bf16[4,128,1024]{2,1,0:T(8,128)(2,1)}, u32[]{:S(2)}, u32[]{:S(2)}) collective-permute-start(bf16[4,128,1024]{2,1,0:T(8,128)(2,1)} %collective-permute-done.18.refs_2_), channel_id=1, source_target_pairs={{0,1},{1,0},{2,3},{3,2},{4,5},{5,4},{6,7},{7,6},{8,9},{9,8},{10,11... | collective-permute-start | bytes 3145736 | tf_op jit(solution)/shard_map/fa_core/ppermute | solution.py:75
  105.1 42.0 %copy-start.4 = (bf16[4,128,1024]{2,1,0:T(8,128)(2,1)}, bf16[4,128,1024]{2,1,0:T(8,128)(2,1)S(1)}, u32[]{:S(2)}) copy-start(bf16[4,128,1024]{2,1,0:T(8,128)(2,1)S(1)} %fb_high.1.refs_1_) | copy-start | bytes 3145732
  105.2 4.5 %collective-permute-start.16 = (s32[4]{0:T(128)S(1)}, s32[4]{0:T(128)S(1)}, u32[]{:S(2)}, u32[]{:S(2)}) collective-permute-start(s32[4]{0:T(128)S(1)} %copy-done.34), channel_id=1, source_target_pairs={{0,16},{1,17},{2,18},{3,19},{4,20},{5,21},{6,22},{7,23},{8,24},{9,... | collective-permute-start | bytes 56 | tf_op jit(solution)/shard_map/ppermute | solution.py:75
  110.2 3.6 %collective-permute-start.17 = (s32[2,4]{1,0:T(2,128)S(1)}, s32[2,4]{1,0:T(2,128)S(1)}, u32[]{:S(2)}, u32[]{:S(2)}) collective-permute-start(s32[2,4]{1,0:T(2,128)S(1)} %gather_fusion), channel_id=1, source_target_pairs={{0,8},{1,9},{2,10},{3,11},{4,12},{5,13},{6,14},{7,15},{8,0},{9,1},... | collective-permute-start | bytes 104 | tf_op jit(solution)/shard_map/ppermute | solution.py:75
  118.4 4.1 %collective-permute-start.27 = (bf16[4,128,1024]{2,1,0:T(8,128)(2,1)}, bf16[4,128,1024]{2,1,0:T(8,128)(2,1)}, u32[]{:S(2)}, u32[]{:S(2)}) collective-permute-start(bf16[4,128,1024]{2,1,0:T(8,128)(2,1)} %collective-permute-done.26.refs_4_), channel_id=1, source_target_pairs={{0,1},{1,0},{2,3},{3,2},{4,5},{5,4},{6,7},{7,6},{8,9},{9,8},{10,11... | collective-permute-start | bytes 3145736 | tf_op jit(solution)/shard_map/fa_core/ppermute | solution.py:75
  119.0 25.6 %collective-permute-start.24 = (bf16[4,128,1024]{2,1,0:T(8,128)(2,1)S(1)}, bf16[4,128,1024]{2,1,0:T(8,128)(2,1)S(1)}, u32[]{:S(2)}, u32[]{:S(2)}) collective-permute-start(bf16[4,128,1024]{2,1,0:T(8,128)(2,1)S(1)} %fb_high.1.refs_1_), channel_id=1, source_target_pairs={{0,4},{1,3},{2,6},{3,1},{4,0},{5,7},{6,2},{7,5},{8,12},{9,11},{10,... | collective-permute-start | bytes 3145736 | tf_op jit(solution)/shard_map/fb_two/ppermute | solution.py:75
  120.2 24.4 %collective-permute-start.23 = (bf16[4,128,1024]{2,1,0:T(8,128)(2,1)S(1)}, bf16[4,128,1024]{2,1,0:T(8,128)(2,1)S(1)}, u32[]{:S(2)}, u32[]{:S(2)}) collective-permute-start(bf16[4,128,1024]{2,1,0:T(8,128)(2,1)S(1)} %fb_high.1.refs_1_), channel_id=1, source_target_pairs={{0,2},{1,5},{2,0},{3,7},{4,6},{5,1},{6,4},{7,3},{8,10},{9,13},{10,... | collective-permute-start | bytes 3145736 | tf_op jit(solution)/shard_map/fb_one/ppermute | solution.py:75
  120.9 23.6 %collective-permute-start.25 = (s32[2,2,4]{2,1,0:T(2,128)S(1)}, s32[2,2,4]{2,1,0:T(2,128)S(1)}, u32[]{:S(2)}, u32[]{:S(2)}) collective-permute-start(s32[2,2,4]{2,1,0:T(2,128)S(1)} %gather_fusion.1), channel_id=1, source_target_pairs={{0,4},{1,5},{2,6},{3,7},{4,0},{5,1},{6,2},{7,3},{8,12},{9,13},{10,... | collective-permute-start | bytes 200 | tf_op jit(solution)/shard_map/ppermute | solution.py:75
  144.6 17.9 %copy-start.22 = (bf16[4,128,1024]{2,1,0:T(8,128)(2,1)}, bf16[4,128,1024]{2,1,0:T(8,128)(2,1)S(1)}, u32[]{:S(2)}) copy-start(bf16[4,128,1024]{2,1,0:T(8,128)(2,1)S(1)} %collective-permute-done.24.refs_3_) | copy-start | bytes 3145732
  144.6 17.8 %copy-start.23 = (bf16[4,128,1024]{2,1,0:T(8,128)(2,1)}, bf16[4,128,1024]{2,1,0:T(8,128)(2,1)S(1)}, u32[]{:S(2)}) copy-start(bf16[4,128,1024]{2,1,0:T(8,128)(2,1)S(1)} %collective-permute-done.23.refs_2_) | copy-start | bytes 3145732
  144.6 14.9 %collective-permute-start.28 = (bf16[4,128,1024]{2,1,0:T(8,128)(2,1)S(1)}, bf16[4,128,1024]{2,1,0:T(8,128)(2,1)}, u32[]{:S(2)}, u32[]{:S(2)}) collective-permute-start(bf16[4,128,1024]{2,1,0:T(8,128)(2,1)S(1)} %collective-permute-done.23.refs_2_), channel_id=1, source_target_pairs={{0,4},{1,3},{2,6},{3,1},{4,0},{5,7},{6,2},{7,5},{8,12},{9,11},{10,... | collective-permute-start | bytes 3145736 | tf_op jit(solution)/shard_map/fb_both/ppermute | solution.py:75
  146.4 13.2 %collective-permute-start.30 = (bf16[4,128,1024]{2,1,0:T(8,128)(2,1)S(1)}, bf16[4,128,1024]{2,1,0:T(8,128)(2,1)}, u32[]{:S(2)}, u32[]{:S(2)}) collective-permute-start(bf16[4,128,1024]{2,1,0:T(8,128)(2,1)S(1)} %collective-permute-done.23.refs_2_), channel_id=1, source_target_pairs={{0,1},{1,0},{2,3},{3,2},{4,5},{5,4},{6,7},{7,6},{8,9},{9,8},{10,11... | collective-permute-start | bytes 3145736 | tf_op jit(solution)/shard_map/fb_core/ppermute | solution.py:75
  147.1 12.4 %collective-permute-start.29 = (bf16[4,128,1024]{2,1,0:T(8,128)(2,1)S(1)}, bf16[4,128,1024]{2,1,0:T(8,128)(2,1)S(1)}, u32[]{:S(2)}, u32[]{:S(2)}) collective-permute-start(bf16[4,128,1024]{2,1,0:T(8,128)(2,1)S(1)} %fb_high.1.refs_1_), channel_id=1, source_target_pairs={{0,1},{1,0},{2,3},{3,2},{4,5},{5,4},{6,7},{7,6},{8,9},{9,8},{10,11... | collective-permute-start | bytes 3145736 | tf_op jit(solution)/shard_map/fb_core/ppermute | solution.py:75
  147.7 11.9 %collective-permute-start.31 = (bf16[4,128,1024]{2,1,0:T(8,128)(2,1)S(1)}, bf16[4,128,1024]{2,1,0:T(8,128)(2,1)S(1)}, u32[]{:S(2)}, u32[]{:S(2)}) collective-permute-start(bf16[4,128,1024]{2,1,0:T(8,128)(2,1)S(1)} %collective-permute-done.24.refs_3_), channel_id=1, source_target_pairs={{0,1},{1,0},{2,3},{3,2},{4,5},{5,4},{6,7},{7,6},{8,9},{9,8},{10,11... | collective-permute-start | bytes 3145736 | tf_op jit(solution)/shard_map/fb_core/ppermute | solution.py:75
  159.6 2.9 %collective-permute-start.32 = (bf16[4,128,1024]{2,1,0:T(8,128)(2,1)}, bf16[4,128,1024]{2,1,0:T(8,128)(2,1)S(1)}, u32[]{:S(2)}, u32[]{:S(2)}) collective-permute-start(bf16[4,128,1024]{2,1,0:T(8,128)(2,1)} %collective-permute-done.28.refs_4_), channel_id=1, source_target_pairs={{0,1},{1,0},{2,3},{3,2},{4,5},{5,4},{6,7},{7,6},{8,9},{9,8},{10,11... | collective-permute-start | bytes 3145736 | tf_op jit(solution)/shard_map/fb_core/ppermute | solution.py:75
  181.3 17.2 %all-to-all-start.1 = ((bf16[32,16,384]{2,1,0:T(8,128)(2,1)}), bf16[32,16,384]{2,1,0:T(8,128)(2,1)S(1)}, u32[]{:S(2)}, u32[]{:S(2)}) async-start(bf16[32,16,384]{2,1,0:T(8,128)(2,1)} %get-tuple-element.137), calls=%async_computation.1 | async-start | bytes 786432 | tf_op jit(solution)/shard_map/grads_b_send/all_to_all | solution.py:716
  185.0 12.2 %collective-permute-start.33 = (bf16[320,256]{1,0:T(8,128)(2,1)}, bf16[320,256]{1,0:T(8,128)(2,1)S(1)}, u32[]{:S(2)}, u32[]{:S(2)}) collective-permute-start(bf16[320,256]{1,0:T(8,128)(2,1)} %get-tuple-element.134), channel_id=1, source_target_pairs={{0,1},{1,0},{2,3},{3,2},{4,5},{5,4},{6,7},{7,6},{8,9},{9,8},{10,11... | collective-permute-start | bytes 491528 | tf_op jit(solution)/shard_map/layer_out/ppermute | solution.py:75
  185.3 11.9 %collective-permute-start.34 = (bf16[320,256]{1,0:T(8,128)(2,1)}, bf16[320,256]{1,0:T(8,128)(2,1)S(1)}, u32[]{:S(2)}, u32[]{:S(2)}) collective-permute-start(bf16[320,256]{1,0:T(8,128)(2,1)} %get-tuple-element.135), channel_id=1, source_target_pairs={{0,2},{1,3},{2,0},{3,1},{4,6},{5,7},{6,4},{7,5},{8,10},{9,11},{10,... | collective-permute-start | bytes 491528 | tf_op jit(solution)/shard_map/layer_out/ppermute | solution.py:75
  187.0 11.6 %collective-permute-start.35 = (bf16[320,256]{1,0:T(8,128)(2,1)}, bf16[320,256]{1,0:T(8,128)(2,1)S(1)}, u32[]{:S(2)}, u32[]{:S(2)}) collective-permute-start(bf16[320,256]{1,0:T(8,128)(2,1)} %get-tuple-element.136), channel_id=1, source_target_pairs={{0,3},{1,2},{2,1},{3,0},{4,7},{5,6},{6,5},{7,4},{8,11},{9,10},{10,... | collective-permute-start | bytes 491528 | tf_op jit(solution)/shard_map/layer_out/ppermute | solution.py:75
  199.3 8.1 %collective-permute-start.36 = (bf16[128,384]{1,0:T(8,128)(2,1)S(1)}, bf16[128,384]{1,0:T(8,128)(2,1)S(1)}, u32[]{:S(2)}, u32[]{:S(2)}) collective-permute-start(bf16[128,384]{1,0:T(8,128)(2,1)S(1)} %bitcast.43), channel_id=1, source_target_pairs={{0,16},{1,17},{2,18},{3,19},{4,20},{5,21},{6,22},{7,23},{8,24},{9,... | collective-permute-start | bytes 294920 | tf_op jit(solution)/shard_map/grads_b/ppermute | solution.py:75
  201.9 11.2 %all-to-all-start.2 = ((bf16[32,16,128]{2,1,0:T(8,128)(2,1)}), bf16[32,16,128]{2,1,0:T(8,128)(2,1)S(1)}, u32[]{:S(2)}, u32[]{:S(2)}) async-start(bf16[32,16,128]{2,1,0:T(8,128)(2,1)} %get-tuple-element.144), calls=%async_computation.2 | async-start | bytes 262144 | tf_op jit(solution)/shard_map/grads_c_send/all_to_all | solution.py:716
  207.7 13.2 %collective-permute-start.37 = (bf16[2,128,384]{2,1,0:T(8,128)(2,1)S(1)}, bf16[2,128,384]{2,1,0:T(8,128)(2,1)S(1)}, u32[]{:S(2)}, u32[]{:S(2)}) collective-permute-start(bf16[2,128,384]{2,1,0:T(8,128)(2,1)S(1)} %grads_b.7), channel_id=1, source_target_pairs={{0,8},{1,9},{2,10},{3,11},{4,12},{5,13},{6,14},{7,15},{8,0},{9,1},... | collective-permute-start | bytes 589832 | tf_op jit(solution)/shard_map/grads_b/ppermute | solution.py:75
  213.8 6.1 %collective-permute-start.40 = (bf16[128,128]{1,0:T(8,128)(2,1)S(1)}, bf16[128,128]{1,0:T(8,128)(2,1)S(1)}, u32[]{:S(2)}, u32[]{:S(2)}) collective-permute-start(bf16[128,128]{1,0:T(8,128)(2,1)S(1)} %bitcast.46), channel_id=1, source_target_pairs={{0,24},{1,25},{2,26},{3,27},{4,28},{5,29},{6,30},{7,31},{8,16},{9,... | collective-permute-start | bytes 98312 | tf_op jit(solution)/shard_map/grads_b/ppermute | solution.py:75
  215.2 5.5 %collective-permute-start.39 = (bf16[128,128]{1,0:T(8,128)(2,1)S(1)}, bf16[128,128]{1,0:T(8,128)(2,1)S(1)}, u32[]{:S(2)}, u32[]{:S(2)}) collective-permute-start(bf16[128,128]{1,0:T(8,128)(2,1)S(1)} %bitcast.47), channel_id=1, source_target_pairs={{0,16},{1,17},{2,18},{3,19},{4,20},{5,21},{6,22},{7,23},{8,24},{9,... | collective-permute-start | bytes 98312 | tf_op jit(solution)/shard_map/grads_b/ppermute | solution.py:75
  216.1 4.6 %collective-permute-start.38 = (bf16[128,128]{1,0:T(8,128)(2,1)S(1)}, bf16[128,128]{1,0:T(8,128)(2,1)S(1)}, u32[]{:S(2)}, u32[]{:S(2)}) collective-permute-start(bf16[128,128]{1,0:T(8,128)(2,1)S(1)} %bitcast.48), channel_id=1, source_target_pairs={{0,8},{1,9},{2,10},{3,11},{4,12},{5,13},{6,14},{7,15},{8,0},{9,1},... | collective-permute-start | bytes 98312 | tf_op jit(solution)/shard_map/grads_b/ppermute | solution.py:75
  221.6 13.9 %collective-permute-start.42 = (bf16[4,128,512]{2,1,0:T(8,128)(2,1)S(1)}, bf16[4,128,512]{2,1,0:T(8,128)(2,1)S(1)}, u32[]{:S(2)}, u32[]{:S(2)}) collective-permute-start(bf16[4,128,512]{2,1,0:T(8,128)(2,1)S(1)} %grads_b.11.refs_1_), channel_id=1, source_target_pairs={{0,4},{1,3},{2,6},{3,1},{4,0},{5,7},{6,2},{7,5},{8,12},{9,11},{10,... | collective-permute-start | bytes 1572872 | tf_op jit(solution)/shard_map/grads/ppermute | solution.py:75
  222.2 13.3 %collective-permute-start.41 = (bf16[4,128,512]{2,1,0:T(8,128)(2,1)S(1)}, bf16[4,128,512]{2,1,0:T(8,128)(2,1)S(1)}, u32[]{:S(2)}, u32[]{:S(2)}) collective-permute-start(bf16[4,128,512]{2,1,0:T(8,128)(2,1)S(1)} %grads_b.11.refs_1_), channel_id=1, source_target_pairs={{0,2},{1,5},{2,0},{3,7},{4,6},{5,1},{6,4},{7,3},{8,10},{9,13},{10,... | collective-permute-start | bytes 1572872 | tf_op jit(solution)/shard_map/grads/ppermute | solution.py:75
  235.5 9.2 %collective-permute-start.49 = (bf16[4,128,512]{2,1,0:T(8,128)(2,1)S(1)}, bf16[4,128,512]{2,1,0:T(8,128)(2,1)S(1)}, u32[]{:S(2)}, u32[]{:S(2)}) collective-permute-start(bf16[4,128,512]{2,1,0:T(8,128)(2,1)S(1)} %collective-permute-done.41.refs_2_), channel_id=1, source_target_pairs={{0,4},{1,3},{2,6},{3,1},{4,0},{5,7},{6,2},{7,5},{8,12},{9,11},{10,... | collective-permute-start | bytes 1572872 | tf_op jit(solution)/shard_map/grads/ppermute | solution.py:75
  235.8 8.9 %collective-permute-start.43 = (bf16[4,128,512]{2,1,0:T(8,128)(2,1)S(1)}, bf16[4,128,512]{2,1,0:T(8,128)(2,1)S(1)}, u32[]{:S(2)}, u32[]{:S(2)}) collective-permute-start(bf16[4,128,512]{2,1,0:T(8,128)(2,1)S(1)} %grads_b.11.refs_1_), channel_id=1, source_target_pairs={{0,1},{1,0},{2,3},{3,2},{4,5},{5,4},{6,7},{7,6},{8,9},{9,8},{10,11... | collective-permute-start | bytes 1572872 | tf_op jit(solution)/shard_map/grads/ppermute | solution.py:75
  236.4 8.3 %collective-permute-start.45 = (bf16[4,128,512]{2,1,0:T(8,128)(2,1)S(1)}, bf16[4,128,512]{2,1,0:T(8,128)(2,1)S(1)}, u32[]{:S(2)}, u32[]{:S(2)}) collective-permute-start(bf16[4,128,512]{2,1,0:T(8,128)(2,1)S(1)} %collective-permute-done.42.refs_3_), channel_id=1, source_target_pairs={{0,1},{1,0},{2,3},{3,2},{4,5},{5,4},{6,7},{7,6},{8,9},{9,8},{10,11... | collective-permute-start | bytes 1572872 | tf_op jit(solution)/shard_map/grads/ppermute | solution.py:75
  236.4 8.4 %collective-permute-start.44 = (bf16[4,128,512]{2,1,0:T(8,128)(2,1)S(1)}, bf16[4,128,512]{2,1,0:T(8,128)(2,1)S(1)}, u32[]{:S(2)}, u32[]{:S(2)}) collective-permute-start(bf16[4,128,512]{2,1,0:T(8,128)(2,1)S(1)} %collective-permute-done.41.refs_2_), channel_id=1, source_target_pairs={{0,1},{1,0},{2,3},{3,2},{4,5},{5,4},{6,7},{7,6},{8,9},{9,8},{10,11... | collective-permute-start | bytes 1572872 | tf_op jit(solution)/shard_map/grads/ppermute | solution.py:75
  237.8 16.8 %copy-start.12 = (bf16[320,256]{1,0:T(8,128)(2,1)S(1)}, bf16[320,256]{1,0:T(8,128)(2,1)}, u32[]{:S(2)}) copy-start(bf16[320,256]{1,0:T(8,128)(2,1)} %get-tuple-element.169.refs_0_) | copy-start | bytes 491524
  244.7 2.0 collective-permute-start.50
  244.8 9.8 %collective-permute-start.46 = (bf16[320,256]{1,0:T(8,128)(2,1)}, bf16[320,256]{1,0:T(8,128)(2,1)S(1)}, u32[]{:S(2)}, u32[]{:S(2)}) collective-permute-start(bf16[320,256]{1,0:T(8,128)(2,1)} %get-tuple-element.164), channel_id=1, source_target_pairs={{0,1},{1,0},{2,3},{3,2},{4,5},{5,4},{6,7},{7,6},{8,9},{9,8},{10,11... | collective-permute-start | bytes 491528 | tf_op jit(solution)/shard_map/rows_out/ppermute | solution.py:75
  245.3 9.2 %collective-permute-start.47 = (bf16[320,256]{1,0:T(8,128)(2,1)}, bf16[320,256]{1,0:T(8,128)(2,1)S(1)}, u32[]{:S(2)}, u32[]{:S(2)}) collective-permute-start(bf16[320,256]{1,0:T(8,128)(2,1)} %get-tuple-element.165), channel_id=1, source_target_pairs={{0,2},{1,3},{2,0},{3,1},{4,6},{5,7},{6,4},{7,5},{8,10},{9,11},{10,... | collective-permute-start | bytes 491528 | tf_op jit(solution)/shard_map/rows_out/ppermute | solution.py:75
  246.7 7.9 %collective-permute-start.48 = (bf16[320,256]{1,0:T(8,128)(2,1)}, bf16[320,256]{1,0:T(8,128)(2,1)S(1)}, u32[]{:S(2)}, u32[]{:S(2)}) collective-permute-start(bf16[320,256]{1,0:T(8,128)(2,1)} %get-tuple-element.166), channel_id=1, source_target_pairs={{0,3},{1,2},{2,1},{3,0},{4,7},{5,6},{6,5},{7,4},{8,11},{9,10},{10,... | collective-permute-start | bytes 491528 | tf_op jit(solution)/shard_map/rows_out/ppermute | solution.py:75
  (25 other events, 155.1 us)

commit v12 on v11

--- a/solution.py
+++ b/solution.py
@@ -951,7 +951,7 @@
         mine_c = send_grads(late)
     with jax.named_scope("grads_b"):
         own_b, _ = gather_high(
-            sum_grads(after(mine_b, late, *layer), owners, mine_b.shape[2]), 1
+            after(sum_grads(after(mine_b, late), owners, mine_b.shape[2]), *layer), 1
         )
         own_c, _ = gather_high(sum_grads(mine_c, owners, mine_c.shape[2]))
         order_b = tuple(lead.index(place) for place in lead_table(rows, cols, 1))

time: 256 us -> 256 us (level)
  transfers between devices with their start and end apart: 54 -> 54, of which waited for: 21 -> 22; matrix products, arithmetic and copies ran while one was open for 1% -> 1% of each run, Pallas kernels for 25% -> 25%
where the time goes in v12:
time: 256 us; the launch traced here: 255 us
  waiting for transfers between devices  102 us (40%)
  Pallas kernels  87 us (34%)
  starting transfers between devices  54.5 us (21%)
  local copies, waits for them, and re-layouts  7.22 us (3%)
  between operations  3.45 us (1%)
    ppermute x51, waiting for transfers between devices, swap(): return lax.ppermute(block, BOTH, pairs)  96.4 us
    pallas_call x19, Pallas kernels, call(): pl.pallas_call(kernel, out_shape=outs, in_specs=[pl.BlockSpec(memory_spac...  87 us
    ppermute x51, starting transfers between devices, swap(): return lax.ppermute(block, BOTH, pairs)  43.2 us
    all_to_all x2, starting transfers between devices, send_grads(): return lax.all_to_all(grads, BOTH, split_axis=0, concat_axis=0, tiled=True)  6.86 us
    all_to_all x2, waiting for transfers between devices, send_grads(): return lax.all_to_all(grads, BOTH, split_axis=0, concat_axis=0, tiled=True)  5.62 us
  transfers between devices with their start and end apart: 54, of which 22 were waited for; matrix products, arithmetic and copies ran while one was open for 1% of the time, Pallas kernels for 25%

profile of v12, /device:TPU:0, one launch (start us, length us, event | category | flops | bytes accessed | tf_op | source)
XLA Modules:
  0.0 255.0 jit_solution(16429923998762070463)
XLA Ops:
  0.7 2.7 %shard_map.276 = (bf16[4,656,256]{2,1,0:T(8,128)(2,1)}, bf16[128,1024]{1,0:T(8,128)(2,1)}) custom-call(bf16[4,320,256]{2,1,0:T(8,128)(2,1)} %bitcast.50, bf16[4,320,256]{2,1,0:T(8,128)(2,1)} %bitcast.51, bf16[2,256]{1,0:T(2,128)(2,1)} %bias_qv.1, bf16[1024]{0:T(1024)(128)(2,1)} %bias_f.1, bf16[3,128,256]{2,1,0:T(8,128)(2,1)} %wq.1, bf16[256,128]{1,0:T(8,128)(2,1)} %wp.1), custom_call_target="tpu_custom_call" | custom-call | tf_op jit(solution)/shard_map/pallas_call | solution.py:54
  3.4 4.4 %all-to-all-start = ((bf16[4,656,256]{2,1,0:T(8,128)(2,1)}), bf16[4,656,256]{2,1,0:T(8,128)(2,1)}, u32[]{:S(2)}, u32[]{:S(2)}) async-start(bf16[4,656,256]{2,1,0:T(8,128)(2,1)} %get-tuple-element.99), calls=%async_computation | async-start | bytes 2686976 | tf_op jit(solution)/shard_map/all_to_all | solution.py:815
  7.8 5.1 %collective-permute-start.2 = (bf16[128,1024]{1,0:T(8,128)(2,1)S(1)}, bf16[128,1024]{1,0:T(8,128)(2,1)S(1)}, u32[]{:S(2)}, u32[]{:S(2)}) collective-permute-start(bf16[128,1024]{1,0:T(8,128)(2,1)S(1)} %copy-done.8), channel_id=1, source_target_pairs={{0,24},{1,25},{2,26},{3,27},{4,28},{5,29},{6,30},{7,31},{8,16},{9,... | collective-permute-start | bytes 786440 | tf_op jit(solution)/shard_map/q_high/ppermute | solution.py:75
  13.0 0.6 collective-permute-start
  16.1 0.7 pad_add_fusion.3.sc.refs_0_
  16.9 0.8 shard_map.277
  17.7 0.7 copy-done.6
  18.4 0.7 copy-done.7
  19.0 0.6 dynamic-slice_bitcast_fusion.refs_14_.refs_9_
  20.2 15.6 %collective-permute-done.1.refs_2_ = bf16[128,1024]{1,0:T(8,128)(2,1)S(1)} collective-permute-done((bf16[128,1024]{1,0:T(8,128)(2,1)S(1)}, bf16[128,1024]{1,0:T(8,128)(2,1)S(1)}, u32[]{:S(2)}, u32[]{:S(2)}) %collective-permute-start.1) | collective-permute-done | bytes 262176 | tf_op jit(solution)/shard_map/q_high/ppermute | solution.py:75
  36.0 1.6 collective-permute-start.7
  37.5 1.7 collective-permute-start.6
  39.2 2.5 collective-permute-start.5
  41.7 1.9 collective-permute-start.3
  43.6 6.8 %collective-permute-done.5.refs_3_ = bf16[128,1024]{1,0:T(8,128)(2,1)S(1)} collective-permute-done((bf16[128,1024]{1,0:T(8,128)(2,1)S(1)}, bf16[128,1024]{1,0:T(8,128)(2,1)S(1)}, u32[]{:S(2)}, u32[]{:S(2)}) %collective-permute-start.5) | collective-permute-done | bytes 262176 | tf_op jit(solution)/shard_map/fa_high/ppermute | solution.py:75
  50.4 11.8 %collective-permute-done.4.refs_2_ = bf16[128,1024]{1,0:T(8,128)(2,1)S(1)} collective-permute-done((bf16[128,1024]{1,0:T(8,128)(2,1)S(1)}, bf16[128,1024]{1,0:T(8,128)(2,1)S(1)}, u32[]{:S(2)}, u32[]{:S(2)}) %collective-permute-start.4) | collective-permute-done | bytes 262176 | tf_op jit(solution)/shard_map/fa_high/ppermute | solution.py:75
  62.2 1.2 collective-permute-start.14
  63.9 13.1 %collective-permute-done.14.refs_4_.refs_12_ = bf16[4,128,1024]{2,1,0:T(8,128)(2,1)S(1)} collective-permute-done((bf16[4,128,1024]{2,1,0:T(8,128)(2,1)S(1)}, bf16[4,128,1024]{2,1,0:T(8,128)(2,1)S(1)}, u32[]{:S(2)}, u32[]{:S(2)}) %collective-permute-start.14) | collective-permute-done | bytes 1048608 | tf_op jit(solution)/shard_map/q_both/ppermute | solution.py:75
  77.2 1.2 collective-permute-start.19
  78.5 0.6 collective-permute-start.18
  79.1 2.5 collective-permute-start.13
  81.6 1.0 copy-done.21
  82.5 1.9 collective-permute-start.11
  84.5 18.0 %shard_map.278 = (bf16[320,1024]{1,0:T(8,128)(2,1)}, bf16[320,16]{1,0:T(8,128)(2,1)}, bf16[320,1024]{1,0:T(8,128)(2,1)}, bf16[320,1024]{1,0:T(8,128)(2,1)}, bf16...) custom-call(s32[4]{0:T(128)} %copy-done.13, ...), custom_call_target="tpu_custom_call" | custom-call | tf_op jit(solution)/shard_map/pallas_call | solution.py:54
  102.4 0.7 collective-permute-done.12.refs_2_
  103.3 1.2 collective-permute-start.26
  105.2 4.4 %collective-permute-done.16 = s32[4]{0:T(128)S(1)} collective-permute-done((s32[4]{0:T(128)S(1)}, s32[4]{0:T(128)S(1)}, u32[]{:S(2)}, u32[]{:S(2)}) %collective-permute-start.16) | collective-permute-done | bytes 48 | tf_op jit(solution)/shard_map/ppermute | solution.py:75
  110.4 3.4 %collective-permute-done.17 = s32[2,4]{1,0:T(2,128)S(1)} collective-permute-done((s32[2,4]{1,0:T(2,128)S(1)}, s32[2,4]{1,0:T(2,128)S(1)}, u32[]{:S(2)}, u32[]{:S(2)}) %collective-permute-start.17) | collective-permute-done | bytes 64 | tf_op jit(solution)/shard_map/ppermute | solution.py:75
  113.9 4.6 %collective-permute-done.26.refs_4_ = bf16[4,128,1024]{2,1,0:T(8,128)(2,1)} collective-permute-done((bf16[4,128,1024]{2,1,0:T(8,128)(2,1)}, bf16[4,128,1024]{2,1,0:T(8,128)(2,1)}, u32[]{:S(2)}, u32[]{:S(2)}) %collective-permute-start.26) | collective-permute-done | bytes 1048608 | tf_op jit(solution)/shard_map/fa_both/ppermute | solution.py:75
  119.0 1.2 collective-permute-start.24
  120.2 0.7 collective-permute-start.23
  120.9 1.5 collective-permute-start.25
  122.5 15.2 %shard_map.279 = (f32[320,1024]{1,0:T(8,128)}, f32[320,1024]{1,0:T(8,128)}, f32[320,16]{1,0:T(8,128)}, f32[320,16]{1,0:T(8,128)}, bf16[320,1024]{1,0:T(8,128)(2,1)}, /*index=5*/bf16[32,16,128]{2,1,0:T(8,128)(2,1)}) custom-call(s32[4]{0:T(128)} %copy-done.13, bf16[4,128,1024]{2,1,0:T(8,128)(2,1)} %copy-done.3, ...), custom_call_target="tpu_custom_call" | custom-call | tf_op jit(solution)/shard_map/pallas_call | solution.py:54
  137.7 6.9 %collective-permute-done.25 = s32[2,2,4]{2,1,0:T(2,128)S(1)} collective-permute-done((s32[2,2,4]{2,1,0:T(2,128)S(1)}, s32[2,2,4]{2,1,0:T(2,128)S(1)}, u32[]{:S(2)}, u32[]{:S(2)}) %collective-permute-start.25) | collective-permute-done | bytes 96 | tf_op jit(solution)/shard_map/ppermute | solution.py:75
  144.6 1.7 collective-permute-start.28
  147.8 11.8 %collective-permute-done.28.refs_4_ = bf16[4,128,1024]{2,1,0:T(8,128)(2,1)} collective-permute-done((bf16[4,128,1024]{2,1,0:T(8,128)(2,1)S(1)}, bf16[4,128,1024]{2,1,0:T(8,128)(2,1)}, u32[]{:S(2)}, u32[]{:S(2)}) %collective-permute-start.28) | collective-permute-done | bytes 1048608 | tf_op jit(solution)/shard_map/fb_both/ppermute | solution.py:75
  159.6 2.8 %collective-permute-done.32.refs_8_ = bf16[4,128,1024]{2,1,0:T(8,128)(2,1)S(1)} collective-permute-done((bf16[4,128,1024]{2,1,0:T(8,128)(2,1)}, bf16[4,128,1024]{2,1,0:T(8,128)(2,1)S(1)}, u32[]{:S(2)}, u32[]{:S(2)}) %collective-permute-start.32) | collective-permute-done | bytes 1048608 | tf_op jit(solution)/shard_map/fb_core/ppermute | solution.py:75
  162.5 1.0 copy-done.26
  163.4 17.9 %shard_map.280 = (bf16[320,256]{1,0:T(8,128)(2,1)}, bf16[320,256]{1,0:T(8,128)(2,1)}, bf16[320,256]{1,0:T(8,128)(2,1)}, bf16[320,256]{1,0:T(8,128)(2,1)}, bf16[3...) custom-call(s32[4]{0:T(128)} %copy-done.13, bf16[4,128,1024]{2,1,0:T(8,128)(2,1)} %copy-done.4, ...), custom_call_target="tpu_custom_call" | custom-call | tf_op jit(solution)/shard_map/pallas_call | solution.py:54
  181.3 3.6 %all-to-all-start.1 = ((bf16[32,16,384]{2,1,0:T(8,128)(2,1)}), bf16[32,16,384]{2,1,0:T(8,128)(2,1)S(1)}, u32[]{:S(2)}, u32[]{:S(2)}) async-start(bf16[32,16,384]{2,1,0:T(8,128)(2,1)} %get-tuple-element.138), calls=%async_computation.1 | async-start | bytes 786432 | tf_op jit(solution)/shard_map/grads_b_send/all_to_all | solution.py:716
  185.3 1.7 collective-permute-start.34
  187.0 10.2 %shard_map.281 = (bf16[320,1024]{1,0:T(8,128)(2,1)}, bf16[320,1024]{1,0:T(8,128)(2,1)}, bf16[320,1024]{1,0:T(8,128)(2,1)}, bf16[320,16]{1,0:T(8,128)(2,1)}, bf16[32,16,128]{2,1,0:T(8,128)(2,1)}) custom-call(s32[4]{0:T(128)} %copy-done.13, f32[320,1]{1,0:T(8,128)} %copy-done.7, bf16[320,1024]{1,0:T(8,128)(2,1)} %get-tuple-element.139.refs_2_, ...), custom_call_target="tpu_custom_call" | custom-call | tf_op jit(solution)/shard_map/pallas_call | solution.py:54
  197.2 1.0 all-to-all-done.1.mine
  198.1 0.7 grads_b.6
  198.9 2.2 collective-permute-start.36
  201.1 3.2 %all-to-all-start.2 = ((bf16[32,16,128]{2,1,0:T(8,128)(2,1)}), bf16[32,16,128]{2,1,0:T(8,128)(2,1)S(1)}, u32[]{:S(2)}, u32[]{:S(2)}) async-start(bf16[32,16,128]{2,1,0:T(8,128)(2,1)} %get-tuple-element.145), calls=%async_computation.2 | async-start | bytes 262144 | tf_op jit(solution)/shard_map/grads_c_send/all_to_all | solution.py:716
  204.3 2.3 collective-permute-done.36.refs_1_
  206.8 1.1 collective-permute-start.37
  207.9 4.6 %all-to-all-done.2.mine = bf16[32,16,128]{2,1,0:T(8,128)(2,1)S(1)} async-done(((bf16[32,16,128]{2,1,0:T(8,128)(2,1)}), bf16[32,16,128]{2,1,0:T(8,128)(2,1)S(1)}, u32[]{:S(2)}, u32[]{:S(2)}) %all-to-all-start.2) | async-done | bytes 131104 | tf_op jit(solution)/shard_map/grads_c_send/all_to_all | solution.py:716
  212.6 0.7 grads_b.9
  213.3 1.5 collective-permute-start.40
  214.7 0.7 collective-permute-start.39
  215.4 2.3 collective-permute-start.38
  217.7 1.6 collective-permute-done.40.refs_3_
  220.9 0.7 collective-permute-start.42
  221.6 0.8 collective-permute-start.41
  222.4 10.7 %shard_map.282 = (bf16[320,256]{1,0:T(8,128)(2,1)}, bf16[320,256]{1,0:T(8,128)(2,1)}, bf16[320,256]{1,0:T(8,128)(2,1)}, bf16[320,256]{1,0:T(8,128)(2,1)}) custom-call(s32[4]{0:T(128)} %copy-done.13, bf16[4,128,1024]{2,1,0:T(8,128)(2,1)} %copy-done.2, bf16[4,128,1024]{2,1,0:T(8,128)(2,1)} %copy-done.16, bf16[4,128,1024]{2,1,0:T(8,128)(2,1)} %copy-done.15, ...), custom_call_target="tpu_custom_call" | custom-call | tf_op jit(solution)/shard_map/pallas_call | solution.py:54
  233.1 1.7 collective-permute-done.42.refs_3_
  235.7 0.9 grads.2
  236.6 7.5 %collective-permute-done.49.refs_4_ = bf16[4,128,512]{2,1,0:T(8,128)(2,1)S(1)} collective-permute-done((bf16[4,128,512]{2,1,0:T(8,128)(2,1)S(1)}, bf16[4,128,512]{2,1,0:T(8,128)(2,1)S(1)}, u32[]{:S(2)}, u32[]{:S(2)}) %collective-permute-start.49) | collective-permute-done | bytes 524320 | tf_op jit(solution)/shard_map/grads/ppermute | solution.py:75
  244.7 1.0 collective-permute-start.47
  246.1 0.8 copy-done.33
  247.0 6.9 %grads.3 = (f32[128,4096]{1,0:T(8,128)}, f32[128,4096]{1,0:T(8,128)}, f32[128,1024]{1,0:T(8,128)}, f32[128,1024]{1,0:T(8,128)}, f32[128,1024]{1,0:T(8,128)}, /*i...) custom-call(s32[4]{0:T(128)} %copy-done.13, bf16[4,128,512]{2,1,0:T(8,128)(2,1)} %copy-done.5, ...), custom_call_target="tpu_custom_call" | custom-call | tf_op jit(solution)/shard_map/grads/pallas_call | solution.py:54
  253.9 0.9 rows_out.1
  (150 shorter events, 9.7 us)
Async XLA Ops:
  0.6 18.4 %copy-start = (bf16[8,16,3,1024]{3,1,2,0:T(8,128)(2,1)S(1)}, bf16[8,16,3,1024]{3,1,2,0:T(8,128)(2,1)}, u32[]{:S(2)}) copy-start(bf16[8,16,3,1024]{3,1,2,0:T(8,128)(2,1)} %param.35) | copy-start | bytes 2359300
  3.4 32.6 %all-to-all-start = ((bf16[4,656,256]{2,1,0:T(8,128)(2,1)}), bf16[4,656,256]{2,1,0:T(8,128)(2,1)}, u32[]{:S(2)}, u32[]{:S(2)}) async-start(bf16[4,656,256]{2,1,0:T(8,128)(2,1)} %get-tuple-element.99), calls=%async_computation | async-start | bytes 2686976 | tf_op jit(solution)/shard_map/all_to_all | solution.py:815
  7.8 12.4 %collective-permute-start.2 = (bf16[128,1024]{1,0:T(8,128)(2,1)S(1)}, bf16[128,1024]{1,0:T(8,128)(2,1)S(1)}, u32[]{:S(2)}, u32[]{:S(2)}) collective-permute-start(bf16[128,1024]{1,0:T(8,128)(2,1)S(1)} %copy-done.8), channel_id=1, source_target_pairs={{0,24},{1,25},{2,26},{3,27},{4,28},{5,29},{6,30},{7,31},{8,16},{9,... | collective-permute-start | bytes 786440 | tf_op jit(solution)/shard_map/q_high/ppermute | solution.py:75
  13.0 22.8 %collective-permute-start.1 = (bf16[128,1024]{1,0:T(8,128)(2,1)S(1)}, bf16[128,1024]{1,0:T(8,128)(2,1)S(1)}, u32[]{:S(2)}, u32[]{:S(2)}) collective-permute-start(bf16[128,1024]{1,0:T(8,128)(2,1)S(1)} %copy-done.8), channel_id=1, source_target_pairs={{0,16},{1,17},{2,18},{3,19},{4,20},{5,21},{6,22},{7,23},{8,24},{9,... | collective-permute-start | bytes 786440 | tf_op jit(solution)/shard_map/q_high/ppermute | solution.py:75
  13.0 22.8 %collective-permute-start = (bf16[128,1024]{1,0:T(8,128)(2,1)S(1)}, bf16[128,1024]{1,0:T(8,128)(2,1)S(1)}, u32[]{:S(2)}, u32[]{:S(2)}) collective-permute-start(bf16[128,1024]{1,0:T(8,128)(2,1)S(1)} %copy-done.8), channel_id=1, source_target_pairs={{0,8},{1,9},{2,10},{3,11},{4,12},{5,13},{6,14},{7,15},{8,0},{9,1},... | collective-permute-start | bytes 786440 | tf_op jit(solution)/shard_map/q_high/ppermute | solution.py:75
  16.9 19.1 %copy-start.13 = (s32[4]{0:T(128)}, s32[4]{0:T(128)S(1)}, u32[]{:S(2)}) copy-start(s32[4]{0:T(128)S(1)} %pad_add_fusion.3.sc.refs_0_) | copy-start | bytes 52
  35.9 48.5 %copy-start.2 = (bf16[4,128,1024]{2,1,0:T(8,128)(2,1)}, bf16[4,128,1024]{2,1,0:T(8,128)(2,1)S(1)}, u32[]{:S(2)}) copy-start(bf16[4,128,1024]{2,1,0:T(8,128)(2,1)S(1)} %q_high.1.refs_1_.refs_9_) | copy-start | bytes 3145732
  36.0 26.2 %collective-permute-start.7 = (bf16[4,128,1024]{2,1,0:T(8,128)(2,1)S(1)}, bf16[4,128,1024]{2,1,0:T(8,128)(2,1)S(1)}, u32[]{:S(2)}, u32[]{:S(2)}) collective-permute-start(bf16[4,128,1024]{2,1,0:T(8,128)(2,1)S(1)} %q_high.1.refs_1_.refs_9_), channel_id=1, source_target_pairs={{0,4},{1,3},{2,6},{3,1},{4,0},{5,7},{6,2},{7,5},{8,12},{9,11},{10,... | collective-permute-start | bytes 3145736 | tf_op jit(solution)/shard_map/q_two/ppermute | solution.py:75
  37.5 24.6 %collective-permute-start.6 = (bf16[4,128,1024]{2,1,0:T(8,128)(2,1)S(1)}, bf16[4,128,1024]{2,1,0:T(8,128)(2,1)S(1)}, u32[]{:S(2)}, u32[]{:S(2)}) collective-permute-start(bf16[4,128,1024]{2,1,0:T(8,128)(2,1)S(1)} %q_high.1.refs_1_.refs_9_), channel_id=1, source_target_pairs={{0,2},{1,5},{2,0},{3,7},{4,6},{5,1},{6,4},{7,3},{8,10},{9,13},{10,... | collective-permute-start | bytes 3145736 | tf_op jit(solution)/shard_map/q_one/ppermute | solution.py:75
  39.2 11.1 %collective-permute-start.5 = (bf16[128,1024]{1,0:T(8,128)(2,1)S(1)}, bf16[128,1024]{1,0:T(8,128)(2,1)S(1)}, u32[]{:S(2)}, u32[]{:S(2)}) collective-permute-start(bf16[128,1024]{1,0:T(8,128)(2,1)S(1)} %get-tuple-element.102.refs_0_), channel_id=1, source_target_pairs={{0,24},{1,25},{2,26},{3,27},{4,28},{5,29},{6,30},{7,31},{8,16},{9,... | collective-permute-start | bytes 786440 | tf_op jit(solution)/shard_map/fa_high/ppermute | solution.py:75
  41.7 20.4 %collective-permute-start.4 = (bf16[128,1024]{1,0:T(8,128)(2,1)S(1)}, bf16[128,1024]{1,0:T(8,128)(2,1)S(1)}, u32[]{:S(2)}, u32[]{:S(2)}) collective-permute-start(bf16[128,1024]{1,0:T(8,128)(2,1)S(1)} %get-tuple-element.102.refs_0_), channel_id=1, source_target_pairs={{0,16},{1,17},{2,18},{3,19},{4,20},{5,21},{6,22},{7,23},{8,24},{9,... | collective-permute-start | bytes 786440 | tf_op jit(solution)/shard_map/fa_high/ppermute | solution.py:75
  41.7 20.4 %collective-permute-start.3 = (bf16[128,1024]{1,0:T(8,128)(2,1)S(1)}, bf16[128,1024]{1,0:T(8,128)(2,1)S(1)}, u32[]{:S(2)}, u32[]{:S(2)}) collective-permute-start(bf16[128,1024]{1,0:T(8,128)(2,1)S(1)} %get-tuple-element.102.refs_0_), channel_id=1, source_target_pairs={{0,8},{1,9},{2,10},{3,11},{4,12},{5,13},{6,14},{7,15},{8,0},{9,1},... | collective-permute-start | bytes 786440 | tf_op jit(solution)/shard_map/fa_high/ppermute | solution.py:75
  62.1 22.3 %copy-start.15 = (bf16[4,128,1024]{2,1,0:T(8,128)(2,1)}, bf16[4,128,1024]{2,1,0:T(8,128)(2,1)S(1)}, u32[]{:S(2)}) copy-start(bf16[4,128,1024]{2,1,0:T(8,128)(2,1)S(1)} %collective-permute-done.7.refs_3_.refs_11_) | copy-start | bytes 3145732
  62.2 22.3 %copy-start.16 = (bf16[4,128,1024]{2,1,0:T(8,128)(2,1)}, bf16[4,128,1024]{2,1,0:T(8,128)(2,1)S(1)}, u32[]{:S(2)}) copy-start(bf16[4,128,1024]{2,1,0:T(8,128)(2,1)S(1)} %collective-permute-done.6.refs_2_.refs_10_) | copy-start | bytes 3145732
  62.2 14.9 %collective-permute-start.14 = (bf16[4,128,1024]{2,1,0:T(8,128)(2,1)S(1)}, bf16[4,128,1024]{2,1,0:T(8,128)(2,1)S(1)}, u32[]{:S(2)}, u32[]{:S(2)}) collective-permute-start(bf16[4,128,1024]{2,1,0:T(8,128)(2,1)S(1)} %collective-permute-done.6.refs_2_.refs_10_), channel_id=1, source_target_pairs={{0,4},{1,3},{2,6},{3,1},{4,0},{5,7},{6,2},{7,5},{8,12},{9,11},{10,... | collective-permute-start | bytes 3145736 | tf_op jit(solution)/shard_map/q_both/ppermute | solution.py:75
  63.4 13.8 %collective-permute-start.8 = (bf16[4,128,1024]{2,1,0:T(8,128)(2,1)S(1)}, bf16[4,128,1024]{2,1,0:T(8,128)(2,1)S(1)}, u32[]{:S(2)}, u32[]{:S(2)}) collective-permute-start(bf16[4,128,1024]{2,1,0:T(8,128)(2,1)S(1)} %q_high.1.refs_1_.refs_9_), channel_id=1, source_target_pairs={{0,1},{1,0},{2,3},{3,2},{4,5},{5,4},{6,7},{7,6},{8,9},{9,8},{10,11... | collective-permute-start | bytes 3145736 | tf_op jit(solution)/shard_map/q_core/ppermute | solution.py:75
  63.4 13.8 %collective-permute-start.10 = (bf16[4,128,1024]{2,1,0:T(8,128)(2,1)S(1)}, bf16[4,128,1024]{2,1,0:T(8,128)(2,1)S(1)}, u32[]{:S(2)}, u32[]{:S(2)}) collective-permute-start(bf16[4,128,1024]{2,1,0:T(8,128)(2,1)S(1)} %collective-permute-done.7.refs_3_.refs_11_), channel_id=1, source_target_pairs={{0,1},{1,0},{2,3},{3,2},{4,5},{5,4},{6,7},{7,6},{8,9},{9,8},{10,11... | collective-permute-start | bytes 3145736 | tf_op jit(solution)/shard_map/q_core/ppermute | solution.py:75
  63.9 13.3 %collective-permute-start.9 = (bf16[4,128,1024]{2,1,0:T(8,128)(2,1)S(1)}, bf16[4,128,1024]{2,1,0:T(8,128)(2,1)S(1)}, u32[]{:S(2)}, u32[]{:S(2)}) collective-permute-start(bf16[4,128,1024]{2,1,0:T(8,128)(2,1)S(1)} %collective-permute-done.6.refs_2_.refs_10_), channel_id=1, source_target_pairs={{0,1},{1,0},{2,3},{3,2},{4,5},{5,4},{6,7},{7,6},{8,9},{9,8},{10,11... | collective-permute-start | bytes 3145736 | tf_op jit(solution)/shard_map/q_core/ppermute | solution.py:75
  77.0 4.5 %collective-permute-start.15 = (bf16[4,128,1024]{2,1,0:T(8,128)(2,1)S(1)}, bf16[4,128,1024]{2,1,0:T(8,128)(2,1)S(1)}, u32[]{:S(2)}, u32[]{:S(2)}) collective-permute-start(bf16[4,128,1024]{2,1,0:T(8,128)(2,1)S(1)} %collective-permute-done.14.refs_4_.refs_12_), channel_id=1, source_target_pairs={{0,1},{1,0},{2,3},{3,2},{4,5},{5,4},{6,7},{7,6},{8,9},{9,8},{10,11... | collective-permute-start | bytes 3145736 | tf_op jit(solution)/shard_map/q_core/ppermute | solution.py:75
  77.2 27.3 %copy-start.3 = (bf16[4,128,1024]{2,1,0:T(8,128)(2,1)}, bf16[4,128,1024]{2,1,0:T(8,128)(2,1)S(1)}, u32[]{:S(2)}) copy-start(bf16[4,128,1024]{2,1,0:T(8,128)(2,1)S(1)} %fa_high.1.refs_1_) | copy-start | bytes 3145732
  77.2 26.1 %collective-permute-start.19 = (bf16[4,128,1024]{2,1,0:T(8,128)(2,1)S(1)}, bf16[4,128,1024]{2,1,0:T(8,128)(2,1)}, u32[]{:S(2)}, u32[]{:S(2)}) collective-permute-start(bf16[4,128,1024]{2,1,0:T(8,128)(2,1)S(1)} %fa_high.1.refs_1_), channel_id=1, source_target_pairs={{0,4},{1,3},{2,6},{3,1},{4,0},{5,7},{6,2},{7,5},{8,12},{9,11},{10,... | collective-permute-start | bytes 3145736 | tf_op jit(solution)/shard_map/fa_two/ppermute | solution.py:75
  78.5 24.8 %collective-permute-start.18 = (bf16[4,128,1024]{2,1,0:T(8,128)(2,1)S(1)}, bf16[4,128,1024]{2,1,0:T(8,128)(2,1)}, u32[]{:S(2)}, u32[]{:S(2)}) collective-permute-start(bf16[4,128,1024]{2,1,0:T(8,128)(2,1)S(1)} %fa_high.1.refs_1_), channel_id=1, source_target_pairs={{0,2},{1,5},{2,0},{3,7},{4,6},{5,1},{6,4},{7,3},{8,10},{9,13},{10,... | collective-permute-start | bytes 3145736 | tf_op jit(solution)/shard_map/fa_one/ppermute | solution.py:75
  79.1 23.4 %collective-permute-start.13 = (bf16[128,1024]{1,0:T(8,128)(2,1)S(1)}, bf16[128,1024]{1,0:T(8,128)(2,1)S(1)}, u32[]{:S(2)}, u32[]{:S(2)}) collective-permute-start(bf16[128,1024]{1,0:T(8,128)(2,1)S(1)} %get-tuple-element.108.refs_0_), channel_id=1, source_target_pairs={{0,24},{1,25},{2,26},{3,27},{4,28},{5,29},{6,30},{7,31},{8,16},{9,... | collective-permute-start | bytes 786440 | tf_op jit(solution)/shard_map/fb_high/ppermute | solution.py:75
  81.5 21.6 %collective-permute-start.12 = (bf16[128,1024]{1,0:T(8,128)(2,1)S(1)}, bf16[128,1024]{1,0:T(8,128)(2,1)S(1)}, u32[]{:S(2)}, u32[]{:S(2)}) collective-permute-start(bf16[128,1024]{1,0:T(8,128)(2,1)S(1)} %get-tuple-element.108.refs_0_), channel_id=1, source_target_pairs={{0,16},{1,17},{2,18},{3,19},{4,20},{5,21},{6,22},{7,23},{8,24},{9,... | collective-permute-start | bytes 786440 | tf_op jit(solution)/shard_map/fb_high/ppermute | solution.py:75
  82.5 20.6 %collective-permute-start.11 = (bf16[128,1024]{1,0:T(8,128)(2,1)S(1)}, bf16[128,1024]{1,0:T(8,128)(2,1)S(1)}, u32[]{:S(2)}, u32[]{:S(2)}) collective-permute-start(bf16[128,1024]{1,0:T(8,128)(2,1)S(1)} %get-tuple-element.108.refs_0_), channel_id=1, source_target_pairs={{0,8},{1,9},{2,10},{3,11},{4,12},{5,13},{6,14},{7,15},{8,0},{9,1},... | collective-permute-start | bytes 786440 | tf_op jit(solution)/shard_map/fb_high/ppermute | solution.py:75
  103.3 15.1 %collective-permute-start.26 = (bf16[4,128,1024]{2,1,0:T(8,128)(2,1)}, bf16[4,128,1024]{2,1,0:T(8,128)(2,1)}, u32[]{:S(2)}, u32[]{:S(2)}) collective-permute-start(bf16[4,128,1024]{2,1,0:T(8,128)(2,1)} %collective-permute-done.18.refs_2_), channel_id=1, source_target_pairs={{0,4},{1,3},{2,6},{3,1},{4,0},{5,7},{6,2},{7,5},{8,12},{9,11},{10,... | collective-permute-start | bytes 3145736 | tf_op jit(solution)/shard_map/fa_both/ppermute | solution.py:75
  104.5 14.5 %collective-permute-start.20 = (bf16[4,128,1024]{2,1,0:T(8,128)(2,1)S(1)}, bf16[4,128,1024]{2,1,0:T(8,128)(2,1)}, u32[]{:S(2)}, u32[]{:S(2)}) collective-permute-start(bf16[4,128,1024]{2,1,0:T(8,128)(2,1)S(1)} %fa_high.1.refs_1_), channel_id=1, source_target_pairs={{0,1},{1,0},{2,3},{3,2},{4,5},{5,4},{6,7},{7,6},{8,9},{9,8},{10,11... | collective-permute-start | bytes 3145736 | tf_op jit(solution)/shard_map/fa_core/ppermute | solution.py:75
  104.5 14.5 %collective-permute-start.22 = (bf16[4,128,1024]{2,1,0:T(8,128)(2,1)}, bf16[4,128,1024]{2,1,0:T(8,128)(2,1)}, u32[]{:S(2)}, u32[]{:S(2)}) collective-permute-start(bf16[4,128,1024]{2,1,0:T(8,128)(2,1)} %collective-permute-done.19.refs_3_), channel_id=1, source_target_pairs={{0,1},{1,0},{2,3},{3,2},{4,5},{5,4},{6,7},{7,6},{8,9},{9,8},{10,11... | collective-permute-start | bytes 3145736 | tf_op jit(solution)/shard_map/fa_core/ppermute | solution.py:75
  105.0 14.0 %collective-permute-start.21 = (bf16[4,128,1024]{2,1,0:T(8,128)(2,1)}, bf16[4,128,1024]{2,1,0:T(8,128)(2,1)}, u32[]{:S(2)}, u32[]{:S(2)}) collective-permute-start(bf16[4,128,1024]{2,1,0:T(8,128)(2,1)} %collective-permute-done.18.refs_2_), channel_id=1, source_target_pairs={{0,1},{1,0},{2,3},{3,2},{4,5},{5,4},{6,7},{7,6},{8,9},{9,8},{10,11... | collective-permute-start | bytes 3145736 | tf_op jit(solution)/shard_map/fa_core/ppermute | solution.py:75
  105.1 42.0 %copy-start.4 = (bf16[4,128,1024]{2,1,0:T(8,128)(2,1)}, bf16[4,128,1024]{2,1,0:T(8,128)(2,1)S(1)}, u32[]{:S(2)}) copy-start(bf16[4,128,1024]{2,1,0:T(8,128)(2,1)S(1)} %fb_high.1.refs_1_) | copy-start | bytes 3145732
  105.2 4.5 %collective-permute-start.16 = (s32[4]{0:T(128)S(1)}, s32[4]{0:T(128)S(1)}, u32[]{:S(2)}, u32[]{:S(2)}) collective-permute-start(s32[4]{0:T(128)S(1)} %copy-done.34), channel_id=1, source_target_pairs={{0,16},{1,17},{2,18},{3,19},{4,20},{5,21},{6,22},{7,23},{8,24},{9,... | collective-permute-start | bytes 56 | tf_op jit(solution)/shard_map/ppermute | solution.py:75
  110.2 3.6 %collective-permute-start.17 = (s32[2,4]{1,0:T(2,128)S(1)}, s32[2,4]{1,0:T(2,128)S(1)}, u32[]{:S(2)}, u32[]{:S(2)}) collective-permute-start(s32[2,4]{1,0:T(2,128)S(1)} %gather_fusion), channel_id=1, source_target_pairs={{0,8},{1,9},{2,10},{3,11},{4,12},{5,13},{6,14},{7,15},{8,0},{9,1},... | collective-permute-start | bytes 104 | tf_op jit(solution)/shard_map/ppermute | solution.py:75
  118.4 4.1 %collective-permute-start.27 = (bf16[4,128,1024]{2,1,0:T(8,128)(2,1)}, bf16[4,128,1024]{2,1,0:T(8,128)(2,1)}, u32[]{:S(2)}, u32[]{:S(2)}) collective-permute-start(bf16[4,128,1024]{2,1,0:T(8,128)(2,1)} %collective-permute-done.26.refs_4_), channel_id=1, source_target_pairs={{0,1},{1,0},{2,3},{3,2},{4,5},{5,4},{6,7},{7,6},{8,9},{9,8},{10,11... | collective-permute-start | bytes 3145736 | tf_op jit(solution)/shard_map/fa_core/ppermute | solution.py:75
  119.0 25.6 %collective-permute-start.24 = (bf16[4,128,1024]{2,1,0:T(8,128)(2,1)S(1)}, bf16[4,128,1024]{2,1,0:T(8,128)(2,1)S(1)}, u32[]{:S(2)}, u32[]{:S(2)}) collective-permute-start(bf16[4,128,1024]{2,1,0:T(8,128)(2,1)S(1)} %fb_high.1.refs_1_), channel_id=1, source_target_pairs={{0,4},{1,3},{2,6},{3,1},{4,0},{5,7},{6,2},{7,5},{8,12},{9,11},{10,... | collective-permute-start | bytes 3145736 | tf_op jit(solution)/shard_map/fb_two/ppermute | solution.py:75
  120.2 24.4 %collective-permute-start.23 = (bf16[4,128,1024]{2,1,0:T(8,128)(2,1)S(1)}, bf16[4,128,1024]{2,1,0:T(8,128)(2,1)S(1)}, u32[]{:S(2)}, u32[]{:S(2)}) collective-permute-start(bf16[4,128,1024]{2,1,0:T(8,128)(2,1)S(1)} %fb_high.1.refs_1_), channel_id=1, source_target_pairs={{0,2},{1,5},{2,0},{3,7},{4,6},{5,1},{6,4},{7,3},{8,10},{9,13},{10,... | collective-permute-start | bytes 3145736 | tf_op jit(solution)/shard_map/fb_one/ppermute | solution.py:75
  120.9 23.6 %collective-permute-start.25 = (s32[2,2,4]{2,1,0:T(2,128)S(1)}, s32[2,2,4]{2,1,0:T(2,128)S(1)}, u32[]{:S(2)}, u32[]{:S(2)}) collective-permute-start(s32[2,2,4]{2,1,0:T(2,128)S(1)} %gather_fusion.1), channel_id=1, source_target_pairs={{0,4},{1,5},{2,6},{3,7},{4,0},{5,1},{6,2},{7,3},{8,12},{9,13},{10,... | collective-permute-start | bytes 200 | tf_op jit(solution)/shard_map/ppermute | solution.py:75
  144.6 17.9 %copy-start.22 = (bf16[4,128,1024]{2,1,0:T(8,128)(2,1)}, bf16[4,128,1024]{2,1,0:T(8,128)(2,1)S(1)}, u32[]{:S(2)}) copy-start(bf16[4,128,1024]{2,1,0:T(8,128)(2,1)S(1)} %collective-permute-done.24.refs_3_) | copy-start | bytes 3145732
  144.6 17.8 %copy-start.23 = (bf16[4,128,1024]{2,1,0:T(8,128)(2,1)}, bf16[4,128,1024]{2,1,0:T(8,128)(2,1)S(1)}, u32[]{:S(2)}) copy-start(bf16[4,128,1024]{2,1,0:T(8,128)(2,1)S(1)} %collective-permute-done.23.refs_2_) | copy-start | bytes 3145732
  144.6 14.9 %collective-permute-start.28 = (bf16[4,128,1024]{2,1,0:T(8,128)(2,1)S(1)}, bf16[4,128,1024]{2,1,0:T(8,128)(2,1)}, u32[]{:S(2)}, u32[]{:S(2)}) collective-permute-start(bf16[4,128,1024]{2,1,0:T(8,128)(2,1)S(1)} %collective-permute-done.23.refs_2_), channel_id=1, source_target_pairs={{0,4},{1,3},{2,6},{3,1},{4,0},{5,7},{6,2},{7,5},{8,12},{9,11},{10,... | collective-permute-start | bytes 3145736 | tf_op jit(solution)/shard_map/fb_both/ppermute | solution.py:75
  146.4 13.2 %collective-permute-start.30 = (bf16[4,128,1024]{2,1,0:T(8,128)(2,1)S(1)}, bf16[4,128,1024]{2,1,0:T(8,128)(2,1)}, u32[]{:S(2)}, u32[]{:S(2)}) collective-permute-start(bf16[4,128,1024]{2,1,0:T(8,128)(2,1)S(1)} %collective-permute-done.23.refs_2_), channel_id=1, source_target_pairs={{0,1},{1,0},{2,3},{3,2},{4,5},{5,4},{6,7},{7,6},{8,9},{9,8},{10,11... | collective-permute-start | bytes 3145736 | tf_op jit(solution)/shard_map/fb_core/ppermute | solution.py:75
  147.1 12.4 %collective-permute-start.29 = (bf16[4,128,1024]{2,1,0:T(8,128)(2,1)S(1)}, bf16[4,128,1024]{2,1,0:T(8,128)(2,1)S(1)}, u32[]{:S(2)}, u32[]{:S(2)}) collective-permute-start(bf16[4,128,1024]{2,1,0:T(8,128)(2,1)S(1)} %fb_high.1.refs_1_), channel_id=1, source_target_pairs={{0,1},{1,0},{2,3},{3,2},{4,5},{5,4},{6,7},{7,6},{8,9},{9,8},{10,11... | collective-permute-start | bytes 3145736 | tf_op jit(solution)/shard_map/fb_core/ppermute | solution.py:75
  147.7 11.9 %collective-permute-start.31 = (bf16[4,128,1024]{2,1,0:T(8,128)(2,1)S(1)}, bf16[4,128,1024]{2,1,0:T(8,128)(2,1)S(1)}, u32[]{:S(2)}, u32[]{:S(2)}) collective-permute-start(bf16[4,128,1024]{2,1,0:T(8,128)(2,1)S(1)} %collective-permute-done.24.refs_3_), channel_id=1, source_target_pairs={{0,1},{1,0},{2,3},{3,2},{4,5},{5,4},{6,7},{7,6},{8,9},{9,8},{10,11... | collective-permute-start | bytes 3145736 | tf_op jit(solution)/shard_map/fb_core/ppermute | solution.py:75
  159.6 2.9 %collective-permute-start.32 = (bf16[4,128,1024]{2,1,0:T(8,128)(2,1)}, bf16[4,128,1024]{2,1,0:T(8,128)(2,1)S(1)}, u32[]{:S(2)}, u32[]{:S(2)}) collective-permute-start(bf16[4,128,1024]{2,1,0:T(8,128)(2,1)} %collective-permute-done.28.refs_4_), channel_id=1, source_target_pairs={{0,1},{1,0},{2,3},{3,2},{4,5},{5,4},{6,7},{7,6},{8,9},{9,8},{10,11... | collective-permute-start | bytes 3145736 | tf_op jit(solution)/shard_map/fb_core/ppermute | solution.py:75
  181.3 16.8 %all-to-all-start.1 = ((bf16[32,16,384]{2,1,0:T(8,128)(2,1)}), bf16[32,16,384]{2,1,0:T(8,128)(2,1)S(1)}, u32[]{:S(2)}, u32[]{:S(2)}) async-start(bf16[32,16,384]{2,1,0:T(8,128)(2,1)} %get-tuple-element.138), calls=%async_computation.1 | async-start | bytes 786432 | tf_op jit(solution)/shard_map/grads_b_send/all_to_all | solution.py:716
  185.0 13.9 %collective-permute-start.33 = (bf16[320,256]{1,0:T(8,128)(2,1)}, bf16[320,256]{1,0:T(8,128)(2,1)S(1)}, u32[]{:S(2)}, u32[]{:S(2)}) collective-permute-start(bf16[320,256]{1,0:T(8,128)(2,1)} %get-tuple-element.135), channel_id=1, source_target_pairs={{0,1},{1,0},{2,3},{3,2},{4,5},{5,4},{6,7},{7,6},{8,9},{9,8},{10,11... | collective-permute-start | bytes 491528 | tf_op jit(solution)/shard_map/layer_out/ppermute | solution.py:75
  185.3 13.6 %collective-permute-start.34 = (bf16[320,256]{1,0:T(8,128)(2,1)}, bf16[320,256]{1,0:T(8,128)(2,1)S(1)}, u32[]{:S(2)}, u32[]{:S(2)}) collective-permute-start(bf16[320,256]{1,0:T(8,128)(2,1)} %get-tuple-element.136), channel_id=1, source_target_pairs={{0,2},{1,3},{2,0},{3,1},{4,6},{5,7},{6,4},{7,5},{8,10},{9,11},{10,... | collective-permute-start | bytes 491528 | tf_op jit(solution)/shard_map/layer_out/ppermute | solution.py:75
  187.0 11.9 %collective-permute-start.35 = (bf16[320,256]{1,0:T(8,128)(2,1)}, bf16[320,256]{1,0:T(8,128)(2,1)S(1)}, u32[]{:S(2)}, u32[]{:S(2)}) collective-permute-start(bf16[320,256]{1,0:T(8,128)(2,1)} %get-tuple-element.137), channel_id=1, source_target_pairs={{0,3},{1,2},{2,1},{3,0},{4,7},{5,6},{6,5},{7,4},{8,11},{9,10},{10,... | collective-permute-start | bytes 491528 | tf_op jit(solution)/shard_map/layer_out/ppermute | solution.py:75
  198.9 7.7 %collective-permute-start.36 = (bf16[128,384]{1,0:T(8,128)(2,1)S(1)}, bf16[128,384]{1,0:T(8,128)(2,1)S(1)}, u32[]{:S(2)}, u32[]{:S(2)}) collective-permute-start(bf16[128,384]{1,0:T(8,128)(2,1)S(1)} %bitcast.43), channel_id=1, source_target_pairs={{0,16},{1,17},{2,18},{3,19},{4,20},{5,21},{6,22},{7,23},{8,24},{9,... | collective-permute-start | bytes 294920 | tf_op jit(solution)/shard_map/grads_b/ppermute | solution.py:75
  201.1 11.5 %all-to-all-start.2 = ((bf16[32,16,128]{2,1,0:T(8,128)(2,1)}), bf16[32,16,128]{2,1,0:T(8,128)(2,1)S(1)}, u32[]{:S(2)}, u32[]{:S(2)}) async-start(bf16[32,16,128]{2,1,0:T(8,128)(2,1)} %get-tuple-element.145), calls=%async_computation.2 | async-start | bytes 262144 | tf_op jit(solution)/shard_map/grads_c_send/all_to_all | solution.py:716
  206.8 13.3 %collective-permute-start.37 = (bf16[2,128,384]{2,1,0:T(8,128)(2,1)S(1)}, bf16[2,128,384]{2,1,0:T(8,128)(2,1)S(1)}, u32[]{:S(2)}, u32[]{:S(2)}) collective-permute-start(bf16[2,128,384]{2,1,0:T(8,128)(2,1)S(1)} %grads_b.7), channel_id=1, source_target_pairs={{0,8},{1,9},{2,10},{3,11},{4,12},{5,13},{6,14},{7,15},{8,0},{9,1},... | collective-permute-start | bytes 589832 | tf_op jit(solution)/shard_map/grads_b/ppermute | solution.py:75
  213.3 6.1 %collective-permute-start.40 = (bf16[128,128]{1,0:T(8,128)(2,1)S(1)}, bf16[128,128]{1,0:T(8,128)(2,1)S(1)}, u32[]{:S(2)}, u32[]{:S(2)}) collective-permute-start(bf16[128,128]{1,0:T(8,128)(2,1)S(1)} %bitcast.46), channel_id=1, source_target_pairs={{0,24},{1,25},{2,26},{3,27},{4,28},{5,29},{6,30},{7,31},{8,16},{9,... | collective-permute-start | bytes 98312 | tf_op jit(solution)/shard_map/grads_b/ppermute | solution.py:75
  214.7 5.1 %collective-permute-start.39 = (bf16[128,128]{1,0:T(8,128)(2,1)S(1)}, bf16[128,128]{1,0:T(8,128)(2,1)S(1)}, u32[]{:S(2)}, u32[]{:S(2)}) collective-permute-start(bf16[128,128]{1,0:T(8,128)(2,1)S(1)} %bitcast.47), channel_id=1, source_target_pairs={{0,16},{1,17},{2,18},{3,19},{4,20},{5,21},{6,22},{7,23},{8,24},{9,... | collective-permute-start | bytes 98312 | tf_op jit(solution)/shard_map/grads_b/ppermute | solution.py:75
  215.4 4.5 %collective-permute-start.38 = (bf16[128,128]{1,0:T(8,128)(2,1)S(1)}, bf16[128,128]{1,0:T(8,128)(2,1)S(1)}, u32[]{:S(2)}, u32[]{:S(2)}) collective-permute-start(bf16[128,128]{1,0:T(8,128)(2,1)S(1)} %bitcast.48), channel_id=1, source_target_pairs={{0,8},{1,9},{2,10},{3,11},{4,12},{5,13},{6,14},{7,15},{8,0},{9,1},... | collective-permute-start | bytes 98312 | tf_op jit(solution)/shard_map/grads_b/ppermute | solution.py:75
  220.9 13.9 %collective-permute-start.42 = (bf16[4,128,512]{2,1,0:T(8,128)(2,1)S(1)}, bf16[4,128,512]{2,1,0:T(8,128)(2,1)S(1)}, u32[]{:S(2)}, u32[]{:S(2)}) collective-permute-start(bf16[4,128,512]{2,1,0:T(8,128)(2,1)S(1)} %grads_b.11.refs_1_), channel_id=1, source_target_pairs={{0,4},{1,3},{2,6},{3,1},{4,0},{5,7},{6,2},{7,5},{8,12},{9,11},{10,... | collective-permute-start | bytes 1572872 | tf_op jit(solution)/shard_map/grads/ppermute | solution.py:75
  221.6 13.2 %collective-permute-start.41 = (bf16[4,128,512]{2,1,0:T(8,128)(2,1)S(1)}, bf16[4,128,512]{2,1,0:T(8,128)(2,1)S(1)}, u32[]{:S(2)}, u32[]{:S(2)}) collective-permute-start(bf16[4,128,512]{2,1,0:T(8,128)(2,1)S(1)} %grads_b.11.refs_1_), channel_id=1, source_target_pairs={{0,2},{1,5},{2,0},{3,7},{4,6},{5,1},{6,4},{7,3},{8,10},{9,13},{10,... | collective-permute-start | bytes 1572872 | tf_op jit(solution)/shard_map/grads/ppermute | solution.py:75
  234.8 9.2 %collective-permute-start.49 = (bf16[4,128,512]{2,1,0:T(8,128)(2,1)S(1)}, bf16[4,128,512]{2,1,0:T(8,128)(2,1)S(1)}, u32[]{:S(2)}, u32[]{:S(2)}) collective-permute-start(bf16[4,128,512]{2,1,0:T(8,128)(2,1)S(1)} %collective-permute-done.41.refs_2_), channel_id=1, source_target_pairs={{0,4},{1,3},{2,6},{3,1},{4,0},{5,7},{6,2},{7,5},{8,12},{9,11},{10,... | collective-permute-start | bytes 1572872 | tf_op jit(solution)/shard_map/grads/ppermute | solution.py:75
  235.1 8.9 %collective-permute-start.43 = (bf16[4,128,512]{2,1,0:T(8,128)(2,1)S(1)}, bf16[4,128,512]{2,1,0:T(8,128)(2,1)S(1)}, u32[]{:S(2)}, u32[]{:S(2)}) collective-permute-start(bf16[4,128,512]{2,1,0:T(8,128)(2,1)S(1)} %grads_b.11.refs_1_), channel_id=1, source_target_pairs={{0,1},{1,0},{2,3},{3,2},{4,5},{5,4},{6,7},{7,6},{8,9},{9,8},{10,11... | collective-permute-start | bytes 1572872 | tf_op jit(solution)/shard_map/grads/ppermute | solution.py:75
  235.1 8.9 %collective-permute-start.45 = (bf16[4,128,512]{2,1,0:T(8,128)(2,1)S(1)}, bf16[4,128,512]{2,1,0:T(8,128)(2,1)S(1)}, u32[]{:S(2)}, u32[]{:S(2)}) collective-permute-start(bf16[4,128,512]{2,1,0:T(8,128)(2,1)S(1)} %collective-permute-done.42.refs_3_), channel_id=1, source_target_pairs={{0,1},{1,0},{2,3},{3,2},{4,5},{5,4},{6,7},{7,6},{8,9},{9,8},{10,11... | collective-permute-start | bytes 1572872 | tf_op jit(solution)/shard_map/grads/ppermute | solution.py:75
  235.6 8.4 %collective-permute-start.44 = (bf16[4,128,512]{2,1,0:T(8,128)(2,1)S(1)}, bf16[4,128,512]{2,1,0:T(8,128)(2,1)S(1)}, u32[]{:S(2)}, u32[]{:S(2)}) collective-permute-start(bf16[4,128,512]{2,1,0:T(8,128)(2,1)S(1)} %collective-permute-done.41.refs_2_), channel_id=1, source_target_pairs={{0,1},{1,0},{2,3},{3,2},{4,5},{5,4},{6,7},{7,6},{8,9},{9,8},{10,11... | collective-permute-start | bytes 1572872 | tf_op jit(solution)/shard_map/grads/ppermute | solution.py:75
  236.5 17.4 %copy-start.12 = (bf16[320,256]{1,0:T(8,128)(2,1)S(1)}, bf16[320,256]{1,0:T(8,128)(2,1)}, u32[]{:S(2)}) copy-start(bf16[320,256]{1,0:T(8,128)(2,1)} %get-tuple-element.171.refs_0_) | copy-start | bytes 491524
  244.0 2.0 collective-permute-start.50
  244.1 9.8 %collective-permute-start.46 = (bf16[320,256]{1,0:T(8,128)(2,1)}, bf16[320,256]{1,0:T(8,128)(2,1)S(1)}, u32[]{:S(2)}, u32[]{:S(2)}) collective-permute-start(bf16[320,256]{1,0:T(8,128)(2,1)} %get-tuple-element.166), channel_id=1, source_target_pairs={{0,1},{1,0},{2,3},{3,2},{4,5},{5,4},{6,7},{7,6},{8,9},{9,8},{10,11... | collective-permute-start | bytes 491528 | tf_op jit(solution)/shard_map/rows_out/ppermute | solution.py:75
  244.7 9.2 %collective-permute-start.47 = (bf16[320,256]{1,0:T(8,128)(2,1)}, bf16[320,256]{1,0:T(8,128)(2,1)S(1)}, u32[]{:S(2)}, u32[]{:S(2)}) collective-permute-start(bf16[320,256]{1,0:T(8,128)(2,1)} %get-tuple-element.167), channel_id=1, source_target_pairs={{0,2},{1,3},{2,0},{3,1},{4,6},{5,7},{6,4},{7,5},{8,10},{9,11},{10,... | collective-permute-start | bytes 491528 | tf_op jit(solution)/shard_map/rows_out/ppermute | solution.py:75
  245.6 8.3 %collective-permute-start.48 = (bf16[320,256]{1,0:T(8,128)(2,1)}, bf16[320,256]{1,0:T(8,128)(2,1)S(1)}, u32[]{:S(2)}, u32[]{:S(2)}) collective-permute-start(bf16[320,256]{1,0:T(8,128)(2,1)} %get-tuple-element.168), channel_id=1, source_target_pairs={{0,3},{1,2},{2,1},{3,0},{4,7},{5,6},{6,5},{7,4},{8,11},{9,10},{10,... | collective-permute-start | bytes 491528 | tf_op jit(solution)/shard_map/rows_out/ppermute | solution.py:75
  (25 other events, 154.7 us)

commit v13 on v12

--- a/solution.py
+++ b/solution.py
@@ -596,7 +596,7 @@
         gv[:, at] = low(mm(low(soft), g_both))
         return 0
 
-    lax.fori_loop(0, H // 2, attend, 0, unroll=4)
+    lax.fori_loop(0, H // 2, attend, 0, unroll=8)
     lat1_t = low(lat1[...].astype(F32).T)
 
     def step(slot, acc):

time: 256 us -> 255 us (level)
  transfers between devices with their start and end apart: 54 -> 54, of which waited for: 22 -> 21; matrix products, arithmetic and copies ran while one was open for 1% -> 1% of each run, Pallas kernels for 25% -> 25%
where the time goes in v13:
time: 255 us; the launch traced here: 254 us
  waiting for transfers between devices  101 us (40%)
  Pallas kernels  86.7 us (34%)
  starting transfers between devices  55.3 us (22%)
  local copies, waits for them, and re-layouts  7.22 us (3%)
  between operations  3.45 us (1%)
    ppermute x51, waiting for transfers between devices, swap(): return lax.ppermute(block, BOTH, pairs)  95.9 us
    pallas_call x19, Pallas kernels, call(): pl.pallas_call(kernel, out_shape=outs, in_specs=[pl.BlockSpec(memory_spac...  86.7 us
    ppermute x51, starting transfers between devices, swap(): return lax.ppermute(block, BOTH, pairs)  44.1 us
    all_to_all x2, starting transfers between devices, send_grads(): return lax.all_to_all(grads, BOTH, split_axis=0, concat_axis=0, tiled=True)  6.81 us
  transfers between devices with their start and end apart: 54, of which 21 were waited for; matrix products, arithmetic and copies ran while one was open for 1% of the time, Pallas kernels for 25%

profile of v13, /device:TPU:0, one launch (start us, length us, event | category | flops | bytes accessed | tf_op | source)
XLA Modules:
  0.0 254.4 jit_solution(17571174437087751222)
XLA Ops:
  0.7 2.7 %shard_map.276 = (bf16[4,656,256]{2,1,0:T(8,128)(2,1)}, bf16[128,1024]{1,0:T(8,128)(2,1)}) custom-call(bf16[4,320,256]{2,1,0:T(8,128)(2,1)} %bitcast.50, bf16[4,320,256]{2,1,0:T(8,128)(2,1)} %bitcast.51, bf16[2,256]{1,0:T(2,128)(2,1)} %bias_qv.1, bf16[1024]{0:T(1024)(128)(2,1)} %bias_f.1, bf16[3,128,256]{2,1,0:T(8,128)(2,1)} %wq.1, bf16[256,128]{1,0:T(8,128)(2,1)} %wp.1), custom_call_target="tpu_custom_call" | custom-call | tf_op jit(solution)/shard_map/pallas_call | solution.py:54
  3.4 4.4 %all-to-all-start = ((bf16[4,656,256]{2,1,0:T(8,128)(2,1)}), bf16[4,656,256]{2,1,0:T(8,128)(2,1)}, u32[]{:S(2)}, u32[]{:S(2)}) async-start(bf16[4,656,256]{2,1,0:T(8,128)(2,1)} %get-tuple-element.99), calls=%async_computation | async-start | bytes 2686976 | tf_op jit(solution)/shard_map/all_to_all | solution.py:815
  7.8 5.1 %collective-permute-start.2 = (bf16[128,1024]{1,0:T(8,128)(2,1)S(1)}, bf16[128,1024]{1,0:T(8,128)(2,1)S(1)}, u32[]{:S(2)}, u32[]{:S(2)}) collective-permute-start(bf16[128,1024]{1,0:T(8,128)(2,1)S(1)} %copy-done.8), channel_id=1, source_target_pairs={{0,24},{1,25},{2,26},{3,27},{4,28},{5,29},{6,30},{7,31},{8,16},{9,... | collective-permute-start | bytes 786440 | tf_op jit(solution)/shard_map/q_high/ppermute | solution.py:75
  13.0 0.6 collective-permute-start
  16.1 0.7 pad_add_fusion.3.sc.refs_0_
  16.9 0.8 shard_map.277
  17.7 0.7 copy-done.6
  18.4 0.7 copy-done.7
  19.0 0.6 dynamic-slice_bitcast_fusion.refs_14_.refs_9_
  20.2 15.6 %collective-permute-done.1.refs_2_ = bf16[128,1024]{1,0:T(8,128)(2,1)S(1)} collective-permute-done((bf16[128,1024]{1,0:T(8,128)(2,1)S(1)}, bf16[128,1024]{1,0:T(8,128)(2,1)S(1)}, u32[]{:S(2)}, u32[]{:S(2)}) %collective-permute-start.1) | collective-permute-done | bytes 262176 | tf_op jit(solution)/shard_map/q_high/ppermute | solution.py:75
  36.0 1.6 collective-permute-start.7
  37.5 1.7 collective-permute-start.6
  39.2 2.5 collective-permute-start.5
  41.7 1.9 collective-permute-start.3
  43.6 6.8 %collective-permute-done.5.refs_3_ = bf16[128,1024]{1,0:T(8,128)(2,1)S(1)} collective-permute-done((bf16[128,1024]{1,0:T(8,128)(2,1)S(1)}, bf16[128,1024]{1,0:T(8,128)(2,1)S(1)}, u32[]{:S(2)}, u32[]{:S(2)}) %collective-permute-start.5) | collective-permute-done | bytes 262176 | tf_op jit(solution)/shard_map/fa_high/ppermute | solution.py:75
  50.4 11.8 %collective-permute-done.4.refs_2_ = bf16[128,1024]{1,0:T(8,128)(2,1)S(1)} collective-permute-done((bf16[128,1024]{1,0:T(8,128)(2,1)S(1)}, bf16[128,1024]{1,0:T(8,128)(2,1)S(1)}, u32[]{:S(2)}, u32[]{:S(2)}) %collective-permute-start.4) | collective-permute-done | bytes 262176 | tf_op jit(solution)/shard_map/fa_high/ppermute | solution.py:75
  62.2 1.2 collective-permute-start.14
  63.9 13.1 %collective-permute-done.14.refs_4_.refs_12_ = bf16[4,128,1024]{2,1,0:T(8,128)(2,1)S(1)} collective-permute-done((bf16[4,128,1024]{2,1,0:T(8,128)(2,1)S(1)}, bf16[4,128,1024]{2,1,0:T(8,128)(2,1)S(1)}, u32[]{:S(2)}, u32[]{:S(2)}) %collective-permute-start.14) | collective-permute-done | bytes 1048608 | tf_op jit(solution)/shard_map/q_both/ppermute | solution.py:75
  77.2 1.2 collective-permute-start.19
  79.1 2.5 collective-permute-start.13
  81.6 1.0 copy-done.21
  82.5 1.9 collective-permute-start.11
  84.5 18.0 %shard_map.278 = (bf16[320,1024]{1,0:T(8,128)(2,1)}, bf16[320,16]{1,0:T(8,128)(2,1)}, bf16[320,1024]{1,0:T(8,128)(2,1)}, bf16[320,1024]{1,0:T(8,128)(2,1)}, bf16...) custom-call(s32[4]{0:T(128)} %copy-done.13, ...), custom_call_target="tpu_custom_call" | custom-call | tf_op jit(solution)/shard_map/pallas_call | solution.py:54
  102.4 0.7 collective-permute-done.12.refs_2_
  103.3 1.2 collective-permute-start.26
  105.2 4.4 %collective-permute-done.16 = s32[4]{0:T(128)S(1)} collective-permute-done((s32[4]{0:T(128)S(1)}, s32[4]{0:T(128)S(1)}, u32[]{:S(2)}, u32[]{:S(2)}) %collective-permute-start.16) | collective-permute-done | bytes 48 | tf_op jit(solution)/shard_map/ppermute | solution.py:75
  110.4 3.4 %collective-permute-done.17 = s32[2,4]{1,0:T(2,128)S(1)} collective-permute-done((s32[2,4]{1,0:T(2,128)S(1)}, s32[2,4]{1,0:T(2,128)S(1)}, u32[]{:S(2)}, u32[]{:S(2)}) %collective-permute-start.17) | collective-permute-done | bytes 64 | tf_op jit(solution)/shard_map/ppermute | solution.py:75
  113.9 4.6 %collective-permute-done.26.refs_4_ = bf16[4,128,1024]{2,1,0:T(8,128)(2,1)} collective-permute-done((bf16[4,128,1024]{2,1,0:T(8,128)(2,1)}, bf16[4,128,1024]{2,1,0:T(8,128)(2,1)}, u32[]{:S(2)}, u32[]{:S(2)}) %collective-permute-start.26) | collective-permute-done | bytes 1048608 | tf_op jit(solution)/shard_map/fa_both/ppermute | solution.py:75
  119.0 1.2 collective-permute-start.24
  120.2 0.7 collective-permute-start.23
  120.9 1.5 collective-permute-start.25
  122.5 15.2 %shard_map.279 = (f32[320,1024]{1,0:T(8,128)}, f32[320,1024]{1,0:T(8,128)}, f32[320,16]{1,0:T(8,128)}, f32[320,16]{1,0:T(8,128)}, bf16[320,1024]{1,0:T(8,128)(2,1)}, /*index=5*/bf16[32,16,128]{2,1,0:T(8,128)(2,1)}) custom-call(s32[4]{0:T(128)} %copy-done.13, bf16[4,128,1024]{2,1,0:T(8,128)(2,1)} %copy-done.3, ...), custom_call_target="tpu_custom_call" | custom-call | tf_op jit(solution)/shard_map/pallas_call | solution.py:54
  137.7 6.9 %collective-permute-done.25 = s32[2,2,4]{2,1,0:T(2,128)S(1)} collective-permute-done((s32[2,2,4]{2,1,0:T(2,128)S(1)}, s32[2,2,4]{2,1,0:T(2,128)S(1)}, u32[]{:S(2)}, u32[]{:S(2)}) %collective-permute-start.25) | collective-permute-done | bytes 96 | tf_op jit(solution)/shard_map/ppermute | solution.py:75
  144.6 1.7 collective-permute-start.28
  147.8 11.8 %collective-permute-done.28.refs_4_ = bf16[4,128,1024]{2,1,0:T(8,128)(2,1)} collective-permute-done((bf16[4,128,1024]{2,1,0:T(8,128)(2,1)S(1)}, bf16[4,128,1024]{2,1,0:T(8,128)(2,1)}, u32[]{:S(2)}, u32[]{:S(2)}) %collective-permute-start.28) | collective-permute-done | bytes 1048608 | tf_op jit(solution)/shard_map/fb_both/ppermute | solution.py:75
  159.6 2.8 %collective-permute-done.32.refs_8_ = bf16[4,128,1024]{2,1,0:T(8,128)(2,1)S(1)} collective-permute-done((bf16[4,128,1024]{2,1,0:T(8,128)(2,1)}, bf16[4,128,1024]{2,1,0:T(8,128)(2,1)S(1)}, u32[]{:S(2)}, u32[]{:S(2)}) %collective-permute-start.32) | collective-permute-done | bytes 1048608 | tf_op jit(solution)/shard_map/fb_core/ppermute | solution.py:75
  162.5 1.0 copy-done.26
  163.4 17.9 %shard_map.280 = (bf16[320,256]{1,0:T(8,128)(2,1)}, bf16[320,256]{1,0:T(8,128)(2,1)}, bf16[320,256]{1,0:T(8,128)(2,1)}, bf16[320,256]{1,0:T(8,128)(2,1)}, bf16[3...) custom-call(s32[4]{0:T(128)} %copy-done.13, bf16[4,128,1024]{2,1,0:T(8,128)(2,1)} %copy-done.4, ...), custom_call_target="tpu_custom_call" | custom-call | tf_op jit(solution)/shard_map/pallas_call | solution.py:54
  181.3 3.8 %all-to-all-start.1 = ((bf16[32,16,384]{2,1,0:T(8,128)(2,1)}), bf16[32,16,384]{2,1,0:T(8,128)(2,1)S(1)}, u32[]{:S(2)}, u32[]{:S(2)}) async-start(bf16[32,16,384]{2,1,0:T(8,128)(2,1)} %get-tuple-element.138), calls=%async_computation.1 | async-start | bytes 786432 | tf_op jit(solution)/shard_map/grads_b_send/all_to_all | solution.py:716
  185.3 1.7 collective-permute-start.34
  187.1 9.9 %shard_map.281 = (bf16[320,1024]{1,0:T(8,128)(2,1)}, bf16[320,1024]{1,0:T(8,128)(2,1)}, bf16[320,1024]{1,0:T(8,128)(2,1)}, bf16[320,16]{1,0:T(8,128)(2,1)}, bf16[32,16,128]{2,1,0:T(8,128)(2,1)}) custom-call(s32[4]{0:T(128)} %copy-done.13, f32[320,1]{1,0:T(8,128)} %copy-done.7, bf16[320,1024]{1,0:T(8,128)(2,1)} %get-tuple-element.139.refs_2_, ...), custom_call_target="tpu_custom_call" | custom-call | tf_op jit(solution)/shard_map/pallas_call | solution.py:54
  197.0 1.1 all-to-all-done.1.mine
  198.1 0.7 grads_b.6
  198.9 2.2 collective-permute-start.36
  201.1 3.0 %all-to-all-start.2 = ((bf16[32,16,128]{2,1,0:T(8,128)(2,1)}), bf16[32,16,128]{2,1,0:T(8,128)(2,1)S(1)}, u32[]{:S(2)}, u32[]{:S(2)}) async-start(bf16[32,16,128]{2,1,0:T(8,128)(2,1)} %get-tuple-element.145), calls=%async_computation.2 | async-start | bytes 262144 | tf_op jit(solution)/shard_map/grads_c_send/all_to_all | solution.py:716
  204.1 2.5 collective-permute-done.36.refs_1_
  206.9 1.6 collective-permute-start.37
  208.5 3.8 %all-to-all-done.2.mine = bf16[32,16,128]{2,1,0:T(8,128)(2,1)S(1)} async-done(((bf16[32,16,128]{2,1,0:T(8,128)(2,1)}), bf16[32,16,128]{2,1,0:T(8,128)(2,1)S(1)}, u32[]{:S(2)}, u32[]{:S(2)}) %all-to-all-start.2) | async-done | bytes 131104 | tf_op jit(solution)/shard_map/grads_c_send/all_to_all | solution.py:716
  212.3 0.7 grads_b.9
  213.0 1.5 collective-permute-start.40
  214.5 0.7 collective-permute-start.39
  215.2 2.3 collective-permute-start.38
  217.4 1.6 collective-permute-done.40.refs_3_
  219.1 0.6 collective-permute-done.39.refs_2_
  220.6 0.7 collective-permute-start.42
  221.3 1.0 collective-permute-start.41
  222.3 10.7 %shard_map.282 = (bf16[320,256]{1,0:T(8,128)(2,1)}, bf16[320,256]{1,0:T(8,128)(2,1)}, bf16[320,256]{1,0:T(8,128)(2,1)}, bf16[320,256]{1,0:T(8,128)(2,1)}) custom-call(s32[4]{0:T(128)} %copy-done.13, bf16[4,128,1024]{2,1,0:T(8,128)(2,1)} %copy-done.2, bf16[4,128,1024]{2,1,0:T(8,128)(2,1)} %copy-done.16, bf16[4,128,1024]{2,1,0:T(8,128)(2,1)} %copy-done.15, ...), custom_call_target="tpu_custom_call" | custom-call | tf_op jit(solution)/shard_map/pallas_call | solution.py:54
  233.0 1.2 collective-permute-done.42.refs_3_
  235.3 0.9 grads.2
  236.2 7.2 %collective-permute-done.49.refs_4_ = bf16[4,128,512]{2,1,0:T(8,128)(2,1)S(1)} collective-permute-done((bf16[4,128,512]{2,1,0:T(8,128)(2,1)S(1)}, bf16[4,128,512]{2,1,0:T(8,128)(2,1)S(1)}, u32[]{:S(2)}, u32[]{:S(2)}) %collective-permute-start.49) | collective-permute-done | bytes 524320 | tf_op jit(solution)/shard_map/grads/ppermute | solution.py:75
  244.0 1.4 collective-permute-start.47
  245.5 0.8 copy-done.33
  246.3 6.9 %grads.3 = (f32[128,4096]{1,0:T(8,128)}, f32[128,4096]{1,0:T(8,128)}, f32[128,1024]{1,0:T(8,128)}, f32[128,1024]{1,0:T(8,128)}, f32[128,1024]{1,0:T(8,128)}, /*i...) custom-call(s32[4]{0:T(128)} %copy-done.13, bf16[4,128,512]{2,1,0:T(8,128)(2,1)} %copy-done.5, ...), custom_call_target="tpu_custom_call" | custom-call | tf_op jit(solution)/shard_map/grads/pallas_call | solution.py:54
  253.3 0.9 rows_out.1
  (150 shorter events, 9.5 us)
Async XLA Ops:
  0.6 18.4 %copy-start = (bf16[8,16,3,1024]{3,1,2,0:T(8,128)(2,1)S(1)}, bf16[8,16,3,1024]{3,1,2,0:T(8,128)(2,1)}, u32[]{:S(2)}) copy-start(bf16[8,16,3,1024]{3,1,2,0:T(8,128)(2,1)} %param.35) | copy-start | bytes 2359300
  3.4 32.6 %all-to-all-start = ((bf16[4,656,256]{2,1,0:T(8,128)(2,1)}), bf16[4,656,256]{2,1,0:T(8,128)(2,1)}, u32[]{:S(2)}, u32[]{:S(2)}) async-start(bf16[4,656,256]{2,1,0:T(8,128)(2,1)} %get-tuple-element.99), calls=%async_computation | async-start | bytes 2686976 | tf_op jit(solution)/shard_map/all_to_all | solution.py:815
  7.8 12.4 %collective-permute-start.2 = (bf16[128,1024]{1,0:T(8,128)(2,1)S(1)}, bf16[128,1024]{1,0:T(8,128)(2,1)S(1)}, u32[]{:S(2)}, u32[]{:S(2)}) collective-permute-start(bf16[128,1024]{1,0:T(8,128)(2,1)S(1)} %copy-done.8), channel_id=1, source_target_pairs={{0,24},{1,25},{2,26},{3,27},{4,28},{5,29},{6,30},{7,31},{8,16},{9,... | collective-permute-start | bytes 786440 | tf_op jit(solution)/shard_map/q_high/ppermute | solution.py:75
  13.0 22.8 %collective-permute-start.1 = (bf16[128,1024]{1,0:T(8,128)(2,1)S(1)}, bf16[128,1024]{1,0:T(8,128)(2,1)S(1)}, u32[]{:S(2)}, u32[]{:S(2)}) collective-permute-start(bf16[128,1024]{1,0:T(8,128)(2,1)S(1)} %copy-done.8), channel_id=1, source_target_pairs={{0,16},{1,17},{2,18},{3,19},{4,20},{5,21},{6,22},{7,23},{8,24},{9,... | collective-permute-start | bytes 786440 | tf_op jit(solution)/shard_map/q_high/ppermute | solution.py:75
  13.0 22.8 %collective-permute-start = (bf16[128,1024]{1,0:T(8,128)(2,1)S(1)}, bf16[128,1024]{1,0:T(8,128)(2,1)S(1)}, u32[]{:S(2)}, u32[]{:S(2)}) collective-permute-start(bf16[128,1024]{1,0:T(8,128)(2,1)S(1)} %copy-done.8), channel_id=1, source_target_pairs={{0,8},{1,9},{2,10},{3,11},{4,12},{5,13},{6,14},{7,15},{8,0},{9,1},... | collective-permute-start | bytes 786440 | tf_op jit(solution)/shard_map/q_high/ppermute | solution.py:75
  16.9 19.1 %copy-start.13 = (s32[4]{0:T(128)}, s32[4]{0:T(128)S(1)}, u32[]{:S(2)}) copy-start(s32[4]{0:T(128)S(1)} %pad_add_fusion.3.sc.refs_0_) | copy-start | bytes 52
  35.9 48.5 %copy-start.2 = (bf16[4,128,1024]{2,1,0:T(8,128)(2,1)}, bf16[4,128,1024]{2,1,0:T(8,128)(2,1)S(1)}, u32[]{:S(2)}) copy-start(bf16[4,128,1024]{2,1,0:T(8,128)(2,1)S(1)} %q_high.1.refs_1_.refs_9_) | copy-start | bytes 3145732
  36.0 26.2 %collective-permute-start.7 = (bf16[4,128,1024]{2,1,0:T(8,128)(2,1)S(1)}, bf16[4,128,1024]{2,1,0:T(8,128)(2,1)S(1)}, u32[]{:S(2)}, u32[]{:S(2)}) collective-permute-start(bf16[4,128,1024]{2,1,0:T(8,128)(2,1)S(1)} %q_high.1.refs_1_.refs_9_), channel_id=1, source_target_pairs={{0,4},{1,3},{2,6},{3,1},{4,0},{5,7},{6,2},{7,5},{8,12},{9,11},{10,... | collective-permute-start | bytes 3145736 | tf_op jit(solution)/shard_map/q_two/ppermute | solution.py:75
  37.5 24.6 %collective-permute-start.6 = (bf16[4,128,1024]{2,1,0:T(8,128)(2,1)S(1)}, bf16[4,128,1024]{2,1,0:T(8,128)(2,1)S(1)}, u32[]{:S(2)}, u32[]{:S(2)}) collective-permute-start(bf16[4,128,1024]{2,1,0:T(8,128)(2,1)S(1)} %q_high.1.refs_1_.refs_9_), channel_id=1, source_target_pairs={{0,2},{1,5},{2,0},{3,7},{4,6},{5,1},{6,4},{7,3},{8,10},{9,13},{10,... | collective-permute-start | bytes 3145736 | tf_op jit(solution)/shard_map/q_one/ppermute | solution.py:75
  39.2 11.1 %collective-permute-start.5 = (bf16[128,1024]{1,0:T(8,128)(2,1)S(1)}, bf16[128,1024]{1,0:T(8,128)(2,1)S(1)}, u32[]{:S(2)}, u32[]{:S(2)}) collective-permute-start(bf16[128,1024]{1,0:T(8,128)(2,1)S(1)} %get-tuple-element.102.refs_0_), channel_id=1, source_target_pairs={{0,24},{1,25},{2,26},{3,27},{4,28},{5,29},{6,30},{7,31},{8,16},{9,... | collective-permute-start | bytes 786440 | tf_op jit(solution)/shard_map/fa_high/ppermute | solution.py:75
  41.7 20.4 %collective-permute-start.4 = (bf16[128,1024]{1,0:T(8,128)(2,1)S(1)}, bf16[128,1024]{1,0:T(8,128)(2,1)S(1)}, u32[]{:S(2)}, u32[]{:S(2)}) collective-permute-start(bf16[128,1024]{1,0:T(8,128)(2,1)S(1)} %get-tuple-element.102.refs_0_), channel_id=1, source_target_pairs={{0,16},{1,17},{2,18},{3,19},{4,20},{5,21},{6,22},{7,23},{8,24},{9,... | collective-permute-start | bytes 786440 | tf_op jit(solution)/shard_map/fa_high/ppermute | solution.py:75
  41.7 20.4 %collective-permute-start.3 = (bf16[128,1024]{1,0:T(8,128)(2,1)S(1)}, bf16[128,1024]{1,0:T(8,128)(2,1)S(1)}, u32[]{:S(2)}, u32[]{:S(2)}) collective-permute-start(bf16[128,1024]{1,0:T(8,128)(2,1)S(1)} %get-tuple-element.102.refs_0_), channel_id=1, source_target_pairs={{0,8},{1,9},{2,10},{3,11},{4,12},{5,13},{6,14},{7,15},{8,0},{9,1},... | collective-permute-start | bytes 786440 | tf_op jit(solution)/shard_map/fa_high/ppermute | solution.py:75
  62.1 22.3 %copy-start.15 = (bf16[4,128,1024]{2,1,0:T(8,128)(2,1)}, bf16[4,128,1024]{2,1,0:T(8,128)(2,1)S(1)}, u32[]{:S(2)}) copy-start(bf16[4,128,1024]{2,1,0:T(8,128)(2,1)S(1)} %collective-permute-done.7.refs_3_.refs_11_) | copy-start | bytes 3145732
  62.2 22.3 %copy-start.16 = (bf16[4,128,1024]{2,1,0:T(8,128)(2,1)}, bf16[4,128,1024]{2,1,0:T(8,128)(2,1)S(1)}, u32[]{:S(2)}) copy-start(bf16[4,128,1024]{2,1,0:T(8,128)(2,1)S(1)} %collective-permute-done.6.refs_2_.refs_10_) | copy-start | bytes 3145732
  62.2 14.9 %collective-permute-start.14 = (bf16[4,128,1024]{2,1,0:T(8,128)(2,1)S(1)}, bf16[4,128,1024]{2,1,0:T(8,128)(2,1)S(1)}, u32[]{:S(2)}, u32[]{:S(2)}) collective-permute-start(bf16[4,128,1024]{2,1,0:T(8,128)(2,1)S(1)} %collective-permute-done.6.refs_2_.refs_10_), channel_id=1, source_target_pairs={{0,4},{1,3},{2,6},{3,1},{4,0},{5,7},{6,2},{7,5},{8,12},{9,11},{10,... | collective-permute-start | bytes 3145736 | tf_op jit(solution)/shard_map/q_both/ppermute | solution.py:75
  63.4 13.8 %collective-permute-start.8 = (bf16[4,128,1024]{2,1,0:T(8,128)(2,1)S(1)}, bf16[4,128,1024]{2,1,0:T(8,128)(2,1)S(1)}, u32[]{:S(2)}, u32[]{:S(2)}) collective-permute-start(bf16[4,128,1024]{2,1,0:T(8,128)(2,1)S(1)} %q_high.1.refs_1_.refs_9_), channel_id=1, source_target_pairs={{0,1},{1,0},{2,3},{3,2},{4,5},{5,4},{6,7},{7,6},{8,9},{9,8},{10,11... | collective-permute-start | bytes 3145736 | tf_op jit(solution)/shard_map/q_core/ppermute | solution.py:75
  63.4 13.8 %collective-permute-start.10 = (bf16[4,128,1024]{2,1,0:T(8,128)(2,1)S(1)}, bf16[4,128,1024]{2,1,0:T(8,128)(2,1)S(1)}, u32[]{:S(2)}, u32[]{:S(2)}) collective-permute-start(bf16[4,128,1024]{2,1,0:T(8,128)(2,1)S(1)} %collective-permute-done.7.refs_3_.refs_11_), channel_id=1, source_target_pairs={{0,1},{1,0},{2,3},{3,2},{4,5},{5,4},{6,7},{7,6},{8,9},{9,8},{10,11... | collective-permute-start | bytes 3145736 | tf_op jit(solution)/shard_map/q_core/ppermute | solution.py:75
  63.9 13.3 %collective-permute-start.9 = (bf16[4,128,1024]{2,1,0:T(8,128)(2,1)S(1)}, bf16[4,128,1024]{2,1,0:T(8,128)(2,1)S(1)}, u32[]{:S(2)}, u32[]{:S(2)}) collective-permute-start(bf16[4,128,1024]{2,1,0:T(8,128)(2,1)S(1)} %collective-permute-done.6.refs_2_.refs_10_), channel_id=1, source_target_pairs={{0,1},{1,0},{2,3},{3,2},{4,5},{5,4},{6,7},{7,6},{8,9},{9,8},{10,11... | collective-permute-start | bytes 3145736 | tf_op jit(solution)/shard_map/q_core/ppermute | solution.py:75
  77.0 4.5 %collective-permute-start.15 = (bf16[4,128,1024]{2,1,0:T(8,128)(2,1)S(1)}, bf16[4,128,1024]{2,1,0:T(8,128)(2,1)S(1)}, u32[]{:S(2)}, u32[]{:S(2)}) collective-permute-start(bf16[4,128,1024]{2,1,0:T(8,128)(2,1)S(1)} %collective-permute-done.14.refs_4_.refs_12_), channel_id=1, source_target_pairs={{0,1},{1,0},{2,3},{3,2},{4,5},{5,4},{6,7},{7,6},{8,9},{9,8},{10,11... | collective-permute-start | bytes 3145736 | tf_op jit(solution)/shard_map/q_core/ppermute | solution.py:75
  77.2 27.3 %copy-start.3 = (bf16[4,128,1024]{2,1,0:T(8,128)(2,1)}, bf16[4,128,1024]{2,1,0:T(8,128)(2,1)S(1)}, u32[]{:S(2)}) copy-start(bf16[4,128,1024]{2,1,0:T(8,128)(2,1)S(1)} %fa_high.1.refs_1_) | copy-start | bytes 3145732
  77.2 26.1 %collective-permute-start.19 = (bf16[4,128,1024]{2,1,0:T(8,128)(2,1)S(1)}, bf16[4,128,1024]{2,1,0:T(8,128)(2,1)}, u32[]{:S(2)}, u32[]{:S(2)}) collective-permute-start(bf16[4,128,1024]{2,1,0:T(8,128)(2,1)S(1)} %fa_high.1.refs_1_), channel_id=1, source_target_pairs={{0,4},{1,3},{2,6},{3,1},{4,0},{5,7},{6,2},{7,5},{8,12},{9,11},{10,... | collective-permute-start | bytes 3145736 | tf_op jit(solution)/shard_map/fa_two/ppermute | solution.py:75
  78.5 24.8 %collective-permute-start.18 = (bf16[4,128,1024]{2,1,0:T(8,128)(2,1)S(1)}, bf16[4,128,1024]{2,1,0:T(8,128)(2,1)}, u32[]{:S(2)}, u32[]{:S(2)}) collective-permute-start(bf16[4,128,1024]{2,1,0:T(8,128)(2,1)S(1)} %fa_high.1.refs_1_), channel_id=1, source_target_pairs={{0,2},{1,5},{2,0},{3,7},{4,6},{5,1},{6,4},{7,3},{8,10},{9,13},{10,... | collective-permute-start | bytes 3145736 | tf_op jit(solution)/shard_map/fa_one/ppermute | solution.py:75
  79.1 23.4 %collective-permute-start.13 = (bf16[128,1024]{1,0:T(8,128)(2,1)S(1)}, bf16[128,1024]{1,0:T(8,128)(2,1)S(1)}, u32[]{:S(2)}, u32[]{:S(2)}) collective-permute-start(bf16[128,1024]{1,0:T(8,128)(2,1)S(1)} %get-tuple-element.108.refs_0_), channel_id=1, source_target_pairs={{0,24},{1,25},{2,26},{3,27},{4,28},{5,29},{6,30},{7,31},{8,16},{9,... | collective-permute-start | bytes 786440 | tf_op jit(solution)/shard_map/fb_high/ppermute | solution.py:75
  81.5 21.6 %collective-permute-start.12 = (bf16[128,1024]{1,0:T(8,128)(2,1)S(1)}, bf16[128,1024]{1,0:T(8,128)(2,1)S(1)}, u32[]{:S(2)}, u32[]{:S(2)}) collective-permute-start(bf16[128,1024]{1,0:T(8,128)(2,1)S(1)} %get-tuple-element.108.refs_0_), channel_id=1, source_target_pairs={{0,16},{1,17},{2,18},{3,19},{4,20},{5,21},{6,22},{7,23},{8,24},{9,... | collective-permute-start | bytes 786440 | tf_op jit(solution)/shard_map/fb_high/ppermute | solution.py:75
  82.5 20.6 %collective-permute-start.11 = (bf16[128,1024]{1,0:T(8,128)(2,1)S(1)}, bf16[128,1024]{1,0:T(8,128)(2,1)S(1)}, u32[]{:S(2)}, u32[]{:S(2)}) collective-permute-start(bf16[128,1024]{1,0:T(8,128)(2,1)S(1)} %get-tuple-element.108.refs_0_), channel_id=1, source_target_pairs={{0,8},{1,9},{2,10},{3,11},{4,12},{5,13},{6,14},{7,15},{8,0},{9,1},... | collective-permute-start | bytes 786440 | tf_op jit(solution)/shard_map/fb_high/ppermute | solution.py:75
  103.3 15.1 %collective-permute-start.26 = (bf16[4,128,1024]{2,1,0:T(8,128)(2,1)}, bf16[4,128,1024]{2,1,0:T(8,128)(2,1)}, u32[]{:S(2)}, u32[]{:S(2)}) collective-permute-start(bf16[4,128,1024]{2,1,0:T(8,128)(2,1)} %collective-permute-done.18.refs_2_), channel_id=1, source_target_pairs={{0,4},{1,3},{2,6},{3,1},{4,0},{5,7},{6,2},{7,5},{8,12},{9,11},{10,... | collective-permute-start | bytes 3145736 | tf_op jit(solution)/shard_map/fa_both/ppermute | solution.py:75
  104.5 14.5 %collective-permute-start.20 = (bf16[4,128,1024]{2,1,0:T(8,128)(2,1)S(1)}, bf16[4,128,1024]{2,1,0:T(8,128)(2,1)}, u32[]{:S(2)}, u32[]{:S(2)}) collective-permute-start(bf16[4,128,1024]{2,1,0:T(8,128)(2,1)S(1)} %fa_high.1.refs_1_), channel_id=1, source_target_pairs={{0,1},{1,0},{2,3},{3,2},{4,5},{5,4},{6,7},{7,6},{8,9},{9,8},{10,11... | collective-permute-start | bytes 3145736 | tf_op jit(solution)/shard_map/fa_core/ppermute | solution.py:75
  104.5 14.5 %collective-permute-start.22 = (bf16[4,128,1024]{2,1,0:T(8,128)(2,1)}, bf16[4,128,1024]{2,1,0:T(8,128)(2,1)}, u32[]{:S(2)}, u32[]{:S(2)}) collective-permute-start(bf16[4,128,1024]{2,1,0:T(8,128)(2,1)} %collective-permute-done.19.refs_3_), channel_id=1, source_target_pairs={{0,1},{1,0},{2,3},{3,2},{4,5},{5,4},{6,7},{7,6},{8,9},{9,8},{10,11... | collective-permute-start | bytes 3145736 | tf_op jit(solution)/shard_map/fa_core/ppermute | solution.py:75
  105.0 14.0 %collective-permute-start.21 = (bf16[4,128,1024]{2,1,0:T(8,128)(2,1)}, bf16[4,128,1024]{2,1,0:T(8,128)(2,1)}, u32[]{:S(2)}, u32[]{:S(2)}) collective-permute-start(bf16[4,128,1024]{2,1,0:T(8,128)(2,1)} %collective-permute-done.18.refs_2_), channel_id=1, source_target_pairs={{0,1},{1,0},{2,3},{3,2},{4,5},{5,4},{6,7},{7,6},{8,9},{9,8},{10,11... | collective-permute-start | bytes 3145736 | tf_op jit(solution)/shard_map/fa_core/ppermute | solution.py:75
  105.1 42.0 %copy-start.4 = (bf16[4,128,1024]{2,1,0:T(8,128)(2,1)}, bf16[4,128,1024]{2,1,0:T(8,128)(2,1)S(1)}, u32[]{:S(2)}) copy-start(bf16[4,128,1024]{2,1,0:T(8,128)(2,1)S(1)} %fb_high.1.refs_1_) | copy-start | bytes 3145732
  105.2 4.5 %collective-permute-start.16 = (s32[4]{0:T(128)S(1)}, s32[4]{0:T(128)S(1)}, u32[]{:S(2)}, u32[]{:S(2)}) collective-permute-start(s32[4]{0:T(128)S(1)} %copy-done.34), channel_id=1, source_target_pairs={{0,16},{1,17},{2,18},{3,19},{4,20},{5,21},{6,22},{7,23},{8,24},{9,... | collective-permute-start | bytes 56 | tf_op jit(solution)/shard_map/ppermute | solution.py:75
  110.2 3.6 %collective-permute-start.17 = (s32[2,4]{1,0:T(2,128)S(1)}, s32[2,4]{1,0:T(2,128)S(1)}, u32[]{:S(2)}, u32[]{:S(2)}) collective-permute-start(s32[2,4]{1,0:T(2,128)S(1)} %gather_fusion), channel_id=1, source_target_pairs={{0,8},{1,9},{2,10},{3,11},{4,12},{5,13},{6,14},{7,15},{8,0},{9,1},... | collective-permute-start | bytes 104 | tf_op jit(solution)/shard_map/ppermute | solution.py:75
  118.4 4.1 %collective-permute-start.27 = (bf16[4,128,1024]{2,1,0:T(8,128)(2,1)}, bf16[4,128,1024]{2,1,0:T(8,128)(2,1)}, u32[]{:S(2)}, u32[]{:S(2)}) collective-permute-start(bf16[4,128,1024]{2,1,0:T(8,128)(2,1)} %collective-permute-done.26.refs_4_), channel_id=1, source_target_pairs={{0,1},{1,0},{2,3},{3,2},{4,5},{5,4},{6,7},{7,6},{8,9},{9,8},{10,11... | collective-permute-start | bytes 3145736 | tf_op jit(solution)/shard_map/fa_core/ppermute | solution.py:75
  119.0 25.6 %collective-permute-start.24 = (bf16[4,128,1024]{2,1,0:T(8,128)(2,1)S(1)}, bf16[4,128,1024]{2,1,0:T(8,128)(2,1)S(1)}, u32[]{:S(2)}, u32[]{:S(2)}) collective-permute-start(bf16[4,128,1024]{2,1,0:T(8,128)(2,1)S(1)} %fb_high.1.refs_1_), channel_id=1, source_target_pairs={{0,4},{1,3},{2,6},{3,1},{4,0},{5,7},{6,2},{7,5},{8,12},{9,11},{10,... | collective-permute-start | bytes 3145736 | tf_op jit(solution)/shard_map/fb_two/ppermute | solution.py:75
  120.2 24.4 %collective-permute-start.23 = (bf16[4,128,1024]{2,1,0:T(8,128)(2,1)S(1)}, bf16[4,128,1024]{2,1,0:T(8,128)(2,1)S(1)}, u32[]{:S(2)}, u32[]{:S(2)}) collective-permute-start(bf16[4,128,1024]{2,1,0:T(8,128)(2,1)S(1)} %fb_high.1.refs_1_), channel_id=1, source_target_pairs={{0,2},{1,5},{2,0},{3,7},{4,6},{5,1},{6,4},{7,3},{8,10},{9,13},{10,... | collective-permute-start | bytes 3145736 | tf_op jit(solution)/shard_map/fb_one/ppermute | solution.py:75
  120.9 23.6 %collective-permute-start.25 = (s32[2,2,4]{2,1,0:T(2,128)S(1)}, s32[2,2,4]{2,1,0:T(2,128)S(1)}, u32[]{:S(2)}, u32[]{:S(2)}) collective-permute-start(s32[2,2,4]{2,1,0:T(2,128)S(1)} %gather_fusion.1), channel_id=1, source_target_pairs={{0,4},{1,5},{2,6},{3,7},{4,0},{5,1},{6,2},{7,3},{8,12},{9,13},{10,... | collective-permute-start | bytes 200 | tf_op jit(solution)/shard_map/ppermute | solution.py:75
  144.6 17.9 %copy-start.22 = (bf16[4,128,1024]{2,1,0:T(8,128)(2,1)}, bf16[4,128,1024]{2,1,0:T(8,128)(2,1)S(1)}, u32[]{:S(2)}) copy-start(bf16[4,128,1024]{2,1,0:T(8,128)(2,1)S(1)} %collective-permute-done.24.refs_3_) | copy-start | bytes 3145732
  144.6 17.8 %copy-start.23 = (bf16[4,128,1024]{2,1,0:T(8,128)(2,1)}, bf16[4,128,1024]{2,1,0:T(8,128)(2,1)S(1)}, u32[]{:S(2)}) copy-start(bf16[4,128,1024]{2,1,0:T(8,128)(2,1)S(1)} %collective-permute-done.23.refs_2_) | copy-start | bytes 3145732
  144.6 14.9 %collective-permute-start.28 = (bf16[4,128,1024]{2,1,0:T(8,128)(2,1)S(1)}, bf16[4,128,1024]{2,1,0:T(8,128)(2,1)}, u32[]{:S(2)}, u32[]{:S(2)}) collective-permute-start(bf16[4,128,1024]{2,1,0:T(8,128)(2,1)S(1)} %collective-permute-done.23.refs_2_), channel_id=1, source_target_pairs={{0,4},{1,3},{2,6},{3,1},{4,0},{5,7},{6,2},{7,5},{8,12},{9,11},{10,... | collective-permute-start | bytes 3145736 | tf_op jit(solution)/shard_map/fb_both/ppermute | solution.py:75
  146.4 13.2 %collective-permute-start.30 = (bf16[4,128,1024]{2,1,0:T(8,128)(2,1)S(1)}, bf16[4,128,1024]{2,1,0:T(8,128)(2,1)}, u32[]{:S(2)}, u32[]{:S(2)}) collective-permute-start(bf16[4,128,1024]{2,1,0:T(8,128)(2,1)S(1)} %collective-permute-done.23.refs_2_), channel_id=1, source_target_pairs={{0,1},{1,0},{2,3},{3,2},{4,5},{5,4},{6,7},{7,6},{8,9},{9,8},{10,11... | collective-permute-start | bytes 3145736 | tf_op jit(solution)/shard_map/fb_core/ppermute | solution.py:75
  147.1 12.4 %collective-permute-start.29 = (bf16[4,128,1024]{2,1,0:T(8,128)(2,1)S(1)}, bf16[4,128,1024]{2,1,0:T(8,128)(2,1)S(1)}, u32[]{:S(2)}, u32[]{:S(2)}) collective-permute-start(bf16[4,128,1024]{2,1,0:T(8,128)(2,1)S(1)} %fb_high.1.refs_1_), channel_id=1, source_target_pairs={{0,1},{1,0},{2,3},{3,2},{4,5},{5,4},{6,7},{7,6},{8,9},{9,8},{10,11... | collective-permute-start | bytes 3145736 | tf_op jit(solution)/shard_map/fb_core/ppermute | solution.py:75
  147.7 11.9 %collective-permute-start.31 = (bf16[4,128,1024]{2,1,0:T(8,128)(2,1)S(1)}, bf16[4,128,1024]{2,1,0:T(8,128)(2,1)S(1)}, u32[]{:S(2)}, u32[]{:S(2)}) collective-permute-start(bf16[4,128,1024]{2,1,0:T(8,128)(2,1)S(1)} %collective-permute-done.24.refs_3_), channel_id=1, source_target_pairs={{0,1},{1,0},{2,3},{3,2},{4,5},{5,4},{6,7},{7,6},{8,9},{9,8},{10,11... | collective-permute-start | bytes 3145736 | tf_op jit(solution)/shard_map/fb_core/ppermute | solution.py:75
  159.6 2.9 %collective-permute-start.32 = (bf16[4,128,1024]{2,1,0:T(8,128)(2,1)}, bf16[4,128,1024]{2,1,0:T(8,128)(2,1)S(1)}, u32[]{:S(2)}, u32[]{:S(2)}) collective-permute-start(bf16[4,128,1024]{2,1,0:T(8,128)(2,1)} %collective-permute-done.28.refs_4_), channel_id=1, source_target_pairs={{0,1},{1,0},{2,3},{3,2},{4,5},{5,4},{6,7},{7,6},{8,9},{9,8},{10,11... | collective-permute-start | bytes 3145736 | tf_op jit(solution)/shard_map/fb_core/ppermute | solution.py:75
  181.3 16.8 %all-to-all-start.1 = ((bf16[32,16,384]{2,1,0:T(8,128)(2,1)}), bf16[32,16,384]{2,1,0:T(8,128)(2,1)S(1)}, u32[]{:S(2)}, u32[]{:S(2)}) async-start(bf16[32,16,384]{2,1,0:T(8,128)(2,1)} %get-tuple-element.138), calls=%async_computation.1 | async-start | bytes 786432 | tf_op jit(solution)/shard_map/grads_b_send/all_to_all | solution.py:716
  185.2 13.7 %collective-permute-start.33 = (bf16[320,256]{1,0:T(8,128)(2,1)}, bf16[320,256]{1,0:T(8,128)(2,1)S(1)}, u32[]{:S(2)}, u32[]{:S(2)}) collective-permute-start(bf16[320,256]{1,0:T(8,128)(2,1)} %get-tuple-element.135), channel_id=1, source_target_pairs={{0,1},{1,0},{2,3},{3,2},{4,5},{5,4},{6,7},{7,6},{8,9},{9,8},{10,11... | collective-permute-start | bytes 491528 | tf_op jit(solution)/shard_map/layer_out/ppermute | solution.py:75
  185.3 13.6 %collective-permute-start.34 = (bf16[320,256]{1,0:T(8,128)(2,1)}, bf16[320,256]{1,0:T(8,128)(2,1)S(1)}, u32[]{:S(2)}, u32[]{:S(2)}) collective-permute-start(bf16[320,256]{1,0:T(8,128)(2,1)} %get-tuple-element.136), channel_id=1, source_target_pairs={{0,2},{1,3},{2,0},{3,1},{4,6},{5,7},{6,4},{7,5},{8,10},{9,11},{10,... | collective-permute-start | bytes 491528 | tf_op jit(solution)/shard_map/layer_out/ppermute | solution.py:75
  187.0 11.9 %collective-permute-start.35 = (bf16[320,256]{1,0:T(8,128)(2,1)}, bf16[320,256]{1,0:T(8,128)(2,1)S(1)}, u32[]{:S(2)}, u32[]{:S(2)}) collective-permute-start(bf16[320,256]{1,0:T(8,128)(2,1)} %get-tuple-element.137), channel_id=1, source_target_pairs={{0,3},{1,2},{2,1},{3,0},{4,7},{5,6},{6,5},{7,4},{8,11},{9,10},{10,... | collective-permute-start | bytes 491528 | tf_op jit(solution)/shard_map/layer_out/ppermute | solution.py:75
  198.9 7.7 %collective-permute-start.36 = (bf16[128,384]{1,0:T(8,128)(2,1)S(1)}, bf16[128,384]{1,0:T(8,128)(2,1)S(1)}, u32[]{:S(2)}, u32[]{:S(2)}) collective-permute-start(bf16[128,384]{1,0:T(8,128)(2,1)S(1)} %bitcast.43), channel_id=1, source_target_pairs={{0,16},{1,17},{2,18},{3,19},{4,20},{5,21},{6,22},{7,23},{8,24},{9,... | collective-permute-start | bytes 294920 | tf_op jit(solution)/shard_map/grads_b/ppermute | solution.py:75
  201.1 11.2 %all-to-all-start.2 = ((bf16[32,16,128]{2,1,0:T(8,128)(2,1)}), bf16[32,16,128]{2,1,0:T(8,128)(2,1)S(1)}, u32[]{:S(2)}, u32[]{:S(2)}) async-start(bf16[32,16,128]{2,1,0:T(8,128)(2,1)} %get-tuple-element.145), calls=%async_computation.2 | async-start | bytes 262144 | tf_op jit(solution)/shard_map/grads_c_send/all_to_all | solution.py:716
  206.9 13.0 %collective-permute-start.37 = (bf16[2,128,384]{2,1,0:T(8,128)(2,1)S(1)}, bf16[2,128,384]{2,1,0:T(8,128)(2,1)S(1)}, u32[]{:S(2)}, u32[]{:S(2)}) collective-permute-start(bf16[2,128,384]{2,1,0:T(8,128)(2,1)S(1)} %grads_b.7), channel_id=1, source_target_pairs={{0,8},{1,9},{2,10},{3,11},{4,12},{5,13},{6,14},{7,15},{8,0},{9,1},... | collective-permute-start | bytes 589832 | tf_op jit(solution)/shard_map/grads_b/ppermute | solution.py:75
  213.0 6.1 %collective-permute-start.40 = (bf16[128,128]{1,0:T(8,128)(2,1)S(1)}, bf16[128,128]{1,0:T(8,128)(2,1)S(1)}, u32[]{:S(2)}, u32[]{:S(2)}) collective-permute-start(bf16[128,128]{1,0:T(8,128)(2,1)S(1)} %bitcast.46), channel_id=1, source_target_pairs={{0,24},{1,25},{2,26},{3,27},{4,28},{5,29},{6,30},{7,31},{8,16},{9,... | collective-permute-start | bytes 98312 | tf_op jit(solution)/shard_map/grads_b/ppermute | solution.py:75
  214.5 5.2 %collective-permute-start.39 = (bf16[128,128]{1,0:T(8,128)(2,1)S(1)}, bf16[128,128]{1,0:T(8,128)(2,1)S(1)}, u32[]{:S(2)}, u32[]{:S(2)}) collective-permute-start(bf16[128,128]{1,0:T(8,128)(2,1)S(1)} %bitcast.47), channel_id=1, source_target_pairs={{0,16},{1,17},{2,18},{3,19},{4,20},{5,21},{6,22},{7,23},{8,24},{9,... | collective-permute-start | bytes 98312 | tf_op jit(solution)/shard_map/grads_b/ppermute | solution.py:75
  215.2 4.5 %collective-permute-start.38 = (bf16[128,128]{1,0:T(8,128)(2,1)S(1)}, bf16[128,128]{1,0:T(8,128)(2,1)S(1)}, u32[]{:S(2)}, u32[]{:S(2)}) collective-permute-start(bf16[128,128]{1,0:T(8,128)(2,1)S(1)} %bitcast.48), channel_id=1, source_target_pairs={{0,8},{1,9},{2,10},{3,11},{4,12},{5,13},{6,14},{7,15},{8,0},{9,1},... | collective-permute-start | bytes 98312 | tf_op jit(solution)/shard_map/grads_b/ppermute | solution.py:75
  220.6 13.6 %collective-permute-start.42 = (bf16[4,128,512]{2,1,0:T(8,128)(2,1)S(1)}, bf16[4,128,512]{2,1,0:T(8,128)(2,1)S(1)}, u32[]{:S(2)}, u32[]{:S(2)}) collective-permute-start(bf16[4,128,512]{2,1,0:T(8,128)(2,1)S(1)} %grads_b.11.refs_1_), channel_id=1, source_target_pairs={{0,4},{1,3},{2,6},{3,1},{4,0},{5,7},{6,2},{7,5},{8,12},{9,11},{10,... | collective-permute-start | bytes 1572872 | tf_op jit(solution)/shard_map/grads/ppermute | solution.py:75
  221.3 12.9 %collective-permute-start.41 = (bf16[4,128,512]{2,1,0:T(8,128)(2,1)S(1)}, bf16[4,128,512]{2,1,0:T(8,128)(2,1)S(1)}, u32[]{:S(2)}, u32[]{:S(2)}) collective-permute-start(bf16[4,128,512]{2,1,0:T(8,128)(2,1)S(1)} %grads_b.11.refs_1_), channel_id=1, source_target_pairs={{0,2},{1,5},{2,0},{3,7},{4,6},{5,1},{6,4},{7,3},{8,10},{9,13},{10,... | collective-permute-start | bytes 1572872 | tf_op jit(solution)/shard_map/grads/ppermute | solution.py:75
  234.2 9.2 %collective-permute-start.49 = (bf16[4,128,512]{2,1,0:T(8,128)(2,1)S(1)}, bf16[4,128,512]{2,1,0:T(8,128)(2,1)S(1)}, u32[]{:S(2)}, u32[]{:S(2)}) collective-permute-start(bf16[4,128,512]{2,1,0:T(8,128)(2,1)S(1)} %collective-permute-done.41.refs_2_), channel_id=1, source_target_pairs={{0,4},{1,3},{2,6},{3,1},{4,0},{5,7},{6,2},{7,5},{8,12},{9,11},{10,... | collective-permute-start | bytes 1572872 | tf_op jit(solution)/shard_map/grads/ppermute | solution.py:75
  234.5 8.9 %collective-permute-start.43 = (bf16[4,128,512]{2,1,0:T(8,128)(2,1)S(1)}, bf16[4,128,512]{2,1,0:T(8,128)(2,1)S(1)}, u32[]{:S(2)}, u32[]{:S(2)}) collective-permute-start(bf16[4,128,512]{2,1,0:T(8,128)(2,1)S(1)} %grads_b.11.refs_1_), channel_id=1, source_target_pairs={{0,1},{1,0},{2,3},{3,2},{4,5},{5,4},{6,7},{7,6},{8,9},{9,8},{10,11... | collective-permute-start | bytes 1572872 | tf_op jit(solution)/shard_map/grads/ppermute | solution.py:75
  234.8 8.6 %collective-permute-start.45 = (bf16[4,128,512]{2,1,0:T(8,128)(2,1)S(1)}, bf16[4,128,512]{2,1,0:T(8,128)(2,1)S(1)}, u32[]{:S(2)}, u32[]{:S(2)}) collective-permute-start(bf16[4,128,512]{2,1,0:T(8,128)(2,1)S(1)} %collective-permute-done.42.refs_3_), channel_id=1, source_target_pairs={{0,1},{1,0},{2,3},{3,2},{4,5},{5,4},{6,7},{7,6},{8,9},{9,8},{10,11... | collective-permute-start | bytes 1572872 | tf_op jit(solution)/shard_map/grads/ppermute | solution.py:75
  235.0 8.4 %collective-permute-start.44 = (bf16[4,128,512]{2,1,0:T(8,128)(2,1)S(1)}, bf16[4,128,512]{2,1,0:T(8,128)(2,1)S(1)}, u32[]{:S(2)}, u32[]{:S(2)}) collective-permute-start(bf16[4,128,512]{2,1,0:T(8,128)(2,1)S(1)} %collective-permute-done.41.refs_2_), channel_id=1, source_target_pairs={{0,1},{1,0},{2,3},{3,2},{4,5},{5,4},{6,7},{7,6},{8,9},{9,8},{10,11... | collective-permute-start | bytes 1572872 | tf_op jit(solution)/shard_map/grads/ppermute | solution.py:75
  236.2 17.1 %copy-start.12 = (bf16[320,256]{1,0:T(8,128)(2,1)S(1)}, bf16[320,256]{1,0:T(8,128)(2,1)}, u32[]{:S(2)}) copy-start(bf16[320,256]{1,0:T(8,128)(2,1)} %get-tuple-element.171.refs_0_) | copy-start | bytes 491524
  243.4 2.0 collective-permute-start.50
  243.5 9.8 %collective-permute-start.46 = (bf16[320,256]{1,0:T(8,128)(2,1)}, bf16[320,256]{1,0:T(8,128)(2,1)S(1)}, u32[]{:S(2)}, u32[]{:S(2)}) collective-permute-start(bf16[320,256]{1,0:T(8,128)(2,1)} %get-tuple-element.166), channel_id=1, source_target_pairs={{0,1},{1,0},{2,3},{3,2},{4,5},{5,4},{6,7},{7,6},{8,9},{9,8},{10,11... | collective-permute-start | bytes 491528 | tf_op jit(solution)/shard_map/rows_out/ppermute | solution.py:75
  244.0 9.2 %collective-permute-start.47 = (bf16[320,256]{1,0:T(8,128)(2,1)}, bf16[320,256]{1,0:T(8,128)(2,1)S(1)}, u32[]{:S(2)}, u32[]{:S(2)}) collective-permute-start(bf16[320,256]{1,0:T(8,128)(2,1)} %get-tuple-element.167), channel_id=1, source_target_pairs={{0,2},{1,3},{2,0},{3,1},{4,6},{5,7},{6,4},{7,5},{8,10},{9,11},{10,... | collective-permute-start | bytes 491528 | tf_op jit(solution)/shard_map/rows_out/ppermute | solution.py:75
  245.4 7.9 %collective-permute-start.48 = (bf16[320,256]{1,0:T(8,128)(2,1)}, bf16[320,256]{1,0:T(8,128)(2,1)S(1)}, u32[]{:S(2)}, u32[]{:S(2)}) collective-permute-start(bf16[320,256]{1,0:T(8,128)(2,1)} %get-tuple-element.168), channel_id=1, source_target_pairs={{0,3},{1,2},{2,1},{3,0},{4,7},{5,6},{6,5},{7,4},{8,11},{9,10},{10,... | collective-permute-start | bytes 491528 | tf_op jit(solution)/shard_map/rows_out/ppermute | solution.py:75
  (25 other events, 154.2 us)
